TPU v7x, 128 devices: a whole 4x4x4 slice. The times are simulated.
128 devices in a mesh: past: 8 (over y, z_lo), second: 16 (over x, z_hi, core).
Axes of the slice: x: 4, y: 4, z: 4 (z_hi: 2, z_lo: 2; z = z_hi * 2 + z_lo), core: 2. Of those that a mesh axis runs over, the one named last changes fastest.
Arguments:
- resident: bfloat16 [24576, 24576], P('past', 'second'), may hold values from -6 to 6
- memory: bfloat16 [2, 384, 24576], P(None, None, 'past'), may hold values from -0.0390625 to 0.0390625
- previous: bfloat16 [2, 384, 24576], P(None, None, 'second'), may hold values from -6 to 6
- inverse_part: float32 [2, 384, 384], replicated, may hold values from -0.3125 to 0.3125
- pair_coupling: float32 [32, 32], replicated, may hold values from 0.000318944 to 0.00318944
Outputs:
- fronts: bfloat16 [2, 384, 24576], P(None, None, 'second')
All inputs are finite; a program needn't handle non-finite values.
Results may differ from a plain program's by a relative error of at most 0.017.
Values may be sent and summed in bfloat16 or wider, within the bound.
No kernel may reach another device: no remote copies, remote signals or barrier semaphores. Data moves between devices by JAX's collectives and lax.ppermute only.
A program may use at most 128 MiB of HBM per device.

v0:
```python
import jax
import jax.numpy as jnp
from jax import lax
from jax.sharding import PartitionSpec as P

step_size = 0.5


def orbital_flip(block, orbitals):
    row_count, col_count = block.shape
    blocks = block.reshape(row_count // orbitals, orbitals, col_count // orbitals, orbitals)
    return blocks.transpose(0, 3, 2, 1).reshape(row_count, col_count)


def solve_front(summed, prior, inverse_block):
    source = prior.astype(jnp.float32) - step_size * summed
    solved = source + jnp.dot(
        inverse_block, source, precision=lax.Precision.HIGHEST, preferred_element_type=jnp.float32
    )
    return solved.astype(jnp.bfloat16)


def self_energy(front, pair_coupling):
    orbitals = pair_coupling.shape[0]
    row_count, col_count = front.shape
    values = front.astype(jnp.float32)
    mirror = orbital_flip(values, orbitals)
    blocks = (values * values * mirror).reshape(
        row_count // orbitals, orbitals, col_count // orbitals, orbitals
    )
    return (
        (blocks * pair_coupling[None, :, None, :])
        .reshape(row_count, col_count)
        .astype(jnp.bfloat16)
    )


def per_device(resident, memory, previous, inverse_part, pair_coupling):

    def advance(memory_row, front_index):
        partial_value = jnp.dot(memory_row, resident, preferred_element_type=jnp.float32)
        summed = lax.psum(partial_value.astype(jnp.bfloat16), "past").astype(jnp.float32)
        prior_cols = previous[front_index]
        return solve_front(summed, prior_cols, inverse_part[front_index])

    front_one = advance(memory[0], 0)
    energy_one = self_energy(front_one, pair_coupling)
    span_cols = memory.shape[2]
    whole_row = lax.all_gather(energy_one, "second", axis=1, tiled=True)
    gathered = lax.dynamic_slice_in_dim(whole_row, lax.axis_index("past") * span_cols, span_cols, 1)
    orbitals = pair_coupling.shape[0]
    memory_next = (
        memory[1].astype(jnp.float32) + orbital_flip(gathered, orbitals).astype(jnp.float32)
    ).astype(jnp.bfloat16)
    front_two = advance(memory_next, 1)
    return jnp.stack([front_one, front_two])


def solution(mesh):
    in_specs = (P("past", "second"), P(None, None, "past"), P(None, None, "second"), P(), P())
    out_specs = P(None, None, "second")
    return jax.shard_map(
        per_device, mesh=mesh, in_specs=in_specs, out_specs=out_specs, check_vma=False
    )
```

profile of v0, /device:TPU:0, one launch (start us, length us, event | category | flops | bytes accessed | tf_op | source)
XLA Modules:
  0.0 406.2 jit_solution(5935509110012505917)
XLA Ops:
  6.5 0.0 copy-start
  6.5 0.0 all-reduce.3.cloned.1.call-start
  6.5 9.2 %convolution_convert_fusion.1 = bf16[384,1536]{1,0:T(8,128)(2,1)} fusion(bf16[3072,1536]{1,0:T(8,128)(2,1)} %param.5, bf16[2,384,3072]{2,1,0:T(8,128)(2,1)} %param.6), kind=kOutput, calls=%fused_computation.9 | convolution fusion | flops 3624468480 | bytes 12976128 | tf_op jit(solution)/shard_map/dot_general | solution.py:41
  15.8 0.0 all-reduce.3.cloned.1.call-update
  15.8 0.0 all-gather.2.cloned.1.call-start
  15.8 0.0 copy-done
  15.9 4.4 %mul.29 = f32[12,32,48,32]{3,2,1,0:T(8,128)} broadcast(f32[32,32]{1,0:T(8,128)S(1)} %copy-done), dimensions={1,3} | broadcast | bytes 2363392 | tf_op jit(solution)/shard_map/mul | solution.py:32
  20.3 6.7 %mul.30 = f32[384,1536]{1,0:T(8,128)S(1)} reshape(f32[12,32,48,32]{3,2,1,0:T(8,128)} %mul.29) | data formatting | bytes 4718592 | tf_op jit(solution)/shard_map/mul | solution.py:32
  27.0 70.5 %all-reduce.3.cloned.1.call-done = bf16[384,1536]{1,0:T(8,128)(2,1)} async-done(((bf16[384,1536]{1,0:T(8,128)(2,1)}), bf16[384,1536]{1,0:T(8,128)(2,1)}) %all-reduce.3.cloned.1.call-update) | async-done | bytes 1179664 | tf_op jit(solution)/shard_map/psum | solution.py:42
  97.5 6.8 %fusion.3 = bf16[384,1536]{1,0:T(8,128)(2,1)S(1)} fusion(bf16[384,1536]{1,0:T(8,128)(2,1)} %all-reduce.3.cloned.1.call-done, bf16[2,384,1536]{2,1,0:T(8,128)(2,1)} %param.7, f32[2,384,384]{2,1,0:T(8,128)} %param.8), kind=kOutput, calls=%fused_computation.6 | convolution fusion | flops 2723807232 | bytes 6488064 | tf_op jit(solution)/shard_map/dot_general | solution.py:17
  104.3 4.9 %reshape.22 = f32[12,32,48,32]{3,2,1,0:T(8,128)} reshape(bf16[384,1536]{1,0:T(8,128)(2,1)S(1)} %fusion.3) | data formatting | bytes 3538944 | tf_op jit(solution)/shard_map/reshape | solution.py:11
  109.2 10.8 %copy.11 = f32[12,32,48,32]{3,2,1,0:T(8,128)} copy(f32[12,32,48,32]{1,2,3,0:T(8,128)} %bitcast.55) | data formatting | bytes 4718592 | tf_op jit(solution)/shard_map/transpose | solution.py:12
  120.0 7.7 %reshape.23 = f32[384,1536]{1,0:T(8,128)} reshape(f32[12,32,48,32]{3,2,1,0:T(8,128)} %copy.11) | data formatting | bytes 4718592 | tf_op jit(solution)/shard_map/reshape | solution.py:12
  127.8 3.3 multiply_convert_fusion
  131.1 0.0 all-gather.2.cloned.1.call-update
  131.1 0.2 all-reduce.5.cloned.1.call-start
  131.3 119.3 %all-gather.2.cloned.1.call-done = bf16[384,24576]{1,0:T(8,128)(2,1)} async-done(((bf16[384,1536]{1,0:T(8,128)(2,1)}), bf16[384,24576]{1,0:T(8,128)(2,1)}) %all-gather.2.cloned.1.call-update) | async-done | bytes 18874384 | tf_op jit(solution)/shard_map/all_gather | solution.py:49
  250.6 4.4 %dynamic-slice_convert_fusion = f32[384,3072]{1,0:T(8,128)} fusion(bf16[384,24576]{1,0:T(8,128)(2,1)} %all-gather.2.cloned.1.call-done, s32[]{:T(128)S(6)} %select_n.3), kind=kLoop, calls=%fused_computation.18 | loop fusion | flops 1179648 | bytes 7077892 | tf_op jit(solution)/shard_map/convert_element_type | solution.py:53
  255.0 12.3 %reshape.28 = f32[12,32,96,32]{3,2,1,0:T(8,128)} reshape(f32[384,3072]{1,0:T(8,128)} %dynamic-slice_convert_fusion) | data formatting | bytes 9437184 | tf_op jit(solution)/shard_map/convert_element_type | solution.py:53
  267.3 22.5 %copy.12 = f32[12,32,96,32]{3,2,1,0:T(8,128)} copy(f32[12,32,96,32]{1,2,3,0:T(8,128)} %bitcast.54) | data formatting | bytes 9437184 | tf_op jit(solution)/shard_map/convert_element_type | solution.py:53
  289.7 14.6 %reshape.27 = f32[384,3072]{1,0:T(8,128)} reshape(f32[12,32,96,32]{3,2,1,0:T(8,128)} %copy.12) | data formatting | bytes 9437184 | tf_op jit(solution)/shard_map/convert_element_type | solution.py:53
  304.3 0.0 copy-start.1
  304.3 10.7 %convolution_convert_fusion = bf16[384,1536]{1,0:T(8,128)(2,1)} fusion(bf16[3072,1536]{1,0:T(8,128)(2,1)} %param.5, f32[384,3072]{1,0:T(8,128)} %reshape.27, bf16[2,384,3072]{2,1,0:T(8,128)(2,1)} %param.6), kind=kOutput, calls=%fused_computation.8 | convolution fusion | flops 3628007424 | bytes 17694720 | tf_op jit(solution)/shard_map/dot_general | solution.py:41
  315.0 0.0 all-reduce.5.cloned.1.call-update
  315.1 77.0 %all-reduce.5.cloned.1.call-done = bf16[384,1536]{1,0:T(8,128)(2,1)} async-done(((bf16[384,1536]{1,0:T(8,128)(2,1)}), bf16[384,1536]{1,0:T(8,128)(2,1)}) %all-reduce.5.cloned.1.call-update) | async-done | bytes 1179664 | tf_op jit(solution)/shard_map/psum | solution.py:42
  392.0 0.0 copy-done.1
  392.0 6.1 %fusion.5 = bf16[1,384,1536]{2,1,0:T(8,128)(2,1)S(1)} fusion(bf16[384,1536]{1,0:T(8,128)(2,1)} %all-reduce.5.cloned.1.call-done, bf16[2,384,1536]{2,1,0:T(8,128)(2,1)S(1)} %copy-done.1, f32[2,384,384]{2,1,0:T(8,128)} %param.8), kind=kOutput, calls=%fused_computation.10 | convolution fusion | flops 2723807232 | bytes 6488064 | tf_op jit(solution)/shard_map/dot_general | solution.py:17
  398.1 1.6 pad_maximum_fusion
Async XLA Ops:
  6.5 9.3 %copy-start = (f32[32,32]{1,0:T(8,128)S(1)}, f32[32,32]{1,0:T(8,128)}, u32[]{:S(2)}) copy-start(f32[32,32]{1,0:T(8,128)} %param.9) | copy-start | bytes 12292
  6.5 91.0 %all-reduce.3.cloned.1.call-start = ((), (), s32[]{:S(2)}) async-start(), calls=%async_computation | async-start | bytes 2359296 | tf_op jit(solution)/shard_map/psum | solution.py:42
  15.8 234.8 %all-gather.2.cloned.1.call-start = ((), (), s32[]{:S(2)}) async-start(), calls=%async_computation.1 | async-start | bytes 20054016 | tf_op jit(solution)/shard_map/all_gather | solution.py:49
  131.1 260.9 %all-reduce.5.cloned.1.call-start = ((), (), s32[]{:S(2)}) async-start(), calls=%async_computation.2 | async-start | bytes 2359296 | tf_op jit(solution)/shard_map/psum | solution.py:42
  304.3 87.7 %copy-start.1 = (bf16[2,384,1536]{2,1,0:T(8,128)(2,1)S(1)}, bf16[2,384,1536]{2,1,0:T(8,128)(2,1)}, u32[]{:S(2)}) copy-start(bf16[2,384,1536]{2,1,0:T(8,128)(2,1)} %param.7) | copy-start | bytes 7077892
Sparse Core Ops, SparseCore 0:
  15.9 81.5 all-reduce.2
  131.2 119.3 all-gather.1
  315.2 76.7 all-reduce.4
where the time goes:
time: 407 us; the launch traced here: 406 us
  waiting for transfers between devices  267 us (66%)
  local copies, waits for them, and re-layouts  83.9 us (21%)
  matrix products  32.8 us (8%)
  between operations  13.1 us (3%)
  other arithmetic  9.31 us (2%)
    psum x2, waiting for transfers between devices, advance(): lax.psum(partial_value.astype(jnp.bfloat16), 'past').astype(jnp.float32)  147 us
    all_gather x1, waiting for transfers between devices, per_device(): whole_row = lax.all_gather(energy_one, 'second', axis=1, tiled=True)  119 us
    convert_element_type x3, local copies, waits for them, and re-layouts, per_device(): orbital_flip(gathered, orbitals).astype(jnp.float32)  49.3 us
    dot_general x2, matrix products, advance(): jnp.dot(memory_row, resident, preferred_element_type=jnp.float32)  19.9 us
    dot_general x2, matrix products, solve_front(): jnp.dot(inverse_block, source, precision=lax.Precision.HIGHEST, preferred...  12.9 us
    mul x2, local copies, waits for them, and re-layouts, self_energy(): blocks * pair_coupling[None, :, None, :]  11.2 us
    transpose x1, local copies, waits for them, and re-layouts, orbital_flip(): return blocks.transpose(0, 3, 2, 1).reshape(row_count, col_count)  10.8 us
  transfers between devices with their start and end apart: 3, of which 3 were waited for; matrix products, arithmetic and copies ran while one was open for 3% of the time, Pallas kernels for 0%

commit v1 on v0

v1 whole, which is shorter than its diff:
```python
import functools

import jax
import jax.numpy as jnp
from jax import lax
from jax.experimental import pallas as pl
from jax.experimental.pallas import tpu as pltpu
from jax.sharding import Mesh, PartitionSpec as P

step_size = 0.5
ORB = 32
f32 = jnp.float32
bf16 = jnp.bfloat16
PASTS = ("y", "zl")
SECONDS = ("x", "zh", "c")
ALL = PASTS + SECONDS
VMEM = pl.BlockSpec(memory_space=pltpu.VMEM)
SMEM = pl.BlockSpec(memory_space=pltpu.SMEM)


def params(megabytes):
    return pltpu.CompilerParams(vmem_limit_bytes=megabytes << 20)


def first_product_kernel(memory_ref, resident_ref, out_ref):
    product = jnp.dot(memory_ref[...], resident_ref[...], preferred_element_type=f32)
    out_ref[...] = product.T.astype(bf16)


def first_product(memory, resident):
    _, rows, depth = memory.shape
    cols = resident.shape[1]
    tile = 512
    return pl.pallas_call(
        first_product_kernel,
        grid=(cols // tile,),
        in_specs=[
            pl.BlockSpec((None, rows, depth), lambda n: (0, 0, 0)),
            pl.BlockSpec((depth, tile), lambda n: (0, n)),
        ],
        out_specs=pl.BlockSpec((tile, rows), lambda n: (n, 0)),
        out_shape=jax.ShapeDtypeStruct((cols, rows), bf16),
        compiler_params=params(40),
        name="first_product",
    )(memory, resident)


def second_product_kernel(place_ref, memory_ref, own_ref, other_ref, resident_ref, out_ref, lhs_ref):
    @pl.when(pl.program_id(0) == 0)
    def _():
        z_high, core = place_ref[0], place_ref[1]
        half = memory_ref.shape[1] // 2
        for side, ref in enumerate((own_ref, other_ref)):
            start = (core ^ side) * half
            for x in range(4):
                near, far = ref[x, 0].astype(f32), ref[x, 1].astype(f32)
                low = jnp.where(z_high == 0, near, far)
                high = jnp.where(z_high == 0, far, near)
                pair = jnp.concatenate([low, high], axis=0).T
                width = pair.shape[1]
                at = pl.ds(pl.multiple_of(start + x * width, 128), width)
                lhs_ref[:, at] = (memory_ref[:, at].astype(f32) + pair).astype(bf16)

    product = jnp.dot(lhs_ref[...], resident_ref[...], preferred_element_type=f32)
    out_ref[...] = product.T.astype(bf16)


def second_product(place, memory, own, other, resident):
    _, rows, depth = memory.shape
    cols = resident.shape[1]
    tile = 512
    whole = lambda n: (0, 0, 0, 0)
    return pl.pallas_call(
        second_product_kernel,
        grid=(cols // tile,),
        in_specs=[
            SMEM,
            pl.BlockSpec((None, rows, depth), lambda n: (1, 0, 0)),
            pl.BlockSpec(own.shape, whole),
            pl.BlockSpec(other.shape, whole),
            pl.BlockSpec((depth, tile), lambda n: (0, n)),
        ],
        out_specs=pl.BlockSpec((tile, rows), lambda n: (n, 0)),
        out_shape=jax.ShapeDtypeStruct((cols, rows), bf16),
        scratch_shapes=[pltpu.VMEM((rows, depth), bf16)],
        compiler_params=params(48),
        name="second_product",
    )(place, memory, own, other, resident)


def solve_into(parts_ref, prior_ref, inverse_ref):
    summed = parts_ref[0].astype(f32)
    for i in range(1, parts_ref.shape[0]):
        summed = summed + parts_ref[i].astype(f32)
    source = prior_ref[...].astype(f32) - step_size * summed
    mixed = lax.dot_general(
        source,
        inverse_ref[...],
        (((1,), (1,)), ((), ())),
        precision=lax.Precision.HIGHEST,
        preferred_element_type=f32,
    )
    return (source + mixed).astype(bf16)


def flipped(values):
    rows, cols = values.shape
    strips = []
    pad = jnp.zeros((128 - ORB, 128), f32)
    for s in range(rows // ORB):
        pieces = []
        for q in range(cols // 128):
            block = values[s * ORB : (s + 1) * ORB, q * 128 : (q + 1) * 128]
            turned = jnp.concatenate([block, pad], axis=0).T
            piece = turned[:ORB]
            for t in range(1, 128 // ORB):
                piece = piece + pltpu.roll(turned[t * ORB : (t + 1) * ORB], t * ORB, 1)
            pieces.append(piece)
        strips.append(jnp.concatenate(pieces, axis=1))
    return jnp.concatenate(strips, axis=0)


def first_solve_kernel(parts_ref, prior_ref, inverse_ref, coupling_ref, front_ref, energy_ref):
    front = solve_into(parts_ref, prior_ref, inverse_ref)
    for i in range(front_ref.shape[0]):
        front_ref[i] = front
    values = front.astype(f32)
    mirror = flipped(values)
    energy_ref[...] = (mirror * mirror * values * coupling_ref[...]).astype(bf16)


def second_solve_kernel(parts_ref, prior_ref, inverse_ref, front_ref):
    front = solve_into(parts_ref, prior_ref, inverse_ref)
    for i in range(front_ref.shape[0]):
        front_ref[i] = front


def first_solve(parts, prior, inverse, coupling):
    return pl.pallas_call(
        first_solve_kernel,
        in_specs=[VMEM] * 4,
        out_specs=[VMEM] * 2,
        out_shape=[
            jax.ShapeDtypeStruct(parts.shape, bf16),
            jax.ShapeDtypeStruct(prior.shape, bf16),
        ],
        compiler_params=params(24),
        name="first_solve",
    )(parts, prior, inverse, coupling)


def second_solve(parts, prior, inverse):
    return pl.pallas_call(
        second_solve_kernel,
        in_specs=[VMEM] * 3,
        out_specs=VMEM,
        out_shape=jax.ShapeDtypeStruct(parts.shape, bf16),
        compiler_params=params(24),
        name="second_solve",
    )(parts, prior, inverse)


def join_kernel(one_ref, two_ref, out_ref):
    for front, ref in enumerate((one_ref, two_ref)):
        width = 2 * ref.shape[1]
        for m in range(ref.shape[0] // 2):
            pair = jnp.concatenate([ref[2 * m], ref[2 * m + 1]], axis=0)
            out_ref[front, :, m * width : (m + 1) * width] = pair.astype(f32).T.astype(bf16)


def join(one, two, rows, cols):
    return pl.pallas_call(
        join_kernel,
        in_specs=[VMEM] * 2,
        out_specs=VMEM,
        out_shape=jax.ShapeDtypeStruct((2, rows, cols), bf16),
        compiler_params=params(24),
        name="join",
    )(one, two)


def turn_pairs(size, flip):
    pairs = []
    for i in range(128):
        rest, c = divmod(i, 2)
        rest, zh = divmod(rest, 2)
        rest, x = divmod(rest, 4)
        y, zl = divmod(rest, 2)
        target = (((x * 2 + zh) * 4 + y) * 2 + (zl ^ flip)) * 2 + c
        pairs.append((i, target))
    return pairs


def per_device(resident, memory, previous, inverse_part, pair_coupling):
    rows = memory.shape[1]
    cols = resident.shape[1]
    width = cols // 8
    past = lax.axis_index("y") * 2 + lax.axis_index("zl")
    place = jnp.stack([lax.axis_index("zh"), lax.axis_index("c")]).astype(jnp.int32)
    priors = lax.dynamic_slice_in_dim(previous, past * width, width, 2).transpose(0, 2, 1)
    coupling = jnp.tile(pair_coupling, (width // ORB, rows // ORB))

    def scatter(partial):
        return lax.all_to_all(partial.reshape(8, width, rows), PASTS, 0, 0, tiled=True)

    parts = scatter(first_product(memory, resident))
    copies, energy = first_solve(parts, priors[0], inverse_part[0], coupling)
    near = lax.ppermute(energy, ALL, turn_pairs(128, 0))
    far = lax.ppermute(energy, ALL, turn_pairs(128, 1))
    both = jnp.broadcast_to(jnp.stack([near, far])[None], (4, 2, width, rows))
    own = lax.all_to_all(both, "x", 0, 0, tiled=True)
    other = lax.ppermute(own, "c", [(0, 1), (1, 0)])
    parts = scatter(second_product(place, memory, own, other, resident))
    front_one = lax.all_to_all(copies, PASTS, 0, 0, tiled=True)
    copies = second_solve(parts, priors[1], inverse_part[1])
    front_two = lax.all_to_all(copies, PASTS, 0, 0, tiled=True)
    return join(front_one, front_two, rows, cols)


def solution(mesh):
    fine = Mesh(mesh.devices.reshape(4, 2, 4, 2, 2), ALL)
    in_specs = (P(PASTS, SECONDS), P(None, None, PASTS), P(None, None, SECONDS), P(), P())
    out_specs = P(None, None, SECONDS)
    return jax.shard_map(
        per_device, mesh=fine, in_specs=in_specs, out_specs=out_specs, check_vma=False
    )
```

time: 407 us -> 155 us (0.38)
  waiting for transfers between devices: 267 us -> 24.8 us
  blocking collectives: 0 us -> 73.5 us
  local copies, waits for them, and re-layouts: 83.9 us -> 20.2 us
  matrix products: 32.8 us -> 0 us
  Pallas kernels: 0 us -> 21.1 us
  starting transfers between devices: 0.27 us -> 14.5 us
  between operations: 13.1 us -> 0.13 us
  other arithmetic: 9.31 us -> 0.11 us
    psum x2 -> x0, waiting for transfers between devices: 147 us -> none  [advance(): lax.psum(partial_value.astype(jnp.bfloat16), 'past').astype(jnp.float32)]
    all_gather x1 -> x0, waiting for transfers between devices: 119 us -> none  [per_device(): whole_row = lax.all_gather(energy_one, 'second', axis=1, tiled=True)]
    all_to_all x0 -> x3, blocking collectives: none -> 73.5 us  [the longest x1 34.2 us: per_device(): own = lax.all_to_all(both, 'x', 0, 0, tiled=True)]
    convert_element_type x3 -> x0, local copies, waits for them, and re-layouts: 49.3 us -> none  [per_device(): orbital_flip(gathered, orbitals).astype(jnp.float32)]
    dot_general x4 -> x0, matrix products: 32.8 us -> none  [the longest x2 19.9 us: advance(): jnp.dot(memory_row, resident, preferred_element_type=jnp.float32)]
    pallas_call x0 -> x5, Pallas kernels: none -> 21.1 us  [the longest x1 8.82 us: second_product(): pl.pallas_call(second_product_kernel, grid=(cols // tile,), in_specs=[SME...]
    all_to_all x0 -> x2, waiting for transfers between devices: none -> 19.9 us  [the longest x1 12.7 us: per_device(): front_one = lax.all_to_all(copies, PASTS, 0, 0, tiled=True)]
    reshape x2 -> x0, local copies, waits for them, and re-layouts: 12.6 us -> none  [the longest x1 7.74 us: orbital_flip(): return blocks.transpose(0, 3, 2, 1).reshape(row_count, col_count)]
  transfers between devices with their start and end apart: 3 -> 5, of which waited for: 3 -> 4; matrix products, arithmetic and copies ran while one was open for 3% -> 7% of each run, Pallas kernels for 0% -> 1%
where the time goes in v1:
time: 155 us; the launch traced here: 154 us
  blocking collectives  73.5 us (47%)
  waiting for transfers between devices  24.8 us (16%)
  Pallas kernels  21.1 us (14%)
  local copies, waits for them, and re-layouts  20.2 us (13%)
  starting transfers between devices  14.5 us (9%)
    all_to_all x1, blocking collectives, per_device(): own = lax.all_to_all(both, 'x', 0, 0, tiled=True)  34.2 us
    all_to_all x1, blocking collectives, scatter(): lax.all_to_all(partial.reshape(8, width, rows), PASTS, 0, 0, tiled=True)  19.9 us
    all_to_all x1, blocking collectives, per_device(): front_two = lax.all_to_all(copies, PASTS, 0, 0, tiled=True)  19.4 us
    all_to_all x1, waiting for transfers between devices, per_device(): front_one = lax.all_to_all(copies, PASTS, 0, 0, tiled=True)  12.7 us
    unnamed x23, local copies, waits for them, and re-layouts  11.3 us
    pallas_call x1, Pallas kernels, second_product(): pl.pallas_call(second_product_kernel, grid=(cols // tile,), in_specs=[SME...  8.82 us
    all_to_all x1, waiting for transfers between devices, scatter(): lax.all_to_all(partial.reshape(8, width, rows), PASTS, 0, 0, tiled=True)  7.18 us
    pallas_call x1, Pallas kernels, first_product(): pl.pallas_call(first_product_kernel, grid=(cols // tile,), in_specs=[pl.B...  6.71 us
  transfers between devices with their start and end apart: 5, of which 4 were waited for; matrix products, arithmetic and copies ran while one was open for 7% of the time, Pallas kernels for 1%

profile of v1, /device:TPU:0, one launch (start us, length us, event | category | flops | bytes accessed | tf_op | source)
XLA Modules:
  0.0 154.4 jit_solution(6019467592752296336)
XLA Ops:
  0.0 0.0 copy-start
  0.0 0.0 copy-start.1
  0.0 2.5 %copy-done.1 = bf16[2,384,3072]{2,1,0:T(8,128)(2,1)S(1)} copy-done((bf16[2,384,3072]{2,1,0:T(8,128)(2,1)S(1)}, bf16[2,384,3072]{2,1,0:T(8,128)(2,1)}, u32[]{:S(2)}) %copy-start.1) | copy-done | bytes 4718616
  2.5 6.7 %first_product.1 = bf16[1536,384]{1,0:T(8,128)(2,1)S(1)} custom-call(bf16[2,384,3072]{2,1,0:T(8,128)(2,1)S(1)} %copy-done.1, bf16[3072,1536]{1,0:T(8,128)(2,1)} %resident_ref.3), custom_call_target="tpu_custom_call" | custom-call | tf_op jit(solution)/shard_map/first_product/pallas_call | solution.py:34
  9.2 0.0 copy-start.3
  9.2 1.0 copy-done.3
  10.3 5.9 %all-to-all-start = ((bf16[8,192,384]{2,1,0:T(8,128)(2,1)}), bf16[8,192,384]{2,1,0:T(8,128)(2,1)S(1)}, u32[]{:S(2)}, u32[]{:S(2)}) async-start(bf16[8,192,384]{2,1,0:T(8,128)(2,1)} %bitcast.16), calls=%async_computation | async-start | bytes 2359296 | tf_op jit(solution)/shard_map/all_to_all | solution.py:204
  16.2 0.0 copy-start.10
  16.2 0.0 copy-done
  16.2 0.9 constant_dynamic-slice_fusion
  17.1 1.9 %copy.8 = bf16[2,384,192]{1,2,0:T(8,128)(2,1)} copy(bf16[2,384,192]{2,1,0:T(8,128)(2,1)} %constant_dynamic-slice_fusion) | data formatting | bytes 589824
  19.0 0.0 copy-done.10
  19.0 1.3 tile.4
  20.3 2.6 %tile.10.coupling_ref = f32[192,384]{1,0:T(8,128)} reshape(f32[6,32,12,32]{3,2,1,0:T(8,128)} %tile.4) | data formatting | bytes 589824 | tf_op jit(solution)/shard_map/tile | solution.py:201
  22.8 1.7 %slice_bitcast_fusion.2 = (bf16[192,384]{1,0:T(8,128)(2,1)}, bf16[192,384]{1,0:T(8,128)(2,1)}) fusion(bf16[2,192,384]{2,1,0:T(8,128)(2,1)} %bitcast.17), kind=kLoop, calls=%fused_computation.3 | loop fusion | bytes 589824 | tf_op jit(solution)/shard_map/squeeze | solution.py:215
  24.6 2.3 %slice_bitcast_fusion = (f32[384,384]{1,0:T(8,128)}, f32[384,384]{1,0:T(8,128)}) fusion(f32[2,384,384]{2,1,0:T(8,128)} %param.8), kind=kLoop, calls=%fused_computation | loop fusion | bytes 2359296 | tf_op jit(solution)/shard_map/squeeze | solution.py:215
  26.9 7.2 %all-to-all-done.parts_ref = bf16[8,192,384]{2,1,0:T(8,128)(2,1)S(1)} async-done(((bf16[8,192,384]{2,1,0:T(8,128)(2,1)}), bf16[8,192,384]{2,1,0:T(8,128)(2,1)S(1)}, u32[]{:S(2)}, u32[]{:S(2)}) %all-to-all-start) | async-done | bytes 1179680 | tf_op jit(solution)/shard_map/all_to_all | solution.py:204
  34.1 0.0 copy-start.5
  34.1 1.1 copy-done.5
  35.1 0.0 copy-start.6
  35.1 1.0 copy-done.6
  36.1 0.0 copy-start.9
  36.1 0.9 copy-done.9
  37.0 1.3 first_solve.1
  38.3 0.0 copy-start.7
  38.3 3.7 %collective-permute-start.1 = (bf16[192,384]{1,0:T(8,128)(2,1)S(1)}, bf16[192,384]{1,0:T(8,128)(2,1)S(1)}, u32[]{:S(2)}, u32[]{:S(2)}) collective-permute-start(bf16[192,384]{1,0:T(8,128)(2,1)S(1)} %get-tuple-element.8), channel_id=1, source_target_pairs={{0,2},{1,3},{2,18},{3,19},{4,34},{5,35},{6,50},{7,51},{8,66},{9,67... | collective-permute-start | bytes 442376 | tf_op jit(solution)/shard_map/ppermute | solution.py:209
  42.0 0.7 collective-permute-start
  42.7 2.0 %collective-permute-done.1 = bf16[192,384]{1,0:T(8,128)(2,1)S(1)} collective-permute-done((bf16[192,384]{1,0:T(8,128)(2,1)S(1)}, bf16[192,384]{1,0:T(8,128)(2,1)S(1)}, u32[]{:S(2)}, u32[]{:S(2)}) %collective-permute-start.1) | collective-permute-done | bytes 147488 | tf_op jit(solution)/shard_map/ppermute | solution.py:209
  44.7 0.0 collective-permute-done
  44.7 0.1 broadcast_in_dim.2
  44.8 34.2 %all_to_all.25.own_ref = bf16[4,2,192,384]{3,2,1,0:T(8,128)(2,1)S(1)} all-to-all(bf16[4,2,192,384]{3,2,1,0:T(8,128)(2,1)S(1)} %broadcast_in_dim.2), channel_id=1, replica_groups=mesh['y'=4,'zl'=2,'x'=4,'zh'=2,'c'=2] {'x'}, dimensions={0} | all-to-all | bytes 2359296 | tf_op jit(solution)/shard_map/all_to_all | solution.py:211
  79.0 0.0 copy-done.7
  79.0 0.0 collective-permute-start.2
  79.0 0.1 pad_add_fusion.place_ref
  79.1 2.9 %collective-permute-done.2.other_ref = bf16[4,2,192,384]{3,2,1,0:T(8,128)(2,1)} collective-permute-done((bf16[4,2,192,384]{3,2,1,0:T(8,128)(2,1)S(1)}, bf16[4,2,192,384]{3,2,1,0:T(8,128)(2,1)}, u32[]{:S(2)}, u32[]{:S(2)}) %collective-permute-start.2) | collective-permute-done | bytes 1179680 | tf_op jit(solution)/shard_map/ppermute | solution.py:212
  82.0 8.8 %second_product.1 = bf16[1536,384]{1,0:T(8,128)(2,1)S(1)} custom-call(s32[2]{0:T(128)S(1)} %pad_add_fusion.place_ref, bf16[2,384,3072]{2,1,0:T(8,128)(2,1)} %memory_ref.3, bf16[4,2,192,384]{3,2,1,0:T(8,128)(2,1)S(1)} %all_to_all.25.own_ref, bf16[4,2,192,384]{3,2,1,0:T(8,128)(2,1)} %collective-permute-done.2.other_ref, bf16[3072,1536]{1,0:T(8,128)(2,1)} %resident_ref.3), custom_call_target="tpu_custom_call" | custom-call | tf_op jit(solution)/shard_map/second_product/pallas_call | solution.py:73
  90.8 19.9 %all_to_all.26.parts_ref = bf16[8,192,384]{2,1,0:T(8,128)(2,1)S(1)} all-to-all(bf16[8,192,384]{2,1,0:T(8,128)(2,1)S(1)} %bitcast.15), channel_id=1, replica_groups=mesh['y'=4,'zl'=2,'x'=4,'zh'=2,'c'=2] {'y','zl'}, dimensions={0} | all-to-all | bytes 2359296 | tf_op jit(solution)/shard_map/all_to_all | solution.py:204
  110.7 4.2 %all-to-all-start.1 = ((bf16[8,192,384]{2,1,0:T(8,128)(2,1)}), bf16[8,192,384]{2,1,0:T(8,128)(2,1)}, u32[]{:S(2)}, u32[]{:S(2)}) async-start(bf16[8,192,384]{2,1,0:T(8,128)(2,1)} %copy-done.7), calls=%async_computation.1 | async-start | bytes 2359296 | tf_op jit(solution)/shard_map/all_to_all | solution.py:214
  115.0 0.0 copy-start.4
  115.0 1.1 copy-done.4
  116.1 0.0 copy-start.8
  116.1 0.9 copy-done.8
  117.0 0.9 second_solve.1
  117.9 0.0 copy-start.2
  117.9 1.0 copy-done.2
  118.9 12.7 %all-to-all-done.1.one_ref = bf16[8,192,384]{2,1,0:T(8,128)(2,1)} async-done(((bf16[8,192,384]{2,1,0:T(8,128)(2,1)}), bf16[8,192,384]{2,1,0:T(8,128)(2,1)}, u32[]{:S(2)}, u32[]{:S(2)}) %all-to-all-start.1) | async-done | bytes 1179680 | tf_op jit(solution)/shard_map/all_to_all | solution.py:214
  131.6 19.4 %all_to_all.27.two_ref = bf16[8,192,384]{2,1,0:T(8,128)(2,1)S(1)} all-to-all(bf16[8,192,384]{2,1,0:T(8,128)(2,1)} %copy-done.2), channel_id=1, replica_groups=mesh['y'=4,'zl'=2,'x'=4,'zh'=2,'c'=2] {'y','zl'}, dimensions={0} | all-to-all | bytes 2359296 | tf_op jit(solution)/shard_map/all_to_all | solution.py:216
  151.1 3.4 %join.1 = bf16[2,384,1536]{2,1,0:T(8,128)(2,1)} custom-call(bf16[8,192,384]{2,1,0:T(8,128)(2,1)} %all-to-all-done.1.one_ref, bf16[8,192,384]{2,1,0:T(8,128)(2,1)S(1)} %all_to_all.27.two_ref), custom_call_target="tpu_custom_call" | custom-call | tf_op jit(solution)/shard_map/join/pallas_call | solution.py:172
  (1 shorter events, 0.0 us)
Async XLA Ops:
  0.0 16.2 %copy-start = (bf16[2,384,1536]{2,1,0:T(8,128)(2,1)S(1)}, bf16[2,384,1536]{2,1,0:T(8,128)(2,1)}, u32[]{:S(2)}) copy-start(bf16[2,384,1536]{2,1,0:T(8,128)(2,1)} %param.7) | copy-start | bytes 7077892
  0.0 2.5 %copy-start.1 = (bf16[2,384,3072]{2,1,0:T(8,128)(2,1)S(1)}, bf16[2,384,3072]{2,1,0:T(8,128)(2,1)}, u32[]{:S(2)}) copy-start(bf16[2,384,3072]{2,1,0:T(8,128)(2,1)} %memory_ref.3) | copy-start | bytes 14155780
  9.2 1.0 copy-start.3
  10.3 23.8 %all-to-all-start = ((bf16[8,192,384]{2,1,0:T(8,128)(2,1)}), bf16[8,192,384]{2,1,0:T(8,128)(2,1)S(1)}, u32[]{:S(2)}, u32[]{:S(2)}) async-start(bf16[8,192,384]{2,1,0:T(8,128)(2,1)} %bitcast.16), calls=%async_computation | async-start | bytes 2359296 | tf_op jit(solution)/shard_map/all_to_all | solution.py:204
  16.2 2.8 %copy-start.10 = (f32[32,32]{1,0:T(8,128)S(1)}, f32[32,32]{1,0:T(8,128)}, u32[]{:S(2)}) copy-start(f32[32,32]{1,0:T(8,128)} %param.9) | copy-start | bytes 12292
  34.1 1.1 copy-start.5
  35.1 1.0 copy-start.6
  36.1 0.9 copy-start.9
  38.3 40.7 %copy-start.7 = (bf16[8,192,384]{2,1,0:T(8,128)(2,1)}, bf16[8,192,384]{2,1,0:T(8,128)(2,1)S(1)}, u32[]{:S(2)}) copy-start(bf16[8,192,384]{2,1,0:T(8,128)(2,1)S(1)} %get-tuple-element.7) | copy-start | bytes 3538948
  38.3 6.3 %collective-permute-start.1 = (bf16[192,384]{1,0:T(8,128)(2,1)S(1)}, bf16[192,384]{1,0:T(8,128)(2,1)S(1)}, u32[]{:S(2)}, u32[]{:S(2)}) collective-permute-start(bf16[192,384]{1,0:T(8,128)(2,1)S(1)} %get-tuple-element.8), channel_id=1, source_target_pairs={{0,2},{1,3},{2,18},{3,19},{4,34},{5,35},{6,50},{7,51},{8,66},{9,67... | collective-permute-start | bytes 442376 | tf_op jit(solution)/shard_map/ppermute | solution.py:209
  42.0 2.7 %collective-permute-start = (bf16[192,384]{1,0:T(8,128)(2,1)S(1)}, bf16[192,384]{1,0:T(8,128)(2,1)S(1)}, u32[]{:S(2)}, u32[]{:S(2)}) collective-permute-start(bf16[192,384]{1,0:T(8,128)(2,1)S(1)} %get-tuple-element.8), channel_id=1, source_target_pairs={{0,0},{1,1},{2,16},{3,17},{4,32},{5,33},{6,48},{7,49},{8,64},{9,65... | collective-permute-start | bytes 442376 | tf_op jit(solution)/shard_map/ppermute | solution.py:208
  79.0 3.0 %collective-permute-start.2 = (bf16[4,2,192,384]{3,2,1,0:T(8,128)(2,1)S(1)}, bf16[4,2,192,384]{3,2,1,0:T(8,128)(2,1)}, u32[]{:S(2)}, u32[]{:S(2)}) collective-permute-start(bf16[4,2,192,384]{3,2,1,0:T(8,128)(2,1)S(1)} %all_to_all.25.own_ref), channel_id=1, source_target_pairs={{0,1},{1,0},{2,3},{3,2},{4,5},{5,4},{6,7},{7,6},{8,9},{9,8},{10,11... | collective-permute-start | bytes 3538952 | tf_op jit(solution)/shard_map/ppermute | solution.py:212
  110.7 20.9 %all-to-all-start.1 = ((bf16[8,192,384]{2,1,0:T(8,128)(2,1)}), bf16[8,192,384]{2,1,0:T(8,128)(2,1)}, u32[]{:S(2)}, u32[]{:S(2)}) async-start(bf16[8,192,384]{2,1,0:T(8,128)(2,1)} %copy-done.7), calls=%async_computation.1 | async-start | bytes 2359296 | tf_op jit(solution)/shard_map/all_to_all | solution.py:214
  115.0 1.1 copy-start.4
  116.1 0.9 copy-start.8
  117.9 1.0 copy-start.2

commit v2 on v1

v2 whole, which is shorter than its diff:
```python
import functools

import jax
import jax.numpy as jnp
from jax import lax
from jax.experimental import pallas as pl
from jax.experimental.pallas import tpu as pltpu
from jax.sharding import Mesh, PartitionSpec as P

step_size = 0.5
ORB = 32
f32 = jnp.float32
bf16 = jnp.bfloat16
PASTS = ("y", "zl")
SECONDS = ("x", "zh", "c")
ALL = PASTS + SECONDS
VMEM = pl.BlockSpec(memory_space=pltpu.VMEM)
SMEM = pl.BlockSpec(memory_space=pltpu.SMEM)


def params(megabytes):
    return pltpu.CompilerParams(vmem_limit_bytes=megabytes << 20)


def first_product_kernel(memory_ref, resident_ref, out_ref):
    product = jnp.dot(memory_ref[...], resident_ref[...], preferred_element_type=f32)
    out_ref[...] = product.T.astype(bf16)


def first_product(memory, resident):
    _, rows, depth = memory.shape
    cols = resident.shape[1]
    tile = 512
    return pl.pallas_call(
        first_product_kernel,
        grid=(cols // tile,),
        in_specs=[
            pl.BlockSpec((None, rows, depth), lambda n: (0, 0, 0)),
            pl.BlockSpec((depth, tile), lambda n: (0, n)),
        ],
        out_specs=pl.BlockSpec((tile, rows), lambda n: (n, 0)),
        out_shape=jax.ShapeDtypeStruct((cols, rows), bf16),
        compiler_params=params(56),
        name="first_product",
    )(memory, resident)


def place_pair(own, other, first, at, out_ref, base_ref):
    near, far = own.astype(f32), other.astype(f32)
    low = jnp.where(first == 0, near, far)
    high = jnp.where(first == 0, far, near)
    pair = jnp.concatenate([low, high], axis=0).T
    if base_ref is not None:
        pair = pair + base_ref[:, at].astype(f32)
    out_ref[:, at] = pair.astype(bf16)


def second_product_kernel(place_ref, memory_ref, *refs):
    chunk_refs, resident_ref, out_ref, lhs_ref = refs[:16], refs[16], refs[17], refs[18]

    @pl.when(pl.program_id(0) == 0)
    def _():
        x, z_high, core = place_ref[0], place_ref[1], place_ref[2]
        half = memory_ref.shape[1] // 2
        width = half // 4
        for side in range(2):
            for dx in range(4):
                own, other = chunk_refs[side * 8 + dx * 2], chunk_refs[side * 8 + dx * 2 + 1]
                start = (core ^ side) * half + ((x - dx) & 3) * width
                at = pl.ds(pl.multiple_of(start, 128), width)
                place_pair(own[...], other[...], z_high, at, lhs_ref, memory_ref)

    product = jnp.dot(lhs_ref[...], resident_ref[...], preferred_element_type=f32)
    out_ref[...] = product.T.astype(bf16)


def second_product(place, memory, chunks, resident):
    _, rows, depth = memory.shape
    cols = resident.shape[1]
    tile = 512
    return pl.pallas_call(
        second_product_kernel,
        grid=(cols // tile,),
        in_specs=[
            SMEM,
            pl.BlockSpec((None, rows, depth), lambda n: (1, 0, 0)),
            *[pl.BlockSpec(chunk.shape, lambda n: (0, 0)) for chunk in chunks],
            pl.BlockSpec((depth, tile), lambda n: (0, n)),
        ],
        out_specs=pl.BlockSpec((tile, rows), lambda n: (n, 0)),
        out_shape=jax.ShapeDtypeStruct((cols, rows), bf16),
        scratch_shapes=[pltpu.VMEM((rows, depth), bf16)],
        compiler_params=params(56),
        name="second_product",
    )(place, memory, *chunks, resident)


def solve_into(parts_ref, prior_ref, inverse_ref):
    summed = parts_ref[0].astype(f32)
    for i in range(1, parts_ref.shape[0]):
        summed = summed + parts_ref[i].astype(f32)
    source = prior_ref[...].astype(f32) - step_size * summed
    mixed = lax.dot_general(
        source,
        inverse_ref[...],
        (((1,), (1,)), ((), ())),
        precision=lax.Precision.HIGHEST,
        preferred_element_type=f32,
    )
    return (source + mixed).astype(bf16)


def flipped(values):
    rows, cols = values.shape
    strips = []
    pad = jnp.zeros((128 - ORB, 128), f32)
    for s in range(rows // ORB):
        pieces = []
        for q in range(cols // 128):
            block = values[s * ORB : (s + 1) * ORB, q * 128 : (q + 1) * 128]
            turned = jnp.concatenate([block, pad], axis=0).T
            piece = turned[:ORB]
            for t in range(1, 128 // ORB):
                piece = piece + pltpu.roll(turned[t * ORB : (t + 1) * ORB], t * ORB, 1)
            pieces.append(piece)
        strips.append(jnp.concatenate(pieces, axis=1))
    return jnp.concatenate(strips, axis=0)


def first_solve_kernel(parts_ref, prior_ref, inverse_ref, coupling_ref, front_ref, energy_ref):
    front = solve_into(parts_ref, prior_ref, inverse_ref)
    front_ref[...] = front
    values = front.astype(f32)
    mirror = flipped(values)
    energy_ref[...] = (mirror * mirror * values * coupling_ref[...]).astype(bf16)


def second_solve_kernel(parts_ref, prior_ref, inverse_ref, front_ref):
    front = solve_into(parts_ref, prior_ref, inverse_ref)
    front_ref[...] = front


def first_solve(parts, prior, inverse, coupling):
    return pl.pallas_call(
        first_solve_kernel,
        in_specs=[VMEM] * 4,
        out_specs=[VMEM] * 2,
        out_shape=[
            jax.ShapeDtypeStruct(prior.shape, bf16),
            jax.ShapeDtypeStruct(prior.shape, bf16),
        ],
        compiler_params=params(24),
        name="first_solve",
    )(parts, prior, inverse, coupling)


def second_solve(parts, prior, inverse):
    return pl.pallas_call(
        second_solve_kernel,
        in_specs=[VMEM] * 3,
        out_specs=VMEM,
        out_shape=jax.ShapeDtypeStruct(prior.shape, bf16),
        compiler_params=params(24),
        name="second_solve",
    )(parts, prior, inverse)


def join_one_kernel(front_ref, out_ref):
    width = front_ref.shape[0] // 4
    for m in range(4):
        at = slice(m * width, (m + 1) * width)
        out_ref[:, at] = front_ref[at, :].astype(f32).T.astype(bf16)


def join_one(front):
    cols, rows = front.shape
    return pl.pallas_call(
        join_one_kernel,
        grid=(1,),
        in_specs=[pl.BlockSpec((cols, rows), lambda i: (0, 0))],
        out_specs=pl.BlockSpec((None, rows, cols), lambda i: (0, 0, 0)),
        out_shape=jax.ShapeDtypeStruct((2, rows, cols), bf16),
        compiler_params=params(24),
        name="join_one",
    )(front)


def join_two_kernel(place_ref, *refs):
    chunk_refs, out_ref = refs[:8], refs[9]
    y, z_low = place_ref[3], place_ref[4]
    width = out_ref.shape[1] // 4
    for dy in range(4):
        at = pl.ds(pl.multiple_of(((y - dy) & 3) * width, 128), width)
        place_pair(chunk_refs[2 * dy][...], chunk_refs[2 * dy + 1][...], z_low, at, out_ref, None)


def join_two(place, chunks, fronts):
    _, rows, cols = fronts.shape
    return pl.pallas_call(
        join_two_kernel,
        grid=(1,),
        in_specs=[
            SMEM,
            *[pl.BlockSpec(chunk.shape, lambda i: (0, 0)) for chunk in chunks],
            pl.BlockSpec(memory_space=pl.ANY),
        ],
        out_specs=pl.BlockSpec((None, rows, cols), lambda i: (1, 0, 0)),
        out_shape=jax.ShapeDtypeStruct(fronts.shape, bf16),
        input_output_aliases={9: 0},
        compiler_params=params(24),
        name="join_two",
    )(place, *chunks, fronts)


def ring(shape, move):
    pairs = []
    for i in range(shape[0] * shape[1]):
        a, b = divmod(i, shape[1])
        c, d = (a + move[0]) % shape[0], b ^ move[1]
        pairs.append((i, c * shape[1] + d))
    return pairs


def spread(value, axes):
    moved = {}
    for move in ((2, 1), (2, 0), (1, 1), (3, 1), (1, 0), (3, 0), (0, 1)):
        moved[move] = lax.ppermute(value, axes, ring((4, 2), move))
    moved[0, 0] = value
    return [moved[a, b] for a in range(4) for b in range(2)]


def turn_pairs():
    pairs = []
    for i in range(128):
        rest, c = divmod(i, 2)
        rest, zh = divmod(rest, 2)
        rest, x = divmod(rest, 4)
        y, zl = divmod(rest, 2)
        pairs.append((i, (((x * 2 + zh) * 4 + y) * 2 + zl) * 2 + c))
    return pairs


def per_device(resident, memory, previous, inverse_part, pair_coupling):
    rows = memory.shape[1]
    cols = resident.shape[1]
    width = cols // 8
    past = lax.axis_index("y") * 2 + lax.axis_index("zl")
    place = jnp.stack([lax.axis_index(name) for name in ("x", "zh", "c", "y", "zl")]).astype(jnp.int32)
    priors = lax.dynamic_slice_in_dim(previous, past * width, width, 2).transpose(0, 2, 1)
    coupling = jnp.tile(pair_coupling, (width // ORB, rows // ORB))

    def scatter(partial):
        return lax.all_to_all(partial.reshape(8, width, rows), PASTS, 0, 0, tiled=True)

    parts = scatter(first_product(memory, resident))
    front_one, energy = first_solve(parts, priors[0], inverse_part[0], coupling)
    whole_one = lax.all_gather(front_one, PASTS, axis=0, tiled=True)
    turned = lax.ppermute(energy, ALL, turn_pairs())
    own = spread(turned, ("x", "zh"))
    other = [lax.ppermute(chunk, "c", [(0, 1), (1, 0)]) for chunk in own]
    parts = scatter(second_product(place, memory, own + other, resident))
    front_two = second_solve(parts, priors[1], inverse_part[1])
    chunks = spread(front_two, PASTS)
    return join_two(place, chunks, join_one(whole_one))


def solution(mesh):
    fine = Mesh(mesh.devices.reshape(4, 2, 4, 2, 2), ALL)
    in_specs = (P(PASTS, SECONDS), P(None, None, PASTS), P(None, None, SECONDS), P(), P())
    out_specs = P(None, None, SECONDS)
    return jax.shard_map(
        per_device, mesh=fine, in_specs=in_specs, out_specs=out_specs, check_vma=False
    )
```

time: 155 us -> 157 us (1.013)
  blocking collectives: 73.5 us -> 21.4 us
  starting transfers between devices: 14.5 us -> 45.3 us
  between operations: 0.13 us -> 13.6 us
  waiting for transfers between devices: 24.8 us -> 33.3 us
  Pallas kernels: 21.1 us -> 24.1 us
  local copies, waits for them, and re-layouts: 20.2 us -> 17.7 us
    all_to_all x2 -> x0, blocking collectives: 53.6 us -> none  [the longest x1 34.2 us: per_device(): own = lax.all_to_all(both, 'x', 0, 0, tiled=True)]
    ppermute x3 -> x23, starting transfers between devices: 4.31 us -> 39.2 us  [the longest x14 35.9 us: spread(): moved[move] = lax.ppermute(value, axes, ring((4, 2), move))]
    ppermute x3 -> x23, waiting for transfers between devices: 4.91 us -> 26.2 us  [the longest x14 25.4 us: spread(): moved[move] = lax.ppermute(value, axes, ring((4, 2), move))]
    all_to_all x1 -> x0, waiting for transfers between devices: 12.7 us -> none  [per_device(): front_one = lax.all_to_all(copies, PASTS, 0, 0, tiled=True)]
    all_to_all x1 -> x0, starting transfers between devices: 4.25 us -> none  [per_device(): front_one = lax.all_to_all(copies, PASTS, 0, 0, tiled=True)]
    unnamed x23 -> x43, local copies, waits for them, and re-layouts: 11.3 us -> 8.26 us
    pallas_call x1, Pallas kernels: 6.71 us -> 8.48 us  [first_product(): pl.pallas_call(first_product_kernel, grid=(cols // tile,), in_specs=[pl.B...]
    pallas_call x1 -> x2, Pallas kernels: 3.35 us -> 3.41 us  [the longest x1 2.02 us: join_two(): pl.pallas_call(join_two_kernel, grid=(1,), in_specs=[SMEM, *[pl.BlockSpec...]
  transfers between devices with their start and end apart: 5 -> 25, of which waited for: 4 -> 11; matrix products, arithmetic and copies ran while one was open for 7% -> 7% of each run, Pallas kernels for 1% -> 8%
where the time goes in v2:
time: 157 us; the launch traced here: 155 us
  starting transfers between devices  45.3 us (29%)
  waiting for transfers between devices  33.3 us (21%)
  Pallas kernels  24.1 us (15%)
  blocking collectives  21.4 us (14%)
  local copies, waits for them, and re-layouts  17.7 us (11%)
  between operations  13.6 us (9%)
    ppermute x14, starting transfers between devices, spread(): moved[move] = lax.ppermute(value, axes, ring((4, 2), move))  35.9 us
    ppermute x14, waiting for transfers between devices, spread(): moved[move] = lax.ppermute(value, axes, ring((4, 2), move))  25.4 us
    all_to_all x1, blocking collectives, scatter(): lax.all_to_all(partial.reshape(8, width, rows), PASTS, 0, 0, tiled=True)  21.4 us
    pallas_call x1, Pallas kernels, second_product(): pl.pallas_call(second_product_kernel, grid=(cols // tile,), in_specs=[SME...  10 us
    pallas_call x1, Pallas kernels, first_product(): pl.pallas_call(first_product_kernel, grid=(cols // tile,), in_specs=[pl.B...  8.48 us
    unnamed x43, local copies, waits for them, and re-layouts  8.26 us
    all_to_all x1, waiting for transfers between devices, scatter(): lax.all_to_all(partial.reshape(8, width, rows), PASTS, 0, 0, tiled=True)  7.11 us
    all_to_all x1, starting transfers between devices, scatter(): lax.all_to_all(partial.reshape(8, width, rows), PASTS, 0, 0, tiled=True)  6.04 us
  transfers between devices with their start and end apart: 25, of which 11 were waited for; matrix products, arithmetic and copies ran while one was open for 7% of the time, Pallas kernels for 8%

profile of v2, /device:TPU:0, one launch (start us, length us, event | category | flops | bytes accessed | tf_op | source)
XLA Modules:
  0.0 155.3 jit_solution(5483089796502523461)
XLA Ops:
  6.5 8.5 %first_product.1 = bf16[1536,384]{1,0:T(8,128)(2,1)} custom-call(bf16[2,384,3072]{2,1,0:T(8,128)(2,1)} %memory_ref.3, bf16[3072,1536]{1,0:T(8,128)(2,1)} %refs_16_.1), custom_call_target="tpu_custom_call" | custom-call | tf_op jit(solution)/shard_map/first_product/pallas_call | solution.py:34
  15.0 6.0 %all-to-all-start = ((bf16[8,192,384]{2,1,0:T(8,128)(2,1)}), bf16[8,192,384]{2,1,0:T(8,128)(2,1)S(1)}, u32[]{:S(2)}, u32[]{:S(2)}) async-start(bf16[8,192,384]{2,1,0:T(8,128)(2,1)} %bitcast.17), calls=%async_computation | async-start | bytes 2359296 | tf_op jit(solution)/shard_map/all_to_all | solution.py:253
  21.1 0.9 constant_dynamic-slice_fusion
  22.1 1.9 %copy.9 = bf16[2,384,192]{1,2,0:T(8,128)(2,1)} copy(bf16[2,384,192]{2,1,0:T(8,128)(2,1)} %constant_dynamic-slice_fusion) | data formatting | bytes 589824
  24.0 1.3 tile.4
  25.2 2.5 %tile.10.coupling_ref = f32[192,384]{1,0:T(8,128)} reshape(f32[6,32,12,32]{3,2,1,0:T(8,128)} %tile.4) | data formatting | bytes 589824 | tf_op jit(solution)/shard_map/tile | solution.py:250
  27.8 1.8 %slice_bitcast_fusion.2 = (bf16[192,384]{1,0:T(8,128)(2,1)}, bf16[192,384]{1,0:T(8,128)(2,1)}) fusion(bf16[2,192,384]{2,1,0:T(8,128)(2,1)} %bitcast.18), kind=kLoop, calls=%fused_computation.2 | loop fusion | bytes 589824 | tf_op jit(solution)/shard_map/squeeze | solution.py:262
  29.5 2.3 %slice_bitcast_fusion = (f32[384,384]{1,0:T(8,128)}, f32[384,384]{1,0:T(8,128)}) fusion(f32[2,384,384]{2,1,0:T(8,128)} %param.8), kind=kLoop, calls=%fused_computation | loop fusion | bytes 2359296 | tf_op jit(solution)/shard_map/squeeze | solution.py:262
  31.9 7.1 %all-to-all-done.parts_ref = bf16[8,192,384]{2,1,0:T(8,128)(2,1)S(1)} async-done(((bf16[8,192,384]{2,1,0:T(8,128)(2,1)}), bf16[8,192,384]{2,1,0:T(8,128)(2,1)S(1)}, u32[]{:S(2)}, u32[]{:S(2)}) %all-to-all-start) | async-done | bytes 1179680 | tf_op jit(solution)/shard_map/all_to_all | solution.py:253
  39.0 1.1 copy-done.2
  40.0 1.0 copy-done.3
  41.0 0.9 copy-done.6
  41.9 1.3 first_solve.1
  43.2 0.6 copy-done.7
  43.8 0.7 copy-done.9
  44.5 1.6 %collective-permute-start = (bf16[192,384]{1,0:T(8,128)(2,1)}, bf16[192,384]{1,0:T(8,128)(2,1)S(1)}, u32[]{:S(2)}, u32[]{:S(2)}) collective-permute-start(bf16[192,384]{1,0:T(8,128)(2,1)} %copy-done.9), channel_id=1, source_target_pairs={{0,0},{1,1},{2,16},{3,17},{4,32},{5,33},{6,48},{7,49},{8,64},{9,65... | collective-permute-start | bytes 442376 | tf_op jit(solution)/shard_map/ppermute | solution.py:258
  46.1 18.3 %collective-permute-start.7 = (bf16[192,384]{1,0:T(8,128)(2,1)S(1)}, bf16[192,384]{1,0:T(8,128)(2,1)S(1)}, u32[]{:S(2)}, u32[]{:S(2)}) collective-permute-start(bf16[192,384]{1,0:T(8,128)(2,1)S(1)} %collective-permute-done.refs_0_), channel_id=1, source_target_pairs={{0,14},{2,12},{4,2},{6,0},{8,6},{10,4},{12,10},{14,8},{1,15},{3,13... | collective-permute-start | bytes 442376 | tf_op jit(solution)/shard_map/ppermute | solution.py:227
  64.3 3.6 %collective-permute-start.4 = (bf16[192,384]{1,0:T(8,128)(2,1)S(1)}, bf16[192,384]{1,0:T(8,128)(2,1)S(1)}, u32[]{:S(2)}, u32[]{:S(2)}) collective-permute-start(bf16[192,384]{1,0:T(8,128)(2,1)S(1)} %collective-permute-done.refs_0_), channel_id=1, source_target_pairs={{0,8},{2,10},{4,12},{6,14},{8,0},{10,2},{12,4},{14,6},{1,9},{3,11}... | collective-permute-start | bytes 442376 | tf_op jit(solution)/shard_map/ppermute | solution.py:227
  68.0 4.4 %collective-permute-start.3 = (bf16[192,384]{1,0:T(8,128)(2,1)S(1)}, bf16[192,384]{1,0:T(8,128)(2,1)S(1)}, u32[]{:S(2)}, u32[]{:S(2)}) collective-permute-start(bf16[192,384]{1,0:T(8,128)(2,1)S(1)} %collective-permute-done.refs_0_), channel_id=1, source_target_pairs={{0,6},{2,4},{4,10},{6,8},{8,14},{10,12},{12,2},{14,0},{1,7},{3,5},... | collective-permute-start | bytes 442376 | tf_op jit(solution)/shard_map/ppermute | solution.py:227
  72.3 5.3 %collective-permute-done.6.refs_6_ = bf16[192,384]{1,0:T(8,128)(2,1)S(1)} collective-permute-done((bf16[192,384]{1,0:T(8,128)(2,1)S(1)}, bf16[192,384]{1,0:T(8,128)(2,1)S(1)}, u32[]{:S(2)}, u32[]{:S(2)}) %collective-permute-start.6) | collective-permute-done | bytes 147488 | tf_op jit(solution)/shard_map/ppermute | solution.py:227
  77.8 0.5 collective-permute-start.14
  78.3 2.6 %collective-permute-done.3.refs_3_ = bf16[192,384]{1,0:T(8,128)(2,1)S(1)} collective-permute-done((bf16[192,384]{1,0:T(8,128)(2,1)S(1)}, bf16[192,384]{1,0:T(8,128)(2,1)S(1)}, u32[]{:S(2)}, u32[]{:S(2)}) %collective-permute-start.3) | collective-permute-done | bytes 147488 | tf_op jit(solution)/shard_map/ppermute | solution.py:227
  80.9 0.4 collective-permute-done.2.refs_2_
  81.4 10.9 %collective-permute-done.1.refs_1_ = bf16[192,384]{1,0:T(8,128)(2,1)} collective-permute-done((bf16[192,384]{1,0:T(8,128)(2,1)S(1)}, bf16[192,384]{1,0:T(8,128)(2,1)}, u32[]{:S(2)}, u32[]{:S(2)}) %collective-permute-start.1) | collective-permute-done | bytes 147488 | tf_op jit(solution)/shard_map/ppermute | solution.py:227
  92.3 0.5 collective-permute-start.10
  92.8 0.1 copy-done.18
  93.0 0.6 copy-done.19
  93.6 0.5 collective-permute-start.9
  94.1 0.6 stack.23.place_ref
  94.8 0.7 collective-permute-done.9.refs_9_
  95.5 10.0 %second_product.1 = bf16[1536,384]{1,0:T(8,128)(2,1)} custom-call(s32[5]{0:T(128)} %stack.23.place_ref, bf16[2,384,3072]{2,1,0:T(8,128)(2,1)} %memory_ref.3, bf16[192,384]{1,0:T(8,128)(2,1)} %copy-done.10, bf16[192,384]{1,0:T(8,128)(2,1)} %collective-permute-done.1.refs_1_, bf16[192,384]{1,0:T(8,128)(2,1)} %copy-done.17, bf16[192,384]{1,0:T(8,128)(2,1)} %copy-done.16, ...), custom_call_target="tpu_custom_call" | custom-call | tf_op jit(solution)/shard_map/second_product/pallas_call | solution.py:81
  105.6 21.4 %all_to_all.10.parts_ref = bf16[8,192,384]{2,1,0:T(8,128)(2,1)S(1)} all-to-all(bf16[8,192,384]{2,1,0:T(8,128)(2,1)} %bitcast.16), channel_id=1, replica_groups=mesh['y'=4,'zl'=2,'x'=4,'zh'=2,'c'=2] {'y','zl'}, dimensions={0} | all-to-all | bytes 2359296 | tf_op jit(solution)/shard_map/all_to_all | solution.py:253
  127.0 0.9 second_solve.1.refs_0_
  127.9 1.7 %collective-permute-start.22 = (bf16[192,384]{1,0:T(8,128)(2,1)S(1)}, bf16[192,384]{1,0:T(8,128)(2,1)S(1)}, u32[]{:S(2)}, u32[]{:S(2)}) collective-permute-start(bf16[192,384]{1,0:T(8,128)(2,1)S(1)} %second_solve.1.refs_0_), channel_id=1, source_target_pairs={{0,112},{16,96},{32,16},{48,0},{64,48},{80,32},{96,80},{112,64},{1... | collective-permute-start | bytes 442376 | tf_op jit(solution)/shard_map/ppermute | solution.py:227
  129.6 0.2 collective-permute-start.21
  129.8 3.1 %collective-permute-start.20 = (bf16[192,384]{1,0:T(8,128)(2,1)S(1)}, bf16[192,384]{1,0:T(8,128)(2,1)S(1)}, u32[]{:S(2)}, u32[]{:S(2)}) collective-permute-start(bf16[192,384]{1,0:T(8,128)(2,1)S(1)} %second_solve.1.refs_0_), channel_id=1, source_target_pairs={{0,80},{16,64},{32,112},{48,96},{64,16},{80,0},{96,48},{112,32},{1... | collective-permute-start | bytes 442376 | tf_op jit(solution)/shard_map/ppermute | solution.py:227
  132.9 1.5 collective-permute-start.19
  134.4 1.6 %collective-permute-start.18 = (bf16[192,384]{1,0:T(8,128)(2,1)S(1)}, bf16[192,384]{1,0:T(8,128)(2,1)S(1)}, u32[]{:S(2)}, u32[]{:S(2)}) collective-permute-start(bf16[192,384]{1,0:T(8,128)(2,1)S(1)} %second_solve.1.refs_0_), channel_id=1, source_target_pairs={{0,48},{16,32},{32,80},{48,64},{64,112},{80,96},{96,16},{112,0},{1... | collective-permute-start | bytes 442376 | tf_op jit(solution)/shard_map/ppermute | solution.py:227
  136.0 0.3 collective-permute-done.22.refs_7_
  136.3 0.6 collective-permute-start.17
  136.9 1.4 collective-permute-done.21.refs_6_
  138.3 1.0 collective-permute-start.16
  139.3 1.3 copy-done.4
  140.6 1.4 join_one.1.refs_8_
  142.0 0.3 collective-permute-done.19.refs_4_
  142.3 1.8 %collective-permute-done.18.refs_3_ = bf16[192,384]{1,0:T(8,128)(2,1)S(1)} collective-permute-done((bf16[192,384]{1,0:T(8,128)(2,1)S(1)}, bf16[192,384]{1,0:T(8,128)(2,1)S(1)}, u32[]{:S(2)}, u32[]{:S(2)}) %collective-permute-start.18) | collective-permute-done | bytes 147488 | tf_op jit(solution)/shard_map/ppermute | solution.py:227
  144.1 2.3 %collective-permute-done.17.refs_2_ = bf16[192,384]{1,0:T(8,128)(2,1)S(1)} collective-permute-done((bf16[192,384]{1,0:T(8,128)(2,1)S(1)}, bf16[192,384]{1,0:T(8,128)(2,1)S(1)}, u32[]{:S(2)}, u32[]{:S(2)}) %collective-permute-start.17) | collective-permute-done | bytes 147488 | tf_op jit(solution)/shard_map/ppermute | solution.py:227
  146.4 2.0 %join_two.1 = bf16[2,384,1536]{2,1,0:T(8,128)(2,1)} custom-call(s32[5]{0:T(128)S(1)} %copy-done.8, bf16[192,384]{1,0:T(8,128)(2,1)S(1)} %second_solve.1.refs_0_, bf16[192,384]{1,0:T(8,128)(2,1)S(1)} %collective-permute-done.16.refs_1_, bf16[192,384]{1,0:T(8,128)(2,1)S(1)} %collective-permute-done.17.refs_2_, ...), custom_call_target="tpu_custom_call", output_to_operand_aliasing={{}: (9, {})} | custom-call | tf_op jit(solution)/shard_map/join_two/pallas_call | solution.py:199
  (59 shorter events, 0.4 us)
Async XLA Ops:
  6.5 14.6 %copy-start = (bf16[2,384,1536]{2,1,0:T(8,128)(2,1)S(1)}, bf16[2,384,1536]{2,1,0:T(8,128)(2,1)}, u32[]{:S(2)}) copy-start(bf16[2,384,1536]{2,1,0:T(8,128)(2,1)} %param.7) | copy-start | bytes 7077892
  15.0 8.9 %copy-start.20 = (f32[32,32]{1,0:T(8,128)S(1)}, f32[32,32]{1,0:T(8,128)}, u32[]{:S(2)}) copy-start(f32[32,32]{1,0:T(8,128)} %param.9) | copy-start | bytes 12292
  15.0 23.9 %all-to-all-start = ((bf16[8,192,384]{2,1,0:T(8,128)(2,1)}), bf16[8,192,384]{2,1,0:T(8,128)(2,1)S(1)}, u32[]{:S(2)}, u32[]{:S(2)}) async-start(bf16[8,192,384]{2,1,0:T(8,128)(2,1)} %bitcast.17), calls=%async_computation | async-start | bytes 2359296 | tf_op jit(solution)/shard_map/all_to_all | solution.py:253
  21.1 118.3 %all-gather.2.cloned.1.call-start = ((), (), s32[]{:S(2)}) async-start(), calls=%async_computation.2 | async-start | bytes 1327104 | tf_op jit(solution)/shard_map/all_gather | solution.py:257
  39.0 1.1 copy-start.2
  40.0 1.0 copy-start.3
  41.0 0.9 copy-start.6
  43.2 0.7 copy-start.7
  43.8 0.7 copy-start.9
  44.5 1.6 %collective-permute-start = (bf16[192,384]{1,0:T(8,128)(2,1)}, bf16[192,384]{1,0:T(8,128)(2,1)S(1)}, u32[]{:S(2)}, u32[]{:S(2)}) collective-permute-start(bf16[192,384]{1,0:T(8,128)(2,1)} %copy-done.9), channel_id=1, source_target_pairs={{0,0},{1,1},{2,16},{3,17},{4,32},{5,33},{6,48},{7,49},{8,64},{9,65... | collective-permute-start | bytes 442376 | tf_op jit(solution)/shard_map/ppermute | solution.py:258
  46.1 49.4 %copy-start.10 = (bf16[192,384]{1,0:T(8,128)(2,1)}, bf16[192,384]{1,0:T(8,128)(2,1)S(1)}, u32[]{:S(2)}) copy-start(bf16[192,384]{1,0:T(8,128)(2,1)S(1)} %collective-permute-done.refs_0_) | copy-start | bytes 442372
  46.1 21.9 %collective-permute-start.8 = (bf16[192,384]{1,0:T(8,128)(2,1)S(1)}, bf16[192,384]{1,0:T(8,128)(2,1)S(1)}, u32[]{:S(2)}, u32[]{:S(2)}) collective-permute-start(bf16[192,384]{1,0:T(8,128)(2,1)S(1)} %collective-permute-done.refs_0_), channel_id=1, source_target_pairs={{0,1},{1,0},{2,3},{3,2},{4,5},{5,4},{6,7},{7,6},{8,9},{9,8},{10,11... | collective-permute-start | bytes 442376 | tf_op jit(solution)/shard_map/ppermute | solution.py:260
  46.1 26.2 %collective-permute-start.7 = (bf16[192,384]{1,0:T(8,128)(2,1)S(1)}, bf16[192,384]{1,0:T(8,128)(2,1)S(1)}, u32[]{:S(2)}, u32[]{:S(2)}) collective-permute-start(bf16[192,384]{1,0:T(8,128)(2,1)S(1)} %collective-permute-done.refs_0_), channel_id=1, source_target_pairs={{0,14},{2,12},{4,2},{6,0},{8,6},{10,4},{12,10},{14,8},{1,15},{3,13... | collective-permute-start | bytes 442376 | tf_op jit(solution)/shard_map/ppermute | solution.py:227
  64.3 13.3 %collective-permute-start.6 = (bf16[192,384]{1,0:T(8,128)(2,1)S(1)}, bf16[192,384]{1,0:T(8,128)(2,1)S(1)}, u32[]{:S(2)}, u32[]{:S(2)}) collective-permute-start(bf16[192,384]{1,0:T(8,128)(2,1)S(1)} %collective-permute-done.refs_0_), channel_id=1, source_target_pairs={{0,12},{2,14},{4,0},{6,2},{8,4},{10,6},{12,8},{14,10},{1,13},{3,15... | collective-permute-start | bytes 442376 | tf_op jit(solution)/shard_map/ppermute | solution.py:227
  64.3 13.3 %collective-permute-start.5 = (bf16[192,384]{1,0:T(8,128)(2,1)S(1)}, bf16[192,384]{1,0:T(8,128)(2,1)S(1)}, u32[]{:S(2)}, u32[]{:S(2)}) collective-permute-start(bf16[192,384]{1,0:T(8,128)(2,1)S(1)} %collective-permute-done.refs_0_), channel_id=1, source_target_pairs={{0,10},{2,8},{4,14},{6,12},{8,2},{10,0},{12,6},{14,4},{1,11},{3,9}... | collective-permute-start | bytes 442376 | tf_op jit(solution)/shard_map/ppermute | solution.py:227
  64.3 13.4 %collective-permute-start.4 = (bf16[192,384]{1,0:T(8,128)(2,1)S(1)}, bf16[192,384]{1,0:T(8,128)(2,1)S(1)}, u32[]{:S(2)}, u32[]{:S(2)}) collective-permute-start(bf16[192,384]{1,0:T(8,128)(2,1)S(1)} %collective-permute-done.refs_0_), channel_id=1, source_target_pairs={{0,8},{2,10},{4,12},{6,14},{8,0},{10,2},{12,4},{14,6},{1,9},{3,11}... | collective-permute-start | bytes 442376 | tf_op jit(solution)/shard_map/ppermute | solution.py:227
  67.9 27.5 %copy-start.11 = (bf16[192,384]{1,0:T(8,128)(2,1)}, bf16[192,384]{1,0:T(8,128)(2,1)S(1)}, u32[]{:S(2)}) copy-start(bf16[192,384]{1,0:T(8,128)(2,1)S(1)} %collective-permute-done.8.refs_8_) | copy-start | bytes 442372
  68.0 12.9 %collective-permute-start.3 = (bf16[192,384]{1,0:T(8,128)(2,1)S(1)}, bf16[192,384]{1,0:T(8,128)(2,1)S(1)}, u32[]{:S(2)}, u32[]{:S(2)}) collective-permute-start(bf16[192,384]{1,0:T(8,128)(2,1)S(1)} %collective-permute-done.refs_0_), channel_id=1, source_target_pairs={{0,6},{2,4},{4,10},{6,8},{8,14},{10,12},{12,2},{14,0},{1,7},{3,5},... | collective-permute-start | bytes 442376 | tf_op jit(solution)/shard_map/ppermute | solution.py:227
  72.3 23.2 %copy-start.12 = (bf16[192,384]{1,0:T(8,128)(2,1)}, bf16[192,384]{1,0:T(8,128)(2,1)S(1)}, u32[]{:S(2)}) copy-start(bf16[192,384]{1,0:T(8,128)(2,1)S(1)} %collective-permute-done.7.refs_7_) | copy-start | bytes 442372
  72.3 9.0 %collective-permute-start.2 = (bf16[192,384]{1,0:T(8,128)(2,1)S(1)}, bf16[192,384]{1,0:T(8,128)(2,1)S(1)}, u32[]{:S(2)}, u32[]{:S(2)}) collective-permute-start(bf16[192,384]{1,0:T(8,128)(2,1)S(1)} %collective-permute-done.refs_0_), channel_id=1, source_target_pairs={{0,4},{2,6},{4,8},{6,10},{8,12},{10,14},{12,0},{14,2},{1,5},{3,7},... | collective-permute-start | bytes 442376 | tf_op jit(solution)/shard_map/ppermute | solution.py:227
  77.6 17.9 %copy-start.13 = (bf16[192,384]{1,0:T(8,128)(2,1)}, bf16[192,384]{1,0:T(8,128)(2,1)S(1)}, u32[]{:S(2)}) copy-start(bf16[192,384]{1,0:T(8,128)(2,1)S(1)} %collective-permute-done.6.refs_6_) | copy-start | bytes 442372
  77.6 14.7 %collective-permute-start.1 = (bf16[192,384]{1,0:T(8,128)(2,1)S(1)}, bf16[192,384]{1,0:T(8,128)(2,1)}, u32[]{:S(2)}, u32[]{:S(2)}) collective-permute-start(bf16[192,384]{1,0:T(8,128)(2,1)S(1)} %collective-permute-done.refs_0_), channel_id=1, source_target_pairs={{0,2},{2,0},{4,6},{6,4},{8,10},{10,8},{12,14},{14,12},{1,3},{3,1},... | collective-permute-start | bytes 442376 | tf_op jit(solution)/shard_map/ppermute | solution.py:227
  77.7 17.8 %copy-start.14 = (bf16[192,384]{1,0:T(8,128)(2,1)}, bf16[192,384]{1,0:T(8,128)(2,1)S(1)}, u32[]{:S(2)}) copy-start(bf16[192,384]{1,0:T(8,128)(2,1)S(1)} %collective-permute-done.5.refs_5_) | copy-start | bytes 442372
  77.7 14.7 %collective-permute-start.15 = (bf16[192,384]{1,0:T(8,128)(2,1)S(1)}, bf16[192,384]{1,0:T(8,128)(2,1)S(1)}, u32[]{:S(2)}, u32[]{:S(2)}) collective-permute-start(bf16[192,384]{1,0:T(8,128)(2,1)S(1)} %collective-permute-done.7.refs_7_), channel_id=1, source_target_pairs={{0,1},{1,0},{2,3},{3,2},{4,5},{5,4},{6,7},{7,6},{8,9},{9,8},{10,11... | collective-permute-start | bytes 442376 | tf_op jit(solution)/shard_map/ppermute | solution.py:260
  77.8 17.7 %copy-start.15 = (bf16[192,384]{1,0:T(8,128)(2,1)}, bf16[192,384]{1,0:T(8,128)(2,1)S(1)}, u32[]{:S(2)}) copy-start(bf16[192,384]{1,0:T(8,128)(2,1)S(1)} %collective-permute-done.4.refs_4_) | copy-start | bytes 442372
  77.8 15.1 %collective-permute-start.14 = (bf16[192,384]{1,0:T(8,128)(2,1)S(1)}, bf16[192,384]{1,0:T(8,128)(2,1)S(1)}, u32[]{:S(2)}, u32[]{:S(2)}) collective-permute-start(bf16[192,384]{1,0:T(8,128)(2,1)S(1)} %collective-permute-done.6.refs_6_), channel_id=1, source_target_pairs={{0,1},{1,0},{2,3},{3,2},{4,5},{5,4},{6,7},{7,6},{8,9},{9,8},{10,11... | collective-permute-start | bytes 442376 | tf_op jit(solution)/shard_map/ppermute | solution.py:260
  80.9 14.6 %copy-start.16 = (bf16[192,384]{1,0:T(8,128)(2,1)}, bf16[192,384]{1,0:T(8,128)(2,1)S(1)}, u32[]{:S(2)}) copy-start(bf16[192,384]{1,0:T(8,128)(2,1)S(1)} %collective-permute-done.3.refs_3_) | copy-start | bytes 442372
  80.9 13.9 %collective-permute-start.13 = (bf16[192,384]{1,0:T(8,128)(2,1)S(1)}, bf16[192,384]{1,0:T(8,128)(2,1)}, u32[]{:S(2)}, u32[]{:S(2)}) collective-permute-start(bf16[192,384]{1,0:T(8,128)(2,1)S(1)} %collective-permute-done.5.refs_5_), channel_id=1, source_target_pairs={{0,1},{1,0},{2,3},{3,2},{4,5},{5,4},{6,7},{7,6},{8,9},{9,8},{10,11... | collective-permute-start | bytes 442376 | tf_op jit(solution)/shard_map/ppermute | solution.py:260
  81.3 14.2 %copy-start.17 = (bf16[192,384]{1,0:T(8,128)(2,1)}, bf16[192,384]{1,0:T(8,128)(2,1)S(1)}, u32[]{:S(2)}) copy-start(bf16[192,384]{1,0:T(8,128)(2,1)S(1)} %collective-permute-done.2.refs_2_) | copy-start | bytes 442372
  81.3 13.5 %collective-permute-start.12 = (bf16[192,384]{1,0:T(8,128)(2,1)S(1)}, bf16[192,384]{1,0:T(8,128)(2,1)}, u32[]{:S(2)}, u32[]{:S(2)}) collective-permute-start(bf16[192,384]{1,0:T(8,128)(2,1)S(1)} %collective-permute-done.4.refs_4_), channel_id=1, source_target_pairs={{0,1},{1,0},{2,3},{3,2},{4,5},{5,4},{6,7},{7,6},{8,9},{9,8},{10,11... | collective-permute-start | bytes 442376 | tf_op jit(solution)/shard_map/ppermute | solution.py:260
  92.3 2.5 %collective-permute-start.11 = (bf16[192,384]{1,0:T(8,128)(2,1)S(1)}, bf16[192,384]{1,0:T(8,128)(2,1)}, u32[]{:S(2)}, u32[]{:S(2)}) collective-permute-start(bf16[192,384]{1,0:T(8,128)(2,1)S(1)} %collective-permute-done.3.refs_3_), channel_id=1, source_target_pairs={{0,1},{1,0},{2,3},{3,2},{4,5},{5,4},{6,7},{7,6},{8,9},{9,8},{10,11... | collective-permute-start | bytes 442376 | tf_op jit(solution)/shard_map/ppermute | solution.py:260
  92.3 0.7 copy-start.18
  92.3 2.5 %collective-permute-start.10 = (bf16[192,384]{1,0:T(8,128)(2,1)S(1)}, bf16[192,384]{1,0:T(8,128)(2,1)}, u32[]{:S(2)}, u32[]{:S(2)}) collective-permute-start(bf16[192,384]{1,0:T(8,128)(2,1)S(1)} %collective-permute-done.2.refs_2_), channel_id=1, source_target_pairs={{0,1},{1,0},{2,3},{3,2},{4,5},{5,4},{6,7},{7,6},{8,9},{9,8},{10,11... | collective-permute-start | bytes 442376 | tf_op jit(solution)/shard_map/ppermute | solution.py:260
  93.0 0.7 copy-start.19
  93.6 1.9 %collective-permute-start.9 = (bf16[192,384]{1,0:T(8,128)(2,1)}, bf16[192,384]{1,0:T(8,128)(2,1)}, u32[]{:S(2)}, u32[]{:S(2)}) collective-permute-start(bf16[192,384]{1,0:T(8,128)(2,1)} %collective-permute-done.1.refs_1_), channel_id=1, source_target_pairs={{0,1},{1,0},{2,3},{3,2},{4,5},{5,4},{6,7},{7,6},{8,9},{9,8},{10,11... | collective-permute-start | bytes 442376 | tf_op jit(solution)/shard_map/ppermute | solution.py:260
  105.6 21.4 %copy-start.1 = (f32[384,384]{1,0:T(8,128)S(1)}, f32[384,384]{1,0:T(8,128)}, u32[]{:S(2)}) copy-start(f32[384,384]{1,0:T(8,128)} %get-tuple-element.9.inverse_ref) | copy-start | bytes 1769476
  105.6 21.4 %copy-start.5 = (bf16[192,384]{1,0:T(8,128)(2,1)S(1)}, bf16[192,384]{1,0:T(8,128)(2,1)}, u32[]{:S(2)}) copy-start(bf16[192,384]{1,0:T(8,128)(2,1)} %get-tuple-element.11.prior_ref) | copy-start | bytes 442372
  127.0 19.5 %copy-start.8 = (s32[5]{0:T(128)S(1)}, s32[5]{0:T(128)}, u32[]{:S(2)}) copy-start(s32[5]{0:T(128)} %stack.23.place_ref) | copy-start | bytes 64
  127.9 8.4 %collective-permute-start.22 = (bf16[192,384]{1,0:T(8,128)(2,1)S(1)}, bf16[192,384]{1,0:T(8,128)(2,1)S(1)}, u32[]{:S(2)}, u32[]{:S(2)}) collective-permute-start(bf16[192,384]{1,0:T(8,128)(2,1)S(1)} %second_solve.1.refs_0_), channel_id=1, source_target_pairs={{0,112},{16,96},{32,16},{48,0},{64,48},{80,32},{96,80},{112,64},{1... | collective-permute-start | bytes 442376 | tf_op jit(solution)/shard_map/ppermute | solution.py:227
  129.6 8.8 %collective-permute-start.21 = (bf16[192,384]{1,0:T(8,128)(2,1)S(1)}, bf16[192,384]{1,0:T(8,128)(2,1)S(1)}, u32[]{:S(2)}, u32[]{:S(2)}) collective-permute-start(bf16[192,384]{1,0:T(8,128)(2,1)S(1)} %second_solve.1.refs_0_), channel_id=1, source_target_pairs={{0,96},{16,112},{32,0},{48,16},{64,32},{80,48},{96,64},{112,80},{1... | collective-permute-start | bytes 442376 | tf_op jit(solution)/shard_map/ppermute | solution.py:227
  129.8 12.2 %collective-permute-start.20 = (bf16[192,384]{1,0:T(8,128)(2,1)S(1)}, bf16[192,384]{1,0:T(8,128)(2,1)S(1)}, u32[]{:S(2)}, u32[]{:S(2)}) collective-permute-start(bf16[192,384]{1,0:T(8,128)(2,1)S(1)} %second_solve.1.refs_0_), channel_id=1, source_target_pairs={{0,80},{16,64},{32,112},{48,96},{64,16},{80,0},{96,48},{112,32},{1... | collective-permute-start | bytes 442376 | tf_op jit(solution)/shard_map/ppermute | solution.py:227
  132.9 9.4 %collective-permute-start.19 = (bf16[192,384]{1,0:T(8,128)(2,1)S(1)}, bf16[192,384]{1,0:T(8,128)(2,1)S(1)}, u32[]{:S(2)}, u32[]{:S(2)}) collective-permute-start(bf16[192,384]{1,0:T(8,128)(2,1)S(1)} %second_solve.1.refs_0_), channel_id=1, source_target_pairs={{0,64},{16,80},{32,96},{48,112},{64,0},{80,16},{96,32},{112,48},{1... | collective-permute-start | bytes 442376 | tf_op jit(solution)/shard_map/ppermute | solution.py:227
  134.4 9.7 %collective-permute-start.18 = (bf16[192,384]{1,0:T(8,128)(2,1)S(1)}, bf16[192,384]{1,0:T(8,128)(2,1)S(1)}, u32[]{:S(2)}, u32[]{:S(2)}) collective-permute-start(bf16[192,384]{1,0:T(8,128)(2,1)S(1)} %second_solve.1.refs_0_), channel_id=1, source_target_pairs={{0,48},{16,32},{32,80},{48,64},{64,112},{80,96},{96,16},{112,0},{1... | collective-permute-start | bytes 442376 | tf_op jit(solution)/shard_map/ppermute | solution.py:227
  136.3 10.1 %collective-permute-start.17 = (bf16[192,384]{1,0:T(8,128)(2,1)S(1)}, bf16[192,384]{1,0:T(8,128)(2,1)S(1)}, u32[]{:S(2)}, u32[]{:S(2)}) collective-permute-start(bf16[192,384]{1,0:T(8,128)(2,1)S(1)} %second_solve.1.refs_0_), channel_id=1, source_target_pairs={{0,32},{16,48},{32,64},{48,80},{64,96},{80,112},{96,0},{112,16},{1... | collective-permute-start | bytes 442376 | tf_op jit(solution)/shard_map/ppermute | solution.py:227
  138.3 8.1 %collective-permute-start.16 = (bf16[192,384]{1,0:T(8,128)(2,1)S(1)}, bf16[192,384]{1,0:T(8,128)(2,1)S(1)}, u32[]{:S(2)}, u32[]{:S(2)}) collective-permute-start(bf16[192,384]{1,0:T(8,128)(2,1)S(1)} %second_solve.1.refs_0_), channel_id=1, source_target_pairs={{0,16},{16,0},{32,48},{48,32},{64,80},{80,64},{96,112},{112,96},{1... | collective-permute-start | bytes 442376 | tf_op jit(solution)/shard_map/ppermute | solution.py:227
  139.3 1.3 copy-start.4
Sparse Core Ops, SparseCore 0:
  44.6 50.6 all-gather.1

commit v3 on v0

v3 whole, which is shorter than its diff:
```python
import functools

import jax
import jax.numpy as jnp
from jax import lax
from jax.experimental import pallas as pl
from jax.experimental.pallas import tpu as pltpu
from jax.sharding import Mesh, PartitionSpec as P

step_size = 0.5
ORB = 32
f32 = jnp.float32
bf16 = jnp.bfloat16
PASTS = ("y", "zl")
SECONDS = ("x", "zh", "c")
ALL = PASTS + SECONDS
SWAP = [(0, 1), (1, 0)]
X, ZH, C, Y, ZL = range(5)


VMEM = pl.BlockSpec(memory_space=pltpu.VMEM)
SMEM = pl.BlockSpec(memory_space=pltpu.SMEM)


def in_hbm(array):
    return pltpu.with_memory_space_constraint(array, pltpu.HBM)


def params(megabytes):
    return pltpu.CompilerParams(vmem_limit_bytes=megabytes << 20)


def cost(flops, nbytes):
    return pl.CostEstimate(flops=flops, bytes_accessed=nbytes, transcendentals=0)


def whole(shape):
    return pl.BlockSpec(shape, lambda i, place: (0,) * len(shape))


def placed_call(kernel, place, args, in_specs, out_specs, out_shape, name, limit, estimate, grid=1, scratch=(), aliases=None):
    return pl.pallas_call(
        kernel,
        grid_spec=pltpu.PrefetchScalarGridSpec(
            num_scalar_prefetch=1,
            grid=(grid,),
            in_specs=in_specs,
            out_specs=out_specs,
            scratch_shapes=list(scratch),
        ),
        out_shape=out_shape,
        input_output_aliases=aliases or {},
        compiler_params=params(limit),
        cost_estimate=cost(*estimate),
        name=name,
    )(place, *args)


def store_shares(place_ref, turned_ref, out_refs):
    width = out_refs[0].shape[0]
    for k, out_ref in enumerate(out_refs):
        share = ((place_ref[Y] & 1) ^ (k >> 1)) * 2 + (place_ref[ZL] ^ (k & 1))
        out_ref[...] = turned_ref[pl.ds(pl.multiple_of(share * width, width), width), :]


def first_half_kernel(place_ref, lhs_ref, resident_ref, *refs):
    out_refs, turned_ref = refs[:4], refs[4]
    step, tile = pl.program_id(0), resident_ref.shape[1]
    product = jnp.dot(lhs_ref[...], resident_ref[...], preferred_element_type=f32)
    turned_ref[pl.ds(pl.multiple_of(step * tile, tile), tile), :] = product.T.astype(bf16)

    @pl.when(step == pl.num_programs(0) - 1)
    def _():
        store_shares(place_ref, turned_ref, out_refs)


def first_half(place, memory, resident, far):
    _, rows, depth = memory.shape
    cols = resident.shape[1]
    width = cols // 8
    tile = 256
    steps = cols // 2 // tile
    return placed_call(
        first_half_kernel,
        place,
        (memory, resident),
        [
            pl.BlockSpec((None, rows, depth), lambda i, place: (0, 0, 0)),
            pl.BlockSpec((depth, tile), lambda i, place: (0, ((place[Y] >> 1) ^ far) * steps + i)),
        ],
        [whole((width, rows))] * 4,
        [jax.ShapeDtypeStruct((width, rows), bf16)] * 4,
        "first_half",
        16,
        (rows * depth * cols, depth * cols + 2 * rows * depth),
        grid=steps,
        scratch=[pltpu.VMEM((cols // 2, rows), bf16)],
    )


def second_half_kernel(far, place_ref, lhs_ref, resident_ref, *refs):
    out_refs, turned_ref = refs[:4], refs[4]
    cols = resident_ref.shape[1] // 2
    at = pl.ds(pl.multiple_of(((place_ref[Y] >> 1) ^ far) * cols, cols), cols)
    product = jnp.dot(lhs_ref[...], resident_ref[:, at], preferred_element_type=f32)
    turned_ref[...] = product.T.astype(bf16)
    store_shares(place_ref, turned_ref, out_refs)


def second_half(place, lhs, resident, far):
    rows, depth = lhs.shape
    cols = resident.shape[1]
    width = cols // 8
    return pl.pallas_call(
        functools.partial(second_half_kernel, far),
        in_specs=[SMEM, VMEM, VMEM],
        out_specs=[VMEM] * 4,
        out_shape=[jax.ShapeDtypeStruct((width, rows), bf16)] * 4,
        scratch_shapes=[pltpu.VMEM((cols // 2, rows), bf16)],
        compiler_params=params(6),
        cost_estimate=cost(rows * depth * cols, 4 * width * rows),
        name="second_half",
    )(place, lhs, resident)


def product(half, place, lhs, resident):
    far = half(place, lhs, resident, 1)
    near = half(place, lhs, resident, 0)
    moves = {}
    for k in range(4):
        moves[2 + (k >> 1), k & 1] = far[k]
        moves[k >> 1, k & 1] = near[k]
    return moves


def bring_kernel(place_ref, resident_ref, memory_ref, previous_ref, resident_out, memory_out, one_out, two_out, prior_ref, turned_ref, sems):
    width, rows = one_out.shape
    cols = pl.ds(pl.multiple_of(place_ref[Y] * 2 * width, 128), 2 * width)
    copies = [
        pltpu.make_async_copy(previous_ref.at[:, :, cols], prior_ref, sems.at[0]),
        pltpu.make_async_copy(memory_ref.at[1], memory_out, sems.at[1]),
        pltpu.make_async_copy(resident_ref, resident_out, sems.at[2]),
    ]
    for copy in copies:
        copy.start()
    copies[0].wait()
    for front, out_ref in enumerate((one_out, two_out)):
        turned_ref[...] = prior_ref[front].astype(f32).T
        share = turned_ref[pl.ds(pl.multiple_of(place_ref[ZL] * width, width), width), :]
        out_ref[...] = share.astype(bf16)
    copies[1].wait()
    copies[2].wait()


def bring(place, resident, memory, previous):
    _, rows, depth = memory.shape
    cols = resident.shape[1]
    width = cols // 8
    anywhere = pl.BlockSpec(memory_space=pltpu.HBM)
    return pl.pallas_call(
        bring_kernel,
        in_specs=[SMEM, anywhere, anywhere, anywhere],
        out_specs=[VMEM] * 4,
        out_shape=[
            jax.ShapeDtypeStruct(resident.shape, bf16),
            jax.ShapeDtypeStruct((rows, depth), bf16),
            jax.ShapeDtypeStruct((width, rows), bf16),
            jax.ShapeDtypeStruct((width, rows), bf16),
        ],
        scratch_shapes=[
            pltpu.VMEM((2, rows, 2 * width), bf16),
            pltpu.VMEM((2 * width, rows), f32),
            pltpu.SemaphoreType.DMA((3,)),
        ],
        compiler_params=params(6),
        cost_estimate=cost(0, 2 * depth * (rows + cols)),
        name="bring",
    )(place, resident, memory, previous)


def place_pair(own, other, first, at, out_ref, base_ref):
    near, far = own.astype(f32), other.astype(f32)
    low = jnp.where(first == 0, near, far)
    high = jnp.where(first == 0, far, near)
    pair = jnp.concatenate([low, high], axis=0).T
    if base_ref is not None:
        pair = pair + base_ref[:, at].astype(f32)
    out_ref[:, at] = pair.astype(bf16)


def next_memory_kernel(place_ref, memory_ref, *refs):
    pair_refs, out_ref = refs[:8], refs[8]
    half = memory_ref.shape[1] // 2
    width = half // 4
    for side in range(2):
        for dx in range(4):
            pair = pair_refs[side * 4 + dx]
            share = ((place_ref[X] - dx) & 3) ^ place_ref[Y]
            start = (place_ref[C] ^ side) * half + share * width
            at = pl.ds(pl.multiple_of(start, 128), width)
            place_pair(pair[0], pair[1], place_ref[ZH], at, out_ref, memory_ref)


def next_memory(place, memory, pairs):
    rows, depth = memory.shape
    return pl.pallas_call(
        next_memory_kernel,
        in_specs=[SMEM] + [VMEM] * 9,
        out_specs=VMEM,
        out_shape=jax.ShapeDtypeStruct((rows, depth), bf16),
        compiler_params=params(6),
        cost_estimate=cost(rows * depth, 6 * rows * depth),
        name="next_memory",
    )(place, memory, *pairs)


def solve_into(part_refs, prior_ref, inverse_ref):
    summed = part_refs[0][...].astype(f32)
    for part_ref in part_refs[1:]:
        summed = summed + part_ref[...].astype(f32)
    source = prior_ref[...].astype(f32) - step_size * summed
    mixed = lax.dot_general(
        source,
        inverse_ref[...],
        (((1,), (1,)), ((), ())),
        precision=lax.Precision.HIGHEST,
        preferred_element_type=f32,
    )
    return (source + mixed).astype(bf16)


def flipped(values):
    rows, cols = values.shape
    strips = []
    pad = jnp.zeros((128 - ORB, 128), f32)
    for s in range(rows // ORB):
        pieces = []
        for q in range(cols // 128):
            block = values[s * ORB : (s + 1) * ORB, q * 128 : (q + 1) * 128]
            turned = jnp.concatenate([block, pad], axis=0).T
            piece = turned[:ORB]
            for t in range(1, 128 // ORB):
                piece = piece + pltpu.roll(turned[t * ORB : (t + 1) * ORB], t * ORB, 1)
            pieces.append(piece)
        strips.append(jnp.concatenate(pieces, axis=1))
    return jnp.concatenate(strips, axis=0)


def first_solve_kernel(place_ref, *refs):
    front_ref, energy_ref = refs[11:]
    front = solve_into(refs[:8], refs[8], refs[9])
    front_ref[...] = front
    values = front.astype(f32)
    mirror = flipped(values)
    rows, cols = values.shape
    coupling = jnp.tile(refs[10][...], (rows // ORB, cols // 128))
    energy_ref[...] = (mirror * mirror * values * coupling).astype(bf16)


def second_solve_kernel(place_ref, *refs):
    refs[10][...] = solve_into(refs[:8], refs[8], refs[9])


def solve(kernel, front, place, parts, prior, inverse, extra, outputs, name):
    width, rows = prior.shape
    return placed_call(
        kernel,
        place,
        (*parts, prior, inverse, *extra),
        [
            *[whole(array.shape) for array in (*parts, prior)],
            pl.BlockSpec((None, rows, rows), lambda i, place: (front, 0, 0)),
            *[whole(array.shape) for array in extra],
        ],
        [whole((width, rows))] * outputs,
        [jax.ShapeDtypeStruct((width, rows), bf16)] * outputs,
        name,
        10,
        (12 * rows * rows * width, 24 * rows * width),
    )


def join_one_kernel(place_ref, *refs):
    pair_refs, out_ref = refs[:4], refs[4]
    width = out_ref.shape[1] // 4
    for dy in range(4):
        at = pl.ds(pl.multiple_of(((place_ref[Y] - dy) & 3) * width, 128), width)
        place_pair(pair_refs[dy][0], pair_refs[dy][1], place_ref[ZL], at, out_ref, None)


def join_one(place, pairs, rows, cols):
    return placed_call(
        join_one_kernel,
        place,
        pairs,
        [whole(pair.shape) for pair in pairs],
        pl.BlockSpec((None, rows, cols), lambda i, place: (0, 0, 0)),
        jax.ShapeDtypeStruct((2, rows, cols), bf16),
        "join_one",
        10,
        (rows * cols, 4 * rows * cols),
    )


def join_two_kernel(place_ref, *refs):
    chunk_refs, out_ref = refs[:8], refs[9]
    width = out_ref.shape[1] // 4
    for dy in range(4):
        at = pl.ds(pl.multiple_of(((place_ref[Y] - dy) & 3) * width, 128), width)
        own, other = chunk_refs[2 * dy][...], chunk_refs[2 * dy + 1][...]
        place_pair(own, other, place_ref[ZL], at, out_ref, None)


def join_two(place, chunks, fronts):
    _, rows, cols = fronts.shape
    return placed_call(
        join_two_kernel,
        place,
        (*chunks, fronts),
        [*[whole(chunk.shape) for chunk in chunks], pl.BlockSpec(memory_space=pl.ANY)],
        pl.BlockSpec((None, rows, cols), lambda i, place: (1, 0, 0)),
        jax.ShapeDtypeStruct(fronts.shape, bf16),
        "join_two",
        10,
        (rows * cols, 4 * rows * cols),
        aliases={9: 0},
    )


def move(value, target):
    pairs = []
    for i in range(128):
        rest, c = divmod(i, 2)
        rest, zh = divmod(rest, 2)
        rest, x = divmod(rest, 4)
        y, zl = divmod(rest, 2)
        y, zl, x, zh = target(y, zl, x, zh)
        pairs.append((i, (((y * 2 + zl) * 4 + x) * 2 + zh) * 2 + c))
    return lax.ppermute(value, ALL, pairs)


def turn(flip):
    return lambda y, zl, x, zh: (x, zh, x ^ y, zl ^ flip)


def scatter(shares):
    parts = []
    for dy, dz in ((2, 1), (2, 0), (3, 1), (3, 0), (1, 1), (1, 0), (0, 1)):
        parts.append(move(shares[dy, dz], lambda y, zl, x, zh: (y ^ dy, zl ^ dz, x, zh)))
    return [*parts, shares[0, 0]]


def spread_pairs(pair, axis):
    pairs = {0: pair}
    for d in (2, 1, 3):
        pairs[d] = lax.ppermute(pair, axis, [(i, (i + d) % 4) for i in range(4)])
    return [pairs[d] for d in range(4)]


def spread_chunks(value):
    chunks = {(0, 0): value}
    for dy, dz in ((2, 1), (2, 0), (1, 1), (3, 1), (1, 0), (3, 0), (0, 1)):
        chunks[dy, dz] = move(value, lambda y, zl, x, zh: ((y + dy) % 4, zl ^ dz, x, zh))
    return [chunks[dy, dz] for dy in range(4) for dz in range(2)]


def per_device(resident, memory, previous, inverse_part, pair_coupling):
    rows, cols = memory.shape[1], resident.shape[1]
    place = jnp.stack([lax.axis_index(name) for name in ("x", "zh", "c", "y", "zl")]).astype(jnp.int32)
    coupling = jnp.tile(pair_coupling, (1, 128 // ORB))

    resident, memory, previous = in_hbm(resident), in_hbm(memory), in_hbm(previous)
    shares = product(first_half, place, memory, resident)
    place, shares[0, 0] = lax.optimization_barrier((place, shares[0, 0]))
    resident, memory, prior_one, prior_two = bring(place, resident, memory, previous)
    parts = scatter(shares)
    front_one, energy = solve(
        first_solve_kernel, 0, place, parts, prior_one, inverse_part, [coupling], 2, "first_solve"
    )
    own = spread_pairs(jnp.stack([move(energy, turn(0)), move(energy, turn(1))]), "x")
    other = [lax.ppermute(pair, "c", SWAP) for pair in own]
    ones = spread_pairs(jnp.stack([front_one, lax.ppermute(front_one, "zl", SWAP)]), "y")
    own, other, ones = lax.optimization_barrier((own, other, ones))
    lhs = next_memory(place, memory, own + other)
    parts = scatter(product(second_half, place, lhs, resident))
    (front_two,) = solve(
        second_solve_kernel, 1, place, parts, prior_two, inverse_part, [], 1, "second_solve"
    )
    chunks = spread_chunks(front_two)
    return join_two(place, chunks, join_one(place, ones, rows, cols))


def solution(mesh):
    fine = Mesh(mesh.devices.reshape(4, 2, 4, 2, 2), ALL)
    in_specs = (P(PASTS, SECONDS), P(None, None, PASTS), P(None, None, SECONDS), P(), P())
    out_specs = P(None, None, SECONDS)
    return jax.shard_map(
        per_device, mesh=fine, in_specs=in_specs, out_specs=out_specs, check_vma=False
    )
```

time: 407 us -> 123 us (0.30)
  waiting for transfers between devices: 267 us -> 37.7 us
  local copies, waits for them, and re-layouts: 83.9 us -> 0.2 us
  starting transfers between devices: 0.27 us -> 52.9 us
  matrix products: 32.8 us -> 0 us
  Pallas kernels: 0 us -> 31.2 us
  between operations: 13.1 us -> 0.16 us
  other arithmetic: 9.31 us -> 0.07 us
    psum x2 -> x0, waiting for transfers between devices: 147 us -> none  [advance(): lax.psum(partial_value.astype(jnp.bfloat16), 'past').astype(jnp.float32)]
    all_gather x1 -> x0, waiting for transfers between devices: 119 us -> none  [per_device(): whole_row = lax.all_gather(energy_one, 'second', axis=1, tiled=True)]
    ppermute x0 -> x34, starting transfers between devices: none -> 52.9 us  [the longest x23 37.5 us: move(): return lax.ppermute(value, ALL, pairs)]
    convert_element_type x3 -> x0, local copies, waits for them, and re-layouts: 49.3 us -> none  [per_device(): orbital_flip(gathered, orbitals).astype(jnp.float32)]
    ppermute x0 -> x34, waiting for transfers between devices: none -> 37.7 us  [the longest x23 21.4 us: move(): return lax.ppermute(value, ALL, pairs)]
    dot_general x4 -> x0, matrix products: 32.8 us -> none  [the longest x2 19.9 us: advance(): jnp.dot(memory_row, resident, preferred_element_type=jnp.float32)]
    pallas_call x0 -> x10, Pallas kernels: none -> 31.2 us  [the longest x6 19.1 us: placed_call(): pl.pallas_call(kernel, grid_spec=pltpu.PrefetchScalarGridSpec(num_scalar_...]
    reshape x2 -> x0, local copies, waits for them, and re-layouts: 12.6 us -> none  [the longest x1 7.74 us: orbital_flip(): return blocks.transpose(0, 3, 2, 1).reshape(row_count, col_count)]
  transfers between devices with their start and end apart: 3 -> 34, of which waited for: 3 -> 16; matrix products, arithmetic and copies ran while one was open for 3% -> 0% of each run, Pallas kernels for 0% -> 13%
where the time goes in v3:
time: 123 us; the launch traced here: 122 us
  starting transfers between devices  52.9 us (43%)
  waiting for transfers between devices  37.7 us (31%)
  Pallas kernels  31.2 us (25%)
    ppermute x23, starting transfers between devices, move(): return lax.ppermute(value, ALL, pairs)  37.5 us
    ppermute x23, waiting for transfers between devices, move(): return lax.ppermute(value, ALL, pairs)  21.4 us
    pallas_call x6, Pallas kernels, placed_call(): pl.pallas_call(kernel, grid_spec=pltpu.PrefetchScalarGridSpec(num_scalar_...  19.1 us
    ppermute x6, starting transfers between devices, spread_pairs(): pairs[d] = lax.ppermute(pair, axis, [(i, (i + d) % 4) for i in range(4)])  15.1 us
    ppermute x6, waiting for transfers between devices, spread_pairs(): pairs[d] = lax.ppermute(pair, axis, [(i, (i + d) % 4) for i in range(4)])  12.9 us
    pallas_call x2, Pallas kernels, second_half(): pl.pallas_call(functools.partial(second_half_kernel, far), in_specs=[SMEM...  5.35 us
    pallas_call x1, Pallas kernels, bring(): pl.pallas_call(bring_kernel, in_specs=[SMEM, anywhere, anywhere, anywhere...  5.17 us
  transfers between devices with their start and end apart: 34, of which 16 were waited for; matrix products, arithmetic and copies ran while one was open for 0% of the time, Pallas kernels for 13%

profile of v3, /device:TPU:0, one launch (start us, length us, event | category | flops | bytes accessed | tf_op | source)
XLA Modules:
  0.0 122.3 jit_solution(10468048318507740939)
XLA Ops:
  0.1 5.9 %first_half.2 = (bf16[192,384]{1,0:T(8,128)(2,1)S(1)}, bf16[192,384]{1,0:T(8,128)(2,1)S(1)}, bf16[192,384]{1,0:T(8,128)(2,1)S(1)}, bf16[192,384]{1,0:T(8,128)(2,1)S(1)}) custom-call(s32[5]{0:T(128)S(1)} %stack.41.place_ref, bf16[2,384,3072]{2,1,0:T(8,128)(2,1)} %lhs_ref.3, bf16[3072,1536]{1,0:T(8,128)(2,1)} %resident_ref.5), custom_call_target="tpu_custom_call" | custom-call | flops 1811939328 | bytes 7077888 | tf_op jit(solution)/shard_map/first_half/pallas_call | solution.py:42
  6.0 3.1 %collective-permute-start.4 = (bf16[192,384]{1,0:T(8,128)(2,1)S(1)}, bf16[192,384]{1,0:T(8,128)(2,1)S(1)}, u32[]{:S(2)}, u32[]{:S(2)}) collective-permute-start(bf16[192,384]{1,0:T(8,128)(2,1)S(1)} %get-tuple-element.48), channel_id=1, source_target_pairs={{0,48},{1,49},{2,50},{3,51},{4,52},{5,53},{6,54},{7,55},{8,56},{9,... | collective-permute-start | bytes 442376 | tf_op jit(solution)/shard_map/ppermute | solution.py:339
  9.1 0.4 collective-permute-start.5
  9.8 5.9 %first_half.3 = (bf16[192,384]{1,0:T(8,128)(2,1)S(1)}, bf16[192,384]{1,0:T(8,128)(2,1)S(1)}, bf16[192,384]{1,0:T(8,128)(2,1)S(1)}, bf16[192,384]{1,0:T(8,128)(2,1)S(1)}) custom-call(s32[5]{0:T(128)S(1)} %stack.41.place_ref, bf16[2,384,3072]{2,1,0:T(8,128)(2,1)} %lhs_ref.3, bf16[3072,1536]{1,0:T(8,128)(2,1)} %resident_ref.5), custom_call_target="tpu_custom_call" | custom-call | flops 1811939328 | bytes 7077888 | tf_op jit(solution)/shard_map/first_half/pallas_call | solution.py:42
  15.7 4.5 %collective-permute-start = (bf16[192,384]{1,0:T(8,128)(2,1)S(1)}, bf16[192,384]{1,0:T(8,128)(2,1)S(1)}, u32[]{:S(2)}, u32[]{:S(2)}) collective-permute-start(bf16[192,384]{1,0:T(8,128)(2,1)S(1)} %get-tuple-element.44), channel_id=1, source_target_pairs={{0,80},{1,81},{2,82},{3,83},{4,84},{5,85},{6,86},{7,87},{8,88},{9,... | collective-permute-start | bytes 442376 | tf_op jit(solution)/shard_map/ppermute | solution.py:339
  20.2 0.3 collective-permute-start.1
  20.5 2.6 %collective-permute-start.2 = (bf16[192,384]{1,0:T(8,128)(2,1)S(1)}, bf16[192,384]{1,0:T(8,128)(2,1)S(1)}, u32[]{:S(2)}, u32[]{:S(2)}) collective-permute-start(bf16[192,384]{1,0:T(8,128)(2,1)S(1)} %get-tuple-element.46), channel_id=1, source_target_pairs={{0,112},{1,113},{2,114},{3,115},{4,116},{5,117},{6,118},{7,119},{8... | collective-permute-start | bytes 442376 | tf_op jit(solution)/shard_map/ppermute | solution.py:339
  23.1 0.5 collective-permute-start.3
  23.8 5.2 %bring.1 = (bf16[3072,1536]{1,0:T(8,128)(2,1)S(1)}, bf16[384,3072]{1,0:T(8,128)(2,1)S(1)}, bf16[192,384]{1,0:T(8,128)(2,1)S(1)}, bf16[192,384]{1,0:T(8,128)(2,1)S(1)}) custom-call(s32[5]{0:T(128)S(1)} %stack.41.place_ref, bf16[3072,1536]{1,0:T(8,128)(2,1)} %resident_ref.5, bf16[2,384,3072]{2,1,0:T(8,128)(2,1)} %lhs_ref.3, bf16[2,384,1536]{2,1,0:T(8,128)(2,1)} %previous_ref.1), custom_call_target="tpu_custom_call" | custom-call | bytes 11796480 | tf_op jit(solution)/shard_map/bring/pallas_call | solution.py:160
  29.0 0.8 collective-permute-done.2.refs_2_
  29.7 3.4 %collective-permute-done.3.refs_3_ = bf16[192,384]{1,0:T(8,128)(2,1)S(1)} collective-permute-done((bf16[192,384]{1,0:T(8,128)(2,1)S(1)}, bf16[192,384]{1,0:T(8,128)(2,1)S(1)}, u32[]{:S(2)}, u32[]{:S(2)}) %collective-permute-start.3) | collective-permute-done | bytes 147488 | tf_op jit(solution)/shard_map/ppermute | solution.py:339
  33.1 1.8 %first_solve.1 = (bf16[192,384]{1,0:T(8,128)(2,1)S(1)}, bf16[192,384]{1,0:T(8,128)(2,1)S(1)}) custom-call(s32[5]{0:T(128)S(1)} %stack.41.place_ref, bf16[192,384]{1,0:T(8,128)(2,1)S(1)} %collective-permute-done.refs_0_, bf16[192,384]{1,0:T(8,128)(2,1)S(1)} %collective-permute-done.1.refs_1_, bf16[192,384]{1,0:T(8,128)(2,1)S(1)} %collective-permute-done.2.refs_2_, ...), custom_call_target="tpu_custom_call" | custom-call | flops 339738624 | bytes 1769472 | tf_op jit(solution)/shard_map/first_solve/pallas_call | solution.py:42
  35.3 3.8 %collective-permute-start.8 = (bf16[192,384]{1,0:T(8,128)(2,1)S(1)}, bf16[192,384]{1,0:T(8,128)(2,1)S(1)}, u32[]{:S(2)}, u32[]{:S(2)}) collective-permute-start(bf16[192,384]{1,0:T(8,128)(2,1)S(1)} %get-tuple-element.53), channel_id=1, source_target_pairs={{0,2},{1,3},{2,18},{3,19},{4,38},{5,39},{6,54},{7,55},{8,74},{9,75... | collective-permute-start | bytes 442376 | tf_op jit(solution)/shard_map/ppermute | solution.py:339
  39.0 0.7 collective-permute-start.7
  39.7 2.1 %collective-permute-done.16 = bf16[192,384]{1,0:T(8,128)(2,1)S(1)} collective-permute-done((bf16[192,384]{1,0:T(8,128)(2,1)S(1)}, bf16[192,384]{1,0:T(8,128)(2,1)S(1)}, u32[]{:S(2)}, u32[]{:S(2)}) %collective-permute-start.16) | collective-permute-done | bytes 147488 | tf_op jit(solution)/shard_map/ppermute | solution.py:382
  41.8 6.8 %collective-permute-start.19 = (bf16[2,192,384]{2,1,0:T(8,128)(2,1)S(1)}, bf16[2,192,384]{2,1,0:T(8,128)(2,1)S(1)}, u32[]{:S(2)}, u32[]{:S(2)}) collective-permute-start(bf16[2,192,384]{2,1,0:T(8,128)(2,1)S(1)} %pad_maximum_fusion.1.refs_0_), channel_id=1, source_target_pairs={{0,96},{32,0},{64,32},{96,64},{1,97},{33,1},{65,33},{97,65},{2,98}... | collective-permute-start | bytes 884744 | tf_op jit(solution)/shard_map/ppermute | solution.py:356
  48.5 0.8 collective-permute-start.18
  49.4 6.5 %collective-permute-start.11 = (bf16[2,192,384]{2,1,0:T(8,128)(2,1)S(1)}, bf16[2,192,384]{2,1,0:T(8,128)(2,1)S(1)}, u32[]{:S(2)}, u32[]{:S(2)}) collective-permute-start(bf16[2,192,384]{2,1,0:T(8,128)(2,1)S(1)} %pad_maximum_fusion.refs_0_), channel_id=1, source_target_pairs={{0,12},{4,0},{8,4},{12,8},{1,13},{5,1},{9,5},{13,9},{2,14},{6,2},{... | collective-permute-start | bytes 884744 | tf_op jit(solution)/shard_map/ppermute | solution.py:356
  55.9 1.0 collective-permute-start.9
  56.9 3.6 %collective-permute-done.19.refs_3_ = bf16[2,192,384]{2,1,0:T(8,128)(2,1)S(1)} collective-permute-done((bf16[2,192,384]{2,1,0:T(8,128)(2,1)S(1)}, bf16[2,192,384]{2,1,0:T(8,128)(2,1)S(1)}, u32[]{:S(2)}, u32[]{:S(2)}) %collective-permute-start.19) | collective-permute-done | bytes 294944 | tf_op jit(solution)/shard_map/ppermute | solution.py:356
  60.5 5.4 %collective-permute-done.11.refs_3_ = bf16[2,192,384]{2,1,0:T(8,128)(2,1)S(1)} collective-permute-done((bf16[2,192,384]{2,1,0:T(8,128)(2,1)S(1)}, bf16[2,192,384]{2,1,0:T(8,128)(2,1)S(1)}, u32[]{:S(2)}, u32[]{:S(2)}) %collective-permute-start.11) | collective-permute-done | bytes 294944 | tf_op jit(solution)/shard_map/ppermute | solution.py:356
  65.9 0.6 collective-permute-done.10.refs_2_
  66.5 3.1 %collective-permute-done.9.refs_1_ = bf16[2,192,384]{2,1,0:T(8,128)(2,1)S(1)} collective-permute-done((bf16[2,192,384]{2,1,0:T(8,128)(2,1)S(1)}, bf16[2,192,384]{2,1,0:T(8,128)(2,1)S(1)}, u32[]{:S(2)}, u32[]{:S(2)}) %collective-permute-start.9) | collective-permute-done | bytes 294944 | tf_op jit(solution)/shard_map/ppermute | solution.py:356
  69.8 1.4 %collective-permute-done.13.refs_5_ = bf16[2,192,384]{2,1,0:T(8,128)(2,1)S(1)} collective-permute-done((bf16[2,192,384]{2,1,0:T(8,128)(2,1)S(1)}, bf16[2,192,384]{2,1,0:T(8,128)(2,1)S(1)}, u32[]{:S(2)}, u32[]{:S(2)}) %collective-permute-start.13) | collective-permute-done | bytes 294944 | tf_op jit(solution)/shard_map/ppermute | solution.py:381
  71.1 1.6 %next_memory.1.lhs_ref = bf16[384,3072]{1,0:T(8,128)(2,1)S(1)} custom-call(s32[5]{0:T(128)S(1)} %stack.41.place_ref, bf16[384,3072]{1,0:T(8,128)(2,1)S(1)} %get-tuple-element.43.memory_ref, bf16[2,192,384]{2,1,0:T(8,128)(2,1)S(1)} %pad_maximum_fusion.refs_0_, bf16[2,192,384]{2,1,0:T(8,128)(2,1)S(1)} %collective-permute-done.9.refs_1_, ...), custom_call_target="tpu_custom_call" | custom-call | flops 1179648 | bytes 7077888 | tf_op jit(solution)/shard_map/next_memory/pallas_call | solution.py:206
  72.8 2.7 %second_half.3 = (bf16[192,384]{1,0:T(8,128)(2,1)S(1)}, bf16[192,384]{1,0:T(8,128)(2,1)S(1)}, bf16[192,384]{1,0:T(8,128)(2,1)S(1)}, bf16[192,384]{1,0:T(8,128)(2,1)S(1)}) custom-call(s32[5]{0:T(128)S(1)} %stack.41.place_ref, bf16[384,3072]{1,0:T(8,128)(2,1)S(1)} %next_memory.1.lhs_ref, bf16[3072,1536]{1,0:T(8,128)(2,1)S(1)} %get-tuple-element.63.resident_ref), custom_call_target="tpu_custom_call" | custom-call | flops 1811939328 | bytes 294912 | tf_op jit(solution)/shard_map/second_half/pallas_call | solution.py:114
  75.5 2.3 %collective-permute-start.25 = (bf16[192,384]{1,0:T(8,128)(2,1)S(1)}, bf16[192,384]{1,0:T(8,128)(2,1)S(1)}, u32[]{:S(2)}, u32[]{:S(2)}) collective-permute-start(bf16[192,384]{1,0:T(8,128)(2,1)S(1)} %get-tuple-element.69), channel_id=1, source_target_pairs={{0,32},{1,33},{2,34},{3,35},{4,36},{5,37},{6,38},{7,39},{8,40},{9,... | collective-permute-start | bytes 442376 | tf_op jit(solution)/shard_map/ppermute | solution.py:339
  77.9 1.1 collective-permute-start.26
  79.0 2.7 %second_half.2 = (bf16[192,384]{1,0:T(8,128)(2,1)S(1)}, bf16[192,384]{1,0:T(8,128)(2,1)S(1)}, bf16[192,384]{1,0:T(8,128)(2,1)S(1)}, bf16[192,384]{1,0:T(8,128)(2,1)S(1)}) custom-call(s32[5]{0:T(128)S(1)} %stack.41.place_ref, bf16[384,3072]{1,0:T(8,128)(2,1)S(1)} %next_memory.1.lhs_ref, bf16[3072,1536]{1,0:T(8,128)(2,1)S(1)} %get-tuple-element.63.resident_ref), custom_call_target="tpu_custom_call" | custom-call | flops 1811939328 | bytes 294912 | tf_op jit(solution)/shard_map/second_half/pallas_call | solution.py:114
  81.7 0.4 collective-permute-start.20
  82.1 3.6 %collective-permute-start.21 = (bf16[192,384]{1,0:T(8,128)(2,1)S(1)}, bf16[192,384]{1,0:T(8,128)(2,1)S(1)}, u32[]{:S(2)}, u32[]{:S(2)}) collective-permute-start(bf16[192,384]{1,0:T(8,128)(2,1)S(1)} %get-tuple-element.65), channel_id=1, source_target_pairs={{0,64},{1,65},{2,66},{3,67},{4,68},{5,69},{6,70},{7,71},{8,72},{9,... | collective-permute-start | bytes 442376 | tf_op jit(solution)/shard_map/ppermute | solution.py:339
  85.6 0.9 collective-permute-start.22
  86.6 2.9 %collective-permute-start.23 = (bf16[192,384]{1,0:T(8,128)(2,1)S(1)}, bf16[192,384]{1,0:T(8,128)(2,1)S(1)}, u32[]{:S(2)}, u32[]{:S(2)}) collective-permute-start(bf16[192,384]{1,0:T(8,128)(2,1)S(1)} %get-tuple-element.67), channel_id=1, source_target_pairs={{0,96},{1,97},{2,98},{3,99},{4,100},{5,101},{6,102},{7,103},{8,104... | collective-permute-start | bytes 442376 | tf_op jit(solution)/shard_map/ppermute | solution.py:339
  89.5 1.4 %collective-permute-done.20.refs_0_ = bf16[192,384]{1,0:T(8,128)(2,1)S(1)} collective-permute-done((bf16[192,384]{1,0:T(8,128)(2,1)S(1)}, bf16[192,384]{1,0:T(8,128)(2,1)S(1)}, u32[]{:S(2)}, u32[]{:S(2)}) %collective-permute-start.20) | collective-permute-done | bytes 147488 | tf_op jit(solution)/shard_map/ppermute | solution.py:339
  90.9 1.0 collective-permute-done.21.refs_1_
  91.9 3.7 %collective-permute-done.22.refs_2_ = bf16[192,384]{1,0:T(8,128)(2,1)S(1)} collective-permute-done((bf16[192,384]{1,0:T(8,128)(2,1)S(1)}, bf16[192,384]{1,0:T(8,128)(2,1)S(1)}, u32[]{:S(2)}, u32[]{:S(2)}) %collective-permute-start.22) | collective-permute-done | bytes 147488 | tf_op jit(solution)/shard_map/ppermute | solution.py:339
  95.6 2.5 %collective-permute-done.23.refs_3_ = bf16[192,384]{1,0:T(8,128)(2,1)S(1)} collective-permute-done((bf16[192,384]{1,0:T(8,128)(2,1)S(1)}, bf16[192,384]{1,0:T(8,128)(2,1)S(1)}, u32[]{:S(2)}, u32[]{:S(2)}) %collective-permute-start.23) | collective-permute-done | bytes 147488 | tf_op jit(solution)/shard_map/ppermute | solution.py:339
  98.1 1.4 %second_solve.1.refs_0_ = bf16[192,384]{1,0:T(8,128)(2,1)S(1)} custom-call(s32[5]{0:T(128)S(1)} %stack.41.place_ref, bf16[192,384]{1,0:T(8,128)(2,1)S(1)} %collective-permute-done.20.refs_0_, bf16[192,384]{1,0:T(8,128)(2,1)S(1)} %collective-permute-done.21.refs_1_, bf16[192,384]{1,0:T(8,128)(2,1)S(1)} %collective-permute-done.22.refs_2_, ...), custom_call_target="tpu_custom_call" | custom-call | flops 339738624 | bytes 1769472 | tf_op jit(solution)/shard_map/second_solve/pallas_call | solution.py:42
  99.6 2.7 %collective-permute-start.33 = (bf16[192,384]{1,0:T(8,128)(2,1)S(1)}, bf16[192,384]{1,0:T(8,128)(2,1)S(1)}, u32[]{:S(2)}, u32[]{:S(2)}) collective-permute-start(bf16[192,384]{1,0:T(8,128)(2,1)S(1)} %second_solve.1.refs_0_), channel_id=1, source_target_pairs={{0,112},{1,113},{2,114},{3,115},{4,116},{5,117},{6,118},{7,119},{8... | collective-permute-start | bytes 442376 | tf_op jit(solution)/shard_map/ppermute | solution.py:339
  102.3 2.4 %collective-permute-start.31 = (bf16[192,384]{1,0:T(8,128)(2,1)S(1)}, bf16[192,384]{1,0:T(8,128)(2,1)S(1)}, u32[]{:S(2)}, u32[]{:S(2)}) collective-permute-start(bf16[192,384]{1,0:T(8,128)(2,1)S(1)} %second_solve.1.refs_0_), channel_id=1, source_target_pairs={{0,80},{1,81},{2,82},{3,83},{4,84},{5,85},{6,86},{7,87},{8,88},{9,... | collective-permute-start | bytes 442376 | tf_op jit(solution)/shard_map/ppermute | solution.py:339
  104.6 1.5 %collective-permute-start.30 = (bf16[192,384]{1,0:T(8,128)(2,1)S(1)}, bf16[192,384]{1,0:T(8,128)(2,1)S(1)}, u32[]{:S(2)}, u32[]{:S(2)}) collective-permute-start(bf16[192,384]{1,0:T(8,128)(2,1)S(1)} %second_solve.1.refs_0_), channel_id=1, source_target_pairs={{0,64},{1,65},{2,66},{3,67},{4,68},{5,69},{6,70},{7,71},{8,72},{9,... | collective-permute-start | bytes 442376 | tf_op jit(solution)/shard_map/ppermute | solution.py:339
  106.2 2.6 %collective-permute-start.29 = (bf16[192,384]{1,0:T(8,128)(2,1)S(1)}, bf16[192,384]{1,0:T(8,128)(2,1)S(1)}, u32[]{:S(2)}, u32[]{:S(2)}) collective-permute-start(bf16[192,384]{1,0:T(8,128)(2,1)S(1)} %second_solve.1.refs_0_), channel_id=1, source_target_pairs={{0,48},{1,49},{2,50},{3,51},{4,52},{5,53},{6,54},{7,55},{8,56},{9,... | collective-permute-start | bytes 442376 | tf_op jit(solution)/shard_map/ppermute | solution.py:339
  108.8 6.3 %collective-permute-done.32.refs_6_ = bf16[192,384]{1,0:T(8,128)(2,1)S(1)} collective-permute-done((bf16[192,384]{1,0:T(8,128)(2,1)S(1)}, bf16[192,384]{1,0:T(8,128)(2,1)S(1)}, u32[]{:S(2)}, u32[]{:S(2)}) %collective-permute-start.32) | collective-permute-done | bytes 147488 | tf_op jit(solution)/shard_map/ppermute | solution.py:339
  115.1 0.9 collective-permute-start.27
  116.0 2.0 %join_one.1.refs_8_ = bf16[2,384,1536]{2,1,0:T(8,128)(2,1)} custom-call(s32[5]{0:T(128)S(1)} %stack.41.place_ref, bf16[2,192,384]{2,1,0:T(8,128)(2,1)S(1)} %pad_maximum_fusion.1.refs_0_, bf16[2,192,384]{2,1,0:T(8,128)(2,1)S(1)} %collective-permute-done.17.refs_1_, bf16[2,192,384]{2,1,0:T(8,128)(2,1)S(1)} %collective-permute-done.18.refs_2_, ...), custom_call_target="tpu_custom_call" | custom-call | flops 589824 | bytes 2359296 | tf_op jit(solution)/shard_map/join_one/pallas_call | solution.py:42
  118.0 1.1 collective-permute-done.28.refs_2_
  119.1 1.1 collective-permute-done.27.refs_1_
  120.2 2.0 %join_two.1 = bf16[2,384,1536]{2,1,0:T(8,128)(2,1)} custom-call(s32[5]{0:T(128)S(1)} %stack.41.place_ref, bf16[192,384]{1,0:T(8,128)(2,1)S(1)} %second_solve.1.refs_0_, bf16[192,384]{1,0:T(8,128)(2,1)S(1)} %collective-permute-done.27.refs_1_, bf16[192,384]{1,0:T(8,128)(2,1)S(1)} %collective-permute-done.28.refs_2_, ...), custom_call_target="tpu_custom_call", output_to_operand_aliasing={{}: (9, {})} | custom-call | flops 589824 | bytes 2359296 | tf_op jit(solution)/shard_map/join_two/pallas_call | solution.py:42
  (39 shorter events, 1.2 us)
Async XLA Ops:
  6.0 14.5 %collective-permute-start.4 = (bf16[192,384]{1,0:T(8,128)(2,1)S(1)}, bf16[192,384]{1,0:T(8,128)(2,1)S(1)}, u32[]{:S(2)}, u32[]{:S(2)}) collective-permute-start(bf16[192,384]{1,0:T(8,128)(2,1)S(1)} %get-tuple-element.48), channel_id=1, source_target_pairs={{0,48},{1,49},{2,50},{3,51},{4,52},{5,53},{6,54},{7,55},{8,56},{9,... | collective-permute-start | bytes 442376 | tf_op jit(solution)/shard_map/ppermute | solution.py:339
  9.1 14.0 %collective-permute-start.5 = (bf16[192,384]{1,0:T(8,128)(2,1)S(1)}, bf16[192,384]{1,0:T(8,128)(2,1)S(1)}, u32[]{:S(2)}, u32[]{:S(2)}) collective-permute-start(bf16[192,384]{1,0:T(8,128)(2,1)S(1)} %get-tuple-element.49), channel_id=1, source_target_pairs={{0,32},{1,33},{2,34},{3,35},{4,36},{5,37},{6,38},{7,39},{8,40},{9,... | collective-permute-start | bytes 442376 | tf_op jit(solution)/shard_map/ppermute | solution.py:339
  9.5 14.1 %copy-start.1 = (f32[32,32]{1,0:T(8,128)S(1)}, f32[32,32]{1,0:T(8,128)}, u32[]{:S(2)}) copy-start(f32[32,32]{1,0:T(8,128)} %param.9) | copy-start | bytes 12292
  9.5 19.4 %collective-permute-start.6 = (bf16[192,384]{1,0:T(8,128)(2,1)S(1)}, bf16[192,384]{1,0:T(8,128)(2,1)S(1)}, u32[]{:S(2)}, u32[]{:S(2)}) collective-permute-start(bf16[192,384]{1,0:T(8,128)(2,1)S(1)} %get-tuple-element.50), channel_id=1, source_target_pairs={{0,16},{1,17},{2,18},{3,19},{4,20},{5,21},{6,22},{7,23},{8,24},{9,... | collective-permute-start | bytes 442376 | tf_op jit(solution)/shard_map/ppermute | solution.py:339
  15.7 13.3 %collective-permute-start = (bf16[192,384]{1,0:T(8,128)(2,1)S(1)}, bf16[192,384]{1,0:T(8,128)(2,1)S(1)}, u32[]{:S(2)}, u32[]{:S(2)}) collective-permute-start(bf16[192,384]{1,0:T(8,128)(2,1)S(1)} %get-tuple-element.44), channel_id=1, source_target_pairs={{0,80},{1,81},{2,82},{3,83},{4,84},{5,85},{6,86},{7,87},{8,88},{9,... | collective-permute-start | bytes 442376 | tf_op jit(solution)/shard_map/ppermute | solution.py:339
  20.2 8.8 %collective-permute-start.1 = (bf16[192,384]{1,0:T(8,128)(2,1)S(1)}, bf16[192,384]{1,0:T(8,128)(2,1)S(1)}, u32[]{:S(2)}, u32[]{:S(2)}) collective-permute-start(bf16[192,384]{1,0:T(8,128)(2,1)S(1)} %get-tuple-element.45), channel_id=1, source_target_pairs={{0,64},{1,65},{2,66},{3,67},{4,68},{5,69},{6,70},{7,71},{8,72},{9,... | collective-permute-start | bytes 442376 | tf_op jit(solution)/shard_map/ppermute | solution.py:339
  20.5 9.2 %collective-permute-start.2 = (bf16[192,384]{1,0:T(8,128)(2,1)S(1)}, bf16[192,384]{1,0:T(8,128)(2,1)S(1)}, u32[]{:S(2)}, u32[]{:S(2)}) collective-permute-start(bf16[192,384]{1,0:T(8,128)(2,1)S(1)} %get-tuple-element.46), channel_id=1, source_target_pairs={{0,112},{1,113},{2,114},{3,115},{4,116},{5,117},{6,118},{7,119},{8... | collective-permute-start | bytes 442376 | tf_op jit(solution)/shard_map/ppermute | solution.py:339
  23.1 10.0 %collective-permute-start.3 = (bf16[192,384]{1,0:T(8,128)(2,1)S(1)}, bf16[192,384]{1,0:T(8,128)(2,1)S(1)}, u32[]{:S(2)}, u32[]{:S(2)}) collective-permute-start(bf16[192,384]{1,0:T(8,128)(2,1)S(1)} %get-tuple-element.47), channel_id=1, source_target_pairs={{0,96},{1,97},{2,98},{3,99},{4,100},{5,101},{6,102},{7,103},{8,104... | collective-permute-start | bytes 442376 | tf_op jit(solution)/shard_map/ppermute | solution.py:339
  23.8 9.4 %copy-start = (f32[2,384,384]{2,1,0:T(8,128)S(1)}, f32[2,384,384]{2,1,0:T(8,128)}, u32[]{:S(2)}) copy-start(f32[2,384,384]{2,1,0:T(8,128)} %refs_9_.3) | copy-start | bytes 3538948
  34.9 6.8 %collective-permute-start.16 = (bf16[192,384]{1,0:T(8,128)(2,1)S(1)}, bf16[192,384]{1,0:T(8,128)(2,1)S(1)}, u32[]{:S(2)}, u32[]{:S(2)}) collective-permute-start(bf16[192,384]{1,0:T(8,128)(2,1)S(1)} %get-tuple-element.54), channel_id=1, source_target_pairs={{0,16},{16,0},{1,17},{17,1},{2,18},{18,2},{3,19},{19,3},{4,20},{20... | collective-permute-start | bytes 442376 | tf_op jit(solution)/shard_map/ppermute | solution.py:382
  35.3 14.1 %collective-permute-start.8 = (bf16[192,384]{1,0:T(8,128)(2,1)S(1)}, bf16[192,384]{1,0:T(8,128)(2,1)S(1)}, u32[]{:S(2)}, u32[]{:S(2)}) collective-permute-start(bf16[192,384]{1,0:T(8,128)(2,1)S(1)} %get-tuple-element.53), channel_id=1, source_target_pairs={{0,2},{1,3},{2,18},{3,19},{4,38},{5,39},{6,54},{7,55},{8,74},{9,75... | collective-permute-start | bytes 442376 | tf_op jit(solution)/shard_map/ppermute | solution.py:339
  39.0 10.4 %collective-permute-start.7 = (bf16[192,384]{1,0:T(8,128)(2,1)S(1)}, bf16[192,384]{1,0:T(8,128)(2,1)S(1)}, u32[]{:S(2)}, u32[]{:S(2)}) collective-permute-start(bf16[192,384]{1,0:T(8,128)(2,1)S(1)} %get-tuple-element.53), channel_id=1, source_target_pairs={{0,0},{1,1},{2,16},{3,17},{4,36},{5,37},{6,52},{7,53},{8,72},{9,73... | collective-permute-start | bytes 442376 | tf_op jit(solution)/shard_map/ppermute | solution.py:339
  41.8 18.7 %collective-permute-start.19 = (bf16[2,192,384]{2,1,0:T(8,128)(2,1)S(1)}, bf16[2,192,384]{2,1,0:T(8,128)(2,1)S(1)}, u32[]{:S(2)}, u32[]{:S(2)}) collective-permute-start(bf16[2,192,384]{2,1,0:T(8,128)(2,1)S(1)} %pad_maximum_fusion.1.refs_0_), channel_id=1, source_target_pairs={{0,96},{32,0},{64,32},{96,64},{1,97},{33,1},{65,33},{97,65},{2,98}... | collective-permute-start | bytes 884744 | tf_op jit(solution)/shard_map/ppermute | solution.py:356
  48.5 11.9 %collective-permute-start.18 = (bf16[2,192,384]{2,1,0:T(8,128)(2,1)S(1)}, bf16[2,192,384]{2,1,0:T(8,128)(2,1)S(1)}, u32[]{:S(2)}, u32[]{:S(2)}) collective-permute-start(bf16[2,192,384]{2,1,0:T(8,128)(2,1)S(1)} %pad_maximum_fusion.1.refs_0_), channel_id=1, source_target_pairs={{0,64},{32,96},{64,0},{96,32},{1,65},{33,97},{65,1},{97,33},{2,66}... | collective-permute-start | bytes 884744 | tf_op jit(solution)/shard_map/ppermute | solution.py:356
  49.4 16.4 %collective-permute-start.11 = (bf16[2,192,384]{2,1,0:T(8,128)(2,1)S(1)}, bf16[2,192,384]{2,1,0:T(8,128)(2,1)S(1)}, u32[]{:S(2)}, u32[]{:S(2)}) collective-permute-start(bf16[2,192,384]{2,1,0:T(8,128)(2,1)S(1)} %pad_maximum_fusion.refs_0_), channel_id=1, source_target_pairs={{0,12},{4,0},{8,4},{12,8},{1,13},{5,1},{9,5},{13,9},{2,14},{6,2},{... | collective-permute-start | bytes 884744 | tf_op jit(solution)/shard_map/ppermute | solution.py:356
  55.9 10.6 %collective-permute-start.10 = (bf16[2,192,384]{2,1,0:T(8,128)(2,1)S(1)}, bf16[2,192,384]{2,1,0:T(8,128)(2,1)S(1)}, u32[]{:S(2)}, u32[]{:S(2)}) collective-permute-start(bf16[2,192,384]{2,1,0:T(8,128)(2,1)S(1)} %pad_maximum_fusion.refs_0_), channel_id=1, source_target_pairs={{0,8},{4,12},{8,0},{12,4},{1,9},{5,13},{9,1},{13,5},{2,10},{6,14},... | collective-permute-start | bytes 884744 | tf_op jit(solution)/shard_map/ppermute | solution.py:356
  55.9 13.7 %collective-permute-start.9 = (bf16[2,192,384]{2,1,0:T(8,128)(2,1)S(1)}, bf16[2,192,384]{2,1,0:T(8,128)(2,1)S(1)}, u32[]{:S(2)}, u32[]{:S(2)}) collective-permute-start(bf16[2,192,384]{2,1,0:T(8,128)(2,1)S(1)} %pad_maximum_fusion.refs_0_), channel_id=1, source_target_pairs={{0,4},{4,8},{8,12},{12,0},{1,5},{5,9},{9,13},{13,1},{2,6},{6,10},{... | collective-permute-start | bytes 884744 | tf_op jit(solution)/shard_map/ppermute | solution.py:356
  60.5 9.3 %collective-permute-start.17 = (bf16[2,192,384]{2,1,0:T(8,128)(2,1)S(1)}, bf16[2,192,384]{2,1,0:T(8,128)(2,1)S(1)}, u32[]{:S(2)}, u32[]{:S(2)}) collective-permute-start(bf16[2,192,384]{2,1,0:T(8,128)(2,1)S(1)} %pad_maximum_fusion.1.refs_0_), channel_id=1, source_target_pairs={{0,32},{32,64},{64,96},{96,0},{1,33},{33,65},{65,97},{97,1},{2,34}... | collective-permute-start | bytes 884744 | tf_op jit(solution)/shard_map/ppermute | solution.py:356
  60.5 9.3 %collective-permute-start.12 = (bf16[2,192,384]{2,1,0:T(8,128)(2,1)S(1)}, bf16[2,192,384]{2,1,0:T(8,128)(2,1)S(1)}, u32[]{:S(2)}, u32[]{:S(2)}) collective-permute-start(bf16[2,192,384]{2,1,0:T(8,128)(2,1)S(1)} %pad_maximum_fusion.refs_0_), channel_id=1, source_target_pairs={{0,1},{1,0},{2,3},{3,2},{4,5},{5,4},{6,7},{7,6},{8,9},{9,8},{10,11... | collective-permute-start | bytes 884744 | tf_op jit(solution)/shard_map/ppermute | solution.py:381
  65.9 3.9 %collective-permute-start.15 = (bf16[2,192,384]{2,1,0:T(8,128)(2,1)S(1)}, bf16[2,192,384]{2,1,0:T(8,128)(2,1)S(1)}, u32[]{:S(2)}, u32[]{:S(2)}) collective-permute-start(bf16[2,192,384]{2,1,0:T(8,128)(2,1)S(1)} %collective-permute-done.11.refs_3_), channel_id=1, source_target_pairs={{0,1},{1,0},{2,3},{3,2},{4,5},{5,4},{6,7},{7,6},{8,9},{9,8},{10,11... | collective-permute-start | bytes 884744 | tf_op jit(solution)/shard_map/ppermute | solution.py:381
  66.5 3.3 %collective-permute-start.14 = (bf16[2,192,384]{2,1,0:T(8,128)(2,1)S(1)}, bf16[2,192,384]{2,1,0:T(8,128)(2,1)S(1)}, u32[]{:S(2)}, u32[]{:S(2)}) collective-permute-start(bf16[2,192,384]{2,1,0:T(8,128)(2,1)S(1)} %collective-permute-done.10.refs_2_), channel_id=1, source_target_pairs={{0,1},{1,0},{2,3},{3,2},{4,5},{5,4},{6,7},{7,6},{8,9},{9,8},{10,11... | collective-permute-start | bytes 884744 | tf_op jit(solution)/shard_map/ppermute | solution.py:381
  69.6 1.6 %collective-permute-start.13 = (bf16[2,192,384]{2,1,0:T(8,128)(2,1)S(1)}, bf16[2,192,384]{2,1,0:T(8,128)(2,1)S(1)}, u32[]{:S(2)}, u32[]{:S(2)}) collective-permute-start(bf16[2,192,384]{2,1,0:T(8,128)(2,1)S(1)} %collective-permute-done.9.refs_1_), channel_id=1, source_target_pairs={{0,1},{1,0},{2,3},{3,2},{4,5},{5,4},{6,7},{7,6},{8,9},{9,8},{10,11... | collective-permute-start | bytes 884744 | tf_op jit(solution)/shard_map/ppermute | solution.py:381
  75.4 10.2 %collective-permute-start.24 = (bf16[192,384]{1,0:T(8,128)(2,1)S(1)}, bf16[192,384]{1,0:T(8,128)(2,1)S(1)}, u32[]{:S(2)}, u32[]{:S(2)}) collective-permute-start(bf16[192,384]{1,0:T(8,128)(2,1)S(1)} %get-tuple-element.68), channel_id=1, source_target_pairs={{0,48},{1,49},{2,50},{3,51},{4,52},{5,53},{6,54},{7,55},{8,56},{9,... | collective-permute-start | bytes 442376 | tf_op jit(solution)/shard_map/ppermute | solution.py:339
  75.5 11.1 %collective-permute-start.25 = (bf16[192,384]{1,0:T(8,128)(2,1)S(1)}, bf16[192,384]{1,0:T(8,128)(2,1)S(1)}, u32[]{:S(2)}, u32[]{:S(2)}) collective-permute-start(bf16[192,384]{1,0:T(8,128)(2,1)S(1)} %get-tuple-element.69), channel_id=1, source_target_pairs={{0,32},{1,33},{2,34},{3,35},{4,36},{5,37},{6,38},{7,39},{8,40},{9,... | collective-permute-start | bytes 442376 | tf_op jit(solution)/shard_map/ppermute | solution.py:339
  77.9 11.6 %collective-permute-start.26 = (bf16[192,384]{1,0:T(8,128)(2,1)S(1)}, bf16[192,384]{1,0:T(8,128)(2,1)S(1)}, u32[]{:S(2)}, u32[]{:S(2)}) collective-permute-start(bf16[192,384]{1,0:T(8,128)(2,1)S(1)} %get-tuple-element.70), channel_id=1, source_target_pairs={{0,16},{1,17},{2,18},{3,19},{4,20},{5,21},{6,22},{7,23},{8,24},{9,... | collective-permute-start | bytes 442376 | tf_op jit(solution)/shard_map/ppermute | solution.py:339
  81.7 9.2 %collective-permute-start.20 = (bf16[192,384]{1,0:T(8,128)(2,1)S(1)}, bf16[192,384]{1,0:T(8,128)(2,1)S(1)}, u32[]{:S(2)}, u32[]{:S(2)}) collective-permute-start(bf16[192,384]{1,0:T(8,128)(2,1)S(1)} %get-tuple-element.64), channel_id=1, source_target_pairs={{0,80},{1,81},{2,82},{3,83},{4,84},{5,85},{6,86},{7,87},{8,88},{9,... | collective-permute-start | bytes 442376 | tf_op jit(solution)/shard_map/ppermute | solution.py:339
  82.1 9.8 %collective-permute-start.21 = (bf16[192,384]{1,0:T(8,128)(2,1)S(1)}, bf16[192,384]{1,0:T(8,128)(2,1)S(1)}, u32[]{:S(2)}, u32[]{:S(2)}) collective-permute-start(bf16[192,384]{1,0:T(8,128)(2,1)S(1)} %get-tuple-element.65), channel_id=1, source_target_pairs={{0,64},{1,65},{2,66},{3,67},{4,68},{5,69},{6,70},{7,71},{8,72},{9,... | collective-permute-start | bytes 442376 | tf_op jit(solution)/shard_map/ppermute | solution.py:339
  85.6 10.0 %collective-permute-start.22 = (bf16[192,384]{1,0:T(8,128)(2,1)S(1)}, bf16[192,384]{1,0:T(8,128)(2,1)S(1)}, u32[]{:S(2)}, u32[]{:S(2)}) collective-permute-start(bf16[192,384]{1,0:T(8,128)(2,1)S(1)} %get-tuple-element.66), channel_id=1, source_target_pairs={{0,112},{1,113},{2,114},{3,115},{4,116},{5,117},{6,118},{7,119},{8... | collective-permute-start | bytes 442376 | tf_op jit(solution)/shard_map/ppermute | solution.py:339
  86.6 11.5 %collective-permute-start.23 = (bf16[192,384]{1,0:T(8,128)(2,1)S(1)}, bf16[192,384]{1,0:T(8,128)(2,1)S(1)}, u32[]{:S(2)}, u32[]{:S(2)}) collective-permute-start(bf16[192,384]{1,0:T(8,128)(2,1)S(1)} %get-tuple-element.67), channel_id=1, source_target_pairs={{0,96},{1,97},{2,98},{3,99},{4,100},{5,101},{6,102},{7,103},{8,104... | collective-permute-start | bytes 442376 | tf_op jit(solution)/shard_map/ppermute | solution.py:339
  99.6 9.2 %collective-permute-start.33 = (bf16[192,384]{1,0:T(8,128)(2,1)S(1)}, bf16[192,384]{1,0:T(8,128)(2,1)S(1)}, u32[]{:S(2)}, u32[]{:S(2)}) collective-permute-start(bf16[192,384]{1,0:T(8,128)(2,1)S(1)} %second_solve.1.refs_0_), channel_id=1, source_target_pairs={{0,112},{1,113},{2,114},{3,115},{4,116},{5,117},{6,118},{7,119},{8... | collective-permute-start | bytes 442376 | tf_op jit(solution)/shard_map/ppermute | solution.py:339
  102.3 12.8 %collective-permute-start.32 = (bf16[192,384]{1,0:T(8,128)(2,1)S(1)}, bf16[192,384]{1,0:T(8,128)(2,1)S(1)}, u32[]{:S(2)}, u32[]{:S(2)}) collective-permute-start(bf16[192,384]{1,0:T(8,128)(2,1)S(1)} %second_solve.1.refs_0_), channel_id=1, source_target_pairs={{0,96},{1,97},{2,98},{3,99},{4,100},{5,101},{6,102},{7,103},{8,104... | collective-permute-start | bytes 442376 | tf_op jit(solution)/shard_map/ppermute | solution.py:339
  102.3 15.7 %collective-permute-start.31 = (bf16[192,384]{1,0:T(8,128)(2,1)S(1)}, bf16[192,384]{1,0:T(8,128)(2,1)S(1)}, u32[]{:S(2)}, u32[]{:S(2)}) collective-permute-start(bf16[192,384]{1,0:T(8,128)(2,1)S(1)} %second_solve.1.refs_0_), channel_id=1, source_target_pairs={{0,80},{1,81},{2,82},{3,83},{4,84},{5,85},{6,86},{7,87},{8,88},{9,... | collective-permute-start | bytes 442376 | tf_op jit(solution)/shard_map/ppermute | solution.py:339
  104.6 13.4 %collective-permute-start.30 = (bf16[192,384]{1,0:T(8,128)(2,1)S(1)}, bf16[192,384]{1,0:T(8,128)(2,1)S(1)}, u32[]{:S(2)}, u32[]{:S(2)}) collective-permute-start(bf16[192,384]{1,0:T(8,128)(2,1)S(1)} %second_solve.1.refs_0_), channel_id=1, source_target_pairs={{0,64},{1,65},{2,66},{3,67},{4,68},{5,69},{6,70},{7,71},{8,72},{9,... | collective-permute-start | bytes 442376 | tf_op jit(solution)/shard_map/ppermute | solution.py:339
  106.2 11.9 %collective-permute-start.29 = (bf16[192,384]{1,0:T(8,128)(2,1)S(1)}, bf16[192,384]{1,0:T(8,128)(2,1)S(1)}, u32[]{:S(2)}, u32[]{:S(2)}) collective-permute-start(bf16[192,384]{1,0:T(8,128)(2,1)S(1)} %second_solve.1.refs_0_), channel_id=1, source_target_pairs={{0,48},{1,49},{2,50},{3,51},{4,52},{5,53},{6,54},{7,55},{8,56},{9,... | collective-permute-start | bytes 442376 | tf_op jit(solution)/shard_map/ppermute | solution.py:339
  108.8 10.4 %collective-permute-start.28 = (bf16[192,384]{1,0:T(8,128)(2,1)S(1)}, bf16[192,384]{1,0:T(8,128)(2,1)S(1)}, u32[]{:S(2)}, u32[]{:S(2)}) collective-permute-start(bf16[192,384]{1,0:T(8,128)(2,1)S(1)} %second_solve.1.refs_0_), channel_id=1, source_target_pairs={{0,32},{1,33},{2,34},{3,35},{4,36},{5,37},{6,38},{7,39},{8,40},{9,... | collective-permute-start | bytes 442376 | tf_op jit(solution)/shard_map/ppermute | solution.py:339
  115.1 5.1 %collective-permute-start.27 = (bf16[192,384]{1,0:T(8,128)(2,1)S(1)}, bf16[192,384]{1,0:T(8,128)(2,1)S(1)}, u32[]{:S(2)}, u32[]{:S(2)}) collective-permute-start(bf16[192,384]{1,0:T(8,128)(2,1)S(1)} %second_solve.1.refs_0_), channel_id=1, source_target_pairs={{0,16},{1,17},{2,18},{3,19},{4,20},{5,21},{6,22},{7,23},{8,24},{9,... | collective-permute-start | bytes 442376 | tf_op jit(solution)/shard_map/ppermute | solution.py:339

commit v4 on v3

--- a/solution.py
+++ b/solution.py
@@ -56,91 +56,112 @@
     )(place, *args)
 
 
+def position(y):
+    return (y & 1) * 2 + (y >> 1)
+
+
 def store_shares(place_ref, turned_ref, out_refs):
     width = out_refs[0].shape[0]
     for k, out_ref in enumerate(out_refs):
-        share = ((place_ref[Y] & 1) ^ (k >> 1)) * 2 + (place_ref[ZL] ^ (k & 1))
+        share = ((place_ref[Y] >> 1) ^ (k >> 1)) * 2 + (place_ref[ZL] ^ (k & 1))
         out_ref[...] = turned_ref[pl.ds(pl.multiple_of(share * width, width), width), :]
 
 
-def first_half_kernel(place_ref, lhs_ref, resident_ref, *refs):
+def half_product_kernel(place_ref, lhs_ref, resident_ref, *refs):
     out_refs, turned_ref = refs[:4], refs[4]
-    step, tile = pl.program_id(0), resident_ref.shape[1]
     product = jnp.dot(lhs_ref[...], resident_ref[...], preferred_element_type=f32)
-    turned_ref[pl.ds(pl.multiple_of(step * tile, tile), tile), :] = product.T.astype(bf16)
-
-    @pl.when(step == pl.num_programs(0) - 1)
-    def _():
-        store_shares(place_ref, turned_ref, out_refs)
-
-
-def first_half(place, memory, resident, far):
+    turned_ref[...] = product.T.astype(bf16)
+    store_shares(place_ref, turned_ref, out_refs)
+
+
+def half_product(place, lhs, resident):
+    rows, depth = lhs.shape
+    cols = resident.shape[1]
+    width = cols // 4
+    return pl.pallas_call(
+        half_product_kernel,
+        in_specs=[SMEM, VMEM, VMEM],
+        out_specs=[VMEM] * 4,
+        out_shape=[jax.ShapeDtypeStruct((width, rows), bf16)] * 4,
+        scratch_shapes=[pltpu.VMEM((cols, rows), bf16)],
+        compiler_params=params(6),
+        cost_estimate=cost(2 * rows * depth * cols, 4 * width * rows),
+        name="half_product",
+    )(place, lhs, resident)
+
+
+TILES = 3
+
+
+def first_product_kernel(place_ref, memory_ref, resident_ref, *refs):
+    out_refs, lhs_ref, even_ref, odd_ref, turned_ref, sems = refs[:4], *refs[4:]
+    depth, cols = odd_ref.shape
+    tile = cols // TILES
+    parity = place_ref[Y] & 1
+
+    def tile_copy(half_ref, side, i):
+        start = pl.multiple_of((parity ^ side) * cols + i * tile, tile)
+        return pltpu.make_async_copy(
+            resident_ref.at[:, pl.ds(start, tile)],
+            half_ref.at[:, i * tile : (i + 1) * tile],
+            sems.at[side * TILES + i],
+        )
+
+    memory_copy = pltpu.make_async_copy(memory_ref.at[0], lhs_ref, sems.at[2 * TILES])
+    odd = [tile_copy(odd_ref, 1, i) for i in range(TILES)]
+    even = [tile_copy(even_ref, 0, i) for i in range(TILES)]
+    for copy in (memory_copy, *odd, *even):
+        copy.start()
+    memory_copy.wait()
+    for i, copy in enumerate(odd):
+        copy.wait()
+        at = slice(i * tile, (i + 1) * tile)
+        product = jnp.dot(lhs_ref[...], odd_ref[:, at], preferred_element_type=f32)
+        turned_ref[at, :] = product.T.astype(bf16)
+    store_shares(place_ref, turned_ref, out_refs)
+    for copy in even:
+        copy.wait()
+
+
+def first_product(place, memory, resident):
     _, rows, depth = memory.shape
     cols = resident.shape[1]
     width = cols // 8
-    tile = 256
-    steps = cols // 2 // tile
-    return placed_call(
-        first_half_kernel,
-        place,
-        (memory, resident),
-        [
-            pl.BlockSpec((None, rows, depth), lambda i, place: (0, 0, 0)),
-            pl.BlockSpec((depth, tile), lambda i, place: (0, ((place[Y] >> 1) ^ far) * steps + i)),
+    outs = [((width, rows), 4), ((rows, depth), 1), ((depth, cols // 2), 1)]
+    shapes = [jax.ShapeDtypeStruct(shape, bf16) for shape, count in outs for _ in range(count)]
+    *odd, lhs, even_resident = pl.pallas_call(
+        first_product_kernel,
+        in_specs=[SMEM] + [pl.BlockSpec(memory_space=pltpu.HBM)] * 2,
+        out_specs=[VMEM] * 6,
+        out_shape=shapes,
+        scratch_shapes=[
+            pltpu.VMEM((depth, cols // 2), bf16),
+            pltpu.VMEM((cols // 2, rows), bf16),
+            pltpu.SemaphoreType.DMA((2 * TILES + 1,)),
         ],
-        [whole((width, rows))] * 4,
-        [jax.ShapeDtypeStruct((width, rows), bf16)] * 4,
-        "first_half",
-        16,
-        (rows * depth * cols, depth * cols + 2 * rows * depth),
-        grid=steps,
-        scratch=[pltpu.VMEM((cols // 2, rows), bf16)],
-    )
-
-
-def second_half_kernel(far, place_ref, lhs_ref, resident_ref, *refs):
-    out_refs, turned_ref = refs[:4], refs[4]
-    cols = resident_ref.shape[1] // 2
-    at = pl.ds(pl.multiple_of(((place_ref[Y] >> 1) ^ far) * cols, cols), cols)
-    product = jnp.dot(lhs_ref[...], resident_ref[:, at], preferred_element_type=f32)
-    turned_ref[...] = product.T.astype(bf16)
-    store_shares(place_ref, turned_ref, out_refs)
-
-
-def second_half(place, lhs, resident, far):
-    rows, depth = lhs.shape
-    cols = resident.shape[1]
-    width = cols // 8
-    return pl.pallas_call(
-        functools.partial(second_half_kernel, far),
-        in_specs=[SMEM, VMEM, VMEM],
-        out_specs=[VMEM] * 4,
-        out_shape=[jax.ShapeDtypeStruct((width, rows), bf16)] * 4,
-        scratch_shapes=[pltpu.VMEM((cols // 2, rows), bf16)],
-        compiler_params=params(6),
-        cost_estimate=cost(rows * depth * cols, 4 * width * rows),
-        name="second_half",
-    )(place, lhs, resident)
-
-
-def product(half, place, lhs, resident):
-    far = half(place, lhs, resident, 1)
-    near = half(place, lhs, resident, 0)
-    moves = {}
-    for k in range(4):
-        moves[2 + (k >> 1), k & 1] = far[k]
-        moves[k >> 1, k & 1] = near[k]
-    return moves
-
-
-def bring_kernel(place_ref, resident_ref, memory_ref, previous_ref, resident_out, memory_out, one_out, two_out, prior_ref, turned_ref, sems):
+        compiler_params=params(12),
+        cost_estimate=cost(rows * depth * cols, 4 * depth * cols),
+        name="first_product",
+    )(place, memory, resident)
+    return odd, lhs, even_resident
+
+
+def bring_kernel(
+    place_ref, memory_ref, previous_ref, resident_ref, memory_out, one_out, two_out, odd_out, even_out, prior_ref, turned_ref, sems
+):
     width, rows = one_out.shape
-    cols = pl.ds(pl.multiple_of(place_ref[Y] * 2 * width, 128), 2 * width)
+    start = position(place_ref[Y]) * 2 * width
+    cols = pl.ds(pl.multiple_of(start, 128), 2 * width)
     copies = [
         pltpu.make_async_copy(previous_ref.at[:, :, cols], prior_ref, sems.at[0]),
         pltpu.make_async_copy(memory_ref.at[1], memory_out, sems.at[1]),
-        pltpu.make_async_copy(resident_ref, resident_out, sems.at[2]),
     ]
+    half = odd_out.shape[1]
+    for side, out_ref in ((1, odd_out), (0, even_out)):
+        start = pl.multiple_of(((place_ref[Y] & 1) ^ side) * half, half)
+        copies.append(
+            pltpu.make_async_copy(resident_ref.at[:, pl.ds(start, half)], out_ref, sems.at[2 + side])
+        )
     for copy in copies:
         copy.start()
     copies[0].wait()
@@ -148,34 +169,34 @@
         turned_ref[...] = prior_ref[front].astype(f32).T
         share = turned_ref[pl.ds(pl.multiple_of(place_ref[ZL] * width, width), width), :]
         out_ref[...] = share.astype(bf16)
-    copies[1].wait()
-    copies[2].wait()
-
-
-def bring(place, resident, memory, previous):
+    for copy in copies[1:]:
+        copy.wait()
+
+
+def bring(place, memory, previous, resident):
     _, rows, depth = memory.shape
     cols = resident.shape[1]
-    width = cols // 8
-    anywhere = pl.BlockSpec(memory_space=pltpu.HBM)
+    width = previous.shape[2] // 8
     return pl.pallas_call(
         bring_kernel,
-        in_specs=[SMEM, anywhere, anywhere, anywhere],
-        out_specs=[VMEM] * 4,
+        in_specs=[SMEM] + [pl.BlockSpec(memory_space=pltpu.HBM)] * 3,
+        out_specs=[VMEM] * 5,
         out_shape=[
-            jax.ShapeDtypeStruct(resident.shape, bf16),
             jax.ShapeDtypeStruct((rows, depth), bf16),
             jax.ShapeDtypeStruct((width, rows), bf16),
             jax.ShapeDtypeStruct((width, rows), bf16),
+            jax.ShapeDtypeStruct((depth, cols // 2), bf16),
+            jax.ShapeDtypeStruct((depth, cols // 2), bf16),
         ],
         scratch_shapes=[
             pltpu.VMEM((2, rows, 2 * width), bf16),
             pltpu.VMEM((2 * width, rows), f32),
-            pltpu.SemaphoreType.DMA((3,)),
+            pltpu.SemaphoreType.DMA((4,)),
         ],
         compiler_params=params(6),
         cost_estimate=cost(0, 2 * depth * (rows + cols)),
         name="bring",
-    )(place, resident, memory, previous)
+    )(place, memory, previous, resident)
 
 
 def place_pair(own, other, first, at, out_ref, base_ref):
@@ -195,7 +216,7 @@
     for side in range(2):
         for dx in range(4):
             pair = pair_refs[side * 4 + dx]
-            share = ((place_ref[X] - dx) & 3) ^ place_ref[Y]
+            share = position(((place_ref[X] - dx) & 3) ^ place_ref[Y])
             start = (place_ref[C] ^ side) * half + share * width
             at = pl.ds(pl.multiple_of(start, 128), width)
             place_pair(pair[0], pair[1], place_ref[ZH], at, out_ref, memory_ref)
@@ -284,7 +305,7 @@
     pair_refs, out_ref = refs[:4], refs[4]
     width = out_ref.shape[1] // 4
     for dy in range(4):
-        at = pl.ds(pl.multiple_of(((place_ref[Y] - dy) & 3) * width, 128), width)
+        at = pl.ds(pl.multiple_of(position((place_ref[Y] - dy) & 3) * width, 128), width)
         place_pair(pair_refs[dy][0], pair_refs[dy][1], place_ref[ZL], at, out_ref, None)
 
 
@@ -306,7 +327,7 @@
     chunk_refs, out_ref = refs[:8], refs[9]
     width = out_ref.shape[1] // 4
     for dy in range(4):
-        at = pl.ds(pl.multiple_of(((place_ref[Y] - dy) & 3) * width, 128), width)
+        at = pl.ds(pl.multiple_of(position((place_ref[Y] - dy) & 3) * width, 128), width)
         own, other = chunk_refs[2 * dy][...], chunk_refs[2 * dy + 1][...]
         place_pair(own, other, place_ref[ZL], at, out_ref, None)
 
@@ -343,11 +364,15 @@
     return lambda y, zl, x, zh: (x, zh, x ^ y, zl ^ flip)
 
 
-def scatter(shares):
+def scatter(shares, first):
     parts = []
-    for dy, dz in ((2, 1), (2, 0), (3, 1), (3, 0), (1, 1), (1, 0), (0, 1)):
-        parts.append(move(shares[dy, dz], lambda y, zl, x, zh: (y ^ dy, zl ^ dz, x, zh)))
-    return [*parts, shares[0, 0]]
+    for k in (3, 2, 1, 0) if first == 0 else (1, 0, 3, 2):
+        dy, dz = first + 2 * (k >> 1), k & 1
+        if (dy, dz) == (0, 0):
+            parts.append(shares[k])
+        else:
+            parts.append(move(shares[k], lambda y, zl, x, zh: (y ^ dy, zl ^ dz, x, zh)))
+    return parts
 
 
 def spread_pairs(pair, axis):
@@ -370,10 +395,14 @@
     coupling = jnp.tile(pair_coupling, (1, 128 // ORB))
 
     resident, memory, previous = in_hbm(resident), in_hbm(memory), in_hbm(previous)
-    shares = product(first_half, place, memory, resident)
-    place, shares[0, 0] = lax.optimization_barrier((place, shares[0, 0]))
-    resident, memory, prior_one, prior_two = bring(place, resident, memory, previous)
-    parts = scatter(shares)
+    odd, lhs, even_resident = first_product(place, memory, resident)
+    odd_parts = scatter(odd, 1)
+    lhs, odd = lax.optimization_barrier((lhs, odd))
+    even = half_product(place, lhs, even_resident)
+    even_parts = scatter(even, 0)
+    place, _, odd_parts = lax.optimization_barrier((place, even[0], odd_parts))
+    memory, prior_one, prior_two, odd_resident, even_resident = bring(place, memory, previous, resident)
+    parts = odd_parts + even_parts
     front_one, energy = solve(
         first_solve_kernel, 0, place, parts, prior_one, inverse_part, [coupling], 2, "first_solve"
     )
@@ -382,7 +411,10 @@
     ones = spread_pairs(jnp.stack([front_one, lax.ppermute(front_one, "zl", SWAP)]), "y")
     own, other, ones = lax.optimization_barrier((own, other, ones))
     lhs = next_memory(place, memory, own + other)
-    parts = scatter(product(second_half, place, lhs, resident))
+    odd = half_product(place, lhs, odd_resident)
+    lhs, odd = lax.optimization_barrier((lhs, odd))
+    even = half_product(place, lhs, even_resident)
+    parts = scatter(odd, 1) + scatter(even, 0)
     (front_two,) = solve(
         second_solve_kernel, 1, place, parts, prior_two, inverse_part, [], 1, "second_solve"
     )

time: 123 us -> 113 us (0.919)
  waiting for transfers between devices: 37.7 us -> 23.8 us
  starting transfers between devices: 52.9 us -> 58.9 us
  Pallas kernels: 31.2 us -> 28.6 us
    pallas_call x6 -> x4, Pallas kernels: 19.1 us -> 7.3 us  [placed_call(): pl.pallas_call(kernel, grid_spec=pltpu.PrefetchScalarGridSpec(num_scalar_...]
    pallas_call x3 -> x5, Pallas kernels: 10.5 us -> 19.7 us  [the longest x3 7.98 us: half_product(): pl.pallas_call(half_product_kernel, in_specs=[SMEM, VMEM, VMEM], out_spec...]
    ppermute x6, waiting for transfers between devices: 12.9 us -> 5.36 us  [spread_pairs(): pairs[d] = lax.ppermute(pair, axis, [(i, (i + d) % 4) for i in range(4)])]
    ppermute x6, starting transfers between devices: 15.1 us -> 20.1 us  [spread_pairs(): pairs[d] = lax.ppermute(pair, axis, [(i, (i + d) % 4) for i in range(4)])]
    ppermute x23, waiting for transfers between devices: 21.4 us -> 17.4 us  [move(): return lax.ppermute(value, ALL, pairs)]
    ppermute x1, waiting for transfers between devices: 2.06 us -> 0.81 us  [per_device(): lax.ppermute(front_one, 'zl', SWAP)]
  transfers between devices with their start and end apart: 34 -> 34, of which waited for: 16 -> 10; matrix products, arithmetic and copies ran while one was open for 0% -> 0% of each run, Pallas kernels for 13% -> 11%
where the time goes in v4:
time: 113 us; the launch traced here: 112 us
  starting transfers between devices  58.9 us (52%)
  Pallas kernels  28.6 us (25%)
  waiting for transfers between devices  23.8 us (21%)
    ppermute x23, starting transfers between devices, move(): return lax.ppermute(value, ALL, pairs)  38.1 us
    ppermute x6, starting transfers between devices, spread_pairs(): pairs[d] = lax.ppermute(pair, axis, [(i, (i + d) % 4) for i in range(4)])  20.1 us
    ppermute x23, waiting for transfers between devices, move(): return lax.ppermute(value, ALL, pairs)  17.4 us
    pallas_call x3, Pallas kernels, half_product(): pl.pallas_call(half_product_kernel, in_specs=[SMEM, VMEM, VMEM], out_spec...  7.98 us
    pallas_call x4, Pallas kernels, placed_call(): pl.pallas_call(kernel, grid_spec=pltpu.PrefetchScalarGridSpec(num_scalar_...  7.3 us
    pallas_call x1, Pallas kernels, first_product(): pl.pallas_call(first_product_kernel, in_specs=[SMEM] + [pl.BlockSpec(memo...  6.5 us
    ppermute x6, waiting for transfers between devices, spread_pairs(): pairs[d] = lax.ppermute(pair, axis, [(i, (i + d) % 4) for i in range(4)])  5.36 us
    pallas_call x1, Pallas kernels, bring(): pl.pallas_call(bring_kernel, in_specs=[SMEM] + [pl.BlockSpec(memory_space...  5.18 us
  transfers between devices with their start and end apart: 34, of which 10 were waited for; matrix products, arithmetic and copies ran while one was open for 0% of the time, Pallas kernels for 11%

profile of v4, /device:TPU:0, one launch (start us, length us, event | category | flops | bytes accessed | tf_op | source)
XLA Modules:
  0.0 111.7 jit_solution(12776541041766496075)
XLA Ops:
  0.1 6.5 %first_product.1 = (bf16[192,384]{1,0:T(8,128)(2,1)S(1)}, bf16[192,384]{1,0:T(8,128)(2,1)S(1)}, bf16[192,384]{1,0:T(8,128)(2,1)S(1)}, bf16[192,384]{1,0:T(8,128)...) custom-call(s32[5]{0:T(128)S(1)} %stack.41.place_ref, bf16[2,384,3072]{2,1,0:T(8,128)(2,1)} %memory_ref.3, ...), custom_call_target="tpu_custom_call" | custom-call | flops 1811939328 | bytes 18874368 | tf_op jit(solution)/shard_map/first_product/pallas_call | solution.py:132
  6.6 1.7 %collective-permute-start.1 = (bf16[192,384]{1,0:T(8,128)(2,1)S(1)}, bf16[192,384]{1,0:T(8,128)(2,1)S(1)}, u32[]{:S(2)}, u32[]{:S(2)}) collective-permute-start(bf16[192,384]{1,0:T(8,128)(2,1)S(1)} %get-tuple-element.54), channel_id=1, source_target_pairs={{0,32},{1,33},{2,34},{3,35},{4,36},{5,37},{6,38},{7,39},{8,40},{9,... | collective-permute-start | bytes 442376 | tf_op jit(solution)/shard_map/ppermute | solution.py:360
  8.3 1.8 %collective-permute-start = (bf16[192,384]{1,0:T(8,128)(2,1)S(1)}, bf16[192,384]{1,0:T(8,128)(2,1)S(1)}, u32[]{:S(2)}, u32[]{:S(2)}) collective-permute-start(bf16[192,384]{1,0:T(8,128)(2,1)S(1)} %get-tuple-element.55), channel_id=1, source_target_pairs={{0,48},{1,49},{2,50},{3,51},{4,52},{5,53},{6,54},{7,55},{8,56},{9,... | collective-permute-start | bytes 442376 | tf_op jit(solution)/shard_map/ppermute | solution.py:360
  10.1 3.0 %collective-permute-start.3 = (bf16[192,384]{1,0:T(8,128)(2,1)S(1)}, bf16[192,384]{1,0:T(8,128)(2,1)S(1)}, u32[]{:S(2)}, u32[]{:S(2)}) collective-permute-start(bf16[192,384]{1,0:T(8,128)(2,1)S(1)} %get-tuple-element.56), channel_id=1, source_target_pairs={{0,96},{1,97},{2,98},{3,99},{4,100},{5,101},{6,102},{7,103},{8,104... | collective-permute-start | bytes 442376 | tf_op jit(solution)/shard_map/ppermute | solution.py:360
  13.2 2.7 %half_product.3 = (bf16[192,384]{1,0:T(8,128)(2,1)S(1)}, bf16[192,384]{1,0:T(8,128)(2,1)S(1)}, bf16[192,384]{1,0:T(8,128)(2,1)S(1)}, bf16[192,384]{1,0:T(8,128)(2,1)S(1)}) custom-call(s32[5]{0:T(128)S(1)} %stack.41.place_ref, bf16[384,3072]{1,0:T(8,128)(2,1)S(1)} %get-tuple-element.58.lhs_ref, bf16[3072,768]{1,0:T(8,128)(2,1)S(1)} %get-tuple-element.59.resident_ref), custom_call_target="tpu_custom_call" | custom-call | flops 1811939328 | bytes 294912 | tf_op jit(solution)/shard_map/half_product/pallas_call | solution.py:81
  15.8 3.2 %collective-permute-start.4 = (bf16[192,384]{1,0:T(8,128)(2,1)S(1)}, bf16[192,384]{1,0:T(8,128)(2,1)S(1)}, u32[]{:S(2)}, u32[]{:S(2)}) collective-permute-start(bf16[192,384]{1,0:T(8,128)(2,1)S(1)} %get-tuple-element.67), channel_id=1, source_target_pairs={{0,80},{1,81},{2,82},{3,83},{4,84},{5,85},{6,86},{7,87},{8,88},{9,... | collective-permute-start | bytes 442376 | tf_op jit(solution)/shard_map/ppermute | solution.py:360
  19.0 1.5 %collective-permute-start.5 = (bf16[192,384]{1,0:T(8,128)(2,1)S(1)}, bf16[192,384]{1,0:T(8,128)(2,1)S(1)}, u32[]{:S(2)}, u32[]{:S(2)}) collective-permute-start(bf16[192,384]{1,0:T(8,128)(2,1)S(1)} %get-tuple-element.68), channel_id=1, source_target_pairs={{0,64},{1,65},{2,66},{3,67},{4,68},{5,69},{6,70},{7,71},{8,72},{9,... | collective-permute-start | bytes 442376 | tf_op jit(solution)/shard_map/ppermute | solution.py:360
  20.6 0.3 collective-permute-start.6
  20.9 0.1 tile.10.refs_10_
  21.0 5.7 %collective-permute-done.2.refs_2_ = bf16[192,384]{1,0:T(8,128)(2,1)S(1)} collective-permute-done((bf16[192,384]{1,0:T(8,128)(2,1)S(1)}, bf16[192,384]{1,0:T(8,128)(2,1)S(1)}, u32[]{:S(2)}, u32[]{:S(2)}) %collective-permute-start.2) | collective-permute-done | bytes 147488 | tf_op jit(solution)/shard_map/ppermute | solution.py:360
  26.7 5.2 %bring.1 = (bf16[384,3072]{1,0:T(8,128)(2,1)S(1)}, bf16[192,384]{1,0:T(8,128)(2,1)S(1)}, bf16[192,384]{1,0:T(8,128)(2,1)S(1)}, bf16[3072,768]{1,0:T(8,128)(2,1)S(1)}, bf16[3072,768]{1,0:T(8,128)(2,1)S(1)}) custom-call(s32[5]{0:T(128)S(1)} %stack.41.place_ref, bf16[2,384,3072]{2,1,0:T(8,128)(2,1)} %memory_ref.3, bf16[2,384,1536]{2,1,0:T(8,128)(2,1)} %previous_ref.1, ...), custom_call_target="tpu_custom_call" | custom-call | bytes 11796480 | tf_op jit(solution)/shard_map/bring/pallas_call | solution.py:180
  32.0 1.8 %first_solve.1 = (bf16[192,384]{1,0:T(8,128)(2,1)S(1)}, bf16[192,384]{1,0:T(8,128)(2,1)S(1)}) custom-call(s32[5]{0:T(128)S(1)} %stack.41.place_ref, bf16[192,384]{1,0:T(8,128)(2,1)S(1)} %collective-permute-done.refs_0_, bf16[192,384]{1,0:T(8,128)(2,1)S(1)} %collective-permute-done.1.refs_1_, bf16[192,384]{1,0:T(8,128)(2,1)S(1)} %collective-permute-done.2.refs_2_, ...), custom_call_target="tpu_custom_call" | custom-call | flops 339738624 | bytes 1769472 | tf_op jit(solution)/shard_map/first_solve/pallas_call | solution.py:42
  33.8 0.1 collective-permute-start.16
  33.9 3.7 %collective-permute-start.8 = (bf16[192,384]{1,0:T(8,128)(2,1)S(1)}, bf16[192,384]{1,0:T(8,128)(2,1)S(1)}, u32[]{:S(2)}, u32[]{:S(2)}) collective-permute-start(bf16[192,384]{1,0:T(8,128)(2,1)S(1)} %get-tuple-element.71), channel_id=1, source_target_pairs={{0,2},{1,3},{2,18},{3,19},{4,38},{5,39},{6,54},{7,55},{8,74},{9,75... | collective-permute-start | bytes 442376 | tf_op jit(solution)/shard_map/ppermute | solution.py:360
  37.5 0.7 collective-permute-start.7
  38.2 0.8 collective-permute-done.16
  39.0 5.4 %collective-permute-start.19 = (bf16[2,192,384]{2,1,0:T(8,128)(2,1)S(1)}, bf16[2,192,384]{2,1,0:T(8,128)(2,1)S(1)}, u32[]{:S(2)}, u32[]{:S(2)}) collective-permute-start(bf16[2,192,384]{2,1,0:T(8,128)(2,1)S(1)} %pad_maximum_fusion.1.refs_0_), channel_id=1, source_target_pairs={{0,96},{32,0},{64,32},{96,64},{1,97},{33,1},{65,33},{97,65},{2,98}... | collective-permute-start | bytes 884744 | tf_op jit(solution)/shard_map/ppermute | solution.py:381
  44.5 3.6 %collective-permute-start.18 = (bf16[2,192,384]{2,1,0:T(8,128)(2,1)S(1)}, bf16[2,192,384]{2,1,0:T(8,128)(2,1)S(1)}, u32[]{:S(2)}, u32[]{:S(2)}) collective-permute-start(bf16[2,192,384]{2,1,0:T(8,128)(2,1)S(1)} %pad_maximum_fusion.1.refs_0_), channel_id=1, source_target_pairs={{0,64},{32,96},{64,0},{96,32},{1,65},{33,97},{65,1},{97,33},{2,66}... | collective-permute-start | bytes 884744 | tf_op jit(solution)/shard_map/ppermute | solution.py:381
  48.2 4.2 %collective-permute-start.11 = (bf16[2,192,384]{2,1,0:T(8,128)(2,1)S(1)}, bf16[2,192,384]{2,1,0:T(8,128)(2,1)S(1)}, u32[]{:S(2)}, u32[]{:S(2)}) collective-permute-start(bf16[2,192,384]{2,1,0:T(8,128)(2,1)S(1)} %pad_maximum_fusion.refs_0_), channel_id=1, source_target_pairs={{0,12},{4,0},{8,4},{12,8},{1,13},{5,1},{9,5},{13,9},{2,14},{6,2},{... | collective-permute-start | bytes 884744 | tf_op jit(solution)/shard_map/ppermute | solution.py:381
  52.4 3.4 %collective-permute-start.10 = (bf16[2,192,384]{2,1,0:T(8,128)(2,1)S(1)}, bf16[2,192,384]{2,1,0:T(8,128)(2,1)S(1)}, u32[]{:S(2)}, u32[]{:S(2)}) collective-permute-start(bf16[2,192,384]{2,1,0:T(8,128)(2,1)S(1)} %pad_maximum_fusion.refs_0_), channel_id=1, source_target_pairs={{0,8},{4,12},{8,0},{12,4},{1,9},{5,13},{9,1},{13,5},{2,10},{6,14},... | collective-permute-start | bytes 884744 | tf_op jit(solution)/shard_map/ppermute | solution.py:381
  55.8 1.3 %collective-permute-start.9 = (bf16[2,192,384]{2,1,0:T(8,128)(2,1)S(1)}, bf16[2,192,384]{2,1,0:T(8,128)(2,1)S(1)}, u32[]{:S(2)}, u32[]{:S(2)}) collective-permute-start(bf16[2,192,384]{2,1,0:T(8,128)(2,1)S(1)} %pad_maximum_fusion.refs_0_), channel_id=1, source_target_pairs={{0,4},{4,8},{8,12},{12,0},{1,5},{5,9},{9,13},{13,1},{2,6},{6,10},{... | collective-permute-start | bytes 884744 | tf_op jit(solution)/shard_map/ppermute | solution.py:381
  57.2 2.1 %collective-permute-start.17 = (bf16[2,192,384]{2,1,0:T(8,128)(2,1)S(1)}, bf16[2,192,384]{2,1,0:T(8,128)(2,1)S(1)}, u32[]{:S(2)}, u32[]{:S(2)}) collective-permute-start(bf16[2,192,384]{2,1,0:T(8,128)(2,1)S(1)} %pad_maximum_fusion.1.refs_0_), channel_id=1, source_target_pairs={{0,32},{32,64},{64,96},{96,0},{1,33},{33,65},{65,97},{97,1},{2,34}... | collective-permute-start | bytes 884744 | tf_op jit(solution)/shard_map/ppermute | solution.py:381
  59.2 0.5 collective-permute-start.15
  59.7 0.9 collective-permute-done.10.refs_2_
  60.6 3.2 %collective-permute-done.9.refs_1_ = bf16[2,192,384]{2,1,0:T(8,128)(2,1)S(1)} collective-permute-done((bf16[2,192,384]{2,1,0:T(8,128)(2,1)S(1)}, bf16[2,192,384]{2,1,0:T(8,128)(2,1)S(1)}, u32[]{:S(2)}, u32[]{:S(2)}) %collective-permute-start.9) | collective-permute-done | bytes 294944 | tf_op jit(solution)/shard_map/ppermute | solution.py:381
  63.8 1.3 %collective-permute-done.17.refs_1_ = bf16[2,192,384]{2,1,0:T(8,128)(2,1)S(1)} collective-permute-done((bf16[2,192,384]{2,1,0:T(8,128)(2,1)S(1)}, bf16[2,192,384]{2,1,0:T(8,128)(2,1)S(1)}, u32[]{:S(2)}, u32[]{:S(2)}) %collective-permute-start.17) | collective-permute-done | bytes 294944 | tf_op jit(solution)/shard_map/ppermute | solution.py:381
  65.1 0.3 collective-permute-done.13.refs_5_
  65.4 1.6 %next_memory.1.lhs_ref = bf16[384,3072]{1,0:T(8,128)(2,1)S(1)} custom-call(s32[5]{0:T(128)S(1)} %stack.41.place_ref, bf16[384,3072]{1,0:T(8,128)(2,1)S(1)} %get-tuple-element.62.memory_ref, bf16[2,192,384]{2,1,0:T(8,128)(2,1)S(1)} %pad_maximum_fusion.refs_0_, bf16[2,192,384]{2,1,0:T(8,128)(2,1)S(1)} %collective-permute-done.9.refs_1_, ...), custom_call_target="tpu_custom_call" | custom-call | flops 1179648 | bytes 7077888 | tf_op jit(solution)/shard_map/next_memory/pallas_call | solution.py:227
  67.0 2.7 %half_product.4 = (bf16[192,384]{1,0:T(8,128)(2,1)S(1)}, bf16[192,384]{1,0:T(8,128)(2,1)S(1)}, bf16[192,384]{1,0:T(8,128)(2,1)S(1)}, bf16[192,384]{1,0:T(8,128)(2,1)S(1)}) custom-call(s32[5]{0:T(128)S(1)} %stack.41.place_ref, bf16[384,3072]{1,0:T(8,128)(2,1)S(1)} %next_memory.1.lhs_ref, bf16[3072,768]{1,0:T(8,128)(2,1)S(1)} %get-tuple-element.81.resident_ref), custom_call_target="tpu_custom_call" | custom-call | flops 1811939328 | bytes 294912 | tf_op jit(solution)/shard_map/half_product/pallas_call | solution.py:81
  69.8 2.3 %collective-permute-start.21 = (bf16[192,384]{1,0:T(8,128)(2,1)S(1)}, bf16[192,384]{1,0:T(8,128)(2,1)S(1)}, u32[]{:S(2)}, u32[]{:S(2)}) collective-permute-start(bf16[192,384]{1,0:T(8,128)(2,1)S(1)} %get-tuple-element.87), channel_id=1, source_target_pairs={{0,32},{1,33},{2,34},{3,35},{4,36},{5,37},{6,38},{7,39},{8,40},{9,... | collective-permute-start | bytes 442376 | tf_op jit(solution)/shard_map/ppermute | solution.py:360
  72.1 3.1 %collective-permute-start.22 = (bf16[192,384]{1,0:T(8,128)(2,1)S(1)}, bf16[192,384]{1,0:T(8,128)(2,1)S(1)}, u32[]{:S(2)}, u32[]{:S(2)}) collective-permute-start(bf16[192,384]{1,0:T(8,128)(2,1)S(1)} %get-tuple-element.88), channel_id=1, source_target_pairs={{0,112},{1,113},{2,114},{3,115},{4,116},{5,117},{6,118},{7,119},{8... | collective-permute-start | bytes 442376 | tf_op jit(solution)/shard_map/ppermute | solution.py:360
  75.2 0.7 collective-permute-start.23
  75.9 2.7 %half_product.5 = (bf16[192,384]{1,0:T(8,128)(2,1)S(1)}, bf16[192,384]{1,0:T(8,128)(2,1)S(1)}, bf16[192,384]{1,0:T(8,128)(2,1)S(1)}, bf16[192,384]{1,0:T(8,128)(2,1)S(1)}) custom-call(s32[5]{0:T(128)S(1)} %stack.41.place_ref, bf16[384,3072]{1,0:T(8,128)(2,1)S(1)} %next_memory.1.lhs_ref, bf16[3072,768]{1,0:T(8,128)(2,1)S(1)} %get-tuple-element.91.resident_ref), custom_call_target="tpu_custom_call" | custom-call | flops 1811939328 | bytes 294912 | tf_op jit(solution)/shard_map/half_product/pallas_call | solution.py:81
  78.6 0.9 collective-permute-start.24
  79.5 3.0 %collective-permute-start.25 = (bf16[192,384]{1,0:T(8,128)(2,1)S(1)}, bf16[192,384]{1,0:T(8,128)(2,1)S(1)}, u32[]{:S(2)}, u32[]{:S(2)}) collective-permute-start(bf16[192,384]{1,0:T(8,128)(2,1)S(1)} %get-tuple-element.93), channel_id=1, source_target_pairs={{0,64},{1,65},{2,66},{3,67},{4,68},{5,69},{6,70},{7,71},{8,72},{9,... | collective-permute-start | bytes 442376 | tf_op jit(solution)/shard_map/ppermute | solution.py:360
  82.5 1.2 %collective-permute-start.26 = (bf16[192,384]{1,0:T(8,128)(2,1)S(1)}, bf16[192,384]{1,0:T(8,128)(2,1)S(1)}, u32[]{:S(2)}, u32[]{:S(2)}) collective-permute-start(bf16[192,384]{1,0:T(8,128)(2,1)S(1)} %get-tuple-element.94), channel_id=1, source_target_pairs={{0,16},{1,17},{2,18},{3,19},{4,20},{5,21},{6,22},{7,23},{8,24},{9,... | collective-permute-start | bytes 442376 | tf_op jit(solution)/shard_map/ppermute | solution.py:360
  83.7 5.3 %collective-permute-done.23.refs_3_ = bf16[192,384]{1,0:T(8,128)(2,1)S(1)} collective-permute-done((bf16[192,384]{1,0:T(8,128)(2,1)S(1)}, bf16[192,384]{1,0:T(8,128)(2,1)S(1)}, u32[]{:S(2)}, u32[]{:S(2)}) %collective-permute-start.23) | collective-permute-done | bytes 147488 | tf_op jit(solution)/shard_map/ppermute | solution.py:360
  89.0 0.3 collective-permute-done.26.refs_6_
  89.3 1.4 %second_solve.1.refs_0_ = bf16[192,384]{1,0:T(8,128)(2,1)S(1)} custom-call(s32[5]{0:T(128)S(1)} %stack.41.place_ref, bf16[192,384]{1,0:T(8,128)(2,1)S(1)} %collective-permute-done.20.refs_0_, bf16[192,384]{1,0:T(8,128)(2,1)S(1)} %collective-permute-done.21.refs_1_, bf16[192,384]{1,0:T(8,128)(2,1)S(1)} %collective-permute-done.22.refs_2_, ...), custom_call_target="tpu_custom_call" | custom-call | flops 339738624 | bytes 1769472 | tf_op jit(solution)/shard_map/second_solve/pallas_call | solution.py:42
  90.7 2.3 %collective-permute-start.33 = (bf16[192,384]{1,0:T(8,128)(2,1)S(1)}, bf16[192,384]{1,0:T(8,128)(2,1)S(1)}, u32[]{:S(2)}, u32[]{:S(2)}) collective-permute-start(bf16[192,384]{1,0:T(8,128)(2,1)S(1)} %second_solve.1.refs_0_), channel_id=1, source_target_pairs={{0,112},{1,113},{2,114},{3,115},{4,116},{5,117},{6,118},{7,119},{8... | collective-permute-start | bytes 442376 | tf_op jit(solution)/shard_map/ppermute | solution.py:360
  93.1 2.7 %collective-permute-start.31 = (bf16[192,384]{1,0:T(8,128)(2,1)S(1)}, bf16[192,384]{1,0:T(8,128)(2,1)S(1)}, u32[]{:S(2)}, u32[]{:S(2)}) collective-permute-start(bf16[192,384]{1,0:T(8,128)(2,1)S(1)} %second_solve.1.refs_0_), channel_id=1, source_target_pairs={{0,80},{1,81},{2,82},{3,83},{4,84},{5,85},{6,86},{7,87},{8,88},{9,... | collective-permute-start | bytes 442376 | tf_op jit(solution)/shard_map/ppermute | solution.py:360
  95.8 1.7 %collective-permute-start.30 = (bf16[192,384]{1,0:T(8,128)(2,1)S(1)}, bf16[192,384]{1,0:T(8,128)(2,1)S(1)}, u32[]{:S(2)}, u32[]{:S(2)}) collective-permute-start(bf16[192,384]{1,0:T(8,128)(2,1)S(1)} %second_solve.1.refs_0_), channel_id=1, source_target_pairs={{0,64},{1,65},{2,66},{3,67},{4,68},{5,69},{6,70},{7,71},{8,72},{9,... | collective-permute-start | bytes 442376 | tf_op jit(solution)/shard_map/ppermute | solution.py:360
  97.4 2.0 %collective-permute-start.29 = (bf16[192,384]{1,0:T(8,128)(2,1)S(1)}, bf16[192,384]{1,0:T(8,128)(2,1)S(1)}, u32[]{:S(2)}, u32[]{:S(2)}) collective-permute-start(bf16[192,384]{1,0:T(8,128)(2,1)S(1)} %second_solve.1.refs_0_), channel_id=1, source_target_pairs={{0,48},{1,49},{2,50},{3,51},{4,52},{5,53},{6,54},{7,55},{8,56},{9,... | collective-permute-start | bytes 442376 | tf_op jit(solution)/shard_map/ppermute | solution.py:360
  99.5 5.0 %collective-permute-done.32.refs_6_ = bf16[192,384]{1,0:T(8,128)(2,1)S(1)} collective-permute-done((bf16[192,384]{1,0:T(8,128)(2,1)S(1)}, bf16[192,384]{1,0:T(8,128)(2,1)S(1)}, u32[]{:S(2)}, u32[]{:S(2)}) %collective-permute-start.32) | collective-permute-done | bytes 147488 | tf_op jit(solution)/shard_map/ppermute | solution.py:360
  104.4 2.1 %collective-permute-start.27 = (bf16[192,384]{1,0:T(8,128)(2,1)S(1)}, bf16[192,384]{1,0:T(8,128)(2,1)S(1)}, u32[]{:S(2)}, u32[]{:S(2)}) collective-permute-start(bf16[192,384]{1,0:T(8,128)(2,1)S(1)} %second_solve.1.refs_0_), channel_id=1, source_target_pairs={{0,16},{1,17},{2,18},{3,19},{4,20},{5,21},{6,22},{7,23},{8,24},{9,... | collective-permute-start | bytes 442376 | tf_op jit(solution)/shard_map/ppermute | solution.py:360
  106.6 2.0 %join_one.1.refs_8_ = bf16[2,384,1536]{2,1,0:T(8,128)(2,1)} custom-call(s32[5]{0:T(128)S(1)} %stack.41.place_ref, bf16[2,192,384]{2,1,0:T(8,128)(2,1)S(1)} %pad_maximum_fusion.1.refs_0_, bf16[2,192,384]{2,1,0:T(8,128)(2,1)S(1)} %collective-permute-done.17.refs_1_, bf16[2,192,384]{2,1,0:T(8,128)(2,1)S(1)} %collective-permute-done.18.refs_2_, ...), custom_call_target="tpu_custom_call" | custom-call | flops 589824 | bytes 2359296 | tf_op jit(solution)/shard_map/join_one/pallas_call | solution.py:42
  108.6 1.1 collective-permute-done.28.refs_2_
  109.7 2.0 %join_two.1 = bf16[2,384,1536]{2,1,0:T(8,128)(2,1)} custom-call(s32[5]{0:T(128)S(1)} %stack.41.place_ref, bf16[192,384]{1,0:T(8,128)(2,1)S(1)} %second_solve.1.refs_0_, bf16[192,384]{1,0:T(8,128)(2,1)S(1)} %collective-permute-done.27.refs_1_, bf16[192,384]{1,0:T(8,128)(2,1)S(1)} %collective-permute-done.28.refs_2_, ...), custom_call_target="tpu_custom_call", output_to_operand_aliasing={{}: (9, {})} | custom-call | flops 589824 | bytes 2359296 | tf_op jit(solution)/shard_map/join_two/pallas_call | solution.py:42
  (39 shorter events, 0.4 us)
Async XLA Ops:
  6.6 12.4 %collective-permute-start.1 = (bf16[192,384]{1,0:T(8,128)(2,1)S(1)}, bf16[192,384]{1,0:T(8,128)(2,1)S(1)}, u32[]{:S(2)}, u32[]{:S(2)}) collective-permute-start(bf16[192,384]{1,0:T(8,128)(2,1)S(1)} %get-tuple-element.54), channel_id=1, source_target_pairs={{0,32},{1,33},{2,34},{3,35},{4,36},{5,37},{6,38},{7,39},{8,40},{9,... | collective-permute-start | bytes 442376 | tf_op jit(solution)/shard_map/ppermute | solution.py:360
  8.3 12.2 %collective-permute-start = (bf16[192,384]{1,0:T(8,128)(2,1)S(1)}, bf16[192,384]{1,0:T(8,128)(2,1)S(1)}, u32[]{:S(2)}, u32[]{:S(2)}) collective-permute-start(bf16[192,384]{1,0:T(8,128)(2,1)S(1)} %get-tuple-element.55), channel_id=1, source_target_pairs={{0,48},{1,49},{2,50},{3,51},{4,52},{5,53},{6,54},{7,55},{8,56},{9,... | collective-permute-start | bytes 442376 | tf_op jit(solution)/shard_map/ppermute | solution.py:360
  10.1 10.9 %collective-permute-start.3 = (bf16[192,384]{1,0:T(8,128)(2,1)S(1)}, bf16[192,384]{1,0:T(8,128)(2,1)S(1)}, u32[]{:S(2)}, u32[]{:S(2)}) collective-permute-start(bf16[192,384]{1,0:T(8,128)(2,1)S(1)} %get-tuple-element.56), channel_id=1, source_target_pairs={{0,96},{1,97},{2,98},{3,99},{4,100},{5,101},{6,102},{7,103},{8,104... | collective-permute-start | bytes 442376 | tf_op jit(solution)/shard_map/ppermute | solution.py:360
  13.2 13.6 %collective-permute-start.2 = (bf16[192,384]{1,0:T(8,128)(2,1)S(1)}, bf16[192,384]{1,0:T(8,128)(2,1)S(1)}, u32[]{:S(2)}, u32[]{:S(2)}) collective-permute-start(bf16[192,384]{1,0:T(8,128)(2,1)S(1)} %get-tuple-element.57), channel_id=1, source_target_pairs={{0,112},{1,113},{2,114},{3,115},{4,116},{5,117},{6,118},{7,119},{8... | collective-permute-start | bytes 442376 | tf_op jit(solution)/shard_map/ppermute | solution.py:360
  13.2 7.8 %copy-start.1 = (f32[32,32]{1,0:T(8,128)S(1)}, f32[32,32]{1,0:T(8,128)}, u32[]{:S(2)}) copy-start(f32[32,32]{1,0:T(8,128)} %param.9) | copy-start | bytes 12292
  15.8 16.1 %collective-permute-start.4 = (bf16[192,384]{1,0:T(8,128)(2,1)S(1)}, bf16[192,384]{1,0:T(8,128)(2,1)S(1)}, u32[]{:S(2)}, u32[]{:S(2)}) collective-permute-start(bf16[192,384]{1,0:T(8,128)(2,1)S(1)} %get-tuple-element.67), channel_id=1, source_target_pairs={{0,80},{1,81},{2,82},{3,83},{4,84},{5,85},{6,86},{7,87},{8,88},{9,... | collective-permute-start | bytes 442376 | tf_op jit(solution)/shard_map/ppermute | solution.py:360
  19.0 12.9 %collective-permute-start.5 = (bf16[192,384]{1,0:T(8,128)(2,1)S(1)}, bf16[192,384]{1,0:T(8,128)(2,1)S(1)}, u32[]{:S(2)}, u32[]{:S(2)}) collective-permute-start(bf16[192,384]{1,0:T(8,128)(2,1)S(1)} %get-tuple-element.68), channel_id=1, source_target_pairs={{0,64},{1,65},{2,66},{3,67},{4,68},{5,69},{6,70},{7,71},{8,72},{9,... | collective-permute-start | bytes 442376 | tf_op jit(solution)/shard_map/ppermute | solution.py:360
  20.6 11.4 %collective-permute-start.6 = (bf16[192,384]{1,0:T(8,128)(2,1)S(1)}, bf16[192,384]{1,0:T(8,128)(2,1)S(1)}, u32[]{:S(2)}, u32[]{:S(2)}) collective-permute-start(bf16[192,384]{1,0:T(8,128)(2,1)S(1)} %get-tuple-element.69), channel_id=1, source_target_pairs={{0,16},{1,17},{2,18},{3,19},{4,20},{5,21},{6,22},{7,23},{8,24},{9,... | collective-permute-start | bytes 442376 | tf_op jit(solution)/shard_map/ppermute | solution.py:360
  26.7 5.2 %copy-start = (f32[2,384,384]{2,1,0:T(8,128)S(1)}, f32[2,384,384]{2,1,0:T(8,128)}, u32[]{:S(2)}) copy-start(f32[2,384,384]{2,1,0:T(8,128)} %refs_9_.3) | copy-start | bytes 3538948
  33.8 5.2 %collective-permute-start.16 = (bf16[192,384]{1,0:T(8,128)(2,1)S(1)}, bf16[192,384]{1,0:T(8,128)(2,1)S(1)}, u32[]{:S(2)}, u32[]{:S(2)}) collective-permute-start(bf16[192,384]{1,0:T(8,128)(2,1)S(1)} %get-tuple-element.72), channel_id=1, source_target_pairs={{0,16},{16,0},{1,17},{17,1},{2,18},{18,2},{3,19},{19,3},{4,20},{20... | collective-permute-start | bytes 442376 | tf_op jit(solution)/shard_map/ppermute | solution.py:411
  33.9 14.3 %collective-permute-start.8 = (bf16[192,384]{1,0:T(8,128)(2,1)S(1)}, bf16[192,384]{1,0:T(8,128)(2,1)S(1)}, u32[]{:S(2)}, u32[]{:S(2)}) collective-permute-start(bf16[192,384]{1,0:T(8,128)(2,1)S(1)} %get-tuple-element.71), channel_id=1, source_target_pairs={{0,2},{1,3},{2,18},{3,19},{4,38},{5,39},{6,54},{7,55},{8,74},{9,75... | collective-permute-start | bytes 442376 | tf_op jit(solution)/shard_map/ppermute | solution.py:360
  37.5 10.6 %collective-permute-start.7 = (bf16[192,384]{1,0:T(8,128)(2,1)S(1)}, bf16[192,384]{1,0:T(8,128)(2,1)S(1)}, u32[]{:S(2)}, u32[]{:S(2)}) collective-permute-start(bf16[192,384]{1,0:T(8,128)(2,1)S(1)} %get-tuple-element.71), channel_id=1, source_target_pairs={{0,0},{1,1},{2,16},{3,17},{4,36},{5,37},{6,52},{7,53},{8,72},{9,73... | collective-permute-start | bytes 442376 | tf_op jit(solution)/shard_map/ppermute | solution.py:360
  39.0 18.1 %collective-permute-start.19 = (bf16[2,192,384]{2,1,0:T(8,128)(2,1)S(1)}, bf16[2,192,384]{2,1,0:T(8,128)(2,1)S(1)}, u32[]{:S(2)}, u32[]{:S(2)}) collective-permute-start(bf16[2,192,384]{2,1,0:T(8,128)(2,1)S(1)} %pad_maximum_fusion.1.refs_0_), channel_id=1, source_target_pairs={{0,96},{32,0},{64,32},{96,64},{1,97},{33,1},{65,33},{97,65},{2,98}... | collective-permute-start | bytes 884744 | tf_op jit(solution)/shard_map/ppermute | solution.py:381
  44.5 14.8 %collective-permute-start.18 = (bf16[2,192,384]{2,1,0:T(8,128)(2,1)S(1)}, bf16[2,192,384]{2,1,0:T(8,128)(2,1)S(1)}, u32[]{:S(2)}, u32[]{:S(2)}) collective-permute-start(bf16[2,192,384]{2,1,0:T(8,128)(2,1)S(1)} %pad_maximum_fusion.1.refs_0_), channel_id=1, source_target_pairs={{0,64},{32,96},{64,0},{96,32},{1,65},{33,97},{65,1},{97,33},{2,66}... | collective-permute-start | bytes 884744 | tf_op jit(solution)/shard_map/ppermute | solution.py:381
  48.2 11.1 %collective-permute-start.11 = (bf16[2,192,384]{2,1,0:T(8,128)(2,1)S(1)}, bf16[2,192,384]{2,1,0:T(8,128)(2,1)S(1)}, u32[]{:S(2)}, u32[]{:S(2)}) collective-permute-start(bf16[2,192,384]{2,1,0:T(8,128)(2,1)S(1)} %pad_maximum_fusion.refs_0_), channel_id=1, source_target_pairs={{0,12},{4,0},{8,4},{12,8},{1,13},{5,1},{9,5},{13,9},{2,14},{6,2},{... | collective-permute-start | bytes 884744 | tf_op jit(solution)/shard_map/ppermute | solution.py:381
  52.4 8.2 %collective-permute-start.10 = (bf16[2,192,384]{2,1,0:T(8,128)(2,1)S(1)}, bf16[2,192,384]{2,1,0:T(8,128)(2,1)S(1)}, u32[]{:S(2)}, u32[]{:S(2)}) collective-permute-start(bf16[2,192,384]{2,1,0:T(8,128)(2,1)S(1)} %pad_maximum_fusion.refs_0_), channel_id=1, source_target_pairs={{0,8},{4,12},{8,0},{12,4},{1,9},{5,13},{9,1},{13,5},{2,10},{6,14},... | collective-permute-start | bytes 884744 | tf_op jit(solution)/shard_map/ppermute | solution.py:381
  55.8 8.0 %collective-permute-start.9 = (bf16[2,192,384]{2,1,0:T(8,128)(2,1)S(1)}, bf16[2,192,384]{2,1,0:T(8,128)(2,1)S(1)}, u32[]{:S(2)}, u32[]{:S(2)}) collective-permute-start(bf16[2,192,384]{2,1,0:T(8,128)(2,1)S(1)} %pad_maximum_fusion.refs_0_), channel_id=1, source_target_pairs={{0,4},{4,8},{8,12},{12,0},{1,5},{5,9},{9,13},{13,1},{2,6},{6,10},{... | collective-permute-start | bytes 884744 | tf_op jit(solution)/shard_map/ppermute | solution.py:381
  57.2 7.9 %collective-permute-start.17 = (bf16[2,192,384]{2,1,0:T(8,128)(2,1)S(1)}, bf16[2,192,384]{2,1,0:T(8,128)(2,1)S(1)}, u32[]{:S(2)}, u32[]{:S(2)}) collective-permute-start(bf16[2,192,384]{2,1,0:T(8,128)(2,1)S(1)} %pad_maximum_fusion.1.refs_0_), channel_id=1, source_target_pairs={{0,32},{32,64},{64,96},{96,0},{1,33},{33,65},{65,97},{97,1},{2,34}... | collective-permute-start | bytes 884744 | tf_op jit(solution)/shard_map/ppermute | solution.py:381
  59.2 5.9 %collective-permute-start.12 = (bf16[2,192,384]{2,1,0:T(8,128)(2,1)S(1)}, bf16[2,192,384]{2,1,0:T(8,128)(2,1)S(1)}, u32[]{:S(2)}, u32[]{:S(2)}) collective-permute-start(bf16[2,192,384]{2,1,0:T(8,128)(2,1)S(1)} %pad_maximum_fusion.refs_0_), channel_id=1, source_target_pairs={{0,1},{1,0},{2,3},{3,2},{4,5},{5,4},{6,7},{7,6},{8,9},{9,8},{10,11... | collective-permute-start | bytes 884744 | tf_op jit(solution)/shard_map/ppermute | solution.py:410
  59.2 5.9 %collective-permute-start.15 = (bf16[2,192,384]{2,1,0:T(8,128)(2,1)S(1)}, bf16[2,192,384]{2,1,0:T(8,128)(2,1)S(1)}, u32[]{:S(2)}, u32[]{:S(2)}) collective-permute-start(bf16[2,192,384]{2,1,0:T(8,128)(2,1)S(1)} %collective-permute-done.11.refs_3_), channel_id=1, source_target_pairs={{0,1},{1,0},{2,3},{3,2},{4,5},{5,4},{6,7},{7,6},{8,9},{9,8},{10,11... | collective-permute-start | bytes 884744 | tf_op jit(solution)/shard_map/ppermute | solution.py:410
  60.6 4.5 %collective-permute-start.14 = (bf16[2,192,384]{2,1,0:T(8,128)(2,1)S(1)}, bf16[2,192,384]{2,1,0:T(8,128)(2,1)S(1)}, u32[]{:S(2)}, u32[]{:S(2)}) collective-permute-start(bf16[2,192,384]{2,1,0:T(8,128)(2,1)S(1)} %collective-permute-done.10.refs_2_), channel_id=1, source_target_pairs={{0,1},{1,0},{2,3},{3,2},{4,5},{5,4},{6,7},{7,6},{8,9},{9,8},{10,11... | collective-permute-start | bytes 884744 | tf_op jit(solution)/shard_map/ppermute | solution.py:410
  63.8 1.6 %collective-permute-start.13 = (bf16[2,192,384]{2,1,0:T(8,128)(2,1)S(1)}, bf16[2,192,384]{2,1,0:T(8,128)(2,1)S(1)}, u32[]{:S(2)}, u32[]{:S(2)}) collective-permute-start(bf16[2,192,384]{2,1,0:T(8,128)(2,1)S(1)} %collective-permute-done.9.refs_1_), channel_id=1, source_target_pairs={{0,1},{1,0},{2,3},{3,2},{4,5},{5,4},{6,7},{7,6},{8,9},{9,8},{10,11... | collective-permute-start | bytes 884744 | tf_op jit(solution)/shard_map/ppermute | solution.py:410
  69.7 9.8 %collective-permute-start.20 = (bf16[192,384]{1,0:T(8,128)(2,1)S(1)}, bf16[192,384]{1,0:T(8,128)(2,1)S(1)}, u32[]{:S(2)}, u32[]{:S(2)}) collective-permute-start(bf16[192,384]{1,0:T(8,128)(2,1)S(1)} %get-tuple-element.86), channel_id=1, source_target_pairs={{0,48},{1,49},{2,50},{3,51},{4,52},{5,53},{6,54},{7,55},{8,56},{9,... | collective-permute-start | bytes 442376 | tf_op jit(solution)/shard_map/ppermute | solution.py:360
  69.8 12.7 %collective-permute-start.21 = (bf16[192,384]{1,0:T(8,128)(2,1)S(1)}, bf16[192,384]{1,0:T(8,128)(2,1)S(1)}, u32[]{:S(2)}, u32[]{:S(2)}) collective-permute-start(bf16[192,384]{1,0:T(8,128)(2,1)S(1)} %get-tuple-element.87), channel_id=1, source_target_pairs={{0,32},{1,33},{2,34},{3,35},{4,36},{5,37},{6,38},{7,39},{8,40},{9,... | collective-permute-start | bytes 442376 | tf_op jit(solution)/shard_map/ppermute | solution.py:360
  72.1 11.6 %collective-permute-start.22 = (bf16[192,384]{1,0:T(8,128)(2,1)S(1)}, bf16[192,384]{1,0:T(8,128)(2,1)S(1)}, u32[]{:S(2)}, u32[]{:S(2)}) collective-permute-start(bf16[192,384]{1,0:T(8,128)(2,1)S(1)} %get-tuple-element.88), channel_id=1, source_target_pairs={{0,112},{1,113},{2,114},{3,115},{4,116},{5,117},{6,118},{7,119},{8... | collective-permute-start | bytes 442376 | tf_op jit(solution)/shard_map/ppermute | solution.py:360
  75.2 13.8 %collective-permute-start.23 = (bf16[192,384]{1,0:T(8,128)(2,1)S(1)}, bf16[192,384]{1,0:T(8,128)(2,1)S(1)}, u32[]{:S(2)}, u32[]{:S(2)}) collective-permute-start(bf16[192,384]{1,0:T(8,128)(2,1)S(1)} %get-tuple-element.89), channel_id=1, source_target_pairs={{0,96},{1,97},{2,98},{3,99},{4,100},{5,101},{6,102},{7,103},{8,104... | collective-permute-start | bytes 442376 | tf_op jit(solution)/shard_map/ppermute | solution.py:360
  78.6 10.4 %collective-permute-start.24 = (bf16[192,384]{1,0:T(8,128)(2,1)S(1)}, bf16[192,384]{1,0:T(8,128)(2,1)S(1)}, u32[]{:S(2)}, u32[]{:S(2)}) collective-permute-start(bf16[192,384]{1,0:T(8,128)(2,1)S(1)} %get-tuple-element.92), channel_id=1, source_target_pairs={{0,80},{1,81},{2,82},{3,83},{4,84},{5,85},{6,86},{7,87},{8,88},{9,... | collective-permute-start | bytes 442376 | tf_op jit(solution)/shard_map/ppermute | solution.py:360
  79.5 9.5 %collective-permute-start.25 = (bf16[192,384]{1,0:T(8,128)(2,1)S(1)}, bf16[192,384]{1,0:T(8,128)(2,1)S(1)}, u32[]{:S(2)}, u32[]{:S(2)}) collective-permute-start(bf16[192,384]{1,0:T(8,128)(2,1)S(1)} %get-tuple-element.93), channel_id=1, source_target_pairs={{0,64},{1,65},{2,66},{3,67},{4,68},{5,69},{6,70},{7,71},{8,72},{9,... | collective-permute-start | bytes 442376 | tf_op jit(solution)/shard_map/ppermute | solution.py:360
  82.5 6.8 %collective-permute-start.26 = (bf16[192,384]{1,0:T(8,128)(2,1)S(1)}, bf16[192,384]{1,0:T(8,128)(2,1)S(1)}, u32[]{:S(2)}, u32[]{:S(2)}) collective-permute-start(bf16[192,384]{1,0:T(8,128)(2,1)S(1)} %get-tuple-element.94), channel_id=1, source_target_pairs={{0,16},{1,17},{2,18},{3,19},{4,20},{5,21},{6,22},{7,23},{8,24},{9,... | collective-permute-start | bytes 442376 | tf_op jit(solution)/shard_map/ppermute | solution.py:360
  90.7 8.7 %collective-permute-start.33 = (bf16[192,384]{1,0:T(8,128)(2,1)S(1)}, bf16[192,384]{1,0:T(8,128)(2,1)S(1)}, u32[]{:S(2)}, u32[]{:S(2)}) collective-permute-start(bf16[192,384]{1,0:T(8,128)(2,1)S(1)} %second_solve.1.refs_0_), channel_id=1, source_target_pairs={{0,112},{1,113},{2,114},{3,115},{4,116},{5,117},{6,118},{7,119},{8... | collective-permute-start | bytes 442376 | tf_op jit(solution)/shard_map/ppermute | solution.py:360
  93.0 11.4 %collective-permute-start.32 = (bf16[192,384]{1,0:T(8,128)(2,1)S(1)}, bf16[192,384]{1,0:T(8,128)(2,1)S(1)}, u32[]{:S(2)}, u32[]{:S(2)}) collective-permute-start(bf16[192,384]{1,0:T(8,128)(2,1)S(1)} %second_solve.1.refs_0_), channel_id=1, source_target_pairs={{0,96},{1,97},{2,98},{3,99},{4,100},{5,101},{6,102},{7,103},{8,104... | collective-permute-start | bytes 442376 | tf_op jit(solution)/shard_map/ppermute | solution.py:360
  93.1 15.5 %collective-permute-start.31 = (bf16[192,384]{1,0:T(8,128)(2,1)S(1)}, bf16[192,384]{1,0:T(8,128)(2,1)S(1)}, u32[]{:S(2)}, u32[]{:S(2)}) collective-permute-start(bf16[192,384]{1,0:T(8,128)(2,1)S(1)} %second_solve.1.refs_0_), channel_id=1, source_target_pairs={{0,80},{1,81},{2,82},{3,83},{4,84},{5,85},{6,86},{7,87},{8,88},{9,... | collective-permute-start | bytes 442376 | tf_op jit(solution)/shard_map/ppermute | solution.py:360
  95.8 12.8 %collective-permute-start.30 = (bf16[192,384]{1,0:T(8,128)(2,1)S(1)}, bf16[192,384]{1,0:T(8,128)(2,1)S(1)}, u32[]{:S(2)}, u32[]{:S(2)}) collective-permute-start(bf16[192,384]{1,0:T(8,128)(2,1)S(1)} %second_solve.1.refs_0_), channel_id=1, source_target_pairs={{0,64},{1,65},{2,66},{3,67},{4,68},{5,69},{6,70},{7,71},{8,72},{9,... | collective-permute-start | bytes 442376 | tf_op jit(solution)/shard_map/ppermute | solution.py:360
  97.4 11.2 %collective-permute-start.29 = (bf16[192,384]{1,0:T(8,128)(2,1)S(1)}, bf16[192,384]{1,0:T(8,128)(2,1)S(1)}, u32[]{:S(2)}, u32[]{:S(2)}) collective-permute-start(bf16[192,384]{1,0:T(8,128)(2,1)S(1)} %second_solve.1.refs_0_), channel_id=1, source_target_pairs={{0,48},{1,49},{2,50},{3,51},{4,52},{5,53},{6,54},{7,55},{8,56},{9,... | collective-permute-start | bytes 442376 | tf_op jit(solution)/shard_map/ppermute | solution.py:360
  99.5 10.2 %collective-permute-start.28 = (bf16[192,384]{1,0:T(8,128)(2,1)S(1)}, bf16[192,384]{1,0:T(8,128)(2,1)S(1)}, u32[]{:S(2)}, u32[]{:S(2)}) collective-permute-start(bf16[192,384]{1,0:T(8,128)(2,1)S(1)} %second_solve.1.refs_0_), channel_id=1, source_target_pairs={{0,32},{1,33},{2,34},{3,35},{4,36},{5,37},{6,38},{7,39},{8,40},{9,... | collective-permute-start | bytes 442376 | tf_op jit(solution)/shard_map/ppermute | solution.py:360
  104.4 5.2 %collective-permute-start.27 = (bf16[192,384]{1,0:T(8,128)(2,1)S(1)}, bf16[192,384]{1,0:T(8,128)(2,1)S(1)}, u32[]{:S(2)}, u32[]{:S(2)}) collective-permute-start(bf16[192,384]{1,0:T(8,128)(2,1)S(1)} %second_solve.1.refs_0_), channel_id=1, source_target_pairs={{0,16},{1,17},{2,18},{3,19},{4,20},{5,21},{6,22},{7,23},{8,24},{9,... | collective-permute-start | bytes 442376 | tf_op jit(solution)/shard_map/ppermute | solution.py:360

commit v5 on v4

--- a/solution.py
+++ b/solution.py
@@ -34,28 +34,6 @@
     return pl.CostEstimate(flops=flops, bytes_accessed=nbytes, transcendentals=0)
 
 
-def whole(shape):
-    return pl.BlockSpec(shape, lambda i, place: (0,) * len(shape))
-
-
-def placed_call(kernel, place, args, in_specs, out_specs, out_shape, name, limit, estimate, grid=1, scratch=(), aliases=None):
-    return pl.pallas_call(
-        kernel,
-        grid_spec=pltpu.PrefetchScalarGridSpec(
-            num_scalar_prefetch=1,
-            grid=(grid,),
-            in_specs=in_specs,
-            out_specs=out_specs,
-            scratch_shapes=list(scratch),
-        ),
-        out_shape=out_shape,
-        input_output_aliases=aliases or {},
-        compiler_params=params(limit),
-        cost_estimate=cost(*estimate),
-        name=name,
-    )(place, *args)
-
-
 def position(y):
     return (y & 1) * 2 + (y >> 1)
 
@@ -110,11 +88,12 @@
     memory_copy = pltpu.make_async_copy(memory_ref.at[0], lhs_ref, sems.at[2 * TILES])
     odd = [tile_copy(odd_ref, 1, i) for i in range(TILES)]
     even = [tile_copy(even_ref, 0, i) for i in range(TILES)]
-    for copy in (memory_copy, *odd, *even):
+    for copy in (memory_copy, *odd):
         copy.start()
     memory_copy.wait()
     for i, copy in enumerate(odd):
         copy.wait()
+        even[i].start()
         at = slice(i * tile, (i + 1) * tile)
         product = jnp.dot(lhs_ref[...], odd_ref[:, at], preferred_element_type=f32)
         turned_ref[at, :] = product.T.astype(bf16)
@@ -215,11 +194,11 @@
     width = half // 4
     for side in range(2):
         for dx in range(4):
-            pair = pair_refs[side * 4 + dx]
+            near, far = pair_refs[side * 4 + dx], pair_refs[side * 4 + (dx ^ 2)]
             share = position(((place_ref[X] - dx) & 3) ^ place_ref[Y])
             start = (place_ref[C] ^ side) * half + share * width
             at = pl.ds(pl.multiple_of(start, 128), width)
-            place_pair(pair[0], pair[1], place_ref[ZH], at, out_ref, memory_ref)
+            place_pair(near[0], far[1], place_ref[ZH], at, out_ref, memory_ref)
 
 
 def next_memory(place, memory, pairs):
@@ -282,70 +261,50 @@
     refs[10][...] = solve_into(refs[:8], refs[8], refs[9])
 
 
-def solve(kernel, front, place, parts, prior, inverse, extra, outputs, name):
+def solve(kernel, place, parts, prior, inverse, extra, outputs, name):
     width, rows = prior.shape
-    return placed_call(
+    return pl.pallas_call(
         kernel,
-        place,
-        (*parts, prior, inverse, *extra),
-        [
-            *[whole(array.shape) for array in (*parts, prior)],
-            pl.BlockSpec((None, rows, rows), lambda i, place: (front, 0, 0)),
-            *[whole(array.shape) for array in extra],
-        ],
-        [whole((width, rows))] * outputs,
-        [jax.ShapeDtypeStruct((width, rows), bf16)] * outputs,
-        name,
-        10,
-        (12 * rows * rows * width, 24 * rows * width),
-    )
-
-
-def join_one_kernel(place_ref, *refs):
-    pair_refs, out_ref = refs[:4], refs[4]
-    width = out_ref.shape[1] // 4
-    for dy in range(4):
+        in_specs=[SMEM] + [VMEM] * (len(parts) + 2 + len(extra)),
+        out_specs=[VMEM] * outputs,
+        out_shape=[jax.ShapeDtypeStruct((width, rows), bf16)] * outputs,
+        compiler_params=params(8),
+        cost_estimate=cost(12 * rows * rows * width, 24 * rows * width),
+        name=name,
+    )(place, *parts, prior, inverse, *extra)
+
+
+def join_kernel(front, moves, pairs, place_ref, *refs):
+    chunk_refs, (out_ref, block_ref, sems) = refs[: 2 * len(moves)] if not pairs else refs[: len(moves)], refs[-3:]
+    width = block_ref.shape[2]
+    copies = []
+    for i, dy in enumerate(moves):
+        own, other = (chunk_refs[i][0], chunk_refs[i][1]) if pairs else (chunk_refs[2 * i][...], chunk_refs[2 * i + 1][...])
+        if i >= 2:
+            copies[i - 2].wait()
+        place_pair(own, other, place_ref[ZL], slice(None), block_ref.at[i % 2], None)
         at = pl.ds(pl.multiple_of(position((place_ref[Y] - dy) & 3) * width, 128), width)
-        place_pair(pair_refs[dy][0], pair_refs[dy][1], place_ref[ZL], at, out_ref, None)
-
-
-def join_one(place, pairs, rows, cols):
-    return placed_call(
-        join_one_kernel,
-        place,
-        pairs,
-        [whole(pair.shape) for pair in pairs],
-        pl.BlockSpec((None, rows, cols), lambda i, place: (0, 0, 0)),
-        jax.ShapeDtypeStruct((2, rows, cols), bf16),
-        "join_one",
-        10,
-        (rows * cols, 4 * rows * cols),
-    )
-
-
-def join_two_kernel(place_ref, *refs):
-    chunk_refs, out_ref = refs[:8], refs[9]
-    width = out_ref.shape[1] // 4
-    for dy in range(4):
-        at = pl.ds(pl.multiple_of(position((place_ref[Y] - dy) & 3) * width, 128), width)
-        own, other = chunk_refs[2 * dy][...], chunk_refs[2 * dy + 1][...]
-        place_pair(own, other, place_ref[ZL], at, out_ref, None)
-
-
-def join_two(place, chunks, fronts):
-    _, rows, cols = fronts.shape
-    return placed_call(
-        join_two_kernel,
-        place,
-        (*chunks, fronts),
-        [*[whole(chunk.shape) for chunk in chunks], pl.BlockSpec(memory_space=pl.ANY)],
-        pl.BlockSpec((None, rows, cols), lambda i, place: (1, 0, 0)),
-        jax.ShapeDtypeStruct(fronts.shape, bf16),
-        "join_two",
-        10,
-        (rows * cols, 4 * rows * cols),
-        aliases={9: 0},
-    )
+        copies.append(pltpu.make_async_copy(block_ref.at[i % 2], out_ref.at[front, :, at], sems.at[i % 2]))
+        copies[i].start()
+    for copy in copies[-2:]:
+        copy.wait()
+
+
+def join(front, moves, pairs, place, chunks, fronts, shape):
+    _, rows, cols = shape
+    hbm = pl.BlockSpec(memory_space=pltpu.HBM)
+    before = [] if fronts is None else [fronts]
+    return pl.pallas_call(
+        functools.partial(join_kernel, front, moves, pairs),
+        in_specs=[SMEM] + [VMEM] * len(chunks) + [hbm] * len(before),
+        out_specs=hbm,
+        out_shape=jax.ShapeDtypeStruct(shape, bf16),
+        scratch_shapes=[pltpu.VMEM((2, rows, cols // 4), bf16), pltpu.SemaphoreType.DMA((2,))],
+        input_output_aliases={1 + len(chunks): 0} if before else {},
+        compiler_params=params(6),
+        cost_estimate=cost(rows * cols, len(moves) * rows * cols),
+        name="join",
+    )(place, *chunks, *before)
 
 
 def move(value, target):
@@ -361,7 +320,7 @@
 
 
 def turn(flip):
-    return lambda y, zl, x, zh: (x, zh, x ^ y, zl ^ flip)
+    return lambda y, zl, x, zh: (x, zh, x ^ y ^ (2 * flip), zl ^ flip)
 
 
 def scatter(shares, first):
@@ -384,13 +343,12 @@
 
 def spread_chunks(value):
     chunks = {(0, 0): value}
-    for dy, dz in ((2, 1), (2, 0), (1, 1), (3, 1), (1, 0), (3, 0), (0, 1)):
+    for dy, dz in ((2, 1), (2, 0), (0, 1), (1, 1), (3, 1), (1, 0), (3, 0)):
         chunks[dy, dz] = move(value, lambda y, zl, x, zh: ((y + dy) % 4, zl ^ dz, x, zh))
-    return [chunks[dy, dz] for dy in range(4) for dz in range(2)]
+    return chunks
 
 
 def per_device(resident, memory, previous, inverse_part, pair_coupling):
-    rows, cols = memory.shape[1], resident.shape[1]
     place = jnp.stack([lax.axis_index(name) for name in ("x", "zh", "c", "y", "zl")]).astype(jnp.int32)
     coupling = jnp.tile(pair_coupling, (1, 128 // ORB))
 
@@ -404,7 +362,7 @@
     memory, prior_one, prior_two, odd_resident, even_resident = bring(place, memory, previous, resident)
     parts = odd_parts + even_parts
     front_one, energy = solve(
-        first_solve_kernel, 0, place, parts, prior_one, inverse_part, [coupling], 2, "first_solve"
+        first_solve_kernel, place, parts, prior_one, inverse_part[0], [coupling], 2, "first_solve"
     )
     own = spread_pairs(jnp.stack([move(energy, turn(0)), move(energy, turn(1))]), "x")
     other = [lax.ppermute(pair, "c", SWAP) for pair in own]
@@ -416,10 +374,14 @@
     even = half_product(place, lhs, even_resident)
     parts = scatter(odd, 1) + scatter(even, 0)
     (front_two,) = solve(
-        second_solve_kernel, 1, place, parts, prior_two, inverse_part, [], 1, "second_solve"
+        second_solve_kernel, place, parts, prior_two, inverse_part[1], [], 1, "second_solve"
     )
     chunks = spread_chunks(front_two)
-    return join_two(place, chunks, join_one(place, ones, rows, cols))
+    fronts = join(0, (0, 1, 2, 3), True, place, ones, None, previous.shape)
+    for moves in ((0, 2), (1, 3)):
+        some = [chunks[dy, dz] for dy in moves for dz in range(2)]
+        fronts = join(1, moves, False, place, some, fronts, previous.shape)
+    return fronts
 
 
 def solution(mesh):

time: 113 us -> 114 us (level); the launches traced: 112 us -> 114 us
  waiting for transfers between devices: 23.8 us -> 27.9 us
  starting transfers between devices: 58.9 us -> 55.3 us
  Pallas kernels: 28.6 us -> 30.2 us
    ppermute x6, waiting for transfers between devices: 5.36 us -> 8.33 us  [spread_pairs(): pairs[d] = lax.ppermute(pair, axis, [(i, (i + d) % 4) for i in range(4)])]
    ppermute x6, starting transfers between devices: 20.1 us -> 18 us  [spread_pairs(): pairs[d] = lax.ppermute(pair, axis, [(i, (i + d) % 4) for i in range(4)])]
    pallas_call x4 -> x5, Pallas kernels: 7.3 us -> 8.93 us  [the longest x3 5.69 us: join(): pl.pallas_call(functools.partial(join_kernel, front, moves, pairs), in_sp...]
    ppermute x4, waiting for transfers between devices: 0.26 us -> 1.56 us  [per_device(): other = [lax.ppermute(pair, 'c', SWAP) for pair in own]]
  transfers between devices with their start and end apart: 34 -> 34, of which waited for: 10 -> 11; matrix products, arithmetic and copies ran while one was open for 0% -> 0% of each run, Pallas kernels for 11% -> 13%
where the time goes in v5:
time: 114 us
  starting transfers between devices  55.3 us (49%)
  Pallas kernels  30.2 us (26%)
  waiting for transfers between devices  27.9 us (24%)
    ppermute x23, starting transfers between devices, move(): return lax.ppermute(value, ALL, pairs)  37.2 us
    ppermute x23, waiting for transfers between devices, move(): return lax.ppermute(value, ALL, pairs)  18 us
    ppermute x6, starting transfers between devices, spread_pairs(): pairs[d] = lax.ppermute(pair, axis, [(i, (i + d) % 4) for i in range(4)])  18 us
    ppermute x6, waiting for transfers between devices, spread_pairs(): pairs[d] = lax.ppermute(pair, axis, [(i, (i + d) % 4) for i in range(4)])  8.33 us
    pallas_call x3, Pallas kernels, half_product(): pl.pallas_call(half_product_kernel, in_specs=[SMEM, VMEM, VMEM], out_spec...  7.98 us
    pallas_call x1, Pallas kernels, first_product(): pl.pallas_call(first_product_kernel, in_specs=[SMEM] + [pl.BlockSpec(memo...  6.5 us
    pallas_call x3, Pallas kernels, join(): pl.pallas_call(functools.partial(join_kernel, front, moves, pairs), in_sp...  5.69 us
    pallas_call x1, Pallas kernels, bring(): pl.pallas_call(bring_kernel, in_specs=[SMEM] + [pl.BlockSpec(memory_space...  5.18 us
  transfers between devices with their start and end apart: 34, of which 11 were waited for; matrix products, arithmetic and copies ran while one was open for 0% of the time, Pallas kernels for 13%

profile of v5, /device:TPU:0, one launch (start us, length us, event | category | flops | bytes accessed | tf_op | source)
XLA Modules:
  0.0 114.1 jit_solution(6862867822606989300)
XLA Ops:
  0.1 6.5 %first_product.1 = (bf16[192,384]{1,0:T(8,128)(2,1)S(1)}, bf16[192,384]{1,0:T(8,128)(2,1)S(1)}, bf16[192,384]{1,0:T(8,128)(2,1)S(1)}, bf16[192,384]{1,0:T(8,128)...) custom-call(s32[5]{0:T(128)S(1)} %stack.41.place_ref, bf16[2,384,3072]{2,1,0:T(8,128)(2,1)} %memory_ref.3, ...), custom_call_target="tpu_custom_call" | custom-call | flops 1811939328 | bytes 18874368 | tf_op jit(solution)/shard_map/first_product/pallas_call | solution.py:111
  6.6 1.7 %collective-permute-start.1 = (bf16[192,384]{1,0:T(8,128)(2,1)S(1)}, bf16[192,384]{1,0:T(8,128)(2,1)S(1)}, u32[]{:S(2)}, u32[]{:S(2)}) collective-permute-start(bf16[192,384]{1,0:T(8,128)(2,1)S(1)} %get-tuple-element.54), channel_id=1, source_target_pairs={{0,32},{1,33},{2,34},{3,35},{4,36},{5,37},{6,38},{7,39},{8,40},{9,... | collective-permute-start | bytes 442376 | tf_op jit(solution)/shard_map/ppermute | solution.py:319
  8.3 1.8 %collective-permute-start = (bf16[192,384]{1,0:T(8,128)(2,1)S(1)}, bf16[192,384]{1,0:T(8,128)(2,1)S(1)}, u32[]{:S(2)}, u32[]{:S(2)}) collective-permute-start(bf16[192,384]{1,0:T(8,128)(2,1)S(1)} %get-tuple-element.55), channel_id=1, source_target_pairs={{0,48},{1,49},{2,50},{3,51},{4,52},{5,53},{6,54},{7,55},{8,56},{9,... | collective-permute-start | bytes 442376 | tf_op jit(solution)/shard_map/ppermute | solution.py:319
  10.1 3.0 %collective-permute-start.3 = (bf16[192,384]{1,0:T(8,128)(2,1)S(1)}, bf16[192,384]{1,0:T(8,128)(2,1)S(1)}, u32[]{:S(2)}, u32[]{:S(2)}) collective-permute-start(bf16[192,384]{1,0:T(8,128)(2,1)S(1)} %get-tuple-element.56), channel_id=1, source_target_pairs={{0,96},{1,97},{2,98},{3,99},{4,100},{5,101},{6,102},{7,103},{8,104... | collective-permute-start | bytes 442376 | tf_op jit(solution)/shard_map/ppermute | solution.py:319
  13.2 2.7 %half_product.3 = (bf16[192,384]{1,0:T(8,128)(2,1)S(1)}, bf16[192,384]{1,0:T(8,128)(2,1)S(1)}, bf16[192,384]{1,0:T(8,128)(2,1)S(1)}, bf16[192,384]{1,0:T(8,128)(2,1)S(1)}) custom-call(s32[5]{0:T(128)S(1)} %stack.41.place_ref, bf16[384,3072]{1,0:T(8,128)(2,1)S(1)} %get-tuple-element.58.lhs_ref, bf16[3072,768]{1,0:T(8,128)(2,1)S(1)} %get-tuple-element.59.resident_ref), custom_call_target="tpu_custom_call" | custom-call | flops 1811939328 | bytes 294912 | tf_op jit(solution)/shard_map/half_product/pallas_call | solution.py:59
  15.8 3.2 %collective-permute-start.4 = (bf16[192,384]{1,0:T(8,128)(2,1)S(1)}, bf16[192,384]{1,0:T(8,128)(2,1)S(1)}, u32[]{:S(2)}, u32[]{:S(2)}) collective-permute-start(bf16[192,384]{1,0:T(8,128)(2,1)S(1)} %get-tuple-element.67), channel_id=1, source_target_pairs={{0,80},{1,81},{2,82},{3,83},{4,84},{5,85},{6,86},{7,87},{8,88},{9,... | collective-permute-start | bytes 442376 | tf_op jit(solution)/shard_map/ppermute | solution.py:319
  19.0 0.1 tile.10.refs_10_
  19.1 1.6 %collective-permute-start.5 = (bf16[192,384]{1,0:T(8,128)(2,1)S(1)}, bf16[192,384]{1,0:T(8,128)(2,1)S(1)}, u32[]{:S(2)}, u32[]{:S(2)}) collective-permute-start(bf16[192,384]{1,0:T(8,128)(2,1)S(1)} %get-tuple-element.68), channel_id=1, source_target_pairs={{0,64},{1,65},{2,66},{3,67},{4,68},{5,69},{6,70},{7,71},{8,72},{9,... | collective-permute-start | bytes 442376 | tf_op jit(solution)/shard_map/ppermute | solution.py:319
  20.8 0.3 collective-permute-start.6
  21.2 5.5 %collective-permute-done.2.refs_2_ = bf16[192,384]{1,0:T(8,128)(2,1)S(1)} collective-permute-done((bf16[192,384]{1,0:T(8,128)(2,1)S(1)}, bf16[192,384]{1,0:T(8,128)(2,1)S(1)}, u32[]{:S(2)}, u32[]{:S(2)}) %collective-permute-start.2) | collective-permute-done | bytes 147488 | tf_op jit(solution)/shard_map/ppermute | solution.py:319
  26.7 5.2 %bring.1 = (bf16[384,3072]{1,0:T(8,128)(2,1)S(1)}, bf16[192,384]{1,0:T(8,128)(2,1)S(1)}, bf16[192,384]{1,0:T(8,128)(2,1)S(1)}, bf16[3072,768]{1,0:T(8,128)(2,1)S(1)}, bf16[3072,768]{1,0:T(8,128)(2,1)S(1)}) custom-call(s32[5]{0:T(128)S(1)} %stack.41.place_ref, bf16[2,384,3072]{2,1,0:T(8,128)(2,1)} %memory_ref.3, bf16[2,384,1536]{2,1,0:T(8,128)(2,1)} %previous_ref.1, ...), custom_call_target="tpu_custom_call" | custom-call | bytes 11796480 | tf_op jit(solution)/shard_map/bring/pallas_call | solution.py:159
  31.9 1.8 %first_solve.1 = (bf16[192,384]{1,0:T(8,128)(2,1)S(1)}, bf16[192,384]{1,0:T(8,128)(2,1)S(1)}) custom-call(s32[5]{0:T(128)S(1)} %stack.41.place_ref, bf16[192,384]{1,0:T(8,128)(2,1)S(1)} %collective-permute-done.refs_0_, bf16[192,384]{1,0:T(8,128)(2,1)S(1)} %collective-permute-done.1.refs_1_, bf16[192,384]{1,0:T(8,128)(2,1)S(1)} %collective-permute-done.2.refs_2_, ...), custom_call_target="tpu_custom_call" | custom-call | flops 339738624 | bytes 1769472 | tf_op jit(solution)/shard_map/first_solve/pallas_call | solution.py:266
  33.8 0.1 collective-permute-start.16
  33.8 6.1 %collective-permute-start.8 = (bf16[192,384]{1,0:T(8,128)(2,1)S(1)}, bf16[192,384]{1,0:T(8,128)(2,1)S(1)}, u32[]{:S(2)}, u32[]{:S(2)}) collective-permute-start(bf16[192,384]{1,0:T(8,128)(2,1)S(1)} %get-tuple-element.71), channel_id=1, source_target_pairs={{0,10},{1,11},{2,26},{3,27},{4,46},{5,47},{6,62},{7,63},{8,66},{9,... | collective-permute-start | bytes 442376 | tf_op jit(solution)/shard_map/ppermute | solution.py:319
  40.0 0.7 collective-permute-start.7
  40.7 4.6 %collective-permute-start.19 = (bf16[2,192,384]{2,1,0:T(8,128)(2,1)S(1)}, bf16[2,192,384]{2,1,0:T(8,128)(2,1)S(1)}, u32[]{:S(2)}, u32[]{:S(2)}) collective-permute-start(bf16[2,192,384]{2,1,0:T(8,128)(2,1)S(1)} %pad_maximum_fusion.1.refs_0_), channel_id=1, source_target_pairs={{0,96},{32,0},{64,32},{96,64},{1,97},{33,1},{65,33},{97,65},{2,98}... | collective-permute-start | bytes 884744 | tf_op jit(solution)/shard_map/ppermute | solution.py:340
  45.3 2.7 %collective-permute-start.18 = (bf16[2,192,384]{2,1,0:T(8,128)(2,1)S(1)}, bf16[2,192,384]{2,1,0:T(8,128)(2,1)S(1)}, u32[]{:S(2)}, u32[]{:S(2)}) collective-permute-start(bf16[2,192,384]{2,1,0:T(8,128)(2,1)S(1)} %pad_maximum_fusion.1.refs_0_), channel_id=1, source_target_pairs={{0,64},{32,96},{64,0},{96,32},{1,65},{33,97},{65,1},{97,33},{2,66}... | collective-permute-start | bytes 884744 | tf_op jit(solution)/shard_map/ppermute | solution.py:340
  48.1 7.8 %collective-permute-start.11 = (bf16[2,192,384]{2,1,0:T(8,128)(2,1)S(1)}, bf16[2,192,384]{2,1,0:T(8,128)(2,1)S(1)}, u32[]{:S(2)}, u32[]{:S(2)}) collective-permute-start(bf16[2,192,384]{2,1,0:T(8,128)(2,1)S(1)} %pad_maximum_fusion.refs_0_), channel_id=1, source_target_pairs={{0,12},{4,0},{8,4},{12,8},{1,13},{5,1},{9,5},{13,9},{2,14},{6,2},{... | collective-permute-start | bytes 884744 | tf_op jit(solution)/shard_map/ppermute | solution.py:340
  55.9 1.1 collective-permute-start.9
  57.1 1.6 %collective-permute-start.17 = (bf16[2,192,384]{2,1,0:T(8,128)(2,1)S(1)}, bf16[2,192,384]{2,1,0:T(8,128)(2,1)S(1)}, u32[]{:S(2)}, u32[]{:S(2)}) collective-permute-start(bf16[2,192,384]{2,1,0:T(8,128)(2,1)S(1)} %pad_maximum_fusion.1.refs_0_), channel_id=1, source_target_pairs={{0,32},{32,64},{64,96},{96,0},{1,33},{33,65},{65,97},{97,1},{2,34}... | collective-permute-start | bytes 884744 | tf_op jit(solution)/shard_map/ppermute | solution.py:340
  58.7 4.6 %collective-permute-done.11.refs_3_ = bf16[2,192,384]{2,1,0:T(8,128)(2,1)S(1)} collective-permute-done((bf16[2,192,384]{2,1,0:T(8,128)(2,1)S(1)}, bf16[2,192,384]{2,1,0:T(8,128)(2,1)S(1)}, u32[]{:S(2)}, u32[]{:S(2)}) %collective-permute-start.11) | collective-permute-done | bytes 294944 | tf_op jit(solution)/shard_map/ppermute | solution.py:340
  63.3 0.9 collective-permute-done.10.refs_2_
  64.3 2.8 %collective-permute-done.9.refs_1_ = bf16[2,192,384]{2,1,0:T(8,128)(2,1)S(1)} collective-permute-done((bf16[2,192,384]{2,1,0:T(8,128)(2,1)S(1)}, bf16[2,192,384]{2,1,0:T(8,128)(2,1)S(1)}, u32[]{:S(2)}, u32[]{:S(2)}) %collective-permute-start.9) | collective-permute-done | bytes 294944 | tf_op jit(solution)/shard_map/ppermute | solution.py:340
  67.1 1.5 %collective-permute-done.13.refs_5_ = bf16[2,192,384]{2,1,0:T(8,128)(2,1)S(1)} collective-permute-done((bf16[2,192,384]{2,1,0:T(8,128)(2,1)S(1)}, bf16[2,192,384]{2,1,0:T(8,128)(2,1)S(1)}, u32[]{:S(2)}, u32[]{:S(2)}) %collective-permute-start.13) | collective-permute-done | bytes 294944 | tf_op jit(solution)/shard_map/ppermute | solution.py:368
  68.6 1.6 %next_memory.1.lhs_ref = bf16[384,3072]{1,0:T(8,128)(2,1)S(1)} custom-call(s32[5]{0:T(128)S(1)} %stack.41.place_ref, bf16[384,3072]{1,0:T(8,128)(2,1)S(1)} %get-tuple-element.62.memory_ref, bf16[2,192,384]{2,1,0:T(8,128)(2,1)S(1)} %pad_maximum_fusion.refs_0_, bf16[2,192,384]{2,1,0:T(8,128)(2,1)S(1)} %collective-permute-done.9.refs_1_, ...), custom_call_target="tpu_custom_call" | custom-call | flops 1179648 | bytes 7077888 | tf_op jit(solution)/shard_map/next_memory/pallas_call | solution.py:206
  70.2 2.7 %half_product.4 = (bf16[192,384]{1,0:T(8,128)(2,1)S(1)}, bf16[192,384]{1,0:T(8,128)(2,1)S(1)}, bf16[192,384]{1,0:T(8,128)(2,1)S(1)}, bf16[192,384]{1,0:T(8,128)(2,1)S(1)}) custom-call(s32[5]{0:T(128)S(1)} %stack.41.place_ref, bf16[384,3072]{1,0:T(8,128)(2,1)S(1)} %next_memory.1.lhs_ref, bf16[3072,768]{1,0:T(8,128)(2,1)S(1)} %get-tuple-element.81.resident_ref), custom_call_target="tpu_custom_call" | custom-call | flops 1811939328 | bytes 294912 | tf_op jit(solution)/shard_map/half_product/pallas_call | solution.py:59
  72.9 0.1 collective-permute-start.20
  73.1 0.4 collective-permute-start.22
  73.5 5.7 %collective-permute-start.23 = (bf16[192,384]{1,0:T(8,128)(2,1)S(1)}, bf16[192,384]{1,0:T(8,128)(2,1)S(1)}, u32[]{:S(2)}, u32[]{:S(2)}) collective-permute-start(bf16[192,384]{1,0:T(8,128)(2,1)S(1)} %get-tuple-element.89), channel_id=1, source_target_pairs={{0,96},{1,97},{2,98},{3,99},{4,100},{5,101},{6,102},{7,103},{8,104... | collective-permute-start | bytes 442376 | tf_op jit(solution)/shard_map/ppermute | solution.py:319
  79.1 2.7 %half_product.5 = (bf16[192,384]{1,0:T(8,128)(2,1)S(1)}, bf16[192,384]{1,0:T(8,128)(2,1)S(1)}, bf16[192,384]{1,0:T(8,128)(2,1)S(1)}, bf16[192,384]{1,0:T(8,128)(2,1)S(1)}) custom-call(s32[5]{0:T(128)S(1)} %stack.41.place_ref, bf16[384,3072]{1,0:T(8,128)(2,1)S(1)} %next_memory.1.lhs_ref, bf16[3072,768]{1,0:T(8,128)(2,1)S(1)} %get-tuple-element.91.resident_ref), custom_call_target="tpu_custom_call" | custom-call | flops 1811939328 | bytes 294912 | tf_op jit(solution)/shard_map/half_product/pallas_call | solution.py:59
  81.9 0.3 collective-permute-done.20.refs_0_
  82.2 1.4 %collective-permute-start.25 = (bf16[192,384]{1,0:T(8,128)(2,1)S(1)}, bf16[192,384]{1,0:T(8,128)(2,1)S(1)}, u32[]{:S(2)}, u32[]{:S(2)}) collective-permute-start(bf16[192,384]{1,0:T(8,128)(2,1)S(1)} %get-tuple-element.93), channel_id=1, source_target_pairs={{0,64},{1,65},{2,66},{3,67},{4,68},{5,69},{6,70},{7,71},{8,72},{9,... | collective-permute-start | bytes 442376 | tf_op jit(solution)/shard_map/ppermute | solution.py:319
  83.6 3.3 %collective-permute-start.26 = (bf16[192,384]{1,0:T(8,128)(2,1)S(1)}, bf16[192,384]{1,0:T(8,128)(2,1)S(1)}, u32[]{:S(2)}, u32[]{:S(2)}) collective-permute-start(bf16[192,384]{1,0:T(8,128)(2,1)S(1)} %get-tuple-element.94), channel_id=1, source_target_pairs={{0,16},{1,17},{2,18},{3,19},{4,20},{5,21},{6,22},{7,23},{8,24},{9,... | collective-permute-start | bytes 442376 | tf_op jit(solution)/shard_map/ppermute | solution.py:319
  86.9 5.0 %collective-permute-done.23.refs_3_ = bf16[192,384]{1,0:T(8,128)(2,1)S(1)} collective-permute-done((bf16[192,384]{1,0:T(8,128)(2,1)S(1)}, bf16[192,384]{1,0:T(8,128)(2,1)S(1)}, u32[]{:S(2)}, u32[]{:S(2)}) %collective-permute-start.23) | collective-permute-done | bytes 147488 | tf_op jit(solution)/shard_map/ppermute | solution.py:319
  91.9 0.3 collective-permute-done.26.refs_6_
  92.2 1.4 %second_solve.1.refs_0_ = bf16[192,384]{1,0:T(8,128)(2,1)S(1)} custom-call(s32[5]{0:T(128)S(1)} %stack.41.place_ref, bf16[192,384]{1,0:T(8,128)(2,1)S(1)} %collective-permute-done.20.refs_0_, bf16[192,384]{1,0:T(8,128)(2,1)S(1)} %collective-permute-done.21.refs_1_, bf16[192,384]{1,0:T(8,128)(2,1)S(1)} %collective-permute-done.22.refs_2_, ...), custom_call_target="tpu_custom_call" | custom-call | flops 339738624 | bytes 1769472 | tf_op jit(solution)/shard_map/second_solve/pallas_call | solution.py:266
  93.7 0.8 collective-permute-start.33
  94.5 2.8 %collective-permute-start.32 = (bf16[192,384]{1,0:T(8,128)(2,1)S(1)}, bf16[192,384]{1,0:T(8,128)(2,1)S(1)}, u32[]{:S(2)}, u32[]{:S(2)}) collective-permute-start(bf16[192,384]{1,0:T(8,128)(2,1)S(1)} %second_solve.1.refs_0_), channel_id=1, source_target_pairs={{0,64},{1,65},{2,66},{3,67},{4,68},{5,69},{6,70},{7,71},{8,72},{9,... | collective-permute-start | bytes 442376 | tf_op jit(solution)/shard_map/ppermute | solution.py:319
  97.3 1.5 %collective-permute-start.31 = (bf16[192,384]{1,0:T(8,128)(2,1)S(1)}, bf16[192,384]{1,0:T(8,128)(2,1)S(1)}, u32[]{:S(2)}, u32[]{:S(2)}) collective-permute-start(bf16[192,384]{1,0:T(8,128)(2,1)S(1)} %second_solve.1.refs_0_), channel_id=1, source_target_pairs={{0,16},{1,17},{2,18},{3,19},{4,20},{5,21},{6,22},{7,23},{8,24},{9,... | collective-permute-start | bytes 442376 | tf_op jit(solution)/shard_map/ppermute | solution.py:319
  98.8 0.4 collective-permute-start.30
  99.1 0.9 collective-permute-start.29
  100.1 2.9 %collective-permute-done.33.refs_3_ = bf16[192,384]{1,0:T(8,128)(2,1)S(1)} collective-permute-done((bf16[192,384]{1,0:T(8,128)(2,1)S(1)}, bf16[192,384]{1,0:T(8,128)(2,1)S(1)}, u32[]{:S(2)}, u32[]{:S(2)}) %collective-permute-start.33) | collective-permute-done | bytes 147488 | tf_op jit(solution)/shard_map/ppermute | solution.py:319
  103.0 0.2 collective-permute-done.32.refs_2_
  103.1 1.3 %collective-permute-start.27 = (bf16[192,384]{1,0:T(8,128)(2,1)S(1)}, bf16[192,384]{1,0:T(8,128)(2,1)S(1)}, u32[]{:S(2)}, u32[]{:S(2)}) collective-permute-start(bf16[192,384]{1,0:T(8,128)(2,1)S(1)} %second_solve.1.refs_0_), channel_id=1, source_target_pairs={{0,32},{1,33},{2,34},{3,35},{4,36},{5,37},{6,38},{7,39},{8,40},{9,... | collective-permute-start | bytes 442376 | tf_op jit(solution)/shard_map/ppermute | solution.py:319
  104.4 2.6 %join.3.refs_4_ = bf16[2,384,1536]{2,1,0:T(8,128)(2,1)} custom-call(s32[5]{0:T(128)S(1)} %stack.41.place_ref, bf16[2,192,384]{2,1,0:T(8,128)(2,1)S(1)} %pad_maximum_fusion.1.refs_0_, bf16[2,192,384]{2,1,0:T(8,128)(2,1)S(1)} %collective-permute-done.17.refs_1_, bf16[2,192,384]{2,1,0:T(8,128)(2,1)S(1)} %collective-permute-done.18.refs_2_, ...), custom_call_target="tpu_custom_call" | custom-call | flops 589824 | bytes 2359296 | tf_op jit(solution)/shard_map/join/pallas_call | solution.py:297
  107.0 3.8 %collective-permute-done.31.refs_1_ = bf16[192,384]{1,0:T(8,128)(2,1)S(1)} collective-permute-done((bf16[192,384]{1,0:T(8,128)(2,1)S(1)}, bf16[192,384]{1,0:T(8,128)(2,1)S(1)}, u32[]{:S(2)}, u32[]{:S(2)}) %collective-permute-start.31) | collective-permute-done | bytes 147488 | tf_op jit(solution)/shard_map/ppermute | solution.py:319
  110.8 1.6 %join.4.refs_4_ = bf16[2,384,1536]{2,1,0:T(8,128)(2,1)} custom-call(s32[5]{0:T(128)S(1)} %stack.41.place_ref, bf16[192,384]{1,0:T(8,128)(2,1)S(1)} %second_solve.1.refs_0_, bf16[192,384]{1,0:T(8,128)(2,1)S(1)} %collective-permute-done.31.refs_1_, bf16[192,384]{1,0:T(8,128)(2,1)S(1)} %collective-permute-done.32.refs_2_, ...), custom_call_target="tpu_custom_call", output_to_operand_aliasing={{}: (5, {})} | custom-call | flops 589824 | bytes 1179648 | tf_op jit(solution)/shard_map/join/pallas_call | solution.py:297
  112.4 1.6 %join.5 = bf16[2,384,1536]{2,1,0:T(8,128)(2,1)} custom-call(s32[5]{0:T(128)S(1)} %stack.41.place_ref, bf16[192,384]{1,0:T(8,128)(2,1)S(1)} %collective-permute-done.27.refs_0_, bf16[192,384]{1,0:T(8,128)(2,1)S(1)} %collective-permute-done.28.refs_1_, bf16[192,384]{1,0:T(8,128)(2,1)S(1)} %collective-permute-done.29.refs_2_, ...), custom_call_target="tpu_custom_call", output_to_operand_aliasing={{}: (5, {})} | custom-call | flops 589824 | bytes 1179648 | tf_op jit(solution)/shard_map/join/pallas_call | solution.py:297
  (41 shorter events, 0.5 us)
Async XLA Ops:
  6.6 12.5 %collective-permute-start.1 = (bf16[192,384]{1,0:T(8,128)(2,1)S(1)}, bf16[192,384]{1,0:T(8,128)(2,1)S(1)}, u32[]{:S(2)}, u32[]{:S(2)}) collective-permute-start(bf16[192,384]{1,0:T(8,128)(2,1)S(1)} %get-tuple-element.54), channel_id=1, source_target_pairs={{0,32},{1,33},{2,34},{3,35},{4,36},{5,37},{6,38},{7,39},{8,40},{9,... | collective-permute-start | bytes 442376 | tf_op jit(solution)/shard_map/ppermute | solution.py:319
  8.3 12.4 %collective-permute-start = (bf16[192,384]{1,0:T(8,128)(2,1)S(1)}, bf16[192,384]{1,0:T(8,128)(2,1)S(1)}, u32[]{:S(2)}, u32[]{:S(2)}) collective-permute-start(bf16[192,384]{1,0:T(8,128)(2,1)S(1)} %get-tuple-element.55), channel_id=1, source_target_pairs={{0,48},{1,49},{2,50},{3,51},{4,52},{5,53},{6,54},{7,55},{8,56},{9,... | collective-permute-start | bytes 442376 | tf_op jit(solution)/shard_map/ppermute | solution.py:319
  10.1 11.1 %collective-permute-start.3 = (bf16[192,384]{1,0:T(8,128)(2,1)S(1)}, bf16[192,384]{1,0:T(8,128)(2,1)S(1)}, u32[]{:S(2)}, u32[]{:S(2)}) collective-permute-start(bf16[192,384]{1,0:T(8,128)(2,1)S(1)} %get-tuple-element.56), channel_id=1, source_target_pairs={{0,96},{1,97},{2,98},{3,99},{4,100},{5,101},{6,102},{7,103},{8,104... | collective-permute-start | bytes 442376 | tf_op jit(solution)/shard_map/ppermute | solution.py:319
  13.2 13.6 %collective-permute-start.2 = (bf16[192,384]{1,0:T(8,128)(2,1)S(1)}, bf16[192,384]{1,0:T(8,128)(2,1)S(1)}, u32[]{:S(2)}, u32[]{:S(2)}) collective-permute-start(bf16[192,384]{1,0:T(8,128)(2,1)S(1)} %get-tuple-element.57), channel_id=1, source_target_pairs={{0,112},{1,113},{2,114},{3,115},{4,116},{5,117},{6,118},{7,119},{8... | collective-permute-start | bytes 442376 | tf_op jit(solution)/shard_map/ppermute | solution.py:319
  13.2 5.9 %copy-start.1 = (f32[32,32]{1,0:T(8,128)S(1)}, f32[32,32]{1,0:T(8,128)}, u32[]{:S(2)}) copy-start(f32[32,32]{1,0:T(8,128)} %param.9) | copy-start | bytes 12292
  13.2 8.0 %copy-start = (f32[2,384,384]{2,1,0:T(8,128)S(1)}, f32[2,384,384]{2,1,0:T(8,128)}, u32[]{:S(2)}) copy-start(f32[2,384,384]{2,1,0:T(8,128)} %param.8) | copy-start | bytes 3538948
  15.8 16.1 %collective-permute-start.4 = (bf16[192,384]{1,0:T(8,128)(2,1)S(1)}, bf16[192,384]{1,0:T(8,128)(2,1)S(1)}, u32[]{:S(2)}, u32[]{:S(2)}) collective-permute-start(bf16[192,384]{1,0:T(8,128)(2,1)S(1)} %get-tuple-element.67), channel_id=1, source_target_pairs={{0,80},{1,81},{2,82},{3,83},{4,84},{5,85},{6,86},{7,87},{8,88},{9,... | collective-permute-start | bytes 442376 | tf_op jit(solution)/shard_map/ppermute | solution.py:319
  19.1 12.8 %collective-permute-start.5 = (bf16[192,384]{1,0:T(8,128)(2,1)S(1)}, bf16[192,384]{1,0:T(8,128)(2,1)S(1)}, u32[]{:S(2)}, u32[]{:S(2)}) collective-permute-start(bf16[192,384]{1,0:T(8,128)(2,1)S(1)} %get-tuple-element.68), channel_id=1, source_target_pairs={{0,64},{1,65},{2,66},{3,67},{4,68},{5,69},{6,70},{7,71},{8,72},{9,... | collective-permute-start | bytes 442376 | tf_op jit(solution)/shard_map/ppermute | solution.py:319
  20.8 11.2 %collective-permute-start.6 = (bf16[192,384]{1,0:T(8,128)(2,1)S(1)}, bf16[192,384]{1,0:T(8,128)(2,1)S(1)}, u32[]{:S(2)}, u32[]{:S(2)}) collective-permute-start(bf16[192,384]{1,0:T(8,128)(2,1)S(1)} %get-tuple-element.69), channel_id=1, source_target_pairs={{0,16},{1,17},{2,18},{3,19},{4,20},{5,21},{6,22},{7,23},{8,24},{9,... | collective-permute-start | bytes 442376 | tf_op jit(solution)/shard_map/ppermute | solution.py:319
  33.8 6.9 %collective-permute-start.16 = (bf16[192,384]{1,0:T(8,128)(2,1)S(1)}, bf16[192,384]{1,0:T(8,128)(2,1)S(1)}, u32[]{:S(2)}, u32[]{:S(2)}) collective-permute-start(bf16[192,384]{1,0:T(8,128)(2,1)S(1)} %get-tuple-element.72), channel_id=1, source_target_pairs={{0,16},{16,0},{1,17},{17,1},{2,18},{18,2},{3,19},{19,3},{4,20},{20... | collective-permute-start | bytes 442376 | tf_op jit(solution)/shard_map/ppermute | solution.py:369
  33.8 14.2 %collective-permute-start.8 = (bf16[192,384]{1,0:T(8,128)(2,1)S(1)}, bf16[192,384]{1,0:T(8,128)(2,1)S(1)}, u32[]{:S(2)}, u32[]{:S(2)}) collective-permute-start(bf16[192,384]{1,0:T(8,128)(2,1)S(1)} %get-tuple-element.71), channel_id=1, source_target_pairs={{0,10},{1,11},{2,26},{3,27},{4,46},{5,47},{6,62},{7,63},{8,66},{9,... | collective-permute-start | bytes 442376 | tf_op jit(solution)/shard_map/ppermute | solution.py:319
  40.0 8.1 %collective-permute-start.7 = (bf16[192,384]{1,0:T(8,128)(2,1)S(1)}, bf16[192,384]{1,0:T(8,128)(2,1)S(1)}, u32[]{:S(2)}, u32[]{:S(2)}) collective-permute-start(bf16[192,384]{1,0:T(8,128)(2,1)S(1)} %get-tuple-element.71), channel_id=1, source_target_pairs={{0,0},{1,1},{2,16},{3,17},{4,36},{5,37},{6,52},{7,53},{8,72},{9,73... | collective-permute-start | bytes 442376 | tf_op jit(solution)/shard_map/ppermute | solution.py:319
  40.7 16.4 %collective-permute-start.19 = (bf16[2,192,384]{2,1,0:T(8,128)(2,1)S(1)}, bf16[2,192,384]{2,1,0:T(8,128)(2,1)S(1)}, u32[]{:S(2)}, u32[]{:S(2)}) collective-permute-start(bf16[2,192,384]{2,1,0:T(8,128)(2,1)S(1)} %pad_maximum_fusion.1.refs_0_), channel_id=1, source_target_pairs={{0,96},{32,0},{64,32},{96,64},{1,97},{33,1},{65,33},{97,65},{2,98}... | collective-permute-start | bytes 884744 | tf_op jit(solution)/shard_map/ppermute | solution.py:340
  45.3 13.4 %collective-permute-start.18 = (bf16[2,192,384]{2,1,0:T(8,128)(2,1)S(1)}, bf16[2,192,384]{2,1,0:T(8,128)(2,1)S(1)}, u32[]{:S(2)}, u32[]{:S(2)}) collective-permute-start(bf16[2,192,384]{2,1,0:T(8,128)(2,1)S(1)} %pad_maximum_fusion.1.refs_0_), channel_id=1, source_target_pairs={{0,64},{32,96},{64,0},{96,32},{1,65},{33,97},{65,1},{97,33},{2,66}... | collective-permute-start | bytes 884744 | tf_op jit(solution)/shard_map/ppermute | solution.py:340
  48.1 15.2 %collective-permute-start.11 = (bf16[2,192,384]{2,1,0:T(8,128)(2,1)S(1)}, bf16[2,192,384]{2,1,0:T(8,128)(2,1)S(1)}, u32[]{:S(2)}, u32[]{:S(2)}) collective-permute-start(bf16[2,192,384]{2,1,0:T(8,128)(2,1)S(1)} %pad_maximum_fusion.refs_0_), channel_id=1, source_target_pairs={{0,12},{4,0},{8,4},{12,8},{1,13},{5,1},{9,5},{13,9},{2,14},{6,2},{... | collective-permute-start | bytes 884744 | tf_op jit(solution)/shard_map/ppermute | solution.py:340
  55.9 8.3 %collective-permute-start.10 = (bf16[2,192,384]{2,1,0:T(8,128)(2,1)S(1)}, bf16[2,192,384]{2,1,0:T(8,128)(2,1)S(1)}, u32[]{:S(2)}, u32[]{:S(2)}) collective-permute-start(bf16[2,192,384]{2,1,0:T(8,128)(2,1)S(1)} %pad_maximum_fusion.refs_0_), channel_id=1, source_target_pairs={{0,8},{4,12},{8,0},{12,4},{1,9},{5,13},{9,1},{13,5},{2,10},{6,14},... | collective-permute-start | bytes 884744 | tf_op jit(solution)/shard_map/ppermute | solution.py:340
  55.9 11.1 %collective-permute-start.9 = (bf16[2,192,384]{2,1,0:T(8,128)(2,1)S(1)}, bf16[2,192,384]{2,1,0:T(8,128)(2,1)S(1)}, u32[]{:S(2)}, u32[]{:S(2)}) collective-permute-start(bf16[2,192,384]{2,1,0:T(8,128)(2,1)S(1)} %pad_maximum_fusion.refs_0_), channel_id=1, source_target_pairs={{0,4},{4,8},{8,12},{12,0},{1,5},{5,9},{9,13},{13,1},{2,6},{6,10},{... | collective-permute-start | bytes 884744 | tf_op jit(solution)/shard_map/ppermute | solution.py:340
  57.1 10.0 %collective-permute-start.17 = (bf16[2,192,384]{2,1,0:T(8,128)(2,1)S(1)}, bf16[2,192,384]{2,1,0:T(8,128)(2,1)S(1)}, u32[]{:S(2)}, u32[]{:S(2)}) collective-permute-start(bf16[2,192,384]{2,1,0:T(8,128)(2,1)S(1)} %pad_maximum_fusion.1.refs_0_), channel_id=1, source_target_pairs={{0,32},{32,64},{64,96},{96,0},{1,33},{33,65},{65,97},{97,1},{2,34}... | collective-permute-start | bytes 884744 | tf_op jit(solution)/shard_map/ppermute | solution.py:340
  58.7 8.3 %collective-permute-start.12 = (bf16[2,192,384]{2,1,0:T(8,128)(2,1)S(1)}, bf16[2,192,384]{2,1,0:T(8,128)(2,1)S(1)}, u32[]{:S(2)}, u32[]{:S(2)}) collective-permute-start(bf16[2,192,384]{2,1,0:T(8,128)(2,1)S(1)} %pad_maximum_fusion.refs_0_), channel_id=1, source_target_pairs={{0,1},{1,0},{2,3},{3,2},{4,5},{5,4},{6,7},{7,6},{8,9},{9,8},{10,11... | collective-permute-start | bytes 884744 | tf_op jit(solution)/shard_map/ppermute | solution.py:368
  63.3 3.7 %collective-permute-start.15 = (bf16[2,192,384]{2,1,0:T(8,128)(2,1)S(1)}, bf16[2,192,384]{2,1,0:T(8,128)(2,1)S(1)}, u32[]{:S(2)}, u32[]{:S(2)}) collective-permute-start(bf16[2,192,384]{2,1,0:T(8,128)(2,1)S(1)} %collective-permute-done.11.refs_3_), channel_id=1, source_target_pairs={{0,1},{1,0},{2,3},{3,2},{4,5},{5,4},{6,7},{7,6},{8,9},{9,8},{10,11... | collective-permute-start | bytes 884744 | tf_op jit(solution)/shard_map/ppermute | solution.py:368
  64.3 2.8 %collective-permute-start.14 = (bf16[2,192,384]{2,1,0:T(8,128)(2,1)S(1)}, bf16[2,192,384]{2,1,0:T(8,128)(2,1)S(1)}, u32[]{:S(2)}, u32[]{:S(2)}) collective-permute-start(bf16[2,192,384]{2,1,0:T(8,128)(2,1)S(1)} %collective-permute-done.10.refs_2_), channel_id=1, source_target_pairs={{0,1},{1,0},{2,3},{3,2},{4,5},{5,4},{6,7},{7,6},{8,9},{9,8},{10,11... | collective-permute-start | bytes 884744 | tf_op jit(solution)/shard_map/ppermute | solution.py:368
  67.0 1.6 %collective-permute-start.13 = (bf16[2,192,384]{2,1,0:T(8,128)(2,1)S(1)}, bf16[2,192,384]{2,1,0:T(8,128)(2,1)S(1)}, u32[]{:S(2)}, u32[]{:S(2)}) collective-permute-start(bf16[2,192,384]{2,1,0:T(8,128)(2,1)S(1)} %collective-permute-done.9.refs_1_), channel_id=1, source_target_pairs={{0,1},{1,0},{2,3},{3,2},{4,5},{5,4},{6,7},{7,6},{8,9},{9,8},{10,11... | collective-permute-start | bytes 884744 | tf_op jit(solution)/shard_map/ppermute | solution.py:368
  72.9 9.3 %collective-permute-start.20 = (bf16[192,384]{1,0:T(8,128)(2,1)S(1)}, bf16[192,384]{1,0:T(8,128)(2,1)S(1)}, u32[]{:S(2)}, u32[]{:S(2)}) collective-permute-start(bf16[192,384]{1,0:T(8,128)(2,1)S(1)} %get-tuple-element.86), channel_id=1, source_target_pairs={{0,48},{1,49},{2,50},{3,51},{4,52},{5,53},{6,54},{7,55},{8,56},{9,... | collective-permute-start | bytes 442376 | tf_op jit(solution)/shard_map/ppermute | solution.py:319
  73.0 10.6 %collective-permute-start.21 = (bf16[192,384]{1,0:T(8,128)(2,1)S(1)}, bf16[192,384]{1,0:T(8,128)(2,1)S(1)}, u32[]{:S(2)}, u32[]{:S(2)}) collective-permute-start(bf16[192,384]{1,0:T(8,128)(2,1)S(1)} %get-tuple-element.87), channel_id=1, source_target_pairs={{0,32},{1,33},{2,34},{3,35},{4,36},{5,37},{6,38},{7,39},{8,40},{9,... | collective-permute-start | bytes 442376 | tf_op jit(solution)/shard_map/ppermute | solution.py:319
  73.1 13.8 %collective-permute-start.22 = (bf16[192,384]{1,0:T(8,128)(2,1)S(1)}, bf16[192,384]{1,0:T(8,128)(2,1)S(1)}, u32[]{:S(2)}, u32[]{:S(2)}) collective-permute-start(bf16[192,384]{1,0:T(8,128)(2,1)S(1)} %get-tuple-element.88), channel_id=1, source_target_pairs={{0,112},{1,113},{2,114},{3,115},{4,116},{5,117},{6,118},{7,119},{8... | collective-permute-start | bytes 442376 | tf_op jit(solution)/shard_map/ppermute | solution.py:319
  73.5 18.4 %collective-permute-start.23 = (bf16[192,384]{1,0:T(8,128)(2,1)S(1)}, bf16[192,384]{1,0:T(8,128)(2,1)S(1)}, u32[]{:S(2)}, u32[]{:S(2)}) collective-permute-start(bf16[192,384]{1,0:T(8,128)(2,1)S(1)} %get-tuple-element.89), channel_id=1, source_target_pairs={{0,96},{1,97},{2,98},{3,99},{4,100},{5,101},{6,102},{7,103},{8,104... | collective-permute-start | bytes 442376 | tf_op jit(solution)/shard_map/ppermute | solution.py:319
  81.8 10.1 %collective-permute-start.24 = (bf16[192,384]{1,0:T(8,128)(2,1)S(1)}, bf16[192,384]{1,0:T(8,128)(2,1)S(1)}, u32[]{:S(2)}, u32[]{:S(2)}) collective-permute-start(bf16[192,384]{1,0:T(8,128)(2,1)S(1)} %get-tuple-element.92), channel_id=1, source_target_pairs={{0,80},{1,81},{2,82},{3,83},{4,84},{5,85},{6,86},{7,87},{8,88},{9,... | collective-permute-start | bytes 442376 | tf_op jit(solution)/shard_map/ppermute | solution.py:319
  82.2 9.8 %collective-permute-start.25 = (bf16[192,384]{1,0:T(8,128)(2,1)S(1)}, bf16[192,384]{1,0:T(8,128)(2,1)S(1)}, u32[]{:S(2)}, u32[]{:S(2)}) collective-permute-start(bf16[192,384]{1,0:T(8,128)(2,1)S(1)} %get-tuple-element.93), channel_id=1, source_target_pairs={{0,64},{1,65},{2,66},{3,67},{4,68},{5,69},{6,70},{7,71},{8,72},{9,... | collective-permute-start | bytes 442376 | tf_op jit(solution)/shard_map/ppermute | solution.py:319
  83.6 8.6 %collective-permute-start.26 = (bf16[192,384]{1,0:T(8,128)(2,1)S(1)}, bf16[192,384]{1,0:T(8,128)(2,1)S(1)}, u32[]{:S(2)}, u32[]{:S(2)}) collective-permute-start(bf16[192,384]{1,0:T(8,128)(2,1)S(1)} %get-tuple-element.94), channel_id=1, source_target_pairs={{0,16},{1,17},{2,18},{3,19},{4,20},{5,21},{6,22},{7,23},{8,24},{9,... | collective-permute-start | bytes 442376 | tf_op jit(solution)/shard_map/ppermute | solution.py:319
  93.7 9.3 %collective-permute-start.33 = (bf16[192,384]{1,0:T(8,128)(2,1)S(1)}, bf16[192,384]{1,0:T(8,128)(2,1)S(1)}, u32[]{:S(2)}, u32[]{:S(2)}) collective-permute-start(bf16[192,384]{1,0:T(8,128)(2,1)S(1)} %second_solve.1.refs_0_), channel_id=1, source_target_pairs={{0,80},{1,81},{2,82},{3,83},{4,84},{5,85},{6,86},{7,87},{8,88},{9,... | collective-permute-start | bytes 442376 | tf_op jit(solution)/shard_map/ppermute | solution.py:319
  94.5 8.6 %collective-permute-start.32 = (bf16[192,384]{1,0:T(8,128)(2,1)S(1)}, bf16[192,384]{1,0:T(8,128)(2,1)S(1)}, u32[]{:S(2)}, u32[]{:S(2)}) collective-permute-start(bf16[192,384]{1,0:T(8,128)(2,1)S(1)} %second_solve.1.refs_0_), channel_id=1, source_target_pairs={{0,64},{1,65},{2,66},{3,67},{4,68},{5,69},{6,70},{7,71},{8,72},{9,... | collective-permute-start | bytes 442376 | tf_op jit(solution)/shard_map/ppermute | solution.py:319
  97.3 13.5 %collective-permute-start.31 = (bf16[192,384]{1,0:T(8,128)(2,1)S(1)}, bf16[192,384]{1,0:T(8,128)(2,1)S(1)}, u32[]{:S(2)}, u32[]{:S(2)}) collective-permute-start(bf16[192,384]{1,0:T(8,128)(2,1)S(1)} %second_solve.1.refs_0_), channel_id=1, source_target_pairs={{0,16},{1,17},{2,18},{3,19},{4,20},{5,21},{6,22},{7,23},{8,24},{9,... | collective-permute-start | bytes 442376 | tf_op jit(solution)/shard_map/ppermute | solution.py:319
  98.8 13.6 %collective-permute-start.30 = (bf16[192,384]{1,0:T(8,128)(2,1)S(1)}, bf16[192,384]{1,0:T(8,128)(2,1)S(1)}, u32[]{:S(2)}, u32[]{:S(2)}) collective-permute-start(bf16[192,384]{1,0:T(8,128)(2,1)S(1)} %second_solve.1.refs_0_), channel_id=1, source_target_pairs={{0,112},{1,113},{2,114},{3,115},{4,116},{5,117},{6,118},{7,119},{8... | collective-permute-start | bytes 442376 | tf_op jit(solution)/shard_map/ppermute | solution.py:319
  99.1 13.2 %collective-permute-start.29 = (bf16[192,384]{1,0:T(8,128)(2,1)S(1)}, bf16[192,384]{1,0:T(8,128)(2,1)S(1)}, u32[]{:S(2)}, u32[]{:S(2)}) collective-permute-start(bf16[192,384]{1,0:T(8,128)(2,1)S(1)} %second_solve.1.refs_0_), channel_id=1, source_target_pairs={{0,96},{1,97},{2,98},{3,99},{4,100},{5,101},{6,102},{7,103},{8,104... | collective-permute-start | bytes 442376 | tf_op jit(solution)/shard_map/ppermute | solution.py:319
  103.0 9.4 %collective-permute-start.28 = (bf16[192,384]{1,0:T(8,128)(2,1)S(1)}, bf16[192,384]{1,0:T(8,128)(2,1)S(1)}, u32[]{:S(2)}, u32[]{:S(2)}) collective-permute-start(bf16[192,384]{1,0:T(8,128)(2,1)S(1)} %second_solve.1.refs_0_), channel_id=1, source_target_pairs={{0,48},{1,49},{2,50},{3,51},{4,52},{5,53},{6,54},{7,55},{8,56},{9,... | collective-permute-start | bytes 442376 | tf_op jit(solution)/shard_map/ppermute | solution.py:319
  103.1 9.2 %collective-permute-start.27 = (bf16[192,384]{1,0:T(8,128)(2,1)S(1)}, bf16[192,384]{1,0:T(8,128)(2,1)S(1)}, u32[]{:S(2)}, u32[]{:S(2)}) collective-permute-start(bf16[192,384]{1,0:T(8,128)(2,1)S(1)} %second_solve.1.refs_0_), channel_id=1, source_target_pairs={{0,32},{1,33},{2,34},{3,35},{4,36},{5,37},{6,38},{7,39},{8,40},{9,... | collective-permute-start | bytes 442376 | tf_op jit(solution)/shard_map/ppermute | solution.py:319

commit v6 on v0

v6 whole, which is shorter than its diff:
```python
import functools

import jax
import jax.numpy as jnp
from jax import lax
from jax.experimental import pallas as pl
from jax.experimental.pallas import tpu as pltpu
from jax.sharding import Mesh, PartitionSpec as P

step_size = 0.5
ORB = 32
f32 = jnp.float32
bf16 = jnp.bfloat16
PASTS = ("y", "zl")
SECONDS = ("x", "zh", "c")
ALL = PASTS + SECONDS
SWAP = [(0, 1), (1, 0)]
X, ZH, C, Y, ZL = range(5)


VMEM = pl.BlockSpec(memory_space=pltpu.VMEM)
SMEM = pl.BlockSpec(memory_space=pltpu.SMEM)
HBM = pl.BlockSpec(memory_space=pltpu.HBM)


def in_hbm(array):
    return pltpu.with_memory_space_constraint(array, pltpu.HBM)


def params(megabytes):
    return pltpu.CompilerParams(vmem_limit_bytes=megabytes << 20)


def cost(flops, nbytes):
    return pl.CostEstimate(flops=flops, bytes_accessed=nbytes, transcendentals=0)


def part_of(place_ref, dy, dz):
    return (place_ref[Y] ^ dy) * 2 + (place_ref[ZL] ^ dz)


def rows_at(part, width):
    return pl.ds(pl.multiple_of(part * width, width), width)


def store_shares(place_ref, turned_ref, out_refs):
    width = out_refs[0].shape[0]
    for k, out_ref in enumerate(out_refs):
        out_ref[...] = turned_ref[rows_at(part_of(place_ref, k >> 1, k & 1), width), :]


TILES = 3


def first_product_kernel(place_ref, memory_ref, resident_ref, *refs):
    out_refs, lhs_ref, next_ref, tile_ref, turned_ref, sems = refs[:8], *refs[8:]
    cols = next_ref.shape[1]
    tile = cols // TILES

    def tile_copy(half, half_ref, i):
        at = slice(half * cols + i * tile, half * cols + (i + 1) * tile)
        return pltpu.make_async_copy(
            resident_ref.at[:, at], half_ref.at[:, i * tile : (i + 1) * tile], sems.at[half * TILES + i]
        )

    memory_copy = pltpu.make_async_copy(memory_ref.at[0], lhs_ref, sems.at[2 * TILES])
    first = [tile_copy(0, tile_ref, i) for i in range(TILES)]
    second = [tile_copy(1, next_ref, i) for i in range(TILES)]
    for copy in (memory_copy, *first):
        copy.start()
    memory_copy.wait()
    for i, copy in enumerate(first):
        copy.wait()
        second[i].start()
        at = slice(i * tile, (i + 1) * tile)
        product = jnp.dot(lhs_ref[...], tile_ref[:, at], preferred_element_type=f32)
        turned_ref[at, :] = product.T.astype(bf16)
    store_shares(place_ref, turned_ref, out_refs)
    for copy in second:
        copy.wait()


def first_product(place, memory, resident):
    _, rows, depth = memory.shape
    half = resident.shape[1] // 2
    outs = [(half // 8, rows)] * 8 + [(rows, depth), (depth, half)]
    *shares, lhs, resident_half = pl.pallas_call(
        first_product_kernel,
        in_specs=[SMEM] + [HBM] * 2,
        out_specs=[VMEM] * 10,
        out_shape=[jax.ShapeDtypeStruct(shape, bf16) for shape in outs],
        scratch_shapes=[
            pltpu.VMEM((depth, half), bf16),
            pltpu.VMEM((half, rows), bf16),
            pltpu.SemaphoreType.DMA((2 * TILES + 1,)),
        ],
        compiler_params=params(12),
        cost_estimate=cost(rows * depth * half * 2, 4 * depth * half),
        name="first_product",
    )(place, memory, resident)
    return shares, lhs, resident_half


def half_product_kernel(place_ref, lhs_ref, resident_ref, *refs):
    out_refs, turned_ref = refs[:8], refs[8]
    product = jnp.dot(lhs_ref[...], resident_ref[...], preferred_element_type=f32)
    turned_ref[...] = product.T.astype(bf16)
    store_shares(place_ref, turned_ref, out_refs)


def half_product(place, lhs, resident):
    rows, depth = lhs.shape
    cols = resident.shape[1]
    return pl.pallas_call(
        half_product_kernel,
        in_specs=[SMEM, VMEM, VMEM],
        out_specs=[VMEM] * 8,
        out_shape=[jax.ShapeDtypeStruct((cols // 8, rows), bf16)] * 8,
        scratch_shapes=[pltpu.VMEM((cols, rows), bf16)],
        compiler_params=params(6),
        cost_estimate=cost(2 * rows * depth * cols, 4 * cols * rows),
        name="half_product",
    )(place, lhs, resident)


def depth_rows(resident_ref, half, core):
    depth = resident_ref.shape[0]
    start = core * (depth // 2) + half * (depth // 4)
    return slice(start, start + depth // 4)


def early_product_kernel(lhs_ref, resident_ref, out_ref):
    quarter = lhs_ref.shape[1] // 2
    for n in range(2):
        at = slice(n * out_ref.shape[1] // 2, (n + 1) * out_ref.shape[1] // 2)
        out_ref[:, at] = sum(
            jnp.dot(
                lhs_ref[:, core * quarter : (core + 1) * quarter],
                resident_ref[depth_rows(resident_ref, 0, core), at],
                preferred_element_type=f32,
            )
            for core in range(2)
        )


def early_product(lhs, resident):
    rows, depth = lhs.shape
    cols = resident.shape[1]
    return pl.pallas_call(
        early_product_kernel,
        in_specs=[VMEM] * 2,
        out_specs=VMEM,
        out_shape=jax.ShapeDtypeStruct((rows, cols), f32),
        compiler_params=params(6),
        cost_estimate=cost(2 * rows * depth * cols, 4 * cols * rows),
        name="early_product",
    )(lhs, resident)


def late_product_kernel(n, place_ref, early_ref, lhs_ref, resident_ref, *refs):
    out_refs, turned_ref = refs[:8], refs[8]
    quarter, half = lhs_ref.shape[1] // 2, resident_ref.shape[1] // 2
    at = slice(n * half, (n + 1) * half)
    product = early_ref[:, at]
    for core in range(2):
        product = product + jnp.dot(
            lhs_ref[:, core * quarter : (core + 1) * quarter],
            resident_ref[depth_rows(resident_ref, 1, core), at],
            preferred_element_type=f32,
        )
    turned_ref[...] = product.T.astype(bf16)
    store_shares(place_ref, turned_ref, out_refs)


def late_product(n, place, early, lhs, resident):
    rows, depth = lhs.shape
    half = resident.shape[1] // 2
    return pl.pallas_call(
        functools.partial(late_product_kernel, n),
        in_specs=[SMEM] + [VMEM] * 3,
        out_specs=[VMEM] * 8,
        out_shape=[jax.ShapeDtypeStruct((half // 8, rows), bf16)] * 8,
        scratch_shapes=[pltpu.VMEM((half, rows), bf16)],
        compiler_params=params(6),
        cost_estimate=cost(2 * rows * depth * half, 4 * half * rows),
        name="late_product",
    )(place, early, lhs, resident)


def priors_kernel(place_ref, previous_ref, *refs):
    out_refs, block_ref, turned_ref, sems = refs[:4], *refs[4:]
    width = out_refs[0].shape[0]
    half = previous_ref.shape[2] // 2
    copies = []
    for k in range(4):
        start = (k & 1) * half + (place_ref[Y] >> 1) * 4 * width
        at = pl.ds(pl.multiple_of(start, 128), 4 * width)
        copies.append(pltpu.make_async_copy(previous_ref.at[k >> 1, :, at], block_ref.at[k], sems.at[k]))
        copies[k].start()
    for k, out_ref in enumerate(out_refs):
        copies[k].wait()
        turned_ref[...] = block_ref[k].astype(f32).T
        part = (place_ref[Y] & 1) * 2 + place_ref[ZL]
        out_ref[...] = turned_ref[rows_at(part, width), :].astype(bf16)


def priors(place, previous):
    _, rows, cols = previous.shape
    width = cols // 16
    return pl.pallas_call(
        priors_kernel,
        in_specs=[SMEM, HBM],
        out_specs=[VMEM] * 4,
        out_shape=[jax.ShapeDtypeStruct((width, rows), bf16)] * 4,
        scratch_shapes=[
            pltpu.VMEM((4, rows, 4 * width), bf16),
            pltpu.VMEM((4 * width, rows), f32),
            pltpu.SemaphoreType.DMA((4,)),
        ],
        compiler_params=params(6),
        cost_estimate=cost(0, 32 * width * rows),
        name="priors",
    )(place, previous)


def bring_kernel(after_ref, memory_ref, resident_ref, memory_out, resident_out, sems):
    copies = [
        pltpu.make_async_copy(memory_ref.at[1], memory_out, sems.at[0]),
        pltpu.make_async_copy(resident_ref, resident_out, sems.at[1]),
    ]
    for copy in copies:
        copy.start()
    for copy in copies:
        copy.wait()


def bring(after, memory, resident):
    _, rows, depth = memory.shape
    return pl.pallas_call(
        bring_kernel,
        in_specs=[SMEM] + [HBM] * 2,
        out_specs=[VMEM] * 2,
        out_shape=[
            jax.ShapeDtypeStruct((rows, depth), bf16),
            jax.ShapeDtypeStruct(resident.shape, bf16),
        ],
        scratch_shapes=[pltpu.SemaphoreType.DMA((2,))],
        compiler_params=params(6),
        cost_estimate=cost(0, 2 * (rows * depth + resident.size)),
        name="bring",
    )(after, memory, resident)


def next_memory_kernel(half, place_ref, memory_ref, *refs):
    pair_refs, out_ref, energy_ref = refs[:8], refs[8], refs[9]
    depth = memory_ref.shape[1]
    width = pair_refs[0].shape[1]
    shift = place_ref[X] ^ place_ref[Y]
    for side in range(2):
        core = place_ref[C] ^ side
        for d in range(4):
            pair = pair_refs[side * 4 + d]
            near = core * 8 + (shift ^ d) * 2 + place_ref[ZH]
            far = core * 8 + (shift ^ d ^ 2) * 2 + (place_ref[ZH] ^ 1)
            energy_ref[rows_at(near, width), :] = pair[0]
            energy_ref[rows_at(far, width), :] = pair[1]
    block = depth // 8
    for i in range(4):
        at = slice(i * block, (i + 1) * block)
        start = (i // 2) * (depth // 2) + half * (depth // 4) + (i % 2) * block
        old = memory_ref[:, start : start + block].astype(f32)
        out_ref[:, at] = (old + energy_ref[at, :].astype(f32).T).astype(bf16)


def next_memory(half, place, memory, pairs):
    rows, depth = memory.shape
    return pl.pallas_call(
        functools.partial(next_memory_kernel, half),
        in_specs=[SMEM] + [VMEM] * 9,
        out_specs=VMEM,
        out_shape=jax.ShapeDtypeStruct((rows, depth // 2), bf16),
        scratch_shapes=[pltpu.VMEM((depth // 2, rows), bf16)],
        compiler_params=params(6),
        cost_estimate=cost(rows * depth, 3 * rows * depth),
        name="next_memory",
    )(place, memory, *pairs)


def solve_into(part_refs, prior_ref, inverse_ref):
    summed = part_refs[0][...].astype(f32)
    for part_ref in part_refs[1:]:
        summed = summed + part_ref[...].astype(f32)
    source = prior_ref[...].astype(f32) - step_size * summed
    mixed = lax.dot_general(
        source,
        inverse_ref[...],
        (((1,), (1,)), ((), ())),
        precision=lax.Precision.HIGHEST,
        preferred_element_type=f32,
    )
    return (source + mixed).astype(bf16)


def flipped(values):
    rows, cols = values.shape
    strips = []
    pad = jnp.zeros((128 - ORB, 128), f32)
    for s in range(rows // ORB):
        pieces = []
        for q in range(cols // 128):
            block = values[s * ORB : (s + 1) * ORB, q * 128 : (q + 1) * 128]
            turned = jnp.concatenate([block, pad], axis=0).T
            piece = turned[:ORB]
            for t in range(1, 128 // ORB):
                piece = piece + pltpu.roll(turned[t * ORB : (t + 1) * ORB], t * ORB, 1)
            pieces.append(piece)
        strips.append(jnp.concatenate(pieces, axis=1))
    return jnp.concatenate(strips, axis=0)


def first_solve_kernel(*refs):
    front_ref, energy_ref = refs[11:]
    front = solve_into(refs[:8], refs[8], refs[9])
    front_ref[...] = front
    values = front.astype(f32)
    mirror = flipped(values)
    rows, cols = values.shape
    coupling = jnp.tile(refs[10][...], (rows // ORB, cols // 128))
    energy_ref[...] = (mirror * mirror * values * coupling).astype(bf16)


def second_solve_kernel(*refs):
    refs[10][...] = solve_into(refs[:8], refs[8], refs[9])


def solve(kernel, parts, prior, inverse, extra, outputs, name):
    width, rows = prior.shape
    return pl.pallas_call(
        kernel,
        in_specs=[VMEM] * (len(parts) + 2 + len(extra)),
        out_specs=[VMEM] * outputs,
        out_shape=[jax.ShapeDtypeStruct((width, rows), bf16)] * outputs,
        compiler_params=params(8),
        cost_estimate=cost(12 * rows * rows * width, 24 * rows * width),
        name=name,
    )(*parts, prior, inverse, *extra)


def put_blocks(turned_ref, block_ref, sems, out_ref, front, start):
    width = block_ref.shape[2]
    copies = []
    for i in range(turned_ref.shape[0] // width):
        at = slice(i * width, (i + 1) * width)
        block_ref[i] = turned_ref[at, :].astype(f32).T.astype(bf16)
        to = slice(start + i * width, start + (i + 1) * width)
        copies.append(pltpu.make_async_copy(block_ref.at[i], out_ref.at[front, :, to], sems.at[i]))
        copies[i].start()
    for copy in copies:
        copy.wait()


def join_one_kernel(front_ref, out_ref, turned_ref, block_ref, sems):
    cols = front_ref.shape[0]
    width = cols // 16
    for part in range(8):
        for half in range(2):
            to, at = (half * 8 + part) * width, (part * 2 + half) * width
            turned_ref[to : to + width, :] = front_ref[at : at + width, :]
    put_blocks(turned_ref, block_ref, sems, out_ref, 0, 0)


def join_one(front):
    cols, rows = front.shape
    return pl.pallas_call(
        join_one_kernel,
        in_specs=[VMEM],
        out_specs=HBM,
        out_shape=jax.ShapeDtypeStruct((2, rows, cols), bf16),
        scratch_shapes=[
            pltpu.VMEM((cols, rows), bf16),
            pltpu.VMEM((4, rows, cols // 4), bf16),
            pltpu.SemaphoreType.DMA((4,)),
        ],
        compiler_params=params(6),
        cost_estimate=cost(rows * cols, 4 * rows * cols),
        name="join_one",
    )(front)


def join_half_kernel(half, place_ref, *refs):
    chunk_refs, (out_ref, turned_ref, block_ref, sems) = refs[:8], refs[9:]
    width = chunk_refs[0].shape[0]
    for k, chunk_ref in enumerate(chunk_refs):
        turned_ref[rows_at(part_of(place_ref, k >> 1, k & 1), width), :] = chunk_ref[...]
    put_blocks(turned_ref, block_ref, sems, out_ref, 1, half * 8 * width)


def join_half(half, place, chunks, fronts):
    _, rows, cols = fronts.shape
    return pl.pallas_call(
        functools.partial(join_half_kernel, half),
        in_specs=[SMEM] + [VMEM] * 8 + [HBM],
        out_specs=HBM,
        out_shape=jax.ShapeDtypeStruct(fronts.shape, bf16),
        scratch_shapes=[
            pltpu.VMEM((cols // 2, rows), bf16),
            pltpu.VMEM((2, rows, cols // 4), bf16),
            pltpu.SemaphoreType.DMA((2,)),
        ],
        input_output_aliases={9: 0},
        compiler_params=params(6),
        cost_estimate=cost(rows * cols, 2 * rows * cols),
        name="join_half",
    )(place, *chunks, fronts)


def move(value, target):
    pairs = []
    for i in range(128):
        rest, c = divmod(i, 2)
        rest, zh = divmod(rest, 2)
        rest, x = divmod(rest, 4)
        y, zl = divmod(rest, 2)
        y, zl, x, zh = target(y, zl, x, zh)
        pairs.append((i, (((y * 2 + zl) * 4 + x) * 2 + zh) * 2 + c))
    return lax.ppermute(value, ALL, pairs)


ROUNDS = ((2, 1), (2, 0), (1, 1), (3, 1), (1, 0), (3, 0), (0, 1))


def exchange(shares):
    parts = [None] * 8
    for dy, dz in ROUNDS:
        k = dy * 2 + dz
        value = shares[k] if isinstance(shares, (list, tuple)) else shares
        parts[k] = move(value, lambda y, zl, x, zh: (y ^ dy, zl ^ dz, x, zh))
    parts[0] = shares[0] if isinstance(shares, (list, tuple)) else shares
    return parts


def after(value, others):
    return lax.optimization_barrier((value, others))


def turned(energy):
    near = move(energy, lambda y, zl, x, zh: (x, zh, x ^ y, zl))
    far = move(energy, lambda y, zl, x, zh: (x, zh, x ^ y ^ 2, zl ^ 1))
    return [near, far]


def spread(pair):
    own = [pair, None, None, None]
    for d in (2, 1, 3):
        own[d] = lax.ppermute(pair, "x", [(i, i ^ d) for i in range(4)])
    return own


def swapped(own):
    return [lax.ppermute(one, "c", SWAP) for one in own]


def per_device(resident, memory, previous, inverse_part, pair_coupling):
    place = jnp.stack([lax.axis_index(name) for name in ("x", "zh", "c", "y", "zl")]).astype(jnp.int32)
    coupling = jnp.tile(pair_coupling, (1, 128 // ORB))
    resident, memory, previous = in_hbm(resident), in_hbm(memory), in_hbm(previous)

    shares_a, lhs, resident_half = first_product(place, memory, resident)
    parts_a = exchange(shares_a)
    lhs, parts_a[4:6] = after(lhs, parts_a[4:6])
    shares_b = half_product(place, lhs, resident_half)
    parts_b = exchange(shares_b)
    later, parts_a = after(place, parts_a)
    prior_one_a, prior_one_b, prior_two_a, prior_two_b = priors(later, previous)
    front_a, energy_a = solve(
        first_solve_kernel, parts_a, prior_one_a, inverse_part[0], [coupling], 2, "first_solve"
    )
    turned_a = turned(energy_a)
    parts_b, turned_a = after(parts_b, turned_a)
    front_b, energy_b = solve(
        first_solve_kernel, parts_b, prior_one_b, inverse_part[0], [coupling], 2, "first_solve"
    )
    whole_one = lax.all_gather(jnp.concatenate([front_a, front_b]), PASTS, axis=0, tiled=True)
    turned_b = turned(energy_b)
    own_a = spread(jnp.stack(turned_a))
    later, _ = after(place, energy_b)
    memory, resident = bring(later, memory, resident)
    turned_b, (own_a, memory) = after(turned_b, (own_a, memory))
    own_b = spread(jnp.stack(turned_b))
    early = early_product(next_memory(0, place, memory, own_a + swapped(own_a)), resident)
    own_b, early = after(own_b, early)
    lhs = next_memory(1, place, memory, own_b + swapped(own_b))
    parts_a = exchange(late_product(0, place, early, lhs, resident))
    lhs, parts_a[4:6] = after(lhs, parts_a[4:6])
    parts_b = exchange(late_product(1, place, early, lhs, resident))
    (front_a,) = solve(
        second_solve_kernel, parts_a, prior_two_a, inverse_part[1], [], 1, "second_solve"
    )
    chunks_a = exchange(front_a)
    parts_b, chunks_a[4:6] = after(parts_b, chunks_a[4:6])
    (front_b,) = solve(
        second_solve_kernel, parts_b, prior_two_b, inverse_part[1], [], 1, "second_solve"
    )
    chunks_b = exchange(front_b)
    fronts = join_half(0, place, chunks_a, join_one(whole_one))
    chunks_b[4:6], fronts = after(chunks_b[4:6], fronts)
    return join_half(1, place, chunks_b, fronts)


def solution(mesh):
    fine = Mesh(mesh.devices.reshape(4, 2, 4, 2, 2), ALL)
    in_specs = (P(PASTS, SECONDS), P(None, None, PASTS), P(None, None, SECONDS), P(), P())
    out_specs = P(None, None, SECONDS)
    return jax.shard_map(
        per_device, mesh=fine, in_specs=in_specs, out_specs=out_specs, check_vma=False
    )
```

time: 407 us -> 161 us (0.40)
  waiting for transfers between devices: 267 us -> 11.2 us
  starting transfers between devices: 0.27 us -> 101 us
  local copies, waits for them, and re-layouts: 83.9 us -> 1.55 us
  matrix products: 32.8 us -> 0 us
  Pallas kernels: 0 us -> 31.9 us
  other arithmetic: 9.31 us -> 0.72 us
    psum x2 -> x0, waiting for transfers between devices: 147 us -> none  [advance(): lax.psum(partial_value.astype(jnp.bfloat16), 'past').astype(jnp.float32)]
    all_gather x1, waiting for transfers between devices: 119 us -> 0.01 us  [per_device(): lax.all_gather(jnp.concatenate([front_a, front_b]), PASTS, axis=0, tiled=...]
    ppermute x0 -> x60, starting transfers between devices: none -> 101 us  [the longest x46 89.6 us: move(): return lax.ppermute(value, ALL, pairs)]
    convert_element_type x3 -> x0, local copies, waits for them, and re-layouts: 49.3 us -> none  [per_device(): orbital_flip(gathered, orbitals).astype(jnp.float32)]
    dot_general x4 -> x0, matrix products: 32.8 us -> none  [the longest x2 19.9 us: advance(): jnp.dot(memory_row, resident, preferred_element_type=jnp.float32)]
    pallas_call x0 -> x16, Pallas kernels: none -> 31.9 us  [the longest x1 6.5 us: first_product(): pl.pallas_call(first_product_kernel, in_specs=[SMEM] + [HBM] * 2, out_spe...]
    reshape x2 -> x0, local copies, waits for them, and re-layouts: 12.6 us -> none  [the longest x1 7.74 us: orbital_flip(): return blocks.transpose(0, 3, 2, 1).reshape(row_count, col_count)]
    ppermute x0 -> x60, waiting for transfers between devices: none -> 11.2 us  [the longest x46 5.63 us: move(): return lax.ppermute(value, ALL, pairs)]
  transfers between devices with their start and end apart: 3 -> 61, of which waited for: 3 -> 10; matrix products, arithmetic and copies ran while one was open for 3% -> 0% of each run, Pallas kernels for 0% -> 14%
where the time goes in v6:
time: 161 us; the launch traced here: 160 us
  starting transfers between devices  101 us (63%)
  Pallas kernels  31.9 us (20%)
  between operations  13.8 us (9%)
  waiting for transfers between devices  11.2 us (7%)
    ppermute x46, starting transfers between devices, move(): return lax.ppermute(value, ALL, pairs)  89.6 us
    ppermute x6, starting transfers between devices, spread(): own[d] = lax.ppermute(pair, 'x', [(i, i ^ d) for i in range(4)])  9.32 us
    pallas_call x1, Pallas kernels, first_product(): pl.pallas_call(first_product_kernel, in_specs=[SMEM] + [HBM] * 2, out_spe...  6.5 us
    ppermute x46, waiting for transfers between devices, move(): return lax.ppermute(value, ALL, pairs)  5.63 us
    pallas_call x1, Pallas kernels, bring(): pl.pallas_call(bring_kernel, in_specs=[SMEM] + [HBM] * 2, out_specs=[VMEM...  4.96 us
    ppermute x6, waiting for transfers between devices, spread(): own[d] = lax.ppermute(pair, 'x', [(i, i ^ d) for i in range(4)])  4.21 us
    pallas_call x4, Pallas kernels, solve(): pl.pallas_call(kernel, in_specs=[VMEM] * (len(parts) + 2 + len(extra)), o...  3.54 us
    pallas_call x2, Pallas kernels, late_product(): pl.pallas_call(functools.partial(late_product_kernel, n), in_specs=[SMEM]...  3.5 us
  transfers between devices with their start and end apart: 61, of which 10 were waited for; matrix products, arithmetic and copies ran while one was open for 0% of the time, Pallas kernels for 14%

profile of v6, /device:TPU:0, one launch (start us, length us, event | category | flops | bytes accessed | tf_op | source)
XLA Modules:
  0.0 160.3 jit_solution(3730917555312264426)
XLA Ops:
  6.6 6.5 %first_product.1 = (bf16[96,384]{1,0:T(8,128)(2,1)S(1)}, bf16[96,384]{1,0:T(8,128)(2,1)S(1)}, bf16[96,384]{1,0:T(8,128)(2,1)S(1)}, bf16[96,384]{1,0:T(8,128)(2,1...) custom-call(s32[5]{0:T(128)S(1)} %stack.41.place_ref.after_ref, ...), custom_call_target="tpu_custom_call" | custom-call | flops 1811939328 | bytes 9437184 | tf_op jit(solution)/shard_map/first_product/pallas_call | solution.py:87
  13.1 3.4 %collective-permute-start = (bf16[96,384]{1,0:T(8,128)(2,1)S(1)}, bf16[96,384]{1,0:T(8,128)(2,1)S(1)}, u32[]{:S(2)}, u32[]{:S(2)}) collective-permute-start(bf16[96,384]{1,0:T(8,128)(2,1)S(1)} %get-tuple-element.101), channel_id=1, source_target_pairs={{0,64},{1,65},{2,66},{3,67},{4,68},{5,69},{6,70},{7,71},{8,72},{9,... | collective-permute-start | bytes 221192 | tf_op jit(solution)/shard_map/ppermute | solution.py:426
  16.5 1.7 %collective-permute-start.1 = (bf16[96,384]{1,0:T(8,128)(2,1)S(1)}, bf16[96,384]{1,0:T(8,128)(2,1)S(1)}, u32[]{:S(2)}, u32[]{:S(2)}) collective-permute-start(bf16[96,384]{1,0:T(8,128)(2,1)S(1)} %get-tuple-element.102), channel_id=1, source_target_pairs={{0,80},{1,81},{2,82},{3,83},{4,84},{5,85},{6,86},{7,87},{8,88},{9,... | collective-permute-start | bytes 221192 | tf_op jit(solution)/shard_map/ppermute | solution.py:426
  18.4 1.5 collective-permute-start.10
  19.9 1.8 %collective-permute-start.11 = (bf16[96,384]{1,0:T(8,128)(2,1)S(1)}, bf16[96,384]{1,0:T(8,128)(2,1)S(1)}, u32[]{:S(2)}, u32[]{:S(2)}) collective-permute-start(bf16[96,384]{1,0:T(8,128)(2,1)S(1)} %get-tuple-element.116), channel_id=1, source_target_pairs={{0,48},{1,49},{2,50},{3,51},{4,52},{5,53},{6,54},{7,55},{8,56},{9,... | collective-permute-start | bytes 221192 | tf_op jit(solution)/shard_map/ppermute | solution.py:426
  21.7 3.0 %collective-permute-start.12 = (bf16[96,384]{1,0:T(8,128)(2,1)S(1)}, bf16[96,384]{1,0:T(8,128)(2,1)S(1)}, u32[]{:S(2)}, u32[]{:S(2)}) collective-permute-start(bf16[96,384]{1,0:T(8,128)(2,1)S(1)} %get-tuple-element.119), channel_id=1, source_target_pairs={{0,96},{1,97},{2,98},{3,99},{4,100},{5,101},{6,102},{7,103},{8,104... | collective-permute-start | bytes 221192 | tf_op jit(solution)/shard_map/ppermute | solution.py:426
  24.7 1.4 collective-permute-start.13
  26.1 2.7 %half_product.1 = (bf16[96,384]{1,0:T(8,128)(2,1)S(1)}, bf16[96,384]{1,0:T(8,128)(2,1)S(1)}, bf16[96,384]{1,0:T(8,128)(2,1)S(1)}, bf16[96,384]{1,0:T(8,128)(2,1)...) custom-call(s32[5]{0:T(128)S(1)} %stack.41.place_ref.after_ref, ...), custom_call_target="tpu_custom_call" | custom-call | flops 1811939328 | bytes 1179648 | tf_op jit(solution)/shard_map/half_product/pallas_call | solution.py:114
  28.8 1.3 collective-permute-start.2
  30.1 2.2 %collective-permute-start.4 = (bf16[96,384]{1,0:T(8,128)(2,1)S(1)}, bf16[96,384]{1,0:T(8,128)(2,1)S(1)}, u32[]{:S(2)}, u32[]{:S(2)}) collective-permute-start(bf16[96,384]{1,0:T(8,128)(2,1)S(1)} %get-tuple-element.108), channel_id=1, source_target_pairs={{0,48},{1,49},{2,50},{3,51},{4,52},{5,53},{6,54},{7,55},{8,56},{9,... | collective-permute-start | bytes 221192 | tf_op jit(solution)/shard_map/ppermute | solution.py:426
  32.4 1.9 %collective-permute-start.5 = (bf16[96,384]{1,0:T(8,128)(2,1)S(1)}, bf16[96,384]{1,0:T(8,128)(2,1)S(1)}, u32[]{:S(2)}, u32[]{:S(2)}) collective-permute-start(bf16[96,384]{1,0:T(8,128)(2,1)S(1)} %get-tuple-element.109), channel_id=1, source_target_pairs={{0,64},{1,65},{2,66},{3,67},{4,68},{5,69},{6,70},{7,71},{8,72},{9,... | collective-permute-start | bytes 221192 | tf_op jit(solution)/shard_map/ppermute | solution.py:426
  34.5 2.4 %collective-permute-start.6 = (bf16[96,384]{1,0:T(8,128)(2,1)S(1)}, bf16[96,384]{1,0:T(8,128)(2,1)S(1)}, u32[]{:S(2)}, u32[]{:S(2)}) collective-permute-start(bf16[96,384]{1,0:T(8,128)(2,1)S(1)} %get-tuple-element.110), channel_id=1, source_target_pairs={{0,80},{1,81},{2,82},{3,83},{4,84},{5,85},{6,86},{7,87},{8,88},{9,... | collective-permute-start | bytes 221192 | tf_op jit(solution)/shard_map/ppermute | solution.py:426
  36.9 2.3 %priors.1 = (bf16[96,384]{1,0:T(8,128)(2,1)S(1)}, bf16[96,384]{1,0:T(8,128)(2,1)S(1)}, bf16[96,384]{1,0:T(8,128)(2,1)S(1)}, bf16[96,384]{1,0:T(8,128)(2,1)S(1)}) custom-call(s32[5]{0:T(128)S(1)} %stack.41.place_ref.after_ref, bf16[2,384,1536]{2,1,0:T(8,128)(2,1)} %previous_ref.1), custom_call_target="tpu_custom_call" | custom-call | bytes 1179648 | tf_op jit(solution)/shard_map/priors/pallas_call | solution.py:210
  40.2 2.1 %collective-permute-start.7 = (bf16[96,384]{1,0:T(8,128)(2,1)S(1)}, bf16[96,384]{1,0:T(8,128)(2,1)S(1)}, u32[]{:S(2)}, u32[]{:S(2)}) collective-permute-start(bf16[96,384]{1,0:T(8,128)(2,1)S(1)} %get-tuple-element.111), channel_id=1, source_target_pairs={{0,96},{1,97},{2,98},{3,99},{4,100},{5,101},{6,102},{7,103},{8,104... | collective-permute-start | bytes 221192 | tf_op jit(solution)/shard_map/ppermute | solution.py:426
  42.3 1.4 collective-permute-start.8
  44.4 7.3 %collective-permute-start.15 = (bf16[96,384]{1,0:T(8,128)(2,1)S(1)}, bf16[96,384]{1,0:T(8,128)(2,1)S(1)}, u32[]{:S(2)}, u32[]{:S(2)}) collective-permute-start(bf16[96,384]{1,0:T(8,128)(2,1)S(1)} %get-tuple-element.131), channel_id=1, source_target_pairs={{0,10},{1,11},{2,26},{3,27},{4,46},{5,47},{6,62},{7,63},{8,66},{9,... | collective-permute-start | bytes 221192 | tf_op jit(solution)/shard_map/ppermute | solution.py:426
  51.8 4.7 %collective-permute-done.15 = bf16[96,384]{1,0:T(8,128)(2,1)S(1)} collective-permute-done((bf16[96,384]{1,0:T(8,128)(2,1)S(1)}, bf16[96,384]{1,0:T(8,128)(2,1)S(1)}, u32[]{:S(2)}, u32[]{:S(2)}) %collective-permute-start.15) | collective-permute-done | bytes 73760 | tf_op jit(solution)/shard_map/ppermute | solution.py:426
  59.2 2.4 %collective-permute-start.19 = (bf16[2,96,384]{2,1,0:T(8,128)(2,1)S(1)}, bf16[2,96,384]{2,1,0:T(8,128)(2,1)S(1)}, u32[]{:S(2)}, u32[]{:S(2)}) collective-permute-start(bf16[2,96,384]{2,1,0:T(8,128)(2,1)S(1)} %pad_maximum_fusion.refs_0_), channel_id=1, source_target_pairs={{0,8},{4,12},{8,0},{12,4},{1,9},{5,13},{9,1},{13,5},{2,10},{6,14},... | collective-permute-start | bytes 442376 | tf_op jit(solution)/shard_map/ppermute | solution.py:455
  61.5 1.4 collective-permute-start.20
  63.6 11.5 %collective-permute-start.17 = (bf16[96,384]{1,0:T(8,128)(2,1)S(1)}, bf16[96,384]{1,0:T(8,128)(2,1)S(1)}, u32[]{:S(2)}, u32[]{:S(2)}) collective-permute-start(bf16[96,384]{1,0:T(8,128)(2,1)S(1)} %get-tuple-element.141), channel_id=1, source_target_pairs={{0,10},{1,11},{2,26},{3,27},{4,46},{5,47},{6,62},{7,63},{8,66},{9,... | collective-permute-start | bytes 221192 | tf_op jit(solution)/shard_map/ppermute | solution.py:426
  75.1 5.0 %bring.1 = (bf16[384,3072]{1,0:T(8,128)(2,1)S(1)}, bf16[3072,1536]{1,0:T(8,128)(2,1)S(1)}) custom-call(s32[5]{0:T(128)S(1)} %stack.41.place_ref.after_ref, bf16[2,384,3072]{2,1,0:T(8,128)(2,1)} %memory_ref.3, bf16[3072,1536]{1,0:T(8,128)(2,1)} %resident_ref.3), custom_call_target="tpu_custom_call" | custom-call | bytes 11796480 | tf_op jit(solution)/shard_map/bring/pallas_call | solution.py:239
  81.7 2.2 %collective-permute-start.22 = (bf16[2,96,384]{2,1,0:T(8,128)(2,1)S(1)}, bf16[2,96,384]{2,1,0:T(8,128)(2,1)S(1)}, u32[]{:S(2)}, u32[]{:S(2)}) collective-permute-start(bf16[2,96,384]{2,1,0:T(8,128)(2,1)S(1)} %pad_maximum_fusion.1.refs_0_), channel_id=1, source_target_pairs={{0,8},{4,12},{8,0},{12,4},{1,9},{5,13},{9,1},{13,5},{2,10},{6,14},... | collective-permute-start | bytes 442376 | tf_op jit(solution)/shard_map/ppermute | solution.py:455
  84.0 2.2 %collective-permute-start.23 = (bf16[2,96,384]{2,1,0:T(8,128)(2,1)S(1)}, bf16[2,96,384]{2,1,0:T(8,128)(2,1)S(1)}, u32[]{:S(2)}, u32[]{:S(2)}) collective-permute-start(bf16[2,96,384]{2,1,0:T(8,128)(2,1)S(1)} %pad_maximum_fusion.1.refs_0_), channel_id=1, source_target_pairs={{0,12},{4,8},{8,4},{12,0},{1,13},{5,9},{9,5},{13,1},{2,14},{6,10},... | collective-permute-start | bytes 442376 | tf_op jit(solution)/shard_map/ppermute | solution.py:455
  87.3 2.0 %early_product.1.early_ref = f32[384,1536]{1,0:T(8,128)S(1)} custom-call(bf16[384,1536]{1,0:T(8,128)(2,1)S(1)} %next_memory.2.lhs_ref, bf16[3072,1536]{1,0:T(8,128)(2,1)S(1)} %get-tuple-element.153.resident_ref), custom_call_target="tpu_custom_call" | custom-call | flops 1811939328 | bytes 2359296 | tf_op jit(solution)/shard_map/early_product/pallas_call | solution.py:149
  89.3 1.8 %collective-permute-done.22.refs_2_ = bf16[2,96,384]{2,1,0:T(8,128)(2,1)S(1)} collective-permute-done((bf16[2,96,384]{2,1,0:T(8,128)(2,1)S(1)}, bf16[2,96,384]{2,1,0:T(8,128)(2,1)S(1)}, u32[]{:S(2)}, u32[]{:S(2)}) %collective-permute-start.22) | collective-permute-done | bytes 147488 | tf_op jit(solution)/shard_map/ppermute | solution.py:455
  91.0 2.4 %collective-permute-done.23.refs_3_ = bf16[2,96,384]{2,1,0:T(8,128)(2,1)S(1)} collective-permute-done((bf16[2,96,384]{2,1,0:T(8,128)(2,1)S(1)}, bf16[2,96,384]{2,1,0:T(8,128)(2,1)S(1)}, u32[]{:S(2)}, u32[]{:S(2)}) %collective-permute-start.23) | collective-permute-done | bytes 147488 | tf_op jit(solution)/shard_map/ppermute | solution.py:455
  96.6 1.8 %late_product.2 = (bf16[96,384]{1,0:T(8,128)(2,1)S(1)}, bf16[96,384]{1,0:T(8,128)(2,1)S(1)}, bf16[96,384]{1,0:T(8,128)(2,1)S(1)}, bf16[96,384]{1,0:T(8,128)(2,1)...) custom-call(s32[5]{0:T(128)S(1)} %stack.41.place_ref.after_ref, ...), custom_call_target="tpu_custom_call" | custom-call | flops 905969664 | bytes 1179648 | tf_op jit(solution)/shard_map/late_product/pallas_call | solution.py:178
  98.4 2.7 %collective-permute-start.32 = (bf16[96,384]{1,0:T(8,128)(2,1)S(1)}, bf16[96,384]{1,0:T(8,128)(2,1)S(1)}, u32[]{:S(2)}, u32[]{:S(2)}) collective-permute-start(bf16[96,384]{1,0:T(8,128)(2,1)S(1)} %get-tuple-element.159), channel_id=1, source_target_pairs={{0,64},{1,65},{2,66},{3,67},{4,68},{5,69},{6,70},{7,71},{8,72},{9,... | collective-permute-start | bytes 221192 | tf_op jit(solution)/shard_map/ppermute | solution.py:426
  102.2 1.2 collective-permute-start.41
  103.4 2.3 %collective-permute-start.42 = (bf16[96,384]{1,0:T(8,128)(2,1)S(1)}, bf16[96,384]{1,0:T(8,128)(2,1)S(1)}, u32[]{:S(2)}, u32[]{:S(2)}) collective-permute-start(bf16[96,384]{1,0:T(8,128)(2,1)S(1)} %get-tuple-element.172), channel_id=1, source_target_pairs={{0,32},{1,33},{2,34},{3,35},{4,36},{5,37},{6,38},{7,39},{8,40},{9,... | collective-permute-start | bytes 221192 | tf_op jit(solution)/shard_map/ppermute | solution.py:426
  105.7 2.0 %collective-permute-start.44 = (bf16[96,384]{1,0:T(8,128)(2,1)S(1)}, bf16[96,384]{1,0:T(8,128)(2,1)S(1)}, u32[]{:S(2)}, u32[]{:S(2)}) collective-permute-start(bf16[96,384]{1,0:T(8,128)(2,1)S(1)} %get-tuple-element.176), channel_id=1, source_target_pairs={{0,96},{1,97},{2,98},{3,99},{4,100},{5,101},{6,102},{7,103},{8,104... | collective-permute-start | bytes 221192 | tf_op jit(solution)/shard_map/ppermute | solution.py:426
  108.3 1.5 collective-permute-start.45
  109.9 1.7 %late_product.3 = (bf16[96,384]{1,0:T(8,128)(2,1)S(1)}, bf16[96,384]{1,0:T(8,128)(2,1)S(1)}, bf16[96,384]{1,0:T(8,128)(2,1)S(1)}, bf16[96,384]{1,0:T(8,128)(2,1)...) custom-call(s32[5]{0:T(128)S(1)} %stack.41.place_ref.after_ref, ...), custom_call_target="tpu_custom_call" | custom-call | flops 905969664 | bytes 1179648 | tf_op jit(solution)/shard_map/late_product/pallas_call | solution.py:178
  111.6 2.6 %collective-permute-start.34 = (bf16[96,384]{1,0:T(8,128)(2,1)S(1)}, bf16[96,384]{1,0:T(8,128)(2,1)S(1)}, u32[]{:S(2)}, u32[]{:S(2)}) collective-permute-start(bf16[96,384]{1,0:T(8,128)(2,1)S(1)} %get-tuple-element.163), channel_id=1, source_target_pairs={{0,16},{1,17},{2,18},{3,19},{4,20},{5,21},{6,22},{7,23},{8,24},{9,... | collective-permute-start | bytes 221192 | tf_op jit(solution)/shard_map/ppermute | solution.py:426
  114.2 1.6 collective-permute-start.36
  115.8 1.9 %collective-permute-start.37 = (bf16[96,384]{1,0:T(8,128)(2,1)S(1)}, bf16[96,384]{1,0:T(8,128)(2,1)S(1)}, u32[]{:S(2)}, u32[]{:S(2)}) collective-permute-start(bf16[96,384]{1,0:T(8,128)(2,1)S(1)} %get-tuple-element.166), channel_id=1, source_target_pairs={{0,64},{1,65},{2,66},{3,67},{4,68},{5,69},{6,70},{7,71},{8,72},{9,... | collective-permute-start | bytes 221192 | tf_op jit(solution)/shard_map/ppermute | solution.py:426
  117.7 3.0 %collective-permute-start.38 = (bf16[96,384]{1,0:T(8,128)(2,1)S(1)}, bf16[96,384]{1,0:T(8,128)(2,1)S(1)}, u32[]{:S(2)}, u32[]{:S(2)}) collective-permute-start(bf16[96,384]{1,0:T(8,128)(2,1)S(1)} %get-tuple-element.167), channel_id=1, source_target_pairs={{0,80},{1,81},{2,82},{3,83},{4,84},{5,85},{6,86},{7,87},{8,88},{9,... | collective-permute-start | bytes 221192 | tf_op jit(solution)/shard_map/ppermute | solution.py:426
  122.1 2.2 %collective-permute-start.40 = (bf16[96,384]{1,0:T(8,128)(2,1)S(1)}, bf16[96,384]{1,0:T(8,128)(2,1)S(1)}, u32[]{:S(2)}, u32[]{:S(2)}) collective-permute-start(bf16[96,384]{1,0:T(8,128)(2,1)S(1)} %get-tuple-element.169), channel_id=1, source_target_pairs={{0,112},{1,113},{2,114},{3,115},{4,116},{5,117},{6,118},{7,119},{8... | collective-permute-start | bytes 221192 | tf_op jit(solution)/shard_map/ppermute | solution.py:426
  125.0 4.2 %collective-permute-start.47 = (bf16[96,384]{1,0:T(8,128)(2,1)S(1)}, bf16[96,384]{1,0:T(8,128)(2,1)S(1)}, u32[]{:S(2)}, u32[]{:S(2)}) collective-permute-start(bf16[96,384]{1,0:T(8,128)(2,1)S(1)} %second_solve.2.refs_0_), channel_id=1, source_target_pairs={{0,80},{1,81},{2,82},{3,83},{4,84},{5,85},{6,86},{7,87},{8,88},{9,... | collective-permute-start | bytes 221192 | tf_op jit(solution)/shard_map/ppermute | solution.py:426
  129.3 3.4 %collective-permute-start.55 = (bf16[96,384]{1,0:T(8,128)(2,1)S(1)}, bf16[96,384]{1,0:T(8,128)(2,1)S(1)}, u32[]{:S(2)}, u32[]{:S(2)}) collective-permute-start(bf16[96,384]{1,0:T(8,128)(2,1)S(1)} %second_solve.2.refs_0_), channel_id=1, source_target_pairs={{0,48},{1,49},{2,50},{3,51},{4,52},{5,53},{6,54},{7,55},{8,56},{9,... | collective-permute-start | bytes 221192 | tf_op jit(solution)/shard_map/ppermute | solution.py:426
  133.4 2.1 %collective-permute-start.57 = (bf16[96,384]{1,0:T(8,128)(2,1)S(1)}, bf16[96,384]{1,0:T(8,128)(2,1)S(1)}, u32[]{:S(2)}, u32[]{:S(2)}) collective-permute-start(bf16[96,384]{1,0:T(8,128)(2,1)S(1)} %second_solve.2.refs_0_), channel_id=1, source_target_pairs={{0,112},{1,113},{2,114},{3,115},{4,116},{5,117},{6,118},{7,119},{8... | collective-permute-start | bytes 221192 | tf_op jit(solution)/shard_map/ppermute | solution.py:426
  137.2 4.0 %collective-permute-start.52 = (bf16[96,384]{1,0:T(8,128)(2,1)S(1)}, bf16[96,384]{1,0:T(8,128)(2,1)S(1)}, u32[]{:S(2)}, u32[]{:S(2)}) collective-permute-start(bf16[96,384]{1,0:T(8,128)(2,1)S(1)} %second_solve.3.refs_0_), channel_id=1, source_target_pairs={{0,80},{1,81},{2,82},{3,83},{4,84},{5,85},{6,86},{7,87},{8,88},{9,... | collective-permute-start | bytes 221192 | tf_op jit(solution)/shard_map/ppermute | solution.py:426
  141.8 3.0 %collective-permute-start.50 = (bf16[96,384]{1,0:T(8,128)(2,1)S(1)}, bf16[96,384]{1,0:T(8,128)(2,1)S(1)}, u32[]{:S(2)}, u32[]{:S(2)}) collective-permute-start(bf16[96,384]{1,0:T(8,128)(2,1)S(1)} %second_solve.3.refs_0_), channel_id=1, source_target_pairs={{0,48},{1,49},{2,50},{3,51},{4,52},{5,53},{6,54},{7,55},{8,56},{9,... | collective-permute-start | bytes 221192 | tf_op jit(solution)/shard_map/ppermute | solution.py:426
  145.4 2.1 %collective-permute-start.59 = (bf16[96,384]{1,0:T(8,128)(2,1)S(1)}, bf16[96,384]{1,0:T(8,128)(2,1)S(1)}, u32[]{:S(2)}, u32[]{:S(2)}) collective-permute-start(bf16[96,384]{1,0:T(8,128)(2,1)S(1)} %second_solve.3.refs_0_), channel_id=1, source_target_pairs={{0,112},{1,113},{2,114},{3,115},{4,116},{5,117},{6,118},{7,119},{8... | collective-permute-start | bytes 221192 | tf_op jit(solution)/shard_map/ppermute | solution.py:426
  147.5 1.3 copy-done
  148.8 1.2 join_one.1.refs_8_
  150.0 1.6 %join_half.2.refs_8_ = bf16[2,384,1536]{2,1,0:T(8,128)(2,1)} custom-call(s32[5]{0:T(128)S(1)} %stack.41.place_ref.after_ref, bf16[96,384]{1,0:T(8,128)(2,1)S(1)} %second_solve.2.refs_0_, bf16[96,384]{1,0:T(8,128)(2,1)S(1)} %collective-permute-done.53.refs_1_, bf16[96,384]{1,0:T(8,128)(2,1)S(1)} %collective-permute-done.54.refs_2_, ...), custom_call_target="tpu_custom_call", output_to_operand_aliasing={{}: (9, {})} | custom-call | flops 589824 | bytes 1179648 | tf_op jit(solution)/shard_map/join_half/pallas_call | solution.py:400
  151.9 1.6 join_half.3
  (104 shorter events, 19.3 us)
Async XLA Ops:
  6.5 141.0 %all-gather.2.cloned.1.call-start = ((), (), s32[]{:S(2)}) async-start(), calls=%async_computation | async-start | bytes 1327104 | tf_op jit(solution)/shard_map/all_gather | solution.py:483
  13.1 8.5 %collective-permute-start = (bf16[96,384]{1,0:T(8,128)(2,1)S(1)}, bf16[96,384]{1,0:T(8,128)(2,1)S(1)}, u32[]{:S(2)}, u32[]{:S(2)}) collective-permute-start(bf16[96,384]{1,0:T(8,128)(2,1)S(1)} %get-tuple-element.101), channel_id=1, source_target_pairs={{0,64},{1,65},{2,66},{3,67},{4,68},{5,69},{6,70},{7,71},{8,72},{9,... | collective-permute-start | bytes 221192 | tf_op jit(solution)/shard_map/ppermute | solution.py:426
  16.5 8.2 %collective-permute-start.1 = (bf16[96,384]{1,0:T(8,128)(2,1)S(1)}, bf16[96,384]{1,0:T(8,128)(2,1)S(1)}, u32[]{:S(2)}, u32[]{:S(2)}) collective-permute-start(bf16[96,384]{1,0:T(8,128)(2,1)S(1)} %get-tuple-element.102), channel_id=1, source_target_pairs={{0,80},{1,81},{2,82},{3,83},{4,84},{5,85},{6,86},{7,87},{8,88},{9,... | collective-permute-start | bytes 221192 | tf_op jit(solution)/shard_map/ppermute | solution.py:426
  18.2 10.6 %collective-permute-start.9 = (bf16[96,384]{1,0:T(8,128)(2,1)S(1)}, bf16[96,384]{1,0:T(8,128)(2,1)S(1)}, u32[]{:S(2)}, u32[]{:S(2)}) collective-permute-start(bf16[96,384]{1,0:T(8,128)(2,1)S(1)} %get-tuple-element.114), channel_id=1, source_target_pairs={{0,16},{1,17},{2,18},{3,19},{4,20},{5,21},{6,22},{7,23},{8,24},{9,... | collective-permute-start | bytes 221192 | tf_op jit(solution)/shard_map/ppermute | solution.py:426
  18.4 11.7 %collective-permute-start.10 = (bf16[96,384]{1,0:T(8,128)(2,1)S(1)}, bf16[96,384]{1,0:T(8,128)(2,1)S(1)}, u32[]{:S(2)}, u32[]{:S(2)}) collective-permute-start(bf16[96,384]{1,0:T(8,128)(2,1)S(1)} %get-tuple-element.115), channel_id=1, source_target_pairs={{0,32},{1,33},{2,34},{3,35},{4,36},{5,37},{6,38},{7,39},{8,40},{9,... | collective-permute-start | bytes 221192 | tf_op jit(solution)/shard_map/ppermute | solution.py:426
  19.9 10.3 %collective-permute-start.11 = (bf16[96,384]{1,0:T(8,128)(2,1)S(1)}, bf16[96,384]{1,0:T(8,128)(2,1)S(1)}, u32[]{:S(2)}, u32[]{:S(2)}) collective-permute-start(bf16[96,384]{1,0:T(8,128)(2,1)S(1)} %get-tuple-element.116), channel_id=1, source_target_pairs={{0,48},{1,49},{2,50},{3,51},{4,52},{5,53},{6,54},{7,55},{8,56},{9,... | collective-permute-start | bytes 221192 | tf_op jit(solution)/shard_map/ppermute | solution.py:426
  21.7 10.7 %collective-permute-start.12 = (bf16[96,384]{1,0:T(8,128)(2,1)S(1)}, bf16[96,384]{1,0:T(8,128)(2,1)S(1)}, u32[]{:S(2)}, u32[]{:S(2)}) collective-permute-start(bf16[96,384]{1,0:T(8,128)(2,1)S(1)} %get-tuple-element.119), channel_id=1, source_target_pairs={{0,96},{1,97},{2,98},{3,99},{4,100},{5,101},{6,102},{7,103},{8,104... | collective-permute-start | bytes 221192 | tf_op jit(solution)/shard_map/ppermute | solution.py:426
  24.7 9.8 %collective-permute-start.13 = (bf16[96,384]{1,0:T(8,128)(2,1)S(1)}, bf16[96,384]{1,0:T(8,128)(2,1)S(1)}, u32[]{:S(2)}, u32[]{:S(2)}) collective-permute-start(bf16[96,384]{1,0:T(8,128)(2,1)S(1)} %get-tuple-element.120), channel_id=1, source_target_pairs={{0,112},{1,113},{2,114},{3,115},{4,116},{5,117},{6,118},{7,119},{8... | collective-permute-start | bytes 221192 | tf_op jit(solution)/shard_map/ppermute | solution.py:426
  28.8 11.4 %collective-permute-start.2 = (bf16[96,384]{1,0:T(8,128)(2,1)S(1)}, bf16[96,384]{1,0:T(8,128)(2,1)S(1)}, u32[]{:S(2)}, u32[]{:S(2)}) collective-permute-start(bf16[96,384]{1,0:T(8,128)(2,1)S(1)} %get-tuple-element.106), channel_id=1, source_target_pairs={{0,16},{1,17},{2,18},{3,19},{4,20},{5,21},{6,22},{7,23},{8,24},{9,... | collective-permute-start | bytes 221192 | tf_op jit(solution)/shard_map/ppermute | solution.py:426
  30.1 12.2 %collective-permute-start.3 = (bf16[96,384]{1,0:T(8,128)(2,1)S(1)}, bf16[96,384]{1,0:T(8,128)(2,1)S(1)}, u32[]{:S(2)}, u32[]{:S(2)}) collective-permute-start(bf16[96,384]{1,0:T(8,128)(2,1)S(1)} %get-tuple-element.107), channel_id=1, source_target_pairs={{0,32},{1,33},{2,34},{3,35},{4,36},{5,37},{6,38},{7,39},{8,40},{9,... | collective-permute-start | bytes 221192 | tf_op jit(solution)/shard_map/ppermute | solution.py:426
  30.1 13.6 %collective-permute-start.4 = (bf16[96,384]{1,0:T(8,128)(2,1)S(1)}, bf16[96,384]{1,0:T(8,128)(2,1)S(1)}, u32[]{:S(2)}, u32[]{:S(2)}) collective-permute-start(bf16[96,384]{1,0:T(8,128)(2,1)S(1)} %get-tuple-element.108), channel_id=1, source_target_pairs={{0,48},{1,49},{2,50},{3,51},{4,52},{5,53},{6,54},{7,55},{8,56},{9,... | collective-permute-start | bytes 221192 | tf_op jit(solution)/shard_map/ppermute | solution.py:426
  32.4 12.0 %collective-permute-start.5 = (bf16[96,384]{1,0:T(8,128)(2,1)S(1)}, bf16[96,384]{1,0:T(8,128)(2,1)S(1)}, u32[]{:S(2)}, u32[]{:S(2)}) collective-permute-start(bf16[96,384]{1,0:T(8,128)(2,1)S(1)} %get-tuple-element.109), channel_id=1, source_target_pairs={{0,64},{1,65},{2,66},{3,67},{4,68},{5,69},{6,70},{7,71},{8,72},{9,... | collective-permute-start | bytes 221192 | tf_op jit(solution)/shard_map/ppermute | solution.py:426
  34.5 17.3 %collective-permute-start.6 = (bf16[96,384]{1,0:T(8,128)(2,1)S(1)}, bf16[96,384]{1,0:T(8,128)(2,1)S(1)}, u32[]{:S(2)}, u32[]{:S(2)}) collective-permute-start(bf16[96,384]{1,0:T(8,128)(2,1)S(1)} %get-tuple-element.110), channel_id=1, source_target_pairs={{0,80},{1,81},{2,82},{3,83},{4,84},{5,85},{6,86},{7,87},{8,88},{9,... | collective-permute-start | bytes 221192 | tf_op jit(solution)/shard_map/ppermute | solution.py:426
  40.2 11.5 %collective-permute-start.7 = (bf16[96,384]{1,0:T(8,128)(2,1)S(1)}, bf16[96,384]{1,0:T(8,128)(2,1)S(1)}, u32[]{:S(2)}, u32[]{:S(2)}) collective-permute-start(bf16[96,384]{1,0:T(8,128)(2,1)S(1)} %get-tuple-element.111), channel_id=1, source_target_pairs={{0,96},{1,97},{2,98},{3,99},{4,100},{5,101},{6,102},{7,103},{8,104... | collective-permute-start | bytes 221192 | tf_op jit(solution)/shard_map/ppermute | solution.py:426
  42.3 9.4 %collective-permute-start.8 = (bf16[96,384]{1,0:T(8,128)(2,1)S(1)}, bf16[96,384]{1,0:T(8,128)(2,1)S(1)}, u32[]{:S(2)}, u32[]{:S(2)}) collective-permute-start(bf16[96,384]{1,0:T(8,128)(2,1)S(1)} %get-tuple-element.112), channel_id=1, source_target_pairs={{0,112},{1,113},{2,114},{3,115},{4,116},{5,117},{6,118},{7,119},{8... | collective-permute-start | bytes 221192 | tf_op jit(solution)/shard_map/ppermute | solution.py:426
  43.7 8.0 %collective-permute-start.14 = (bf16[96,384]{1,0:T(8,128)(2,1)S(1)}, bf16[96,384]{1,0:T(8,128)(2,1)S(1)}, u32[]{:S(2)}, u32[]{:S(2)}) collective-permute-start(bf16[96,384]{1,0:T(8,128)(2,1)S(1)} %get-tuple-element.131), channel_id=1, source_target_pairs={{0,0},{1,1},{2,16},{3,17},{4,36},{5,37},{6,52},{7,53},{8,72},{9,73... | collective-permute-start | bytes 221192 | tf_op jit(solution)/shard_map/ppermute | solution.py:426
  44.4 12.0 %collective-permute-start.15 = (bf16[96,384]{1,0:T(8,128)(2,1)S(1)}, bf16[96,384]{1,0:T(8,128)(2,1)S(1)}, u32[]{:S(2)}, u32[]{:S(2)}) collective-permute-start(bf16[96,384]{1,0:T(8,128)(2,1)S(1)} %get-tuple-element.131), channel_id=1, source_target_pairs={{0,10},{1,11},{2,26},{3,27},{4,46},{5,47},{6,62},{7,63},{8,66},{9,... | collective-permute-start | bytes 221192 | tf_op jit(solution)/shard_map/ppermute | solution.py:426
  58.2 21.9 %collective-permute-start.18 = (bf16[2,96,384]{2,1,0:T(8,128)(2,1)S(1)}, bf16[2,96,384]{2,1,0:T(8,128)(2,1)S(1)}, u32[]{:S(2)}, u32[]{:S(2)}) collective-permute-start(bf16[2,96,384]{2,1,0:T(8,128)(2,1)S(1)} %pad_maximum_fusion.refs_0_), channel_id=1, source_target_pairs={{0,4},{4,0},{8,12},{12,8},{1,5},{5,1},{9,13},{13,9},{2,6},{6,2},{1... | collective-permute-start | bytes 442376 | tf_op jit(solution)/shard_map/ppermute | solution.py:455
  59.2 20.9 %collective-permute-start.19 = (bf16[2,96,384]{2,1,0:T(8,128)(2,1)S(1)}, bf16[2,96,384]{2,1,0:T(8,128)(2,1)S(1)}, u32[]{:S(2)}, u32[]{:S(2)}) collective-permute-start(bf16[2,96,384]{2,1,0:T(8,128)(2,1)S(1)} %pad_maximum_fusion.refs_0_), channel_id=1, source_target_pairs={{0,8},{4,12},{8,0},{12,4},{1,9},{5,13},{9,1},{13,5},{2,10},{6,14},... | collective-permute-start | bytes 442376 | tf_op jit(solution)/shard_map/ppermute | solution.py:455
  61.5 18.6 %collective-permute-start.20 = (bf16[2,96,384]{2,1,0:T(8,128)(2,1)S(1)}, bf16[2,96,384]{2,1,0:T(8,128)(2,1)S(1)}, u32[]{:S(2)}, u32[]{:S(2)}) collective-permute-start(bf16[2,96,384]{2,1,0:T(8,128)(2,1)S(1)} %pad_maximum_fusion.refs_0_), channel_id=1, source_target_pairs={{0,12},{4,8},{8,4},{12,0},{1,13},{5,9},{9,5},{13,1},{2,14},{6,10},... | collective-permute-start | bytes 442376 | tf_op jit(solution)/shard_map/ppermute | solution.py:455
  63.0 17.1 %collective-permute-start.16 = (bf16[96,384]{1,0:T(8,128)(2,1)S(1)}, bf16[96,384]{1,0:T(8,128)(2,1)S(1)}, u32[]{:S(2)}, u32[]{:S(2)}) collective-permute-start(bf16[96,384]{1,0:T(8,128)(2,1)S(1)} %get-tuple-element.141), channel_id=1, source_target_pairs={{0,0},{1,1},{2,16},{3,17},{4,36},{5,37},{6,52},{7,53},{8,72},{9,73... | collective-permute-start | bytes 221192 | tf_op jit(solution)/shard_map/ppermute | solution.py:426
  63.6 16.4 %collective-permute-start.17 = (bf16[96,384]{1,0:T(8,128)(2,1)S(1)}, bf16[96,384]{1,0:T(8,128)(2,1)S(1)}, u32[]{:S(2)}, u32[]{:S(2)}) collective-permute-start(bf16[96,384]{1,0:T(8,128)(2,1)S(1)} %get-tuple-element.141), channel_id=1, source_target_pairs={{0,10},{1,11},{2,26},{3,27},{4,46},{5,47},{6,62},{7,63},{8,66},{9,... | collective-permute-start | bytes 221192 | tf_op jit(solution)/shard_map/ppermute | solution.py:426
  81.4 7.8 %collective-permute-start.21 = (bf16[2,96,384]{2,1,0:T(8,128)(2,1)S(1)}, bf16[2,96,384]{2,1,0:T(8,128)(2,1)S(1)}, u32[]{:S(2)}, u32[]{:S(2)}) collective-permute-start(bf16[2,96,384]{2,1,0:T(8,128)(2,1)S(1)} %pad_maximum_fusion.1.refs_0_), channel_id=1, source_target_pairs={{0,4},{4,0},{8,12},{12,8},{1,5},{5,1},{9,13},{13,9},{2,6},{6,2},{1... | collective-permute-start | bytes 442376 | tf_op jit(solution)/shard_map/ppermute | solution.py:455
  81.7 9.3 %collective-permute-start.22 = (bf16[2,96,384]{2,1,0:T(8,128)(2,1)S(1)}, bf16[2,96,384]{2,1,0:T(8,128)(2,1)S(1)}, u32[]{:S(2)}, u32[]{:S(2)}) collective-permute-start(bf16[2,96,384]{2,1,0:T(8,128)(2,1)S(1)} %pad_maximum_fusion.1.refs_0_), channel_id=1, source_target_pairs={{0,8},{4,12},{8,0},{12,4},{1,9},{5,13},{9,1},{13,5},{2,10},{6,14},... | collective-permute-start | bytes 442376 | tf_op jit(solution)/shard_map/ppermute | solution.py:455
  84.0 9.5 %collective-permute-start.23 = (bf16[2,96,384]{2,1,0:T(8,128)(2,1)S(1)}, bf16[2,96,384]{2,1,0:T(8,128)(2,1)S(1)}, u32[]{:S(2)}, u32[]{:S(2)}) collective-permute-start(bf16[2,96,384]{2,1,0:T(8,128)(2,1)S(1)} %pad_maximum_fusion.1.refs_0_), channel_id=1, source_target_pairs={{0,12},{4,8},{8,4},{12,0},{1,13},{5,9},{9,5},{13,1},{2,14},{6,10},... | collective-permute-start | bytes 442376 | tf_op jit(solution)/shard_map/ppermute | solution.py:455
  98.4 7.4 %collective-permute-start.32 = (bf16[96,384]{1,0:T(8,128)(2,1)S(1)}, bf16[96,384]{1,0:T(8,128)(2,1)S(1)}, u32[]{:S(2)}, u32[]{:S(2)}) collective-permute-start(bf16[96,384]{1,0:T(8,128)(2,1)S(1)} %get-tuple-element.159), channel_id=1, source_target_pairs={{0,64},{1,65},{2,66},{3,67},{4,68},{5,69},{6,70},{7,71},{8,72},{9,... | collective-permute-start | bytes 221192 | tf_op jit(solution)/shard_map/ppermute | solution.py:426
  102.2 9.4 %collective-permute-start.41 = (bf16[96,384]{1,0:T(8,128)(2,1)S(1)}, bf16[96,384]{1,0:T(8,128)(2,1)S(1)}, u32[]{:S(2)}, u32[]{:S(2)}) collective-permute-start(bf16[96,384]{1,0:T(8,128)(2,1)S(1)} %get-tuple-element.171), channel_id=1, source_target_pairs={{0,16},{1,17},{2,18},{3,19},{4,20},{5,21},{6,22},{7,23},{8,24},{9,... | collective-permute-start | bytes 221192 | tf_op jit(solution)/shard_map/ppermute | solution.py:426
  103.4 10.8 %collective-permute-start.42 = (bf16[96,384]{1,0:T(8,128)(2,1)S(1)}, bf16[96,384]{1,0:T(8,128)(2,1)S(1)}, u32[]{:S(2)}, u32[]{:S(2)}) collective-permute-start(bf16[96,384]{1,0:T(8,128)(2,1)S(1)} %get-tuple-element.172), channel_id=1, source_target_pairs={{0,32},{1,33},{2,34},{3,35},{4,36},{5,37},{6,38},{7,39},{8,40},{9,... | collective-permute-start | bytes 221192 | tf_op jit(solution)/shard_map/ppermute | solution.py:426
  105.7 8.5 %collective-permute-start.43 = (bf16[96,384]{1,0:T(8,128)(2,1)S(1)}, bf16[96,384]{1,0:T(8,128)(2,1)S(1)}, u32[]{:S(2)}, u32[]{:S(2)}) collective-permute-start(bf16[96,384]{1,0:T(8,128)(2,1)S(1)} %get-tuple-element.173), channel_id=1, source_target_pairs={{0,48},{1,49},{2,50},{3,51},{4,52},{5,53},{6,54},{7,55},{8,56},{9,... | collective-permute-start | bytes 221192 | tf_op jit(solution)/shard_map/ppermute | solution.py:426
  105.7 10.1 %collective-permute-start.44 = (bf16[96,384]{1,0:T(8,128)(2,1)S(1)}, bf16[96,384]{1,0:T(8,128)(2,1)S(1)}, u32[]{:S(2)}, u32[]{:S(2)}) collective-permute-start(bf16[96,384]{1,0:T(8,128)(2,1)S(1)} %get-tuple-element.176), channel_id=1, source_target_pairs={{0,96},{1,97},{2,98},{3,99},{4,100},{5,101},{6,102},{7,103},{8,104... | collective-permute-start | bytes 221192 | tf_op jit(solution)/shard_map/ppermute | solution.py:426
  108.3 9.4 %collective-permute-start.45 = (bf16[96,384]{1,0:T(8,128)(2,1)S(1)}, bf16[96,384]{1,0:T(8,128)(2,1)S(1)}, u32[]{:S(2)}, u32[]{:S(2)}) collective-permute-start(bf16[96,384]{1,0:T(8,128)(2,1)S(1)} %get-tuple-element.177), channel_id=1, source_target_pairs={{0,112},{1,113},{2,114},{3,115},{4,116},{5,117},{6,118},{7,119},{8... | collective-permute-start | bytes 221192 | tf_op jit(solution)/shard_map/ppermute | solution.py:426
  111.6 9.1 %collective-permute-start.34 = (bf16[96,384]{1,0:T(8,128)(2,1)S(1)}, bf16[96,384]{1,0:T(8,128)(2,1)S(1)}, u32[]{:S(2)}, u32[]{:S(2)}) collective-permute-start(bf16[96,384]{1,0:T(8,128)(2,1)S(1)} %get-tuple-element.163), channel_id=1, source_target_pairs={{0,16},{1,17},{2,18},{3,19},{4,20},{5,21},{6,22},{7,23},{8,24},{9,... | collective-permute-start | bytes 221192 | tf_op jit(solution)/shard_map/ppermute | solution.py:426
  114.2 7.9 %collective-permute-start.35 = (bf16[96,384]{1,0:T(8,128)(2,1)S(1)}, bf16[96,384]{1,0:T(8,128)(2,1)S(1)}, u32[]{:S(2)}, u32[]{:S(2)}) collective-permute-start(bf16[96,384]{1,0:T(8,128)(2,1)S(1)} %get-tuple-element.164), channel_id=1, source_target_pairs={{0,32},{1,33},{2,34},{3,35},{4,36},{5,37},{6,38},{7,39},{8,40},{9,... | collective-permute-start | bytes 221192 | tf_op jit(solution)/shard_map/ppermute | solution.py:426
  114.2 10.1 %collective-permute-start.36 = (bf16[96,384]{1,0:T(8,128)(2,1)S(1)}, bf16[96,384]{1,0:T(8,128)(2,1)S(1)}, u32[]{:S(2)}, u32[]{:S(2)}) collective-permute-start(bf16[96,384]{1,0:T(8,128)(2,1)S(1)} %get-tuple-element.165), channel_id=1, source_target_pairs={{0,48},{1,49},{2,50},{3,51},{4,52},{5,53},{6,54},{7,55},{8,56},{9,... | collective-permute-start | bytes 221192 | tf_op jit(solution)/shard_map/ppermute | solution.py:426
  115.8 9.2 %collective-permute-start.37 = (bf16[96,384]{1,0:T(8,128)(2,1)S(1)}, bf16[96,384]{1,0:T(8,128)(2,1)S(1)}, u32[]{:S(2)}, u32[]{:S(2)}) collective-permute-start(bf16[96,384]{1,0:T(8,128)(2,1)S(1)} %get-tuple-element.166), channel_id=1, source_target_pairs={{0,64},{1,65},{2,66},{3,67},{4,68},{5,69},{6,70},{7,71},{8,72},{9,... | collective-permute-start | bytes 221192 | tf_op jit(solution)/shard_map/ppermute | solution.py:426
  117.7 11.5 %collective-permute-start.38 = (bf16[96,384]{1,0:T(8,128)(2,1)S(1)}, bf16[96,384]{1,0:T(8,128)(2,1)S(1)}, u32[]{:S(2)}, u32[]{:S(2)}) collective-permute-start(bf16[96,384]{1,0:T(8,128)(2,1)S(1)} %get-tuple-element.167), channel_id=1, source_target_pairs={{0,80},{1,81},{2,82},{3,83},{4,84},{5,85},{6,86},{7,87},{8,88},{9,... | collective-permute-start | bytes 221192 | tf_op jit(solution)/shard_map/ppermute | solution.py:426
  120.7 8.6 %collective-permute-start.39 = (bf16[96,384]{1,0:T(8,128)(2,1)S(1)}, bf16[96,384]{1,0:T(8,128)(2,1)S(1)}, u32[]{:S(2)}, u32[]{:S(2)}) collective-permute-start(bf16[96,384]{1,0:T(8,128)(2,1)S(1)} %get-tuple-element.168), channel_id=1, source_target_pairs={{0,96},{1,97},{2,98},{3,99},{4,100},{5,101},{6,102},{7,103},{8,104... | collective-permute-start | bytes 221192 | tf_op jit(solution)/shard_map/ppermute | solution.py:426
  124.3 8.4 %collective-permute-start.46 = (bf16[96,384]{1,0:T(8,128)(2,1)S(1)}, bf16[96,384]{1,0:T(8,128)(2,1)S(1)}, u32[]{:S(2)}, u32[]{:S(2)}) collective-permute-start(bf16[96,384]{1,0:T(8,128)(2,1)S(1)} %second_solve.2.refs_0_), channel_id=1, source_target_pairs={{0,64},{1,65},{2,66},{3,67},{4,68},{5,69},{6,70},{7,71},{8,72},{9,... | collective-permute-start | bytes 221192 | tf_op jit(solution)/shard_map/ppermute | solution.py:426
  125.0 8.4 %collective-permute-start.47 = (bf16[96,384]{1,0:T(8,128)(2,1)S(1)}, bf16[96,384]{1,0:T(8,128)(2,1)S(1)}, u32[]{:S(2)}, u32[]{:S(2)}) collective-permute-start(bf16[96,384]{1,0:T(8,128)(2,1)S(1)} %second_solve.2.refs_0_), channel_id=1, source_target_pairs={{0,80},{1,81},{2,82},{3,83},{4,84},{5,85},{6,86},{7,87},{8,88},{9,... | collective-permute-start | bytes 221192 | tf_op jit(solution)/shard_map/ppermute | solution.py:426
  129.3 7.9 %collective-permute-start.54 = (bf16[96,384]{1,0:T(8,128)(2,1)S(1)}, bf16[96,384]{1,0:T(8,128)(2,1)S(1)}, u32[]{:S(2)}, u32[]{:S(2)}) collective-permute-start(bf16[96,384]{1,0:T(8,128)(2,1)S(1)} %second_solve.2.refs_0_), channel_id=1, source_target_pairs={{0,32},{1,33},{2,34},{3,35},{4,36},{5,37},{6,38},{7,39},{8,40},{9,... | collective-permute-start | bytes 221192 | tf_op jit(solution)/shard_map/ppermute | solution.py:426
  129.3 11.9 %collective-permute-start.55 = (bf16[96,384]{1,0:T(8,128)(2,1)S(1)}, bf16[96,384]{1,0:T(8,128)(2,1)S(1)}, u32[]{:S(2)}, u32[]{:S(2)}) collective-permute-start(bf16[96,384]{1,0:T(8,128)(2,1)S(1)} %second_solve.2.refs_0_), channel_id=1, source_target_pairs={{0,48},{1,49},{2,50},{3,51},{4,52},{5,53},{6,54},{7,55},{8,56},{9,... | collective-permute-start | bytes 221192 | tf_op jit(solution)/shard_map/ppermute | solution.py:426
  132.7 8.6 %collective-permute-start.56 = (bf16[96,384]{1,0:T(8,128)(2,1)S(1)}, bf16[96,384]{1,0:T(8,128)(2,1)S(1)}, u32[]{:S(2)}, u32[]{:S(2)}) collective-permute-start(bf16[96,384]{1,0:T(8,128)(2,1)S(1)} %second_solve.2.refs_0_), channel_id=1, source_target_pairs={{0,96},{1,97},{2,98},{3,99},{4,100},{5,101},{6,102},{7,103},{8,104... | collective-permute-start | bytes 221192 | tf_op jit(solution)/shard_map/ppermute | solution.py:426
  133.4 8.4 %collective-permute-start.57 = (bf16[96,384]{1,0:T(8,128)(2,1)S(1)}, bf16[96,384]{1,0:T(8,128)(2,1)S(1)}, u32[]{:S(2)}, u32[]{:S(2)}) collective-permute-start(bf16[96,384]{1,0:T(8,128)(2,1)S(1)} %second_solve.2.refs_0_), channel_id=1, source_target_pairs={{0,112},{1,113},{2,114},{3,115},{4,116},{5,117},{6,118},{7,119},{8... | collective-permute-start | bytes 221192 | tf_op jit(solution)/shard_map/ppermute | solution.py:426
  136.2 8.5 %collective-permute-start.51 = (bf16[96,384]{1,0:T(8,128)(2,1)S(1)}, bf16[96,384]{1,0:T(8,128)(2,1)S(1)}, u32[]{:S(2)}, u32[]{:S(2)}) collective-permute-start(bf16[96,384]{1,0:T(8,128)(2,1)S(1)} %second_solve.3.refs_0_), channel_id=1, source_target_pairs={{0,64},{1,65},{2,66},{3,67},{4,68},{5,69},{6,70},{7,71},{8,72},{9,... | collective-permute-start | bytes 221192 | tf_op jit(solution)/shard_map/ppermute | solution.py:426
  137.2 8.2 %collective-permute-start.52 = (bf16[96,384]{1,0:T(8,128)(2,1)S(1)}, bf16[96,384]{1,0:T(8,128)(2,1)S(1)}, u32[]{:S(2)}, u32[]{:S(2)}) collective-permute-start(bf16[96,384]{1,0:T(8,128)(2,1)S(1)} %second_solve.3.refs_0_), channel_id=1, source_target_pairs={{0,80},{1,81},{2,82},{3,83},{4,84},{5,85},{6,86},{7,87},{8,88},{9,... | collective-permute-start | bytes 221192 | tf_op jit(solution)/shard_map/ppermute | solution.py:426
  141.2 10.4 %collective-permute-start.48 = (bf16[96,384]{1,0:T(8,128)(2,1)S(1)}, bf16[96,384]{1,0:T(8,128)(2,1)S(1)}, u32[]{:S(2)}, u32[]{:S(2)}) collective-permute-start(bf16[96,384]{1,0:T(8,128)(2,1)S(1)} %second_solve.3.refs_0_), channel_id=1, source_target_pairs={{0,16},{1,17},{2,18},{3,19},{4,20},{5,21},{6,22},{7,23},{8,24},{9,... | collective-permute-start | bytes 221192 | tf_op jit(solution)/shard_map/ppermute | solution.py:426
  141.3 10.3 %collective-permute-start.49 = (bf16[96,384]{1,0:T(8,128)(2,1)S(1)}, bf16[96,384]{1,0:T(8,128)(2,1)S(1)}, u32[]{:S(2)}, u32[]{:S(2)}) collective-permute-start(bf16[96,384]{1,0:T(8,128)(2,1)S(1)} %second_solve.3.refs_0_), channel_id=1, source_target_pairs={{0,32},{1,33},{2,34},{3,35},{4,36},{5,37},{6,38},{7,39},{8,40},{9,... | collective-permute-start | bytes 221192 | tf_op jit(solution)/shard_map/ppermute | solution.py:426
  141.8 9.9 %collective-permute-start.50 = (bf16[96,384]{1,0:T(8,128)(2,1)S(1)}, bf16[96,384]{1,0:T(8,128)(2,1)S(1)}, u32[]{:S(2)}, u32[]{:S(2)}) collective-permute-start(bf16[96,384]{1,0:T(8,128)(2,1)S(1)} %second_solve.3.refs_0_), channel_id=1, source_target_pairs={{0,48},{1,49},{2,50},{3,51},{4,52},{5,53},{6,54},{7,55},{8,56},{9,... | collective-permute-start | bytes 221192 | tf_op jit(solution)/shard_map/ppermute | solution.py:426
  (16 other events, 71.5 us)
Sparse Core Ops, SparseCore 0:
  58.3 42.8 all-gather.1

commit v7 on v5

v7 whole, which is shorter than its diff:
```python
import functools

import jax
import jax.numpy as jnp
from jax import lax
from jax.experimental import pallas as pl
from jax.experimental.pallas import tpu as pltpu
from jax.sharding import Mesh, PartitionSpec as P

step_size = 0.5
ORB = 32
f32 = jnp.float32
bf16 = jnp.bfloat16
PASTS = ("y", "zl")
SECONDS = ("x", "zh", "c")
ALL = PASTS + SECONDS
SWAP = [(0, 1), (1, 0)]
X, ZH, C, Y, ZL = range(5)


VMEM = pl.BlockSpec(memory_space=pltpu.VMEM)
SMEM = pl.BlockSpec(memory_space=pltpu.SMEM)
HBM = pl.BlockSpec(memory_space=pltpu.HBM)


def in_hbm(array):
    return pltpu.with_memory_space_constraint(array, pltpu.HBM)


def params(megabytes):
    return pltpu.CompilerParams(vmem_limit_bytes=megabytes << 20)


def cost(flops, nbytes):
    return pl.CostEstimate(flops=flops, bytes_accessed=nbytes, transcendentals=0)


def position(y):
    return (y & 1) * 2 + (y >> 1)


def block_at(place_ref, dy, width):
    start = position(place_ref[Y] ^ dy) * width
    return pl.ds(pl.multiple_of(start, 128), width)


def store_shares(place_ref, turned_ref, out_refs):
    width = out_refs[0].shape[0]
    for k, out_ref in enumerate(out_refs):
        share = (k >> 1) * 2 + (place_ref[ZL] ^ (k & 1))
        out_ref[...] = turned_ref[pl.ds(pl.multiple_of(share * width, width), width), :]


STEPS = 3


def first_piece_kernel(moves, bring_lhs, place_ref, memory_ref, resident_ref, *refs):
    count = 2 * len(moves)
    if bring_lhs:
        out_refs, (lhs_ref, block_ref, turned_ref, sems) = refs[:count], refs[count:]
    else:
        lhs_ref, out_refs, (block_ref, turned_ref, sems) = memory_ref, refs[:count], refs[count:]
    depth = lhs_ref.shape[1]
    width = block_ref.shape[1] // len(moves)
    step = depth // STEPS
    copies = []
    for k in range(STEPS):
        at = slice(k * step, (k + 1) * step)
        some = [
            pltpu.make_async_copy(
                resident_ref.at[at, block_at(place_ref, dy, width)],
                block_ref.at[at, i * width : (i + 1) * width],
                sems.at[i, k],
            )
            for i, dy in enumerate(moves)
        ]
        if bring_lhs:
            some.append(pltpu.make_async_copy(memory_ref.at[0, :, at], lhs_ref.at[:, at], sems.at[len(moves), k]))
        for copy in some:
            copy.start()
        copies.append(some)
    product = None
    for k in range(STEPS):
        at = slice(k * step, (k + 1) * step)
        for copy in copies[k]:
            copy.wait()
        term = jnp.dot(lhs_ref[:, at], block_ref[at, :], preferred_element_type=f32)
        product = term if product is None else product + term
    turned_ref[...] = product.T.astype(bf16)
    store_shares(place_ref, turned_ref, out_refs)


def first_piece(moves, place, memory, resident):
    rows, depth = memory.shape[-2:]
    cols = resident.shape[1]
    width = cols // 8
    bring_lhs = memory.ndim == 3
    shapes = [(width, rows)] * 2 * len(moves) + [(rows, depth)] * bring_lhs
    return pl.pallas_call(
        functools.partial(first_piece_kernel, moves, bring_lhs),
        in_specs=[SMEM, HBM if bring_lhs else VMEM, HBM],
        out_specs=[VMEM] * len(shapes),
        out_shape=[jax.ShapeDtypeStruct(shape, bf16) for shape in shapes],
        scratch_shapes=[
            pltpu.VMEM((depth, 2 * width * len(moves)), bf16),
            pltpu.VMEM((2 * width * len(moves), rows), bf16),
            pltpu.SemaphoreType.DMA((len(moves) + bring_lhs, STEPS)),
        ],
        compiler_params=params(12),
        cost_estimate=cost(4 * rows * depth * width * len(moves), 4 * depth * width * len(moves)),
        name="first_piece",
    )(place, memory, resident)


def second_piece_kernel(moves, place_ref, lhs_ref, resident_ref, *refs):
    out_refs, turned_ref = refs[: 2 * len(moves)], refs[2 * len(moves)]
    width = turned_ref.shape[0] // len(moves)
    for i, dy in enumerate(moves):
        block = resident_ref[:, block_at(place_ref, dy, width)]
        product = jnp.dot(lhs_ref[...], block, preferred_element_type=f32)
        turned_ref[i * width : (i + 1) * width, :] = product.T.astype(bf16)
    store_shares(place_ref, turned_ref, out_refs)


def second_piece(moves, place, lhs, resident):
    rows, depth = lhs.shape
    width = resident.shape[1] // 8
    return pl.pallas_call(
        functools.partial(second_piece_kernel, moves),
        in_specs=[SMEM, VMEM, VMEM],
        out_specs=[VMEM] * 2 * len(moves),
        out_shape=[jax.ShapeDtypeStruct((width, rows), bf16)] * 2 * len(moves),
        scratch_shapes=[pltpu.VMEM((2 * width * len(moves), rows), bf16)],
        compiler_params=params(6),
        cost_estimate=cost(4 * rows * depth * width * len(moves), 4 * width * rows * len(moves)),
        name="second_piece",
    )(place, lhs, resident)


def priors_kernel(place_ref, previous_ref, one_out, two_out, prior_ref, turned_ref, sem):
    width, rows = one_out.shape
    cols = block_at(place_ref, 0, 2 * width)
    copy = pltpu.make_async_copy(previous_ref.at[:, :, cols], prior_ref, sem)
    copy.start()
    copy.wait()
    for front, out_ref in enumerate((one_out, two_out)):
        turned_ref[...] = prior_ref[front].astype(f32).T
        share = turned_ref[pl.ds(pl.multiple_of(place_ref[ZL] * width, width), width), :]
        out_ref[...] = share.astype(bf16)


def priors(place, previous):
    _, rows, cols = previous.shape
    width = cols // 8
    return pl.pallas_call(
        priors_kernel,
        in_specs=[SMEM, HBM],
        out_specs=[VMEM] * 2,
        out_shape=[jax.ShapeDtypeStruct((width, rows), bf16)] * 2,
        scratch_shapes=[
            pltpu.VMEM((2, rows, 2 * width), bf16),
            pltpu.VMEM((2 * width, rows), f32),
            pltpu.SemaphoreType.DMA,
        ],
        compiler_params=params(6),
        cost_estimate=cost(0, 32 * width * rows),
        name="priors",
    )(place, previous)


def bring_kernel(place_ref, memory_ref, resident_ref, memory_out, resident_out, sems):
    copies = [
        pltpu.make_async_copy(memory_ref.at[1], memory_out, sems.at[0]),
        pltpu.make_async_copy(resident_ref, resident_out, sems.at[1]),
    ]
    for copy in copies:
        copy.start()
    for copy in copies:
        copy.wait()


def bring(place, memory, resident):
    _, rows, depth = memory.shape
    return pl.pallas_call(
        bring_kernel,
        in_specs=[SMEM] + [HBM] * 2,
        out_specs=[VMEM] * 2,
        out_shape=[
            jax.ShapeDtypeStruct((rows, depth), bf16),
            jax.ShapeDtypeStruct(resident.shape, bf16),
        ],
        scratch_shapes=[pltpu.SemaphoreType.DMA((2,))],
        compiler_params=params(6),
        cost_estimate=cost(0, 2 * (rows * depth + resident.size)),
        name="bring",
    )(place, memory, resident)


def place_pair(own, other, first, at, out_ref, base_ref):
    near, far = own.astype(f32), other.astype(f32)
    low = jnp.where(first == 0, near, far)
    high = jnp.where(first == 0, far, near)
    pair = jnp.concatenate([low, high], axis=0).T
    if base_ref is not None:
        pair = pair + base_ref[:, at].astype(f32)
    out_ref[:, at] = pair.astype(bf16)


def next_memory_kernel(place_ref, memory_ref, *refs):
    pair_refs, out_ref = refs[:8], refs[8]
    half = memory_ref.shape[1] // 2
    width = half // 4
    for side in range(2):
        for dx in range(4):
            near, far = pair_refs[side * 4 + dx], pair_refs[side * 4 + (dx ^ 2)]
            share = position(((place_ref[X] - dx) & 3) ^ place_ref[Y])
            start = (place_ref[C] ^ side) * half + share * width
            at = pl.ds(pl.multiple_of(start, 128), width)
            place_pair(near[0], far[1], place_ref[ZH], at, out_ref, memory_ref)


def next_memory(place, memory, pairs):
    rows, depth = memory.shape
    return pl.pallas_call(
        next_memory_kernel,
        in_specs=[SMEM] + [VMEM] * 9,
        out_specs=VMEM,
        out_shape=jax.ShapeDtypeStruct((rows, depth), bf16),
        compiler_params=params(6),
        cost_estimate=cost(rows * depth, 6 * rows * depth),
        name="next_memory",
    )(place, memory, *pairs)


def solve_into(part_refs, prior_ref, inverse_ref):
    summed = part_refs[0][...].astype(f32)
    for part_ref in part_refs[1:]:
        summed = summed + part_ref[...].astype(f32)
    source = prior_ref[...].astype(f32) - step_size * summed
    mixed = lax.dot_general(
        source,
        inverse_ref[...],
        (((1,), (1,)), ((), ())),
        precision=lax.Precision.HIGHEST,
        preferred_element_type=f32,
    )
    return (source + mixed).astype(bf16)


def flipped(values):
    rows, cols = values.shape
    strips = []
    pad = jnp.zeros((128 - ORB, 128), f32)
    for s in range(rows // ORB):
        pieces = []
        for q in range(cols // 128):
            block = values[s * ORB : (s + 1) * ORB, q * 128 : (q + 1) * 128]
            turned = jnp.concatenate([block, pad], axis=0).T
            piece = turned[:ORB]
            for t in range(1, 128 // ORB):
                piece = piece + pltpu.roll(turned[t * ORB : (t + 1) * ORB], t * ORB, 1)
            pieces.append(piece)
        strips.append(jnp.concatenate(pieces, axis=1))
    return jnp.concatenate(strips, axis=0)


def first_solve_kernel(place_ref, *refs):
    front_ref, energy_ref = refs[11:]
    front = solve_into(refs[:8], refs[8], refs[9])
    front_ref[...] = front
    values = front.astype(f32)
    mirror = flipped(values)
    rows, cols = values.shape
    coupling = jnp.tile(refs[10][...], (rows // ORB, cols // 128))
    energy_ref[...] = (mirror * mirror * values * coupling).astype(bf16)


def second_solve_kernel(place_ref, *refs):
    refs[10][...] = solve_into(refs[:8], refs[8], refs[9])


def solve(kernel, place, parts, prior, inverse, extra, outputs, name):
    width, rows = prior.shape
    return pl.pallas_call(
        kernel,
        in_specs=[SMEM] + [VMEM] * (len(parts) + 2 + len(extra)),
        out_specs=[VMEM] * outputs,
        out_shape=[jax.ShapeDtypeStruct((width, rows), bf16)] * outputs,
        compiler_params=params(8),
        cost_estimate=cost(12 * rows * rows * width, 24 * rows * width),
        name=name,
    )(place, *parts, prior, inverse, *extra)


def put_blocks(blocks, block_ref, sems, out_ref, front):
    width = block_ref.shape[2]
    copies = []
    for i, (start, write) in enumerate(blocks):
        write(block_ref.at[i])
        at = pl.ds(pl.multiple_of(start, 128), width)
        copies.append(pltpu.make_async_copy(block_ref.at[i], out_ref.at[front, :, at], sems.at[i]))
        copies[i].start()
    for copy in copies:
        copy.wait()


def join_one_kernel(front_ref, out_ref, block_ref, sems):
    width = block_ref.shape[2]

    def block(y):
        def write(ref):
            ref[...] = front_ref[y * width : (y + 1) * width, :].astype(f32).T.astype(bf16)

        return position(y) * width, write

    put_blocks([block(y) for y in range(4)], block_ref, sems, out_ref, 0)


def join_two_kernel(place_ref, *refs):
    chunk_refs, (out_ref, block_ref, sems) = refs[:8], refs[9:]
    width = block_ref.shape[2]

    def block(dy):
        def write(ref):
            own, other = chunk_refs[2 * dy][...], chunk_refs[2 * dy + 1][...]
            place_pair(own, other, place_ref[ZL], slice(None), ref, None)

        return position((place_ref[Y] - dy) & 3) * width, write

    put_blocks([block(dy) for dy in (0, 2, 1, 3)], block_ref, sems, out_ref, 1)


def join(kernel, args, in_specs, shape, aliases, name):
    _, rows, cols = shape
    return pl.pallas_call(
        kernel,
        in_specs=in_specs,
        out_specs=HBM,
        out_shape=jax.ShapeDtypeStruct(shape, bf16),
        scratch_shapes=[pltpu.VMEM((4, rows, cols // 4), bf16), pltpu.SemaphoreType.DMA((4,))],
        input_output_aliases=aliases,
        compiler_params=params(6),
        cost_estimate=cost(rows * cols, 4 * rows * cols),
        name=name,
    )(*args)


def move(value, target):
    pairs = []
    for i in range(128):
        rest, c = divmod(i, 2)
        rest, zh = divmod(rest, 2)
        rest, x = divmod(rest, 4)
        y, zl = divmod(rest, 2)
        y, zl, x, zh = target(y, zl, x, zh)
        pairs.append((i, (((y * 2 + zl) * 4 + x) * 2 + zh) * 2 + c))
    return lax.ppermute(value, ALL, pairs)


def turn(flip):
    return lambda y, zl, x, zh: (x, zh, x ^ y ^ (2 * flip), zl ^ flip)


def after(value, others):
    return lax.optimization_barrier((value, others))


def scatter(shares, moves):
    parts = []
    for i, dy in enumerate(moves):
        for dz in (1, 0):
            share = shares[2 * i + dz]
            if (dy, dz) != (0, 0):
                share = move(share, lambda y, zl, x, zh: (y ^ dy, zl ^ dz, x, zh))
            parts.append(share)
    return parts


def spread_pairs(pair, axis):
    pairs = {0: pair}
    for d in (2, 1, 3):
        pairs[d] = lax.ppermute(pair, axis, [(i, (i + d) % 4) for i in range(4)])
    return [pairs[d] for d in range(4)]


def spread_chunks(value):
    chunks = {(0, 0): value}
    for dy, dz in ((2, 1), (2, 0), (0, 1), (1, 1), (3, 1), (1, 0), (3, 0)):
        chunks[dy, dz] = move(value, lambda y, zl, x, zh: ((y + dy) % 4, zl ^ dz, x, zh))
    return chunks


def per_device(resident, memory, previous, inverse_part, pair_coupling):
    place = jnp.stack([lax.axis_index(name) for name in ("x", "zh", "c", "y", "zl")]).astype(jnp.int32)
    coupling = jnp.tile(pair_coupling, (1, 128 // ORB))

    resident, memory, previous = in_hbm(resident), in_hbm(memory), in_hbm(previous)

    *shares, lhs = first_piece((1,), place, memory, resident)
    parts = scatter(shares, (1,))
    lhs, shares = after(lhs, shares)
    shares = first_piece((3,), place, lhs, resident)
    parts += scatter(shares, (3,))
    lhs, shares = after(lhs, shares)
    shares = first_piece((2, 0), place, lhs, resident)
    later, _ = after(place, (shares, parts))
    parts += scatter(shares, (2, 0))
    prior_one, prior_two = priors(later, previous)
    front_one, energy = solve(
        first_solve_kernel, place, parts, prior_one, inverse_part[0], [coupling], 2, "first_solve"
    )
    whole_one = lax.all_gather(front_one, PASTS, axis=0, tiled=True)
    pair = [move(energy, turn(0)), move(energy, turn(1))]
    later, _ = after(place, energy)
    memory, resident = bring(later, memory, resident)
    pair, memory = after(pair, memory)
    own = spread_pairs(jnp.stack(pair), "x")
    other = [lax.ppermute(pair, "c", SWAP) for pair in own]
    lhs = next_memory(place, memory, own + other)
    shares = second_piece((1,), place, lhs, resident)
    parts = scatter(shares, (1,))
    lhs, shares = after(lhs, shares)
    shares = second_piece((3,), place, lhs, resident)
    more = scatter(shares, (3,))
    lhs, parts = after(lhs, parts)
    parts += more + scatter(second_piece((2, 0), place, lhs, resident), (2, 0))
    (front_two,) = solve(
        second_solve_kernel, place, parts, prior_two, inverse_part[1], [], 1, "second_solve"
    )
    chunks = spread_chunks(front_two)
    chunks = [chunks[dy, dz] for dy in range(4) for dz in range(2)]
    fronts = join(join_one_kernel, (whole_one,), [VMEM], previous.shape, {}, "join_one")
    return join(
        join_two_kernel, (place, *chunks, fronts), [SMEM] + [VMEM] * 8 + [HBM], previous.shape, {9: 0}, "join_two"
    )


def solution(mesh):
    fine = Mesh(mesh.devices.reshape(4, 2, 4, 2, 2), ALL)
    in_specs = (P(PASTS, SECONDS), P(None, None, PASTS), P(None, None, SECONDS), P(), P())
    out_specs = P(None, None, SECONDS)
    return jax.shard_map(
        per_device, mesh=fine, in_specs=in_specs, out_specs=out_specs, check_vma=False
    )
```

time: 114 us -> 131 us (1.15)
  between operations: 0.42 us -> 13.6 us
  Pallas kernels: 30.2 us -> 34.9 us
  starting transfers between devices: 55.3 us -> 53.4 us
    ppermute x6 -> x3, starting transfers between devices: 18 us -> 6.68 us  [spread_pairs(): pairs[d] = lax.ppermute(pair, axis, [(i, (i + d) % 4) for i in range(4)])]
    ppermute x23, starting transfers between devices: 37.2 us -> 46.2 us  [move(): return lax.ppermute(value, ALL, pairs)]
    pallas_call x8 -> x10, Pallas kernels: 25.3 us -> 29.8 us  [the longest x3 12.5 us: first_piece(): pl.pallas_call(functools.partial(first_piece_kernel, moves, bring_lhs), i...]
    ppermute x23, waiting for transfers between devices: 18 us -> 16.3 us  [move(): return lax.ppermute(value, ALL, pairs)]
    ppermute x6 -> x3, waiting for transfers between devices: 8.33 us -> 9.34 us  [spread_pairs(): pairs[d] = lax.ppermute(pair, axis, [(i, (i + d) % 4) for i in range(4)])]
  transfers between devices with their start and end apart: 34 -> 31, of which waited for: 11 -> 13; matrix products, arithmetic and copies ran while one was open for 0% -> 0% of each run, Pallas kernels for 13% -> 21%
where the time goes in v7:
time: 131 us
  starting transfers between devices  53.4 us (41%)
  Pallas kernels  34.9 us (27%)
  waiting for transfers between devices  27.1 us (21%)
  between operations  13.6 us (10%)
  local copies, waits for them, and re-layouts  1.54 us (1%)
    ppermute x23, starting transfers between devices, move(): return lax.ppermute(value, ALL, pairs)  46.2 us
    ppermute x23, waiting for transfers between devices, move(): return lax.ppermute(value, ALL, pairs)  16.3 us
    pallas_call x3, Pallas kernels, first_piece(): pl.pallas_call(functools.partial(first_piece_kernel, moves, bring_lhs), i...  12.5 us
    ppermute x3, waiting for transfers between devices, spread_pairs(): pairs[d] = lax.ppermute(pair, axis, [(i, (i + d) % 4) for i in range(4)])  9.34 us
    pallas_call x3, Pallas kernels, second_piece(): pl.pallas_call(functools.partial(second_piece_kernel, moves), in_specs=[S...  7.34 us
    ppermute x3, starting transfers between devices, spread_pairs(): pairs[d] = lax.ppermute(pair, axis, [(i, (i + d) % 4) for i in range(4)])  6.68 us
    pallas_call x1, Pallas kernels, bring(): pl.pallas_call(bring_kernel, in_specs=[SMEM] + [HBM] * 2, out_specs=[VMEM...  4.98 us
    pallas_call x2, Pallas kernels, solve(): pl.pallas_call(kernel, in_specs=[SMEM] + [VMEM] * (len(parts) + 2 + len(e...  3.54 us
  transfers between devices with their start and end apart: 31, of which 13 were waited for; matrix products, arithmetic and copies ran while one was open for 0% of the time, Pallas kernels for 21%

profile of v7, /device:TPU:0, one launch (start us, length us, event | category | flops | bytes accessed | tf_op | source)
XLA Modules:
  0.0 130.6 jit_solution(12858405530648460392)
XLA Ops:
  6.6 4.0 %first_piece.3 = (bf16[192,384]{1,0:T(8,128)(2,1)S(1)}, bf16[192,384]{1,0:T(8,128)(2,1)S(1)}, bf16[384,3072]{1,0:T(8,128)(2,1)S(1)}) custom-call(s32[5]{0:T(128)S(1)} %stack.32.place_ref, bf16[2,384,3072]{2,1,0:T(8,128)(2,1)} %memory_ref.3, bf16[3072,1536]{1,0:T(8,128)(2,1)} %resident_ref.7), custom_call_target="tpu_custom_call" | custom-call | flops 905969664 | bytes 2359296 | tf_op jit(solution)/shard_map/first_piece/pallas_call | solution.py:99
  10.6 3.1 %collective-permute-start = (bf16[192,384]{1,0:T(8,128)(2,1)S(1)}, bf16[192,384]{1,0:T(8,128)(2,1)S(1)}, u32[]{:S(2)}, u32[]{:S(2)}) collective-permute-start(bf16[192,384]{1,0:T(8,128)(2,1)S(1)} %get-tuple-element.39), channel_id=1, source_target_pairs={{0,48},{1,49},{2,50},{3,51},{4,52},{5,53},{6,54},{7,55},{8,56},{9,... | collective-permute-start | bytes 442376 | tf_op jit(solution)/shard_map/ppermute | solution.py:357
  14.2 3.5 %first_piece.4 = (bf16[192,384]{1,0:T(8,128)(2,1)S(1)}, bf16[192,384]{1,0:T(8,128)(2,1)S(1)}) custom-call(s32[5]{0:T(128)S(1)} %stack.32.place_ref, bf16[384,3072]{1,0:T(8,128)(2,1)S(1)} %get-tuple-element.45.memory_ref, bf16[3072,1536]{1,0:T(8,128)(2,1)} %resident_ref.7), custom_call_target="tpu_custom_call" | custom-call | flops 905969664 | bytes 2359296 | tf_op jit(solution)/shard_map/first_piece/pallas_call | solution.py:99
  17.7 2.6 %collective-permute-start.2 = (bf16[192,384]{1,0:T(8,128)(2,1)S(1)}, bf16[192,384]{1,0:T(8,128)(2,1)S(1)}, u32[]{:S(2)}, u32[]{:S(2)}) collective-permute-start(bf16[192,384]{1,0:T(8,128)(2,1)S(1)} %get-tuple-element.43), channel_id=1, source_target_pairs={{0,112},{1,113},{2,114},{3,115},{4,116},{5,117},{6,118},{7,119},{8... | collective-permute-start | bytes 442376 | tf_op jit(solution)/shard_map/ppermute | solution.py:357
  20.3 0.6 collective-permute-start.3
  20.9 5.0 %first_piece.5 = (bf16[192,384]{1,0:T(8,128)(2,1)S(1)}, bf16[192,384]{1,0:T(8,128)(2,1)S(1)}, bf16[192,384]{1,0:T(8,128)(2,1)S(1)}, bf16[192,384]{1,0:T(8,128)(2,1)S(1)}) custom-call(s32[5]{0:T(128)S(1)} %stack.32.place_ref, bf16[384,3072]{1,0:T(8,128)(2,1)S(1)} %get-tuple-element.45.memory_ref, bf16[3072,1536]{1,0:T(8,128)(2,1)} %resident_ref.7), custom_call_target="tpu_custom_call" | custom-call | flops 1811939328 | bytes 4718592 | tf_op jit(solution)/shard_map/first_piece/pallas_call | solution.py:99
  25.9 3.1 %collective-permute-start.4 = (bf16[192,384]{1,0:T(8,128)(2,1)S(1)}, bf16[192,384]{1,0:T(8,128)(2,1)S(1)}, u32[]{:S(2)}, u32[]{:S(2)}) collective-permute-start(bf16[192,384]{1,0:T(8,128)(2,1)S(1)} %get-tuple-element.46), channel_id=1, source_target_pairs={{0,80},{1,81},{2,82},{3,83},{4,84},{5,85},{6,86},{7,87},{8,88},{9,... | collective-permute-start | bytes 442376 | tf_op jit(solution)/shard_map/ppermute | solution.py:357
  29.1 1.6 %collective-permute-start.5 = (bf16[192,384]{1,0:T(8,128)(2,1)S(1)}, bf16[192,384]{1,0:T(8,128)(2,1)S(1)}, u32[]{:S(2)}, u32[]{:S(2)}) collective-permute-start(bf16[192,384]{1,0:T(8,128)(2,1)S(1)} %get-tuple-element.47), channel_id=1, source_target_pairs={{0,64},{1,65},{2,66},{3,67},{4,68},{5,69},{6,70},{7,71},{8,72},{9,... | collective-permute-start | bytes 442376 | tf_op jit(solution)/shard_map/ppermute | solution.py:357
  31.3 1.9 %priors.1 = (bf16[192,384]{1,0:T(8,128)(2,1)S(1)}, bf16[192,384]{1,0:T(8,128)(2,1)S(1)}) custom-call(s32[5]{0:T(128)S(1)} %stack.32.place_ref, bf16[2,384,1536]{2,1,0:T(8,128)(2,1)} %previous_ref.1), custom_call_target="tpu_custom_call" | custom-call | bytes 2359296 | tf_op jit(solution)/shard_map/priors/pallas_call | solution.py:155
  33.2 1.6 %collective-permute-done.4.refs_4_ = bf16[192,384]{1,0:T(8,128)(2,1)S(1)} collective-permute-done((bf16[192,384]{1,0:T(8,128)(2,1)S(1)}, bf16[192,384]{1,0:T(8,128)(2,1)S(1)}, u32[]{:S(2)}, u32[]{:S(2)}) %collective-permute-start.4) | collective-permute-done | bytes 147488 | tf_op jit(solution)/shard_map/ppermute | solution.py:357
  34.8 1.7 %collective-permute-done.5.refs_5_ = bf16[192,384]{1,0:T(8,128)(2,1)S(1)} collective-permute-done((bf16[192,384]{1,0:T(8,128)(2,1)S(1)}, bf16[192,384]{1,0:T(8,128)(2,1)S(1)}, u32[]{:S(2)}, u32[]{:S(2)}) %collective-permute-start.5) | collective-permute-done | bytes 147488 | tf_op jit(solution)/shard_map/ppermute | solution.py:357
  36.5 2.1 %first_solve.1 = (bf16[192,384]{1,0:T(8,128)(2,1)}, bf16[192,384]{1,0:T(8,128)(2,1)S(1)}) custom-call(s32[5]{0:T(128)S(1)} %stack.32.place_ref, bf16[192,384]{1,0:T(8,128)(2,1)S(1)} %collective-permute-done.refs_0_, bf16[192,384]{1,0:T(8,128)(2,1)S(1)} %collective-permute-done.1.refs_1_, bf16[192,384]{1,0:T(8,128)(2,1)S(1)} %collective-permute-done.2.refs_2_, ...), custom_call_target="tpu_custom_call" | custom-call | flops 339738624 | bytes 1769472 | tf_op jit(solution)/shard_map/first_solve/pallas_call | solution.py:284
  38.6 0.7 collective-permute-start.7
  39.3 8.4 %collective-permute-start.8 = (bf16[192,384]{1,0:T(8,128)(2,1)S(1)}, bf16[192,384]{1,0:T(8,128)(2,1)S(1)}, u32[]{:S(2)}, u32[]{:S(2)}) collective-permute-start(bf16[192,384]{1,0:T(8,128)(2,1)S(1)} %get-tuple-element.52), channel_id=1, source_target_pairs={{0,10},{1,11},{2,26},{3,27},{4,46},{5,47},{6,62},{7,63},{8,66},{9,... | collective-permute-start | bytes 442376 | tf_op jit(solution)/shard_map/ppermute | solution.py:357
  47.7 5.0 %bring.1 = (bf16[384,3072]{1,0:T(8,128)(2,1)S(1)}, bf16[3072,1536]{1,0:T(8,128)(2,1)S(1)}) custom-call(s32[5]{0:T(128)S(1)} %stack.32.place_ref, bf16[2,384,3072]{2,1,0:T(8,128)(2,1)} %memory_ref.3, bf16[3072,1536]{1,0:T(8,128)(2,1)} %resident_ref.7), custom_call_target="tpu_custom_call" | custom-call | bytes 11796480 | tf_op jit(solution)/shard_map/bring/pallas_call | solution.py:184
  52.7 2.2 %collective-permute-start.9 = (bf16[2,192,384]{2,1,0:T(8,128)(2,1)S(1)}, bf16[2,192,384]{2,1,0:T(8,128)(2,1)S(1)}, u32[]{:S(2)}, u32[]{:S(2)}) collective-permute-start(bf16[2,192,384]{2,1,0:T(8,128)(2,1)S(1)} %pad_maximum_fusion.refs_0_), channel_id=1, source_target_pairs={{0,4},{4,8},{8,12},{12,0},{1,5},{5,9},{9,13},{13,1},{2,6},{6,10},{... | collective-permute-start | bytes 884744 | tf_op jit(solution)/shard_map/ppermute | solution.py:382
  55.0 1.9 %collective-permute-start.10 = (bf16[2,192,384]{2,1,0:T(8,128)(2,1)S(1)}, bf16[2,192,384]{2,1,0:T(8,128)(2,1)S(1)}, u32[]{:S(2)}, u32[]{:S(2)}) collective-permute-start(bf16[2,192,384]{2,1,0:T(8,128)(2,1)S(1)} %pad_maximum_fusion.refs_0_), channel_id=1, source_target_pairs={{0,8},{4,12},{8,0},{12,4},{1,9},{5,13},{9,1},{13,5},{2,10},{6,14},... | collective-permute-start | bytes 884744 | tf_op jit(solution)/shard_map/ppermute | solution.py:382
  56.9 2.5 %collective-permute-start.11 = (bf16[2,192,384]{2,1,0:T(8,128)(2,1)S(1)}, bf16[2,192,384]{2,1,0:T(8,128)(2,1)S(1)}, u32[]{:S(2)}, u32[]{:S(2)}) collective-permute-start(bf16[2,192,384]{2,1,0:T(8,128)(2,1)S(1)} %pad_maximum_fusion.refs_0_), channel_id=1, source_target_pairs={{0,12},{4,0},{8,4},{12,8},{1,13},{5,1},{9,5},{13,9},{2,14},{6,2},{... | collective-permute-start | bytes 884744 | tf_op jit(solution)/shard_map/ppermute | solution.py:382
  59.4 3.0 %collective-permute-done.9.refs_1_ = bf16[2,192,384]{2,1,0:T(8,128)(2,1)S(1)} collective-permute-done((bf16[2,192,384]{2,1,0:T(8,128)(2,1)S(1)}, bf16[2,192,384]{2,1,0:T(8,128)(2,1)S(1)}, u32[]{:S(2)}, u32[]{:S(2)}) %collective-permute-start.9) | collective-permute-done | bytes 294944 | tf_op jit(solution)/shard_map/ppermute | solution.py:382
  62.5 6.3 %collective-permute-done.10.refs_2_ = bf16[2,192,384]{2,1,0:T(8,128)(2,1)S(1)} collective-permute-done((bf16[2,192,384]{2,1,0:T(8,128)(2,1)S(1)}, bf16[2,192,384]{2,1,0:T(8,128)(2,1)S(1)}, u32[]{:S(2)}, u32[]{:S(2)}) %collective-permute-start.10) | collective-permute-done | bytes 294944 | tf_op jit(solution)/shard_map/ppermute | solution.py:382
  69.3 1.1 collective-permute-done.14.refs_6_
  70.8 1.6 %next_memory.1.lhs_ref = bf16[384,3072]{1,0:T(8,128)(2,1)S(1)} custom-call(s32[5]{0:T(128)S(1)} %stack.32.place_ref, bf16[384,3072]{1,0:T(8,128)(2,1)S(1)} %get-tuple-element.55.memory_ref, bf16[2,192,384]{2,1,0:T(8,128)(2,1)S(1)} %pad_maximum_fusion.refs_0_, bf16[2,192,384]{2,1,0:T(8,128)(2,1)S(1)} %collective-permute-done.9.refs_1_, ...), custom_call_target="tpu_custom_call" | custom-call | flops 1179648 | bytes 7077888 | tf_op jit(solution)/shard_map/next_memory/pallas_call | solution.py:224
  72.4 2.0 %second_piece.3 = (bf16[192,384]{1,0:T(8,128)(2,1)S(1)}, bf16[192,384]{1,0:T(8,128)(2,1)S(1)}) custom-call(s32[5]{0:T(128)S(1)} %stack.32.place_ref, bf16[384,3072]{1,0:T(8,128)(2,1)S(1)} %next_memory.1.lhs_ref, bf16[3072,1536]{1,0:T(8,128)(2,1)S(1)} %get-tuple-element.58.resident_ref), custom_call_target="tpu_custom_call" | custom-call | flops 905969664 | bytes 294912 | tf_op jit(solution)/shard_map/second_piece/pallas_call | solution.py:128
  74.4 2.9 %collective-permute-start.16 = (bf16[192,384]{1,0:T(8,128)(2,1)S(1)}, bf16[192,384]{1,0:T(8,128)(2,1)S(1)}, u32[]{:S(2)}, u32[]{:S(2)}) collective-permute-start(bf16[192,384]{1,0:T(8,128)(2,1)S(1)} %get-tuple-element.60), channel_id=1, source_target_pairs={{0,48},{1,49},{2,50},{3,51},{4,52},{5,53},{6,54},{7,55},{8,56},{9,... | collective-permute-start | bytes 442376 | tf_op jit(solution)/shard_map/ppermute | solution.py:357
  77.4 0.6 collective-permute-start.17
  78.0 2.0 %second_piece.4 = (bf16[192,384]{1,0:T(8,128)(2,1)S(1)}, bf16[192,384]{1,0:T(8,128)(2,1)S(1)}) custom-call(s32[5]{0:T(128)S(1)} %stack.32.place_ref, bf16[384,3072]{1,0:T(8,128)(2,1)S(1)} %next_memory.1.lhs_ref, bf16[3072,1536]{1,0:T(8,128)(2,1)S(1)} %get-tuple-element.58.resident_ref), custom_call_target="tpu_custom_call" | custom-call | flops 905969664 | bytes 294912 | tf_op jit(solution)/shard_map/second_piece/pallas_call | solution.py:128
  80.0 3.0 %collective-permute-start.18 = (bf16[192,384]{1,0:T(8,128)(2,1)S(1)}, bf16[192,384]{1,0:T(8,128)(2,1)S(1)}, u32[]{:S(2)}, u32[]{:S(2)}) collective-permute-start(bf16[192,384]{1,0:T(8,128)(2,1)S(1)} %get-tuple-element.64), channel_id=1, source_target_pairs={{0,112},{1,113},{2,114},{3,115},{4,116},{5,117},{6,118},{7,119},{8... | collective-permute-start | bytes 442376 | tf_op jit(solution)/shard_map/ppermute | solution.py:357
  83.0 1.4 %collective-permute-start.19 = (bf16[192,384]{1,0:T(8,128)(2,1)S(1)}, bf16[192,384]{1,0:T(8,128)(2,1)S(1)}, u32[]{:S(2)}, u32[]{:S(2)}) collective-permute-start(bf16[192,384]{1,0:T(8,128)(2,1)S(1)} %get-tuple-element.65), channel_id=1, source_target_pairs={{0,96},{1,97},{2,98},{3,99},{4,100},{5,101},{6,102},{7,103},{8,104... | collective-permute-start | bytes 442376 | tf_op jit(solution)/shard_map/ppermute | solution.py:357
  84.4 1.2 collective-permute-done.17.refs_1_
  85.6 3.3 %second_piece.5 = (bf16[192,384]{1,0:T(8,128)(2,1)S(1)}, bf16[192,384]{1,0:T(8,128)(2,1)S(1)}, bf16[192,384]{1,0:T(8,128)(2,1)S(1)}, bf16[192,384]{1,0:T(8,128)(2,1)S(1)}) custom-call(s32[5]{0:T(128)S(1)} %stack.32.place_ref, bf16[384,3072]{1,0:T(8,128)(2,1)S(1)} %next_memory.1.lhs_ref, bf16[3072,1536]{1,0:T(8,128)(2,1)S(1)} %get-tuple-element.58.resident_ref), custom_call_target="tpu_custom_call" | custom-call | flops 1811939328 | bytes 589824 | tf_op jit(solution)/shard_map/second_piece/pallas_call | solution.py:128
  88.9 3.7 %collective-permute-start.20 = (bf16[192,384]{1,0:T(8,128)(2,1)S(1)}, bf16[192,384]{1,0:T(8,128)(2,1)S(1)}, u32[]{:S(2)}, u32[]{:S(2)}) collective-permute-start(bf16[192,384]{1,0:T(8,128)(2,1)S(1)} %get-tuple-element.67), channel_id=1, source_target_pairs={{0,80},{1,81},{2,82},{3,83},{4,84},{5,85},{6,86},{7,87},{8,88},{9,... | collective-permute-start | bytes 442376 | tf_op jit(solution)/shard_map/ppermute | solution.py:357
  93.0 1.4 %collective-permute-start.22 = (bf16[192,384]{1,0:T(8,128)(2,1)S(1)}, bf16[192,384]{1,0:T(8,128)(2,1)S(1)}, u32[]{:S(2)}, u32[]{:S(2)}) collective-permute-start(bf16[192,384]{1,0:T(8,128)(2,1)S(1)} %get-tuple-element.69), channel_id=1, source_target_pairs={{0,16},{1,17},{2,18},{3,19},{4,20},{5,21},{6,22},{7,23},{8,24},{9,... | collective-permute-start | bytes 442376 | tf_op jit(solution)/shard_map/ppermute | solution.py:357
  94.4 2.5 %collective-permute-done.20.refs_4_ = bf16[192,384]{1,0:T(8,128)(2,1)S(1)} collective-permute-done((bf16[192,384]{1,0:T(8,128)(2,1)S(1)}, bf16[192,384]{1,0:T(8,128)(2,1)S(1)}, u32[]{:S(2)}, u32[]{:S(2)}) %collective-permute-start.20) | collective-permute-done | bytes 147488 | tf_op jit(solution)/shard_map/ppermute | solution.py:357
  96.9 2.7 %collective-permute-done.21.refs_5_ = bf16[192,384]{1,0:T(8,128)(2,1)S(1)} collective-permute-done((bf16[192,384]{1,0:T(8,128)(2,1)S(1)}, bf16[192,384]{1,0:T(8,128)(2,1)S(1)}, u32[]{:S(2)}, u32[]{:S(2)}) %collective-permute-start.21) | collective-permute-done | bytes 147488 | tf_op jit(solution)/shard_map/ppermute | solution.py:357
  99.8 1.4 %second_solve.1.refs_0_ = bf16[192,384]{1,0:T(8,128)(2,1)S(1)} custom-call(s32[5]{0:T(128)S(1)} %stack.32.place_ref, bf16[192,384]{1,0:T(8,128)(2,1)S(1)} %collective-permute-done.16.refs_0_, bf16[192,384]{1,0:T(8,128)(2,1)S(1)} %collective-permute-done.17.refs_1_, bf16[192,384]{1,0:T(8,128)(2,1)S(1)} %collective-permute-done.18.refs_2_, ...), custom_call_target="tpu_custom_call" | custom-call | flops 339738624 | bytes 1769472 | tf_op jit(solution)/shard_map/second_solve/pallas_call | solution.py:284
  101.2 1.3 %collective-permute-start.23 = (bf16[192,384]{1,0:T(8,128)(2,1)S(1)}, bf16[192,384]{1,0:T(8,128)(2,1)S(1)}, u32[]{:S(2)}, u32[]{:S(2)}) collective-permute-start(bf16[192,384]{1,0:T(8,128)(2,1)S(1)} %second_solve.1.refs_0_), channel_id=1, source_target_pairs={{0,16},{1,17},{2,18},{3,19},{4,20},{5,21},{6,22},{7,23},{8,24},{9,... | collective-permute-start | bytes 442376 | tf_op jit(solution)/shard_map/ppermute | solution.py:357
  102.6 0.7 collective-permute-start.24
  103.3 3.4 %collective-permute-start.25 = (bf16[192,384]{1,0:T(8,128)(2,1)S(1)}, bf16[192,384]{1,0:T(8,128)(2,1)S(1)}, u32[]{:S(2)}, u32[]{:S(2)}) collective-permute-start(bf16[192,384]{1,0:T(8,128)(2,1)S(1)} %second_solve.1.refs_0_), channel_id=1, source_target_pairs={{0,48},{1,49},{2,50},{3,51},{4,52},{5,53},{6,54},{7,55},{8,56},{9,... | collective-permute-start | bytes 442376 | tf_op jit(solution)/shard_map/ppermute | solution.py:357
  106.7 1.2 collective-permute-start.26
  107.8 2.4 %collective-permute-start.27 = (bf16[192,384]{1,0:T(8,128)(2,1)S(1)}, bf16[192,384]{1,0:T(8,128)(2,1)S(1)}, u32[]{:S(2)}, u32[]{:S(2)}) collective-permute-start(bf16[192,384]{1,0:T(8,128)(2,1)S(1)} %second_solve.1.refs_0_), channel_id=1, source_target_pairs={{0,80},{1,81},{2,82},{3,83},{4,84},{5,85},{6,86},{7,87},{8,88},{9,... | collective-permute-start | bytes 442376 | tf_op jit(solution)/shard_map/ppermute | solution.py:357
  110.2 0.7 collective-permute-start.28
  110.9 2.2 %collective-permute-start.29 = (bf16[192,384]{1,0:T(8,128)(2,1)S(1)}, bf16[192,384]{1,0:T(8,128)(2,1)S(1)}, u32[]{:S(2)}, u32[]{:S(2)}) collective-permute-start(bf16[192,384]{1,0:T(8,128)(2,1)S(1)} %second_solve.1.refs_0_), channel_id=1, source_target_pairs={{0,112},{1,113},{2,114},{3,115},{4,116},{5,117},{6,118},{7,119},{8... | collective-permute-start | bytes 442376 | tf_op jit(solution)/shard_map/ppermute | solution.py:357
  113.2 1.3 copy-done
  114.4 1.2 join_one.1.refs_8_
  115.7 2.1 %collective-permute-done.26.refs_4_ = bf16[192,384]{1,0:T(8,128)(2,1)S(1)} collective-permute-done((bf16[192,384]{1,0:T(8,128)(2,1)S(1)}, bf16[192,384]{1,0:T(8,128)(2,1)S(1)}, u32[]{:S(2)}, u32[]{:S(2)}) %collective-permute-start.26) | collective-permute-done | bytes 147488 | tf_op jit(solution)/shard_map/ppermute | solution.py:357
  117.7 3.7 %collective-permute-done.27.refs_5_ = bf16[192,384]{1,0:T(8,128)(2,1)S(1)} collective-permute-done((bf16[192,384]{1,0:T(8,128)(2,1)S(1)}, bf16[192,384]{1,0:T(8,128)(2,1)S(1)}, u32[]{:S(2)}, u32[]{:S(2)}) %collective-permute-start.27) | collective-permute-done | bytes 147488 | tf_op jit(solution)/shard_map/ppermute | solution.py:357
  121.5 0.5 collective-permute-done.29.refs_7_
  122.0 1.8 %join_two.1 = bf16[2,384,1536]{2,1,0:T(8,128)(2,1)} custom-call(s32[5]{0:T(128)S(1)} %stack.32.place_ref, bf16[192,384]{1,0:T(8,128)(2,1)S(1)} %second_solve.1.refs_0_, bf16[192,384]{1,0:T(8,128)(2,1)S(1)} %collective-permute-done.23.refs_1_, bf16[192,384]{1,0:T(8,128)(2,1)S(1)} %collective-permute-done.24.refs_2_, ...), custom_call_target="tpu_custom_call", output_to_operand_aliasing={{}: (9, {})} | custom-call | flops 589824 | bytes 2359296 | tf_op jit(solution)/shard_map/join_two/pallas_call | solution.py:335
  (39 shorter events, 2.8 us)
Async XLA Ops:
  6.5 106.6 %all-gather.2.cloned.1.call-start = ((), (), s32[]{:S(2)}) async-start(), calls=%async_computation | async-start | bytes 1327104 | tf_op jit(solution)/shard_map/all_gather | solution.py:412
  10.6 20.7 %collective-permute-start = (bf16[192,384]{1,0:T(8,128)(2,1)S(1)}, bf16[192,384]{1,0:T(8,128)(2,1)S(1)}, u32[]{:S(2)}, u32[]{:S(2)}) collective-permute-start(bf16[192,384]{1,0:T(8,128)(2,1)S(1)} %get-tuple-element.39), channel_id=1, source_target_pairs={{0,48},{1,49},{2,50},{3,51},{4,52},{5,53},{6,54},{7,55},{8,56},{9,... | collective-permute-start | bytes 442376 | tf_op jit(solution)/shard_map/ppermute | solution.py:357
  13.7 17.6 %collective-permute-start.1 = (bf16[192,384]{1,0:T(8,128)(2,1)S(1)}, bf16[192,384]{1,0:T(8,128)(2,1)S(1)}, u32[]{:S(2)}, u32[]{:S(2)}) collective-permute-start(bf16[192,384]{1,0:T(8,128)(2,1)S(1)} %get-tuple-element.40), channel_id=1, source_target_pairs={{0,32},{1,33},{2,34},{3,35},{4,36},{5,37},{6,38},{7,39},{8,40},{9,... | collective-permute-start | bytes 442376 | tf_op jit(solution)/shard_map/ppermute | solution.py:357
  17.7 11.4 %collective-permute-start.2 = (bf16[192,384]{1,0:T(8,128)(2,1)S(1)}, bf16[192,384]{1,0:T(8,128)(2,1)S(1)}, u32[]{:S(2)}, u32[]{:S(2)}) collective-permute-start(bf16[192,384]{1,0:T(8,128)(2,1)S(1)} %get-tuple-element.43), channel_id=1, source_target_pairs={{0,112},{1,113},{2,114},{3,115},{4,116},{5,117},{6,118},{7,119},{8... | collective-permute-start | bytes 442376 | tf_op jit(solution)/shard_map/ppermute | solution.py:357
  20.3 8.7 %copy-start.2 = (f32[32,32]{1,0:T(8,128)S(1)}, f32[32,32]{1,0:T(8,128)}, u32[]{:S(2)}) copy-start(f32[32,32]{1,0:T(8,128)} %param.9) | copy-start | bytes 12292
  20.3 10.9 %copy-start.1 = (f32[2,384,384]{2,1,0:T(8,128)S(1)}, f32[2,384,384]{2,1,0:T(8,128)}, u32[]{:S(2)}) copy-start(f32[2,384,384]{2,1,0:T(8,128)} %param.8) | copy-start | bytes 3538948
  20.3 10.4 %collective-permute-start.3 = (bf16[192,384]{1,0:T(8,128)(2,1)S(1)}, bf16[192,384]{1,0:T(8,128)(2,1)S(1)}, u32[]{:S(2)}, u32[]{:S(2)}) collective-permute-start(bf16[192,384]{1,0:T(8,128)(2,1)S(1)} %get-tuple-element.44), channel_id=1, source_target_pairs={{0,96},{1,97},{2,98},{3,99},{4,100},{5,101},{6,102},{7,103},{8,104... | collective-permute-start | bytes 442376 | tf_op jit(solution)/shard_map/ppermute | solution.py:357
  25.9 8.9 %collective-permute-start.4 = (bf16[192,384]{1,0:T(8,128)(2,1)S(1)}, bf16[192,384]{1,0:T(8,128)(2,1)S(1)}, u32[]{:S(2)}, u32[]{:S(2)}) collective-permute-start(bf16[192,384]{1,0:T(8,128)(2,1)S(1)} %get-tuple-element.46), channel_id=1, source_target_pairs={{0,80},{1,81},{2,82},{3,83},{4,84},{5,85},{6,86},{7,87},{8,88},{9,... | collective-permute-start | bytes 442376 | tf_op jit(solution)/shard_map/ppermute | solution.py:357
  29.1 7.4 %collective-permute-start.5 = (bf16[192,384]{1,0:T(8,128)(2,1)S(1)}, bf16[192,384]{1,0:T(8,128)(2,1)S(1)}, u32[]{:S(2)}, u32[]{:S(2)}) collective-permute-start(bf16[192,384]{1,0:T(8,128)(2,1)S(1)} %get-tuple-element.47), channel_id=1, source_target_pairs={{0,64},{1,65},{2,66},{3,67},{4,68},{5,69},{6,70},{7,71},{8,72},{9,... | collective-permute-start | bytes 442376 | tf_op jit(solution)/shard_map/ppermute | solution.py:357
  30.8 5.7 %collective-permute-start.6 = (bf16[192,384]{1,0:T(8,128)(2,1)S(1)}, bf16[192,384]{1,0:T(8,128)(2,1)S(1)}, u32[]{:S(2)}, u32[]{:S(2)}) collective-permute-start(bf16[192,384]{1,0:T(8,128)(2,1)S(1)} %get-tuple-element.48), channel_id=1, source_target_pairs={{0,16},{1,17},{2,18},{3,19},{4,20},{5,21},{6,22},{7,23},{8,24},{9,... | collective-permute-start | bytes 442376 | tf_op jit(solution)/shard_map/ppermute | solution.py:357
  38.6 14.1 %collective-permute-start.7 = (bf16[192,384]{1,0:T(8,128)(2,1)S(1)}, bf16[192,384]{1,0:T(8,128)(2,1)S(1)}, u32[]{:S(2)}, u32[]{:S(2)}) collective-permute-start(bf16[192,384]{1,0:T(8,128)(2,1)S(1)} %get-tuple-element.52), channel_id=1, source_target_pairs={{0,0},{1,1},{2,16},{3,17},{4,36},{5,37},{6,52},{7,53},{8,72},{9,73... | collective-permute-start | bytes 442376 | tf_op jit(solution)/shard_map/ppermute | solution.py:357
  39.3 13.4 %collective-permute-start.8 = (bf16[192,384]{1,0:T(8,128)(2,1)S(1)}, bf16[192,384]{1,0:T(8,128)(2,1)S(1)}, u32[]{:S(2)}, u32[]{:S(2)}) collective-permute-start(bf16[192,384]{1,0:T(8,128)(2,1)S(1)} %get-tuple-element.52), channel_id=1, source_target_pairs={{0,10},{1,11},{2,26},{3,27},{4,46},{5,47},{6,62},{7,63},{8,66},{9,... | collective-permute-start | bytes 442376 | tf_op jit(solution)/shard_map/ppermute | solution.py:357
  52.7 9.7 %collective-permute-start.9 = (bf16[2,192,384]{2,1,0:T(8,128)(2,1)S(1)}, bf16[2,192,384]{2,1,0:T(8,128)(2,1)S(1)}, u32[]{:S(2)}, u32[]{:S(2)}) collective-permute-start(bf16[2,192,384]{2,1,0:T(8,128)(2,1)S(1)} %pad_maximum_fusion.refs_0_), channel_id=1, source_target_pairs={{0,4},{4,8},{8,12},{12,0},{1,5},{5,9},{9,13},{13,1},{2,6},{6,10},{... | collective-permute-start | bytes 884744 | tf_op jit(solution)/shard_map/ppermute | solution.py:382
  55.0 13.8 %collective-permute-start.10 = (bf16[2,192,384]{2,1,0:T(8,128)(2,1)S(1)}, bf16[2,192,384]{2,1,0:T(8,128)(2,1)S(1)}, u32[]{:S(2)}, u32[]{:S(2)}) collective-permute-start(bf16[2,192,384]{2,1,0:T(8,128)(2,1)S(1)} %pad_maximum_fusion.refs_0_), channel_id=1, source_target_pairs={{0,8},{4,12},{8,0},{12,4},{1,9},{5,13},{9,1},{13,5},{2,10},{6,14},... | collective-permute-start | bytes 884744 | tf_op jit(solution)/shard_map/ppermute | solution.py:382
  56.9 11.9 %collective-permute-start.11 = (bf16[2,192,384]{2,1,0:T(8,128)(2,1)S(1)}, bf16[2,192,384]{2,1,0:T(8,128)(2,1)S(1)}, u32[]{:S(2)}, u32[]{:S(2)}) collective-permute-start(bf16[2,192,384]{2,1,0:T(8,128)(2,1)S(1)} %pad_maximum_fusion.refs_0_), channel_id=1, source_target_pairs={{0,12},{4,0},{8,4},{12,8},{1,13},{5,1},{9,5},{13,9},{2,14},{6,2},{... | collective-permute-start | bytes 884744 | tf_op jit(solution)/shard_map/ppermute | solution.py:382
  59.4 9.9 %collective-permute-start.12 = (bf16[2,192,384]{2,1,0:T(8,128)(2,1)S(1)}, bf16[2,192,384]{2,1,0:T(8,128)(2,1)S(1)}, u32[]{:S(2)}, u32[]{:S(2)}) collective-permute-start(bf16[2,192,384]{2,1,0:T(8,128)(2,1)S(1)} %pad_maximum_fusion.refs_0_), channel_id=1, source_target_pairs={{0,1},{1,0},{2,3},{3,2},{4,5},{5,4},{6,7},{7,6},{8,9},{9,8},{10,11... | collective-permute-start | bytes 884744 | tf_op jit(solution)/shard_map/ppermute | solution.py:418
  62.5 6.8 %collective-permute-start.13 = (bf16[2,192,384]{2,1,0:T(8,128)(2,1)S(1)}, bf16[2,192,384]{2,1,0:T(8,128)(2,1)S(1)}, u32[]{:S(2)}, u32[]{:S(2)}) collective-permute-start(bf16[2,192,384]{2,1,0:T(8,128)(2,1)S(1)} %collective-permute-done.9.refs_1_), channel_id=1, source_target_pairs={{0,1},{1,0},{2,3},{3,2},{4,5},{5,4},{6,7},{7,6},{8,9},{9,8},{10,11... | collective-permute-start | bytes 884744 | tf_op jit(solution)/shard_map/ppermute | solution.py:418
  68.8 1.6 %collective-permute-start.14 = (bf16[2,192,384]{2,1,0:T(8,128)(2,1)S(1)}, bf16[2,192,384]{2,1,0:T(8,128)(2,1)S(1)}, u32[]{:S(2)}, u32[]{:S(2)}) collective-permute-start(bf16[2,192,384]{2,1,0:T(8,128)(2,1)S(1)} %collective-permute-done.10.refs_2_), channel_id=1, source_target_pairs={{0,1},{1,0},{2,3},{3,2},{4,5},{5,4},{6,7},{7,6},{8,9},{9,8},{10,11... | collective-permute-start | bytes 884744 | tf_op jit(solution)/shard_map/ppermute | solution.py:418
  68.8 2.0 %collective-permute-start.15 = (bf16[2,192,384]{2,1,0:T(8,128)(2,1)S(1)}, bf16[2,192,384]{2,1,0:T(8,128)(2,1)S(1)}, u32[]{:S(2)}, u32[]{:S(2)}) collective-permute-start(bf16[2,192,384]{2,1,0:T(8,128)(2,1)S(1)} %collective-permute-done.11.refs_3_), channel_id=1, source_target_pairs={{0,1},{1,0},{2,3},{3,2},{4,5},{5,4},{6,7},{7,6},{8,9},{9,8},{10,11... | collective-permute-start | bytes 884744 | tf_op jit(solution)/shard_map/ppermute | solution.py:418
  74.4 10.0 %collective-permute-start.16 = (bf16[192,384]{1,0:T(8,128)(2,1)S(1)}, bf16[192,384]{1,0:T(8,128)(2,1)S(1)}, u32[]{:S(2)}, u32[]{:S(2)}) collective-permute-start(bf16[192,384]{1,0:T(8,128)(2,1)S(1)} %get-tuple-element.60), channel_id=1, source_target_pairs={{0,48},{1,49},{2,50},{3,51},{4,52},{5,53},{6,54},{7,55},{8,56},{9,... | collective-permute-start | bytes 442376 | tf_op jit(solution)/shard_map/ppermute | solution.py:357
  77.4 8.3 %collective-permute-start.17 = (bf16[192,384]{1,0:T(8,128)(2,1)S(1)}, bf16[192,384]{1,0:T(8,128)(2,1)S(1)}, u32[]{:S(2)}, u32[]{:S(2)}) collective-permute-start(bf16[192,384]{1,0:T(8,128)(2,1)S(1)} %get-tuple-element.59), channel_id=1, source_target_pairs={{0,32},{1,33},{2,34},{3,35},{4,36},{5,37},{6,38},{7,39},{8,40},{9,... | collective-permute-start | bytes 442376 | tf_op jit(solution)/shard_map/ppermute | solution.py:357
  80.0 14.3 %collective-permute-start.18 = (bf16[192,384]{1,0:T(8,128)(2,1)S(1)}, bf16[192,384]{1,0:T(8,128)(2,1)S(1)}, u32[]{:S(2)}, u32[]{:S(2)}) collective-permute-start(bf16[192,384]{1,0:T(8,128)(2,1)S(1)} %get-tuple-element.64), channel_id=1, source_target_pairs={{0,112},{1,113},{2,114},{3,115},{4,116},{5,117},{6,118},{7,119},{8... | collective-permute-start | bytes 442376 | tf_op jit(solution)/shard_map/ppermute | solution.py:357
  83.0 11.3 %collective-permute-start.19 = (bf16[192,384]{1,0:T(8,128)(2,1)S(1)}, bf16[192,384]{1,0:T(8,128)(2,1)S(1)}, u32[]{:S(2)}, u32[]{:S(2)}) collective-permute-start(bf16[192,384]{1,0:T(8,128)(2,1)S(1)} %get-tuple-element.65), channel_id=1, source_target_pairs={{0,96},{1,97},{2,98},{3,99},{4,100},{5,101},{6,102},{7,103},{8,104... | collective-permute-start | bytes 442376 | tf_op jit(solution)/shard_map/ppermute | solution.py:357
  88.9 8.0 %collective-permute-start.20 = (bf16[192,384]{1,0:T(8,128)(2,1)S(1)}, bf16[192,384]{1,0:T(8,128)(2,1)S(1)}, u32[]{:S(2)}, u32[]{:S(2)}) collective-permute-start(bf16[192,384]{1,0:T(8,128)(2,1)S(1)} %get-tuple-element.67), channel_id=1, source_target_pairs={{0,80},{1,81},{2,82},{3,83},{4,84},{5,85},{6,86},{7,87},{8,88},{9,... | collective-permute-start | bytes 442376 | tf_op jit(solution)/shard_map/ppermute | solution.py:357
  92.6 7.0 %collective-permute-start.21 = (bf16[192,384]{1,0:T(8,128)(2,1)S(1)}, bf16[192,384]{1,0:T(8,128)(2,1)S(1)}, u32[]{:S(2)}, u32[]{:S(2)}) collective-permute-start(bf16[192,384]{1,0:T(8,128)(2,1)S(1)} %get-tuple-element.68), channel_id=1, source_target_pairs={{0,64},{1,65},{2,66},{3,67},{4,68},{5,69},{6,70},{7,71},{8,72},{9,... | collective-permute-start | bytes 442376 | tf_op jit(solution)/shard_map/ppermute | solution.py:357
  93.0 6.8 %collective-permute-start.22 = (bf16[192,384]{1,0:T(8,128)(2,1)S(1)}, bf16[192,384]{1,0:T(8,128)(2,1)S(1)}, u32[]{:S(2)}, u32[]{:S(2)}) collective-permute-start(bf16[192,384]{1,0:T(8,128)(2,1)S(1)} %get-tuple-element.69), channel_id=1, source_target_pairs={{0,16},{1,17},{2,18},{3,19},{4,20},{5,21},{6,22},{7,23},{8,24},{9,... | collective-permute-start | bytes 442376 | tf_op jit(solution)/shard_map/ppermute | solution.py:357
  101.2 9.0 %collective-permute-start.23 = (bf16[192,384]{1,0:T(8,128)(2,1)S(1)}, bf16[192,384]{1,0:T(8,128)(2,1)S(1)}, u32[]{:S(2)}, u32[]{:S(2)}) collective-permute-start(bf16[192,384]{1,0:T(8,128)(2,1)S(1)} %second_solve.1.refs_0_), channel_id=1, source_target_pairs={{0,16},{1,17},{2,18},{3,19},{4,20},{5,21},{6,22},{7,23},{8,24},{9,... | collective-permute-start | bytes 442376 | tf_op jit(solution)/shard_map/ppermute | solution.py:357
  102.6 8.4 %collective-permute-start.24 = (bf16[192,384]{1,0:T(8,128)(2,1)S(1)}, bf16[192,384]{1,0:T(8,128)(2,1)S(1)}, u32[]{:S(2)}, u32[]{:S(2)}) collective-permute-start(bf16[192,384]{1,0:T(8,128)(2,1)S(1)} %second_solve.1.refs_0_), channel_id=1, source_target_pairs={{0,32},{1,33},{2,34},{3,35},{4,36},{5,37},{6,38},{7,39},{8,40},{9,... | collective-permute-start | bytes 442376 | tf_op jit(solution)/shard_map/ppermute | solution.py:357
  103.3 12.4 %collective-permute-start.25 = (bf16[192,384]{1,0:T(8,128)(2,1)S(1)}, bf16[192,384]{1,0:T(8,128)(2,1)S(1)}, u32[]{:S(2)}, u32[]{:S(2)}) collective-permute-start(bf16[192,384]{1,0:T(8,128)(2,1)S(1)} %second_solve.1.refs_0_), channel_id=1, source_target_pairs={{0,48},{1,49},{2,50},{3,51},{4,52},{5,53},{6,54},{7,55},{8,56},{9,... | collective-permute-start | bytes 442376 | tf_op jit(solution)/shard_map/ppermute | solution.py:357
  106.7 11.1 %collective-permute-start.26 = (bf16[192,384]{1,0:T(8,128)(2,1)S(1)}, bf16[192,384]{1,0:T(8,128)(2,1)S(1)}, u32[]{:S(2)}, u32[]{:S(2)}) collective-permute-start(bf16[192,384]{1,0:T(8,128)(2,1)S(1)} %second_solve.1.refs_0_), channel_id=1, source_target_pairs={{0,64},{1,65},{2,66},{3,67},{4,68},{5,69},{6,70},{7,71},{8,72},{9,... | collective-permute-start | bytes 442376 | tf_op jit(solution)/shard_map/ppermute | solution.py:357
  107.8 13.6 %collective-permute-start.27 = (bf16[192,384]{1,0:T(8,128)(2,1)S(1)}, bf16[192,384]{1,0:T(8,128)(2,1)S(1)}, u32[]{:S(2)}, u32[]{:S(2)}) collective-permute-start(bf16[192,384]{1,0:T(8,128)(2,1)S(1)} %second_solve.1.refs_0_), channel_id=1, source_target_pairs={{0,80},{1,81},{2,82},{3,83},{4,84},{5,85},{6,86},{7,87},{8,88},{9,... | collective-permute-start | bytes 442376 | tf_op jit(solution)/shard_map/ppermute | solution.py:357
  110.2 11.3 %collective-permute-start.28 = (bf16[192,384]{1,0:T(8,128)(2,1)S(1)}, bf16[192,384]{1,0:T(8,128)(2,1)S(1)}, u32[]{:S(2)}, u32[]{:S(2)}) collective-permute-start(bf16[192,384]{1,0:T(8,128)(2,1)S(1)} %second_solve.1.refs_0_), channel_id=1, source_target_pairs={{0,96},{1,97},{2,98},{3,99},{4,100},{5,101},{6,102},{7,103},{8,104... | collective-permute-start | bytes 442376 | tf_op jit(solution)/shard_map/ppermute | solution.py:357
  110.9 11.1 %collective-permute-start.29 = (bf16[192,384]{1,0:T(8,128)(2,1)S(1)}, bf16[192,384]{1,0:T(8,128)(2,1)S(1)}, u32[]{:S(2)}, u32[]{:S(2)}) collective-permute-start(bf16[192,384]{1,0:T(8,128)(2,1)S(1)} %second_solve.1.refs_0_), channel_id=1, source_target_pairs={{0,112},{1,113},{2,114},{3,115},{4,116},{5,117},{6,118},{7,119},{8... | collective-permute-start | bytes 442376 | tf_op jit(solution)/shard_map/ppermute | solution.py:357
  113.2 1.3 copy-start
Sparse Core Ops, SparseCore 0:
  38.7 45.0 all-gather.1

commit v8 on v5

--- a/solution.py
+++ b/solution.py
@@ -20,6 +20,7 @@
 
 VMEM = pl.BlockSpec(memory_space=pltpu.VMEM)
 SMEM = pl.BlockSpec(memory_space=pltpu.SMEM)
+HBM = pl.BlockSpec(memory_space=pltpu.HBM)
 
 
 def in_hbm(array):
@@ -274,37 +275,54 @@
     )(place, *parts, prior, inverse, *extra)
 
 
-def join_kernel(front, moves, pairs, place_ref, *refs):
-    chunk_refs, (out_ref, block_ref, sems) = refs[: 2 * len(moves)] if not pairs else refs[: len(moves)], refs[-3:]
+def put_blocks(blocks, block_ref, sems, out_ref, front):
     width = block_ref.shape[2]
     copies = []
-    for i, dy in enumerate(moves):
-        own, other = (chunk_refs[i][0], chunk_refs[i][1]) if pairs else (chunk_refs[2 * i][...], chunk_refs[2 * i + 1][...])
-        if i >= 2:
-            copies[i - 2].wait()
-        place_pair(own, other, place_ref[ZL], slice(None), block_ref.at[i % 2], None)
-        at = pl.ds(pl.multiple_of(position((place_ref[Y] - dy) & 3) * width, 128), width)
-        copies.append(pltpu.make_async_copy(block_ref.at[i % 2], out_ref.at[front, :, at], sems.at[i % 2]))
+    for i, (start, write) in enumerate(blocks):
+        write(block_ref.at[i])
+        at = pl.ds(pl.multiple_of(start, 128), width)
+        copies.append(pltpu.make_async_copy(block_ref.at[i], out_ref.at[front, :, at], sems.at[i]))
         copies[i].start()
-    for copy in copies[-2:]:
+    for copy in copies:
         copy.wait()
 
 
-def join(front, moves, pairs, place, chunks, fronts, shape):
+def join_one_kernel(place_ref, own_ref, other_ref, out_ref, block_ref, sems):
+    def block(dy):
+        def write(ref):
+            place_pair(own_ref[dy], other_ref[dy], place_ref[ZL], slice(None), ref, None)
+
+        return position((place_ref[Y] - dy) & 3) * block_ref.shape[2], write
+
+    put_blocks([block(dy) for dy in range(4)], block_ref, sems, out_ref, 0)
+
+
+def join_two_kernel(place_ref, *refs):
+    chunk_refs, (out_ref, block_ref, sems) = refs[:8], refs[9:]
+
+    def block(dy):
+        def write(ref):
+            own, other = chunk_refs[2 * dy][...], chunk_refs[2 * dy + 1][...]
+            place_pair(own, other, place_ref[ZL], slice(None), ref, None)
+
+        return position((place_ref[Y] - dy) & 3) * block_ref.shape[2], write
+
+    put_blocks([block(dy) for dy in (0, 2, 1, 3)], block_ref, sems, out_ref, 1)
+
+
+def join(kernel, args, in_specs, shape, aliases, name):
     _, rows, cols = shape
-    hbm = pl.BlockSpec(memory_space=pltpu.HBM)
-    before = [] if fronts is None else [fronts]
     return pl.pallas_call(
-        functools.partial(join_kernel, front, moves, pairs),
-        in_specs=[SMEM] + [VMEM] * len(chunks) + [hbm] * len(before),
-        out_specs=hbm,
+        kernel,
+        in_specs=in_specs,
+        out_specs=HBM,
         out_shape=jax.ShapeDtypeStruct(shape, bf16),
-        scratch_shapes=[pltpu.VMEM((2, rows, cols // 4), bf16), pltpu.SemaphoreType.DMA((2,))],
-        input_output_aliases={1 + len(chunks): 0} if before else {},
+        scratch_shapes=[pltpu.VMEM((4, rows, cols // 4), bf16), pltpu.SemaphoreType.DMA((4,))],
+        input_output_aliases=aliases,
         compiler_params=params(6),
-        cost_estimate=cost(rows * cols, len(moves) * rows * cols),
-        name="join",
-    )(place, *chunks, *before)
+        cost_estimate=cost(rows * cols, 4 * rows * cols),
+        name=name,
+    )(*args)
 
 
 def move(value, target):
@@ -334,7 +352,7 @@
     return parts
 
 
-def spread_pairs(pair, axis):
+def spread(pair, axis):
     pairs = {0: pair}
     for d in (2, 1, 3):
         pairs[d] = lax.ppermute(pair, axis, [(i, (i + d) % 4) for i in range(4)])
@@ -364,10 +382,14 @@
     front_one, energy = solve(
         first_solve_kernel, place, parts, prior_one, inverse_part[0], [coupling], 2, "first_solve"
     )
-    own = spread_pairs(jnp.stack([move(energy, turn(0)), move(energy, turn(1))]), "x")
+    pair = [move(energy, turn(0)), move(energy, turn(1))]
+    ones = spread(front_one, "y")
+    pair, ones = lax.optimization_barrier((pair, ones))
+    own = spread(jnp.stack(pair), "x")
+    ones = jnp.stack(ones)
+    others = lax.ppermute(ones, "zl", SWAP)
     other = [lax.ppermute(pair, "c", SWAP) for pair in own]
-    ones = spread_pairs(jnp.stack([front_one, lax.ppermute(front_one, "zl", SWAP)]), "y")
-    own, other, ones = lax.optimization_barrier((own, other, ones))
+    own, other, others = lax.optimization_barrier((own, other, others))
     lhs = next_memory(place, memory, own + other)
     odd = half_product(place, lhs, odd_resident)
     lhs, odd = lax.optimization_barrier((lhs, odd))
@@ -377,11 +399,11 @@
         second_solve_kernel, place, parts, prior_two, inverse_part[1], [], 1, "second_solve"
     )
     chunks = spread_chunks(front_two)
-    fronts = join(0, (0, 1, 2, 3), True, place, ones, None, previous.shape)
-    for moves in ((0, 2), (1, 3)):
-        some = [chunks[dy, dz] for dy in moves for dz in range(2)]
-        fronts = join(1, moves, False, place, some, fronts, previous.shape)
-    return fronts
+    chunks = [chunks[dy, dz] for dy in range(4) for dz in range(2)]
+    fronts = join(join_one_kernel, (place, ones, others), [SMEM, VMEM, VMEM], previous.shape, {}, "join_one")
+    return join(
+        join_two_kernel, (place, *chunks, fronts), [SMEM] + [VMEM] * 8 + [HBM], previous.shape, {9: 0}, "join_two"
+    )
 
 
 def solution(mesh):

time: 114 us -> 113 us (level)
  waiting for transfers between devices: 27.9 us -> 34.7 us
  starting transfers between devices: 55.3 us -> 48.6 us
  Pallas kernels: 30.2 us -> 28.1 us
    ppermute x7, starting transfers between devices: 18 us -> 9.63 us  [the longest x6 8.73 us: spread(): pairs[d] = lax.ppermute(pair, axis, [(i, (i + d) % 4) for i in range(4)])]
    ppermute x7, waiting for transfers between devices: 8.33 us -> 15.3 us  [the longest x6 15.3 us: spread(): pairs[d] = lax.ppermute(pair, axis, [(i, (i + d) % 4) for i in range(4)])]
    pallas_call x3 -> x2, Pallas kernels: 5.69 us -> 3.6 us  [join(): pl.pallas_call(kernel, in_specs=in_specs, out_specs=HBM, out_shape=jax.Sh...]
    ppermute x23, starting transfers between devices: 37.2 us -> 39 us  [move(): return lax.ppermute(value, ALL, pairs)]
  transfers between devices with their start and end apart: 34 -> 34, of which waited for: 11 -> 15; matrix products, arithmetic and copies ran while one was open for 0% -> 0% of each run, Pallas kernels for 13% -> 11%
where the time goes in v8:
time: 113 us; the launch traced here: 112 us
  starting transfers between devices  48.6 us (43%)
  waiting for transfers between devices  34.7 us (31%)
  Pallas kernels  28.1 us (25%)
    ppermute x23, starting transfers between devices, move(): return lax.ppermute(value, ALL, pairs)  39 us
    ppermute x23, waiting for transfers between devices, move(): return lax.ppermute(value, ALL, pairs)  17.8 us
    ppermute x6, waiting for transfers between devices, spread(): pairs[d] = lax.ppermute(pair, axis, [(i, (i + d) % 4) for i in range(4)])  15.3 us
    ppermute x6, starting transfers between devices, spread(): pairs[d] = lax.ppermute(pair, axis, [(i, (i + d) % 4) for i in range(4)])  8.73 us
    pallas_call x3, Pallas kernels, half_product(): pl.pallas_call(half_product_kernel, in_specs=[SMEM, VMEM, VMEM], out_spec...  7.98 us
    pallas_call x1, Pallas kernels, first_product(): pl.pallas_call(first_product_kernel, in_specs=[SMEM] + [pl.BlockSpec(memo...  6.5 us
    pallas_call x1, Pallas kernels, bring(): pl.pallas_call(bring_kernel, in_specs=[SMEM] + [pl.BlockSpec(memory_space...  5.18 us
    pallas_call x2, Pallas kernels, join(): pl.pallas_call(kernel, in_specs=in_specs, out_specs=HBM, out_shape=jax.Sh...  3.6 us
  transfers between devices with their start and end apart: 34, of which 15 were waited for; matrix products, arithmetic and copies ran while one was open for 0% of the time, Pallas kernels for 11%

profile of v8, /device:TPU:0, one launch (start us, length us, event | category | flops | bytes accessed | tf_op | source)
XLA Modules:
  0.0 112.2 jit_solution(1491954097786437804)
XLA Ops:
  0.1 6.5 %first_product.1 = (bf16[192,384]{1,0:T(8,128)(2,1)S(1)}, bf16[192,384]{1,0:T(8,128)(2,1)S(1)}, bf16[192,384]{1,0:T(8,128)(2,1)S(1)}, bf16[192,384]{1,0:T(8,128)...) custom-call(s32[5]{0:T(128)S(1)} %stack.47.place_ref, bf16[2,384,3072]{2,1,0:T(8,128)(2,1)} %memory_ref.3, ...), custom_call_target="tpu_custom_call" | custom-call | flops 1811939328 | bytes 18874368 | tf_op jit(solution)/shard_map/first_product/pallas_call | solution.py:112
  6.6 1.7 %collective-permute-start.1 = (bf16[192,384]{1,0:T(8,128)(2,1)S(1)}, bf16[192,384]{1,0:T(8,128)(2,1)S(1)}, u32[]{:S(2)}, u32[]{:S(2)}) collective-permute-start(bf16[192,384]{1,0:T(8,128)(2,1)S(1)} %get-tuple-element.57), channel_id=1, source_target_pairs={{0,32},{1,33},{2,34},{3,35},{4,36},{5,37},{6,38},{7,39},{8,40},{9,... | collective-permute-start | bytes 442376 | tf_op jit(solution)/shard_map/ppermute | solution.py:337
  8.3 1.8 %collective-permute-start = (bf16[192,384]{1,0:T(8,128)(2,1)S(1)}, bf16[192,384]{1,0:T(8,128)(2,1)S(1)}, u32[]{:S(2)}, u32[]{:S(2)}) collective-permute-start(bf16[192,384]{1,0:T(8,128)(2,1)S(1)} %get-tuple-element.58), channel_id=1, source_target_pairs={{0,48},{1,49},{2,50},{3,51},{4,52},{5,53},{6,54},{7,55},{8,56},{9,... | collective-permute-start | bytes 442376 | tf_op jit(solution)/shard_map/ppermute | solution.py:337
  10.1 3.0 %collective-permute-start.3 = (bf16[192,384]{1,0:T(8,128)(2,1)S(1)}, bf16[192,384]{1,0:T(8,128)(2,1)S(1)}, u32[]{:S(2)}, u32[]{:S(2)}) collective-permute-start(bf16[192,384]{1,0:T(8,128)(2,1)S(1)} %get-tuple-element.59), channel_id=1, source_target_pairs={{0,96},{1,97},{2,98},{3,99},{4,100},{5,101},{6,102},{7,103},{8,104... | collective-permute-start | bytes 442376 | tf_op jit(solution)/shard_map/ppermute | solution.py:337
  13.2 2.7 %half_product.3 = (bf16[192,384]{1,0:T(8,128)(2,1)S(1)}, bf16[192,384]{1,0:T(8,128)(2,1)S(1)}, bf16[192,384]{1,0:T(8,128)(2,1)S(1)}, bf16[192,384]{1,0:T(8,128)(2,1)S(1)}) custom-call(s32[5]{0:T(128)S(1)} %stack.47.place_ref, bf16[384,3072]{1,0:T(8,128)(2,1)S(1)} %get-tuple-element.61.lhs_ref, bf16[3072,768]{1,0:T(8,128)(2,1)S(1)} %get-tuple-element.62.resident_ref), custom_call_target="tpu_custom_call" | custom-call | flops 1811939328 | bytes 294912 | tf_op jit(solution)/shard_map/half_product/pallas_call | solution.py:60
  15.8 3.2 %collective-permute-start.4 = (bf16[192,384]{1,0:T(8,128)(2,1)S(1)}, bf16[192,384]{1,0:T(8,128)(2,1)S(1)}, u32[]{:S(2)}, u32[]{:S(2)}) collective-permute-start(bf16[192,384]{1,0:T(8,128)(2,1)S(1)} %get-tuple-element.70), channel_id=1, source_target_pairs={{0,80},{1,81},{2,82},{3,83},{4,84},{5,85},{6,86},{7,87},{8,88},{9,... | collective-permute-start | bytes 442376 | tf_op jit(solution)/shard_map/ppermute | solution.py:337
  19.1 1.6 %collective-permute-start.5 = (bf16[192,384]{1,0:T(8,128)(2,1)S(1)}, bf16[192,384]{1,0:T(8,128)(2,1)S(1)}, u32[]{:S(2)}, u32[]{:S(2)}) collective-permute-start(bf16[192,384]{1,0:T(8,128)(2,1)S(1)} %get-tuple-element.71), channel_id=1, source_target_pairs={{0,64},{1,65},{2,66},{3,67},{4,68},{5,69},{6,70},{7,71},{8,72},{9,... | collective-permute-start | bytes 442376 | tf_op jit(solution)/shard_map/ppermute | solution.py:337
  20.8 0.3 collective-permute-start.6
  21.2 5.5 %collective-permute-done.2.refs_2_ = bf16[192,384]{1,0:T(8,128)(2,1)S(1)} collective-permute-done((bf16[192,384]{1,0:T(8,128)(2,1)S(1)}, bf16[192,384]{1,0:T(8,128)(2,1)S(1)}, u32[]{:S(2)}, u32[]{:S(2)}) %collective-permute-start.2) | collective-permute-done | bytes 147488 | tf_op jit(solution)/shard_map/ppermute | solution.py:337
  26.7 5.2 %bring.1 = (bf16[384,3072]{1,0:T(8,128)(2,1)S(1)}, bf16[192,384]{1,0:T(8,128)(2,1)S(1)}, bf16[192,384]{1,0:T(8,128)(2,1)S(1)}, bf16[3072,768]{1,0:T(8,128)(2,1)S(1)}, bf16[3072,768]{1,0:T(8,128)(2,1)S(1)}) custom-call(s32[5]{0:T(128)S(1)} %stack.47.place_ref, bf16[2,384,3072]{2,1,0:T(8,128)(2,1)} %memory_ref.3, bf16[2,384,1536]{2,1,0:T(8,128)(2,1)} %previous_ref.1, ...), custom_call_target="tpu_custom_call" | custom-call | bytes 11796480 | tf_op jit(solution)/shard_map/bring/pallas_call | solution.py:160
  31.9 1.8 %first_solve.1 = (bf16[192,384]{1,0:T(8,128)(2,1)S(1)}, bf16[192,384]{1,0:T(8,128)(2,1)S(1)}) custom-call(s32[5]{0:T(128)S(1)} %stack.47.place_ref, bf16[192,384]{1,0:T(8,128)(2,1)S(1)} %collective-permute-done.refs_0_, bf16[192,384]{1,0:T(8,128)(2,1)S(1)} %collective-permute-done.1.refs_1_, bf16[192,384]{1,0:T(8,128)(2,1)S(1)} %collective-permute-done.2.refs_2_, ...), custom_call_target="tpu_custom_call" | custom-call | flops 339738624 | bytes 1769472 | tf_op jit(solution)/shard_map/first_solve/pallas_call | solution.py:267
  33.8 6.1 %collective-permute-start.8 = (bf16[192,384]{1,0:T(8,128)(2,1)S(1)}, bf16[192,384]{1,0:T(8,128)(2,1)S(1)}, u32[]{:S(2)}, u32[]{:S(2)}) collective-permute-start(bf16[192,384]{1,0:T(8,128)(2,1)S(1)} %get-tuple-element.74), channel_id=1, source_target_pairs={{0,10},{1,11},{2,26},{3,27},{4,46},{5,47},{6,62},{7,63},{8,66},{9,... | collective-permute-start | bytes 442376 | tf_op jit(solution)/shard_map/ppermute | solution.py:337
  39.9 0.7 collective-permute-start.7
  40.5 2.5 %collective-permute-start.11 = (bf16[192,384]{1,0:T(8,128)(2,1)S(1)}, bf16[192,384]{1,0:T(8,128)(2,1)S(1)}, u32[]{:S(2)}, u32[]{:S(2)}) collective-permute-start(bf16[192,384]{1,0:T(8,128)(2,1)S(1)} %get-tuple-element.78), channel_id=1, source_target_pairs={{0,96},{32,0},{64,32},{96,64},{1,97},{33,1},{65,33},{97,65},{2,98}... | collective-permute-start | bytes 442376 | tf_op jit(solution)/shard_map/ppermute | solution.py:358
  43.0 2.1 %collective-permute-start.10 = (bf16[192,384]{1,0:T(8,128)(2,1)S(1)}, bf16[192,384]{1,0:T(8,128)(2,1)S(1)}, u32[]{:S(2)}, u32[]{:S(2)}) collective-permute-start(bf16[192,384]{1,0:T(8,128)(2,1)S(1)} %get-tuple-element.78), channel_id=1, source_target_pairs={{0,64},{32,96},{64,0},{96,32},{1,65},{33,97},{65,1},{97,33},{2,66}... | collective-permute-start | bytes 442376 | tf_op jit(solution)/shard_map/ppermute | solution.py:358
  45.1 2.1 %collective-permute-done.11 = bf16[192,384]{1,0:T(8,128)(2,1)S(1)} collective-permute-done((bf16[192,384]{1,0:T(8,128)(2,1)S(1)}, bf16[192,384]{1,0:T(8,128)(2,1)S(1)}, u32[]{:S(2)}, u32[]{:S(2)}) %collective-permute-start.11) | collective-permute-done | bytes 147488 | tf_op jit(solution)/shard_map/ppermute | solution.py:358
  47.3 2.4 %collective-permute-done.10 = bf16[192,384]{1,0:T(8,128)(2,1)S(1)} collective-permute-done((bf16[192,384]{1,0:T(8,128)(2,1)S(1)}, bf16[192,384]{1,0:T(8,128)(2,1)S(1)}, u32[]{:S(2)}, u32[]{:S(2)}) %collective-permute-start.10) | collective-permute-done | bytes 147488 | tf_op jit(solution)/shard_map/ppermute | solution.py:358
  49.6 1.8 %collective-permute-done.9 = bf16[192,384]{1,0:T(8,128)(2,1)S(1)} collective-permute-done((bf16[192,384]{1,0:T(8,128)(2,1)S(1)}, bf16[192,384]{1,0:T(8,128)(2,1)S(1)}, u32[]{:S(2)}, u32[]{:S(2)}) %collective-permute-start.9) | collective-permute-done | bytes 147488 | tf_op jit(solution)/shard_map/ppermute | solution.py:358
  51.5 2.8 %collective-permute-start.14 = (bf16[2,192,384]{2,1,0:T(8,128)(2,1)S(1)}, bf16[2,192,384]{2,1,0:T(8,128)(2,1)S(1)}, u32[]{:S(2)}, u32[]{:S(2)}) collective-permute-start(bf16[2,192,384]{2,1,0:T(8,128)(2,1)S(1)} %pad_maximum_fusion.1.refs_0_), channel_id=1, source_target_pairs={{0,12},{4,0},{8,4},{12,8},{1,13},{5,1},{9,5},{13,9},{2,14},{6,2},{... | collective-permute-start | bytes 884744 | tf_op jit(solution)/shard_map/ppermute | solution.py:358
  54.3 1.4 %collective-permute-start.13 = (bf16[2,192,384]{2,1,0:T(8,128)(2,1)S(1)}, bf16[2,192,384]{2,1,0:T(8,128)(2,1)S(1)}, u32[]{:S(2)}, u32[]{:S(2)}) collective-permute-start(bf16[2,192,384]{2,1,0:T(8,128)(2,1)S(1)} %pad_maximum_fusion.1.refs_0_), channel_id=1, source_target_pairs={{0,8},{4,12},{8,0},{12,4},{1,9},{5,13},{9,1},{13,5},{2,10},{6,14},... | collective-permute-start | bytes 884744 | tf_op jit(solution)/shard_map/ppermute | solution.py:358
  55.8 0.9 collective-permute-start.19
  56.7 5.0 %collective-permute-done.14.refs_3_ = bf16[2,192,384]{2,1,0:T(8,128)(2,1)S(1)} collective-permute-done((bf16[2,192,384]{2,1,0:T(8,128)(2,1)S(1)}, bf16[2,192,384]{2,1,0:T(8,128)(2,1)S(1)}, u32[]{:S(2)}, u32[]{:S(2)}) %collective-permute-start.14) | collective-permute-done | bytes 294944 | tf_op jit(solution)/shard_map/ppermute | solution.py:358
  61.7 0.9 collective-permute-done.13.refs_2_
  62.6 3.1 %collective-permute-done.12.refs_1_ = bf16[2,192,384]{2,1,0:T(8,128)(2,1)S(1)} collective-permute-done((bf16[2,192,384]{2,1,0:T(8,128)(2,1)S(1)}, bf16[2,192,384]{2,1,0:T(8,128)(2,1)S(1)}, u32[]{:S(2)}, u32[]{:S(2)}) %collective-permute-start.12) | collective-permute-done | bytes 294944 | tf_op jit(solution)/shard_map/ppermute | solution.py:358
  65.7 1.6 %collective-permute-done.16.refs_5_ = bf16[2,192,384]{2,1,0:T(8,128)(2,1)S(1)} collective-permute-done((bf16[2,192,384]{2,1,0:T(8,128)(2,1)S(1)}, bf16[2,192,384]{2,1,0:T(8,128)(2,1)S(1)}, u32[]{:S(2)}, u32[]{:S(2)}) %collective-permute-start.16) | collective-permute-done | bytes 294944 | tf_op jit(solution)/shard_map/ppermute | solution.py:391
  67.2 1.6 %next_memory.1.lhs_ref = bf16[384,3072]{1,0:T(8,128)(2,1)S(1)} custom-call(s32[5]{0:T(128)S(1)} %stack.47.place_ref, bf16[384,3072]{1,0:T(8,128)(2,1)S(1)} %get-tuple-element.65.memory_ref, bf16[2,192,384]{2,1,0:T(8,128)(2,1)S(1)} %pad_maximum_fusion.1.refs_0_, bf16[2,192,384]{2,1,0:T(8,128)(2,1)S(1)} %collective-permute-done.12.refs_1_, ...), custom_call_target="tpu_custom_call" | custom-call | flops 1179648 | bytes 7077888 | tf_op jit(solution)/shard_map/next_memory/pallas_call | solution.py:207
  68.9 2.7 %half_product.4 = (bf16[192,384]{1,0:T(8,128)(2,1)S(1)}, bf16[192,384]{1,0:T(8,128)(2,1)S(1)}, bf16[192,384]{1,0:T(8,128)(2,1)S(1)}, bf16[192,384]{1,0:T(8,128)(2,1)S(1)}) custom-call(s32[5]{0:T(128)S(1)} %stack.47.place_ref, bf16[384,3072]{1,0:T(8,128)(2,1)S(1)} %next_memory.1.lhs_ref, bf16[3072,768]{1,0:T(8,128)(2,1)S(1)} %get-tuple-element.90.resident_ref), custom_call_target="tpu_custom_call" | custom-call | flops 1811939328 | bytes 294912 | tf_op jit(solution)/shard_map/half_product/pallas_call | solution.py:60
  71.5 0.6 collective-permute-start.20
  72.1 1.7 %collective-permute-start.21 = (bf16[192,384]{1,0:T(8,128)(2,1)S(1)}, bf16[192,384]{1,0:T(8,128)(2,1)S(1)}, u32[]{:S(2)}, u32[]{:S(2)}) collective-permute-start(bf16[192,384]{1,0:T(8,128)(2,1)S(1)} %get-tuple-element.96), channel_id=1, source_target_pairs={{0,32},{1,33},{2,34},{3,35},{4,36},{5,37},{6,38},{7,39},{8,40},{9,... | collective-permute-start | bytes 442376 | tf_op jit(solution)/shard_map/ppermute | solution.py:337
  73.8 1.7 %collective-permute-start.22 = (bf16[192,384]{1,0:T(8,128)(2,1)S(1)}, bf16[192,384]{1,0:T(8,128)(2,1)S(1)}, u32[]{:S(2)}, u32[]{:S(2)}) collective-permute-start(bf16[192,384]{1,0:T(8,128)(2,1)S(1)} %get-tuple-element.97), channel_id=1, source_target_pairs={{0,112},{1,113},{2,114},{3,115},{4,116},{5,117},{6,118},{7,119},{8... | collective-permute-start | bytes 442376 | tf_op jit(solution)/shard_map/ppermute | solution.py:337
  75.4 2.4 %collective-permute-start.23 = (bf16[192,384]{1,0:T(8,128)(2,1)S(1)}, bf16[192,384]{1,0:T(8,128)(2,1)S(1)}, u32[]{:S(2)}, u32[]{:S(2)}) collective-permute-start(bf16[192,384]{1,0:T(8,128)(2,1)S(1)} %get-tuple-element.98), channel_id=1, source_target_pairs={{0,96},{1,97},{2,98},{3,99},{4,100},{5,101},{6,102},{7,103},{8,104... | collective-permute-start | bytes 442376 | tf_op jit(solution)/shard_map/ppermute | solution.py:337
  77.8 2.7 %half_product.5 = (bf16[192,384]{1,0:T(8,128)(2,1)S(1)}, bf16[192,384]{1,0:T(8,128)(2,1)S(1)}, bf16[192,384]{1,0:T(8,128)(2,1)S(1)}, bf16[192,384]{1,0:T(8,128)(2,1)S(1)}) custom-call(s32[5]{0:T(128)S(1)} %stack.47.place_ref, bf16[384,3072]{1,0:T(8,128)(2,1)S(1)} %next_memory.1.lhs_ref, bf16[3072,768]{1,0:T(8,128)(2,1)S(1)} %get-tuple-element.100.resident_ref), custom_call_target="tpu_custom_call" | custom-call | flops 1811939328 | bytes 294912 | tf_op jit(solution)/shard_map/half_product/pallas_call | solution.py:60
  80.5 3.6 %collective-permute-start.25 = (bf16[192,384]{1,0:T(8,128)(2,1)S(1)}, bf16[192,384]{1,0:T(8,128)(2,1)S(1)}, u32[]{:S(2)}, u32[]{:S(2)}) collective-permute-start(bf16[192,384]{1,0:T(8,128)(2,1)S(1)} %get-tuple-element.102), channel_id=1, source_target_pairs={{0,64},{1,65},{2,66},{3,67},{4,68},{5,69},{6,70},{7,71},{8,72},{9,... | collective-permute-start | bytes 442376 | tf_op jit(solution)/shard_map/ppermute | solution.py:337
  84.2 1.3 %collective-permute-start.26 = (bf16[192,384]{1,0:T(8,128)(2,1)S(1)}, bf16[192,384]{1,0:T(8,128)(2,1)S(1)}, u32[]{:S(2)}, u32[]{:S(2)}) collective-permute-start(bf16[192,384]{1,0:T(8,128)(2,1)S(1)} %get-tuple-element.103), channel_id=1, source_target_pairs={{0,16},{1,17},{2,18},{3,19},{4,20},{5,21},{6,22},{7,23},{8,24},{9,... | collective-permute-start | bytes 442376 | tf_op jit(solution)/shard_map/ppermute | solution.py:337
  85.5 5.0 %collective-permute-done.23.refs_3_ = bf16[192,384]{1,0:T(8,128)(2,1)S(1)} collective-permute-done((bf16[192,384]{1,0:T(8,128)(2,1)S(1)}, bf16[192,384]{1,0:T(8,128)(2,1)S(1)}, u32[]{:S(2)}, u32[]{:S(2)}) %collective-permute-start.23) | collective-permute-done | bytes 147488 | tf_op jit(solution)/shard_map/ppermute | solution.py:337
  90.9 1.4 %second_solve.1.refs_0_ = bf16[192,384]{1,0:T(8,128)(2,1)S(1)} custom-call(s32[5]{0:T(128)S(1)} %stack.47.place_ref, bf16[192,384]{1,0:T(8,128)(2,1)S(1)} %collective-permute-done.20.refs_0_, bf16[192,384]{1,0:T(8,128)(2,1)S(1)} %collective-permute-done.21.refs_1_, bf16[192,384]{1,0:T(8,128)(2,1)S(1)} %collective-permute-done.22.refs_2_, ...), custom_call_target="tpu_custom_call" | custom-call | flops 339738624 | bytes 1769472 | tf_op jit(solution)/shard_map/second_solve/pallas_call | solution.py:267
  92.3 0.9 collective-permute-start.33
  93.3 0.4 collective-permute-start.32
  93.7 3.7 %collective-permute-start.31 = (bf16[192,384]{1,0:T(8,128)(2,1)S(1)}, bf16[192,384]{1,0:T(8,128)(2,1)S(1)}, u32[]{:S(2)}, u32[]{:S(2)}) collective-permute-start(bf16[192,384]{1,0:T(8,128)(2,1)S(1)} %second_solve.1.refs_0_), channel_id=1, source_target_pairs={{0,80},{1,81},{2,82},{3,83},{4,84},{5,85},{6,86},{7,87},{8,88},{9,... | collective-permute-start | bytes 442376 | tf_op jit(solution)/shard_map/ppermute | solution.py:337
  97.7 2.0 %collective-permute-start.29 = (bf16[192,384]{1,0:T(8,128)(2,1)S(1)}, bf16[192,384]{1,0:T(8,128)(2,1)S(1)}, u32[]{:S(2)}, u32[]{:S(2)}) collective-permute-start(bf16[192,384]{1,0:T(8,128)(2,1)S(1)} %second_solve.1.refs_0_), channel_id=1, source_target_pairs={{0,48},{1,49},{2,50},{3,51},{4,52},{5,53},{6,54},{7,55},{8,56},{9,... | collective-permute-start | bytes 442376 | tf_op jit(solution)/shard_map/ppermute | solution.py:337
  99.7 0.8 collective-permute-done.33.refs_7_
  100.5 0.6 collective-permute-start.28
  101.1 1.5 %collective-permute-done.32.refs_6_ = bf16[192,384]{1,0:T(8,128)(2,1)S(1)} collective-permute-done((bf16[192,384]{1,0:T(8,128)(2,1)S(1)}, bf16[192,384]{1,0:T(8,128)(2,1)S(1)}, u32[]{:S(2)}, u32[]{:S(2)}) %collective-permute-start.32) | collective-permute-done | bytes 147488 | tf_op jit(solution)/shard_map/ppermute | solution.py:337
  102.5 1.2 %collective-permute-start.27 = (bf16[192,384]{1,0:T(8,128)(2,1)S(1)}, bf16[192,384]{1,0:T(8,128)(2,1)S(1)}, u32[]{:S(2)}, u32[]{:S(2)}) collective-permute-start(bf16[192,384]{1,0:T(8,128)(2,1)S(1)} %second_solve.1.refs_0_), channel_id=1, source_target_pairs={{0,16},{1,17},{2,18},{3,19},{4,20},{5,21},{6,22},{7,23},{8,24},{9,... | collective-permute-start | bytes 442376 | tf_op jit(solution)/shard_map/ppermute | solution.py:337
  103.8 1.8 %join_one.1.refs_8_ = bf16[2,384,1536]{2,1,0:T(8,128)(2,1)} custom-call(s32[5]{0:T(128)S(1)} %stack.47.place_ref, bf16[4,192,384]{2,1,0:T(8,128)(2,1)S(1)} %pad_maximum_fusion.own_ref, bf16[4,192,384]{2,1,0:T(8,128)(2,1)S(1)} %collective-permute-done.19.other_ref), custom_call_target="tpu_custom_call" | custom-call | flops 589824 | bytes 2359296 | tf_op jit(solution)/shard_map/join_one/pallas_call | solution.py:315
  105.7 2.2 %collective-permute-done.29.refs_3_ = bf16[192,384]{1,0:T(8,128)(2,1)S(1)} collective-permute-done((bf16[192,384]{1,0:T(8,128)(2,1)S(1)}, bf16[192,384]{1,0:T(8,128)(2,1)S(1)}, u32[]{:S(2)}, u32[]{:S(2)}) %collective-permute-start.29) | collective-permute-done | bytes 147488 | tf_op jit(solution)/shard_map/ppermute | solution.py:337
  107.8 2.4 %collective-permute-done.28.refs_2_ = bf16[192,384]{1,0:T(8,128)(2,1)S(1)} collective-permute-done((bf16[192,384]{1,0:T(8,128)(2,1)S(1)}, bf16[192,384]{1,0:T(8,128)(2,1)S(1)}, u32[]{:S(2)}, u32[]{:S(2)}) %collective-permute-start.28) | collective-permute-done | bytes 147488 | tf_op jit(solution)/shard_map/ppermute | solution.py:337
  110.3 1.8 %join_two.1 = bf16[2,384,1536]{2,1,0:T(8,128)(2,1)} custom-call(s32[5]{0:T(128)S(1)} %stack.47.place_ref, bf16[192,384]{1,0:T(8,128)(2,1)S(1)} %second_solve.1.refs_0_, bf16[192,384]{1,0:T(8,128)(2,1)S(1)} %collective-permute-done.27.refs_1_, bf16[192,384]{1,0:T(8,128)(2,1)S(1)} %collective-permute-done.28.refs_2_, ...), custom_call_target="tpu_custom_call", output_to_operand_aliasing={{}: (9, {})} | custom-call | flops 589824 | bytes 2359296 | tf_op jit(solution)/shard_map/join_two/pallas_call | solution.py:315
  (40 shorter events, 1.2 us)
Async XLA Ops:
  6.6 12.5 %collective-permute-start.1 = (bf16[192,384]{1,0:T(8,128)(2,1)S(1)}, bf16[192,384]{1,0:T(8,128)(2,1)S(1)}, u32[]{:S(2)}, u32[]{:S(2)}) collective-permute-start(bf16[192,384]{1,0:T(8,128)(2,1)S(1)} %get-tuple-element.57), channel_id=1, source_target_pairs={{0,32},{1,33},{2,34},{3,35},{4,36},{5,37},{6,38},{7,39},{8,40},{9,... | collective-permute-start | bytes 442376 | tf_op jit(solution)/shard_map/ppermute | solution.py:337
  8.3 12.4 %collective-permute-start = (bf16[192,384]{1,0:T(8,128)(2,1)S(1)}, bf16[192,384]{1,0:T(8,128)(2,1)S(1)}, u32[]{:S(2)}, u32[]{:S(2)}) collective-permute-start(bf16[192,384]{1,0:T(8,128)(2,1)S(1)} %get-tuple-element.58), channel_id=1, source_target_pairs={{0,48},{1,49},{2,50},{3,51},{4,52},{5,53},{6,54},{7,55},{8,56},{9,... | collective-permute-start | bytes 442376 | tf_op jit(solution)/shard_map/ppermute | solution.py:337
  10.1 11.1 %collective-permute-start.3 = (bf16[192,384]{1,0:T(8,128)(2,1)S(1)}, bf16[192,384]{1,0:T(8,128)(2,1)S(1)}, u32[]{:S(2)}, u32[]{:S(2)}) collective-permute-start(bf16[192,384]{1,0:T(8,128)(2,1)S(1)} %get-tuple-element.59), channel_id=1, source_target_pairs={{0,96},{1,97},{2,98},{3,99},{4,100},{5,101},{6,102},{7,103},{8,104... | collective-permute-start | bytes 442376 | tf_op jit(solution)/shard_map/ppermute | solution.py:337
  13.2 13.6 %collective-permute-start.2 = (bf16[192,384]{1,0:T(8,128)(2,1)S(1)}, bf16[192,384]{1,0:T(8,128)(2,1)S(1)}, u32[]{:S(2)}, u32[]{:S(2)}) collective-permute-start(bf16[192,384]{1,0:T(8,128)(2,1)S(1)} %get-tuple-element.60), channel_id=1, source_target_pairs={{0,112},{1,113},{2,114},{3,115},{4,116},{5,117},{6,118},{7,119},{8... | collective-permute-start | bytes 442376 | tf_op jit(solution)/shard_map/ppermute | solution.py:337
  13.2 5.9 %copy-start.1 = (f32[32,32]{1,0:T(8,128)S(1)}, f32[32,32]{1,0:T(8,128)}, u32[]{:S(2)}) copy-start(f32[32,32]{1,0:T(8,128)} %param.9) | copy-start | bytes 12292
  13.2 8.0 %copy-start = (f32[2,384,384]{2,1,0:T(8,128)S(1)}, f32[2,384,384]{2,1,0:T(8,128)}, u32[]{:S(2)}) copy-start(f32[2,384,384]{2,1,0:T(8,128)} %param.8) | copy-start | bytes 3538948
  15.8 16.1 %collective-permute-start.4 = (bf16[192,384]{1,0:T(8,128)(2,1)S(1)}, bf16[192,384]{1,0:T(8,128)(2,1)S(1)}, u32[]{:S(2)}, u32[]{:S(2)}) collective-permute-start(bf16[192,384]{1,0:T(8,128)(2,1)S(1)} %get-tuple-element.70), channel_id=1, source_target_pairs={{0,80},{1,81},{2,82},{3,83},{4,84},{5,85},{6,86},{7,87},{8,88},{9,... | collective-permute-start | bytes 442376 | tf_op jit(solution)/shard_map/ppermute | solution.py:337
  19.1 12.8 %collective-permute-start.5 = (bf16[192,384]{1,0:T(8,128)(2,1)S(1)}, bf16[192,384]{1,0:T(8,128)(2,1)S(1)}, u32[]{:S(2)}, u32[]{:S(2)}) collective-permute-start(bf16[192,384]{1,0:T(8,128)(2,1)S(1)} %get-tuple-element.71), channel_id=1, source_target_pairs={{0,64},{1,65},{2,66},{3,67},{4,68},{5,69},{6,70},{7,71},{8,72},{9,... | collective-permute-start | bytes 442376 | tf_op jit(solution)/shard_map/ppermute | solution.py:337
  20.8 11.2 %collective-permute-start.6 = (bf16[192,384]{1,0:T(8,128)(2,1)S(1)}, bf16[192,384]{1,0:T(8,128)(2,1)S(1)}, u32[]{:S(2)}, u32[]{:S(2)}) collective-permute-start(bf16[192,384]{1,0:T(8,128)(2,1)S(1)} %get-tuple-element.72), channel_id=1, source_target_pairs={{0,16},{1,17},{2,18},{3,19},{4,20},{5,21},{6,22},{7,23},{8,24},{9,... | collective-permute-start | bytes 442376 | tf_op jit(solution)/shard_map/ppermute | solution.py:337
  33.8 11.4 %collective-permute-start.8 = (bf16[192,384]{1,0:T(8,128)(2,1)S(1)}, bf16[192,384]{1,0:T(8,128)(2,1)S(1)}, u32[]{:S(2)}, u32[]{:S(2)}) collective-permute-start(bf16[192,384]{1,0:T(8,128)(2,1)S(1)} %get-tuple-element.74), channel_id=1, source_target_pairs={{0,10},{1,11},{2,26},{3,27},{4,46},{5,47},{6,62},{7,63},{8,66},{9,... | collective-permute-start | bytes 442376 | tf_op jit(solution)/shard_map/ppermute | solution.py:337
  39.9 5.3 %collective-permute-start.7 = (bf16[192,384]{1,0:T(8,128)(2,1)S(1)}, bf16[192,384]{1,0:T(8,128)(2,1)S(1)}, u32[]{:S(2)}, u32[]{:S(2)}) collective-permute-start(bf16[192,384]{1,0:T(8,128)(2,1)S(1)} %get-tuple-element.74), channel_id=1, source_target_pairs={{0,0},{1,1},{2,16},{3,17},{4,36},{5,37},{6,52},{7,53},{8,72},{9,73... | collective-permute-start | bytes 442376 | tf_op jit(solution)/shard_map/ppermute | solution.py:337
  40.5 6.7 %collective-permute-start.11 = (bf16[192,384]{1,0:T(8,128)(2,1)S(1)}, bf16[192,384]{1,0:T(8,128)(2,1)S(1)}, u32[]{:S(2)}, u32[]{:S(2)}) collective-permute-start(bf16[192,384]{1,0:T(8,128)(2,1)S(1)} %get-tuple-element.78), channel_id=1, source_target_pairs={{0,96},{32,0},{64,32},{96,64},{1,97},{33,1},{65,33},{97,65},{2,98}... | collective-permute-start | bytes 442376 | tf_op jit(solution)/shard_map/ppermute | solution.py:358
  43.0 6.6 %collective-permute-start.10 = (bf16[192,384]{1,0:T(8,128)(2,1)S(1)}, bf16[192,384]{1,0:T(8,128)(2,1)S(1)}, u32[]{:S(2)}, u32[]{:S(2)}) collective-permute-start(bf16[192,384]{1,0:T(8,128)(2,1)S(1)} %get-tuple-element.78), channel_id=1, source_target_pairs={{0,64},{32,96},{64,0},{96,32},{1,65},{33,97},{65,1},{97,33},{2,66}... | collective-permute-start | bytes 442376 | tf_op jit(solution)/shard_map/ppermute | solution.py:358
  45.1 6.4 %collective-permute-start.9 = (bf16[192,384]{1,0:T(8,128)(2,1)S(1)}, bf16[192,384]{1,0:T(8,128)(2,1)S(1)}, u32[]{:S(2)}, u32[]{:S(2)}) collective-permute-start(bf16[192,384]{1,0:T(8,128)(2,1)S(1)} %get-tuple-element.78), channel_id=1, source_target_pairs={{0,32},{32,64},{64,96},{96,0},{1,33},{33,65},{65,97},{97,1},{2,34}... | collective-permute-start | bytes 442376 | tf_op jit(solution)/shard_map/ppermute | solution.py:358
  51.5 10.2 %collective-permute-start.14 = (bf16[2,192,384]{2,1,0:T(8,128)(2,1)S(1)}, bf16[2,192,384]{2,1,0:T(8,128)(2,1)S(1)}, u32[]{:S(2)}, u32[]{:S(2)}) collective-permute-start(bf16[2,192,384]{2,1,0:T(8,128)(2,1)S(1)} %pad_maximum_fusion.1.refs_0_), channel_id=1, source_target_pairs={{0,12},{4,0},{8,4},{12,8},{1,13},{5,1},{9,5},{13,9},{2,14},{6,2},{... | collective-permute-start | bytes 884744 | tf_op jit(solution)/shard_map/ppermute | solution.py:358
  54.3 8.3 %collective-permute-start.13 = (bf16[2,192,384]{2,1,0:T(8,128)(2,1)S(1)}, bf16[2,192,384]{2,1,0:T(8,128)(2,1)S(1)}, u32[]{:S(2)}, u32[]{:S(2)}) collective-permute-start(bf16[2,192,384]{2,1,0:T(8,128)(2,1)S(1)} %pad_maximum_fusion.1.refs_0_), channel_id=1, source_target_pairs={{0,8},{4,12},{8,0},{12,4},{1,9},{5,13},{9,1},{13,5},{2,10},{6,14},... | collective-permute-start | bytes 884744 | tf_op jit(solution)/shard_map/ppermute | solution.py:358
  55.7 10.0 %collective-permute-start.12 = (bf16[2,192,384]{2,1,0:T(8,128)(2,1)S(1)}, bf16[2,192,384]{2,1,0:T(8,128)(2,1)S(1)}, u32[]{:S(2)}, u32[]{:S(2)}) collective-permute-start(bf16[2,192,384]{2,1,0:T(8,128)(2,1)S(1)} %pad_maximum_fusion.1.refs_0_), channel_id=1, source_target_pairs={{0,4},{4,8},{8,12},{12,0},{1,5},{5,9},{9,13},{13,1},{2,6},{6,10},{... | collective-permute-start | bytes 884744 | tf_op jit(solution)/shard_map/ppermute | solution.py:358
  55.8 11.5 %collective-permute-start.19 = (bf16[4,192,384]{2,1,0:T(8,128)(2,1)S(1)}, bf16[4,192,384]{2,1,0:T(8,128)(2,1)S(1)}, u32[]{:S(2)}, u32[]{:S(2)}) collective-permute-start(bf16[4,192,384]{2,1,0:T(8,128)(2,1)S(1)} %pad_maximum_fusion.own_ref), channel_id=1, source_target_pairs={{0,16},{16,0},{1,17},{17,1},{2,18},{18,2},{3,19},{19,3},{4,20},{20... | collective-permute-start | bytes 1769480 | tf_op jit(solution)/shard_map/ppermute | solution.py:390
  56.6 9.0 %collective-permute-start.15 = (bf16[2,192,384]{2,1,0:T(8,128)(2,1)S(1)}, bf16[2,192,384]{2,1,0:T(8,128)(2,1)S(1)}, u32[]{:S(2)}, u32[]{:S(2)}) collective-permute-start(bf16[2,192,384]{2,1,0:T(8,128)(2,1)S(1)} %pad_maximum_fusion.1.refs_0_), channel_id=1, source_target_pairs={{0,1},{1,0},{2,3},{3,2},{4,5},{5,4},{6,7},{7,6},{8,9},{9,8},{10,11... | collective-permute-start | bytes 884744 | tf_op jit(solution)/shard_map/ppermute | solution.py:391
  61.7 4.0 %collective-permute-start.18 = (bf16[2,192,384]{2,1,0:T(8,128)(2,1)S(1)}, bf16[2,192,384]{2,1,0:T(8,128)(2,1)S(1)}, u32[]{:S(2)}, u32[]{:S(2)}) collective-permute-start(bf16[2,192,384]{2,1,0:T(8,128)(2,1)S(1)} %collective-permute-done.14.refs_3_), channel_id=1, source_target_pairs={{0,1},{1,0},{2,3},{3,2},{4,5},{5,4},{6,7},{7,6},{8,9},{9,8},{10,11... | collective-permute-start | bytes 884744 | tf_op jit(solution)/shard_map/ppermute | solution.py:391
  62.6 3.1 %collective-permute-start.17 = (bf16[2,192,384]{2,1,0:T(8,128)(2,1)S(1)}, bf16[2,192,384]{2,1,0:T(8,128)(2,1)S(1)}, u32[]{:S(2)}, u32[]{:S(2)}) collective-permute-start(bf16[2,192,384]{2,1,0:T(8,128)(2,1)S(1)} %collective-permute-done.13.refs_2_), channel_id=1, source_target_pairs={{0,1},{1,0},{2,3},{3,2},{4,5},{5,4},{6,7},{7,6},{8,9},{9,8},{10,11... | collective-permute-start | bytes 884744 | tf_op jit(solution)/shard_map/ppermute | solution.py:391
  65.6 1.6 %collective-permute-start.16 = (bf16[2,192,384]{2,1,0:T(8,128)(2,1)S(1)}, bf16[2,192,384]{2,1,0:T(8,128)(2,1)S(1)}, u32[]{:S(2)}, u32[]{:S(2)}) collective-permute-start(bf16[2,192,384]{2,1,0:T(8,128)(2,1)S(1)} %collective-permute-done.12.refs_1_), channel_id=1, source_target_pairs={{0,1},{1,0},{2,3},{3,2},{4,5},{5,4},{6,7},{7,6},{8,9},{9,8},{10,11... | collective-permute-start | bytes 884744 | tf_op jit(solution)/shard_map/ppermute | solution.py:391
  71.5 9.0 %collective-permute-start.20 = (bf16[192,384]{1,0:T(8,128)(2,1)S(1)}, bf16[192,384]{1,0:T(8,128)(2,1)S(1)}, u32[]{:S(2)}, u32[]{:S(2)}) collective-permute-start(bf16[192,384]{1,0:T(8,128)(2,1)S(1)} %get-tuple-element.95), channel_id=1, source_target_pairs={{0,48},{1,49},{2,50},{3,51},{4,52},{5,53},{6,54},{7,55},{8,56},{9,... | collective-permute-start | bytes 442376 | tf_op jit(solution)/shard_map/ppermute | solution.py:337
  72.1 12.1 %collective-permute-start.21 = (bf16[192,384]{1,0:T(8,128)(2,1)S(1)}, bf16[192,384]{1,0:T(8,128)(2,1)S(1)}, u32[]{:S(2)}, u32[]{:S(2)}) collective-permute-start(bf16[192,384]{1,0:T(8,128)(2,1)S(1)} %get-tuple-element.96), channel_id=1, source_target_pairs={{0,32},{1,33},{2,34},{3,35},{4,36},{5,37},{6,38},{7,39},{8,40},{9,... | collective-permute-start | bytes 442376 | tf_op jit(solution)/shard_map/ppermute | solution.py:337
  73.8 11.8 %collective-permute-start.22 = (bf16[192,384]{1,0:T(8,128)(2,1)S(1)}, bf16[192,384]{1,0:T(8,128)(2,1)S(1)}, u32[]{:S(2)}, u32[]{:S(2)}) collective-permute-start(bf16[192,384]{1,0:T(8,128)(2,1)S(1)} %get-tuple-element.97), channel_id=1, source_target_pairs={{0,112},{1,113},{2,114},{3,115},{4,116},{5,117},{6,118},{7,119},{8... | collective-permute-start | bytes 442376 | tf_op jit(solution)/shard_map/ppermute | solution.py:337
  75.4 15.1 %collective-permute-start.23 = (bf16[192,384]{1,0:T(8,128)(2,1)S(1)}, bf16[192,384]{1,0:T(8,128)(2,1)S(1)}, u32[]{:S(2)}, u32[]{:S(2)}) collective-permute-start(bf16[192,384]{1,0:T(8,128)(2,1)S(1)} %get-tuple-element.98), channel_id=1, source_target_pairs={{0,96},{1,97},{2,98},{3,99},{4,100},{5,101},{6,102},{7,103},{8,104... | collective-permute-start | bytes 442376 | tf_op jit(solution)/shard_map/ppermute | solution.py:337
  80.4 10.1 %collective-permute-start.24 = (bf16[192,384]{1,0:T(8,128)(2,1)S(1)}, bf16[192,384]{1,0:T(8,128)(2,1)S(1)}, u32[]{:S(2)}, u32[]{:S(2)}) collective-permute-start(bf16[192,384]{1,0:T(8,128)(2,1)S(1)} %get-tuple-element.101), channel_id=1, source_target_pairs={{0,80},{1,81},{2,82},{3,83},{4,84},{5,85},{6,86},{7,87},{8,88},{9,... | collective-permute-start | bytes 442376 | tf_op jit(solution)/shard_map/ppermute | solution.py:337
  80.5 10.0 %collective-permute-start.25 = (bf16[192,384]{1,0:T(8,128)(2,1)S(1)}, bf16[192,384]{1,0:T(8,128)(2,1)S(1)}, u32[]{:S(2)}, u32[]{:S(2)}) collective-permute-start(bf16[192,384]{1,0:T(8,128)(2,1)S(1)} %get-tuple-element.102), channel_id=1, source_target_pairs={{0,64},{1,65},{2,66},{3,67},{4,68},{5,69},{6,70},{7,71},{8,72},{9,... | collective-permute-start | bytes 442376 | tf_op jit(solution)/shard_map/ppermute | solution.py:337
  84.2 6.7 %collective-permute-start.26 = (bf16[192,384]{1,0:T(8,128)(2,1)S(1)}, bf16[192,384]{1,0:T(8,128)(2,1)S(1)}, u32[]{:S(2)}, u32[]{:S(2)}) collective-permute-start(bf16[192,384]{1,0:T(8,128)(2,1)S(1)} %get-tuple-element.103), channel_id=1, source_target_pairs={{0,16},{1,17},{2,18},{3,19},{4,20},{5,21},{6,22},{7,23},{8,24},{9,... | collective-permute-start | bytes 442376 | tf_op jit(solution)/shard_map/ppermute | solution.py:337
  92.3 8.2 %collective-permute-start.33 = (bf16[192,384]{1,0:T(8,128)(2,1)S(1)}, bf16[192,384]{1,0:T(8,128)(2,1)S(1)}, u32[]{:S(2)}, u32[]{:S(2)}) collective-permute-start(bf16[192,384]{1,0:T(8,128)(2,1)S(1)} %second_solve.1.refs_0_), channel_id=1, source_target_pairs={{0,112},{1,113},{2,114},{3,115},{4,116},{5,117},{6,118},{7,119},{8... | collective-permute-start | bytes 442376 | tf_op jit(solution)/shard_map/ppermute | solution.py:337
  93.3 9.3 %collective-permute-start.32 = (bf16[192,384]{1,0:T(8,128)(2,1)S(1)}, bf16[192,384]{1,0:T(8,128)(2,1)S(1)}, u32[]{:S(2)}, u32[]{:S(2)}) collective-permute-start(bf16[192,384]{1,0:T(8,128)(2,1)S(1)} %second_solve.1.refs_0_), channel_id=1, source_target_pairs={{0,96},{1,97},{2,98},{3,99},{4,100},{5,101},{6,102},{7,103},{8,104... | collective-permute-start | bytes 442376 | tf_op jit(solution)/shard_map/ppermute | solution.py:337
  93.7 11.9 %collective-permute-start.31 = (bf16[192,384]{1,0:T(8,128)(2,1)S(1)}, bf16[192,384]{1,0:T(8,128)(2,1)S(1)}, u32[]{:S(2)}, u32[]{:S(2)}) collective-permute-start(bf16[192,384]{1,0:T(8,128)(2,1)S(1)} %second_solve.1.refs_0_), channel_id=1, source_target_pairs={{0,80},{1,81},{2,82},{3,83},{4,84},{5,85},{6,86},{7,87},{8,88},{9,... | collective-permute-start | bytes 442376 | tf_op jit(solution)/shard_map/ppermute | solution.py:337
  97.4 8.3 %collective-permute-start.30 = (bf16[192,384]{1,0:T(8,128)(2,1)S(1)}, bf16[192,384]{1,0:T(8,128)(2,1)S(1)}, u32[]{:S(2)}, u32[]{:S(2)}) collective-permute-start(bf16[192,384]{1,0:T(8,128)(2,1)S(1)} %second_solve.1.refs_0_), channel_id=1, source_target_pairs={{0,64},{1,65},{2,66},{3,67},{4,68},{5,69},{6,70},{7,71},{8,72},{9,... | collective-permute-start | bytes 442376 | tf_op jit(solution)/shard_map/ppermute | solution.py:337
  97.7 10.2 %collective-permute-start.29 = (bf16[192,384]{1,0:T(8,128)(2,1)S(1)}, bf16[192,384]{1,0:T(8,128)(2,1)S(1)}, u32[]{:S(2)}, u32[]{:S(2)}) collective-permute-start(bf16[192,384]{1,0:T(8,128)(2,1)S(1)} %second_solve.1.refs_0_), channel_id=1, source_target_pairs={{0,48},{1,49},{2,50},{3,51},{4,52},{5,53},{6,54},{7,55},{8,56},{9,... | collective-permute-start | bytes 442376 | tf_op jit(solution)/shard_map/ppermute | solution.py:337
  100.5 9.8 %collective-permute-start.28 = (bf16[192,384]{1,0:T(8,128)(2,1)S(1)}, bf16[192,384]{1,0:T(8,128)(2,1)S(1)}, u32[]{:S(2)}, u32[]{:S(2)}) collective-permute-start(bf16[192,384]{1,0:T(8,128)(2,1)S(1)} %second_solve.1.refs_0_), channel_id=1, source_target_pairs={{0,32},{1,33},{2,34},{3,35},{4,36},{5,37},{6,38},{7,39},{8,40},{9,... | collective-permute-start | bytes 442376 | tf_op jit(solution)/shard_map/ppermute | solution.py:337
  102.5 7.7 %collective-permute-start.27 = (bf16[192,384]{1,0:T(8,128)(2,1)S(1)}, bf16[192,384]{1,0:T(8,128)(2,1)S(1)}, u32[]{:S(2)}, u32[]{:S(2)}) collective-permute-start(bf16[192,384]{1,0:T(8,128)(2,1)S(1)} %second_solve.1.refs_0_), channel_id=1, source_target_pairs={{0,16},{1,17},{2,18},{3,19},{4,20},{5,21},{6,22},{7,23},{8,24},{9,... | collective-permute-start | bytes 442376 | tf_op jit(solution)/shard_map/ppermute | solution.py:337

commit v9 on v8

v9 whole, which is shorter than its diff:
```python
import functools

import jax
import jax.numpy as jnp
from jax import lax
from jax.experimental import pallas as pl
from jax.experimental.pallas import tpu as pltpu
from jax.sharding import Mesh, PartitionSpec as P

step_size = 0.5
ORB = 32
f32 = jnp.float32
bf16 = jnp.bfloat16
PASTS = ("y", "zl")
SECONDS = ("x", "zh", "c")
ALL = PASTS + SECONDS
SWAP = [(0, 1), (1, 0)]
X, ZH, C, Y, ZL = range(5)


VMEM = pl.BlockSpec(memory_space=pltpu.VMEM)
SMEM = pl.BlockSpec(memory_space=pltpu.SMEM)
HBM = pl.BlockSpec(memory_space=pltpu.HBM)


def in_hbm(array):
    return pltpu.with_memory_space_constraint(array, pltpu.HBM)


def params(megabytes):
    return pltpu.CompilerParams(vmem_limit_bytes=megabytes << 20)


def cost(flops, nbytes):
    return pl.CostEstimate(flops=flops, bytes_accessed=nbytes, transcendentals=0)


def position(y):
    return (y & 1) * 2 + (y >> 1)


def store_shares(place_ref, turned_ref, out_refs):
    width = out_refs[0].shape[0]
    for k, out_ref in enumerate(out_refs):
        share = ((place_ref[Y] >> 1) ^ (k >> 1)) * 2 + (place_ref[ZL] ^ (k & 1))
        out_ref[...] = turned_ref[pl.ds(pl.multiple_of(share * width, width), width), :]


TILES = 3


def tiled_product(start, lhs_ref, resident_ref, tile_ref, turned_ref, sems, before):
    tile = tile_ref.shape[1] // TILES
    copies = []
    for i in range(TILES):
        at = pl.ds(pl.multiple_of(start + i * tile, tile), tile)
        to = tile_ref.at[:, i * tile : (i + 1) * tile]
        copies.append(pltpu.make_async_copy(resident_ref.at[:, at], to, sems.at[i]))
    for copy in (*before, *copies):
        copy.start()
    for copy in before:
        copy.wait()
    for i, copy in enumerate(copies):
        copy.wait()
        at = slice(i * tile, (i + 1) * tile)
        product = jnp.dot(lhs_ref[...], tile_ref[:, at], preferred_element_type=f32)
        turned_ref[at, :] = product.T.astype(bf16)


def odd_product_kernel(place_ref, memory_ref, resident_ref, *refs):
    out_refs, (lhs_ref, tile_ref, turned_ref, sems) = refs[:4], refs[4:]
    start = ((place_ref[Y] & 1) ^ 1) * tile_ref.shape[1]
    copy = pltpu.make_async_copy(memory_ref.at[0], lhs_ref, sems.at[TILES])
    tiled_product(start, lhs_ref, resident_ref, tile_ref, turned_ref, sems, [copy])
    store_shares(place_ref, turned_ref, out_refs)


def even_product_kernel(place_ref, lhs_ref, resident_ref, *refs):
    out_refs, (tile_ref, turned_ref, sems) = refs[:4], refs[4:]
    start = (place_ref[Y] & 1) * tile_ref.shape[1]
    tiled_product(start, lhs_ref, resident_ref, tile_ref, turned_ref, sems, [])
    store_shares(place_ref, turned_ref, out_refs)


def first_product(kernel, place, left, resident, lhs_shape, name):
    depth, cols = resident.shape
    rows, half = left.shape[-2], cols // 2
    shapes = [(half // 4, rows)] * 4 + lhs_shape
    return pl.pallas_call(
        kernel,
        in_specs=[SMEM, HBM if lhs_shape else VMEM, HBM],
        out_specs=[VMEM] * len(shapes),
        out_shape=[jax.ShapeDtypeStruct(shape, bf16) for shape in shapes],
        scratch_shapes=[
            pltpu.VMEM((depth, half), bf16),
            pltpu.VMEM((half, rows), bf16),
            pltpu.SemaphoreType.DMA((TILES + 1,)),
        ],
        compiler_params=params(12),
        cost_estimate=cost(2 * rows * depth * half, 2 * depth * half),
        name=name,
    )(place, left, resident)


def depth_half(place_ref, side, resident_ref):
    half = resident_ref.shape[0] // 2
    return pl.ds(pl.multiple_of((place_ref[C] ^ side) * half, half), half)


def early_product_kernel(place_ref, lhs_ref, resident_ref, out_ref):
    right = resident_ref[depth_half(place_ref, 0, resident_ref), :]
    out_ref[...] = jnp.dot(lhs_ref[...], right, preferred_element_type=f32)


def early_product(place, lhs, resident):
    rows, depth = lhs.shape
    cols = resident.shape[1]
    return pl.pallas_call(
        early_product_kernel,
        in_specs=[SMEM, VMEM, VMEM],
        out_specs=VMEM,
        out_shape=jax.ShapeDtypeStruct((rows, cols), f32),
        compiler_params=params(6),
        cost_estimate=cost(2 * rows * depth * cols, 4 * rows * cols),
        name="early_product",
    )(place, lhs, resident)


def late_product_kernel(place_ref, early_ref, lhs_ref, resident_ref, *refs):
    out_refs, turned_ref = refs[:4], refs[4]
    right = resident_ref[depth_half(place_ref, 1, resident_ref), :]
    product = early_ref[...] + jnp.dot(lhs_ref[...], right, preferred_element_type=f32)
    turned_ref[...] = product.T.astype(bf16)
    store_shares(place_ref, turned_ref, out_refs)


def both_product_kernel(place_ref, own_ref, other_ref, resident_ref, *refs):
    out_refs, turned_ref = refs[:4], refs[4]
    product = None
    for side, lhs_ref in enumerate((own_ref, other_ref)):
        right = resident_ref[depth_half(place_ref, side, resident_ref), :]
        term = jnp.dot(lhs_ref[...], right, preferred_element_type=f32)
        product = term if product is None else product + term
    turned_ref[...] = product.T.astype(bf16)
    store_shares(place_ref, turned_ref, out_refs)


def second_product(kernel, place, left, lhs, resident, name):
    rows, depth = lhs.shape
    cols = resident.shape[1]
    return pl.pallas_call(
        kernel,
        in_specs=[SMEM] + [VMEM] * 3,
        out_specs=[VMEM] * 4,
        out_shape=[jax.ShapeDtypeStruct((cols // 4, rows), bf16)] * 4,
        scratch_shapes=[pltpu.VMEM((cols, rows), bf16)],
        compiler_params=params(6),
        cost_estimate=cost(2 * rows * depth * cols, 4 * cols * rows),
        name=name,
    )(place, left, lhs, resident)


def half_copy(side, place_ref, resident_ref, out_ref, sem):
    half = out_ref.shape[1]
    at = pl.ds(pl.multiple_of(((place_ref[Y] & 1) ^ side) * half, half), half)
    return pltpu.make_async_copy(resident_ref.at[:, at], out_ref, sem)


def bring_odd_kernel(
    place_ref, memory_ref, previous_ref, resident_ref, memory_out, one_out, two_out, odd_out, prior_ref, turned_ref, sems
):
    width, rows = one_out.shape
    start = position(place_ref[Y]) * 2 * width
    cols = pl.ds(pl.multiple_of(start, 128), 2 * width)
    copies = [
        pltpu.make_async_copy(previous_ref.at[:, :, cols], prior_ref, sems.at[0]),
        pltpu.make_async_copy(memory_ref.at[1], memory_out, sems.at[1]),
        half_copy(1, place_ref, resident_ref, odd_out, sems.at[2]),
    ]
    for copy in copies:
        copy.start()
    copies[0].wait()
    for front, out_ref in enumerate((one_out, two_out)):
        turned_ref[...] = prior_ref[front].astype(f32).T
        share = turned_ref[pl.ds(pl.multiple_of(place_ref[ZL] * width, width), width), :]
        out_ref[...] = share.astype(bf16)
    for copy in copies[1:]:
        copy.wait()


def bring_odd(place, memory, previous, resident):
    _, rows, depth = memory.shape
    cols = resident.shape[1]
    width = previous.shape[2] // 8
    shapes = [(rows, depth), (width, rows), (width, rows), (depth, cols // 2)]
    return pl.pallas_call(
        bring_odd_kernel,
        in_specs=[SMEM] + [HBM] * 3,
        out_specs=[VMEM] * 4,
        out_shape=[jax.ShapeDtypeStruct(shape, bf16) for shape in shapes],
        scratch_shapes=[
            pltpu.VMEM((2, rows, 2 * width), bf16),
            pltpu.VMEM((2 * width, rows), f32),
            pltpu.SemaphoreType.DMA((3,)),
        ],
        compiler_params=params(6),
        cost_estimate=cost(0, depth * (2 * rows + cols)),
        name="bring_odd",
    )(place, memory, previous, resident)


def bring_even_kernel(place_ref, resident_ref, even_out, sem):
    copy = half_copy(0, place_ref, resident_ref, even_out, sem)
    copy.start()
    copy.wait()


def bring_even(place, resident):
    depth, cols = resident.shape
    return pl.pallas_call(
        bring_even_kernel,
        in_specs=[SMEM, HBM],
        out_specs=VMEM,
        out_shape=jax.ShapeDtypeStruct((depth, cols // 2), bf16),
        scratch_shapes=[pltpu.SemaphoreType.DMA],
        compiler_params=params(4),
        cost_estimate=cost(0, depth * cols),
        name="bring_even",
    )(place, resident)


def place_pair(own, other, first, out_ref):
    near, far = own.astype(f32), other.astype(f32)
    low = jnp.where(first == 0, near, far)
    high = jnp.where(first == 0, far, near)
    out_ref[...] = jnp.concatenate([low, high], axis=0).T.astype(bf16)


def next_memory_kernel(side, place_ref, memory_ref, *refs):
    pair_refs, out_ref = refs[:4], refs[4]
    half = out_ref.shape[1]
    width = half // 4
    for dx in range(4):
        near, far = pair_refs[dx][0].astype(f32), pair_refs[dx ^ 2][1].astype(f32)
        start = position(((place_ref[X] - dx) & 3) ^ place_ref[Y]) * width
        low = jnp.where(place_ref[ZH] == 0, near, far)
        high = jnp.where(place_ref[ZH] == 0, far, near)
        pair = jnp.concatenate([low, high], axis=0).T
        at = pl.ds(pl.multiple_of((place_ref[C] ^ side) * half + start, 128), width)
        to = pl.ds(pl.multiple_of(start, 128), width)
        out_ref[:, to] = (memory_ref[:, at].astype(f32) + pair).astype(bf16)


def next_memory(side, place, memory, pairs):
    rows, depth = memory.shape
    return pl.pallas_call(
        functools.partial(next_memory_kernel, side),
        in_specs=[SMEM] + [VMEM] * 5,
        out_specs=VMEM,
        out_shape=jax.ShapeDtypeStruct((rows, depth // 2), bf16),
        compiler_params=params(6),
        cost_estimate=cost(rows * depth, 3 * rows * depth),
        name="next_memory",
    )(place, memory, *pairs)


def solve_into(part_refs, prior_ref, inverse_ref):
    summed = part_refs[0][...].astype(f32)
    for part_ref in part_refs[1:]:
        summed = summed + part_ref[...].astype(f32)
    source = prior_ref[...].astype(f32) - step_size * summed
    mixed = lax.dot_general(
        source,
        inverse_ref[...],
        (((1,), (1,)), ((), ())),
        precision=lax.Precision.HIGHEST,
        preferred_element_type=f32,
    )
    return (source + mixed).astype(bf16)


def flipped(values):
    rows, cols = values.shape
    strips = []
    pad = jnp.zeros((128 - ORB, 128), f32)
    for s in range(rows // ORB):
        pieces = []
        for q in range(cols // 128):
            block = values[s * ORB : (s + 1) * ORB, q * 128 : (q + 1) * 128]
            turned = jnp.concatenate([block, pad], axis=0).T
            piece = turned[:ORB]
            for t in range(1, 128 // ORB):
                piece = piece + pltpu.roll(turned[t * ORB : (t + 1) * ORB], t * ORB, 1)
            pieces.append(piece)
        strips.append(jnp.concatenate(pieces, axis=1))
    return jnp.concatenate(strips, axis=0)


def first_solve_kernel(place_ref, *refs):
    front_ref, energy_ref = refs[11:]
    front = solve_into(refs[:8], refs[8], refs[9])
    front_ref[...] = front
    values = front.astype(f32)
    mirror = flipped(values)
    rows, cols = values.shape
    coupling = jnp.tile(refs[10][...], (rows // ORB, cols // 128))
    energy_ref[...] = (mirror * mirror * values * coupling).astype(bf16)


def second_solve_kernel(place_ref, *refs):
    refs[10][...] = solve_into(refs[:8], refs[8], refs[9])


def solve(kernel, place, parts, prior, inverse, extra, outputs, name):
    width, rows = prior.shape
    return pl.pallas_call(
        kernel,
        in_specs=[SMEM] + [VMEM] * (len(parts) + 2 + len(extra)),
        out_specs=[VMEM] * outputs,
        out_shape=[jax.ShapeDtypeStruct((width, rows), bf16)] * outputs,
        compiler_params=params(8),
        cost_estimate=cost(12 * rows * rows * width, 24 * rows * width),
        name=name,
    )(place, *parts, prior, inverse, *extra)


def put_blocks(blocks, block_ref, sems, out_ref, front):
    width = block_ref.shape[2]
    copies = []
    for i, (start, write) in enumerate(blocks):
        write(block_ref.at[i])
        at = pl.ds(pl.multiple_of(start, 128), width)
        copies.append(pltpu.make_async_copy(block_ref.at[i], out_ref.at[front, :, at], sems.at[i]))
        copies[i].start()
    for copy in copies:
        copy.wait()


def join_one_kernel(place_ref, own_ref, other_ref, out_ref, block_ref, sems):
    def block(dy):
        def write(ref):
            place_pair(own_ref[dy], other_ref[dy], place_ref[ZL], ref)

        return position((place_ref[Y] - dy) & 3) * block_ref.shape[2], write

    put_blocks([block(dy) for dy in range(4)], block_ref, sems, out_ref, 0)


def join_two_kernel(moves, place_ref, *refs):
    chunk_refs, (out_ref, block_ref, sems) = refs[:4], refs[5:]

    def block(i):
        def write(ref):
            own, other = chunk_refs[2 * i][...], chunk_refs[2 * i + 1][...]
            place_pair(own, other, place_ref[ZL], ref)

        return position((place_ref[Y] - moves[i]) & 3) * block_ref.shape[2], write

    put_blocks([block(i) for i in range(2)], block_ref, sems, out_ref, 1)


def join(kernel, args, in_specs, shape, aliases, name):
    _, rows, cols = shape
    return pl.pallas_call(
        kernel,
        in_specs=in_specs,
        out_specs=HBM,
        out_shape=jax.ShapeDtypeStruct(shape, bf16),
        scratch_shapes=[pltpu.VMEM((4, rows, cols // 4), bf16), pltpu.SemaphoreType.DMA((4,))],
        input_output_aliases=aliases,
        compiler_params=params(6),
        cost_estimate=cost(rows * cols, 4 * rows * cols),
        name=name,
    )(*args)


def move(value, target):
    pairs = []
    for i in range(128):
        rest, c = divmod(i, 2)
        rest, zh = divmod(rest, 2)
        rest, x = divmod(rest, 4)
        y, zl = divmod(rest, 2)
        y, zl, x, zh = target(y, zl, x, zh)
        pairs.append((i, (((y * 2 + zl) * 4 + x) * 2 + zh) * 2 + c))
    return lax.ppermute(value, ALL, pairs)


def turn(flip):
    return lambda y, zl, x, zh: (x, zh, x ^ y ^ (2 * flip), zl ^ flip)


def scatter(shares, first):
    parts = []
    for k in (3, 2, 1, 0) if first == 0 else (1, 0, 3, 2):
        dy, dz = first + 2 * (k >> 1), k & 1
        if (dy, dz) == (0, 0):
            parts.append(shares[k])
        else:
            parts.append(move(shares[k], lambda y, zl, x, zh: (y ^ dy, zl ^ dz, x, zh)))
    return parts


def spread(pair, axis):
    pairs = {0: pair}
    for d in (2, 1, 3):
        pairs[d] = lax.ppermute(pair, axis, [(i, (i + d) % 4) for i in range(4)])
    return [pairs[d] for d in range(4)]


def spread_chunks(value):
    chunks = {(0, 0): value}
    for dy, dz in ((2, 1), (2, 0), (0, 1), (1, 1), (3, 1), (1, 0), (3, 0)):
        chunks[dy, dz] = move(value, lambda y, zl, x, zh: ((y + dy) % 4, zl ^ dz, x, zh))
    return chunks


def per_device(resident, memory, previous, inverse_part, pair_coupling):
    place = jnp.stack([lax.axis_index(name) for name in ("x", "zh", "c", "y", "zl")]).astype(jnp.int32)
    coupling = jnp.tile(pair_coupling, (1, 128 // ORB))

    resident, memory, previous = in_hbm(resident), in_hbm(memory), in_hbm(previous)
    *odd, lhs = first_product(odd_product_kernel, place, memory, resident, [memory.shape[1:]], "odd_product")
    odd_parts = scatter(odd, 1)
    lhs, odd = lax.optimization_barrier((lhs, odd))
    even = first_product(even_product_kernel, place, lhs, resident, [], "even_product")
    even_parts = scatter(even, 0)
    place, _, odd_parts = lax.optimization_barrier((place, even[0], odd_parts))
    memory, prior_one, prior_two, odd_resident = bring_odd(place, memory, previous, resident)
    parts = odd_parts + even_parts
    front_one, energy = solve(
        first_solve_kernel, place, parts, prior_one, inverse_part[0], [coupling], 2, "first_solve"
    )
    pair = [move(energy, turn(0)), move(energy, turn(1))]
    ones = spread(front_one, "y")
    later, _ = lax.optimization_barrier((place, energy))
    even_resident = bring_even(later, resident)
    pair, ones, even_resident = lax.optimization_barrier((pair, ones, even_resident))
    own = spread(jnp.stack(pair), "x")
    ones = jnp.stack(ones)
    others = lax.ppermute(ones, "zl", SWAP)
    other = [lax.ppermute(pair, "c", SWAP) for pair in own]
    own_lhs = next_memory(0, place, memory, own)
    early = early_product(place, own_lhs, odd_resident)
    other, others, early = lax.optimization_barrier((other, others, early))
    other_lhs = next_memory(1, place, memory, other)
    odd = second_product(late_product_kernel, place, early, other_lhs, odd_resident, "late_product")
    own_lhs, odd = lax.optimization_barrier((own_lhs, odd))
    even = second_product(both_product_kernel, place, own_lhs, other_lhs, even_resident, "both_product")
    parts = scatter(odd, 1) + scatter(even, 0)
    (front_two,) = solve(
        second_solve_kernel, place, parts, prior_two, inverse_part[1], [], 1, "second_solve"
    )
    chunks = spread_chunks(front_two)
    fronts = join(join_one_kernel, (place, ones, others), [SMEM, VMEM, VMEM], previous.shape, {}, "join_one")
    for moves in ((0, 2), (1, 3)):
        some = [chunks[dy, dz] for dy in moves for dz in range(2)]
        some, fronts = lax.optimization_barrier((some, fronts))
        fronts = join(
            functools.partial(join_two_kernel, moves),
            (place, *some, fronts),
            [SMEM] + [VMEM] * 4 + [HBM],
            previous.shape,
            {5: 0},
            "join_two",
        )
    return fronts


def solution(mesh):
    fine = Mesh(mesh.devices.reshape(4, 2, 4, 2, 2), ALL)
    in_specs = (P(PASTS, SECONDS), P(None, None, PASTS), P(None, None, SECONDS), P(), P())
    out_specs = P(None, None, SECONDS)
    return jax.shard_map(
        per_device, mesh=fine, in_specs=in_specs, out_specs=out_specs, check_vma=False
    )
```

time: 113 us -> 118 us (1.044)
  Pallas kernels: 28.1 us -> 35.4 us
  waiting for transfers between devices: 34.7 us -> 32.1 us
  starting transfers between devices: 48.6 us -> 49.8 us
    pallas_call x6 -> x9, Pallas kernels: 21.3 us -> 27.2 us  [the longest x2 12.2 us: first_product(): pl.pallas_call(kernel, in_specs=[SMEM, HBM if lhs_shape else VMEM, HBM],...]
    ppermute x23, waiting for transfers between devices: 17.8 us -> 15.1 us  [move(): return lax.ppermute(value, ALL, pairs)]
    ppermute x6, starting transfers between devices: 8.73 us -> 10.8 us  [spread(): pairs[d] = lax.ppermute(pair, axis, [(i, (i + d) % 4) for i in range(4)])]
    ppermute x23, starting transfers between devices: 39 us -> 37.3 us  [move(): return lax.ppermute(value, ALL, pairs)]
    ppermute x6, waiting for transfers between devices: 15.3 us -> 17 us  [spread(): pairs[d] = lax.ppermute(pair, axis, [(i, (i + d) % 4) for i in range(4)])]
    ppermute x4, waiting for transfers between devices: 1.57 us -> 0.01 us  [per_device(): other = [lax.ppermute(pair, 'c', SWAP) for pair in own]]
    pallas_call x2 -> x3, Pallas kernels: 3.6 us -> 4.98 us  [join(): pl.pallas_call(kernel, in_specs=in_specs, out_specs=HBM, out_shape=jax.Sh...]
  transfers between devices with their start and end apart: 34 -> 34, of which waited for: 15 -> 11; matrix products, arithmetic and copies ran while one was open for 0% -> 0% of each run, Pallas kernels for 11% -> 18%
where the time goes in v9:
time: 118 us
  starting transfers between devices  49.8 us (42%)
  Pallas kernels  35.4 us (30%)
  waiting for transfers between devices  32.1 us (27%)
    ppermute x23, starting transfers between devices, move(): return lax.ppermute(value, ALL, pairs)  37.3 us
    ppermute x6, waiting for transfers between devices, spread(): pairs[d] = lax.ppermute(pair, axis, [(i, (i + d) % 4) for i in range(4)])  17 us
    ppermute x23, waiting for transfers between devices, move(): return lax.ppermute(value, ALL, pairs)  15.1 us
    pallas_call x2, Pallas kernels, first_product(): pl.pallas_call(kernel, in_specs=[SMEM, HBM if lhs_shape else VMEM, HBM],...  12.2 us
    ppermute x6, starting transfers between devices, spread(): pairs[d] = lax.ppermute(pair, axis, [(i, (i + d) % 4) for i in range(4)])  10.8 us
    pallas_call x3, Pallas kernels, join(): pl.pallas_call(kernel, in_specs=in_specs, out_specs=HBM, out_shape=jax.Sh...  4.98 us
    pallas_call x2, Pallas kernels, second_product(): pl.pallas_call(kernel, in_specs=[SMEM] + [VMEM] * 3, out_specs=[VMEM] * 4...  4.41 us
    pallas_call x1, Pallas kernels, bring_odd(): pl.pallas_call(bring_odd_kernel, in_specs=[SMEM] + [HBM] * 3, out_specs=[...  3.83 us
  transfers between devices with their start and end apart: 34, of which 11 were waited for; matrix products, arithmetic and copies ran while one was open for 0% of the time, Pallas kernels for 18%

profile of v9, /device:TPU:0, one launch (start us, length us, event | category | flops | bytes accessed | tf_op | source)
XLA Modules:
  0.0 118.2 jit_solution(4620724898485771691)
XLA Ops:
  0.1 6.5 %odd_product.1 = (bf16[192,384]{1,0:T(8,128)(2,1)S(1)}, bf16[192,384]{1,0:T(8,128)(2,1)S(1)}, bf16[192,384]{1,0:T(8,128)(2,1)S(1)}, bf16[192,384]{1,0:T(8,128)(2,1)S(1)}, bf16[384,3072]{1,0:T(8,128)(2,1)S(1)}) custom-call(s32[5]{0:T(128)S(1)} %stack.47.place_ref, bf16[2,384,3072]{2,1,0:T(8,128)(2,1)} %memory_ref.3, bf16[3072,1536]{1,0:T(8,128)(2,1)} %resident_ref.7), custom_call_target="tpu_custom_call" | custom-call | flops 1811939328 | bytes 4718592 | tf_op jit(solution)/shard_map/odd_product/pallas_call | solution.py:89
  6.6 1.7 %collective-permute-start.1 = (bf16[192,384]{1,0:T(8,128)(2,1)S(1)}, bf16[192,384]{1,0:T(8,128)(2,1)S(1)}, u32[]{:S(2)}, u32[]{:S(2)}) collective-permute-start(bf16[192,384]{1,0:T(8,128)(2,1)S(1)} %get-tuple-element.64), channel_id=1, source_target_pairs={{0,32},{1,33},{2,34},{3,35},{4,36},{5,37},{6,38},{7,39},{8,40},{9,... | collective-permute-start | bytes 442376 | tf_op jit(solution)/shard_map/ppermute | solution.py:386
  8.3 1.8 %collective-permute-start = (bf16[192,384]{1,0:T(8,128)(2,1)S(1)}, bf16[192,384]{1,0:T(8,128)(2,1)S(1)}, u32[]{:S(2)}, u32[]{:S(2)}) collective-permute-start(bf16[192,384]{1,0:T(8,128)(2,1)S(1)} %get-tuple-element.65), channel_id=1, source_target_pairs={{0,48},{1,49},{2,50},{3,51},{4,52},{5,53},{6,54},{7,55},{8,56},{9,... | collective-permute-start | bytes 442376 | tf_op jit(solution)/shard_map/ppermute | solution.py:386
  10.1 3.0 %collective-permute-start.3 = (bf16[192,384]{1,0:T(8,128)(2,1)S(1)}, bf16[192,384]{1,0:T(8,128)(2,1)S(1)}, u32[]{:S(2)}, u32[]{:S(2)}) collective-permute-start(bf16[192,384]{1,0:T(8,128)(2,1)S(1)} %get-tuple-element.66), channel_id=1, source_target_pairs={{0,96},{1,97},{2,98},{3,99},{4,100},{5,101},{6,102},{7,103},{8,104... | collective-permute-start | bytes 442376 | tf_op jit(solution)/shard_map/ppermute | solution.py:386
  13.1 5.8 %even_product.1 = (bf16[192,384]{1,0:T(8,128)(2,1)S(1)}, bf16[192,384]{1,0:T(8,128)(2,1)S(1)}, bf16[192,384]{1,0:T(8,128)(2,1)S(1)}, bf16[192,384]{1,0:T(8,128)(2,1)S(1)}) custom-call(s32[5]{0:T(128)S(1)} %stack.47.place_ref, bf16[384,3072]{1,0:T(8,128)(2,1)S(1)} %get-tuple-element.68.lhs_ref, bf16[3072,1536]{1,0:T(8,128)(2,1)} %resident_ref.7), custom_call_target="tpu_custom_call" | custom-call | flops 1811939328 | bytes 4718592 | tf_op jit(solution)/shard_map/even_product/pallas_call | solution.py:89
  18.9 3.2 %collective-permute-start.4 = (bf16[192,384]{1,0:T(8,128)(2,1)S(1)}, bf16[192,384]{1,0:T(8,128)(2,1)S(1)}, u32[]{:S(2)}, u32[]{:S(2)}) collective-permute-start(bf16[192,384]{1,0:T(8,128)(2,1)S(1)} %get-tuple-element.76), channel_id=1, source_target_pairs={{0,80},{1,81},{2,82},{3,83},{4,84},{5,85},{6,86},{7,87},{8,88},{9,... | collective-permute-start | bytes 442376 | tf_op jit(solution)/shard_map/ppermute | solution.py:386
  22.2 1.6 %collective-permute-start.5 = (bf16[192,384]{1,0:T(8,128)(2,1)S(1)}, bf16[192,384]{1,0:T(8,128)(2,1)S(1)}, u32[]{:S(2)}, u32[]{:S(2)}) collective-permute-start(bf16[192,384]{1,0:T(8,128)(2,1)S(1)} %get-tuple-element.77), channel_id=1, source_target_pairs={{0,64},{1,65},{2,66},{3,67},{4,68},{5,69},{6,70},{7,71},{8,72},{9,... | collective-permute-start | bytes 442376 | tf_op jit(solution)/shard_map/ppermute | solution.py:386
  24.3 3.8 %bring_odd.1 = (bf16[384,3072]{1,0:T(8,128)(2,1)S(1)}, bf16[192,384]{1,0:T(8,128)(2,1)S(1)}, bf16[192,384]{1,0:T(8,128)(2,1)S(1)}, bf16[3072,768]{1,0:T(8,128)(2,1)S(1)}) custom-call(s32[5]{0:T(128)S(1)} %stack.47.place_ref, bf16[2,384,3072]{2,1,0:T(8,128)(2,1)} %memory_ref.3, bf16[2,384,1536]{2,1,0:T(8,128)(2,1)} %previous_ref.1, ...), custom_call_target="tpu_custom_call" | custom-call | bytes 7077888 | tf_op jit(solution)/shard_map/bring_odd/pallas_call | solution.py:196
  28.1 1.4 %collective-permute-done.5.refs_5_ = bf16[192,384]{1,0:T(8,128)(2,1)S(1)} collective-permute-done((bf16[192,384]{1,0:T(8,128)(2,1)S(1)}, bf16[192,384]{1,0:T(8,128)(2,1)S(1)}, u32[]{:S(2)}, u32[]{:S(2)}) %collective-permute-start.5) | collective-permute-done | bytes 147488 | tf_op jit(solution)/shard_map/ppermute | solution.py:386
  29.6 1.8 %first_solve.1 = (bf16[192,384]{1,0:T(8,128)(2,1)S(1)}, bf16[192,384]{1,0:T(8,128)(2,1)S(1)}) custom-call(s32[5]{0:T(128)S(1)} %stack.47.place_ref, bf16[192,384]{1,0:T(8,128)(2,1)S(1)} %collective-permute-done.refs_0_, bf16[192,384]{1,0:T(8,128)(2,1)S(1)} %collective-permute-done.1.refs_1_, bf16[192,384]{1,0:T(8,128)(2,1)S(1)} %collective-permute-done.2.refs_2_, ...), custom_call_target="tpu_custom_call" | custom-call | flops 339738624 | bytes 1769472 | tf_op jit(solution)/shard_map/first_solve/pallas_call | solution.py:316
  31.4 6.1 %collective-permute-start.8 = (bf16[192,384]{1,0:T(8,128)(2,1)S(1)}, bf16[192,384]{1,0:T(8,128)(2,1)S(1)}, u32[]{:S(2)}, u32[]{:S(2)}) collective-permute-start(bf16[192,384]{1,0:T(8,128)(2,1)S(1)} %get-tuple-element.80), channel_id=1, source_target_pairs={{0,10},{1,11},{2,26},{3,27},{4,46},{5,47},{6,62},{7,63},{8,66},{9,... | collective-permute-start | bytes 442376 | tf_op jit(solution)/shard_map/ppermute | solution.py:386
  37.5 0.7 collective-permute-start.7
  38.1 7.3 %collective-permute-start.11 = (bf16[192,384]{1,0:T(8,128)(2,1)S(1)}, bf16[192,384]{1,0:T(8,128)(2,1)S(1)}, u32[]{:S(2)}, u32[]{:S(2)}) collective-permute-start(bf16[192,384]{1,0:T(8,128)(2,1)S(1)} %get-tuple-element.85), channel_id=1, source_target_pairs={{0,96},{32,0},{64,32},{96,64},{1,97},{33,1},{65,33},{97,65},{2,98}... | collective-permute-start | bytes 442376 | tf_op jit(solution)/shard_map/ppermute | solution.py:407
  45.5 0.9 collective-permute-start.9
  46.4 2.9 %bring_even.1.resident_ref = bf16[3072,768]{1,0:T(8,128)(2,1)S(1)} custom-call(s32[5]{0:T(128)S(1)} %stack.47.place_ref, bf16[3072,1536]{1,0:T(8,128)(2,1)} %resident_ref.7), custom_call_target="tpu_custom_call" | custom-call | bytes 4718592 | tf_op jit(solution)/shard_map/bring_even/pallas_call | solution.py:220
  49.3 0.6 collective-permute-done.11
  50.0 2.3 %collective-permute-done.10 = bf16[192,384]{1,0:T(8,128)(2,1)S(1)} collective-permute-done((bf16[192,384]{1,0:T(8,128)(2,1)S(1)}, bf16[192,384]{1,0:T(8,128)(2,1)S(1)}, u32[]{:S(2)}, u32[]{:S(2)}) %collective-permute-start.10) | collective-permute-done | bytes 147488 | tf_op jit(solution)/shard_map/ppermute | solution.py:407
  52.3 1.2 collective-permute-done.9
  53.4 1.5 %collective-permute-start.14 = (bf16[2,192,384]{2,1,0:T(8,128)(2,1)S(1)}, bf16[2,192,384]{2,1,0:T(8,128)(2,1)S(1)}, u32[]{:S(2)}, u32[]{:S(2)}) collective-permute-start(bf16[2,192,384]{2,1,0:T(8,128)(2,1)S(1)} %pad_maximum_fusion.1.refs_0_), channel_id=1, source_target_pairs={{0,12},{4,0},{8,4},{12,8},{1,13},{5,1},{9,5},{13,9},{2,14},{6,2},{... | collective-permute-start | bytes 884744 | tf_op jit(solution)/shard_map/ppermute | solution.py:407
  54.9 1.0 collective-permute-start.12
  56.1 1.2 %collective-permute-start.19 = (bf16[4,192,384]{2,1,0:T(8,128)(2,1)S(1)}, bf16[4,192,384]{2,1,0:T(8,128)(2,1)S(1)}, u32[]{:S(2)}, u32[]{:S(2)}) collective-permute-start(bf16[4,192,384]{2,1,0:T(8,128)(2,1)S(1)} %pad_maximum_fusion.own_ref), channel_id=1, source_target_pairs={{0,16},{16,0},{1,17},{17,1},{2,18},{18,2},{3,19},{19,3},{4,20},{20... | collective-permute-start | bytes 1769480 | tf_op jit(solution)/shard_map/ppermute | solution.py:441
  57.3 10.0 %collective-permute-done.14.refs_3_ = bf16[2,192,384]{2,1,0:T(8,128)(2,1)S(1)} collective-permute-done((bf16[2,192,384]{2,1,0:T(8,128)(2,1)S(1)}, bf16[2,192,384]{2,1,0:T(8,128)(2,1)S(1)}, u32[]{:S(2)}, u32[]{:S(2)}) %collective-permute-start.14) | collective-permute-done | bytes 294944 | tf_op jit(solution)/shard_map/ppermute | solution.py:407
  67.3 0.5 collective-permute-start.17
  67.8 2.9 %collective-permute-done.12.refs_1_ = bf16[2,192,384]{2,1,0:T(8,128)(2,1)S(1)} collective-permute-done((bf16[2,192,384]{2,1,0:T(8,128)(2,1)S(1)}, bf16[2,192,384]{2,1,0:T(8,128)(2,1)S(1)}, u32[]{:S(2)}, u32[]{:S(2)}) %collective-permute-start.12) | collective-permute-done | bytes 294944 | tf_op jit(solution)/shard_map/ppermute | solution.py:407
  70.7 1.1 next_memory.2.lhs_ref.own_ref
  71.8 1.6 %early_product.1.early_ref = f32[384,768]{1,0:T(8,128)S(1)} custom-call(s32[5]{0:T(128)S(1)} %stack.47.place_ref, bf16[384,1536]{1,0:T(8,128)(2,1)S(1)} %next_memory.2.lhs_ref.own_ref, bf16[3072,768]{1,0:T(8,128)(2,1)S(1)} %get-tuple-element.89.resident_ref), custom_call_target="tpu_custom_call" | custom-call | flops 905969664 | bytes 1179648 | tf_op jit(solution)/shard_map/early_product/pallas_call | solution.py:118
  73.5 1.1 next_memory.3.lhs_ref.other_ref
  74.6 1.8 %late_product.1 = (bf16[192,384]{1,0:T(8,128)(2,1)S(1)}, bf16[192,384]{1,0:T(8,128)(2,1)S(1)}, bf16[192,384]{1,0:T(8,128)(2,1)S(1)}, bf16[192,384]{1,0:T(8,128)(2,1)S(1)}) custom-call(s32[5]{0:T(128)S(1)} %stack.47.place_ref, f32[384,768]{1,0:T(8,128)S(1)} %early_product.1.early_ref, bf16[384,1536]{1,0:T(8,128)(2,1)S(1)} %next_memory.3.lhs_ref.other_ref, ...), custom_call_target="tpu_custom_call" | custom-call | flops 905969664 | bytes 1179648 | tf_op jit(solution)/shard_map/late_product/pallas_call | solution.py:151
  76.5 3.1 %collective-permute-start.21 = (bf16[192,384]{1,0:T(8,128)(2,1)S(1)}, bf16[192,384]{1,0:T(8,128)(2,1)S(1)}, u32[]{:S(2)}, u32[]{:S(2)}) collective-permute-start(bf16[192,384]{1,0:T(8,128)(2,1)S(1)} %get-tuple-element.100), channel_id=1, source_target_pairs={{0,32},{1,33},{2,34},{3,35},{4,36},{5,37},{6,38},{7,39},{8,40},{9,... | collective-permute-start | bytes 442376 | tf_op jit(solution)/shard_map/ppermute | solution.py:386
  79.5 3.1 %collective-permute-start.23 = (bf16[192,384]{1,0:T(8,128)(2,1)S(1)}, bf16[192,384]{1,0:T(8,128)(2,1)S(1)}, u32[]{:S(2)}, u32[]{:S(2)}) collective-permute-start(bf16[192,384]{1,0:T(8,128)(2,1)S(1)} %get-tuple-element.102), channel_id=1, source_target_pairs={{0,96},{1,97},{2,98},{3,99},{4,100},{5,101},{6,102},{7,103},{8,104... | collective-permute-start | bytes 442376 | tf_op jit(solution)/shard_map/ppermute | solution.py:386
  82.6 2.7 %both_product.1 = (bf16[192,384]{1,0:T(8,128)(2,1)S(1)}, bf16[192,384]{1,0:T(8,128)(2,1)S(1)}, bf16[192,384]{1,0:T(8,128)(2,1)S(1)}, bf16[192,384]{1,0:T(8,128)(2,1)S(1)}) custom-call(s32[5]{0:T(128)S(1)} %stack.47.place_ref, bf16[384,1536]{1,0:T(8,128)(2,1)S(1)} %next_memory.2.lhs_ref.own_ref, bf16[384,1536]{1,0:T(8,128)(2,1)S(1)} %next_memory.3.lhs_ref.other_ref, ...), custom_call_target="tpu_custom_call" | custom-call | flops 905969664 | bytes 1179648 | tf_op jit(solution)/shard_map/both_product/pallas_call | solution.py:151
  85.4 4.6 %collective-permute-start.25 = (bf16[192,384]{1,0:T(8,128)(2,1)S(1)}, bf16[192,384]{1,0:T(8,128)(2,1)S(1)}, u32[]{:S(2)}, u32[]{:S(2)}) collective-permute-start(bf16[192,384]{1,0:T(8,128)(2,1)S(1)} %get-tuple-element.106), channel_id=1, source_target_pairs={{0,64},{1,65},{2,66},{3,67},{4,68},{5,69},{6,70},{7,71},{8,72},{9,... | collective-permute-start | bytes 442376 | tf_op jit(solution)/shard_map/ppermute | solution.py:386
  90.0 0.4 collective-permute-start.26
  90.4 4.2 %collective-permute-done.24.refs_4_ = bf16[192,384]{1,0:T(8,128)(2,1)S(1)} collective-permute-done((bf16[192,384]{1,0:T(8,128)(2,1)S(1)}, bf16[192,384]{1,0:T(8,128)(2,1)S(1)}, u32[]{:S(2)}, u32[]{:S(2)}) %collective-permute-start.24) | collective-permute-done | bytes 147488 | tf_op jit(solution)/shard_map/ppermute | solution.py:386
  94.6 1.6 %collective-permute-done.25.refs_5_ = bf16[192,384]{1,0:T(8,128)(2,1)S(1)} collective-permute-done((bf16[192,384]{1,0:T(8,128)(2,1)S(1)}, bf16[192,384]{1,0:T(8,128)(2,1)S(1)}, u32[]{:S(2)}, u32[]{:S(2)}) %collective-permute-start.25) | collective-permute-done | bytes 147488 | tf_op jit(solution)/shard_map/ppermute | solution.py:386
  96.2 1.4 %second_solve.1.refs_0_ = bf16[192,384]{1,0:T(8,128)(2,1)S(1)} custom-call(s32[5]{0:T(128)S(1)} %stack.47.place_ref, bf16[192,384]{1,0:T(8,128)(2,1)S(1)} %collective-permute-done.20.refs_0_, bf16[192,384]{1,0:T(8,128)(2,1)S(1)} %collective-permute-done.21.refs_1_, bf16[192,384]{1,0:T(8,128)(2,1)S(1)} %collective-permute-done.22.refs_2_, ...), custom_call_target="tpu_custom_call" | custom-call | flops 339738624 | bytes 1769472 | tf_op jit(solution)/shard_map/second_solve/pallas_call | solution.py:316
  97.7 0.5 collective-permute-start.33
  98.2 4.0 %collective-permute-start.32 = (bf16[192,384]{1,0:T(8,128)(2,1)S(1)}, bf16[192,384]{1,0:T(8,128)(2,1)S(1)}, u32[]{:S(2)}, u32[]{:S(2)}) collective-permute-start(bf16[192,384]{1,0:T(8,128)(2,1)S(1)} %second_solve.1.refs_0_), channel_id=1, source_target_pairs={{0,64},{1,65},{2,66},{3,67},{4,68},{5,69},{6,70},{7,71},{8,72},{9,... | collective-permute-start | bytes 442376 | tf_op jit(solution)/shard_map/ppermute | solution.py:386
  102.2 0.6 collective-permute-start.31
  102.8 1.2 collective-permute-start.30
  104.2 2.6 %collective-permute-done.33.refs_3_ = bf16[192,384]{1,0:T(8,128)(2,1)S(1)} collective-permute-done((bf16[192,384]{1,0:T(8,128)(2,1)S(1)}, bf16[192,384]{1,0:T(8,128)(2,1)S(1)}, u32[]{:S(2)}, u32[]{:S(2)}) %collective-permute-start.33) | collective-permute-done | bytes 147488 | tf_op jit(solution)/shard_map/ppermute | solution.py:386
  106.8 0.6 collective-permute-start.28
  107.4 1.8 %collective-permute-done.32.refs_2_ = bf16[192,384]{1,0:T(8,128)(2,1)S(1)} collective-permute-done((bf16[192,384]{1,0:T(8,128)(2,1)S(1)}, bf16[192,384]{1,0:T(8,128)(2,1)S(1)}, u32[]{:S(2)}, u32[]{:S(2)}) %collective-permute-start.32) | collective-permute-done | bytes 147488 | tf_op jit(solution)/shard_map/ppermute | solution.py:386
  109.3 0.4 collective-permute-start.27
  109.6 1.8 %join_one.1.refs_4_ = bf16[2,384,1536]{2,1,0:T(8,128)(2,1)} custom-call(s32[5]{0:T(128)S(1)} %stack.47.place_ref, bf16[4,192,384]{2,1,0:T(8,128)(2,1)S(1)} %pad_maximum_fusion.own_ref, bf16[4,192,384]{2,1,0:T(8,128)(2,1)S(1)} %collective-permute-done.19.other_ref), custom_call_target="tpu_custom_call" | custom-call | flops 589824 | bytes 2359296 | tf_op jit(solution)/shard_map/join_one/pallas_call | solution.py:364
  111.4 3.4 %collective-permute-done.31.refs_1_ = bf16[192,384]{1,0:T(8,128)(2,1)S(1)} collective-permute-done((bf16[192,384]{1,0:T(8,128)(2,1)S(1)}, bf16[192,384]{1,0:T(8,128)(2,1)S(1)}, u32[]{:S(2)}, u32[]{:S(2)}) %collective-permute-start.31) | collective-permute-done | bytes 147488 | tf_op jit(solution)/shard_map/ppermute | solution.py:386
  114.8 1.6 %join_two.2.refs_4_ = bf16[2,384,1536]{2,1,0:T(8,128)(2,1)} custom-call(s32[5]{0:T(128)S(1)} %stack.47.place_ref, bf16[192,384]{1,0:T(8,128)(2,1)S(1)} %second_solve.1.refs_0_, bf16[192,384]{1,0:T(8,128)(2,1)S(1)} %collective-permute-done.31.refs_1_, bf16[192,384]{1,0:T(8,128)(2,1)S(1)} %collective-permute-done.32.refs_2_, ...), custom_call_target="tpu_custom_call", output_to_operand_aliasing={{}: (5, {})} | custom-call | flops 589824 | bytes 2359296 | tf_op jit(solution)/shard_map/join_two/pallas_call | solution.py:364
  116.4 1.6 %join_two.3 = bf16[2,384,1536]{2,1,0:T(8,128)(2,1)} custom-call(s32[5]{0:T(128)S(1)} %stack.47.place_ref, bf16[192,384]{1,0:T(8,128)(2,1)S(1)} %collective-permute-done.27.refs_0_, bf16[192,384]{1,0:T(8,128)(2,1)S(1)} %collective-permute-done.28.refs_1_, bf16[192,384]{1,0:T(8,128)(2,1)S(1)} %collective-permute-done.29.refs_2_, ...), custom_call_target="tpu_custom_call", output_to_operand_aliasing={{}: (5, {})} | custom-call | flops 589824 | bytes 2359296 | tf_op jit(solution)/shard_map/join_two/pallas_call | solution.py:364
  (44 shorter events, 1.3 us)
Async XLA Ops:
  6.6 15.6 %collective-permute-start.1 = (bf16[192,384]{1,0:T(8,128)(2,1)S(1)}, bf16[192,384]{1,0:T(8,128)(2,1)S(1)}, u32[]{:S(2)}, u32[]{:S(2)}) collective-permute-start(bf16[192,384]{1,0:T(8,128)(2,1)S(1)} %get-tuple-element.64), channel_id=1, source_target_pairs={{0,32},{1,33},{2,34},{3,35},{4,36},{5,37},{6,38},{7,39},{8,40},{9,... | collective-permute-start | bytes 442376 | tf_op jit(solution)/shard_map/ppermute | solution.py:386
  8.3 15.5 %collective-permute-start = (bf16[192,384]{1,0:T(8,128)(2,1)S(1)}, bf16[192,384]{1,0:T(8,128)(2,1)S(1)}, u32[]{:S(2)}, u32[]{:S(2)}) collective-permute-start(bf16[192,384]{1,0:T(8,128)(2,1)S(1)} %get-tuple-element.65), channel_id=1, source_target_pairs={{0,48},{1,49},{2,50},{3,51},{4,52},{5,53},{6,54},{7,55},{8,56},{9,... | collective-permute-start | bytes 442376 | tf_op jit(solution)/shard_map/ppermute | solution.py:386
  10.1 14.2 %collective-permute-start.3 = (bf16[192,384]{1,0:T(8,128)(2,1)S(1)}, bf16[192,384]{1,0:T(8,128)(2,1)S(1)}, u32[]{:S(2)}, u32[]{:S(2)}) collective-permute-start(bf16[192,384]{1,0:T(8,128)(2,1)S(1)} %get-tuple-element.66), channel_id=1, source_target_pairs={{0,96},{1,97},{2,98},{3,99},{4,100},{5,101},{6,102},{7,103},{8,104... | collective-permute-start | bytes 442376 | tf_op jit(solution)/shard_map/ppermute | solution.py:386
  13.1 11.2 %collective-permute-start.2 = (bf16[192,384]{1,0:T(8,128)(2,1)S(1)}, bf16[192,384]{1,0:T(8,128)(2,1)S(1)}, u32[]{:S(2)}, u32[]{:S(2)}) collective-permute-start(bf16[192,384]{1,0:T(8,128)(2,1)S(1)} %get-tuple-element.67), channel_id=1, source_target_pairs={{0,112},{1,113},{2,114},{3,115},{4,116},{5,117},{6,118},{7,119},{8... | collective-permute-start | bytes 442376 | tf_op jit(solution)/shard_map/ppermute | solution.py:386
  13.1 9.0 %copy-start.1 = (f32[32,32]{1,0:T(8,128)S(1)}, f32[32,32]{1,0:T(8,128)}, u32[]{:S(2)}) copy-start(f32[32,32]{1,0:T(8,128)} %param.9) | copy-start | bytes 12292
  13.1 11.1 %copy-start = (f32[2,384,384]{2,1,0:T(8,128)S(1)}, f32[2,384,384]{2,1,0:T(8,128)}, u32[]{:S(2)}) copy-start(f32[2,384,384]{2,1,0:T(8,128)} %param.8) | copy-start | bytes 3538948
  18.9 9.2 %collective-permute-start.4 = (bf16[192,384]{1,0:T(8,128)(2,1)S(1)}, bf16[192,384]{1,0:T(8,128)(2,1)S(1)}, u32[]{:S(2)}, u32[]{:S(2)}) collective-permute-start(bf16[192,384]{1,0:T(8,128)(2,1)S(1)} %get-tuple-element.76), channel_id=1, source_target_pairs={{0,80},{1,81},{2,82},{3,83},{4,84},{5,85},{6,86},{7,87},{8,88},{9,... | collective-permute-start | bytes 442376 | tf_op jit(solution)/shard_map/ppermute | solution.py:386
  22.2 7.4 %collective-permute-start.5 = (bf16[192,384]{1,0:T(8,128)(2,1)S(1)}, bf16[192,384]{1,0:T(8,128)(2,1)S(1)}, u32[]{:S(2)}, u32[]{:S(2)}) collective-permute-start(bf16[192,384]{1,0:T(8,128)(2,1)S(1)} %get-tuple-element.77), channel_id=1, source_target_pairs={{0,64},{1,65},{2,66},{3,67},{4,68},{5,69},{6,70},{7,71},{8,72},{9,... | collective-permute-start | bytes 442376 | tf_op jit(solution)/shard_map/ppermute | solution.py:386
  23.8 5.7 %collective-permute-start.6 = (bf16[192,384]{1,0:T(8,128)(2,1)S(1)}, bf16[192,384]{1,0:T(8,128)(2,1)S(1)}, u32[]{:S(2)}, u32[]{:S(2)}) collective-permute-start(bf16[192,384]{1,0:T(8,128)(2,1)S(1)} %get-tuple-element.78), channel_id=1, source_target_pairs={{0,16},{1,17},{2,18},{3,19},{4,20},{5,21},{6,22},{7,23},{8,24},{9,... | collective-permute-start | bytes 442376 | tf_op jit(solution)/shard_map/ppermute | solution.py:386
  31.4 18.0 %collective-permute-start.8 = (bf16[192,384]{1,0:T(8,128)(2,1)S(1)}, bf16[192,384]{1,0:T(8,128)(2,1)S(1)}, u32[]{:S(2)}, u32[]{:S(2)}) collective-permute-start(bf16[192,384]{1,0:T(8,128)(2,1)S(1)} %get-tuple-element.80), channel_id=1, source_target_pairs={{0,10},{1,11},{2,26},{3,27},{4,46},{5,47},{6,62},{7,63},{8,66},{9,... | collective-permute-start | bytes 442376 | tf_op jit(solution)/shard_map/ppermute | solution.py:386
  37.5 11.9 %collective-permute-start.7 = (bf16[192,384]{1,0:T(8,128)(2,1)S(1)}, bf16[192,384]{1,0:T(8,128)(2,1)S(1)}, u32[]{:S(2)}, u32[]{:S(2)}) collective-permute-start(bf16[192,384]{1,0:T(8,128)(2,1)S(1)} %get-tuple-element.80), channel_id=1, source_target_pairs={{0,0},{1,1},{2,16},{3,17},{4,36},{5,37},{6,52},{7,53},{8,72},{9,73... | collective-permute-start | bytes 442376 | tf_op jit(solution)/shard_map/ppermute | solution.py:386
  38.1 11.8 %collective-permute-start.11 = (bf16[192,384]{1,0:T(8,128)(2,1)S(1)}, bf16[192,384]{1,0:T(8,128)(2,1)S(1)}, u32[]{:S(2)}, u32[]{:S(2)}) collective-permute-start(bf16[192,384]{1,0:T(8,128)(2,1)S(1)} %get-tuple-element.85), channel_id=1, source_target_pairs={{0,96},{32,0},{64,32},{96,64},{1,97},{33,1},{65,33},{97,65},{2,98}... | collective-permute-start | bytes 442376 | tf_op jit(solution)/shard_map/ppermute | solution.py:407
  45.5 6.8 %collective-permute-start.10 = (bf16[192,384]{1,0:T(8,128)(2,1)S(1)}, bf16[192,384]{1,0:T(8,128)(2,1)S(1)}, u32[]{:S(2)}, u32[]{:S(2)}) collective-permute-start(bf16[192,384]{1,0:T(8,128)(2,1)S(1)} %get-tuple-element.85), channel_id=1, source_target_pairs={{0,64},{32,96},{64,0},{96,32},{1,65},{33,97},{65,1},{97,33},{2,66}... | collective-permute-start | bytes 442376 | tf_op jit(solution)/shard_map/ppermute | solution.py:407
  45.5 7.9 %collective-permute-start.9 = (bf16[192,384]{1,0:T(8,128)(2,1)S(1)}, bf16[192,384]{1,0:T(8,128)(2,1)S(1)}, u32[]{:S(2)}, u32[]{:S(2)}) collective-permute-start(bf16[192,384]{1,0:T(8,128)(2,1)S(1)} %get-tuple-element.85), channel_id=1, source_target_pairs={{0,32},{32,64},{64,96},{96,0},{1,33},{33,65},{65,97},{97,1},{2,34}... | collective-permute-start | bytes 442376 | tf_op jit(solution)/shard_map/ppermute | solution.py:407
  53.4 13.9 %collective-permute-start.14 = (bf16[2,192,384]{2,1,0:T(8,128)(2,1)S(1)}, bf16[2,192,384]{2,1,0:T(8,128)(2,1)S(1)}, u32[]{:S(2)}, u32[]{:S(2)}) collective-permute-start(bf16[2,192,384]{2,1,0:T(8,128)(2,1)S(1)} %pad_maximum_fusion.1.refs_0_), channel_id=1, source_target_pairs={{0,12},{4,0},{8,4},{12,8},{1,13},{5,1},{9,5},{13,9},{2,14},{6,2},{... | collective-permute-start | bytes 884744 | tf_op jit(solution)/shard_map/ppermute | solution.py:407
  54.9 12.4 %collective-permute-start.13 = (bf16[2,192,384]{2,1,0:T(8,128)(2,1)S(1)}, bf16[2,192,384]{2,1,0:T(8,128)(2,1)S(1)}, u32[]{:S(2)}, u32[]{:S(2)}) collective-permute-start(bf16[2,192,384]{2,1,0:T(8,128)(2,1)S(1)} %pad_maximum_fusion.1.refs_0_), channel_id=1, source_target_pairs={{0,8},{4,12},{8,0},{12,4},{1,9},{5,13},{9,1},{13,5},{2,10},{6,14},... | collective-permute-start | bytes 884744 | tf_op jit(solution)/shard_map/ppermute | solution.py:407
  54.9 15.8 %collective-permute-start.12 = (bf16[2,192,384]{2,1,0:T(8,128)(2,1)S(1)}, bf16[2,192,384]{2,1,0:T(8,128)(2,1)S(1)}, u32[]{:S(2)}, u32[]{:S(2)}) collective-permute-start(bf16[2,192,384]{2,1,0:T(8,128)(2,1)S(1)} %pad_maximum_fusion.1.refs_0_), channel_id=1, source_target_pairs={{0,4},{4,8},{8,12},{12,0},{1,5},{5,9},{9,13},{13,1},{2,6},{6,10},{... | collective-permute-start | bytes 884744 | tf_op jit(solution)/shard_map/ppermute | solution.py:407
  56.1 17.4 %collective-permute-start.19 = (bf16[4,192,384]{2,1,0:T(8,128)(2,1)S(1)}, bf16[4,192,384]{2,1,0:T(8,128)(2,1)S(1)}, u32[]{:S(2)}, u32[]{:S(2)}) collective-permute-start(bf16[4,192,384]{2,1,0:T(8,128)(2,1)S(1)} %pad_maximum_fusion.own_ref), channel_id=1, source_target_pairs={{0,16},{16,0},{1,17},{17,1},{2,18},{18,2},{3,19},{19,3},{4,20},{20... | collective-permute-start | bytes 1769480 | tf_op jit(solution)/shard_map/ppermute | solution.py:441
  57.3 16.2 %collective-permute-start.15 = (bf16[2,192,384]{2,1,0:T(8,128)(2,1)S(1)}, bf16[2,192,384]{2,1,0:T(8,128)(2,1)S(1)}, u32[]{:S(2)}, u32[]{:S(2)}) collective-permute-start(bf16[2,192,384]{2,1,0:T(8,128)(2,1)S(1)} %pad_maximum_fusion.1.refs_0_), channel_id=1, source_target_pairs={{0,1},{1,0},{2,3},{3,2},{4,5},{5,4},{6,7},{7,6},{8,9},{9,8},{10,11... | collective-permute-start | bytes 884744 | tf_op jit(solution)/shard_map/ppermute | solution.py:442
  67.3 6.2 %collective-permute-start.18 = (bf16[2,192,384]{2,1,0:T(8,128)(2,1)S(1)}, bf16[2,192,384]{2,1,0:T(8,128)(2,1)S(1)}, u32[]{:S(2)}, u32[]{:S(2)}) collective-permute-start(bf16[2,192,384]{2,1,0:T(8,128)(2,1)S(1)} %collective-permute-done.14.refs_3_), channel_id=1, source_target_pairs={{0,1},{1,0},{2,3},{3,2},{4,5},{5,4},{6,7},{7,6},{8,9},{9,8},{10,11... | collective-permute-start | bytes 884744 | tf_op jit(solution)/shard_map/ppermute | solution.py:442
  67.3 6.2 %collective-permute-start.17 = (bf16[2,192,384]{2,1,0:T(8,128)(2,1)S(1)}, bf16[2,192,384]{2,1,0:T(8,128)(2,1)S(1)}, u32[]{:S(2)}, u32[]{:S(2)}) collective-permute-start(bf16[2,192,384]{2,1,0:T(8,128)(2,1)S(1)} %collective-permute-done.13.refs_2_), channel_id=1, source_target_pairs={{0,1},{1,0},{2,3},{3,2},{4,5},{5,4},{6,7},{7,6},{8,9},{9,8},{10,11... | collective-permute-start | bytes 884744 | tf_op jit(solution)/shard_map/ppermute | solution.py:442
  70.7 2.8 %collective-permute-start.16 = (bf16[2,192,384]{2,1,0:T(8,128)(2,1)S(1)}, bf16[2,192,384]{2,1,0:T(8,128)(2,1)S(1)}, u32[]{:S(2)}, u32[]{:S(2)}) collective-permute-start(bf16[2,192,384]{2,1,0:T(8,128)(2,1)S(1)} %collective-permute-done.12.refs_1_), channel_id=1, source_target_pairs={{0,1},{1,0},{2,3},{3,2},{4,5},{5,4},{6,7},{7,6},{8,9},{9,8},{10,11... | collective-permute-start | bytes 884744 | tf_op jit(solution)/shard_map/ppermute | solution.py:442
  76.4 9.0 %collective-permute-start.20 = (bf16[192,384]{1,0:T(8,128)(2,1)S(1)}, bf16[192,384]{1,0:T(8,128)(2,1)S(1)}, u32[]{:S(2)}, u32[]{:S(2)}) collective-permute-start(bf16[192,384]{1,0:T(8,128)(2,1)S(1)} %get-tuple-element.99), channel_id=1, source_target_pairs={{0,48},{1,49},{2,50},{3,51},{4,52},{5,53},{6,54},{7,55},{8,56},{9,... | collective-permute-start | bytes 442376 | tf_op jit(solution)/shard_map/ppermute | solution.py:386
  76.5 13.5 %collective-permute-start.21 = (bf16[192,384]{1,0:T(8,128)(2,1)S(1)}, bf16[192,384]{1,0:T(8,128)(2,1)S(1)}, u32[]{:S(2)}, u32[]{:S(2)}) collective-permute-start(bf16[192,384]{1,0:T(8,128)(2,1)S(1)} %get-tuple-element.100), channel_id=1, source_target_pairs={{0,32},{1,33},{2,34},{3,35},{4,36},{5,37},{6,38},{7,39},{8,40},{9,... | collective-permute-start | bytes 442376 | tf_op jit(solution)/shard_map/ppermute | solution.py:386
  79.5 10.8 %collective-permute-start.22 = (bf16[192,384]{1,0:T(8,128)(2,1)S(1)}, bf16[192,384]{1,0:T(8,128)(2,1)S(1)}, u32[]{:S(2)}, u32[]{:S(2)}) collective-permute-start(bf16[192,384]{1,0:T(8,128)(2,1)S(1)} %get-tuple-element.101), channel_id=1, source_target_pairs={{0,112},{1,113},{2,114},{3,115},{4,116},{5,117},{6,118},{7,119},{8... | collective-permute-start | bytes 442376 | tf_op jit(solution)/shard_map/ppermute | solution.py:386
  79.5 10.8 %collective-permute-start.23 = (bf16[192,384]{1,0:T(8,128)(2,1)S(1)}, bf16[192,384]{1,0:T(8,128)(2,1)S(1)}, u32[]{:S(2)}, u32[]{:S(2)}) collective-permute-start(bf16[192,384]{1,0:T(8,128)(2,1)S(1)} %get-tuple-element.102), channel_id=1, source_target_pairs={{0,96},{1,97},{2,98},{3,99},{4,100},{5,101},{6,102},{7,103},{8,104... | collective-permute-start | bytes 442376 | tf_op jit(solution)/shard_map/ppermute | solution.py:386
  85.3 9.3 %collective-permute-start.24 = (bf16[192,384]{1,0:T(8,128)(2,1)S(1)}, bf16[192,384]{1,0:T(8,128)(2,1)S(1)}, u32[]{:S(2)}, u32[]{:S(2)}) collective-permute-start(bf16[192,384]{1,0:T(8,128)(2,1)S(1)} %get-tuple-element.105), channel_id=1, source_target_pairs={{0,80},{1,81},{2,82},{3,83},{4,84},{5,85},{6,86},{7,87},{8,88},{9,... | collective-permute-start | bytes 442376 | tf_op jit(solution)/shard_map/ppermute | solution.py:386
  85.4 10.8 %collective-permute-start.25 = (bf16[192,384]{1,0:T(8,128)(2,1)S(1)}, bf16[192,384]{1,0:T(8,128)(2,1)S(1)}, u32[]{:S(2)}, u32[]{:S(2)}) collective-permute-start(bf16[192,384]{1,0:T(8,128)(2,1)S(1)} %get-tuple-element.106), channel_id=1, source_target_pairs={{0,64},{1,65},{2,66},{3,67},{4,68},{5,69},{6,70},{7,71},{8,72},{9,... | collective-permute-start | bytes 442376 | tf_op jit(solution)/shard_map/ppermute | solution.py:386
  90.0 6.3 %collective-permute-start.26 = (bf16[192,384]{1,0:T(8,128)(2,1)S(1)}, bf16[192,384]{1,0:T(8,128)(2,1)S(1)}, u32[]{:S(2)}, u32[]{:S(2)}) collective-permute-start(bf16[192,384]{1,0:T(8,128)(2,1)S(1)} %get-tuple-element.107), channel_id=1, source_target_pairs={{0,16},{1,17},{2,18},{3,19},{4,20},{5,21},{6,22},{7,23},{8,24},{9,... | collective-permute-start | bytes 442376 | tf_op jit(solution)/shard_map/ppermute | solution.py:386
  97.7 9.1 %collective-permute-start.33 = (bf16[192,384]{1,0:T(8,128)(2,1)S(1)}, bf16[192,384]{1,0:T(8,128)(2,1)S(1)}, u32[]{:S(2)}, u32[]{:S(2)}) collective-permute-start(bf16[192,384]{1,0:T(8,128)(2,1)S(1)} %second_solve.1.refs_0_), channel_id=1, source_target_pairs={{0,80},{1,81},{2,82},{3,83},{4,84},{5,85},{6,86},{7,87},{8,88},{9,... | collective-permute-start | bytes 442376 | tf_op jit(solution)/shard_map/ppermute | solution.py:386
  98.2 11.1 %collective-permute-start.32 = (bf16[192,384]{1,0:T(8,128)(2,1)S(1)}, bf16[192,384]{1,0:T(8,128)(2,1)S(1)}, u32[]{:S(2)}, u32[]{:S(2)}) collective-permute-start(bf16[192,384]{1,0:T(8,128)(2,1)S(1)} %second_solve.1.refs_0_), channel_id=1, source_target_pairs={{0,64},{1,65},{2,66},{3,67},{4,68},{5,69},{6,70},{7,71},{8,72},{9,... | collective-permute-start | bytes 442376 | tf_op jit(solution)/shard_map/ppermute | solution.py:386
  102.2 12.6 %collective-permute-start.31 = (bf16[192,384]{1,0:T(8,128)(2,1)S(1)}, bf16[192,384]{1,0:T(8,128)(2,1)S(1)}, u32[]{:S(2)}, u32[]{:S(2)}) collective-permute-start(bf16[192,384]{1,0:T(8,128)(2,1)S(1)} %second_solve.1.refs_0_), channel_id=1, source_target_pairs={{0,16},{1,17},{2,18},{3,19},{4,20},{5,21},{6,22},{7,23},{8,24},{9,... | collective-permute-start | bytes 442376 | tf_op jit(solution)/shard_map/ppermute | solution.py:386
  102.8 13.6 %collective-permute-start.30 = (bf16[192,384]{1,0:T(8,128)(2,1)S(1)}, bf16[192,384]{1,0:T(8,128)(2,1)S(1)}, u32[]{:S(2)}, u32[]{:S(2)}) collective-permute-start(bf16[192,384]{1,0:T(8,128)(2,1)S(1)} %second_solve.1.refs_0_), channel_id=1, source_target_pairs={{0,112},{1,113},{2,114},{3,115},{4,116},{5,117},{6,118},{7,119},{8... | collective-permute-start | bytes 442376 | tf_op jit(solution)/shard_map/ppermute | solution.py:386
  103.9 12.5 %collective-permute-start.29 = (bf16[192,384]{1,0:T(8,128)(2,1)S(1)}, bf16[192,384]{1,0:T(8,128)(2,1)S(1)}, u32[]{:S(2)}, u32[]{:S(2)}) collective-permute-start(bf16[192,384]{1,0:T(8,128)(2,1)S(1)} %second_solve.1.refs_0_), channel_id=1, source_target_pairs={{0,96},{1,97},{2,98},{3,99},{4,100},{5,101},{6,102},{7,103},{8,104... | collective-permute-start | bytes 442376 | tf_op jit(solution)/shard_map/ppermute | solution.py:386
  106.8 9.6 %collective-permute-start.28 = (bf16[192,384]{1,0:T(8,128)(2,1)S(1)}, bf16[192,384]{1,0:T(8,128)(2,1)S(1)}, u32[]{:S(2)}, u32[]{:S(2)}) collective-permute-start(bf16[192,384]{1,0:T(8,128)(2,1)S(1)} %second_solve.1.refs_0_), channel_id=1, source_target_pairs={{0,48},{1,49},{2,50},{3,51},{4,52},{5,53},{6,54},{7,55},{8,56},{9,... | collective-permute-start | bytes 442376 | tf_op jit(solution)/shard_map/ppermute | solution.py:386
  109.3 7.2 %collective-permute-start.27 = (bf16[192,384]{1,0:T(8,128)(2,1)S(1)}, bf16[192,384]{1,0:T(8,128)(2,1)S(1)}, u32[]{:S(2)}, u32[]{:S(2)}) collective-permute-start(bf16[192,384]{1,0:T(8,128)(2,1)S(1)} %second_solve.1.refs_0_), channel_id=1, source_target_pairs={{0,32},{1,33},{2,34},{3,35},{4,36},{5,37},{6,38},{7,39},{8,40},{9,... | collective-permute-start | bytes 442376 | tf_op jit(solution)/shard_map/ppermute | solution.py:386

commit v10 on v9

--- a/solution.py
+++ b/solution.py
@@ -46,60 +46,84 @@
         out_ref[...] = turned_ref[pl.ds(pl.multiple_of(share * width, width), width), :]
 
 
+def half_product_kernel(place_ref, lhs_ref, resident_ref, *refs):
+    out_refs, turned_ref = refs[:4], refs[4]
+    product = jnp.dot(lhs_ref[...], resident_ref[...], preferred_element_type=f32)
+    turned_ref[...] = product.T.astype(bf16)
+    store_shares(place_ref, turned_ref, out_refs)
+
+
+def half_product(place, lhs, resident):
+    rows, depth = lhs.shape
+    cols = resident.shape[1]
+    width = cols // 4
+    return pl.pallas_call(
+        half_product_kernel,
+        in_specs=[SMEM, VMEM, VMEM],
+        out_specs=[VMEM] * 4,
+        out_shape=[jax.ShapeDtypeStruct((width, rows), bf16)] * 4,
+        scratch_shapes=[pltpu.VMEM((cols, rows), bf16)],
+        compiler_params=params(6),
+        cost_estimate=cost(2 * rows * depth * cols, 4 * width * rows),
+        name="half_product",
+    )(place, lhs, resident)
+
+
 TILES = 3
 
 
-def tiled_product(start, lhs_ref, resident_ref, tile_ref, turned_ref, sems, before):
-    tile = tile_ref.shape[1] // TILES
-    copies = []
-    for i in range(TILES):
-        at = pl.ds(pl.multiple_of(start + i * tile, tile), tile)
-        to = tile_ref.at[:, i * tile : (i + 1) * tile]
-        copies.append(pltpu.make_async_copy(resident_ref.at[:, at], to, sems.at[i]))
-    for copy in (*before, *copies):
+def first_product_kernel(place_ref, memory_ref, resident_ref, *refs):
+    out_refs, lhs_ref, odd_ref, even_ref, turned_ref, sems = refs[:4], *refs[4:]
+    depth, cols = odd_ref.shape
+    tile = cols // TILES
+    parity = place_ref[Y] & 1
+
+    def tile_copy(half_ref, side, i):
+        start = pl.multiple_of((parity ^ side) * cols + i * tile, tile)
+        return pltpu.make_async_copy(
+            resident_ref.at[:, pl.ds(start, tile)],
+            half_ref.at[:, i * tile : (i + 1) * tile],
+            sems.at[side * TILES + i],
+        )
+
+    memory_copy = pltpu.make_async_copy(memory_ref.at[0], lhs_ref, sems.at[2 * TILES])
+    odd = [tile_copy(odd_ref, 1, i) for i in range(TILES)]
+    even = [tile_copy(even_ref, 0, i) for i in range(TILES)]
+    for copy in (memory_copy, *even):
         copy.start()
-    for copy in before:
+    memory_copy.wait()
+    for i, copy in enumerate(even):
         copy.wait()
-    for i, copy in enumerate(copies):
+        odd[i].start()
+        at = slice(i * tile, (i + 1) * tile)
+        product = jnp.dot(lhs_ref[...], even_ref[:, at], preferred_element_type=f32)
+        turned_ref[at, :] = product.T.astype(bf16)
+    store_shares(place_ref, turned_ref, out_refs)
+    for copy in odd:
         copy.wait()
-        at = slice(i * tile, (i + 1) * tile)
-        product = jnp.dot(lhs_ref[...], tile_ref[:, at], preferred_element_type=f32)
-        turned_ref[at, :] = product.T.astype(bf16)
-
-
-def odd_product_kernel(place_ref, memory_ref, resident_ref, *refs):
-    out_refs, (lhs_ref, tile_ref, turned_ref, sems) = refs[:4], refs[4:]
-    start = ((place_ref[Y] & 1) ^ 1) * tile_ref.shape[1]
-    copy = pltpu.make_async_copy(memory_ref.at[0], lhs_ref, sems.at[TILES])
-    tiled_product(start, lhs_ref, resident_ref, tile_ref, turned_ref, sems, [copy])
-    store_shares(place_ref, turned_ref, out_refs)
-
-
-def even_product_kernel(place_ref, lhs_ref, resident_ref, *refs):
-    out_refs, (tile_ref, turned_ref, sems) = refs[:4], refs[4:]
-    start = (place_ref[Y] & 1) * tile_ref.shape[1]
-    tiled_product(start, lhs_ref, resident_ref, tile_ref, turned_ref, sems, [])
-    store_shares(place_ref, turned_ref, out_refs)
-
-
-def first_product(kernel, place, left, resident, lhs_shape, name):
-    depth, cols = resident.shape
-    rows, half = left.shape[-2], cols // 2
-    shapes = [(half // 4, rows)] * 4 + lhs_shape
-    return pl.pallas_call(
-        kernel,
-        in_specs=[SMEM, HBM if lhs_shape else VMEM, HBM],
-        out_specs=[VMEM] * len(shapes),
-        out_shape=[jax.ShapeDtypeStruct(shape, bf16) for shape in shapes],
+
+
+def first_product(place, memory, resident):
+    _, rows, depth = memory.shape
+    cols = resident.shape[1]
+    width = cols // 8
+    outs = [((width, rows), 4), ((rows, depth), 1), ((depth, cols // 2), 1)]
+    shapes = [jax.ShapeDtypeStruct(shape, bf16) for shape, count in outs for _ in range(count)]
+    *even, lhs, odd_resident = pl.pallas_call(
+        first_product_kernel,
+        in_specs=[SMEM] + [pl.BlockSpec(memory_space=pltpu.HBM)] * 2,
+        out_specs=[VMEM] * 6,
+        out_shape=shapes,
         scratch_shapes=[
-            pltpu.VMEM((depth, half), bf16),
-            pltpu.VMEM((half, rows), bf16),
-            pltpu.SemaphoreType.DMA((TILES + 1,)),
+            pltpu.VMEM((depth, cols // 2), bf16),
+            pltpu.VMEM((cols // 2, rows), bf16),
+            pltpu.SemaphoreType.DMA((2 * TILES + 1,)),
         ],
         compiler_params=params(12),
-        cost_estimate=cost(2 * rows * depth * half, 2 * depth * half),
-        name=name,
-    )(place, left, resident)
+        cost_estimate=cost(rows * depth * cols, 4 * depth * cols),
+        name="first_product",
+    )(place, memory, resident)
+    return even, lhs, odd_resident
 
 
 def depth_half(place_ref, side, resident_ref):
@@ -166,8 +190,8 @@
     return pltpu.make_async_copy(resident_ref.at[:, at], out_ref, sem)
 
 
-def bring_odd_kernel(
-    place_ref, memory_ref, previous_ref, resident_ref, memory_out, one_out, two_out, odd_out, prior_ref, turned_ref, sems
+def bring_soon_kernel(
+    place_ref, memory_ref, previous_ref, resident_ref, memory_out, one_out, two_out, even_out, prior_ref, turned_ref, sems
 ):
     width, rows = one_out.shape
     start = position(place_ref[Y]) * 2 * width
@@ -175,7 +199,7 @@
     copies = [
         pltpu.make_async_copy(previous_ref.at[:, :, cols], prior_ref, sems.at[0]),
         pltpu.make_async_copy(memory_ref.at[1], memory_out, sems.at[1]),
-        half_copy(1, place_ref, resident_ref, odd_out, sems.at[2]),
+        half_copy(0, place_ref, resident_ref, even_out, sems.at[2]),
     ]
     for copy in copies:
         copy.start()
@@ -188,13 +212,13 @@
         copy.wait()
 
 
-def bring_odd(place, memory, previous, resident):
+def bring_soon(place, memory, previous, resident):
     _, rows, depth = memory.shape
     cols = resident.shape[1]
     width = previous.shape[2] // 8
     shapes = [(rows, depth), (width, rows), (width, rows), (depth, cols // 2)]
     return pl.pallas_call(
-        bring_odd_kernel,
+        bring_soon_kernel,
         in_specs=[SMEM] + [HBM] * 3,
         out_specs=[VMEM] * 4,
         out_shape=[jax.ShapeDtypeStruct(shape, bf16) for shape in shapes],
@@ -205,27 +229,27 @@
         ],
         compiler_params=params(6),
         cost_estimate=cost(0, depth * (2 * rows + cols)),
-        name="bring_odd",
+        name="bring_soon",
     )(place, memory, previous, resident)
 
 
-def bring_even_kernel(place_ref, resident_ref, even_out, sem):
-    copy = half_copy(0, place_ref, resident_ref, even_out, sem)
+def bring_late_kernel(place_ref, resident_ref, odd_out, sem):
+    copy = half_copy(1, place_ref, resident_ref, odd_out, sem)
     copy.start()
     copy.wait()
 
 
-def bring_even(place, resident):
+def bring_late(place, resident):
     depth, cols = resident.shape
     return pl.pallas_call(
-        bring_even_kernel,
+        bring_late_kernel,
         in_specs=[SMEM, HBM],
         out_specs=VMEM,
         out_shape=jax.ShapeDtypeStruct((depth, cols // 2), bf16),
         scratch_shapes=[pltpu.SemaphoreType.DMA],
         compiler_params=params(4),
         cost_estimate=cost(0, depth * cols),
-        name="bring_even",
+        name="bring_late",
     )(place, resident)
 
 
@@ -297,18 +321,18 @@
 
 
 def first_solve_kernel(place_ref, *refs):
-    front_ref, energy_ref = refs[11:]
-    front = solve_into(refs[:8], refs[8], refs[9])
+    front_ref, energy_ref = refs[8:]
+    front = solve_into(refs[:5], refs[5], refs[6])
     front_ref[...] = front
     values = front.astype(f32)
     mirror = flipped(values)
     rows, cols = values.shape
-    coupling = jnp.tile(refs[10][...], (rows // ORB, cols // 128))
+    coupling = jnp.tile(refs[7][...], (rows // ORB, cols // 128))
     energy_ref[...] = (mirror * mirror * values * coupling).astype(bf16)
 
 
 def second_solve_kernel(place_ref, *refs):
-    refs[10][...] = solve_into(refs[:8], refs[8], refs[9])
+    refs[7][...] = solve_into(refs[:5], refs[5], refs[6])
 
 
 def solve(kernel, place, parts, prior, inverse, extra, outputs, name):
@@ -346,17 +370,16 @@
     put_blocks([block(dy) for dy in range(4)], block_ref, sems, out_ref, 0)
 
 
-def join_two_kernel(moves, place_ref, *refs):
-    chunk_refs, (out_ref, block_ref, sems) = refs[:4], refs[5:]
-
-    def block(i):
+def join_two_kernel(place_ref, *refs):
+    own_refs, twin_refs, (out_ref, block_ref, sems) = refs[:4], refs[4:8], refs[9:]
+
+    def block(dy):
         def write(ref):
-            own, other = chunk_refs[2 * i][...], chunk_refs[2 * i + 1][...]
-            place_pair(own, other, place_ref[ZL], ref)
-
-        return position((place_ref[Y] - moves[i]) & 3) * block_ref.shape[2], write
-
-    put_blocks([block(i) for i in range(2)], block_ref, sems, out_ref, 1)
+            place_pair(own_refs[dy][...], twin_refs[dy][...], place_ref[ZL], ref)
+
+        return position((place_ref[Y] - dy) & 3) * block_ref.shape[2], write
+
+    put_blocks([block(dy) for dy in range(4)], block_ref, sems, out_ref, 1)
 
 
 def join(kernel, args, in_specs, shape, aliases, name):
@@ -390,15 +413,35 @@
     return lambda y, zl, x, zh: (x, zh, x ^ y ^ (2 * flip), zl ^ flip)
 
 
-def scatter(shares, first):
-    parts = []
-    for k in (3, 2, 1, 0) if first == 0 else (1, 0, 3, 2):
-        dy, dz = first + 2 * (k >> 1), k & 1
-        if (dy, dz) == (0, 0):
-            parts.append(shares[k])
-        else:
-            parts.append(move(shares[k], lambda y, zl, x, zh: (y ^ dy, zl ^ dz, x, zh)))
-    return parts
+def sum_kernel(*refs):
+    total = refs[0][...].astype(f32)
+    for ref in refs[1:-1]:
+        total = total + ref[...].astype(f32)
+    refs[-1][...] = total.astype(bf16)
+
+
+def add_up(values):
+    return pl.pallas_call(
+        sum_kernel,
+        in_specs=[VMEM] * len(values),
+        out_specs=VMEM,
+        out_shape=jax.ShapeDtypeStruct(values[0].shape, bf16),
+        compiler_params=params(4),
+        cost_estimate=cost(4 * values[0].size, 10 * values[0].size),
+        name="add_up",
+    )(*values)
+
+
+def scatter(even, odd):
+    def along_y(share, dy):
+        return move(share, lambda y, zl, x, zh: (y ^ dy, zl, x, zh))
+
+    far = along_y(even[3], 2)
+    own_two, far, odd = lax.optimization_barrier((even[2], far, odd))
+    far = [far, along_y(odd[1], 1), along_y(odd[3], 3)]
+    near = [along_y(own_two, 2), along_y(odd[0], 1), along_y(odd[2], 3)]
+    for_twin = add_up([even[1], *far])
+    return [even[0], *near, lax.ppermute(for_twin, "zl", SWAP)], for_twin
 
 
 def spread(pair, axis):
@@ -408,63 +451,46 @@
     return [pairs[d] for d in range(4)]
 
 
-def spread_chunks(value):
-    chunks = {(0, 0): value}
-    for dy, dz in ((2, 1), (2, 0), (0, 1), (1, 1), (3, 1), (1, 0), (3, 0)):
-        chunks[dy, dz] = move(value, lambda y, zl, x, zh: ((y + dy) % 4, zl ^ dz, x, zh))
-    return chunks
-
-
 def per_device(resident, memory, previous, inverse_part, pair_coupling):
     place = jnp.stack([lax.axis_index(name) for name in ("x", "zh", "c", "y", "zl")]).astype(jnp.int32)
     coupling = jnp.tile(pair_coupling, (1, 128 // ORB))
 
     resident, memory, previous = in_hbm(resident), in_hbm(memory), in_hbm(previous)
-    *odd, lhs = first_product(odd_product_kernel, place, memory, resident, [memory.shape[1:]], "odd_product")
-    odd_parts = scatter(odd, 1)
-    lhs, odd = lax.optimization_barrier((lhs, odd))
-    even = first_product(even_product_kernel, place, lhs, resident, [], "even_product")
-    even_parts = scatter(even, 0)
-    place, _, odd_parts = lax.optimization_barrier((place, even[0], odd_parts))
-    memory, prior_one, prior_two, odd_resident = bring_odd(place, memory, previous, resident)
-    parts = odd_parts + even_parts
+    even, lhs, odd_resident = first_product(place, memory, resident)
+    lhs, even = lax.optimization_barrier((lhs, even))
+    odd = half_product(place, lhs, odd_resident)
+    parts, for_twin = scatter(even, odd)
+    later, _ = lax.optimization_barrier((place, for_twin))
+    memory, prior_one, prior_two, even_resident = bring_soon(later, memory, previous, resident)
     front_one, energy = solve(
         first_solve_kernel, place, parts, prior_one, inverse_part[0], [coupling], 2, "first_solve"
     )
     pair = [move(energy, turn(0)), move(energy, turn(1))]
     ones = spread(front_one, "y")
     later, _ = lax.optimization_barrier((place, energy))
-    even_resident = bring_even(later, resident)
-    pair, ones, even_resident = lax.optimization_barrier((pair, ones, even_resident))
+    odd_resident = bring_late(later, resident)
+    pair, ones, odd_resident = lax.optimization_barrier((pair, ones, odd_resident))
     own = spread(jnp.stack(pair), "x")
     ones = jnp.stack(ones)
     others = lax.ppermute(ones, "zl", SWAP)
     other = [lax.ppermute(pair, "c", SWAP) for pair in own]
     own_lhs = next_memory(0, place, memory, own)
-    early = early_product(place, own_lhs, odd_resident)
+    early = early_product(place, own_lhs, even_resident)
     other, others, early = lax.optimization_barrier((other, others, early))
     other_lhs = next_memory(1, place, memory, other)
-    odd = second_product(late_product_kernel, place, early, other_lhs, odd_resident, "late_product")
-    own_lhs, odd = lax.optimization_barrier((own_lhs, odd))
-    even = second_product(both_product_kernel, place, own_lhs, other_lhs, even_resident, "both_product")
-    parts = scatter(odd, 1) + scatter(even, 0)
+    even = second_product(late_product_kernel, place, early, other_lhs, even_resident, "late_product")
+    own_lhs, even = lax.optimization_barrier((own_lhs, even))
+    odd = second_product(both_product_kernel, place, own_lhs, other_lhs, odd_resident, "both_product")
+    parts, _ = scatter(even, odd)
     (front_two,) = solve(
         second_solve_kernel, place, parts, prior_two, inverse_part[1], [], 1, "second_solve"
     )
-    chunks = spread_chunks(front_two)
+    twin = lax.ppermute(front_two, "zl", SWAP)
+    chunks = [*spread(front_two, "y"), *spread(twin, "y")]
     fronts = join(join_one_kernel, (place, ones, others), [SMEM, VMEM, VMEM], previous.shape, {}, "join_one")
-    for moves in ((0, 2), (1, 3)):
-        some = [chunks[dy, dz] for dy in moves for dz in range(2)]
-        some, fronts = lax.optimization_barrier((some, fronts))
-        fronts = join(
-            functools.partial(join_two_kernel, moves),
-            (place, *some, fronts),
-            [SMEM] + [VMEM] * 4 + [HBM],
-            previous.shape,
-            {5: 0},
-            "join_two",
-        )
-    return fronts
+    return join(
+        join_two_kernel, (place, *chunks, fronts), [SMEM] + [VMEM] * 8 + [HBM], previous.shape, {9: 0}, "join_two"
+    )
 
 
 def solution(mesh):

time: 118 us -> 117 us (level)
  waiting for transfers between devices: 32.1 us -> 37.3 us
  Pallas kernels: 35.4 us -> 31 us
  starting transfers between devices: 49.8 us -> 47.5 us
    ppermute x23 -> x14, starting transfers between devices: 37.3 us -> 24.1 us  [move(): return lax.ppermute(value, ALL, pairs)]
    ppermute x6 -> x12, starting transfers between devices: 10.8 us -> 19.5 us  [spread(): pairs[d] = lax.ppermute(pair, axis, [(i, (i + d) % 4) for i in range(4)])]
    ppermute x0 -> x3, waiting for transfers between devices: none -> 3.74 us  [the longest x2 3.3 us: scatter(): return ([even[0], *near, lax.ppermute(for_twin, 'zl', SWAP)], for_twin)]
    ppermute x0 -> x3, starting transfers between devices: none -> 3.21 us  [the longest x2 2.6 us: scatter(): return ([even[0], *near, lax.ppermute(for_twin, 'zl', SWAP)], for_twin)]
    pallas_call x4 -> x6, Pallas kernels: 19 us -> 16 us  [the longest x1 6.5 us: first_product(): pl.pallas_call(first_product_kernel, in_specs=[SMEM] + [pl.BlockSpec(memo...]
    ppermute x23 -> x14, waiting for transfers between devices: 15.1 us -> 16.5 us  [move(): return lax.ppermute(value, ALL, pairs)]
    pallas_call x3 -> x2, Pallas kernels: 4.98 us -> 3.61 us  [join(): pl.pallas_call(kernel, in_specs=in_specs, out_specs=HBM, out_shape=jax.Sh...]
    ppermute x6 -> x12, waiting for transfers between devices: 17 us -> 17 us  [spread(): pairs[d] = lax.ppermute(pair, axis, [(i, (i + d) % 4) for i in range(4)])]
  transfers between devices with their start and end apart: 34 -> 34, of which waited for: 11 -> 17; matrix products, arithmetic and copies ran while one was open for 0% -> 0% of each run, Pallas kernels for 18% -> 14%
where the time goes in v10:
time: 117 us
  starting transfers between devices  47.5 us (41%)
  waiting for transfers between devices  37.3 us (32%)
  Pallas kernels  31 us (26%)
    ppermute x14, starting transfers between devices, move(): return lax.ppermute(value, ALL, pairs)  24.1 us
    ppermute x12, starting transfers between devices, spread(): pairs[d] = lax.ppermute(pair, axis, [(i, (i + d) % 4) for i in range(4)])  19.5 us
    ppermute x12, waiting for transfers between devices, spread(): pairs[d] = lax.ppermute(pair, axis, [(i, (i + d) % 4) for i in range(4)])  17 us
    ppermute x14, waiting for transfers between devices, move(): return lax.ppermute(value, ALL, pairs)  16.5 us
    pallas_call x1, Pallas kernels, first_product(): pl.pallas_call(first_product_kernel, in_specs=[SMEM] + [pl.BlockSpec(memo...  6.5 us
    pallas_call x2, Pallas kernels, second_product(): pl.pallas_call(kernel, in_specs=[SMEM] + [VMEM] * 3, out_specs=[VMEM] * 4...  4.41 us
    pallas_call x1, Pallas kernels, bring_soon(): pl.pallas_call(bring_soon_kernel, in_specs=[SMEM] + [HBM] * 3, out_specs=...  3.83 us
    pallas_call x2, Pallas kernels, join(): pl.pallas_call(kernel, in_specs=in_specs, out_specs=HBM, out_shape=jax.Sh...  3.61 us
  transfers between devices with their start and end apart: 34, of which 17 were waited for; matrix products, arithmetic and copies ran while one was open for 0% of the time, Pallas kernels for 14%

profile of v10, /device:TPU:0, one launch (start us, length us, event | category | flops | bytes accessed | tf_op | source)
XLA Modules:
  0.0 116.6 jit_solution(12372641941872320003)
XLA Ops:
  0.1 6.5 %first_product.1 = (bf16[192,384]{1,0:T(8,128)(2,1)S(1)}, bf16[192,384]{1,0:T(8,128)(2,1)S(1)}, bf16[192,384]{1,0:T(8,128)(2,1)S(1)}, bf16[192,384]{1,0:T(8,128)...) custom-call(s32[5]{0:T(128)S(1)} %stack.47.place_ref, bf16[2,384,3072]{2,1,0:T(8,128)(2,1)} %memory_ref.3, ...), custom_call_target="tpu_custom_call" | custom-call | flops 1811939328 | bytes 18874368 | tf_op jit(solution)/shard_map/first_product/pallas_call | solution.py:112
  6.6 3.4 %collective-permute-start = (bf16[192,384]{1,0:T(8,128)(2,1)S(1)}, bf16[192,384]{1,0:T(8,128)(2,1)S(1)}, u32[]{:S(2)}, u32[]{:S(2)}) collective-permute-start(bf16[192,384]{1,0:T(8,128)(2,1)S(1)} %get-tuple-element.73), channel_id=1, source_target_pairs={{0,64},{1,65},{2,66},{3,67},{4,68},{5,69},{6,70},{7,71},{8,72},{9,... | collective-permute-start | bytes 442376 | tf_op jit(solution)/shard_map/ppermute | solution.py:409
  10.0 2.7 %half_product.1 = (bf16[192,384]{1,0:T(8,128)(2,1)S(1)}, bf16[192,384]{1,0:T(8,128)(2,1)S(1)}, bf16[192,384]{1,0:T(8,128)(2,1)S(1)}, bf16[192,384]{1,0:T(8,128)(2,1)S(1)}) custom-call(s32[5]{0:T(128)S(1)} %stack.47.place_ref, bf16[384,3072]{1,0:T(8,128)(2,1)S(1)} %get-tuple-element.74.lhs_ref, bf16[3072,768]{1,0:T(8,128)(2,1)S(1)} %get-tuple-element.75.resident_ref), custom_call_target="tpu_custom_call" | custom-call | flops 1811939328 | bytes 294912 | tf_op jit(solution)/shard_map/half_product/pallas_call | solution.py:60
  12.6 1.2 %collective-permute-done.refs_1_ = bf16[192,384]{1,0:T(8,128)(2,1)S(1)} collective-permute-done((bf16[192,384]{1,0:T(8,128)(2,1)S(1)}, bf16[192,384]{1,0:T(8,128)(2,1)S(1)}, u32[]{:S(2)}, u32[]{:S(2)}) %collective-permute-start) | collective-permute-done | bytes 147488 | tf_op jit(solution)/shard_map/ppermute | solution.py:409
  13.8 1.6 %collective-permute-start.1 = (bf16[192,384]{1,0:T(8,128)(2,1)S(1)}, bf16[192,384]{1,0:T(8,128)(2,1)S(1)}, u32[]{:S(2)}, u32[]{:S(2)}) collective-permute-start(bf16[192,384]{1,0:T(8,128)(2,1)S(1)} %get-tuple-element.81), channel_id=1, source_target_pairs={{0,32},{1,33},{2,34},{3,35},{4,36},{5,37},{6,38},{7,39},{8,40},{9,... | collective-permute-start | bytes 442376 | tf_op jit(solution)/shard_map/ppermute | solution.py:409
  15.4 2.2 %collective-permute-start.2 = (bf16[192,384]{1,0:T(8,128)(2,1)S(1)}, bf16[192,384]{1,0:T(8,128)(2,1)S(1)}, u32[]{:S(2)}, u32[]{:S(2)}) collective-permute-start(bf16[192,384]{1,0:T(8,128)(2,1)S(1)} %get-tuple-element.82), channel_id=1, source_target_pairs={{0,96},{1,97},{2,98},{3,99},{4,100},{5,101},{6,102},{7,103},{8,104... | collective-permute-start | bytes 442376 | tf_op jit(solution)/shard_map/ppermute | solution.py:409
  17.7 0.8 collective-permute-start.3
  18.5 1.2 %collective-permute-start.4 = (bf16[192,384]{1,0:T(8,128)(2,1)S(1)}, bf16[192,384]{1,0:T(8,128)(2,1)S(1)}, u32[]{:S(2)}, u32[]{:S(2)}) collective-permute-start(bf16[192,384]{1,0:T(8,128)(2,1)S(1)} %get-tuple-element.87), channel_id=1, source_target_pairs={{0,32},{1,33},{2,34},{3,35},{4,36},{5,37},{6,38},{7,39},{8,40},{9,... | collective-permute-start | bytes 442376 | tf_op jit(solution)/shard_map/ppermute | solution.py:409
  19.7 2.2 %collective-permute-start.5 = (bf16[192,384]{1,0:T(8,128)(2,1)S(1)}, bf16[192,384]{1,0:T(8,128)(2,1)S(1)}, u32[]{:S(2)}, u32[]{:S(2)}) collective-permute-start(bf16[192,384]{1,0:T(8,128)(2,1)S(1)} %get-tuple-element.88), channel_id=1, source_target_pairs={{0,96},{1,97},{2,98},{3,99},{4,100},{5,101},{6,102},{7,103},{8,104... | collective-permute-start | bytes 442376 | tf_op jit(solution)/shard_map/ppermute | solution.py:409
  21.9 3.8 %collective-permute-done.2.refs_3_ = bf16[192,384]{1,0:T(8,128)(2,1)S(1)} collective-permute-done((bf16[192,384]{1,0:T(8,128)(2,1)S(1)}, bf16[192,384]{1,0:T(8,128)(2,1)S(1)}, u32[]{:S(2)}, u32[]{:S(2)}) %collective-permute-start.2) | collective-permute-done | bytes 147488 | tf_op jit(solution)/shard_map/ppermute | solution.py:409
  25.8 2.0 %collective-permute-start.6 = (bf16[192,384]{1,0:T(8,128)(2,1)S(1)}, bf16[192,384]{1,0:T(8,128)(2,1)S(1)}, u32[]{:S(2)}, u32[]{:S(2)}) collective-permute-start(bf16[192,384]{1,0:T(8,128)(2,1)S(1)} %add_up.2), channel_id=1, source_target_pairs={{0,16},{16,0},{1,17},{17,1},{2,18},{18,2},{3,19},{19,3},{4,20},{20... | collective-permute-start | bytes 442376 | tf_op jit(solution)/shard_map/ppermute | solution.py:444
  27.9 3.8 %bring_soon.1 = (bf16[384,3072]{1,0:T(8,128)(2,1)S(1)}, bf16[192,384]{1,0:T(8,128)(2,1)S(1)}, bf16[192,384]{1,0:T(8,128)(2,1)S(1)}, bf16[3072,768]{1,0:T(8,128)(2,1)S(1)}) custom-call(s32[5]{0:T(128)S(1)} %stack.47.place_ref, bf16[2,384,3072]{2,1,0:T(8,128)(2,1)} %memory_ref.3, bf16[2,384,1536]{2,1,0:T(8,128)(2,1)} %previous_ref.1, ...), custom_call_target="tpu_custom_call" | custom-call | bytes 7077888 | tf_op jit(solution)/shard_map/bring_soon/pallas_call | solution.py:220
  31.8 1.8 %first_solve.1 = (bf16[192,384]{1,0:T(8,128)(2,1)S(1)}, bf16[192,384]{1,0:T(8,128)(2,1)S(1)}) custom-call(s32[5]{0:T(128)S(1)} %stack.47.place_ref, bf16[192,384]{1,0:T(8,128)(2,1)S(1)} %get-tuple-element.85.refs_0_, bf16[192,384]{1,0:T(8,128)(2,1)S(1)} %collective-permute-done.3.refs_1_, bf16[192,384]{1,0:T(8,128)(2,1)S(1)} %collective-permute-done.4.refs_2_, ...), custom_call_target="tpu_custom_call" | custom-call | flops 339738624 | bytes 1769472 | tf_op jit(solution)/shard_map/first_solve/pallas_call | solution.py:340
  33.5 6.1 %collective-permute-start.8 = (bf16[192,384]{1,0:T(8,128)(2,1)S(1)}, bf16[192,384]{1,0:T(8,128)(2,1)S(1)}, u32[]{:S(2)}, u32[]{:S(2)}) collective-permute-start(bf16[192,384]{1,0:T(8,128)(2,1)S(1)} %get-tuple-element.90), channel_id=1, source_target_pairs={{0,10},{1,11},{2,26},{3,27},{4,46},{5,47},{6,62},{7,63},{8,66},{9,... | collective-permute-start | bytes 442376 | tf_op jit(solution)/shard_map/ppermute | solution.py:409
  39.6 0.7 collective-permute-start.7
  40.3 6.5 %collective-permute-start.11 = (bf16[192,384]{1,0:T(8,128)(2,1)S(1)}, bf16[192,384]{1,0:T(8,128)(2,1)S(1)}, u32[]{:S(2)}, u32[]{:S(2)}) collective-permute-start(bf16[192,384]{1,0:T(8,128)(2,1)S(1)} %get-tuple-element.95), channel_id=1, source_target_pairs={{0,96},{32,0},{64,32},{96,64},{1,97},{33,1},{65,33},{97,65},{2,98}... | collective-permute-start | bytes 442376 | tf_op jit(solution)/shard_map/ppermute | solution.py:450
  46.8 0.9 collective-permute-start.9
  47.8 2.9 %bring_late.1.resident_ref = bf16[3072,768]{1,0:T(8,128)(2,1)S(1)} custom-call(s32[5]{0:T(128)S(1)} %stack.47.place_ref, bf16[3072,1536]{1,0:T(8,128)(2,1)} %resident_ref.5), custom_call_target="tpu_custom_call" | custom-call | bytes 4718592 | tf_op jit(solution)/shard_map/bring_late/pallas_call | solution.py:244
  51.1 2.5 %collective-permute-done.10 = bf16[192,384]{1,0:T(8,128)(2,1)S(1)} collective-permute-done((bf16[192,384]{1,0:T(8,128)(2,1)S(1)}, bf16[192,384]{1,0:T(8,128)(2,1)S(1)}, u32[]{:S(2)}, u32[]{:S(2)}) %collective-permute-start.10) | collective-permute-done | bytes 147488 | tf_op jit(solution)/shard_map/ppermute | solution.py:450
  53.6 1.2 %collective-permute-done.9 = bf16[192,384]{1,0:T(8,128)(2,1)S(1)} collective-permute-done((bf16[192,384]{1,0:T(8,128)(2,1)S(1)}, bf16[192,384]{1,0:T(8,128)(2,1)S(1)}, u32[]{:S(2)}, u32[]{:S(2)}) %collective-permute-start.9) | collective-permute-done | bytes 147488 | tf_op jit(solution)/shard_map/ppermute | solution.py:450
  54.8 1.0 collective-permute-start.14
  55.8 1.1 collective-permute-start.12
  57.7 3.9 %collective-permute-done.14.refs_3_ = bf16[2,192,384]{2,1,0:T(8,128)(2,1)S(1)} collective-permute-done((bf16[2,192,384]{2,1,0:T(8,128)(2,1)S(1)}, bf16[2,192,384]{2,1,0:T(8,128)(2,1)S(1)}, u32[]{:S(2)}, u32[]{:S(2)}) %collective-permute-start.14) | collective-permute-done | bytes 294944 | tf_op jit(solution)/shard_map/ppermute | solution.py:450
  61.6 2.5 %collective-permute-done.13.refs_2_ = bf16[2,192,384]{2,1,0:T(8,128)(2,1)S(1)} collective-permute-done((bf16[2,192,384]{2,1,0:T(8,128)(2,1)S(1)}, bf16[2,192,384]{2,1,0:T(8,128)(2,1)S(1)}, u32[]{:S(2)}, u32[]{:S(2)}) %collective-permute-start.13) | collective-permute-done | bytes 294944 | tf_op jit(solution)/shard_map/ppermute | solution.py:450
  64.1 3.1 %collective-permute-done.12.refs_1_ = bf16[2,192,384]{2,1,0:T(8,128)(2,1)S(1)} collective-permute-done((bf16[2,192,384]{2,1,0:T(8,128)(2,1)S(1)}, bf16[2,192,384]{2,1,0:T(8,128)(2,1)S(1)}, u32[]{:S(2)}, u32[]{:S(2)}) %collective-permute-start.12) | collective-permute-done | bytes 294944 | tf_op jit(solution)/shard_map/ppermute | solution.py:450
  67.2 1.1 next_memory.2.lhs_ref.own_ref
  68.3 1.6 %early_product.1.early_ref = f32[384,768]{1,0:T(8,128)S(1)} custom-call(s32[5]{0:T(128)S(1)} %stack.47.place_ref, bf16[384,1536]{1,0:T(8,128)(2,1)S(1)} %next_memory.2.lhs_ref.own_ref, bf16[3072,768]{1,0:T(8,128)(2,1)S(1)} %get-tuple-element.99.resident_ref), custom_call_target="tpu_custom_call" | custom-call | flops 905969664 | bytes 1179648 | tf_op jit(solution)/shard_map/early_product/pallas_call | solution.py:142
  70.0 1.1 next_memory.3.lhs_ref.other_ref
  71.1 1.8 %late_product.1 = (bf16[192,384]{1,0:T(8,128)(2,1)S(1)}, bf16[192,384]{1,0:T(8,128)(2,1)S(1)}, bf16[192,384]{1,0:T(8,128)(2,1)S(1)}, bf16[192,384]{1,0:T(8,128)(2,1)S(1)}) custom-call(s32[5]{0:T(128)S(1)} %stack.47.place_ref, f32[384,768]{1,0:T(8,128)S(1)} %early_product.1.early_ref, bf16[384,1536]{1,0:T(8,128)(2,1)S(1)} %next_memory.3.lhs_ref.other_ref, ...), custom_call_target="tpu_custom_call" | custom-call | flops 905969664 | bytes 1179648 | tf_op jit(solution)/shard_map/late_product/pallas_call | solution.py:175
  72.9 0.7 collective-permute-start.20
  73.6 2.7 %both_product.1 = (bf16[192,384]{1,0:T(8,128)(2,1)S(1)}, bf16[192,384]{1,0:T(8,128)(2,1)S(1)}, bf16[192,384]{1,0:T(8,128)(2,1)S(1)}, bf16[192,384]{1,0:T(8,128)(2,1)S(1)}) custom-call(s32[5]{0:T(128)S(1)} %stack.47.place_ref, bf16[384,1536]{1,0:T(8,128)(2,1)S(1)} %next_memory.2.lhs_ref.own_ref, bf16[384,1536]{1,0:T(8,128)(2,1)S(1)} %next_memory.3.lhs_ref.other_ref, ...), custom_call_target="tpu_custom_call" | custom-call | flops 905969664 | bytes 1179648 | tf_op jit(solution)/shard_map/both_product/pallas_call | solution.py:175
  76.2 4.5 %collective-permute-done.20.refs_1_ = bf16[192,384]{1,0:T(8,128)(2,1)S(1)} collective-permute-done((bf16[192,384]{1,0:T(8,128)(2,1)S(1)}, bf16[192,384]{1,0:T(8,128)(2,1)S(1)}, u32[]{:S(2)}, u32[]{:S(2)}) %collective-permute-start.20) | collective-permute-done | bytes 147488 | tf_op jit(solution)/shard_map/ppermute | solution.py:409
  80.7 1.2 %collective-permute-start.25 = (bf16[192,384]{1,0:T(8,128)(2,1)S(1)}, bf16[192,384]{1,0:T(8,128)(2,1)S(1)}, u32[]{:S(2)}, u32[]{:S(2)}) collective-permute-start(bf16[192,384]{1,0:T(8,128)(2,1)S(1)} %get-tuple-element.124), channel_id=1, source_target_pairs={{0,96},{1,97},{2,98},{3,99},{4,100},{5,101},{6,102},{7,103},{8,104... | collective-permute-start | bytes 442376 | tf_op jit(solution)/shard_map/ppermute | solution.py:409
  81.9 2.9 %collective-permute-start.21 = (bf16[192,384]{1,0:T(8,128)(2,1)S(1)}, bf16[192,384]{1,0:T(8,128)(2,1)S(1)}, u32[]{:S(2)}, u32[]{:S(2)}) collective-permute-start(bf16[192,384]{1,0:T(8,128)(2,1)S(1)} %get-tuple-element.118), channel_id=1, source_target_pairs={{0,64},{1,65},{2,66},{3,67},{4,68},{5,69},{6,70},{7,71},{8,72},{9,... | collective-permute-start | bytes 442376 | tf_op jit(solution)/shard_map/ppermute | solution.py:409
  84.8 1.2 %collective-permute-start.23 = (bf16[192,384]{1,0:T(8,128)(2,1)S(1)}, bf16[192,384]{1,0:T(8,128)(2,1)S(1)}, u32[]{:S(2)}, u32[]{:S(2)}) collective-permute-start(bf16[192,384]{1,0:T(8,128)(2,1)S(1)} %get-tuple-element.120), channel_id=1, source_target_pairs={{0,96},{1,97},{2,98},{3,99},{4,100},{5,101},{6,102},{7,103},{8,104... | collective-permute-start | bytes 442376 | tf_op jit(solution)/shard_map/ppermute | solution.py:409
  86.0 1.5 %collective-permute-done.24.refs_2_ = bf16[192,384]{1,0:T(8,128)(2,1)S(1)} collective-permute-done((bf16[192,384]{1,0:T(8,128)(2,1)S(1)}, bf16[192,384]{1,0:T(8,128)(2,1)S(1)}, u32[]{:S(2)}, u32[]{:S(2)}) %collective-permute-start.24) | collective-permute-done | bytes 147488 | tf_op jit(solution)/shard_map/ppermute | solution.py:409
  87.5 4.2 %collective-permute-done.25.refs_3_ = bf16[192,384]{1,0:T(8,128)(2,1)S(1)} collective-permute-done((bf16[192,384]{1,0:T(8,128)(2,1)S(1)}, bf16[192,384]{1,0:T(8,128)(2,1)S(1)}, u32[]{:S(2)}, u32[]{:S(2)}) %collective-permute-start.25) | collective-permute-done | bytes 147488 | tf_op jit(solution)/shard_map/ppermute | solution.py:409
  92.5 1.2 %collective-permute-done.23.refs_3_ = bf16[192,384]{1,0:T(8,128)(2,1)S(1)} collective-permute-done((bf16[192,384]{1,0:T(8,128)(2,1)S(1)}, bf16[192,384]{1,0:T(8,128)(2,1)S(1)}, u32[]{:S(2)}, u32[]{:S(2)}) %collective-permute-start.23) | collective-permute-done | bytes 147488 | tf_op jit(solution)/shard_map/ppermute | solution.py:409
  93.7 3.3 %collective-permute-done.26.refs_4_ = bf16[192,384]{1,0:T(8,128)(2,1)S(1)} collective-permute-done((bf16[192,384]{1,0:T(8,128)(2,1)S(1)}, bf16[192,384]{1,0:T(8,128)(2,1)S(1)}, u32[]{:S(2)}, u32[]{:S(2)}) %collective-permute-start.26) | collective-permute-done | bytes 147488 | tf_op jit(solution)/shard_map/ppermute | solution.py:444
  97.0 1.4 %second_solve.1.refs_0_ = bf16[192,384]{1,0:T(8,128)(2,1)S(1)} custom-call(s32[5]{0:T(128)S(1)} %stack.47.place_ref, bf16[192,384]{1,0:T(8,128)(2,1)S(1)} %get-tuple-element.109.refs_0_, bf16[192,384]{1,0:T(8,128)(2,1)S(1)} %collective-permute-done.21.refs_1_, bf16[192,384]{1,0:T(8,128)(2,1)S(1)} %collective-permute-done.22.refs_2_, ...), custom_call_target="tpu_custom_call" | custom-call | flops 339738624 | bytes 1769472 | tf_op jit(solution)/shard_map/second_solve/pallas_call | solution.py:340
  99.0 4.2 %collective-permute-start.28 = (bf16[192,384]{1,0:T(8,128)(2,1)S(1)}, bf16[192,384]{1,0:T(8,128)(2,1)S(1)}, u32[]{:S(2)}, u32[]{:S(2)}) collective-permute-start(bf16[192,384]{1,0:T(8,128)(2,1)S(1)} %second_solve.1.refs_0_), channel_id=1, source_target_pairs={{0,64},{32,96},{64,0},{96,32},{1,65},{33,97},{65,1},{97,33},{2,66}... | collective-permute-start | bytes 442376 | tf_op jit(solution)/shard_map/ppermute | solution.py:450
  103.6 2.8 %collective-permute-start.33 = (bf16[192,384]{1,0:T(8,128)(2,1)S(1)}, bf16[192,384]{1,0:T(8,128)(2,1)S(1)}, u32[]{:S(2)}, u32[]{:S(2)}) collective-permute-start(bf16[192,384]{1,0:T(8,128)(2,1)S(1)} %collective-permute-done.30.refs_4_), channel_id=1, source_target_pairs={{0,96},{32,0},{64,32},{96,64},{1,97},{33,1},{65,33},{97,65},{2,98}... | collective-permute-start | bytes 442376 | tf_op jit(solution)/shard_map/ppermute | solution.py:450
  106.4 1.3 %collective-permute-start.32 = (bf16[192,384]{1,0:T(8,128)(2,1)S(1)}, bf16[192,384]{1,0:T(8,128)(2,1)S(1)}, u32[]{:S(2)}, u32[]{:S(2)}) collective-permute-start(bf16[192,384]{1,0:T(8,128)(2,1)S(1)} %collective-permute-done.30.refs_4_), channel_id=1, source_target_pairs={{0,64},{32,96},{64,0},{96,32},{1,65},{33,97},{65,1},{97,33},{2,66}... | collective-permute-start | bytes 442376 | tf_op jit(solution)/shard_map/ppermute | solution.py:450
  107.8 1.7 %collective-permute-start.31 = (bf16[192,384]{1,0:T(8,128)(2,1)S(1)}, bf16[192,384]{1,0:T(8,128)(2,1)S(1)}, u32[]{:S(2)}, u32[]{:S(2)}) collective-permute-start(bf16[192,384]{1,0:T(8,128)(2,1)S(1)} %collective-permute-done.30.refs_4_), channel_id=1, source_target_pairs={{0,32},{32,64},{64,96},{96,0},{1,33},{33,65},{65,97},{97,1},{2,34}... | collective-permute-start | bytes 442376 | tf_op jit(solution)/shard_map/ppermute | solution.py:450
  109.4 1.8 %join_one.1.refs_8_ = bf16[2,384,1536]{2,1,0:T(8,128)(2,1)} custom-call(s32[5]{0:T(128)S(1)} %stack.47.place_ref, bf16[4,192,384]{2,1,0:T(8,128)(2,1)S(1)} %pad_maximum_fusion.own_ref, bf16[4,192,384]{2,1,0:T(8,128)(2,1)S(1)} %collective-permute-done.19.other_ref), custom_call_target="tpu_custom_call" | custom-call | flops 589824 | bytes 2359296 | tf_op jit(solution)/shard_map/join_one/pallas_call | solution.py:387
  111.3 1.9 %collective-permute-done.32.refs_6_ = bf16[192,384]{1,0:T(8,128)(2,1)S(1)} collective-permute-done((bf16[192,384]{1,0:T(8,128)(2,1)S(1)}, bf16[192,384]{1,0:T(8,128)(2,1)S(1)}, u32[]{:S(2)}, u32[]{:S(2)}) %collective-permute-start.32) | collective-permute-done | bytes 147488 | tf_op jit(solution)/shard_map/ppermute | solution.py:450
  113.1 1.5 %collective-permute-done.31.refs_5_ = bf16[192,384]{1,0:T(8,128)(2,1)S(1)} collective-permute-done((bf16[192,384]{1,0:T(8,128)(2,1)S(1)}, bf16[192,384]{1,0:T(8,128)(2,1)S(1)}, u32[]{:S(2)}, u32[]{:S(2)}) %collective-permute-start.31) | collective-permute-done | bytes 147488 | tf_op jit(solution)/shard_map/ppermute | solution.py:450
  114.7 1.8 %join_two.1 = bf16[2,384,1536]{2,1,0:T(8,128)(2,1)} custom-call(s32[5]{0:T(128)S(1)} %stack.47.place_ref, bf16[192,384]{1,0:T(8,128)(2,1)S(1)} %second_solve.1.refs_0_, bf16[192,384]{1,0:T(8,128)(2,1)S(1)} %collective-permute-done.27.refs_1_, bf16[192,384]{1,0:T(8,128)(2,1)S(1)} %collective-permute-done.28.refs_2_, ...), custom_call_target="tpu_custom_call", output_to_operand_aliasing={{}: (9, {})} | custom-call | flops 589824 | bytes 2359296 | tf_op jit(solution)/shard_map/join_two/pallas_call | solution.py:387
  (45 shorter events, 3.5 us)
Async XLA Ops:
  6.6 7.2 %collective-permute-start = (bf16[192,384]{1,0:T(8,128)(2,1)S(1)}, bf16[192,384]{1,0:T(8,128)(2,1)S(1)}, u32[]{:S(2)}, u32[]{:S(2)}) collective-permute-start(bf16[192,384]{1,0:T(8,128)(2,1)S(1)} %get-tuple-element.73), channel_id=1, source_target_pairs={{0,64},{1,65},{2,66},{3,67},{4,68},{5,69},{6,70},{7,71},{8,72},{9,... | collective-permute-start | bytes 442376 | tf_op jit(solution)/shard_map/ppermute | solution.py:409
  9.9 7.7 %copy-start.1 = (f32[32,32]{1,0:T(8,128)S(1)}, f32[32,32]{1,0:T(8,128)}, u32[]{:S(2)}) copy-start(f32[32,32]{1,0:T(8,128)} %param.9) | copy-start | bytes 12292
  9.9 17.8 %copy-start = (f32[2,384,384]{2,1,0:T(8,128)S(1)}, f32[2,384,384]{2,1,0:T(8,128)}, u32[]{:S(2)}) copy-start(f32[2,384,384]{2,1,0:T(8,128)} %param.8) | copy-start | bytes 3538948
  13.8 8.1 %collective-permute-start.1 = (bf16[192,384]{1,0:T(8,128)(2,1)S(1)}, bf16[192,384]{1,0:T(8,128)(2,1)S(1)}, u32[]{:S(2)}, u32[]{:S(2)}) collective-permute-start(bf16[192,384]{1,0:T(8,128)(2,1)S(1)} %get-tuple-element.81), channel_id=1, source_target_pairs={{0,32},{1,33},{2,34},{3,35},{4,36},{5,37},{6,38},{7,39},{8,40},{9,... | collective-permute-start | bytes 442376 | tf_op jit(solution)/shard_map/ppermute | solution.py:409
  15.4 10.3 %collective-permute-start.2 = (bf16[192,384]{1,0:T(8,128)(2,1)S(1)}, bf16[192,384]{1,0:T(8,128)(2,1)S(1)}, u32[]{:S(2)}, u32[]{:S(2)}) collective-permute-start(bf16[192,384]{1,0:T(8,128)(2,1)S(1)} %get-tuple-element.82), channel_id=1, source_target_pairs={{0,96},{1,97},{2,98},{3,99},{4,100},{5,101},{6,102},{7,103},{8,104... | collective-permute-start | bytes 442376 | tf_op jit(solution)/shard_map/ppermute | solution.py:409
  17.7 14.0 %collective-permute-start.3 = (bf16[192,384]{1,0:T(8,128)(2,1)S(1)}, bf16[192,384]{1,0:T(8,128)(2,1)S(1)}, u32[]{:S(2)}, u32[]{:S(2)}) collective-permute-start(bf16[192,384]{1,0:T(8,128)(2,1)S(1)} %get-tuple-element.86), channel_id=1, source_target_pairs={{0,64},{1,65},{2,66},{3,67},{4,68},{5,69},{6,70},{7,71},{8,72},{9,... | collective-permute-start | bytes 442376 | tf_op jit(solution)/shard_map/ppermute | solution.py:409
  18.5 13.2 %collective-permute-start.4 = (bf16[192,384]{1,0:T(8,128)(2,1)S(1)}, bf16[192,384]{1,0:T(8,128)(2,1)S(1)}, u32[]{:S(2)}, u32[]{:S(2)}) collective-permute-start(bf16[192,384]{1,0:T(8,128)(2,1)S(1)} %get-tuple-element.87), channel_id=1, source_target_pairs={{0,32},{1,33},{2,34},{3,35},{4,36},{5,37},{6,38},{7,39},{8,40},{9,... | collective-permute-start | bytes 442376 | tf_op jit(solution)/shard_map/ppermute | solution.py:409
  19.7 12.0 %collective-permute-start.5 = (bf16[192,384]{1,0:T(8,128)(2,1)S(1)}, bf16[192,384]{1,0:T(8,128)(2,1)S(1)}, u32[]{:S(2)}, u32[]{:S(2)}) collective-permute-start(bf16[192,384]{1,0:T(8,128)(2,1)S(1)} %get-tuple-element.88), channel_id=1, source_target_pairs={{0,96},{1,97},{2,98},{3,99},{4,100},{5,101},{6,102},{7,103},{8,104... | collective-permute-start | bytes 442376 | tf_op jit(solution)/shard_map/ppermute | solution.py:409
  25.8 5.9 %collective-permute-start.6 = (bf16[192,384]{1,0:T(8,128)(2,1)S(1)}, bf16[192,384]{1,0:T(8,128)(2,1)S(1)}, u32[]{:S(2)}, u32[]{:S(2)}) collective-permute-start(bf16[192,384]{1,0:T(8,128)(2,1)S(1)} %add_up.2), channel_id=1, source_target_pairs={{0,16},{16,0},{1,17},{17,1},{2,18},{18,2},{3,19},{19,3},{4,20},{20... | collective-permute-start | bytes 442376 | tf_op jit(solution)/shard_map/ppermute | solution.py:444
  33.5 17.2 %collective-permute-start.8 = (bf16[192,384]{1,0:T(8,128)(2,1)S(1)}, bf16[192,384]{1,0:T(8,128)(2,1)S(1)}, u32[]{:S(2)}, u32[]{:S(2)}) collective-permute-start(bf16[192,384]{1,0:T(8,128)(2,1)S(1)} %get-tuple-element.90), channel_id=1, source_target_pairs={{0,10},{1,11},{2,26},{3,27},{4,46},{5,47},{6,62},{7,63},{8,66},{9,... | collective-permute-start | bytes 442376 | tf_op jit(solution)/shard_map/ppermute | solution.py:409
  39.6 11.1 %collective-permute-start.7 = (bf16[192,384]{1,0:T(8,128)(2,1)S(1)}, bf16[192,384]{1,0:T(8,128)(2,1)S(1)}, u32[]{:S(2)}, u32[]{:S(2)}) collective-permute-start(bf16[192,384]{1,0:T(8,128)(2,1)S(1)} %get-tuple-element.90), channel_id=1, source_target_pairs={{0,0},{1,1},{2,16},{3,17},{4,36},{5,37},{6,52},{7,53},{8,72},{9,73... | collective-permute-start | bytes 442376 | tf_op jit(solution)/shard_map/ppermute | solution.py:409
  40.3 10.8 %collective-permute-start.11 = (bf16[192,384]{1,0:T(8,128)(2,1)S(1)}, bf16[192,384]{1,0:T(8,128)(2,1)S(1)}, u32[]{:S(2)}, u32[]{:S(2)}) collective-permute-start(bf16[192,384]{1,0:T(8,128)(2,1)S(1)} %get-tuple-element.95), channel_id=1, source_target_pairs={{0,96},{32,0},{64,32},{96,64},{1,97},{33,1},{65,33},{97,65},{2,98}... | collective-permute-start | bytes 442376 | tf_op jit(solution)/shard_map/ppermute | solution.py:450
  46.8 6.8 %collective-permute-start.10 = (bf16[192,384]{1,0:T(8,128)(2,1)S(1)}, bf16[192,384]{1,0:T(8,128)(2,1)S(1)}, u32[]{:S(2)}, u32[]{:S(2)}) collective-permute-start(bf16[192,384]{1,0:T(8,128)(2,1)S(1)} %get-tuple-element.95), channel_id=1, source_target_pairs={{0,64},{32,96},{64,0},{96,32},{1,65},{33,97},{65,1},{97,33},{2,66}... | collective-permute-start | bytes 442376 | tf_op jit(solution)/shard_map/ppermute | solution.py:450
  46.8 7.9 %collective-permute-start.9 = (bf16[192,384]{1,0:T(8,128)(2,1)S(1)}, bf16[192,384]{1,0:T(8,128)(2,1)S(1)}, u32[]{:S(2)}, u32[]{:S(2)}) collective-permute-start(bf16[192,384]{1,0:T(8,128)(2,1)S(1)} %get-tuple-element.95), channel_id=1, source_target_pairs={{0,32},{32,64},{64,96},{96,0},{1,33},{33,65},{65,97},{97,1},{2,34}... | collective-permute-start | bytes 442376 | tf_op jit(solution)/shard_map/ppermute | solution.py:450
  54.8 6.8 %collective-permute-start.14 = (bf16[2,192,384]{2,1,0:T(8,128)(2,1)S(1)}, bf16[2,192,384]{2,1,0:T(8,128)(2,1)S(1)}, u32[]{:S(2)}, u32[]{:S(2)}) collective-permute-start(bf16[2,192,384]{2,1,0:T(8,128)(2,1)S(1)} %pad_maximum_fusion.1.refs_0_), channel_id=1, source_target_pairs={{0,12},{4,0},{8,4},{12,8},{1,13},{5,1},{9,5},{13,9},{2,14},{6,2},{... | collective-permute-start | bytes 884744 | tf_op jit(solution)/shard_map/ppermute | solution.py:450
  55.8 8.3 %collective-permute-start.13 = (bf16[2,192,384]{2,1,0:T(8,128)(2,1)S(1)}, bf16[2,192,384]{2,1,0:T(8,128)(2,1)S(1)}, u32[]{:S(2)}, u32[]{:S(2)}) collective-permute-start(bf16[2,192,384]{2,1,0:T(8,128)(2,1)S(1)} %pad_maximum_fusion.1.refs_0_), channel_id=1, source_target_pairs={{0,8},{4,12},{8,0},{12,4},{1,9},{5,13},{9,1},{13,5},{2,10},{6,14},... | collective-permute-start | bytes 884744 | tf_op jit(solution)/shard_map/ppermute | solution.py:450
  55.8 11.4 %collective-permute-start.12 = (bf16[2,192,384]{2,1,0:T(8,128)(2,1)S(1)}, bf16[2,192,384]{2,1,0:T(8,128)(2,1)S(1)}, u32[]{:S(2)}, u32[]{:S(2)}) collective-permute-start(bf16[2,192,384]{2,1,0:T(8,128)(2,1)S(1)} %pad_maximum_fusion.1.refs_0_), channel_id=1, source_target_pairs={{0,4},{4,8},{8,12},{12,0},{1,5},{5,9},{9,13},{13,1},{2,6},{6,10},{... | collective-permute-start | bytes 884744 | tf_op jit(solution)/shard_map/ppermute | solution.py:450
  57.0 13.0 %collective-permute-start.19 = (bf16[4,192,384]{2,1,0:T(8,128)(2,1)S(1)}, bf16[4,192,384]{2,1,0:T(8,128)(2,1)S(1)}, u32[]{:S(2)}, u32[]{:S(2)}) collective-permute-start(bf16[4,192,384]{2,1,0:T(8,128)(2,1)S(1)} %pad_maximum_fusion.own_ref), channel_id=1, source_target_pairs={{0,16},{16,0},{1,17},{17,1},{2,18},{18,2},{3,19},{19,3},{4,20},{20... | collective-permute-start | bytes 1769480 | tf_op jit(solution)/shard_map/ppermute | solution.py:475
  57.7 12.3 %collective-permute-start.15 = (bf16[2,192,384]{2,1,0:T(8,128)(2,1)S(1)}, bf16[2,192,384]{2,1,0:T(8,128)(2,1)S(1)}, u32[]{:S(2)}, u32[]{:S(2)}) collective-permute-start(bf16[2,192,384]{2,1,0:T(8,128)(2,1)S(1)} %pad_maximum_fusion.1.refs_0_), channel_id=1, source_target_pairs={{0,1},{1,0},{2,3},{3,2},{4,5},{5,4},{6,7},{7,6},{8,9},{9,8},{10,11... | collective-permute-start | bytes 884744 | tf_op jit(solution)/shard_map/ppermute | solution.py:476
  61.6 8.3 %collective-permute-start.18 = (bf16[2,192,384]{2,1,0:T(8,128)(2,1)S(1)}, bf16[2,192,384]{2,1,0:T(8,128)(2,1)S(1)}, u32[]{:S(2)}, u32[]{:S(2)}) collective-permute-start(bf16[2,192,384]{2,1,0:T(8,128)(2,1)S(1)} %collective-permute-done.14.refs_3_), channel_id=1, source_target_pairs={{0,1},{1,0},{2,3},{3,2},{4,5},{5,4},{6,7},{7,6},{8,9},{9,8},{10,11... | collective-permute-start | bytes 884744 | tf_op jit(solution)/shard_map/ppermute | solution.py:476
  64.1 5.8 %collective-permute-start.17 = (bf16[2,192,384]{2,1,0:T(8,128)(2,1)S(1)}, bf16[2,192,384]{2,1,0:T(8,128)(2,1)S(1)}, u32[]{:S(2)}, u32[]{:S(2)}) collective-permute-start(bf16[2,192,384]{2,1,0:T(8,128)(2,1)S(1)} %collective-permute-done.13.refs_2_), channel_id=1, source_target_pairs={{0,1},{1,0},{2,3},{3,2},{4,5},{5,4},{6,7},{7,6},{8,9},{9,8},{10,11... | collective-permute-start | bytes 884744 | tf_op jit(solution)/shard_map/ppermute | solution.py:476
  67.2 2.8 %collective-permute-start.16 = (bf16[2,192,384]{2,1,0:T(8,128)(2,1)S(1)}, bf16[2,192,384]{2,1,0:T(8,128)(2,1)S(1)}, u32[]{:S(2)}, u32[]{:S(2)}) collective-permute-start(bf16[2,192,384]{2,1,0:T(8,128)(2,1)S(1)} %collective-permute-done.12.refs_1_), channel_id=1, source_target_pairs={{0,1},{1,0},{2,3},{3,2},{4,5},{5,4},{6,7},{7,6},{8,9},{9,8},{10,11... | collective-permute-start | bytes 884744 | tf_op jit(solution)/shard_map/ppermute | solution.py:476
  72.9 7.8 %collective-permute-start.20 = (bf16[192,384]{1,0:T(8,128)(2,1)S(1)}, bf16[192,384]{1,0:T(8,128)(2,1)S(1)}, u32[]{:S(2)}, u32[]{:S(2)}) collective-permute-start(bf16[192,384]{1,0:T(8,128)(2,1)S(1)} %get-tuple-element.111), channel_id=1, source_target_pairs={{0,64},{1,65},{2,66},{3,67},{4,68},{5,69},{6,70},{7,71},{8,72},{9,... | collective-permute-start | bytes 442376 | tf_op jit(solution)/shard_map/ppermute | solution.py:409
  80.7 6.8 %collective-permute-start.24 = (bf16[192,384]{1,0:T(8,128)(2,1)S(1)}, bf16[192,384]{1,0:T(8,128)(2,1)S(1)}, u32[]{:S(2)}, u32[]{:S(2)}) collective-permute-start(bf16[192,384]{1,0:T(8,128)(2,1)S(1)} %get-tuple-element.123), channel_id=1, source_target_pairs={{0,32},{1,33},{2,34},{3,35},{4,36},{5,37},{6,38},{7,39},{8,40},{9,... | collective-permute-start | bytes 442376 | tf_op jit(solution)/shard_map/ppermute | solution.py:409
  80.7 11.0 %collective-permute-start.25 = (bf16[192,384]{1,0:T(8,128)(2,1)S(1)}, bf16[192,384]{1,0:T(8,128)(2,1)S(1)}, u32[]{:S(2)}, u32[]{:S(2)}) collective-permute-start(bf16[192,384]{1,0:T(8,128)(2,1)S(1)} %get-tuple-element.124), channel_id=1, source_target_pairs={{0,96},{1,97},{2,98},{3,99},{4,100},{5,101},{6,102},{7,103},{8,104... | collective-permute-start | bytes 442376 | tf_op jit(solution)/shard_map/ppermute | solution.py:409
  81.9 10.5 %collective-permute-start.21 = (bf16[192,384]{1,0:T(8,128)(2,1)S(1)}, bf16[192,384]{1,0:T(8,128)(2,1)S(1)}, u32[]{:S(2)}, u32[]{:S(2)}) collective-permute-start(bf16[192,384]{1,0:T(8,128)(2,1)S(1)} %get-tuple-element.118), channel_id=1, source_target_pairs={{0,64},{1,65},{2,66},{3,67},{4,68},{5,69},{6,70},{7,71},{8,72},{9,... | collective-permute-start | bytes 442376 | tf_op jit(solution)/shard_map/ppermute | solution.py:409
  84.8 7.7 %collective-permute-start.22 = (bf16[192,384]{1,0:T(8,128)(2,1)S(1)}, bf16[192,384]{1,0:T(8,128)(2,1)S(1)}, u32[]{:S(2)}, u32[]{:S(2)}) collective-permute-start(bf16[192,384]{1,0:T(8,128)(2,1)S(1)} %get-tuple-element.119), channel_id=1, source_target_pairs={{0,32},{1,33},{2,34},{3,35},{4,36},{5,37},{6,38},{7,39},{8,40},{9,... | collective-permute-start | bytes 442376 | tf_op jit(solution)/shard_map/ppermute | solution.py:409
  84.8 8.9 %collective-permute-start.23 = (bf16[192,384]{1,0:T(8,128)(2,1)S(1)}, bf16[192,384]{1,0:T(8,128)(2,1)S(1)}, u32[]{:S(2)}, u32[]{:S(2)}) collective-permute-start(bf16[192,384]{1,0:T(8,128)(2,1)S(1)} %get-tuple-element.120), channel_id=1, source_target_pairs={{0,96},{1,97},{2,98},{3,99},{4,100},{5,101},{6,102},{7,103},{8,104... | collective-permute-start | bytes 442376 | tf_op jit(solution)/shard_map/ppermute | solution.py:409
  91.8 5.2 %collective-permute-start.26 = (bf16[192,384]{1,0:T(8,128)(2,1)S(1)}, bf16[192,384]{1,0:T(8,128)(2,1)S(1)}, u32[]{:S(2)}, u32[]{:S(2)}) collective-permute-start(bf16[192,384]{1,0:T(8,128)(2,1)S(1)} %add_up.3), channel_id=1, source_target_pairs={{0,16},{16,0},{1,17},{17,1},{2,18},{18,2},{3,19},{19,3},{4,20},{20... | collective-permute-start | bytes 442376 | tf_op jit(solution)/shard_map/ppermute | solution.py:444
  98.4 5.2 %collective-permute-start.30 = (bf16[192,384]{1,0:T(8,128)(2,1)S(1)}, bf16[192,384]{1,0:T(8,128)(2,1)S(1)}, u32[]{:S(2)}, u32[]{:S(2)}) collective-permute-start(bf16[192,384]{1,0:T(8,128)(2,1)S(1)} %second_solve.1.refs_0_), channel_id=1, source_target_pairs={{0,16},{16,0},{1,17},{17,1},{2,18},{18,2},{3,19},{19,3},{4,20},{20... | collective-permute-start | bytes 442376 | tf_op jit(solution)/shard_map/ppermute | solution.py:488
  99.0 8.7 %collective-permute-start.29 = (bf16[192,384]{1,0:T(8,128)(2,1)S(1)}, bf16[192,384]{1,0:T(8,128)(2,1)S(1)}, u32[]{:S(2)}, u32[]{:S(2)}) collective-permute-start(bf16[192,384]{1,0:T(8,128)(2,1)S(1)} %second_solve.1.refs_0_), channel_id=1, source_target_pairs={{0,96},{32,0},{64,32},{96,64},{1,97},{33,1},{65,33},{97,65},{2,98}... | collective-permute-start | bytes 442376 | tf_op jit(solution)/shard_map/ppermute | solution.py:450
  99.0 12.2 %collective-permute-start.28 = (bf16[192,384]{1,0:T(8,128)(2,1)S(1)}, bf16[192,384]{1,0:T(8,128)(2,1)S(1)}, u32[]{:S(2)}, u32[]{:S(2)}) collective-permute-start(bf16[192,384]{1,0:T(8,128)(2,1)S(1)} %second_solve.1.refs_0_), channel_id=1, source_target_pairs={{0,64},{32,96},{64,0},{96,32},{1,65},{33,97},{65,1},{97,33},{2,66}... | collective-permute-start | bytes 442376 | tf_op jit(solution)/shard_map/ppermute | solution.py:450
  103.2 8.1 %collective-permute-start.27 = (bf16[192,384]{1,0:T(8,128)(2,1)S(1)}, bf16[192,384]{1,0:T(8,128)(2,1)S(1)}, u32[]{:S(2)}, u32[]{:S(2)}) collective-permute-start(bf16[192,384]{1,0:T(8,128)(2,1)S(1)} %second_solve.1.refs_0_), channel_id=1, source_target_pairs={{0,32},{32,64},{64,96},{96,0},{1,33},{33,65},{65,97},{97,1},{2,34}... | collective-permute-start | bytes 442376 | tf_op jit(solution)/shard_map/ppermute | solution.py:450
  103.6 7.6 %collective-permute-start.33 = (bf16[192,384]{1,0:T(8,128)(2,1)S(1)}, bf16[192,384]{1,0:T(8,128)(2,1)S(1)}, u32[]{:S(2)}, u32[]{:S(2)}) collective-permute-start(bf16[192,384]{1,0:T(8,128)(2,1)S(1)} %collective-permute-done.30.refs_4_), channel_id=1, source_target_pairs={{0,96},{32,0},{64,32},{96,64},{1,97},{33,1},{65,33},{97,65},{2,98}... | collective-permute-start | bytes 442376 | tf_op jit(solution)/shard_map/ppermute | solution.py:450
  106.4 6.7 %collective-permute-start.32 = (bf16[192,384]{1,0:T(8,128)(2,1)S(1)}, bf16[192,384]{1,0:T(8,128)(2,1)S(1)}, u32[]{:S(2)}, u32[]{:S(2)}) collective-permute-start(bf16[192,384]{1,0:T(8,128)(2,1)S(1)} %collective-permute-done.30.refs_4_), channel_id=1, source_target_pairs={{0,64},{32,96},{64,0},{96,32},{1,65},{33,97},{65,1},{97,33},{2,66}... | collective-permute-start | bytes 442376 | tf_op jit(solution)/shard_map/ppermute | solution.py:450
  107.8 6.9 %collective-permute-start.31 = (bf16[192,384]{1,0:T(8,128)(2,1)S(1)}, bf16[192,384]{1,0:T(8,128)(2,1)S(1)}, u32[]{:S(2)}, u32[]{:S(2)}) collective-permute-start(bf16[192,384]{1,0:T(8,128)(2,1)S(1)} %collective-permute-done.30.refs_4_), channel_id=1, source_target_pairs={{0,32},{32,64},{64,96},{96,0},{1,33},{33,65},{65,97},{97,1},{2,34}... | collective-permute-start | bytes 442376 | tf_op jit(solution)/shard_map/ppermute | solution.py:450

commit v11 on v10

--- a/solution.py
+++ b/solution.py
@@ -73,7 +73,7 @@
 
 
 def first_product_kernel(place_ref, memory_ref, resident_ref, *refs):
-    out_refs, lhs_ref, odd_ref, even_ref, turned_ref, sems = refs[:4], *refs[4:]
+    out_refs, lhs_ref, even_ref, odd_ref, turned_ref, sems = refs[:4], *refs[4:]
     depth, cols = odd_ref.shape
     tile = cols // TILES
     parity = place_ref[Y] & 1
@@ -89,17 +89,17 @@
     memory_copy = pltpu.make_async_copy(memory_ref.at[0], lhs_ref, sems.at[2 * TILES])
     odd = [tile_copy(odd_ref, 1, i) for i in range(TILES)]
     even = [tile_copy(even_ref, 0, i) for i in range(TILES)]
-    for copy in (memory_copy, *even):
+    for copy in (memory_copy, *odd):
         copy.start()
     memory_copy.wait()
-    for i, copy in enumerate(even):
+    for i, copy in enumerate(odd):
         copy.wait()
-        odd[i].start()
+        even[i].start()
         at = slice(i * tile, (i + 1) * tile)
-        product = jnp.dot(lhs_ref[...], even_ref[:, at], preferred_element_type=f32)
+        product = jnp.dot(lhs_ref[...], odd_ref[:, at], preferred_element_type=f32)
         turned_ref[at, :] = product.T.astype(bf16)
     store_shares(place_ref, turned_ref, out_refs)
-    for copy in odd:
+    for copy in even:
         copy.wait()
 
 
@@ -109,7 +109,7 @@
     width = cols // 8
     outs = [((width, rows), 4), ((rows, depth), 1), ((depth, cols // 2), 1)]
     shapes = [jax.ShapeDtypeStruct(shape, bf16) for shape, count in outs for _ in range(count)]
-    *even, lhs, odd_resident = pl.pallas_call(
+    *odd, lhs, even_resident = pl.pallas_call(
         first_product_kernel,
         in_specs=[SMEM] + [pl.BlockSpec(memory_space=pltpu.HBM)] * 2,
         out_specs=[VMEM] * 6,
@@ -123,7 +123,7 @@
         cost_estimate=cost(rows * depth * cols, 4 * depth * cols),
         name="first_product",
     )(place, memory, resident)
-    return even, lhs, odd_resident
+    return odd, lhs, even_resident
 
 
 def depth_half(place_ref, side, resident_ref):
@@ -190,8 +190,8 @@
     return pltpu.make_async_copy(resident_ref.at[:, at], out_ref, sem)
 
 
-def bring_soon_kernel(
-    place_ref, memory_ref, previous_ref, resident_ref, memory_out, one_out, two_out, even_out, prior_ref, turned_ref, sems
+def bring_odd_kernel(
+    place_ref, memory_ref, previous_ref, resident_ref, memory_out, one_out, two_out, odd_out, prior_ref, turned_ref, sems
 ):
     width, rows = one_out.shape
     start = position(place_ref[Y]) * 2 * width
@@ -199,7 +199,7 @@
     copies = [
         pltpu.make_async_copy(previous_ref.at[:, :, cols], prior_ref, sems.at[0]),
         pltpu.make_async_copy(memory_ref.at[1], memory_out, sems.at[1]),
-        half_copy(0, place_ref, resident_ref, even_out, sems.at[2]),
+        half_copy(1, place_ref, resident_ref, odd_out, sems.at[2]),
     ]
     for copy in copies:
         copy.start()
@@ -212,13 +212,13 @@
         copy.wait()
 
 
-def bring_soon(place, memory, previous, resident):
+def bring_odd(place, memory, previous, resident):
     _, rows, depth = memory.shape
     cols = resident.shape[1]
     width = previous.shape[2] // 8
     shapes = [(rows, depth), (width, rows), (width, rows), (depth, cols // 2)]
     return pl.pallas_call(
-        bring_soon_kernel,
+        bring_odd_kernel,
         in_specs=[SMEM] + [HBM] * 3,
         out_specs=[VMEM] * 4,
         out_shape=[jax.ShapeDtypeStruct(shape, bf16) for shape in shapes],
@@ -229,27 +229,27 @@
         ],
         compiler_params=params(6),
         cost_estimate=cost(0, depth * (2 * rows + cols)),
-        name="bring_soon",
+        name="bring_odd",
     )(place, memory, previous, resident)
 
 
-def bring_late_kernel(place_ref, resident_ref, odd_out, sem):
-    copy = half_copy(1, place_ref, resident_ref, odd_out, sem)
+def bring_even_kernel(place_ref, resident_ref, even_out, sem):
+    copy = half_copy(0, place_ref, resident_ref, even_out, sem)
     copy.start()
     copy.wait()
 
 
-def bring_late(place, resident):
+def bring_even(place, resident):
     depth, cols = resident.shape
     return pl.pallas_call(
-        bring_late_kernel,
+        bring_even_kernel,
         in_specs=[SMEM, HBM],
         out_specs=VMEM,
         out_shape=jax.ShapeDtypeStruct((depth, cols // 2), bf16),
         scratch_shapes=[pltpu.SemaphoreType.DMA],
         compiler_params=params(4),
         cost_estimate=cost(0, depth * cols),
-        name="bring_late",
+        name="bring_even",
     )(place, resident)
 
 
@@ -321,18 +321,18 @@
 
 
 def first_solve_kernel(place_ref, *refs):
-    front_ref, energy_ref = refs[8:]
-    front = solve_into(refs[:5], refs[5], refs[6])
+    front_ref, energy_ref = refs[11:]
+    front = solve_into(refs[:8], refs[8], refs[9])
     front_ref[...] = front
     values = front.astype(f32)
     mirror = flipped(values)
     rows, cols = values.shape
-    coupling = jnp.tile(refs[7][...], (rows // ORB, cols // 128))
+    coupling = jnp.tile(refs[10][...], (rows // ORB, cols // 128))
     energy_ref[...] = (mirror * mirror * values * coupling).astype(bf16)
 
 
 def second_solve_kernel(place_ref, *refs):
-    refs[7][...] = solve_into(refs[:5], refs[5], refs[6])
+    refs[10][...] = solve_into(refs[:8], refs[8], refs[9])
 
 
 def solve(kernel, place, parts, prior, inverse, extra, outputs, name):
@@ -413,35 +413,15 @@
     return lambda y, zl, x, zh: (x, zh, x ^ y ^ (2 * flip), zl ^ flip)
 
 
-def sum_kernel(*refs):
-    total = refs[0][...].astype(f32)
-    for ref in refs[1:-1]:
-        total = total + ref[...].astype(f32)
-    refs[-1][...] = total.astype(bf16)
-
-
-def add_up(values):
-    return pl.pallas_call(
-        sum_kernel,
-        in_specs=[VMEM] * len(values),
-        out_specs=VMEM,
-        out_shape=jax.ShapeDtypeStruct(values[0].shape, bf16),
-        compiler_params=params(4),
-        cost_estimate=cost(4 * values[0].size, 10 * values[0].size),
-        name="add_up",
-    )(*values)
-
-
-def scatter(even, odd):
-    def along_y(share, dy):
-        return move(share, lambda y, zl, x, zh: (y ^ dy, zl, x, zh))
-
-    far = along_y(even[3], 2)
-    own_two, far, odd = lax.optimization_barrier((even[2], far, odd))
-    far = [far, along_y(odd[1], 1), along_y(odd[3], 3)]
-    near = [along_y(own_two, 2), along_y(odd[0], 1), along_y(odd[2], 3)]
-    for_twin = add_up([even[1], *far])
-    return [even[0], *near, lax.ppermute(for_twin, "zl", SWAP)], for_twin
+def scatter(shares, first):
+    parts = []
+    for k in (3, 2, 1, 0) if first == 0 else (1, 0, 3, 2):
+        dy, dz = first + 2 * (k >> 1), k & 1
+        if (dy, dz) == (0, 0):
+            parts.append(shares[k])
+        else:
+            parts.append(move(shares[k], lambda y, zl, x, zh: (y ^ dy, zl ^ dz, x, zh)))
+    return parts
 
 
 def spread(pair, axis):
@@ -456,32 +436,34 @@
     coupling = jnp.tile(pair_coupling, (1, 128 // ORB))
 
     resident, memory, previous = in_hbm(resident), in_hbm(memory), in_hbm(previous)
-    even, lhs, odd_resident = first_product(place, memory, resident)
-    lhs, even = lax.optimization_barrier((lhs, even))
-    odd = half_product(place, lhs, odd_resident)
-    parts, for_twin = scatter(even, odd)
-    later, _ = lax.optimization_barrier((place, for_twin))
-    memory, prior_one, prior_two, even_resident = bring_soon(later, memory, previous, resident)
+    odd, lhs, even_resident = first_product(place, memory, resident)
+    odd_parts = scatter(odd, 1)
+    lhs, odd = lax.optimization_barrier((lhs, odd))
+    even = half_product(place, lhs, even_resident)
+    even_parts = scatter(even, 0)
+    place, _, odd_parts = lax.optimization_barrier((place, even[0], odd_parts))
+    memory, prior_one, prior_two, odd_resident = bring_odd(place, memory, previous, resident)
+    parts = odd_parts + even_parts
     front_one, energy = solve(
         first_solve_kernel, place, parts, prior_one, inverse_part[0], [coupling], 2, "first_solve"
     )
     pair = [move(energy, turn(0)), move(energy, turn(1))]
     ones = spread(front_one, "y")
     later, _ = lax.optimization_barrier((place, energy))
-    odd_resident = bring_late(later, resident)
-    pair, ones, odd_resident = lax.optimization_barrier((pair, ones, odd_resident))
+    even_resident = bring_even(later, resident)
+    pair, ones, even_resident = lax.optimization_barrier((pair, ones, even_resident))
     own = spread(jnp.stack(pair), "x")
     ones = jnp.stack(ones)
     others = lax.ppermute(ones, "zl", SWAP)
     other = [lax.ppermute(pair, "c", SWAP) for pair in own]
     own_lhs = next_memory(0, place, memory, own)
-    early = early_product(place, own_lhs, even_resident)
+    early = early_product(place, own_lhs, odd_resident)
     other, others, early = lax.optimization_barrier((other, others, early))
     other_lhs = next_memory(1, place, memory, other)
-    even = second_product(late_product_kernel, place, early, other_lhs, even_resident, "late_product")
-    own_lhs, even = lax.optimization_barrier((own_lhs, even))
-    odd = second_product(both_product_kernel, place, own_lhs, other_lhs, odd_resident, "both_product")
-    parts, _ = scatter(even, odd)
+    odd = second_product(late_product_kernel, place, early, other_lhs, odd_resident, "late_product")
+    own_lhs, odd = lax.optimization_barrier((own_lhs, odd))
+    even = second_product(both_product_kernel, place, own_lhs, other_lhs, even_resident, "both_product")
+    parts = scatter(odd, 1) + scatter(even, 0)
     (front_two,) = solve(
         second_solve_kernel, place, parts, prior_two, inverse_part[1], [], 1, "second_solve"
     )

time: 117 us -> 113 us (0.966)
  waiting for transfers between devices: 37.3 us -> 34.2 us
    ppermute x12, starting transfers between devices: 19.5 us -> 13.7 us  [spread(): pairs[d] = lax.ppermute(pair, axis, [(i, (i + d) % 4) for i in range(4)])]
    ppermute x14 -> x16, starting transfers between devices: 24.1 us -> 29.9 us  [move(): return lax.ppermute(value, ALL, pairs)]
    ppermute x14 -> x16, waiting for transfers between devices: 16.5 us -> 11.8 us  [move(): return lax.ppermute(value, ALL, pairs)]
    ppermute x12, waiting for transfers between devices: 17 us -> 20.9 us  [spread(): pairs[d] = lax.ppermute(pair, axis, [(i, (i + d) % 4) for i in range(4)])]
    ppermute x2 -> x0, waiting for transfers between devices: 3.3 us -> none  [scatter(): return ([even[0], *near, lax.ppermute(for_twin, 'zl', SWAP)], for_twin)]
    ppermute x2 -> x0, starting transfers between devices: 2.6 us -> none  [scatter(): return ([even[0], *near, lax.ppermute(for_twin, 'zl', SWAP)], for_twin)]
    pallas_call x4 -> x2, Pallas kernels: 6.89 us -> 6.72 us  [the longest x1 3.83 us: bring_odd(): pl.pallas_call(bring_odd_kernel, in_specs=[SMEM] + [HBM] * 3, out_specs=[...]
  transfers between devices with their start and end apart: 34 -> 34, of which waited for: 17 -> 12; matrix products, arithmetic and copies ran while one was open for 0% -> 0% of each run, Pallas kernels for 14% -> 15%
where the time goes in v11:
time: 113 us
  starting transfers between devices  46.5 us (41%)
  waiting for transfers between devices  34.2 us (30%)
  Pallas kernels  31 us (27%)
    ppermute x16, starting transfers between devices, move(): return lax.ppermute(value, ALL, pairs)  29.9 us
    ppermute x12, waiting for transfers between devices, spread(): pairs[d] = lax.ppermute(pair, axis, [(i, (i + d) % 4) for i in range(4)])  20.9 us
    ppermute x12, starting transfers between devices, spread(): pairs[d] = lax.ppermute(pair, axis, [(i, (i + d) % 4) for i in range(4)])  13.7 us
    ppermute x16, waiting for transfers between devices, move(): return lax.ppermute(value, ALL, pairs)  11.8 us
    pallas_call x1, Pallas kernels, first_product(): pl.pallas_call(first_product_kernel, in_specs=[SMEM] + [pl.BlockSpec(memo...  6.5 us
    pallas_call x2, Pallas kernels, second_product(): pl.pallas_call(kernel, in_specs=[SMEM] + [VMEM] * 3, out_specs=[VMEM] * 4...  4.41 us
    pallas_call x1, Pallas kernels, bring_odd(): pl.pallas_call(bring_odd_kernel, in_specs=[SMEM] + [HBM] * 3, out_specs=[...  3.83 us
    pallas_call x2, Pallas kernels, join(): pl.pallas_call(kernel, in_specs=in_specs, out_specs=HBM, out_shape=jax.Sh...  3.61 us
  transfers between devices with their start and end apart: 34, of which 12 were waited for; matrix products, arithmetic and copies ran while one was open for 0% of the time, Pallas kernels for 15%

profile of v11, /device:TPU:0, one launch (start us, length us, event | category | flops | bytes accessed | tf_op | source)
XLA Modules:
  0.0 112.6 jit_solution(1585436304796822947)
XLA Ops:
  0.1 6.5 %first_product.1 = (bf16[192,384]{1,0:T(8,128)(2,1)S(1)}, bf16[192,384]{1,0:T(8,128)(2,1)S(1)}, bf16[192,384]{1,0:T(8,128)(2,1)S(1)}, bf16[192,384]{1,0:T(8,128)...) custom-call(s32[5]{0:T(128)S(1)} %stack.47.place_ref, bf16[2,384,3072]{2,1,0:T(8,128)(2,1)} %memory_ref.3, ...), custom_call_target="tpu_custom_call" | custom-call | flops 1811939328 | bytes 18874368 | tf_op jit(solution)/shard_map/first_product/pallas_call | solution.py:112
  6.6 1.7 %collective-permute-start.1 = (bf16[192,384]{1,0:T(8,128)(2,1)S(1)}, bf16[192,384]{1,0:T(8,128)(2,1)S(1)}, u32[]{:S(2)}, u32[]{:S(2)}) collective-permute-start(bf16[192,384]{1,0:T(8,128)(2,1)S(1)} %get-tuple-element.55), channel_id=1, source_target_pairs={{0,32},{1,33},{2,34},{3,35},{4,36},{5,37},{6,38},{7,39},{8,40},{9,... | collective-permute-start | bytes 442376 | tf_op jit(solution)/shard_map/ppermute | solution.py:409
  8.3 1.8 %collective-permute-start = (bf16[192,384]{1,0:T(8,128)(2,1)S(1)}, bf16[192,384]{1,0:T(8,128)(2,1)S(1)}, u32[]{:S(2)}, u32[]{:S(2)}) collective-permute-start(bf16[192,384]{1,0:T(8,128)(2,1)S(1)} %get-tuple-element.56), channel_id=1, source_target_pairs={{0,48},{1,49},{2,50},{3,51},{4,52},{5,53},{6,54},{7,55},{8,56},{9,... | collective-permute-start | bytes 442376 | tf_op jit(solution)/shard_map/ppermute | solution.py:409
  10.1 3.0 %collective-permute-start.3 = (bf16[192,384]{1,0:T(8,128)(2,1)S(1)}, bf16[192,384]{1,0:T(8,128)(2,1)S(1)}, u32[]{:S(2)}, u32[]{:S(2)}) collective-permute-start(bf16[192,384]{1,0:T(8,128)(2,1)S(1)} %get-tuple-element.57), channel_id=1, source_target_pairs={{0,96},{1,97},{2,98},{3,99},{4,100},{5,101},{6,102},{7,103},{8,104... | collective-permute-start | bytes 442376 | tf_op jit(solution)/shard_map/ppermute | solution.py:409
  13.2 2.7 %half_product.1 = (bf16[192,384]{1,0:T(8,128)(2,1)S(1)}, bf16[192,384]{1,0:T(8,128)(2,1)S(1)}, bf16[192,384]{1,0:T(8,128)(2,1)S(1)}, bf16[192,384]{1,0:T(8,128)(2,1)S(1)}) custom-call(s32[5]{0:T(128)S(1)} %stack.47.place_ref, bf16[384,3072]{1,0:T(8,128)(2,1)S(1)} %get-tuple-element.59.lhs_ref, bf16[3072,768]{1,0:T(8,128)(2,1)S(1)} %get-tuple-element.60.resident_ref), custom_call_target="tpu_custom_call" | custom-call | flops 1811939328 | bytes 294912 | tf_op jit(solution)/shard_map/half_product/pallas_call | solution.py:60
  15.8 3.2 %collective-permute-start.4 = (bf16[192,384]{1,0:T(8,128)(2,1)S(1)}, bf16[192,384]{1,0:T(8,128)(2,1)S(1)}, u32[]{:S(2)}, u32[]{:S(2)}) collective-permute-start(bf16[192,384]{1,0:T(8,128)(2,1)S(1)} %get-tuple-element.68), channel_id=1, source_target_pairs={{0,80},{1,81},{2,82},{3,83},{4,84},{5,85},{6,86},{7,87},{8,88},{9,... | collective-permute-start | bytes 442376 | tf_op jit(solution)/shard_map/ppermute | solution.py:409
  19.1 1.6 %collective-permute-start.5 = (bf16[192,384]{1,0:T(8,128)(2,1)S(1)}, bf16[192,384]{1,0:T(8,128)(2,1)S(1)}, u32[]{:S(2)}, u32[]{:S(2)}) collective-permute-start(bf16[192,384]{1,0:T(8,128)(2,1)S(1)} %get-tuple-element.69), channel_id=1, source_target_pairs={{0,64},{1,65},{2,66},{3,67},{4,68},{5,69},{6,70},{7,71},{8,72},{9,... | collective-permute-start | bytes 442376 | tf_op jit(solution)/shard_map/ppermute | solution.py:409
  21.2 5.5 %collective-permute-done.2.refs_2_ = bf16[192,384]{1,0:T(8,128)(2,1)S(1)} collective-permute-done((bf16[192,384]{1,0:T(8,128)(2,1)S(1)}, bf16[192,384]{1,0:T(8,128)(2,1)S(1)}, u32[]{:S(2)}, u32[]{:S(2)}) %collective-permute-start.2) | collective-permute-done | bytes 147488 | tf_op jit(solution)/shard_map/ppermute | solution.py:409
  26.7 3.8 %bring_odd.1 = (bf16[384,3072]{1,0:T(8,128)(2,1)S(1)}, bf16[192,384]{1,0:T(8,128)(2,1)S(1)}, bf16[192,384]{1,0:T(8,128)(2,1)S(1)}, bf16[3072,768]{1,0:T(8,128)(2,1)S(1)}) custom-call(s32[5]{0:T(128)S(1)} %stack.47.place_ref, bf16[2,384,3072]{2,1,0:T(8,128)(2,1)} %memory_ref.3, bf16[2,384,1536]{2,1,0:T(8,128)(2,1)} %previous_ref.1, ...), custom_call_target="tpu_custom_call" | custom-call | bytes 7077888 | tf_op jit(solution)/shard_map/bring_odd/pallas_call | solution.py:220
  30.6 1.8 %first_solve.1 = (bf16[192,384]{1,0:T(8,128)(2,1)S(1)}, bf16[192,384]{1,0:T(8,128)(2,1)S(1)}) custom-call(s32[5]{0:T(128)S(1)} %stack.47.place_ref, bf16[192,384]{1,0:T(8,128)(2,1)S(1)} %collective-permute-done.refs_0_, bf16[192,384]{1,0:T(8,128)(2,1)S(1)} %collective-permute-done.1.refs_1_, bf16[192,384]{1,0:T(8,128)(2,1)S(1)} %collective-permute-done.2.refs_2_, ...), custom_call_target="tpu_custom_call" | custom-call | flops 339738624 | bytes 1769472 | tf_op jit(solution)/shard_map/first_solve/pallas_call | solution.py:340
  32.4 6.1 %collective-permute-start.8 = (bf16[192,384]{1,0:T(8,128)(2,1)S(1)}, bf16[192,384]{1,0:T(8,128)(2,1)S(1)}, u32[]{:S(2)}, u32[]{:S(2)}) collective-permute-start(bf16[192,384]{1,0:T(8,128)(2,1)S(1)} %get-tuple-element.72), channel_id=1, source_target_pairs={{0,10},{1,11},{2,26},{3,27},{4,46},{5,47},{6,62},{7,63},{8,66},{9,... | collective-permute-start | bytes 442376 | tf_op jit(solution)/shard_map/ppermute | solution.py:409
  38.5 0.7 collective-permute-start.7
  39.2 3.2 %collective-permute-start.11 = (bf16[192,384]{1,0:T(8,128)(2,1)S(1)}, bf16[192,384]{1,0:T(8,128)(2,1)S(1)}, u32[]{:S(2)}, u32[]{:S(2)}) collective-permute-start(bf16[192,384]{1,0:T(8,128)(2,1)S(1)} %get-tuple-element.77), channel_id=1, source_target_pairs={{0,96},{32,0},{64,32},{96,64},{1,97},{33,1},{65,33},{97,65},{2,98}... | collective-permute-start | bytes 442376 | tf_op jit(solution)/shard_map/ppermute | solution.py:430
  42.4 1.4 %collective-permute-start.10 = (bf16[192,384]{1,0:T(8,128)(2,1)S(1)}, bf16[192,384]{1,0:T(8,128)(2,1)S(1)}, u32[]{:S(2)}, u32[]{:S(2)}) collective-permute-start(bf16[192,384]{1,0:T(8,128)(2,1)S(1)} %get-tuple-element.77), channel_id=1, source_target_pairs={{0,64},{32,96},{64,0},{96,32},{1,65},{33,97},{65,1},{97,33},{2,66}... | collective-permute-start | bytes 442376 | tf_op jit(solution)/shard_map/ppermute | solution.py:430
  43.8 2.9 %bring_even.1.resident_ref = bf16[3072,768]{1,0:T(8,128)(2,1)S(1)} custom-call(s32[5]{0:T(128)S(1)} %stack.47.place_ref, bf16[3072,1536]{1,0:T(8,128)(2,1)} %resident_ref.5), custom_call_target="tpu_custom_call" | custom-call | bytes 4718592 | tf_op jit(solution)/shard_map/bring_even/pallas_call | solution.py:244
  46.7 2.4 %collective-permute-done.10 = bf16[192,384]{1,0:T(8,128)(2,1)S(1)} collective-permute-done((bf16[192,384]{1,0:T(8,128)(2,1)S(1)}, bf16[192,384]{1,0:T(8,128)(2,1)S(1)}, u32[]{:S(2)}, u32[]{:S(2)}) %collective-permute-start.10) | collective-permute-done | bytes 147488 | tf_op jit(solution)/shard_map/ppermute | solution.py:430
  49.1 1.5 %collective-permute-done.9 = bf16[192,384]{1,0:T(8,128)(2,1)S(1)} collective-permute-done((bf16[192,384]{1,0:T(8,128)(2,1)S(1)}, bf16[192,384]{1,0:T(8,128)(2,1)S(1)}, u32[]{:S(2)}, u32[]{:S(2)}) %collective-permute-start.9) | collective-permute-done | bytes 147488 | tf_op jit(solution)/shard_map/ppermute | solution.py:430
  50.7 2.2 %collective-permute-start.14 = (bf16[2,192,384]{2,1,0:T(8,128)(2,1)S(1)}, bf16[2,192,384]{2,1,0:T(8,128)(2,1)S(1)}, u32[]{:S(2)}, u32[]{:S(2)}) collective-permute-start(bf16[2,192,384]{2,1,0:T(8,128)(2,1)S(1)} %pad_maximum_fusion.1.refs_0_), channel_id=1, source_target_pairs={{0,12},{4,0},{8,4},{12,8},{1,13},{5,1},{9,5},{13,9},{2,14},{6,2},{... | collective-permute-start | bytes 884744 | tf_op jit(solution)/shard_map/ppermute | solution.py:430
  52.9 1.4 %collective-permute-start.13 = (bf16[2,192,384]{2,1,0:T(8,128)(2,1)S(1)}, bf16[2,192,384]{2,1,0:T(8,128)(2,1)S(1)}, u32[]{:S(2)}, u32[]{:S(2)}) collective-permute-start(bf16[2,192,384]{2,1,0:T(8,128)(2,1)S(1)} %pad_maximum_fusion.1.refs_0_), channel_id=1, source_target_pairs={{0,8},{4,12},{8,0},{12,4},{1,9},{5,13},{9,1},{13,5},{2,10},{6,14},... | collective-permute-start | bytes 884744 | tf_op jit(solution)/shard_map/ppermute | solution.py:430
  54.4 0.9 collective-permute-start.19
  55.3 7.0 %collective-permute-done.14.refs_3_ = bf16[2,192,384]{2,1,0:T(8,128)(2,1)S(1)} collective-permute-done((bf16[2,192,384]{2,1,0:T(8,128)(2,1)S(1)}, bf16[2,192,384]{2,1,0:T(8,128)(2,1)S(1)}, u32[]{:S(2)}, u32[]{:S(2)}) %collective-permute-start.14) | collective-permute-done | bytes 294944 | tf_op jit(solution)/shard_map/ppermute | solution.py:430
  62.4 0.5 collective-permute-start.17
  62.9 2.5 %collective-permute-done.12.refs_1_ = bf16[2,192,384]{2,1,0:T(8,128)(2,1)S(1)} collective-permute-done((bf16[2,192,384]{2,1,0:T(8,128)(2,1)S(1)}, bf16[2,192,384]{2,1,0:T(8,128)(2,1)S(1)}, u32[]{:S(2)}, u32[]{:S(2)}) %collective-permute-start.12) | collective-permute-done | bytes 294944 | tf_op jit(solution)/shard_map/ppermute | solution.py:430
  65.4 1.1 next_memory.2.lhs_ref.own_ref
  66.5 1.6 %early_product.1.early_ref = f32[384,768]{1,0:T(8,128)S(1)} custom-call(s32[5]{0:T(128)S(1)} %stack.47.place_ref, bf16[384,1536]{1,0:T(8,128)(2,1)S(1)} %next_memory.2.lhs_ref.own_ref, bf16[3072,768]{1,0:T(8,128)(2,1)S(1)} %get-tuple-element.81.resident_ref), custom_call_target="tpu_custom_call" | custom-call | flops 905969664 | bytes 1179648 | tf_op jit(solution)/shard_map/early_product/pallas_call | solution.py:142
  68.1 1.1 next_memory.3.lhs_ref.other_ref
  69.3 1.8 %late_product.1 = (bf16[192,384]{1,0:T(8,128)(2,1)S(1)}, bf16[192,384]{1,0:T(8,128)(2,1)S(1)}, bf16[192,384]{1,0:T(8,128)(2,1)S(1)}, bf16[192,384]{1,0:T(8,128)(2,1)S(1)}) custom-call(s32[5]{0:T(128)S(1)} %stack.47.place_ref, f32[384,768]{1,0:T(8,128)S(1)} %early_product.1.early_ref, bf16[384,1536]{1,0:T(8,128)(2,1)S(1)} %next_memory.3.lhs_ref.other_ref, ...), custom_call_target="tpu_custom_call" | custom-call | flops 905969664 | bytes 1179648 | tf_op jit(solution)/shard_map/late_product/pallas_call | solution.py:175
  71.1 3.6 %collective-permute-start.21 = (bf16[192,384]{1,0:T(8,128)(2,1)S(1)}, bf16[192,384]{1,0:T(8,128)(2,1)S(1)}, u32[]{:S(2)}, u32[]{:S(2)}) collective-permute-start(bf16[192,384]{1,0:T(8,128)(2,1)S(1)} %get-tuple-element.92), channel_id=1, source_target_pairs={{0,32},{1,33},{2,34},{3,35},{4,36},{5,37},{6,38},{7,39},{8,40},{9,... | collective-permute-start | bytes 442376 | tf_op jit(solution)/shard_map/ppermute | solution.py:409
  74.7 0.4 collective-permute-start.22
  75.1 2.2 %collective-permute-start.23 = (bf16[192,384]{1,0:T(8,128)(2,1)S(1)}, bf16[192,384]{1,0:T(8,128)(2,1)S(1)}, u32[]{:S(2)}, u32[]{:S(2)}) collective-permute-start(bf16[192,384]{1,0:T(8,128)(2,1)S(1)} %get-tuple-element.94), channel_id=1, source_target_pairs={{0,96},{1,97},{2,98},{3,99},{4,100},{5,101},{6,102},{7,103},{8,104... | collective-permute-start | bytes 442376 | tf_op jit(solution)/shard_map/ppermute | solution.py:409
  77.3 2.7 %both_product.1 = (bf16[192,384]{1,0:T(8,128)(2,1)S(1)}, bf16[192,384]{1,0:T(8,128)(2,1)S(1)}, bf16[192,384]{1,0:T(8,128)(2,1)S(1)}, bf16[192,384]{1,0:T(8,128)(2,1)S(1)}) custom-call(s32[5]{0:T(128)S(1)} %stack.47.place_ref, bf16[384,1536]{1,0:T(8,128)(2,1)S(1)} %next_memory.2.lhs_ref.own_ref, bf16[384,1536]{1,0:T(8,128)(2,1)S(1)} %next_memory.3.lhs_ref.other_ref, ...), custom_call_target="tpu_custom_call" | custom-call | flops 905969664 | bytes 1179648 | tf_op jit(solution)/shard_map/both_product/pallas_call | solution.py:175
  79.9 0.7 collective-permute-start.24
  80.7 4.4 %collective-permute-start.25 = (bf16[192,384]{1,0:T(8,128)(2,1)S(1)}, bf16[192,384]{1,0:T(8,128)(2,1)S(1)}, u32[]{:S(2)}, u32[]{:S(2)}) collective-permute-start(bf16[192,384]{1,0:T(8,128)(2,1)S(1)} %get-tuple-element.98), channel_id=1, source_target_pairs={{0,64},{1,65},{2,66},{3,67},{4,68},{5,69},{6,70},{7,71},{8,72},{9,... | collective-permute-start | bytes 442376 | tf_op jit(solution)/shard_map/ppermute | solution.py:409
  85.1 4.1 %collective-permute-done.24.refs_4_ = bf16[192,384]{1,0:T(8,128)(2,1)S(1)} collective-permute-done((bf16[192,384]{1,0:T(8,128)(2,1)S(1)}, bf16[192,384]{1,0:T(8,128)(2,1)S(1)}, u32[]{:S(2)}, u32[]{:S(2)}) %collective-permute-start.24) | collective-permute-done | bytes 147488 | tf_op jit(solution)/shard_map/ppermute | solution.py:409
  89.3 2.1 %collective-permute-done.25.refs_5_ = bf16[192,384]{1,0:T(8,128)(2,1)S(1)} collective-permute-done((bf16[192,384]{1,0:T(8,128)(2,1)S(1)}, bf16[192,384]{1,0:T(8,128)(2,1)S(1)}, u32[]{:S(2)}, u32[]{:S(2)}) %collective-permute-start.25) | collective-permute-done | bytes 147488 | tf_op jit(solution)/shard_map/ppermute | solution.py:409
  91.4 1.4 %second_solve.1.refs_0_ = bf16[192,384]{1,0:T(8,128)(2,1)S(1)} custom-call(s32[5]{0:T(128)S(1)} %stack.47.place_ref, bf16[192,384]{1,0:T(8,128)(2,1)S(1)} %collective-permute-done.20.refs_0_, bf16[192,384]{1,0:T(8,128)(2,1)S(1)} %collective-permute-done.21.refs_1_, bf16[192,384]{1,0:T(8,128)(2,1)S(1)} %collective-permute-done.22.refs_2_, ...), custom_call_target="tpu_custom_call" | custom-call | flops 339738624 | bytes 1769472 | tf_op jit(solution)/shard_map/second_solve/pallas_call | solution.py:340
  92.8 1.5 %collective-permute-start.30 = (bf16[192,384]{1,0:T(8,128)(2,1)S(1)}, bf16[192,384]{1,0:T(8,128)(2,1)S(1)}, u32[]{:S(2)}, u32[]{:S(2)}) collective-permute-start(bf16[192,384]{1,0:T(8,128)(2,1)S(1)} %second_solve.1.refs_0_), channel_id=1, source_target_pairs={{0,16},{16,0},{1,17},{17,1},{2,18},{18,2},{3,19},{19,3},{4,20},{20... | collective-permute-start | bytes 442376 | tf_op jit(solution)/shard_map/ppermute | solution.py:470
  94.7 2.0 %collective-permute-start.28 = (bf16[192,384]{1,0:T(8,128)(2,1)S(1)}, bf16[192,384]{1,0:T(8,128)(2,1)S(1)}, u32[]{:S(2)}, u32[]{:S(2)}) collective-permute-start(bf16[192,384]{1,0:T(8,128)(2,1)S(1)} %second_solve.1.refs_0_), channel_id=1, source_target_pairs={{0,64},{32,96},{64,0},{96,32},{1,65},{33,97},{65,1},{97,33},{2,66}... | collective-permute-start | bytes 442376 | tf_op jit(solution)/shard_map/ppermute | solution.py:430
  96.7 1.5 %collective-permute-done.30.refs_4_ = bf16[192,384]{1,0:T(8,128)(2,1)S(1)} collective-permute-done((bf16[192,384]{1,0:T(8,128)(2,1)S(1)}, bf16[192,384]{1,0:T(8,128)(2,1)S(1)}, u32[]{:S(2)}, u32[]{:S(2)}) %collective-permute-start.30) | collective-permute-done | bytes 147488 | tf_op jit(solution)/shard_map/ppermute | solution.py:470
  98.2 1.7 %collective-permute-start.33 = (bf16[192,384]{1,0:T(8,128)(2,1)S(1)}, bf16[192,384]{1,0:T(8,128)(2,1)S(1)}, u32[]{:S(2)}, u32[]{:S(2)}) collective-permute-start(bf16[192,384]{1,0:T(8,128)(2,1)S(1)} %collective-permute-done.30.refs_4_), channel_id=1, source_target_pairs={{0,96},{32,0},{64,32},{96,64},{1,97},{33,1},{65,33},{97,65},{2,98}... | collective-permute-start | bytes 442376 | tf_op jit(solution)/shard_map/ppermute | solution.py:430
  99.9 0.6 collective-permute-start.32
  100.5 0.6 collective-permute-done.29.refs_3_
  101.1 0.8 collective-permute-start.31
  102.0 1.8 %join_one.1.refs_8_ = bf16[2,384,1536]{2,1,0:T(8,128)(2,1)} custom-call(s32[5]{0:T(128)S(1)} %stack.47.place_ref, bf16[4,192,384]{2,1,0:T(8,128)(2,1)S(1)} %pad_maximum_fusion.own_ref, bf16[4,192,384]{2,1,0:T(8,128)(2,1)S(1)} %collective-permute-done.19.other_ref), custom_call_target="tpu_custom_call" | custom-call | flops 589824 | bytes 2359296 | tf_op jit(solution)/shard_map/join_one/pallas_call | solution.py:387
  103.8 4.1 %collective-permute-done.27.refs_1_ = bf16[192,384]{1,0:T(8,128)(2,1)S(1)} collective-permute-done((bf16[192,384]{1,0:T(8,128)(2,1)S(1)}, bf16[192,384]{1,0:T(8,128)(2,1)S(1)}, u32[]{:S(2)}, u32[]{:S(2)}) %collective-permute-start.27) | collective-permute-done | bytes 147488 | tf_op jit(solution)/shard_map/ppermute | solution.py:430
  107.9 1.0 collective-permute-done.32.refs_6_
  108.9 1.7 %collective-permute-done.31.refs_5_ = bf16[192,384]{1,0:T(8,128)(2,1)S(1)} collective-permute-done((bf16[192,384]{1,0:T(8,128)(2,1)S(1)}, bf16[192,384]{1,0:T(8,128)(2,1)S(1)}, u32[]{:S(2)}, u32[]{:S(2)}) %collective-permute-start.31) | collective-permute-done | bytes 147488 | tf_op jit(solution)/shard_map/ppermute | solution.py:430
  110.6 1.8 %join_two.1 = bf16[2,384,1536]{2,1,0:T(8,128)(2,1)} custom-call(s32[5]{0:T(128)S(1)} %stack.47.place_ref, bf16[192,384]{1,0:T(8,128)(2,1)S(1)} %second_solve.1.refs_0_, bf16[192,384]{1,0:T(8,128)(2,1)S(1)} %collective-permute-done.27.refs_1_, bf16[192,384]{1,0:T(8,128)(2,1)S(1)} %collective-permute-done.28.refs_2_, ...), custom_call_target="tpu_custom_call", output_to_operand_aliasing={{}: (9, {})} | custom-call | flops 589824 | bytes 2359296 | tf_op jit(solution)/shard_map/join_two/pallas_call | solution.py:387
  (43 shorter events, 1.2 us)
Async XLA Ops:
  6.6 12.5 %collective-permute-start.1 = (bf16[192,384]{1,0:T(8,128)(2,1)S(1)}, bf16[192,384]{1,0:T(8,128)(2,1)S(1)}, u32[]{:S(2)}, u32[]{:S(2)}) collective-permute-start(bf16[192,384]{1,0:T(8,128)(2,1)S(1)} %get-tuple-element.55), channel_id=1, source_target_pairs={{0,32},{1,33},{2,34},{3,35},{4,36},{5,37},{6,38},{7,39},{8,40},{9,... | collective-permute-start | bytes 442376 | tf_op jit(solution)/shard_map/ppermute | solution.py:409
  8.3 12.4 %collective-permute-start = (bf16[192,384]{1,0:T(8,128)(2,1)S(1)}, bf16[192,384]{1,0:T(8,128)(2,1)S(1)}, u32[]{:S(2)}, u32[]{:S(2)}) collective-permute-start(bf16[192,384]{1,0:T(8,128)(2,1)S(1)} %get-tuple-element.56), channel_id=1, source_target_pairs={{0,48},{1,49},{2,50},{3,51},{4,52},{5,53},{6,54},{7,55},{8,56},{9,... | collective-permute-start | bytes 442376 | tf_op jit(solution)/shard_map/ppermute | solution.py:409
  10.1 11.1 %collective-permute-start.3 = (bf16[192,384]{1,0:T(8,128)(2,1)S(1)}, bf16[192,384]{1,0:T(8,128)(2,1)S(1)}, u32[]{:S(2)}, u32[]{:S(2)}) collective-permute-start(bf16[192,384]{1,0:T(8,128)(2,1)S(1)} %get-tuple-element.57), channel_id=1, source_target_pairs={{0,96},{1,97},{2,98},{3,99},{4,100},{5,101},{6,102},{7,103},{8,104... | collective-permute-start | bytes 442376 | tf_op jit(solution)/shard_map/ppermute | solution.py:409
  13.2 13.6 %collective-permute-start.2 = (bf16[192,384]{1,0:T(8,128)(2,1)S(1)}, bf16[192,384]{1,0:T(8,128)(2,1)S(1)}, u32[]{:S(2)}, u32[]{:S(2)}) collective-permute-start(bf16[192,384]{1,0:T(8,128)(2,1)S(1)} %get-tuple-element.58), channel_id=1, source_target_pairs={{0,112},{1,113},{2,114},{3,115},{4,116},{5,117},{6,118},{7,119},{8... | collective-permute-start | bytes 442376 | tf_op jit(solution)/shard_map/ppermute | solution.py:409
  13.2 5.9 %copy-start.1 = (f32[32,32]{1,0:T(8,128)S(1)}, f32[32,32]{1,0:T(8,128)}, u32[]{:S(2)}) copy-start(f32[32,32]{1,0:T(8,128)} %param.9) | copy-start | bytes 12292
  13.2 8.0 %copy-start = (f32[2,384,384]{2,1,0:T(8,128)S(1)}, f32[2,384,384]{2,1,0:T(8,128)}, u32[]{:S(2)}) copy-start(f32[2,384,384]{2,1,0:T(8,128)} %param.8) | copy-start | bytes 3538948
  15.8 14.7 %collective-permute-start.4 = (bf16[192,384]{1,0:T(8,128)(2,1)S(1)}, bf16[192,384]{1,0:T(8,128)(2,1)S(1)}, u32[]{:S(2)}, u32[]{:S(2)}) collective-permute-start(bf16[192,384]{1,0:T(8,128)(2,1)S(1)} %get-tuple-element.68), channel_id=1, source_target_pairs={{0,80},{1,81},{2,82},{3,83},{4,84},{5,85},{6,86},{7,87},{8,88},{9,... | collective-permute-start | bytes 442376 | tf_op jit(solution)/shard_map/ppermute | solution.py:409
  19.1 11.4 %collective-permute-start.5 = (bf16[192,384]{1,0:T(8,128)(2,1)S(1)}, bf16[192,384]{1,0:T(8,128)(2,1)S(1)}, u32[]{:S(2)}, u32[]{:S(2)}) collective-permute-start(bf16[192,384]{1,0:T(8,128)(2,1)S(1)} %get-tuple-element.69), channel_id=1, source_target_pairs={{0,64},{1,65},{2,66},{3,67},{4,68},{5,69},{6,70},{7,71},{8,72},{9,... | collective-permute-start | bytes 442376 | tf_op jit(solution)/shard_map/ppermute | solution.py:409
  20.8 9.8 %collective-permute-start.6 = (bf16[192,384]{1,0:T(8,128)(2,1)S(1)}, bf16[192,384]{1,0:T(8,128)(2,1)S(1)}, u32[]{:S(2)}, u32[]{:S(2)}) collective-permute-start(bf16[192,384]{1,0:T(8,128)(2,1)S(1)} %get-tuple-element.70), channel_id=1, source_target_pairs={{0,16},{1,17},{2,18},{3,19},{4,20},{5,21},{6,22},{7,23},{8,24},{9,... | collective-permute-start | bytes 442376 | tf_op jit(solution)/shard_map/ppermute | solution.py:409
  32.4 14.3 %collective-permute-start.8 = (bf16[192,384]{1,0:T(8,128)(2,1)S(1)}, bf16[192,384]{1,0:T(8,128)(2,1)S(1)}, u32[]{:S(2)}, u32[]{:S(2)}) collective-permute-start(bf16[192,384]{1,0:T(8,128)(2,1)S(1)} %get-tuple-element.72), channel_id=1, source_target_pairs={{0,10},{1,11},{2,26},{3,27},{4,46},{5,47},{6,62},{7,63},{8,66},{9,... | collective-permute-start | bytes 442376 | tf_op jit(solution)/shard_map/ppermute | solution.py:409
  38.5 8.2 %collective-permute-start.7 = (bf16[192,384]{1,0:T(8,128)(2,1)S(1)}, bf16[192,384]{1,0:T(8,128)(2,1)S(1)}, u32[]{:S(2)}, u32[]{:S(2)}) collective-permute-start(bf16[192,384]{1,0:T(8,128)(2,1)S(1)} %get-tuple-element.72), channel_id=1, source_target_pairs={{0,0},{1,1},{2,16},{3,17},{4,36},{5,37},{6,52},{7,53},{8,72},{9,73... | collective-permute-start | bytes 442376 | tf_op jit(solution)/shard_map/ppermute | solution.py:409
  39.2 7.5 %collective-permute-start.11 = (bf16[192,384]{1,0:T(8,128)(2,1)S(1)}, bf16[192,384]{1,0:T(8,128)(2,1)S(1)}, u32[]{:S(2)}, u32[]{:S(2)}) collective-permute-start(bf16[192,384]{1,0:T(8,128)(2,1)S(1)} %get-tuple-element.77), channel_id=1, source_target_pairs={{0,96},{32,0},{64,32},{96,64},{1,97},{33,1},{65,33},{97,65},{2,98}... | collective-permute-start | bytes 442376 | tf_op jit(solution)/shard_map/ppermute | solution.py:430
  42.4 6.7 %collective-permute-start.10 = (bf16[192,384]{1,0:T(8,128)(2,1)S(1)}, bf16[192,384]{1,0:T(8,128)(2,1)S(1)}, u32[]{:S(2)}, u32[]{:S(2)}) collective-permute-start(bf16[192,384]{1,0:T(8,128)(2,1)S(1)} %get-tuple-element.77), channel_id=1, source_target_pairs={{0,64},{32,96},{64,0},{96,32},{1,65},{33,97},{65,1},{97,33},{2,66}... | collective-permute-start | bytes 442376 | tf_op jit(solution)/shard_map/ppermute | solution.py:430
  43.8 6.9 %collective-permute-start.9 = (bf16[192,384]{1,0:T(8,128)(2,1)S(1)}, bf16[192,384]{1,0:T(8,128)(2,1)S(1)}, u32[]{:S(2)}, u32[]{:S(2)}) collective-permute-start(bf16[192,384]{1,0:T(8,128)(2,1)S(1)} %get-tuple-element.77), channel_id=1, source_target_pairs={{0,32},{32,64},{64,96},{96,0},{1,33},{33,65},{65,97},{97,1},{2,34}... | collective-permute-start | bytes 442376 | tf_op jit(solution)/shard_map/ppermute | solution.py:430
  50.7 11.7 %collective-permute-start.14 = (bf16[2,192,384]{2,1,0:T(8,128)(2,1)S(1)}, bf16[2,192,384]{2,1,0:T(8,128)(2,1)S(1)}, u32[]{:S(2)}, u32[]{:S(2)}) collective-permute-start(bf16[2,192,384]{2,1,0:T(8,128)(2,1)S(1)} %pad_maximum_fusion.1.refs_0_), channel_id=1, source_target_pairs={{0,12},{4,0},{8,4},{12,8},{1,13},{5,1},{9,5},{13,9},{2,14},{6,2},{... | collective-permute-start | bytes 884744 | tf_op jit(solution)/shard_map/ppermute | solution.py:430
  52.9 9.4 %collective-permute-start.13 = (bf16[2,192,384]{2,1,0:T(8,128)(2,1)S(1)}, bf16[2,192,384]{2,1,0:T(8,128)(2,1)S(1)}, u32[]{:S(2)}, u32[]{:S(2)}) collective-permute-start(bf16[2,192,384]{2,1,0:T(8,128)(2,1)S(1)} %pad_maximum_fusion.1.refs_0_), channel_id=1, source_target_pairs={{0,8},{4,12},{8,0},{12,4},{1,9},{5,13},{9,1},{13,5},{2,10},{6,14},... | collective-permute-start | bytes 884744 | tf_op jit(solution)/shard_map/ppermute | solution.py:430
  54.3 11.1 %collective-permute-start.12 = (bf16[2,192,384]{2,1,0:T(8,128)(2,1)S(1)}, bf16[2,192,384]{2,1,0:T(8,128)(2,1)S(1)}, u32[]{:S(2)}, u32[]{:S(2)}) collective-permute-start(bf16[2,192,384]{2,1,0:T(8,128)(2,1)S(1)} %pad_maximum_fusion.1.refs_0_), channel_id=1, source_target_pairs={{0,4},{4,8},{8,12},{12,0},{1,5},{5,9},{9,13},{13,1},{2,6},{6,10},{... | collective-permute-start | bytes 884744 | tf_op jit(solution)/shard_map/ppermute | solution.py:430
  54.4 13.7 %collective-permute-start.19 = (bf16[4,192,384]{2,1,0:T(8,128)(2,1)S(1)}, bf16[4,192,384]{2,1,0:T(8,128)(2,1)S(1)}, u32[]{:S(2)}, u32[]{:S(2)}) collective-permute-start(bf16[4,192,384]{2,1,0:T(8,128)(2,1)S(1)} %pad_maximum_fusion.own_ref), channel_id=1, source_target_pairs={{0,16},{16,0},{1,17},{17,1},{2,18},{18,2},{3,19},{19,3},{4,20},{20... | collective-permute-start | bytes 1769480 | tf_op jit(solution)/shard_map/ppermute | solution.py:457
  55.3 12.8 %collective-permute-start.15 = (bf16[2,192,384]{2,1,0:T(8,128)(2,1)S(1)}, bf16[2,192,384]{2,1,0:T(8,128)(2,1)S(1)}, u32[]{:S(2)}, u32[]{:S(2)}) collective-permute-start(bf16[2,192,384]{2,1,0:T(8,128)(2,1)S(1)} %pad_maximum_fusion.1.refs_0_), channel_id=1, source_target_pairs={{0,1},{1,0},{2,3},{3,2},{4,5},{5,4},{6,7},{7,6},{8,9},{9,8},{10,11... | collective-permute-start | bytes 884744 | tf_op jit(solution)/shard_map/ppermute | solution.py:458
  62.3 5.8 %collective-permute-start.18 = (bf16[2,192,384]{2,1,0:T(8,128)(2,1)S(1)}, bf16[2,192,384]{2,1,0:T(8,128)(2,1)S(1)}, u32[]{:S(2)}, u32[]{:S(2)}) collective-permute-start(bf16[2,192,384]{2,1,0:T(8,128)(2,1)S(1)} %collective-permute-done.14.refs_3_), channel_id=1, source_target_pairs={{0,1},{1,0},{2,3},{3,2},{4,5},{5,4},{6,7},{7,6},{8,9},{9,8},{10,11... | collective-permute-start | bytes 884744 | tf_op jit(solution)/shard_map/ppermute | solution.py:458
  62.4 5.8 %collective-permute-start.17 = (bf16[2,192,384]{2,1,0:T(8,128)(2,1)S(1)}, bf16[2,192,384]{2,1,0:T(8,128)(2,1)S(1)}, u32[]{:S(2)}, u32[]{:S(2)}) collective-permute-start(bf16[2,192,384]{2,1,0:T(8,128)(2,1)S(1)} %collective-permute-done.13.refs_2_), channel_id=1, source_target_pairs={{0,1},{1,0},{2,3},{3,2},{4,5},{5,4},{6,7},{7,6},{8,9},{9,8},{10,11... | collective-permute-start | bytes 884744 | tf_op jit(solution)/shard_map/ppermute | solution.py:458
  65.4 2.8 %collective-permute-start.16 = (bf16[2,192,384]{2,1,0:T(8,128)(2,1)S(1)}, bf16[2,192,384]{2,1,0:T(8,128)(2,1)S(1)}, u32[]{:S(2)}, u32[]{:S(2)}) collective-permute-start(bf16[2,192,384]{2,1,0:T(8,128)(2,1)S(1)} %collective-permute-done.12.refs_1_), channel_id=1, source_target_pairs={{0,1},{1,0},{2,3},{3,2},{4,5},{5,4},{6,7},{7,6},{8,9},{9,8},{10,11... | collective-permute-start | bytes 884744 | tf_op jit(solution)/shard_map/ppermute | solution.py:458
  71.0 9.6 %collective-permute-start.20 = (bf16[192,384]{1,0:T(8,128)(2,1)S(1)}, bf16[192,384]{1,0:T(8,128)(2,1)S(1)}, u32[]{:S(2)}, u32[]{:S(2)}) collective-permute-start(bf16[192,384]{1,0:T(8,128)(2,1)S(1)} %get-tuple-element.91), channel_id=1, source_target_pairs={{0,48},{1,49},{2,50},{3,51},{4,52},{5,53},{6,54},{7,55},{8,56},{9,... | collective-permute-start | bytes 442376 | tf_op jit(solution)/shard_map/ppermute | solution.py:409
  71.1 14.0 %collective-permute-start.21 = (bf16[192,384]{1,0:T(8,128)(2,1)S(1)}, bf16[192,384]{1,0:T(8,128)(2,1)S(1)}, u32[]{:S(2)}, u32[]{:S(2)}) collective-permute-start(bf16[192,384]{1,0:T(8,128)(2,1)S(1)} %get-tuple-element.92), channel_id=1, source_target_pairs={{0,32},{1,33},{2,34},{3,35},{4,36},{5,37},{6,38},{7,39},{8,40},{9,... | collective-permute-start | bytes 442376 | tf_op jit(solution)/shard_map/ppermute | solution.py:409
  74.7 10.4 %collective-permute-start.22 = (bf16[192,384]{1,0:T(8,128)(2,1)S(1)}, bf16[192,384]{1,0:T(8,128)(2,1)S(1)}, u32[]{:S(2)}, u32[]{:S(2)}) collective-permute-start(bf16[192,384]{1,0:T(8,128)(2,1)S(1)} %get-tuple-element.93), channel_id=1, source_target_pairs={{0,112},{1,113},{2,114},{3,115},{4,116},{5,117},{6,118},{7,119},{8... | collective-permute-start | bytes 442376 | tf_op jit(solution)/shard_map/ppermute | solution.py:409
  75.1 10.1 %collective-permute-start.23 = (bf16[192,384]{1,0:T(8,128)(2,1)S(1)}, bf16[192,384]{1,0:T(8,128)(2,1)S(1)}, u32[]{:S(2)}, u32[]{:S(2)}) collective-permute-start(bf16[192,384]{1,0:T(8,128)(2,1)S(1)} %get-tuple-element.94), channel_id=1, source_target_pairs={{0,96},{1,97},{2,98},{3,99},{4,100},{5,101},{6,102},{7,103},{8,104... | collective-permute-start | bytes 442376 | tf_op jit(solution)/shard_map/ppermute | solution.py:409
  79.9 9.3 %collective-permute-start.24 = (bf16[192,384]{1,0:T(8,128)(2,1)S(1)}, bf16[192,384]{1,0:T(8,128)(2,1)S(1)}, u32[]{:S(2)}, u32[]{:S(2)}) collective-permute-start(bf16[192,384]{1,0:T(8,128)(2,1)S(1)} %get-tuple-element.97), channel_id=1, source_target_pairs={{0,80},{1,81},{2,82},{3,83},{4,84},{5,85},{6,86},{7,87},{8,88},{9,... | collective-permute-start | bytes 442376 | tf_op jit(solution)/shard_map/ppermute | solution.py:409
  80.7 10.7 %collective-permute-start.25 = (bf16[192,384]{1,0:T(8,128)(2,1)S(1)}, bf16[192,384]{1,0:T(8,128)(2,1)S(1)}, u32[]{:S(2)}, u32[]{:S(2)}) collective-permute-start(bf16[192,384]{1,0:T(8,128)(2,1)S(1)} %get-tuple-element.98), channel_id=1, source_target_pairs={{0,64},{1,65},{2,66},{3,67},{4,68},{5,69},{6,70},{7,71},{8,72},{9,... | collective-permute-start | bytes 442376 | tf_op jit(solution)/shard_map/ppermute | solution.py:409
  85.1 6.3 %collective-permute-start.26 = (bf16[192,384]{1,0:T(8,128)(2,1)S(1)}, bf16[192,384]{1,0:T(8,128)(2,1)S(1)}, u32[]{:S(2)}, u32[]{:S(2)}) collective-permute-start(bf16[192,384]{1,0:T(8,128)(2,1)S(1)} %get-tuple-element.99), channel_id=1, source_target_pairs={{0,16},{1,17},{2,18},{3,19},{4,20},{5,21},{6,22},{7,23},{8,24},{9,... | collective-permute-start | bytes 442376 | tf_op jit(solution)/shard_map/ppermute | solution.py:409
  92.8 5.3 %collective-permute-start.30 = (bf16[192,384]{1,0:T(8,128)(2,1)S(1)}, bf16[192,384]{1,0:T(8,128)(2,1)S(1)}, u32[]{:S(2)}, u32[]{:S(2)}) collective-permute-start(bf16[192,384]{1,0:T(8,128)(2,1)S(1)} %second_solve.1.refs_0_), channel_id=1, source_target_pairs={{0,16},{16,0},{1,17},{17,1},{2,18},{18,2},{3,19},{19,3},{4,20},{20... | collective-permute-start | bytes 442376 | tf_op jit(solution)/shard_map/ppermute | solution.py:470
  94.4 6.8 %collective-permute-start.29 = (bf16[192,384]{1,0:T(8,128)(2,1)S(1)}, bf16[192,384]{1,0:T(8,128)(2,1)S(1)}, u32[]{:S(2)}, u32[]{:S(2)}) collective-permute-start(bf16[192,384]{1,0:T(8,128)(2,1)S(1)} %second_solve.1.refs_0_), channel_id=1, source_target_pairs={{0,96},{32,0},{64,32},{96,64},{1,97},{33,1},{65,33},{97,65},{2,98}... | collective-permute-start | bytes 442376 | tf_op jit(solution)/shard_map/ppermute | solution.py:430
  94.7 9.1 %collective-permute-start.28 = (bf16[192,384]{1,0:T(8,128)(2,1)S(1)}, bf16[192,384]{1,0:T(8,128)(2,1)S(1)}, u32[]{:S(2)}, u32[]{:S(2)}) collective-permute-start(bf16[192,384]{1,0:T(8,128)(2,1)S(1)} %second_solve.1.refs_0_), channel_id=1, source_target_pairs={{0,64},{32,96},{64,0},{96,32},{1,65},{33,97},{65,1},{97,33},{2,66}... | collective-permute-start | bytes 442376 | tf_op jit(solution)/shard_map/ppermute | solution.py:430
  96.7 11.2 %collective-permute-start.27 = (bf16[192,384]{1,0:T(8,128)(2,1)S(1)}, bf16[192,384]{1,0:T(8,128)(2,1)S(1)}, u32[]{:S(2)}, u32[]{:S(2)}) collective-permute-start(bf16[192,384]{1,0:T(8,128)(2,1)S(1)} %second_solve.1.refs_0_), channel_id=1, source_target_pairs={{0,32},{32,64},{64,96},{96,0},{1,33},{33,65},{65,97},{97,1},{2,34}... | collective-permute-start | bytes 442376 | tf_op jit(solution)/shard_map/ppermute | solution.py:430
  98.2 9.7 %collective-permute-start.33 = (bf16[192,384]{1,0:T(8,128)(2,1)S(1)}, bf16[192,384]{1,0:T(8,128)(2,1)S(1)}, u32[]{:S(2)}, u32[]{:S(2)}) collective-permute-start(bf16[192,384]{1,0:T(8,128)(2,1)S(1)} %collective-permute-done.30.refs_4_), channel_id=1, source_target_pairs={{0,96},{32,0},{64,32},{96,64},{1,97},{33,1},{65,33},{97,65},{2,98}... | collective-permute-start | bytes 442376 | tf_op jit(solution)/shard_map/ppermute | solution.py:430
  99.9 9.0 %collective-permute-start.32 = (bf16[192,384]{1,0:T(8,128)(2,1)S(1)}, bf16[192,384]{1,0:T(8,128)(2,1)S(1)}, u32[]{:S(2)}, u32[]{:S(2)}) collective-permute-start(bf16[192,384]{1,0:T(8,128)(2,1)S(1)} %collective-permute-done.30.refs_4_), channel_id=1, source_target_pairs={{0,64},{32,96},{64,0},{96,32},{1,65},{33,97},{65,1},{97,33},{2,66}... | collective-permute-start | bytes 442376 | tf_op jit(solution)/shard_map/ppermute | solution.py:430
  101.1 9.5 %collective-permute-start.31 = (bf16[192,384]{1,0:T(8,128)(2,1)S(1)}, bf16[192,384]{1,0:T(8,128)(2,1)S(1)}, u32[]{:S(2)}, u32[]{:S(2)}) collective-permute-start(bf16[192,384]{1,0:T(8,128)(2,1)S(1)} %collective-permute-done.30.refs_4_), channel_id=1, source_target_pairs={{0,32},{32,64},{64,96},{96,0},{1,33},{33,65},{65,97},{97,1},{2,34}... | collective-permute-start | bytes 442376 | tf_op jit(solution)/shard_map/ppermute | solution.py:430

commit v12 on v11

--- a/solution.py
+++ b/solution.py
@@ -261,11 +261,11 @@
 
 
 def next_memory_kernel(side, place_ref, memory_ref, *refs):
-    pair_refs, out_ref = refs[:4], refs[4]
+    near_refs, far_refs, out_ref = refs[:4], refs[4:8], refs[8]
     half = out_ref.shape[1]
     width = half // 4
     for dx in range(4):
-        near, far = pair_refs[dx][0].astype(f32), pair_refs[dx ^ 2][1].astype(f32)
+        near, far = near_refs[dx][...].astype(f32), far_refs[dx ^ 2][...].astype(f32)
         start = position(((place_ref[X] - dx) & 3) ^ place_ref[Y]) * width
         low = jnp.where(place_ref[ZH] == 0, near, far)
         high = jnp.where(place_ref[ZH] == 0, far, near)
@@ -275,17 +275,17 @@
         out_ref[:, to] = (memory_ref[:, at].astype(f32) + pair).astype(bf16)
 
 
-def next_memory(side, place, memory, pairs):
+def next_memory(side, place, memory, energies):
     rows, depth = memory.shape
     return pl.pallas_call(
         functools.partial(next_memory_kernel, side),
-        in_specs=[SMEM] + [VMEM] * 5,
+        in_specs=[SMEM] + [VMEM] * 9,
         out_specs=VMEM,
         out_shape=jax.ShapeDtypeStruct((rows, depth // 2), bf16),
         compiler_params=params(6),
         cost_estimate=cost(rows * depth, 3 * rows * depth),
         name="next_memory",
-    )(place, memory, *pairs)
+    )(place, memory, *energies)
 
 
 def solve_into(part_refs, prior_ref, inverse_ref):
@@ -431,6 +431,13 @@
     return [pairs[d] for d in range(4)]
 
 
+def relayed(value, onward):
+    step = lambda value, d: lax.ppermute(value, "x", [(i, (i + d) % 4) for i in range(4)])
+    values = {0: value, 1: step(value, 1), 3: step(value, 3)}
+    values[2] = step(values[onward], onward)
+    return [values[d] for d in range(4)]
+
+
 def per_device(resident, memory, previous, inverse_part, pair_coupling):
     place = jnp.stack([lax.axis_index(name) for name in ("x", "zh", "c", "y", "zl")]).astype(jnp.int32)
     coupling = jnp.tile(pair_coupling, (1, 128 // ORB))
@@ -447,15 +454,17 @@
     front_one, energy = solve(
         first_solve_kernel, place, parts, prior_one, inverse_part[0], [coupling], 2, "first_solve"
     )
-    pair = [move(energy, turn(0)), move(energy, turn(1))]
+    near, far = move(energy, turn(0)), move(energy, turn(1))
     ones = spread(front_one, "y")
     later, _ = lax.optimization_barrier((place, energy))
     even_resident = bring_even(later, resident)
-    pair, ones, even_resident = lax.optimization_barrier((pair, ones, even_resident))
-    own = spread(jnp.stack(pair), "x")
-    ones = jnp.stack(ones)
+    near, far, ones, even_resident = lax.optimization_barrier((near, far, ones, even_resident))
+    near, far = relayed(near, 1), relayed(far, 3)
+    own = near + far
+    gated = lax.optimization_barrier((near[0], far[0], jnp.stack(ones), near[1], far[3]))
+    near[0], far[0], ones, near[1], far[3] = gated
     others = lax.ppermute(ones, "zl", SWAP)
-    other = [lax.ppermute(pair, "c", SWAP) for pair in own]
+    other = [lax.ppermute(value, "c", SWAP) for value in near + far]
     own_lhs = next_memory(0, place, memory, own)
     early = early_product(place, own_lhs, odd_resident)
     other, others, early = lax.optimization_barrier((other, others, early))

time: 113 us -> 121 us (1.071)
  starting transfers between devices: 46.5 us -> 53.2 us
  waiting for transfers between devices: 34.2 us -> 35.6 us
    ppermute x4 -> x14, waiting for transfers between devices: 0.01 us -> 12.2 us  [the longest x6 12.2 us: relayed(): lax.ppermute(value, 'x', [(i, (i + d) % 4) for i in range(4)])]
    ppermute x12 -> x9, waiting for transfers between devices: 20.9 us -> 11.4 us  [spread(): pairs[d] = lax.ppermute(pair, axis, [(i, (i + d) % 4) for i in range(4)])]
    ppermute x4 -> x14, starting transfers between devices: 0.52 us -> 8.81 us  [the longest x6 7.47 us: relayed(): lax.ppermute(value, 'x', [(i, (i + d) % 4) for i in range(4)])]
    ppermute x12 -> x9, starting transfers between devices: 13.7 us -> 12.1 us  [spread(): pairs[d] = lax.ppermute(pair, axis, [(i, (i + d) % 4) for i in range(4)])]
  transfers between devices with their start and end apart: 34 -> 41, of which waited for: 12 -> 15; matrix products, arithmetic and copies ran while one was open for 0% -> 0% of each run, Pallas kernels for 15% -> 14%
where the time goes in v12:
time: 121 us
  starting transfers between devices  53.2 us (44%)
  waiting for transfers between devices  35.6 us (29%)
  Pallas kernels  31 us (26%)
    ppermute x16, starting transfers between devices, move(): return lax.ppermute(value, ALL, pairs)  29.8 us
    ppermute x6, waiting for transfers between devices, relayed(): lax.ppermute(value, 'x', [(i, (i + d) % 4) for i in range(4)])  12.2 us
    ppermute x9, starting transfers between devices, spread(): pairs[d] = lax.ppermute(pair, axis, [(i, (i + d) % 4) for i in range(4)])  12.1 us
    ppermute x9, waiting for transfers between devices, spread(): pairs[d] = lax.ppermute(pair, axis, [(i, (i + d) % 4) for i in range(4)])  11.4 us
    ppermute x16, waiting for transfers between devices, move(): return lax.ppermute(value, ALL, pairs)  11.3 us
    ppermute x6, starting transfers between devices, relayed(): lax.ppermute(value, 'x', [(i, (i + d) % 4) for i in range(4)])  7.47 us
    pallas_call x1, Pallas kernels, first_product(): pl.pallas_call(first_product_kernel, in_specs=[SMEM] + [pl.BlockSpec(memo...  6.5 us
    pallas_call x2, Pallas kernels, second_product(): pl.pallas_call(kernel, in_specs=[SMEM] + [VMEM] * 3, out_specs=[VMEM] * 4...  4.41 us
  transfers between devices with their start and end apart: 41, of which 15 were waited for; matrix products, arithmetic and copies ran while one was open for 0% of the time, Pallas kernels for 14%

profile of v12, /device:TPU:0, one launch (start us, length us, event | category | flops | bytes accessed | tf_op | source)
XLA Modules:
  0.0 120.5 jit_solution(10718520631008883602)
XLA Ops:
  0.1 6.5 %first_product.1 = (bf16[192,384]{1,0:T(8,128)(2,1)S(1)}, bf16[192,384]{1,0:T(8,128)(2,1)S(1)}, bf16[192,384]{1,0:T(8,128)(2,1)S(1)}, bf16[192,384]{1,0:T(8,128)...) custom-call(s32[5]{0:T(128)S(1)} %stack.38.place_ref, bf16[2,384,3072]{2,1,0:T(8,128)(2,1)} %memory_ref.3, ...), custom_call_target="tpu_custom_call" | custom-call | flops 1811939328 | bytes 18874368 | tf_op jit(solution)/shard_map/first_product/pallas_call | solution.py:112
  6.6 1.7 %collective-permute-start.1 = (bf16[192,384]{1,0:T(8,128)(2,1)S(1)}, bf16[192,384]{1,0:T(8,128)(2,1)S(1)}, u32[]{:S(2)}, u32[]{:S(2)}) collective-permute-start(bf16[192,384]{1,0:T(8,128)(2,1)S(1)} %get-tuple-element.64), channel_id=1, source_target_pairs={{0,32},{1,33},{2,34},{3,35},{4,36},{5,37},{6,38},{7,39},{8,40},{9,... | collective-permute-start | bytes 442376 | tf_op jit(solution)/shard_map/ppermute | solution.py:409
  8.3 1.8 %collective-permute-start = (bf16[192,384]{1,0:T(8,128)(2,1)S(1)}, bf16[192,384]{1,0:T(8,128)(2,1)S(1)}, u32[]{:S(2)}, u32[]{:S(2)}) collective-permute-start(bf16[192,384]{1,0:T(8,128)(2,1)S(1)} %get-tuple-element.65), channel_id=1, source_target_pairs={{0,48},{1,49},{2,50},{3,51},{4,52},{5,53},{6,54},{7,55},{8,56},{9,... | collective-permute-start | bytes 442376 | tf_op jit(solution)/shard_map/ppermute | solution.py:409
  10.1 3.0 %collective-permute-start.3 = (bf16[192,384]{1,0:T(8,128)(2,1)S(1)}, bf16[192,384]{1,0:T(8,128)(2,1)S(1)}, u32[]{:S(2)}, u32[]{:S(2)}) collective-permute-start(bf16[192,384]{1,0:T(8,128)(2,1)S(1)} %get-tuple-element.66), channel_id=1, source_target_pairs={{0,96},{1,97},{2,98},{3,99},{4,100},{5,101},{6,102},{7,103},{8,104... | collective-permute-start | bytes 442376 | tf_op jit(solution)/shard_map/ppermute | solution.py:409
  13.2 2.7 %half_product.1 = (bf16[192,384]{1,0:T(8,128)(2,1)S(1)}, bf16[192,384]{1,0:T(8,128)(2,1)S(1)}, bf16[192,384]{1,0:T(8,128)(2,1)S(1)}, bf16[192,384]{1,0:T(8,128)(2,1)S(1)}) custom-call(s32[5]{0:T(128)S(1)} %stack.38.place_ref, bf16[384,3072]{1,0:T(8,128)(2,1)S(1)} %get-tuple-element.68.lhs_ref, bf16[3072,768]{1,0:T(8,128)(2,1)S(1)} %get-tuple-element.69.resident_ref), custom_call_target="tpu_custom_call" | custom-call | flops 1811939328 | bytes 294912 | tf_op jit(solution)/shard_map/half_product/pallas_call | solution.py:60
  15.8 3.2 %collective-permute-start.4 = (bf16[192,384]{1,0:T(8,128)(2,1)S(1)}, bf16[192,384]{1,0:T(8,128)(2,1)S(1)}, u32[]{:S(2)}, u32[]{:S(2)}) collective-permute-start(bf16[192,384]{1,0:T(8,128)(2,1)S(1)} %get-tuple-element.77), channel_id=1, source_target_pairs={{0,80},{1,81},{2,82},{3,83},{4,84},{5,85},{6,86},{7,87},{8,88},{9,... | collective-permute-start | bytes 442376 | tf_op jit(solution)/shard_map/ppermute | solution.py:409
  19.1 1.6 %collective-permute-start.5 = (bf16[192,384]{1,0:T(8,128)(2,1)S(1)}, bf16[192,384]{1,0:T(8,128)(2,1)S(1)}, u32[]{:S(2)}, u32[]{:S(2)}) collective-permute-start(bf16[192,384]{1,0:T(8,128)(2,1)S(1)} %get-tuple-element.78), channel_id=1, source_target_pairs={{0,64},{1,65},{2,66},{3,67},{4,68},{5,69},{6,70},{7,71},{8,72},{9,... | collective-permute-start | bytes 442376 | tf_op jit(solution)/shard_map/ppermute | solution.py:409
  21.2 5.5 %collective-permute-done.2.refs_2_ = bf16[192,384]{1,0:T(8,128)(2,1)S(1)} collective-permute-done((bf16[192,384]{1,0:T(8,128)(2,1)S(1)}, bf16[192,384]{1,0:T(8,128)(2,1)S(1)}, u32[]{:S(2)}, u32[]{:S(2)}) %collective-permute-start.2) | collective-permute-done | bytes 147488 | tf_op jit(solution)/shard_map/ppermute | solution.py:409
  26.7 3.8 %bring_odd.1 = (bf16[384,3072]{1,0:T(8,128)(2,1)S(1)}, bf16[192,384]{1,0:T(8,128)(2,1)S(1)}, bf16[192,384]{1,0:T(8,128)(2,1)S(1)}, bf16[3072,768]{1,0:T(8,128)(2,1)S(1)}) custom-call(s32[5]{0:T(128)S(1)} %stack.38.place_ref, bf16[2,384,3072]{2,1,0:T(8,128)(2,1)} %memory_ref.3, bf16[2,384,1536]{2,1,0:T(8,128)(2,1)} %previous_ref.1, ...), custom_call_target="tpu_custom_call" | custom-call | bytes 7077888 | tf_op jit(solution)/shard_map/bring_odd/pallas_call | solution.py:220
  30.6 1.8 %first_solve.1 = (bf16[192,384]{1,0:T(8,128)(2,1)S(1)}, bf16[192,384]{1,0:T(8,128)(2,1)S(1)}) custom-call(s32[5]{0:T(128)S(1)} %stack.38.place_ref, bf16[192,384]{1,0:T(8,128)(2,1)S(1)} %collective-permute-done.refs_0_, bf16[192,384]{1,0:T(8,128)(2,1)S(1)} %collective-permute-done.1.refs_1_, bf16[192,384]{1,0:T(8,128)(2,1)S(1)} %collective-permute-done.2.refs_2_, ...), custom_call_target="tpu_custom_call" | custom-call | flops 339738624 | bytes 1769472 | tf_op jit(solution)/shard_map/first_solve/pallas_call | solution.py:340
  32.4 6.1 %collective-permute-start.8 = (bf16[192,384]{1,0:T(8,128)(2,1)S(1)}, bf16[192,384]{1,0:T(8,128)(2,1)S(1)}, u32[]{:S(2)}, u32[]{:S(2)}) collective-permute-start(bf16[192,384]{1,0:T(8,128)(2,1)S(1)} %get-tuple-element.81), channel_id=1, source_target_pairs={{0,10},{1,11},{2,26},{3,27},{4,46},{5,47},{6,62},{7,63},{8,66},{9,... | collective-permute-start | bytes 442376 | tf_op jit(solution)/shard_map/ppermute | solution.py:409
  39.2 3.2 %collective-permute-start.11 = (bf16[192,384]{1,0:T(8,128)(2,1)S(1)}, bf16[192,384]{1,0:T(8,128)(2,1)S(1)}, u32[]{:S(2)}, u32[]{:S(2)}) collective-permute-start(bf16[192,384]{1,0:T(8,128)(2,1)S(1)} %get-tuple-element.86), channel_id=1, source_target_pairs={{0,96},{32,0},{64,32},{96,64},{1,97},{33,1},{65,33},{97,65},{2,98}... | collective-permute-start | bytes 442376 | tf_op jit(solution)/shard_map/ppermute | solution.py:430
  42.4 1.4 %collective-permute-start.10 = (bf16[192,384]{1,0:T(8,128)(2,1)S(1)}, bf16[192,384]{1,0:T(8,128)(2,1)S(1)}, u32[]{:S(2)}, u32[]{:S(2)}) collective-permute-start(bf16[192,384]{1,0:T(8,128)(2,1)S(1)} %get-tuple-element.86), channel_id=1, source_target_pairs={{0,64},{32,96},{64,0},{96,32},{1,65},{33,97},{65,1},{97,33},{2,66}... | collective-permute-start | bytes 442376 | tf_op jit(solution)/shard_map/ppermute | solution.py:430
  43.8 2.9 %bring_even.1.resident_ref = bf16[3072,768]{1,0:T(8,128)(2,1)S(1)} custom-call(s32[5]{0:T(128)S(1)} %stack.38.place_ref, bf16[3072,1536]{1,0:T(8,128)(2,1)} %resident_ref.5), custom_call_target="tpu_custom_call" | custom-call | bytes 4718592 | tf_op jit(solution)/shard_map/bring_even/pallas_call | solution.py:244
  46.7 2.4 %collective-permute-done.10 = bf16[192,384]{1,0:T(8,128)(2,1)S(1)} collective-permute-done((bf16[192,384]{1,0:T(8,128)(2,1)S(1)}, bf16[192,384]{1,0:T(8,128)(2,1)S(1)}, u32[]{:S(2)}, u32[]{:S(2)}) %collective-permute-start.10) | collective-permute-done | bytes 147488 | tf_op jit(solution)/shard_map/ppermute | solution.py:430
  49.1 1.5 %collective-permute-done.9 = bf16[192,384]{1,0:T(8,128)(2,1)S(1)} collective-permute-done((bf16[192,384]{1,0:T(8,128)(2,1)S(1)}, bf16[192,384]{1,0:T(8,128)(2,1)S(1)}, u32[]{:S(2)}, u32[]{:S(2)}) %collective-permute-start.9) | collective-permute-done | bytes 147488 | tf_op jit(solution)/shard_map/ppermute | solution.py:430
  50.6 1.5 %collective-permute-start.12 = (bf16[192,384]{1,0:T(8,128)(2,1)S(1)}, bf16[192,384]{1,0:T(8,128)(2,1)S(1)}, u32[]{:S(2)}, u32[]{:S(2)}) collective-permute-start(bf16[192,384]{1,0:T(8,128)(2,1)S(1)} %collective-permute-done.7.refs_0_), channel_id=1, source_target_pairs={{0,4},{4,8},{8,12},{12,0},{1,5},{5,9},{9,13},{13,1},{2,6},{6,10},{... | collective-permute-start | bytes 442376 | tf_op jit(solution)/shard_map/ppermute | solution.py:435
  52.1 1.7 %collective-permute-start.16 = (bf16[192,384]{1,0:T(8,128)(2,1)S(1)}, bf16[192,384]{1,0:T(8,128)(2,1)S(1)}, u32[]{:S(2)}, u32[]{:S(2)}) collective-permute-start(bf16[192,384]{1,0:T(8,128)(2,1)S(1)} %collective-permute-done.8.refs_4_), channel_id=1, source_target_pairs={{0,12},{4,0},{8,4},{12,8},{1,13},{5,1},{9,5},{13,9},{2,14},{6,2},{... | collective-permute-start | bytes 442376 | tf_op jit(solution)/shard_map/ppermute | solution.py:435
  53.9 1.0 collective-permute-start.14
  54.9 2.1 %collective-permute-done.12.refs_1_ = bf16[192,384]{1,0:T(8,128)(2,1)S(1)} collective-permute-done((bf16[192,384]{1,0:T(8,128)(2,1)S(1)}, bf16[192,384]{1,0:T(8,128)(2,1)S(1)}, u32[]{:S(2)}, u32[]{:S(2)}) %collective-permute-start.12) | collective-permute-done | bytes 147488 | tf_op jit(solution)/shard_map/ppermute | solution.py:435
  57.3 1.4 %collective-permute-start.26 = (bf16[4,192,384]{2,1,0:T(8,128)(2,1)S(1)}, bf16[4,192,384]{2,1,0:T(8,128)(2,1)S(1)}, u32[]{:S(2)}, u32[]{:S(2)}) collective-permute-start(bf16[4,192,384]{2,1,0:T(8,128)(2,1)S(1)} %pad_maximum_fusion.own_ref), channel_id=1, source_target_pairs={{0,16},{16,0},{1,17},{17,1},{2,18},{18,2},{3,19},{19,3},{4,20},{20... | collective-permute-start | bytes 1769480 | tf_op jit(solution)/shard_map/ppermute | solution.py:466
  59.0 1.3 %collective-permute-start.13 = (bf16[192,384]{1,0:T(8,128)(2,1)S(1)}, bf16[192,384]{1,0:T(8,128)(2,1)S(1)}, u32[]{:S(2)}, u32[]{:S(2)}) collective-permute-start(bf16[192,384]{1,0:T(8,128)(2,1)S(1)} %collective-permute-done.12.refs_1_), channel_id=1, source_target_pairs={{0,4},{4,8},{8,12},{12,0},{1,5},{5,9},{9,13},{13,1},{2,6},{6,10},{... | collective-permute-start | bytes 442376 | tf_op jit(solution)/shard_map/ppermute | solution.py:435
  60.5 6.0 %collective-permute-done.15.refs_5_ = bf16[192,384]{1,0:T(8,128)(2,1)S(1)} collective-permute-done((bf16[192,384]{1,0:T(8,128)(2,1)S(1)}, bf16[192,384]{1,0:T(8,128)(2,1)S(1)}, u32[]{:S(2)}, u32[]{:S(2)}) %collective-permute-start.15) | collective-permute-done | bytes 147488 | tf_op jit(solution)/shard_map/ppermute | solution.py:435
  67.0 1.1 collective-permute-done.13.refs_2_
  68.1 2.0 %collective-permute-start.17 = (bf16[192,384]{1,0:T(8,128)(2,1)S(1)}, bf16[192,384]{1,0:T(8,128)(2,1)S(1)}, u32[]{:S(2)}, u32[]{:S(2)}) collective-permute-start(bf16[192,384]{1,0:T(8,128)(2,1)S(1)} %collective-permute-done.16.refs_7_), channel_id=1, source_target_pairs={{0,12},{4,0},{8,4},{12,8},{1,13},{5,1},{9,5},{13,9},{2,14},{6,2},{... | collective-permute-start | bytes 442376 | tf_op jit(solution)/shard_map/ppermute | solution.py:435
  70.7 2.5 %collective-permute-done.17.refs_6_ = bf16[192,384]{1,0:T(8,128)(2,1)S(1)} collective-permute-done((bf16[192,384]{1,0:T(8,128)(2,1)S(1)}, bf16[192,384]{1,0:T(8,128)(2,1)S(1)}, u32[]{:S(2)}, u32[]{:S(2)}) %collective-permute-start.17) | collective-permute-done | bytes 147488 | tf_op jit(solution)/shard_map/ppermute | solution.py:435
  73.2 1.1 next_memory.2.lhs_ref.own_ref
  74.3 1.6 %early_product.1.early_ref = f32[384,768]{1,0:T(8,128)S(1)} custom-call(s32[5]{0:T(128)S(1)} %stack.38.place_ref, bf16[384,1536]{1,0:T(8,128)(2,1)S(1)} %next_memory.2.lhs_ref.own_ref, bf16[3072,768]{1,0:T(8,128)(2,1)S(1)} %get-tuple-element.95.resident_ref), custom_call_target="tpu_custom_call" | custom-call | flops 905969664 | bytes 1179648 | tf_op jit(solution)/shard_map/early_product/pallas_call | solution.py:142
  76.0 1.1 next_memory.3.lhs_ref.other_ref
  77.1 1.8 %late_product.1 = (bf16[192,384]{1,0:T(8,128)(2,1)S(1)}, bf16[192,384]{1,0:T(8,128)(2,1)S(1)}, bf16[192,384]{1,0:T(8,128)(2,1)S(1)}, bf16[192,384]{1,0:T(8,128)(2,1)S(1)}) custom-call(s32[5]{0:T(128)S(1)} %stack.38.place_ref, f32[384,768]{1,0:T(8,128)S(1)} %early_product.1.early_ref, bf16[384,1536]{1,0:T(8,128)(2,1)S(1)} %next_memory.3.lhs_ref.other_ref, ...), custom_call_target="tpu_custom_call" | custom-call | flops 905969664 | bytes 1179648 | tf_op jit(solution)/shard_map/late_product/pallas_call | solution.py:175
  79.7 1.6 %collective-permute-start.28 = (bf16[192,384]{1,0:T(8,128)(2,1)S(1)}, bf16[192,384]{1,0:T(8,128)(2,1)S(1)}, u32[]{:S(2)}, u32[]{:S(2)}) collective-permute-start(bf16[192,384]{1,0:T(8,128)(2,1)S(1)} %get-tuple-element.110), channel_id=1, source_target_pairs={{0,32},{1,33},{2,34},{3,35},{4,36},{5,37},{6,38},{7,39},{8,40},{9,... | collective-permute-start | bytes 442376 | tf_op jit(solution)/shard_map/ppermute | solution.py:409
  81.3 2.4 %collective-permute-start.29 = (bf16[192,384]{1,0:T(8,128)(2,1)S(1)}, bf16[192,384]{1,0:T(8,128)(2,1)S(1)}, u32[]{:S(2)}, u32[]{:S(2)}) collective-permute-start(bf16[192,384]{1,0:T(8,128)(2,1)S(1)} %get-tuple-element.111), channel_id=1, source_target_pairs={{0,112},{1,113},{2,114},{3,115},{4,116},{5,117},{6,118},{7,119},{8... | collective-permute-start | bytes 442376 | tf_op jit(solution)/shard_map/ppermute | solution.py:409
  83.7 1.4 %collective-permute-start.30 = (bf16[192,384]{1,0:T(8,128)(2,1)S(1)}, bf16[192,384]{1,0:T(8,128)(2,1)S(1)}, u32[]{:S(2)}, u32[]{:S(2)}) collective-permute-start(bf16[192,384]{1,0:T(8,128)(2,1)S(1)} %get-tuple-element.112), channel_id=1, source_target_pairs={{0,96},{1,97},{2,98},{3,99},{4,100},{5,101},{6,102},{7,103},{8,104... | collective-permute-start | bytes 442376 | tf_op jit(solution)/shard_map/ppermute | solution.py:409
  85.1 2.7 %both_product.1 = (bf16[192,384]{1,0:T(8,128)(2,1)S(1)}, bf16[192,384]{1,0:T(8,128)(2,1)S(1)}, bf16[192,384]{1,0:T(8,128)(2,1)S(1)}, bf16[192,384]{1,0:T(8,128)(2,1)S(1)}) custom-call(s32[5]{0:T(128)S(1)} %stack.38.place_ref, bf16[384,1536]{1,0:T(8,128)(2,1)S(1)} %next_memory.2.lhs_ref.own_ref, bf16[384,1536]{1,0:T(8,128)(2,1)S(1)} %next_memory.3.lhs_ref.other_ref, ...), custom_call_target="tpu_custom_call" | custom-call | flops 905969664 | bytes 1179648 | tf_op jit(solution)/shard_map/both_product/pallas_call | solution.py:175
  87.8 1.8 %collective-permute-start.31 = (bf16[192,384]{1,0:T(8,128)(2,1)S(1)}, bf16[192,384]{1,0:T(8,128)(2,1)S(1)}, u32[]{:S(2)}, u32[]{:S(2)}) collective-permute-start(bf16[192,384]{1,0:T(8,128)(2,1)S(1)} %get-tuple-element.115), channel_id=1, source_target_pairs={{0,80},{1,81},{2,82},{3,83},{4,84},{5,85},{6,86},{7,87},{8,88},{9,... | collective-permute-start | bytes 442376 | tf_op jit(solution)/shard_map/ppermute | solution.py:409
  89.6 2.1 %collective-permute-start.32 = (bf16[192,384]{1,0:T(8,128)(2,1)S(1)}, bf16[192,384]{1,0:T(8,128)(2,1)S(1)}, u32[]{:S(2)}, u32[]{:S(2)}) collective-permute-start(bf16[192,384]{1,0:T(8,128)(2,1)S(1)} %get-tuple-element.116), channel_id=1, source_target_pairs={{0,64},{1,65},{2,66},{3,67},{4,68},{5,69},{6,70},{7,71},{8,72},{9,... | collective-permute-start | bytes 442376 | tf_op jit(solution)/shard_map/ppermute | solution.py:409
  91.7 1.2 collective-permute-start.33
  92.9 5.4 %collective-permute-done.30.refs_3_ = bf16[192,384]{1,0:T(8,128)(2,1)S(1)} collective-permute-done((bf16[192,384]{1,0:T(8,128)(2,1)S(1)}, bf16[192,384]{1,0:T(8,128)(2,1)S(1)}, u32[]{:S(2)}, u32[]{:S(2)}) %collective-permute-start.30) | collective-permute-done | bytes 147488 | tf_op jit(solution)/shard_map/ppermute | solution.py:409
  98.6 1.4 %second_solve.1.refs_0_ = bf16[192,384]{1,0:T(8,128)(2,1)S(1)} custom-call(s32[5]{0:T(128)S(1)} %stack.38.place_ref, bf16[192,384]{1,0:T(8,128)(2,1)S(1)} %collective-permute-done.27.refs_0_, bf16[192,384]{1,0:T(8,128)(2,1)S(1)} %collective-permute-done.28.refs_1_, bf16[192,384]{1,0:T(8,128)(2,1)S(1)} %collective-permute-done.29.refs_2_, ...), custom_call_target="tpu_custom_call" | custom-call | flops 339738624 | bytes 1769472 | tf_op jit(solution)/shard_map/second_solve/pallas_call | solution.py:340
  100.0 1.0 collective-permute-start.37
  101.1 1.9 %collective-permute-start.36 = (bf16[192,384]{1,0:T(8,128)(2,1)S(1)}, bf16[192,384]{1,0:T(8,128)(2,1)S(1)}, u32[]{:S(2)}, u32[]{:S(2)}) collective-permute-start(bf16[192,384]{1,0:T(8,128)(2,1)S(1)} %second_solve.1.refs_0_), channel_id=1, source_target_pairs={{0,96},{32,0},{64,32},{96,64},{1,97},{33,1},{65,33},{97,65},{2,98}... | collective-permute-start | bytes 442376 | tf_op jit(solution)/shard_map/ppermute | solution.py:430
  103.6 1.1 collective-permute-start.34
  105.3 2.4 %collective-permute-start.40 = (bf16[192,384]{1,0:T(8,128)(2,1)S(1)}, bf16[192,384]{1,0:T(8,128)(2,1)S(1)}, u32[]{:S(2)}, u32[]{:S(2)}) collective-permute-start(bf16[192,384]{1,0:T(8,128)(2,1)S(1)} %collective-permute-done.37.refs_4_), channel_id=1, source_target_pairs={{0,96},{32,0},{64,32},{96,64},{1,97},{33,1},{65,33},{97,65},{2,98}... | collective-permute-start | bytes 442376 | tf_op jit(solution)/shard_map/ppermute | solution.py:430
  109.3 1.8 %join_one.1.refs_8_ = bf16[2,384,1536]{2,1,0:T(8,128)(2,1)} custom-call(s32[5]{0:T(128)S(1)} %stack.38.place_ref, bf16[4,192,384]{2,1,0:T(8,128)(2,1)S(1)} %pad_maximum_fusion.own_ref, bf16[4,192,384]{2,1,0:T(8,128)(2,1)S(1)} %collective-permute-done.26.other_ref), custom_call_target="tpu_custom_call" | custom-call | flops 589824 | bytes 2359296 | tf_op jit(solution)/shard_map/join_one/pallas_call | solution.py:387
  111.1 4.0 %collective-permute-done.34.refs_1_ = bf16[192,384]{1,0:T(8,128)(2,1)S(1)} collective-permute-done((bf16[192,384]{1,0:T(8,128)(2,1)S(1)}, bf16[192,384]{1,0:T(8,128)(2,1)S(1)}, u32[]{:S(2)}, u32[]{:S(2)}) %collective-permute-start.34) | collective-permute-done | bytes 147488 | tf_op jit(solution)/shard_map/ppermute | solution.py:430
  115.1 1.9 %collective-permute-done.39.refs_6_ = bf16[192,384]{1,0:T(8,128)(2,1)S(1)} collective-permute-done((bf16[192,384]{1,0:T(8,128)(2,1)S(1)}, bf16[192,384]{1,0:T(8,128)(2,1)S(1)}, u32[]{:S(2)}, u32[]{:S(2)}) %collective-permute-start.39) | collective-permute-done | bytes 147488 | tf_op jit(solution)/shard_map/ppermute | solution.py:430
  117.0 1.5 %collective-permute-done.38.refs_5_ = bf16[192,384]{1,0:T(8,128)(2,1)S(1)} collective-permute-done((bf16[192,384]{1,0:T(8,128)(2,1)S(1)}, bf16[192,384]{1,0:T(8,128)(2,1)S(1)}, u32[]{:S(2)}, u32[]{:S(2)}) %collective-permute-start.38) | collective-permute-done | bytes 147488 | tf_op jit(solution)/shard_map/ppermute | solution.py:430
  118.6 1.8 %join_two.1 = bf16[2,384,1536]{2,1,0:T(8,128)(2,1)} custom-call(s32[5]{0:T(128)S(1)} %stack.38.place_ref, bf16[192,384]{1,0:T(8,128)(2,1)S(1)} %second_solve.1.refs_0_, bf16[192,384]{1,0:T(8,128)(2,1)S(1)} %collective-permute-done.34.refs_1_, bf16[192,384]{1,0:T(8,128)(2,1)S(1)} %collective-permute-done.35.refs_2_, ...), custom_call_target="tpu_custom_call", output_to_operand_aliasing={{}: (9, {})} | custom-call | flops 589824 | bytes 2359296 | tf_op jit(solution)/shard_map/join_two/pallas_call | solution.py:387
  (56 shorter events, 7.3 us)
Async XLA Ops:
  6.6 12.5 %collective-permute-start.1 = (bf16[192,384]{1,0:T(8,128)(2,1)S(1)}, bf16[192,384]{1,0:T(8,128)(2,1)S(1)}, u32[]{:S(2)}, u32[]{:S(2)}) collective-permute-start(bf16[192,384]{1,0:T(8,128)(2,1)S(1)} %get-tuple-element.64), channel_id=1, source_target_pairs={{0,32},{1,33},{2,34},{3,35},{4,36},{5,37},{6,38},{7,39},{8,40},{9,... | collective-permute-start | bytes 442376 | tf_op jit(solution)/shard_map/ppermute | solution.py:409
  8.3 12.4 %collective-permute-start = (bf16[192,384]{1,0:T(8,128)(2,1)S(1)}, bf16[192,384]{1,0:T(8,128)(2,1)S(1)}, u32[]{:S(2)}, u32[]{:S(2)}) collective-permute-start(bf16[192,384]{1,0:T(8,128)(2,1)S(1)} %get-tuple-element.65), channel_id=1, source_target_pairs={{0,48},{1,49},{2,50},{3,51},{4,52},{5,53},{6,54},{7,55},{8,56},{9,... | collective-permute-start | bytes 442376 | tf_op jit(solution)/shard_map/ppermute | solution.py:409
  10.1 11.1 %collective-permute-start.3 = (bf16[192,384]{1,0:T(8,128)(2,1)S(1)}, bf16[192,384]{1,0:T(8,128)(2,1)S(1)}, u32[]{:S(2)}, u32[]{:S(2)}) collective-permute-start(bf16[192,384]{1,0:T(8,128)(2,1)S(1)} %get-tuple-element.66), channel_id=1, source_target_pairs={{0,96},{1,97},{2,98},{3,99},{4,100},{5,101},{6,102},{7,103},{8,104... | collective-permute-start | bytes 442376 | tf_op jit(solution)/shard_map/ppermute | solution.py:409
  13.2 13.6 %collective-permute-start.2 = (bf16[192,384]{1,0:T(8,128)(2,1)S(1)}, bf16[192,384]{1,0:T(8,128)(2,1)S(1)}, u32[]{:S(2)}, u32[]{:S(2)}) collective-permute-start(bf16[192,384]{1,0:T(8,128)(2,1)S(1)} %get-tuple-element.67), channel_id=1, source_target_pairs={{0,112},{1,113},{2,114},{3,115},{4,116},{5,117},{6,118},{7,119},{8... | collective-permute-start | bytes 442376 | tf_op jit(solution)/shard_map/ppermute | solution.py:409
  13.2 5.9 %copy-start.1 = (f32[32,32]{1,0:T(8,128)S(1)}, f32[32,32]{1,0:T(8,128)}, u32[]{:S(2)}) copy-start(f32[32,32]{1,0:T(8,128)} %param.9) | copy-start | bytes 12292
  13.2 8.0 %copy-start = (f32[2,384,384]{2,1,0:T(8,128)S(1)}, f32[2,384,384]{2,1,0:T(8,128)}, u32[]{:S(2)}) copy-start(f32[2,384,384]{2,1,0:T(8,128)} %param.8) | copy-start | bytes 3538948
  15.8 14.7 %collective-permute-start.4 = (bf16[192,384]{1,0:T(8,128)(2,1)S(1)}, bf16[192,384]{1,0:T(8,128)(2,1)S(1)}, u32[]{:S(2)}, u32[]{:S(2)}) collective-permute-start(bf16[192,384]{1,0:T(8,128)(2,1)S(1)} %get-tuple-element.77), channel_id=1, source_target_pairs={{0,80},{1,81},{2,82},{3,83},{4,84},{5,85},{6,86},{7,87},{8,88},{9,... | collective-permute-start | bytes 442376 | tf_op jit(solution)/shard_map/ppermute | solution.py:409
  19.1 11.4 %collective-permute-start.5 = (bf16[192,384]{1,0:T(8,128)(2,1)S(1)}, bf16[192,384]{1,0:T(8,128)(2,1)S(1)}, u32[]{:S(2)}, u32[]{:S(2)}) collective-permute-start(bf16[192,384]{1,0:T(8,128)(2,1)S(1)} %get-tuple-element.78), channel_id=1, source_target_pairs={{0,64},{1,65},{2,66},{3,67},{4,68},{5,69},{6,70},{7,71},{8,72},{9,... | collective-permute-start | bytes 442376 | tf_op jit(solution)/shard_map/ppermute | solution.py:409
  20.8 9.8 %collective-permute-start.6 = (bf16[192,384]{1,0:T(8,128)(2,1)S(1)}, bf16[192,384]{1,0:T(8,128)(2,1)S(1)}, u32[]{:S(2)}, u32[]{:S(2)}) collective-permute-start(bf16[192,384]{1,0:T(8,128)(2,1)S(1)} %get-tuple-element.79), channel_id=1, source_target_pairs={{0,16},{1,17},{2,18},{3,19},{4,20},{5,21},{6,22},{7,23},{8,24},{9,... | collective-permute-start | bytes 442376 | tf_op jit(solution)/shard_map/ppermute | solution.py:409
  32.4 14.3 %collective-permute-start.8 = (bf16[192,384]{1,0:T(8,128)(2,1)S(1)}, bf16[192,384]{1,0:T(8,128)(2,1)S(1)}, u32[]{:S(2)}, u32[]{:S(2)}) collective-permute-start(bf16[192,384]{1,0:T(8,128)(2,1)S(1)} %get-tuple-element.81), channel_id=1, source_target_pairs={{0,10},{1,11},{2,26},{3,27},{4,46},{5,47},{6,62},{7,63},{8,66},{9,... | collective-permute-start | bytes 442376 | tf_op jit(solution)/shard_map/ppermute | solution.py:409
  38.5 8.2 %collective-permute-start.7 = (bf16[192,384]{1,0:T(8,128)(2,1)S(1)}, bf16[192,384]{1,0:T(8,128)(2,1)S(1)}, u32[]{:S(2)}, u32[]{:S(2)}) collective-permute-start(bf16[192,384]{1,0:T(8,128)(2,1)S(1)} %get-tuple-element.81), channel_id=1, source_target_pairs={{0,0},{1,1},{2,16},{3,17},{4,36},{5,37},{6,52},{7,53},{8,72},{9,73... | collective-permute-start | bytes 442376 | tf_op jit(solution)/shard_map/ppermute | solution.py:409
  39.2 7.5 %collective-permute-start.11 = (bf16[192,384]{1,0:T(8,128)(2,1)S(1)}, bf16[192,384]{1,0:T(8,128)(2,1)S(1)}, u32[]{:S(2)}, u32[]{:S(2)}) collective-permute-start(bf16[192,384]{1,0:T(8,128)(2,1)S(1)} %get-tuple-element.86), channel_id=1, source_target_pairs={{0,96},{32,0},{64,32},{96,64},{1,97},{33,1},{65,33},{97,65},{2,98}... | collective-permute-start | bytes 442376 | tf_op jit(solution)/shard_map/ppermute | solution.py:430
  42.4 6.7 %collective-permute-start.10 = (bf16[192,384]{1,0:T(8,128)(2,1)S(1)}, bf16[192,384]{1,0:T(8,128)(2,1)S(1)}, u32[]{:S(2)}, u32[]{:S(2)}) collective-permute-start(bf16[192,384]{1,0:T(8,128)(2,1)S(1)} %get-tuple-element.86), channel_id=1, source_target_pairs={{0,64},{32,96},{64,0},{96,32},{1,65},{33,97},{65,1},{97,33},{2,66}... | collective-permute-start | bytes 442376 | tf_op jit(solution)/shard_map/ppermute | solution.py:430
  43.8 6.9 %collective-permute-start.9 = (bf16[192,384]{1,0:T(8,128)(2,1)S(1)}, bf16[192,384]{1,0:T(8,128)(2,1)S(1)}, u32[]{:S(2)}, u32[]{:S(2)}) collective-permute-start(bf16[192,384]{1,0:T(8,128)(2,1)S(1)} %get-tuple-element.86), channel_id=1, source_target_pairs={{0,32},{32,64},{64,96},{96,0},{1,33},{33,65},{65,97},{97,1},{2,34}... | collective-permute-start | bytes 442376 | tf_op jit(solution)/shard_map/ppermute | solution.py:430
  50.6 6.4 %collective-permute-start.12 = (bf16[192,384]{1,0:T(8,128)(2,1)S(1)}, bf16[192,384]{1,0:T(8,128)(2,1)S(1)}, u32[]{:S(2)}, u32[]{:S(2)}) collective-permute-start(bf16[192,384]{1,0:T(8,128)(2,1)S(1)} %collective-permute-done.7.refs_0_), channel_id=1, source_target_pairs={{0,4},{4,8},{8,12},{12,0},{1,5},{5,9},{9,13},{13,1},{2,6},{6,10},{... | collective-permute-start | bytes 442376 | tf_op jit(solution)/shard_map/ppermute | solution.py:435
  52.1 5.1 %collective-permute-start.16 = (bf16[192,384]{1,0:T(8,128)(2,1)S(1)}, bf16[192,384]{1,0:T(8,128)(2,1)S(1)}, u32[]{:S(2)}, u32[]{:S(2)}) collective-permute-start(bf16[192,384]{1,0:T(8,128)(2,1)S(1)} %collective-permute-done.8.refs_4_), channel_id=1, source_target_pairs={{0,12},{4,0},{8,4},{12,8},{1,13},{5,1},{9,5},{13,9},{2,14},{6,2},{... | collective-permute-start | bytes 442376 | tf_op jit(solution)/shard_map/ppermute | solution.py:435
  53.9 5.1 %collective-permute-start.14 = (bf16[192,384]{1,0:T(8,128)(2,1)S(1)}, bf16[192,384]{1,0:T(8,128)(2,1)S(1)}, u32[]{:S(2)}, u32[]{:S(2)}) collective-permute-start(bf16[192,384]{1,0:T(8,128)(2,1)S(1)} %collective-permute-done.7.refs_0_), channel_id=1, source_target_pairs={{0,12},{4,0},{8,4},{12,8},{1,13},{5,1},{9,5},{13,9},{2,14},{6,2},{... | collective-permute-start | bytes 442376 | tf_op jit(solution)/shard_map/ppermute | solution.py:435
  57.3 18.7 %collective-permute-start.26 = (bf16[4,192,384]{2,1,0:T(8,128)(2,1)S(1)}, bf16[4,192,384]{2,1,0:T(8,128)(2,1)S(1)}, u32[]{:S(2)}, u32[]{:S(2)}) collective-permute-start(bf16[4,192,384]{2,1,0:T(8,128)(2,1)S(1)} %pad_maximum_fusion.own_ref), channel_id=1, source_target_pairs={{0,16},{16,0},{1,17},{17,1},{2,18},{18,2},{3,19},{19,3},{4,20},{20... | collective-permute-start | bytes 1769480 | tf_op jit(solution)/shard_map/ppermute | solution.py:466
  58.7 7.8 %collective-permute-start.15 = (bf16[192,384]{1,0:T(8,128)(2,1)S(1)}, bf16[192,384]{1,0:T(8,128)(2,1)S(1)}, u32[]{:S(2)}, u32[]{:S(2)}) collective-permute-start(bf16[192,384]{1,0:T(8,128)(2,1)S(1)} %collective-permute-done.8.refs_4_), channel_id=1, source_target_pairs={{0,4},{4,8},{8,12},{12,0},{1,5},{5,9},{9,13},{13,1},{2,6},{6,10},{... | collective-permute-start | bytes 442376 | tf_op jit(solution)/shard_map/ppermute | solution.py:435
  59.0 7.5 %collective-permute-start.21 = (bf16[192,384]{1,0:T(8,128)(2,1)S(1)}, bf16[192,384]{1,0:T(8,128)(2,1)S(1)}, u32[]{:S(2)}, u32[]{:S(2)}) collective-permute-start(bf16[192,384]{1,0:T(8,128)(2,1)S(1)} %collective-permute-done.14.refs_3_), channel_id=1, source_target_pairs={{0,1},{1,0},{2,3},{3,2},{4,5},{5,4},{6,7},{7,6},{8,9},{9,8},{10,11... | collective-permute-start | bytes 442376 | tf_op jit(solution)/shard_map/ppermute | solution.py:467
  59.0 9.1 %collective-permute-start.13 = (bf16[192,384]{1,0:T(8,128)(2,1)S(1)}, bf16[192,384]{1,0:T(8,128)(2,1)S(1)}, u32[]{:S(2)}, u32[]{:S(2)}) collective-permute-start(bf16[192,384]{1,0:T(8,128)(2,1)S(1)} %collective-permute-done.12.refs_1_), channel_id=1, source_target_pairs={{0,4},{4,8},{8,12},{12,0},{1,5},{5,9},{9,13},{13,1},{2,6},{6,10},{... | collective-permute-start | bytes 442376 | tf_op jit(solution)/shard_map/ppermute | solution.py:435
  60.3 9.8 %collective-permute-start.18 = (bf16[192,384]{1,0:T(8,128)(2,1)S(1)}, bf16[192,384]{1,0:T(8,128)(2,1)S(1)}, u32[]{:S(2)}, u32[]{:S(2)}) collective-permute-start(bf16[192,384]{1,0:T(8,128)(2,1)S(1)} %collective-permute-done.7.refs_0_), channel_id=1, source_target_pairs={{0,1},{1,0},{2,3},{3,2},{4,5},{5,4},{6,7},{7,6},{8,9},{9,8},{10,11... | collective-permute-start | bytes 442376 | tf_op jit(solution)/shard_map/ppermute | solution.py:467
  66.5 3.6 %collective-permute-start.19 = (bf16[192,384]{1,0:T(8,128)(2,1)S(1)}, bf16[192,384]{1,0:T(8,128)(2,1)S(1)}, u32[]{:S(2)}, u32[]{:S(2)}) collective-permute-start(bf16[192,384]{1,0:T(8,128)(2,1)S(1)} %collective-permute-done.12.refs_1_), channel_id=1, source_target_pairs={{0,1},{1,0},{2,3},{3,2},{4,5},{5,4},{6,7},{7,6},{8,9},{9,8},{10,11... | collective-permute-start | bytes 442376 | tf_op jit(solution)/shard_map/ppermute | solution.py:467
  66.5 4.1 %collective-permute-start.22 = (bf16[192,384]{1,0:T(8,128)(2,1)S(1)}, bf16[192,384]{1,0:T(8,128)(2,1)S(1)}, u32[]{:S(2)}, u32[]{:S(2)}) collective-permute-start(bf16[192,384]{1,0:T(8,128)(2,1)S(1)} %collective-permute-done.8.refs_4_), channel_id=1, source_target_pairs={{0,1},{1,0},{2,3},{3,2},{4,5},{5,4},{6,7},{7,6},{8,9},{9,8},{10,11... | collective-permute-start | bytes 442376 | tf_op jit(solution)/shard_map/ppermute | solution.py:467
  68.1 5.1 %collective-permute-start.17 = (bf16[192,384]{1,0:T(8,128)(2,1)S(1)}, bf16[192,384]{1,0:T(8,128)(2,1)S(1)}, u32[]{:S(2)}, u32[]{:S(2)}) collective-permute-start(bf16[192,384]{1,0:T(8,128)(2,1)S(1)} %collective-permute-done.16.refs_7_), channel_id=1, source_target_pairs={{0,12},{4,0},{8,4},{12,8},{1,13},{5,1},{9,5},{13,9},{2,14},{6,2},{... | collective-permute-start | bytes 442376 | tf_op jit(solution)/shard_map/ppermute | solution.py:435
  70.1 5.9 %collective-permute-start.25 = (bf16[192,384]{1,0:T(8,128)(2,1)S(1)}, bf16[192,384]{1,0:T(8,128)(2,1)S(1)}, u32[]{:S(2)}, u32[]{:S(2)}) collective-permute-start(bf16[192,384]{1,0:T(8,128)(2,1)S(1)} %collective-permute-done.16.refs_7_), channel_id=1, source_target_pairs={{0,1},{1,0},{2,3},{3,2},{4,5},{5,4},{6,7},{7,6},{8,9},{9,8},{10,11... | collective-permute-start | bytes 442376 | tf_op jit(solution)/shard_map/ppermute | solution.py:467
  70.1 5.9 %collective-permute-start.23 = (bf16[192,384]{1,0:T(8,128)(2,1)S(1)}, bf16[192,384]{1,0:T(8,128)(2,1)S(1)}, u32[]{:S(2)}, u32[]{:S(2)}) collective-permute-start(bf16[192,384]{1,0:T(8,128)(2,1)S(1)} %collective-permute-done.15.refs_5_), channel_id=1, source_target_pairs={{0,1},{1,0},{2,3},{3,2},{4,5},{5,4},{6,7},{7,6},{8,9},{9,8},{10,11... | collective-permute-start | bytes 442376 | tf_op jit(solution)/shard_map/ppermute | solution.py:467
  70.6 5.4 %collective-permute-start.20 = (bf16[192,384]{1,0:T(8,128)(2,1)S(1)}, bf16[192,384]{1,0:T(8,128)(2,1)S(1)}, u32[]{:S(2)}, u32[]{:S(2)}) collective-permute-start(bf16[192,384]{1,0:T(8,128)(2,1)S(1)} %collective-permute-done.13.refs_2_), channel_id=1, source_target_pairs={{0,1},{1,0},{2,3},{3,2},{4,5},{5,4},{6,7},{7,6},{8,9},{9,8},{10,11... | collective-permute-start | bytes 442376 | tf_op jit(solution)/shard_map/ppermute | solution.py:467
  73.2 2.8 %collective-permute-start.24 = (bf16[192,384]{1,0:T(8,128)(2,1)S(1)}, bf16[192,384]{1,0:T(8,128)(2,1)S(1)}, u32[]{:S(2)}, u32[]{:S(2)}) collective-permute-start(bf16[192,384]{1,0:T(8,128)(2,1)S(1)} %collective-permute-done.17.refs_6_), channel_id=1, source_target_pairs={{0,1},{1,0},{2,3},{3,2},{4,5},{5,4},{6,7},{7,6},{8,9},{9,8},{10,11... | collective-permute-start | bytes 442376 | tf_op jit(solution)/shard_map/ppermute | solution.py:467
  78.9 10.7 %collective-permute-start.27 = (bf16[192,384]{1,0:T(8,128)(2,1)S(1)}, bf16[192,384]{1,0:T(8,128)(2,1)S(1)}, u32[]{:S(2)}, u32[]{:S(2)}) collective-permute-start(bf16[192,384]{1,0:T(8,128)(2,1)S(1)} %get-tuple-element.109), channel_id=1, source_target_pairs={{0,48},{1,49},{2,50},{3,51},{4,52},{5,53},{6,54},{7,55},{8,56},{9,... | collective-permute-start | bytes 442376 | tf_op jit(solution)/shard_map/ppermute | solution.py:409
  79.7 12.0 %collective-permute-start.28 = (bf16[192,384]{1,0:T(8,128)(2,1)S(1)}, bf16[192,384]{1,0:T(8,128)(2,1)S(1)}, u32[]{:S(2)}, u32[]{:S(2)}) collective-permute-start(bf16[192,384]{1,0:T(8,128)(2,1)S(1)} %get-tuple-element.110), channel_id=1, source_target_pairs={{0,32},{1,33},{2,34},{3,35},{4,36},{5,37},{6,38},{7,39},{8,40},{9,... | collective-permute-start | bytes 442376 | tf_op jit(solution)/shard_map/ppermute | solution.py:409
  81.3 11.6 %collective-permute-start.29 = (bf16[192,384]{1,0:T(8,128)(2,1)S(1)}, bf16[192,384]{1,0:T(8,128)(2,1)S(1)}, u32[]{:S(2)}, u32[]{:S(2)}) collective-permute-start(bf16[192,384]{1,0:T(8,128)(2,1)S(1)} %get-tuple-element.111), channel_id=1, source_target_pairs={{0,112},{1,113},{2,114},{3,115},{4,116},{5,117},{6,118},{7,119},{8... | collective-permute-start | bytes 442376 | tf_op jit(solution)/shard_map/ppermute | solution.py:409
  83.7 14.5 %collective-permute-start.30 = (bf16[192,384]{1,0:T(8,128)(2,1)S(1)}, bf16[192,384]{1,0:T(8,128)(2,1)S(1)}, u32[]{:S(2)}, u32[]{:S(2)}) collective-permute-start(bf16[192,384]{1,0:T(8,128)(2,1)S(1)} %get-tuple-element.112), channel_id=1, source_target_pairs={{0,96},{1,97},{2,98},{3,99},{4,100},{5,101},{6,102},{7,103},{8,104... | collective-permute-start | bytes 442376 | tf_op jit(solution)/shard_map/ppermute | solution.py:409
  87.8 10.5 %collective-permute-start.31 = (bf16[192,384]{1,0:T(8,128)(2,1)S(1)}, bf16[192,384]{1,0:T(8,128)(2,1)S(1)}, u32[]{:S(2)}, u32[]{:S(2)}) collective-permute-start(bf16[192,384]{1,0:T(8,128)(2,1)S(1)} %get-tuple-element.115), channel_id=1, source_target_pairs={{0,80},{1,81},{2,82},{3,83},{4,84},{5,85},{6,86},{7,87},{8,88},{9,... | collective-permute-start | bytes 442376 | tf_op jit(solution)/shard_map/ppermute | solution.py:409
  89.6 8.7 %collective-permute-start.32 = (bf16[192,384]{1,0:T(8,128)(2,1)S(1)}, bf16[192,384]{1,0:T(8,128)(2,1)S(1)}, u32[]{:S(2)}, u32[]{:S(2)}) collective-permute-start(bf16[192,384]{1,0:T(8,128)(2,1)S(1)} %get-tuple-element.116), channel_id=1, source_target_pairs={{0,64},{1,65},{2,66},{3,67},{4,68},{5,69},{6,70},{7,71},{8,72},{9,... | collective-permute-start | bytes 442376 | tf_op jit(solution)/shard_map/ppermute | solution.py:409
  91.7 6.9 %collective-permute-start.33 = (bf16[192,384]{1,0:T(8,128)(2,1)S(1)}, bf16[192,384]{1,0:T(8,128)(2,1)S(1)}, u32[]{:S(2)}, u32[]{:S(2)}) collective-permute-start(bf16[192,384]{1,0:T(8,128)(2,1)S(1)} %get-tuple-element.117), channel_id=1, source_target_pairs={{0,16},{1,17},{2,18},{3,19},{4,20},{5,21},{6,22},{7,23},{8,24},{9,... | collective-permute-start | bytes 442376 | tf_op jit(solution)/shard_map/ppermute | solution.py:409
  100.0 5.3 %collective-permute-start.37 = (bf16[192,384]{1,0:T(8,128)(2,1)S(1)}, bf16[192,384]{1,0:T(8,128)(2,1)S(1)}, u32[]{:S(2)}, u32[]{:S(2)}) collective-permute-start(bf16[192,384]{1,0:T(8,128)(2,1)S(1)} %second_solve.1.refs_0_), channel_id=1, source_target_pairs={{0,16},{16,0},{1,17},{17,1},{2,18},{18,2},{3,19},{19,3},{4,20},{20... | collective-permute-start | bytes 442376 | tf_op jit(solution)/shard_map/ppermute | solution.py:479
  101.1 7.5 %collective-permute-start.36 = (bf16[192,384]{1,0:T(8,128)(2,1)S(1)}, bf16[192,384]{1,0:T(8,128)(2,1)S(1)}, u32[]{:S(2)}, u32[]{:S(2)}) collective-permute-start(bf16[192,384]{1,0:T(8,128)(2,1)S(1)} %second_solve.1.refs_0_), channel_id=1, source_target_pairs={{0,96},{32,0},{64,32},{96,64},{1,97},{33,1},{65,33},{97,65},{2,98}... | collective-permute-start | bytes 442376 | tf_op jit(solution)/shard_map/ppermute | solution.py:430
  103.0 8.1 %collective-permute-start.35 = (bf16[192,384]{1,0:T(8,128)(2,1)S(1)}, bf16[192,384]{1,0:T(8,128)(2,1)S(1)}, u32[]{:S(2)}, u32[]{:S(2)}) collective-permute-start(bf16[192,384]{1,0:T(8,128)(2,1)S(1)} %second_solve.1.refs_0_), channel_id=1, source_target_pairs={{0,64},{32,96},{64,0},{96,32},{1,65},{33,97},{65,1},{97,33},{2,66}... | collective-permute-start | bytes 442376 | tf_op jit(solution)/shard_map/ppermute | solution.py:430
  103.6 11.5 %collective-permute-start.34 = (bf16[192,384]{1,0:T(8,128)(2,1)S(1)}, bf16[192,384]{1,0:T(8,128)(2,1)S(1)}, u32[]{:S(2)}, u32[]{:S(2)}) collective-permute-start(bf16[192,384]{1,0:T(8,128)(2,1)S(1)} %second_solve.1.refs_0_), channel_id=1, source_target_pairs={{0,32},{32,64},{64,96},{96,0},{1,33},{33,65},{65,97},{97,1},{2,34}... | collective-permute-start | bytes 442376 | tf_op jit(solution)/shard_map/ppermute | solution.py:430
  105.3 9.8 %collective-permute-start.40 = (bf16[192,384]{1,0:T(8,128)(2,1)S(1)}, bf16[192,384]{1,0:T(8,128)(2,1)S(1)}, u32[]{:S(2)}, u32[]{:S(2)}) collective-permute-start(bf16[192,384]{1,0:T(8,128)(2,1)S(1)} %collective-permute-done.37.refs_4_), channel_id=1, source_target_pairs={{0,96},{32,0},{64,32},{96,64},{1,97},{33,1},{65,33},{97,65},{2,98}... | collective-permute-start | bytes 442376 | tf_op jit(solution)/shard_map/ppermute | solution.py:430
  107.7 9.3 %collective-permute-start.39 = (bf16[192,384]{1,0:T(8,128)(2,1)S(1)}, bf16[192,384]{1,0:T(8,128)(2,1)S(1)}, u32[]{:S(2)}, u32[]{:S(2)}) collective-permute-start(bf16[192,384]{1,0:T(8,128)(2,1)S(1)} %collective-permute-done.37.refs_4_), channel_id=1, source_target_pairs={{0,64},{32,96},{64,0},{96,32},{1,65},{33,97},{65,1},{97,33},{2,66}... | collective-permute-start | bytes 442376 | tf_op jit(solution)/shard_map/ppermute | solution.py:430
  108.6 10.0 %collective-permute-start.38 = (bf16[192,384]{1,0:T(8,128)(2,1)S(1)}, bf16[192,384]{1,0:T(8,128)(2,1)S(1)}, u32[]{:S(2)}, u32[]{:S(2)}) collective-permute-start(bf16[192,384]{1,0:T(8,128)(2,1)S(1)} %collective-permute-done.37.refs_4_), channel_id=1, source_target_pairs={{0,32},{32,64},{64,96},{96,0},{1,33},{33,65},{65,97},{97,1},{2,34}... | collective-permute-start | bytes 442376 | tf_op jit(solution)/shard_map/ppermute | solution.py:430

commit v13 on v11

--- a/solution.py
+++ b/solution.py
@@ -451,7 +451,7 @@
     ones = spread(front_one, "y")
     later, _ = lax.optimization_barrier((place, energy))
     even_resident = bring_even(later, resident)
-    pair, ones, even_resident = lax.optimization_barrier((pair, ones, even_resident))
+    pair, even_resident = lax.optimization_barrier((pair, even_resident))
     own = spread(jnp.stack(pair), "x")
     ones = jnp.stack(ones)
     others = lax.ppermute(ones, "zl", SWAP)

time: 113 us -> 109 us (0.965)
  waiting for transfers between devices: 34.2 us -> 29.6 us
  starting transfers between devices: 46.5 us -> 47.8 us
    ppermute x12, waiting for transfers between devices: 20.9 us -> 16.7 us  [spread(): pairs[d] = lax.ppermute(pair, axis, [(i, (i + d) % 4) for i in range(4)])]
    ppermute x12, starting transfers between devices: 13.7 us -> 15.2 us  [spread(): pairs[d] = lax.ppermute(pair, axis, [(i, (i + d) % 4) for i in range(4)])]
  transfers between devices with their start and end apart: 34 -> 34, of which waited for: 12 -> 13; matrix products, arithmetic and copies ran while one was open for 0% -> 0% of each run, Pallas kernels for 15% -> 15%
where the time goes in v13:
time: 109 us
  starting transfers between devices  47.8 us (44%)
  Pallas kernels  31 us (28%)
  waiting for transfers between devices  29.6 us (27%)
    ppermute x16, starting transfers between devices, move(): return lax.ppermute(value, ALL, pairs)  29.8 us
    ppermute x12, waiting for transfers between devices, spread(): pairs[d] = lax.ppermute(pair, axis, [(i, (i + d) % 4) for i in range(4)])  16.7 us
    ppermute x12, starting transfers between devices, spread(): pairs[d] = lax.ppermute(pair, axis, [(i, (i + d) % 4) for i in range(4)])  15.2 us
    ppermute x16, waiting for transfers between devices, move(): return lax.ppermute(value, ALL, pairs)  11.4 us
    pallas_call x1, Pallas kernels, first_product(): pl.pallas_call(first_product_kernel, in_specs=[SMEM] + [pl.BlockSpec(memo...  6.5 us
    pallas_call x2, Pallas kernels, second_product(): pl.pallas_call(kernel, in_specs=[SMEM] + [VMEM] * 3, out_specs=[VMEM] * 4...  4.41 us
    pallas_call x1, Pallas kernels, bring_odd(): pl.pallas_call(bring_odd_kernel, in_specs=[SMEM] + [HBM] * 3, out_specs=[...  3.83 us
    pallas_call x2, Pallas kernels, join(): pl.pallas_call(kernel, in_specs=in_specs, out_specs=HBM, out_shape=jax.Sh...  3.61 us
  transfers between devices with their start and end apart: 34, of which 13 were waited for; matrix products, arithmetic and copies ran while one was open for 0% of the time, Pallas kernels for 15%

profile of v13, /device:TPU:0, one launch (start us, length us, event | category | flops | bytes accessed | tf_op | source)
XLA Modules:
  0.0 109.2 jit_solution(8872148752196591440)
XLA Ops:
  0.1 6.5 %first_product.1 = (bf16[192,384]{1,0:T(8,128)(2,1)S(1)}, bf16[192,384]{1,0:T(8,128)(2,1)S(1)}, bf16[192,384]{1,0:T(8,128)(2,1)S(1)}, bf16[192,384]{1,0:T(8,128)...) custom-call(s32[5]{0:T(128)S(1)} %stack.47.place_ref, bf16[2,384,3072]{2,1,0:T(8,128)(2,1)} %memory_ref.3, ...), custom_call_target="tpu_custom_call" | custom-call | flops 1811939328 | bytes 18874368 | tf_op jit(solution)/shard_map/first_product/pallas_call | solution.py:112
  6.6 1.7 %collective-permute-start.1 = (bf16[192,384]{1,0:T(8,128)(2,1)S(1)}, bf16[192,384]{1,0:T(8,128)(2,1)S(1)}, u32[]{:S(2)}, u32[]{:S(2)}) collective-permute-start(bf16[192,384]{1,0:T(8,128)(2,1)S(1)} %get-tuple-element.51), channel_id=1, source_target_pairs={{0,32},{1,33},{2,34},{3,35},{4,36},{5,37},{6,38},{7,39},{8,40},{9,... | collective-permute-start | bytes 442376 | tf_op jit(solution)/shard_map/ppermute | solution.py:409
  8.3 1.8 %collective-permute-start = (bf16[192,384]{1,0:T(8,128)(2,1)S(1)}, bf16[192,384]{1,0:T(8,128)(2,1)S(1)}, u32[]{:S(2)}, u32[]{:S(2)}) collective-permute-start(bf16[192,384]{1,0:T(8,128)(2,1)S(1)} %get-tuple-element.52), channel_id=1, source_target_pairs={{0,48},{1,49},{2,50},{3,51},{4,52},{5,53},{6,54},{7,55},{8,56},{9,... | collective-permute-start | bytes 442376 | tf_op jit(solution)/shard_map/ppermute | solution.py:409
  10.1 3.0 %collective-permute-start.3 = (bf16[192,384]{1,0:T(8,128)(2,1)S(1)}, bf16[192,384]{1,0:T(8,128)(2,1)S(1)}, u32[]{:S(2)}, u32[]{:S(2)}) collective-permute-start(bf16[192,384]{1,0:T(8,128)(2,1)S(1)} %get-tuple-element.53), channel_id=1, source_target_pairs={{0,96},{1,97},{2,98},{3,99},{4,100},{5,101},{6,102},{7,103},{8,104... | collective-permute-start | bytes 442376 | tf_op jit(solution)/shard_map/ppermute | solution.py:409
  13.2 2.7 %half_product.1 = (bf16[192,384]{1,0:T(8,128)(2,1)S(1)}, bf16[192,384]{1,0:T(8,128)(2,1)S(1)}, bf16[192,384]{1,0:T(8,128)(2,1)S(1)}, bf16[192,384]{1,0:T(8,128)(2,1)S(1)}) custom-call(s32[5]{0:T(128)S(1)} %stack.47.place_ref, bf16[384,3072]{1,0:T(8,128)(2,1)S(1)} %get-tuple-element.55.lhs_ref, bf16[3072,768]{1,0:T(8,128)(2,1)S(1)} %get-tuple-element.56.resident_ref), custom_call_target="tpu_custom_call" | custom-call | flops 1811939328 | bytes 294912 | tf_op jit(solution)/shard_map/half_product/pallas_call | solution.py:60
  15.8 3.2 %collective-permute-start.4 = (bf16[192,384]{1,0:T(8,128)(2,1)S(1)}, bf16[192,384]{1,0:T(8,128)(2,1)S(1)}, u32[]{:S(2)}, u32[]{:S(2)}) collective-permute-start(bf16[192,384]{1,0:T(8,128)(2,1)S(1)} %get-tuple-element.64), channel_id=1, source_target_pairs={{0,80},{1,81},{2,82},{3,83},{4,84},{5,85},{6,86},{7,87},{8,88},{9,... | collective-permute-start | bytes 442376 | tf_op jit(solution)/shard_map/ppermute | solution.py:409
  19.1 1.6 %collective-permute-start.5 = (bf16[192,384]{1,0:T(8,128)(2,1)S(1)}, bf16[192,384]{1,0:T(8,128)(2,1)S(1)}, u32[]{:S(2)}, u32[]{:S(2)}) collective-permute-start(bf16[192,384]{1,0:T(8,128)(2,1)S(1)} %get-tuple-element.65), channel_id=1, source_target_pairs={{0,64},{1,65},{2,66},{3,67},{4,68},{5,69},{6,70},{7,71},{8,72},{9,... | collective-permute-start | bytes 442376 | tf_op jit(solution)/shard_map/ppermute | solution.py:409
  21.2 5.5 %collective-permute-done.2.refs_2_ = bf16[192,384]{1,0:T(8,128)(2,1)S(1)} collective-permute-done((bf16[192,384]{1,0:T(8,128)(2,1)S(1)}, bf16[192,384]{1,0:T(8,128)(2,1)S(1)}, u32[]{:S(2)}, u32[]{:S(2)}) %collective-permute-start.2) | collective-permute-done | bytes 147488 | tf_op jit(solution)/shard_map/ppermute | solution.py:409
  26.7 3.8 %bring_odd.1 = (bf16[384,3072]{1,0:T(8,128)(2,1)S(1)}, bf16[192,384]{1,0:T(8,128)(2,1)S(1)}, bf16[192,384]{1,0:T(8,128)(2,1)S(1)}, bf16[3072,768]{1,0:T(8,128)(2,1)S(1)}) custom-call(s32[5]{0:T(128)S(1)} %stack.47.place_ref, bf16[2,384,3072]{2,1,0:T(8,128)(2,1)} %memory_ref.3, bf16[2,384,1536]{2,1,0:T(8,128)(2,1)} %previous_ref.1, ...), custom_call_target="tpu_custom_call" | custom-call | bytes 7077888 | tf_op jit(solution)/shard_map/bring_odd/pallas_call | solution.py:220
  30.6 1.8 %first_solve.1 = (bf16[192,384]{1,0:T(8,128)(2,1)S(1)}, bf16[192,384]{1,0:T(8,128)(2,1)S(1)}) custom-call(s32[5]{0:T(128)S(1)} %stack.47.place_ref, bf16[192,384]{1,0:T(8,128)(2,1)S(1)} %collective-permute-done.refs_0_, bf16[192,384]{1,0:T(8,128)(2,1)S(1)} %collective-permute-done.1.refs_1_, bf16[192,384]{1,0:T(8,128)(2,1)S(1)} %collective-permute-done.2.refs_2_, ...), custom_call_target="tpu_custom_call" | custom-call | flops 339738624 | bytes 1769472 | tf_op jit(solution)/shard_map/first_solve/pallas_call | solution.py:340
  32.4 6.1 %collective-permute-start.8 = (bf16[192,384]{1,0:T(8,128)(2,1)S(1)}, bf16[192,384]{1,0:T(8,128)(2,1)S(1)}, u32[]{:S(2)}, u32[]{:S(2)}) collective-permute-start(bf16[192,384]{1,0:T(8,128)(2,1)S(1)} %get-tuple-element.68), channel_id=1, source_target_pairs={{0,10},{1,11},{2,26},{3,27},{4,46},{5,47},{6,62},{7,63},{8,66},{9,... | collective-permute-start | bytes 442376 | tf_op jit(solution)/shard_map/ppermute | solution.py:409
  38.5 0.7 collective-permute-start.7
  39.2 3.2 %collective-permute-start.18 = (bf16[192,384]{1,0:T(8,128)(2,1)S(1)}, bf16[192,384]{1,0:T(8,128)(2,1)S(1)}, u32[]{:S(2)}, u32[]{:S(2)}) collective-permute-start(bf16[192,384]{1,0:T(8,128)(2,1)S(1)} %get-tuple-element.72), channel_id=1, source_target_pairs={{0,96},{32,0},{64,32},{96,64},{1,97},{33,1},{65,33},{97,65},{2,98}... | collective-permute-start | bytes 442376 | tf_op jit(solution)/shard_map/ppermute | solution.py:430
  42.4 1.4 %collective-permute-start.17 = (bf16[192,384]{1,0:T(8,128)(2,1)S(1)}, bf16[192,384]{1,0:T(8,128)(2,1)S(1)}, u32[]{:S(2)}, u32[]{:S(2)}) collective-permute-start(bf16[192,384]{1,0:T(8,128)(2,1)S(1)} %get-tuple-element.72), channel_id=1, source_target_pairs={{0,64},{32,96},{64,0},{96,32},{1,65},{33,97},{65,1},{97,33},{2,66}... | collective-permute-start | bytes 442376 | tf_op jit(solution)/shard_map/ppermute | solution.py:430
  43.8 2.9 %bring_even.1.resident_ref = bf16[3072,768]{1,0:T(8,128)(2,1)S(1)} custom-call(s32[5]{0:T(128)S(1)} %stack.47.place_ref, bf16[3072,1536]{1,0:T(8,128)(2,1)} %resident_ref.5), custom_call_target="tpu_custom_call" | custom-call | bytes 4718592 | tf_op jit(solution)/shard_map/bring_even/pallas_call | solution.py:244
  46.7 2.1 %collective-permute-start.11 = (bf16[2,192,384]{2,1,0:T(8,128)(2,1)S(1)}, bf16[2,192,384]{2,1,0:T(8,128)(2,1)S(1)}, u32[]{:S(2)}, u32[]{:S(2)}) collective-permute-start(bf16[2,192,384]{2,1,0:T(8,128)(2,1)S(1)} %pad_maximum_fusion.1.refs_0_), channel_id=1, source_target_pairs={{0,12},{4,0},{8,4},{12,8},{1,13},{5,1},{9,5},{13,9},{2,14},{6,2},{... | collective-permute-start | bytes 884744 | tf_op jit(solution)/shard_map/ppermute | solution.py:430
  48.8 2.0 %collective-permute-start.10 = (bf16[2,192,384]{2,1,0:T(8,128)(2,1)S(1)}, bf16[2,192,384]{2,1,0:T(8,128)(2,1)S(1)}, u32[]{:S(2)}, u32[]{:S(2)}) collective-permute-start(bf16[2,192,384]{2,1,0:T(8,128)(2,1)S(1)} %pad_maximum_fusion.1.refs_0_), channel_id=1, source_target_pairs={{0,8},{4,12},{8,0},{12,4},{1,9},{5,13},{9,1},{13,5},{2,10},{6,14},... | collective-permute-start | bytes 884744 | tf_op jit(solution)/shard_map/ppermute | solution.py:430
  51.0 1.5 %collective-permute-start.19 = (bf16[4,192,384]{2,1,0:T(8,128)(2,1)S(1)}, bf16[4,192,384]{2,1,0:T(8,128)(2,1)S(1)}, u32[]{:S(2)}, u32[]{:S(2)}) collective-permute-start(bf16[4,192,384]{2,1,0:T(8,128)(2,1)S(1)} %pad_maximum_fusion.own_ref), channel_id=1, source_target_pairs={{0,16},{16,0},{1,17},{17,1},{2,18},{18,2},{3,19},{19,3},{4,20},{20... | collective-permute-start | bytes 1769480 | tf_op jit(solution)/shard_map/ppermute | solution.py:457
  53.1 5.1 %collective-permute-done.11.refs_3_ = bf16[2,192,384]{2,1,0:T(8,128)(2,1)S(1)} collective-permute-done((bf16[2,192,384]{2,1,0:T(8,128)(2,1)S(1)}, bf16[2,192,384]{2,1,0:T(8,128)(2,1)S(1)}, u32[]{:S(2)}, u32[]{:S(2)}) %collective-permute-start.11) | collective-permute-done | bytes 294944 | tf_op jit(solution)/shard_map/ppermute | solution.py:430
  58.2 1.3 %collective-permute-done.10.refs_2_ = bf16[2,192,384]{2,1,0:T(8,128)(2,1)S(1)} collective-permute-done((bf16[2,192,384]{2,1,0:T(8,128)(2,1)S(1)}, bf16[2,192,384]{2,1,0:T(8,128)(2,1)S(1)}, u32[]{:S(2)}, u32[]{:S(2)}) %collective-permute-start.10) | collective-permute-done | bytes 294944 | tf_op jit(solution)/shard_map/ppermute | solution.py:430
  59.5 2.4 %collective-permute-done.9.refs_1_ = bf16[2,192,384]{2,1,0:T(8,128)(2,1)S(1)} collective-permute-done((bf16[2,192,384]{2,1,0:T(8,128)(2,1)S(1)}, bf16[2,192,384]{2,1,0:T(8,128)(2,1)S(1)}, u32[]{:S(2)}, u32[]{:S(2)}) %collective-permute-start.9) | collective-permute-done | bytes 294944 | tf_op jit(solution)/shard_map/ppermute | solution.py:430
  61.9 1.1 %next_memory.2.lhs_ref.own_ref = bf16[384,1536]{1,0:T(8,128)(2,1)S(1)} custom-call(s32[5]{0:T(128)S(1)} %stack.47.place_ref, bf16[384,3072]{1,0:T(8,128)(2,1)S(1)} %get-tuple-element.59.memory_ref, bf16[2,192,384]{2,1,0:T(8,128)(2,1)S(1)} %pad_maximum_fusion.1.refs_0_, bf16[2,192,384]{2,1,0:T(8,128)(2,1)S(1)} %collective-permute-done.9.refs_1_, ...), custom_call_target="tpu_custom_call" | custom-call | flops 1179648 | bytes 3538944 | tf_op jit(solution)/shard_map/next_memory/pallas_call | solution.py:280
  63.0 1.6 %early_product.1.early_ref = f32[384,768]{1,0:T(8,128)S(1)} custom-call(s32[5]{0:T(128)S(1)} %stack.47.place_ref, bf16[384,1536]{1,0:T(8,128)(2,1)S(1)} %next_memory.2.lhs_ref.own_ref, bf16[3072,768]{1,0:T(8,128)(2,1)S(1)} %get-tuple-element.73.resident_ref), custom_call_target="tpu_custom_call" | custom-call | flops 905969664 | bytes 1179648 | tf_op jit(solution)/shard_map/early_product/pallas_call | solution.py:142
  64.7 1.1 %next_memory.3.lhs_ref.other_ref = bf16[384,1536]{1,0:T(8,128)(2,1)S(1)} custom-call(s32[5]{0:T(128)S(1)} %stack.47.place_ref, bf16[384,3072]{1,0:T(8,128)(2,1)S(1)} %get-tuple-element.59.memory_ref, bf16[2,192,384]{2,1,0:T(8,128)(2,1)S(1)} %collective-permute-done.12.refs_0_, bf16[2,192,384]{2,1,0:T(8,128)(2,1)S(1)} %collective-permute-done.13.refs_1_, ...), custom_call_target="tpu_custom_call" | custom-call | flops 1179648 | bytes 3538944 | tf_op jit(solution)/shard_map/next_memory/pallas_call | solution.py:280
  65.8 1.8 %late_product.1 = (bf16[192,384]{1,0:T(8,128)(2,1)S(1)}, bf16[192,384]{1,0:T(8,128)(2,1)S(1)}, bf16[192,384]{1,0:T(8,128)(2,1)S(1)}, bf16[192,384]{1,0:T(8,128)(2,1)S(1)}) custom-call(s32[5]{0:T(128)S(1)} %stack.47.place_ref, f32[384,768]{1,0:T(8,128)S(1)} %early_product.1.early_ref, bf16[384,1536]{1,0:T(8,128)(2,1)S(1)} %next_memory.3.lhs_ref.other_ref, ...), custom_call_target="tpu_custom_call" | custom-call | flops 905969664 | bytes 1179648 | tf_op jit(solution)/shard_map/late_product/pallas_call | solution.py:175
  67.6 1.5 %collective-permute-start.20 = (bf16[192,384]{1,0:T(8,128)(2,1)S(1)}, bf16[192,384]{1,0:T(8,128)(2,1)S(1)}, u32[]{:S(2)}, u32[]{:S(2)}) collective-permute-start(bf16[192,384]{1,0:T(8,128)(2,1)S(1)} %get-tuple-element.83), channel_id=1, source_target_pairs={{0,48},{1,49},{2,50},{3,51},{4,52},{5,53},{6,54},{7,55},{8,56},{9,... | collective-permute-start | bytes 442376 | tf_op jit(solution)/shard_map/ppermute | solution.py:409
  69.0 1.2 %collective-permute-start.21 = (bf16[192,384]{1,0:T(8,128)(2,1)S(1)}, bf16[192,384]{1,0:T(8,128)(2,1)S(1)}, u32[]{:S(2)}, u32[]{:S(2)}) collective-permute-start(bf16[192,384]{1,0:T(8,128)(2,1)S(1)} %get-tuple-element.84), channel_id=1, source_target_pairs={{0,32},{1,33},{2,34},{3,35},{4,36},{5,37},{6,38},{7,39},{8,40},{9,... | collective-permute-start | bytes 442376 | tf_op jit(solution)/shard_map/ppermute | solution.py:409
  70.2 1.9 %collective-permute-start.22 = (bf16[192,384]{1,0:T(8,128)(2,1)S(1)}, bf16[192,384]{1,0:T(8,128)(2,1)S(1)}, u32[]{:S(2)}, u32[]{:S(2)}) collective-permute-start(bf16[192,384]{1,0:T(8,128)(2,1)S(1)} %get-tuple-element.85), channel_id=1, source_target_pairs={{0,112},{1,113},{2,114},{3,115},{4,116},{5,117},{6,118},{7,119},{8... | collective-permute-start | bytes 442376 | tf_op jit(solution)/shard_map/ppermute | solution.py:409
  72.2 1.7 %collective-permute-start.23 = (bf16[192,384]{1,0:T(8,128)(2,1)S(1)}, bf16[192,384]{1,0:T(8,128)(2,1)S(1)}, u32[]{:S(2)}, u32[]{:S(2)}) collective-permute-start(bf16[192,384]{1,0:T(8,128)(2,1)S(1)} %get-tuple-element.86), channel_id=1, source_target_pairs={{0,96},{1,97},{2,98},{3,99},{4,100},{5,101},{6,102},{7,103},{8,104... | collective-permute-start | bytes 442376 | tf_op jit(solution)/shard_map/ppermute | solution.py:409
  73.8 2.7 %both_product.1 = (bf16[192,384]{1,0:T(8,128)(2,1)S(1)}, bf16[192,384]{1,0:T(8,128)(2,1)S(1)}, bf16[192,384]{1,0:T(8,128)(2,1)S(1)}, bf16[192,384]{1,0:T(8,128)(2,1)S(1)}) custom-call(s32[5]{0:T(128)S(1)} %stack.47.place_ref, bf16[384,1536]{1,0:T(8,128)(2,1)S(1)} %next_memory.2.lhs_ref.own_ref, bf16[384,1536]{1,0:T(8,128)(2,1)S(1)} %next_memory.3.lhs_ref.other_ref, ...), custom_call_target="tpu_custom_call" | custom-call | flops 905969664 | bytes 1179648 | tf_op jit(solution)/shard_map/both_product/pallas_call | solution.py:175
  76.5 0.6 collective-permute-start.24
  77.1 3.6 %collective-permute-start.25 = (bf16[192,384]{1,0:T(8,128)(2,1)S(1)}, bf16[192,384]{1,0:T(8,128)(2,1)S(1)}, u32[]{:S(2)}, u32[]{:S(2)}) collective-permute-start(bf16[192,384]{1,0:T(8,128)(2,1)S(1)} %get-tuple-element.90), channel_id=1, source_target_pairs={{0,64},{1,65},{2,66},{3,67},{4,68},{5,69},{6,70},{7,71},{8,72},{9,... | collective-permute-start | bytes 442376 | tf_op jit(solution)/shard_map/ppermute | solution.py:409
  80.7 0.9 collective-permute-start.26
  81.6 4.2 %collective-permute-done.24.refs_4_ = bf16[192,384]{1,0:T(8,128)(2,1)S(1)} collective-permute-done((bf16[192,384]{1,0:T(8,128)(2,1)S(1)}, bf16[192,384]{1,0:T(8,128)(2,1)S(1)}, u32[]{:S(2)}, u32[]{:S(2)}) %collective-permute-start.24) | collective-permute-done | bytes 147488 | tf_op jit(solution)/shard_map/ppermute | solution.py:409
  85.8 1.2 %collective-permute-done.25.refs_5_ = bf16[192,384]{1,0:T(8,128)(2,1)S(1)} collective-permute-done((bf16[192,384]{1,0:T(8,128)(2,1)S(1)}, bf16[192,384]{1,0:T(8,128)(2,1)S(1)}, u32[]{:S(2)}, u32[]{:S(2)}) %collective-permute-start.25) | collective-permute-done | bytes 147488 | tf_op jit(solution)/shard_map/ppermute | solution.py:409
  87.4 1.4 %second_solve.1.refs_0_ = bf16[192,384]{1,0:T(8,128)(2,1)S(1)} custom-call(s32[5]{0:T(128)S(1)} %stack.47.place_ref, bf16[192,384]{1,0:T(8,128)(2,1)S(1)} %collective-permute-done.20.refs_0_, bf16[192,384]{1,0:T(8,128)(2,1)S(1)} %collective-permute-done.21.refs_1_, bf16[192,384]{1,0:T(8,128)(2,1)S(1)} %collective-permute-done.22.refs_2_, ...), custom_call_target="tpu_custom_call" | custom-call | flops 339738624 | bytes 1769472 | tf_op jit(solution)/shard_map/second_solve/pallas_call | solution.py:340
  88.8 1.1 %collective-permute-start.30 = (bf16[192,384]{1,0:T(8,128)(2,1)S(1)}, bf16[192,384]{1,0:T(8,128)(2,1)S(1)}, u32[]{:S(2)}, u32[]{:S(2)}) collective-permute-start(bf16[192,384]{1,0:T(8,128)(2,1)S(1)} %second_solve.1.refs_0_), channel_id=1, source_target_pairs={{0,16},{16,0},{1,17},{17,1},{2,18},{18,2},{3,19},{19,3},{4,20},{20... | collective-permute-start | bytes 442376 | tf_op jit(solution)/shard_map/ppermute | solution.py:470
  90.0 1.7 %collective-permute-start.29 = (bf16[192,384]{1,0:T(8,128)(2,1)S(1)}, bf16[192,384]{1,0:T(8,128)(2,1)S(1)}, u32[]{:S(2)}, u32[]{:S(2)}) collective-permute-start(bf16[192,384]{1,0:T(8,128)(2,1)S(1)} %second_solve.1.refs_0_), channel_id=1, source_target_pairs={{0,96},{32,0},{64,32},{96,64},{1,97},{33,1},{65,33},{97,65},{2,98}... | collective-permute-start | bytes 442376 | tf_op jit(solution)/shard_map/ppermute | solution.py:430
  91.7 0.7 collective-permute-start.28
  92.5 1.5 %collective-permute-done.30.refs_4_ = bf16[192,384]{1,0:T(8,128)(2,1)S(1)} collective-permute-done((bf16[192,384]{1,0:T(8,128)(2,1)S(1)}, bf16[192,384]{1,0:T(8,128)(2,1)S(1)}, u32[]{:S(2)}, u32[]{:S(2)}) %collective-permute-start.30) | collective-permute-done | bytes 147488 | tf_op jit(solution)/shard_map/ppermute | solution.py:470
  94.1 1.6 %collective-permute-start.33 = (bf16[192,384]{1,0:T(8,128)(2,1)S(1)}, bf16[192,384]{1,0:T(8,128)(2,1)S(1)}, u32[]{:S(2)}, u32[]{:S(2)}) collective-permute-start(bf16[192,384]{1,0:T(8,128)(2,1)S(1)} %collective-permute-done.30.refs_4_), channel_id=1, source_target_pairs={{0,96},{32,0},{64,32},{96,64},{1,97},{33,1},{65,33},{97,65},{2,98}... | collective-permute-start | bytes 442376 | tf_op jit(solution)/shard_map/ppermute | solution.py:430
  95.6 1.6 %collective-permute-start.32 = (bf16[192,384]{1,0:T(8,128)(2,1)S(1)}, bf16[192,384]{1,0:T(8,128)(2,1)S(1)}, u32[]{:S(2)}, u32[]{:S(2)}) collective-permute-start(bf16[192,384]{1,0:T(8,128)(2,1)S(1)} %collective-permute-done.30.refs_4_), channel_id=1, source_target_pairs={{0,64},{32,96},{64,0},{96,32},{1,65},{33,97},{65,1},{97,33},{2,66}... | collective-permute-start | bytes 442376 | tf_op jit(solution)/shard_map/ppermute | solution.py:430
  97.6 1.8 %join_one.1.refs_8_ = bf16[2,384,1536]{2,1,0:T(8,128)(2,1)} custom-call(s32[5]{0:T(128)S(1)} %stack.47.place_ref, bf16[4,192,384]{2,1,0:T(8,128)(2,1)S(1)} %pad_maximum_fusion.own_ref, bf16[4,192,384]{2,1,0:T(8,128)(2,1)S(1)} %collective-permute-done.19.other_ref), custom_call_target="tpu_custom_call" | custom-call | flops 589824 | bytes 2359296 | tf_op jit(solution)/shard_map/join_one/pallas_call | solution.py:387
  99.4 0.6 collective-permute-done.28.refs_2_
  100.0 3.5 %collective-permute-done.27.refs_1_ = bf16[192,384]{1,0:T(8,128)(2,1)S(1)} collective-permute-done((bf16[192,384]{1,0:T(8,128)(2,1)S(1)}, bf16[192,384]{1,0:T(8,128)(2,1)S(1)}, u32[]{:S(2)}, u32[]{:S(2)}) %collective-permute-start.27) | collective-permute-done | bytes 147488 | tf_op jit(solution)/shard_map/ppermute | solution.py:430
  103.6 2.2 %collective-permute-done.32.refs_6_ = bf16[192,384]{1,0:T(8,128)(2,1)S(1)} collective-permute-done((bf16[192,384]{1,0:T(8,128)(2,1)S(1)}, bf16[192,384]{1,0:T(8,128)(2,1)S(1)}, u32[]{:S(2)}, u32[]{:S(2)}) %collective-permute-start.32) | collective-permute-done | bytes 147488 | tf_op jit(solution)/shard_map/ppermute | solution.py:430
  105.7 1.5 %collective-permute-done.31.refs_5_ = bf16[192,384]{1,0:T(8,128)(2,1)S(1)} collective-permute-done((bf16[192,384]{1,0:T(8,128)(2,1)S(1)}, bf16[192,384]{1,0:T(8,128)(2,1)S(1)}, u32[]{:S(2)}, u32[]{:S(2)}) %collective-permute-start.31) | collective-permute-done | bytes 147488 | tf_op jit(solution)/shard_map/ppermute | solution.py:430
  107.2 1.8 %join_two.1 = bf16[2,384,1536]{2,1,0:T(8,128)(2,1)} custom-call(s32[5]{0:T(128)S(1)} %stack.47.place_ref, bf16[192,384]{1,0:T(8,128)(2,1)S(1)} %second_solve.1.refs_0_, bf16[192,384]{1,0:T(8,128)(2,1)S(1)} %collective-permute-done.27.refs_1_, bf16[192,384]{1,0:T(8,128)(2,1)S(1)} %collective-permute-done.28.refs_2_, ...), custom_call_target="tpu_custom_call", output_to_operand_aliasing={{}: (9, {})} | custom-call | flops 589824 | bytes 2359296 | tf_op jit(solution)/shard_map/join_two/pallas_call | solution.py:387
  (43 shorter events, 2.3 us)
Async XLA Ops:
  6.6 12.5 %collective-permute-start.1 = (bf16[192,384]{1,0:T(8,128)(2,1)S(1)}, bf16[192,384]{1,0:T(8,128)(2,1)S(1)}, u32[]{:S(2)}, u32[]{:S(2)}) collective-permute-start(bf16[192,384]{1,0:T(8,128)(2,1)S(1)} %get-tuple-element.51), channel_id=1, source_target_pairs={{0,32},{1,33},{2,34},{3,35},{4,36},{5,37},{6,38},{7,39},{8,40},{9,... | collective-permute-start | bytes 442376 | tf_op jit(solution)/shard_map/ppermute | solution.py:409
  8.3 12.4 %collective-permute-start = (bf16[192,384]{1,0:T(8,128)(2,1)S(1)}, bf16[192,384]{1,0:T(8,128)(2,1)S(1)}, u32[]{:S(2)}, u32[]{:S(2)}) collective-permute-start(bf16[192,384]{1,0:T(8,128)(2,1)S(1)} %get-tuple-element.52), channel_id=1, source_target_pairs={{0,48},{1,49},{2,50},{3,51},{4,52},{5,53},{6,54},{7,55},{8,56},{9,... | collective-permute-start | bytes 442376 | tf_op jit(solution)/shard_map/ppermute | solution.py:409
  10.1 11.1 %collective-permute-start.3 = (bf16[192,384]{1,0:T(8,128)(2,1)S(1)}, bf16[192,384]{1,0:T(8,128)(2,1)S(1)}, u32[]{:S(2)}, u32[]{:S(2)}) collective-permute-start(bf16[192,384]{1,0:T(8,128)(2,1)S(1)} %get-tuple-element.53), channel_id=1, source_target_pairs={{0,96},{1,97},{2,98},{3,99},{4,100},{5,101},{6,102},{7,103},{8,104... | collective-permute-start | bytes 442376 | tf_op jit(solution)/shard_map/ppermute | solution.py:409
  13.2 13.6 %collective-permute-start.2 = (bf16[192,384]{1,0:T(8,128)(2,1)S(1)}, bf16[192,384]{1,0:T(8,128)(2,1)S(1)}, u32[]{:S(2)}, u32[]{:S(2)}) collective-permute-start(bf16[192,384]{1,0:T(8,128)(2,1)S(1)} %get-tuple-element.54), channel_id=1, source_target_pairs={{0,112},{1,113},{2,114},{3,115},{4,116},{5,117},{6,118},{7,119},{8... | collective-permute-start | bytes 442376 | tf_op jit(solution)/shard_map/ppermute | solution.py:409
  13.2 5.9 %copy-start.1 = (f32[32,32]{1,0:T(8,128)S(1)}, f32[32,32]{1,0:T(8,128)}, u32[]{:S(2)}) copy-start(f32[32,32]{1,0:T(8,128)} %param.9) | copy-start | bytes 12292
  13.2 8.0 %copy-start = (f32[2,384,384]{2,1,0:T(8,128)S(1)}, f32[2,384,384]{2,1,0:T(8,128)}, u32[]{:S(2)}) copy-start(f32[2,384,384]{2,1,0:T(8,128)} %param.8) | copy-start | bytes 3538948
  15.8 14.7 %collective-permute-start.4 = (bf16[192,384]{1,0:T(8,128)(2,1)S(1)}, bf16[192,384]{1,0:T(8,128)(2,1)S(1)}, u32[]{:S(2)}, u32[]{:S(2)}) collective-permute-start(bf16[192,384]{1,0:T(8,128)(2,1)S(1)} %get-tuple-element.64), channel_id=1, source_target_pairs={{0,80},{1,81},{2,82},{3,83},{4,84},{5,85},{6,86},{7,87},{8,88},{9,... | collective-permute-start | bytes 442376 | tf_op jit(solution)/shard_map/ppermute | solution.py:409
  19.1 11.4 %collective-permute-start.5 = (bf16[192,384]{1,0:T(8,128)(2,1)S(1)}, bf16[192,384]{1,0:T(8,128)(2,1)S(1)}, u32[]{:S(2)}, u32[]{:S(2)}) collective-permute-start(bf16[192,384]{1,0:T(8,128)(2,1)S(1)} %get-tuple-element.65), channel_id=1, source_target_pairs={{0,64},{1,65},{2,66},{3,67},{4,68},{5,69},{6,70},{7,71},{8,72},{9,... | collective-permute-start | bytes 442376 | tf_op jit(solution)/shard_map/ppermute | solution.py:409
  20.8 9.8 %collective-permute-start.6 = (bf16[192,384]{1,0:T(8,128)(2,1)S(1)}, bf16[192,384]{1,0:T(8,128)(2,1)S(1)}, u32[]{:S(2)}, u32[]{:S(2)}) collective-permute-start(bf16[192,384]{1,0:T(8,128)(2,1)S(1)} %get-tuple-element.66), channel_id=1, source_target_pairs={{0,16},{1,17},{2,18},{3,19},{4,20},{5,21},{6,22},{7,23},{8,24},{9,... | collective-permute-start | bytes 442376 | tf_op jit(solution)/shard_map/ppermute | solution.py:409
  32.4 14.3 %collective-permute-start.8 = (bf16[192,384]{1,0:T(8,128)(2,1)S(1)}, bf16[192,384]{1,0:T(8,128)(2,1)S(1)}, u32[]{:S(2)}, u32[]{:S(2)}) collective-permute-start(bf16[192,384]{1,0:T(8,128)(2,1)S(1)} %get-tuple-element.68), channel_id=1, source_target_pairs={{0,10},{1,11},{2,26},{3,27},{4,46},{5,47},{6,62},{7,63},{8,66},{9,... | collective-permute-start | bytes 442376 | tf_op jit(solution)/shard_map/ppermute | solution.py:409
  38.5 8.2 %collective-permute-start.7 = (bf16[192,384]{1,0:T(8,128)(2,1)S(1)}, bf16[192,384]{1,0:T(8,128)(2,1)S(1)}, u32[]{:S(2)}, u32[]{:S(2)}) collective-permute-start(bf16[192,384]{1,0:T(8,128)(2,1)S(1)} %get-tuple-element.68), channel_id=1, source_target_pairs={{0,0},{1,1},{2,16},{3,17},{4,36},{5,37},{6,52},{7,53},{8,72},{9,73... | collective-permute-start | bytes 442376 | tf_op jit(solution)/shard_map/ppermute | solution.py:409
  39.2 11.7 %collective-permute-start.18 = (bf16[192,384]{1,0:T(8,128)(2,1)S(1)}, bf16[192,384]{1,0:T(8,128)(2,1)S(1)}, u32[]{:S(2)}, u32[]{:S(2)}) collective-permute-start(bf16[192,384]{1,0:T(8,128)(2,1)S(1)} %get-tuple-element.72), channel_id=1, source_target_pairs={{0,96},{32,0},{64,32},{96,64},{1,97},{33,1},{65,33},{97,65},{2,98}... | collective-permute-start | bytes 442376 | tf_op jit(solution)/shard_map/ppermute | solution.py:430
  42.4 8.5 %collective-permute-start.17 = (bf16[192,384]{1,0:T(8,128)(2,1)S(1)}, bf16[192,384]{1,0:T(8,128)(2,1)S(1)}, u32[]{:S(2)}, u32[]{:S(2)}) collective-permute-start(bf16[192,384]{1,0:T(8,128)(2,1)S(1)} %get-tuple-element.72), channel_id=1, source_target_pairs={{0,64},{32,96},{64,0},{96,32},{1,65},{33,97},{65,1},{97,33},{2,66}... | collective-permute-start | bytes 442376 | tf_op jit(solution)/shard_map/ppermute | solution.py:430
  43.8 7.1 %collective-permute-start.16 = (bf16[192,384]{1,0:T(8,128)(2,1)S(1)}, bf16[192,384]{1,0:T(8,128)(2,1)S(1)}, u32[]{:S(2)}, u32[]{:S(2)}) collective-permute-start(bf16[192,384]{1,0:T(8,128)(2,1)S(1)} %get-tuple-element.72), channel_id=1, source_target_pairs={{0,32},{32,64},{64,96},{96,0},{1,33},{33,65},{65,97},{97,1},{2,34}... | collective-permute-start | bytes 442376 | tf_op jit(solution)/shard_map/ppermute | solution.py:430
  46.7 11.5 %collective-permute-start.11 = (bf16[2,192,384]{2,1,0:T(8,128)(2,1)S(1)}, bf16[2,192,384]{2,1,0:T(8,128)(2,1)S(1)}, u32[]{:S(2)}, u32[]{:S(2)}) collective-permute-start(bf16[2,192,384]{2,1,0:T(8,128)(2,1)S(1)} %pad_maximum_fusion.1.refs_0_), channel_id=1, source_target_pairs={{0,12},{4,0},{8,4},{12,8},{1,13},{5,1},{9,5},{13,9},{2,14},{6,2},{... | collective-permute-start | bytes 884744 | tf_op jit(solution)/shard_map/ppermute | solution.py:430
  48.8 10.7 %collective-permute-start.10 = (bf16[2,192,384]{2,1,0:T(8,128)(2,1)S(1)}, bf16[2,192,384]{2,1,0:T(8,128)(2,1)S(1)}, u32[]{:S(2)}, u32[]{:S(2)}) collective-permute-start(bf16[2,192,384]{2,1,0:T(8,128)(2,1)S(1)} %pad_maximum_fusion.1.refs_0_), channel_id=1, source_target_pairs={{0,8},{4,12},{8,0},{12,4},{1,9},{5,13},{9,1},{13,5},{2,10},{6,14},... | collective-permute-start | bytes 884744 | tf_op jit(solution)/shard_map/ppermute | solution.py:430
  51.0 13.7 %collective-permute-start.19 = (bf16[4,192,384]{2,1,0:T(8,128)(2,1)S(1)}, bf16[4,192,384]{2,1,0:T(8,128)(2,1)S(1)}, u32[]{:S(2)}, u32[]{:S(2)}) collective-permute-start(bf16[4,192,384]{2,1,0:T(8,128)(2,1)S(1)} %pad_maximum_fusion.own_ref), channel_id=1, source_target_pairs={{0,16},{16,0},{1,17},{17,1},{2,18},{18,2},{3,19},{19,3},{4,20},{20... | collective-permute-start | bytes 1769480 | tf_op jit(solution)/shard_map/ppermute | solution.py:457
  52.5 9.4 %collective-permute-start.9 = (bf16[2,192,384]{2,1,0:T(8,128)(2,1)S(1)}, bf16[2,192,384]{2,1,0:T(8,128)(2,1)S(1)}, u32[]{:S(2)}, u32[]{:S(2)}) collective-permute-start(bf16[2,192,384]{2,1,0:T(8,128)(2,1)S(1)} %pad_maximum_fusion.1.refs_0_), channel_id=1, source_target_pairs={{0,4},{4,8},{8,12},{12,0},{1,5},{5,9},{9,13},{13,1},{2,6},{6,10},{... | collective-permute-start | bytes 884744 | tf_op jit(solution)/shard_map/ppermute | solution.py:430
  53.1 11.5 %collective-permute-start.12 = (bf16[2,192,384]{2,1,0:T(8,128)(2,1)S(1)}, bf16[2,192,384]{2,1,0:T(8,128)(2,1)S(1)}, u32[]{:S(2)}, u32[]{:S(2)}) collective-permute-start(bf16[2,192,384]{2,1,0:T(8,128)(2,1)S(1)} %pad_maximum_fusion.1.refs_0_), channel_id=1, source_target_pairs={{0,1},{1,0},{2,3},{3,2},{4,5},{5,4},{6,7},{7,6},{8,9},{9,8},{10,11... | collective-permute-start | bytes 884744 | tf_op jit(solution)/shard_map/ppermute | solution.py:458
  58.2 6.5 %collective-permute-start.15 = (bf16[2,192,384]{2,1,0:T(8,128)(2,1)S(1)}, bf16[2,192,384]{2,1,0:T(8,128)(2,1)S(1)}, u32[]{:S(2)}, u32[]{:S(2)}) collective-permute-start(bf16[2,192,384]{2,1,0:T(8,128)(2,1)S(1)} %collective-permute-done.11.refs_3_), channel_id=1, source_target_pairs={{0,1},{1,0},{2,3},{3,2},{4,5},{5,4},{6,7},{7,6},{8,9},{9,8},{10,11... | collective-permute-start | bytes 884744 | tf_op jit(solution)/shard_map/ppermute | solution.py:458
  59.5 5.2 %collective-permute-start.14 = (bf16[2,192,384]{2,1,0:T(8,128)(2,1)S(1)}, bf16[2,192,384]{2,1,0:T(8,128)(2,1)S(1)}, u32[]{:S(2)}, u32[]{:S(2)}) collective-permute-start(bf16[2,192,384]{2,1,0:T(8,128)(2,1)S(1)} %collective-permute-done.10.refs_2_), channel_id=1, source_target_pairs={{0,1},{1,0},{2,3},{3,2},{4,5},{5,4},{6,7},{7,6},{8,9},{9,8},{10,11... | collective-permute-start | bytes 884744 | tf_op jit(solution)/shard_map/ppermute | solution.py:458
  61.9 2.8 %collective-permute-start.13 = (bf16[2,192,384]{2,1,0:T(8,128)(2,1)S(1)}, bf16[2,192,384]{2,1,0:T(8,128)(2,1)S(1)}, u32[]{:S(2)}, u32[]{:S(2)}) collective-permute-start(bf16[2,192,384]{2,1,0:T(8,128)(2,1)S(1)} %collective-permute-done.9.refs_1_), channel_id=1, source_target_pairs={{0,1},{1,0},{2,3},{3,2},{4,5},{5,4},{6,7},{7,6},{8,9},{9,8},{10,11... | collective-permute-start | bytes 884744 | tf_op jit(solution)/shard_map/ppermute | solution.py:458
  67.6 9.5 %collective-permute-start.20 = (bf16[192,384]{1,0:T(8,128)(2,1)S(1)}, bf16[192,384]{1,0:T(8,128)(2,1)S(1)}, u32[]{:S(2)}, u32[]{:S(2)}) collective-permute-start(bf16[192,384]{1,0:T(8,128)(2,1)S(1)} %get-tuple-element.83), channel_id=1, source_target_pairs={{0,48},{1,49},{2,50},{3,51},{4,52},{5,53},{6,54},{7,55},{8,56},{9,... | collective-permute-start | bytes 442376 | tf_op jit(solution)/shard_map/ppermute | solution.py:409
  69.0 11.6 %collective-permute-start.21 = (bf16[192,384]{1,0:T(8,128)(2,1)S(1)}, bf16[192,384]{1,0:T(8,128)(2,1)S(1)}, u32[]{:S(2)}, u32[]{:S(2)}) collective-permute-start(bf16[192,384]{1,0:T(8,128)(2,1)S(1)} %get-tuple-element.84), channel_id=1, source_target_pairs={{0,32},{1,33},{2,34},{3,35},{4,36},{5,37},{6,38},{7,39},{8,40},{9,... | collective-permute-start | bytes 442376 | tf_op jit(solution)/shard_map/ppermute | solution.py:409
  70.2 11.3 %collective-permute-start.22 = (bf16[192,384]{1,0:T(8,128)(2,1)S(1)}, bf16[192,384]{1,0:T(8,128)(2,1)S(1)}, u32[]{:S(2)}, u32[]{:S(2)}) collective-permute-start(bf16[192,384]{1,0:T(8,128)(2,1)S(1)} %get-tuple-element.85), channel_id=1, source_target_pairs={{0,112},{1,113},{2,114},{3,115},{4,116},{5,117},{6,118},{7,119},{8... | collective-permute-start | bytes 442376 | tf_op jit(solution)/shard_map/ppermute | solution.py:409
  72.2 9.4 %collective-permute-start.23 = (bf16[192,384]{1,0:T(8,128)(2,1)S(1)}, bf16[192,384]{1,0:T(8,128)(2,1)S(1)}, u32[]{:S(2)}, u32[]{:S(2)}) collective-permute-start(bf16[192,384]{1,0:T(8,128)(2,1)S(1)} %get-tuple-element.86), channel_id=1, source_target_pairs={{0,96},{1,97},{2,98},{3,99},{4,100},{5,101},{6,102},{7,103},{8,104... | collective-permute-start | bytes 442376 | tf_op jit(solution)/shard_map/ppermute | solution.py:409
  76.5 9.3 %collective-permute-start.24 = (bf16[192,384]{1,0:T(8,128)(2,1)S(1)}, bf16[192,384]{1,0:T(8,128)(2,1)S(1)}, u32[]{:S(2)}, u32[]{:S(2)}) collective-permute-start(bf16[192,384]{1,0:T(8,128)(2,1)S(1)} %get-tuple-element.89), channel_id=1, source_target_pairs={{0,80},{1,81},{2,82},{3,83},{4,84},{5,85},{6,86},{7,87},{8,88},{9,... | collective-permute-start | bytes 442376 | tf_op jit(solution)/shard_map/ppermute | solution.py:409
  77.1 9.9 %collective-permute-start.25 = (bf16[192,384]{1,0:T(8,128)(2,1)S(1)}, bf16[192,384]{1,0:T(8,128)(2,1)S(1)}, u32[]{:S(2)}, u32[]{:S(2)}) collective-permute-start(bf16[192,384]{1,0:T(8,128)(2,1)S(1)} %get-tuple-element.90), channel_id=1, source_target_pairs={{0,64},{1,65},{2,66},{3,67},{4,68},{5,69},{6,70},{7,71},{8,72},{9,... | collective-permute-start | bytes 442376 | tf_op jit(solution)/shard_map/ppermute | solution.py:409
  80.7 6.7 %collective-permute-start.26 = (bf16[192,384]{1,0:T(8,128)(2,1)S(1)}, bf16[192,384]{1,0:T(8,128)(2,1)S(1)}, u32[]{:S(2)}, u32[]{:S(2)}) collective-permute-start(bf16[192,384]{1,0:T(8,128)(2,1)S(1)} %get-tuple-element.91), channel_id=1, source_target_pairs={{0,16},{1,17},{2,18},{3,19},{4,20},{5,21},{6,22},{7,23},{8,24},{9,... | collective-permute-start | bytes 442376 | tf_op jit(solution)/shard_map/ppermute | solution.py:409
  88.8 5.2 %collective-permute-start.30 = (bf16[192,384]{1,0:T(8,128)(2,1)S(1)}, bf16[192,384]{1,0:T(8,128)(2,1)S(1)}, u32[]{:S(2)}, u32[]{:S(2)}) collective-permute-start(bf16[192,384]{1,0:T(8,128)(2,1)S(1)} %second_solve.1.refs_0_), channel_id=1, source_target_pairs={{0,16},{16,0},{1,17},{17,1},{2,18},{18,2},{3,19},{19,3},{4,20},{20... | collective-permute-start | bytes 442376 | tf_op jit(solution)/shard_map/ppermute | solution.py:470
  90.0 7.4 %collective-permute-start.29 = (bf16[192,384]{1,0:T(8,128)(2,1)S(1)}, bf16[192,384]{1,0:T(8,128)(2,1)S(1)}, u32[]{:S(2)}, u32[]{:S(2)}) collective-permute-start(bf16[192,384]{1,0:T(8,128)(2,1)S(1)} %second_solve.1.refs_0_), channel_id=1, source_target_pairs={{0,96},{32,0},{64,32},{96,64},{1,97},{33,1},{65,33},{97,65},{2,98}... | collective-permute-start | bytes 442376 | tf_op jit(solution)/shard_map/ppermute | solution.py:430
  91.7 8.3 %collective-permute-start.28 = (bf16[192,384]{1,0:T(8,128)(2,1)S(1)}, bf16[192,384]{1,0:T(8,128)(2,1)S(1)}, u32[]{:S(2)}, u32[]{:S(2)}) collective-permute-start(bf16[192,384]{1,0:T(8,128)(2,1)S(1)} %second_solve.1.refs_0_), channel_id=1, source_target_pairs={{0,64},{32,96},{64,0},{96,32},{1,65},{33,97},{65,1},{97,33},{2,66}... | collective-permute-start | bytes 442376 | tf_op jit(solution)/shard_map/ppermute | solution.py:430
  92.3 11.2 %collective-permute-start.27 = (bf16[192,384]{1,0:T(8,128)(2,1)S(1)}, bf16[192,384]{1,0:T(8,128)(2,1)S(1)}, u32[]{:S(2)}, u32[]{:S(2)}) collective-permute-start(bf16[192,384]{1,0:T(8,128)(2,1)S(1)} %second_solve.1.refs_0_), channel_id=1, source_target_pairs={{0,32},{32,64},{64,96},{96,0},{1,33},{33,65},{65,97},{97,1},{2,34}... | collective-permute-start | bytes 442376 | tf_op jit(solution)/shard_map/ppermute | solution.py:430
  94.1 9.5 %collective-permute-start.33 = (bf16[192,384]{1,0:T(8,128)(2,1)S(1)}, bf16[192,384]{1,0:T(8,128)(2,1)S(1)}, u32[]{:S(2)}, u32[]{:S(2)}) collective-permute-start(bf16[192,384]{1,0:T(8,128)(2,1)S(1)} %collective-permute-done.30.refs_4_), channel_id=1, source_target_pairs={{0,96},{32,0},{64,32},{96,64},{1,97},{33,1},{65,33},{97,65},{2,98}... | collective-permute-start | bytes 442376 | tf_op jit(solution)/shard_map/ppermute | solution.py:430
  95.6 10.1 %collective-permute-start.32 = (bf16[192,384]{1,0:T(8,128)(2,1)S(1)}, bf16[192,384]{1,0:T(8,128)(2,1)S(1)}, u32[]{:S(2)}, u32[]{:S(2)}) collective-permute-start(bf16[192,384]{1,0:T(8,128)(2,1)S(1)} %collective-permute-done.30.refs_4_), channel_id=1, source_target_pairs={{0,64},{32,96},{64,0},{96,32},{1,65},{33,97},{65,1},{97,33},{2,66}... | collective-permute-start | bytes 442376 | tf_op jit(solution)/shard_map/ppermute | solution.py:430
  97.4 9.8 %collective-permute-start.31 = (bf16[192,384]{1,0:T(8,128)(2,1)S(1)}, bf16[192,384]{1,0:T(8,128)(2,1)S(1)}, u32[]{:S(2)}, u32[]{:S(2)}) collective-permute-start(bf16[192,384]{1,0:T(8,128)(2,1)S(1)} %collective-permute-done.30.refs_4_), channel_id=1, source_target_pairs={{0,32},{32,64},{64,96},{96,0},{1,33},{33,65},{65,97},{97,1},{2,34}... | collective-permute-start | bytes 442376 | tf_op jit(solution)/shard_map/ppermute | solution.py:430

commit v14 on v13

--- a/solution.py
+++ b/solution.py
@@ -458,10 +458,10 @@
     other = [lax.ppermute(pair, "c", SWAP) for pair in own]
     own_lhs = next_memory(0, place, memory, own)
     early = early_product(place, own_lhs, odd_resident)
-    other, others, early = lax.optimization_barrier((other, others, early))
+    other, early = lax.optimization_barrier((other, early))
     other_lhs = next_memory(1, place, memory, other)
     odd = second_product(late_product_kernel, place, early, other_lhs, odd_resident, "late_product")
-    own_lhs, odd = lax.optimization_barrier((own_lhs, odd))
+    own_lhs, odd, others = lax.optimization_barrier((own_lhs, odd, others))
     even = second_product(both_product_kernel, place, own_lhs, other_lhs, even_resident, "both_product")
     parts = scatter(odd, 1) + scatter(even, 0)
     (front_two,) = solve(

time: 109 us -> 107 us (0.982)
  waiting for transfers between devices: 29.6 us -> 16.6 us
  starting transfers between devices: 47.8 us -> 58.2 us
    ppermute x12, waiting for transfers between devices: 16.7 us -> 9.9 us  [spread(): pairs[d] = lax.ppermute(pair, axis, [(i, (i + d) % 4) for i in range(4)])]
    ppermute x16, starting transfers between devices: 29.8 us -> 35.9 us  [move(): return lax.ppermute(value, ALL, pairs)]
    ppermute x16, waiting for transfers between devices: 11.4 us -> 6.65 us  [move(): return lax.ppermute(value, ALL, pairs)]
    ppermute x12, starting transfers between devices: 15.2 us -> 18.1 us  [spread(): pairs[d] = lax.ppermute(pair, axis, [(i, (i + d) % 4) for i in range(4)])]
    ppermute x1, waiting for transfers between devices: 1.53 us -> 0.01 us  [per_device(): twin = lax.ppermute(front_two, 'zl', SWAP)]
    ppermute x1, starting transfers between devices: 1.55 us -> 2.74 us  [per_device(): others = lax.ppermute(ones, 'zl', SWAP)]
  transfers between devices with their start and end apart: 34 -> 34, of which waited for: 13 -> 8; matrix products, arithmetic and copies ran while one was open for 0% -> 0% of each run, Pallas kernels for 15% -> 18%
where the time goes in v14:
time: 107 us
  starting transfers between devices  58.2 us (54%)
  Pallas kernels  31 us (29%)
  waiting for transfers between devices  16.6 us (16%)
    ppermute x16, starting transfers between devices, move(): return lax.ppermute(value, ALL, pairs)  35.9 us
    ppermute x12, starting transfers between devices, spread(): pairs[d] = lax.ppermute(pair, axis, [(i, (i + d) % 4) for i in range(4)])  18.1 us
    ppermute x12, waiting for transfers between devices, spread(): pairs[d] = lax.ppermute(pair, axis, [(i, (i + d) % 4) for i in range(4)])  9.9 us
    ppermute x16, waiting for transfers between devices, move(): return lax.ppermute(value, ALL, pairs)  6.65 us
    pallas_call x1, Pallas kernels, first_product(): pl.pallas_call(first_product_kernel, in_specs=[SMEM] + [pl.BlockSpec(memo...  6.5 us
    pallas_call x2, Pallas kernels, second_product(): pl.pallas_call(kernel, in_specs=[SMEM] + [VMEM] * 3, out_specs=[VMEM] * 4...  4.41 us
    pallas_call x1, Pallas kernels, bring_odd(): pl.pallas_call(bring_odd_kernel, in_specs=[SMEM] + [HBM] * 3, out_specs=[...  3.83 us
    pallas_call x2, Pallas kernels, join(): pl.pallas_call(kernel, in_specs=in_specs, out_specs=HBM, out_shape=jax.Sh...  3.61 us
  transfers between devices with their start and end apart: 34, of which 8 were waited for; matrix products, arithmetic and copies ran while one was open for 0% of the time, Pallas kernels for 18%

profile of v14, /device:TPU:0, one launch (start us, length us, event | category | flops | bytes accessed | tf_op | source)
XLA Modules:
  0.0 106.5 jit_solution(9623931818576421093)
XLA Ops:
  0.1 6.5 %first_product.1 = (bf16[192,384]{1,0:T(8,128)(2,1)S(1)}, bf16[192,384]{1,0:T(8,128)(2,1)S(1)}, bf16[192,384]{1,0:T(8,128)(2,1)S(1)}, bf16[192,384]{1,0:T(8,128)...) custom-call(s32[5]{0:T(128)S(1)} %stack.47.place_ref, bf16[2,384,3072]{2,1,0:T(8,128)(2,1)} %memory_ref.3, ...), custom_call_target="tpu_custom_call" | custom-call | flops 1811939328 | bytes 18874368 | tf_op jit(solution)/shard_map/first_product/pallas_call | solution.py:112
  6.6 3.1 %collective-permute-start = (bf16[192,384]{1,0:T(8,128)(2,1)S(1)}, bf16[192,384]{1,0:T(8,128)(2,1)S(1)}, u32[]{:S(2)}, u32[]{:S(2)}) collective-permute-start(bf16[192,384]{1,0:T(8,128)(2,1)S(1)} %get-tuple-element.52), channel_id=1, source_target_pairs={{0,48},{1,49},{2,50},{3,51},{4,52},{5,53},{6,54},{7,55},{8,56},{9,... | collective-permute-start | bytes 442376 | tf_op jit(solution)/shard_map/ppermute | solution.py:409
  9.7 0.5 collective-permute-start.1
  10.1 2.6 %collective-permute-start.2 = (bf16[192,384]{1,0:T(8,128)(2,1)S(1)}, bf16[192,384]{1,0:T(8,128)(2,1)S(1)}, u32[]{:S(2)}, u32[]{:S(2)}) collective-permute-start(bf16[192,384]{1,0:T(8,128)(2,1)S(1)} %get-tuple-element.54), channel_id=1, source_target_pairs={{0,112},{1,113},{2,114},{3,115},{4,116},{5,117},{6,118},{7,119},{8... | collective-permute-start | bytes 442376 | tf_op jit(solution)/shard_map/ppermute | solution.py:409
  12.7 0.5 collective-permute-start.3
  13.2 2.7 %half_product.1 = (bf16[192,384]{1,0:T(8,128)(2,1)S(1)}, bf16[192,384]{1,0:T(8,128)(2,1)S(1)}, bf16[192,384]{1,0:T(8,128)(2,1)S(1)}, bf16[192,384]{1,0:T(8,128)(2,1)S(1)}) custom-call(s32[5]{0:T(128)S(1)} %stack.47.place_ref, bf16[384,3072]{1,0:T(8,128)(2,1)S(1)} %get-tuple-element.55.lhs_ref, bf16[3072,768]{1,0:T(8,128)(2,1)S(1)} %get-tuple-element.56.resident_ref), custom_call_target="tpu_custom_call" | custom-call | flops 1811939328 | bytes 294912 | tf_op jit(solution)/shard_map/half_product/pallas_call | solution.py:60
  15.8 3.2 %collective-permute-start.4 = (bf16[192,384]{1,0:T(8,128)(2,1)S(1)}, bf16[192,384]{1,0:T(8,128)(2,1)S(1)}, u32[]{:S(2)}, u32[]{:S(2)}) collective-permute-start(bf16[192,384]{1,0:T(8,128)(2,1)S(1)} %get-tuple-element.64), channel_id=1, source_target_pairs={{0,80},{1,81},{2,82},{3,83},{4,84},{5,85},{6,86},{7,87},{8,88},{9,... | collective-permute-start | bytes 442376 | tf_op jit(solution)/shard_map/ppermute | solution.py:409
  19.1 1.6 %collective-permute-start.5 = (bf16[192,384]{1,0:T(8,128)(2,1)S(1)}, bf16[192,384]{1,0:T(8,128)(2,1)S(1)}, u32[]{:S(2)}, u32[]{:S(2)}) collective-permute-start(bf16[192,384]{1,0:T(8,128)(2,1)S(1)} %get-tuple-element.65), channel_id=1, source_target_pairs={{0,64},{1,65},{2,66},{3,67},{4,68},{5,69},{6,70},{7,71},{8,72},{9,... | collective-permute-start | bytes 442376 | tf_op jit(solution)/shard_map/ppermute | solution.py:409
  20.8 0.3 collective-permute-start.6
  21.2 3.8 %bring_odd.1 = (bf16[384,3072]{1,0:T(8,128)(2,1)S(1)}, bf16[192,384]{1,0:T(8,128)(2,1)S(1)}, bf16[192,384]{1,0:T(8,128)(2,1)S(1)}, bf16[3072,768]{1,0:T(8,128)(2,1)S(1)}) custom-call(s32[5]{0:T(128)S(1)} %stack.47.place_ref, bf16[2,384,3072]{2,1,0:T(8,128)(2,1)} %memory_ref.3, bf16[2,384,1536]{2,1,0:T(8,128)(2,1)} %previous_ref.1, ...), custom_call_target="tpu_custom_call" | custom-call | bytes 7077888 | tf_op jit(solution)/shard_map/bring_odd/pallas_call | solution.py:220
  25.1 1.4 %collective-permute-done.5.refs_5_ = bf16[192,384]{1,0:T(8,128)(2,1)S(1)} collective-permute-done((bf16[192,384]{1,0:T(8,128)(2,1)S(1)}, bf16[192,384]{1,0:T(8,128)(2,1)S(1)}, u32[]{:S(2)}, u32[]{:S(2)}) %collective-permute-start.5) | collective-permute-done | bytes 147488 | tf_op jit(solution)/shard_map/ppermute | solution.py:409
  26.5 1.8 %first_solve.1 = (bf16[192,384]{1,0:T(8,128)(2,1)S(1)}, bf16[192,384]{1,0:T(8,128)(2,1)S(1)}) custom-call(s32[5]{0:T(128)S(1)} %stack.47.place_ref, bf16[192,384]{1,0:T(8,128)(2,1)S(1)} %collective-permute-done.refs_0_, bf16[192,384]{1,0:T(8,128)(2,1)S(1)} %collective-permute-done.1.refs_1_, bf16[192,384]{1,0:T(8,128)(2,1)S(1)} %collective-permute-done.2.refs_2_, ...), custom_call_target="tpu_custom_call" | custom-call | flops 339738624 | bytes 1769472 | tf_op jit(solution)/shard_map/first_solve/pallas_call | solution.py:340
  28.3 0.7 collective-permute-start.7
  29.0 12.2 %collective-permute-start.8 = (bf16[192,384]{1,0:T(8,128)(2,1)S(1)}, bf16[192,384]{1,0:T(8,128)(2,1)S(1)}, u32[]{:S(2)}, u32[]{:S(2)}) collective-permute-start(bf16[192,384]{1,0:T(8,128)(2,1)S(1)} %get-tuple-element.68), channel_id=1, source_target_pairs={{0,10},{1,11},{2,26},{3,27},{4,46},{5,47},{6,62},{7,63},{8,66},{9,... | collective-permute-start | bytes 442376 | tf_op jit(solution)/shard_map/ppermute | solution.py:409
  41.2 4.0 %collective-permute-start.17 = (bf16[192,384]{1,0:T(8,128)(2,1)S(1)}, bf16[192,384]{1,0:T(8,128)(2,1)S(1)}, u32[]{:S(2)}, u32[]{:S(2)}) collective-permute-start(bf16[192,384]{1,0:T(8,128)(2,1)S(1)} %get-tuple-element.82), channel_id=1, source_target_pairs={{0,64},{32,96},{64,0},{96,32},{1,65},{33,97},{65,1},{97,33},{2,66}... | collective-permute-start | bytes 442376 | tf_op jit(solution)/shard_map/ppermute | solution.py:430
  45.2 2.9 %bring_even.1.resident_ref = bf16[3072,768]{1,0:T(8,128)(2,1)S(1)} custom-call(s32[5]{0:T(128)S(1)} %stack.47.place_ref, bf16[3072,1536]{1,0:T(8,128)(2,1)} %resident_ref.5), custom_call_target="tpu_custom_call" | custom-call | bytes 4718592 | tf_op jit(solution)/shard_map/bring_even/pallas_call | solution.py:244
  48.3 3.3 %collective-permute-start.10 = (bf16[2,192,384]{2,1,0:T(8,128)(2,1)S(1)}, bf16[2,192,384]{2,1,0:T(8,128)(2,1)S(1)}, u32[]{:S(2)}, u32[]{:S(2)}) collective-permute-start(bf16[2,192,384]{2,1,0:T(8,128)(2,1)S(1)} %pad_maximum_fusion.1.refs_0_), channel_id=1, source_target_pairs={{0,8},{4,12},{8,0},{12,4},{1,9},{5,13},{9,1},{13,5},{2,10},{6,14},... | collective-permute-start | bytes 884744 | tf_op jit(solution)/shard_map/ppermute | solution.py:430
  51.6 1.1 %collective-permute-start.11 = (bf16[2,192,384]{2,1,0:T(8,128)(2,1)S(1)}, bf16[2,192,384]{2,1,0:T(8,128)(2,1)S(1)}, u32[]{:S(2)}, u32[]{:S(2)}) collective-permute-start(bf16[2,192,384]{2,1,0:T(8,128)(2,1)S(1)} %pad_maximum_fusion.1.refs_0_), channel_id=1, source_target_pairs={{0,12},{4,0},{8,4},{12,8},{1,13},{5,1},{9,5},{13,9},{2,14},{6,2},{... | collective-permute-start | bytes 884744 | tf_op jit(solution)/shard_map/ppermute | solution.py:430
  52.8 2.7 %collective-permute-start.19 = (bf16[4,192,384]{2,1,0:T(8,128)(2,1)S(1)}, bf16[4,192,384]{2,1,0:T(8,128)(2,1)S(1)}, u32[]{:S(2)}, u32[]{:S(2)}) collective-permute-start(bf16[4,192,384]{2,1,0:T(8,128)(2,1)S(1)} %pad_maximum_fusion.own_ref), channel_id=1, source_target_pairs={{0,16},{16,0},{1,17},{17,1},{2,18},{18,2},{3,19},{19,3},{4,20},{20... | collective-permute-start | bytes 1769480 | tf_op jit(solution)/shard_map/ppermute | solution.py:457
  55.5 1.8 %collective-permute-done.9.refs_1_ = bf16[2,192,384]{2,1,0:T(8,128)(2,1)S(1)} collective-permute-done((bf16[2,192,384]{2,1,0:T(8,128)(2,1)S(1)}, bf16[2,192,384]{2,1,0:T(8,128)(2,1)S(1)}, u32[]{:S(2)}, u32[]{:S(2)}) %collective-permute-start.9) | collective-permute-done | bytes 294944 | tf_op jit(solution)/shard_map/ppermute | solution.py:430
  57.4 3.2 %collective-permute-done.10.refs_2_ = bf16[2,192,384]{2,1,0:T(8,128)(2,1)S(1)} collective-permute-done((bf16[2,192,384]{2,1,0:T(8,128)(2,1)S(1)}, bf16[2,192,384]{2,1,0:T(8,128)(2,1)S(1)}, u32[]{:S(2)}, u32[]{:S(2)}) %collective-permute-start.10) | collective-permute-done | bytes 294944 | tf_op jit(solution)/shard_map/ppermute | solution.py:430
  60.5 0.5 collective-permute-start.15
  61.0 1.1 %next_memory.2.lhs_ref.own_ref = bf16[384,1536]{1,0:T(8,128)(2,1)S(1)} custom-call(s32[5]{0:T(128)S(1)} %stack.47.place_ref, bf16[384,3072]{1,0:T(8,128)(2,1)S(1)} %get-tuple-element.59.memory_ref, bf16[2,192,384]{2,1,0:T(8,128)(2,1)S(1)} %pad_maximum_fusion.1.refs_0_, bf16[2,192,384]{2,1,0:T(8,128)(2,1)S(1)} %collective-permute-done.9.refs_1_, ...), custom_call_target="tpu_custom_call" | custom-call | flops 1179648 | bytes 3538944 | tf_op jit(solution)/shard_map/next_memory/pallas_call | solution.py:280
  62.1 1.6 %early_product.1.early_ref = f32[384,768]{1,0:T(8,128)S(1)} custom-call(s32[5]{0:T(128)S(1)} %stack.47.place_ref, bf16[384,1536]{1,0:T(8,128)(2,1)S(1)} %next_memory.2.lhs_ref.own_ref, bf16[3072,768]{1,0:T(8,128)(2,1)S(1)} %get-tuple-element.72.resident_ref), custom_call_target="tpu_custom_call" | custom-call | flops 905969664 | bytes 1179648 | tf_op jit(solution)/shard_map/early_product/pallas_call | solution.py:142
  63.8 1.1 %next_memory.3.lhs_ref.other_ref = bf16[384,1536]{1,0:T(8,128)(2,1)S(1)} custom-call(s32[5]{0:T(128)S(1)} %stack.47.place_ref, bf16[384,3072]{1,0:T(8,128)(2,1)S(1)} %get-tuple-element.59.memory_ref, bf16[2,192,384]{2,1,0:T(8,128)(2,1)S(1)} %collective-permute-done.12.refs_0_, bf16[2,192,384]{2,1,0:T(8,128)(2,1)S(1)} %collective-permute-done.13.refs_1_, ...), custom_call_target="tpu_custom_call" | custom-call | flops 1179648 | bytes 3538944 | tf_op jit(solution)/shard_map/next_memory/pallas_call | solution.py:280
  64.9 1.8 %late_product.1 = (bf16[192,384]{1,0:T(8,128)(2,1)S(1)}, bf16[192,384]{1,0:T(8,128)(2,1)S(1)}, bf16[192,384]{1,0:T(8,128)(2,1)S(1)}, bf16[192,384]{1,0:T(8,128)(2,1)S(1)}) custom-call(s32[5]{0:T(128)S(1)} %stack.47.place_ref, f32[384,768]{1,0:T(8,128)S(1)} %early_product.1.early_ref, bf16[384,1536]{1,0:T(8,128)(2,1)S(1)} %next_memory.3.lhs_ref.other_ref, ...), custom_call_target="tpu_custom_call" | custom-call | flops 905969664 | bytes 1179648 | tf_op jit(solution)/shard_map/late_product/pallas_call | solution.py:175
  66.7 2.0 %collective-permute-start.20 = (bf16[192,384]{1,0:T(8,128)(2,1)S(1)}, bf16[192,384]{1,0:T(8,128)(2,1)S(1)}, u32[]{:S(2)}, u32[]{:S(2)}) collective-permute-start(bf16[192,384]{1,0:T(8,128)(2,1)S(1)} %get-tuple-element.83), channel_id=1, source_target_pairs={{0,48},{1,49},{2,50},{3,51},{4,52},{5,53},{6,54},{7,55},{8,56},{9,... | collective-permute-start | bytes 442376 | tf_op jit(solution)/shard_map/ppermute | solution.py:409
  68.7 3.4 %collective-permute-start.22 = (bf16[192,384]{1,0:T(8,128)(2,1)S(1)}, bf16[192,384]{1,0:T(8,128)(2,1)S(1)}, u32[]{:S(2)}, u32[]{:S(2)}) collective-permute-start(bf16[192,384]{1,0:T(8,128)(2,1)S(1)} %get-tuple-element.85), channel_id=1, source_target_pairs={{0,112},{1,113},{2,114},{3,115},{4,116},{5,117},{6,118},{7,119},{8... | collective-permute-start | bytes 442376 | tf_op jit(solution)/shard_map/ppermute | solution.py:409
  72.1 0.8 collective-permute-start.23
  72.9 2.7 %both_product.1 = (bf16[192,384]{1,0:T(8,128)(2,1)S(1)}, bf16[192,384]{1,0:T(8,128)(2,1)S(1)}, bf16[192,384]{1,0:T(8,128)(2,1)S(1)}, bf16[192,384]{1,0:T(8,128)(2,1)S(1)}) custom-call(s32[5]{0:T(128)S(1)} %stack.47.place_ref, bf16[384,1536]{1,0:T(8,128)(2,1)S(1)} %next_memory.2.lhs_ref.own_ref, bf16[384,1536]{1,0:T(8,128)(2,1)S(1)} %next_memory.3.lhs_ref.other_ref, ...), custom_call_target="tpu_custom_call" | custom-call | flops 905969664 | bytes 1179648 | tf_op jit(solution)/shard_map/both_product/pallas_call | solution.py:175
  75.6 2.3 %collective-permute-start.24 = (bf16[192,384]{1,0:T(8,128)(2,1)S(1)}, bf16[192,384]{1,0:T(8,128)(2,1)S(1)}, u32[]{:S(2)}, u32[]{:S(2)}) collective-permute-start(bf16[192,384]{1,0:T(8,128)(2,1)S(1)} %get-tuple-element.89), channel_id=1, source_target_pairs={{0,80},{1,81},{2,82},{3,83},{4,84},{5,85},{6,86},{7,87},{8,88},{9,... | collective-permute-start | bytes 442376 | tf_op jit(solution)/shard_map/ppermute | solution.py:409
  77.9 1.2 %collective-permute-start.25 = (bf16[192,384]{1,0:T(8,128)(2,1)S(1)}, bf16[192,384]{1,0:T(8,128)(2,1)S(1)}, u32[]{:S(2)}, u32[]{:S(2)}) collective-permute-start(bf16[192,384]{1,0:T(8,128)(2,1)S(1)} %get-tuple-element.90), channel_id=1, source_target_pairs={{0,64},{1,65},{2,66},{3,67},{4,68},{5,69},{6,70},{7,71},{8,72},{9,... | collective-permute-start | bytes 442376 | tf_op jit(solution)/shard_map/ppermute | solution.py:409
  79.1 1.6 %collective-permute-start.26 = (bf16[192,384]{1,0:T(8,128)(2,1)S(1)}, bf16[192,384]{1,0:T(8,128)(2,1)S(1)}, u32[]{:S(2)}, u32[]{:S(2)}) collective-permute-start(bf16[192,384]{1,0:T(8,128)(2,1)S(1)} %get-tuple-element.91), channel_id=1, source_target_pairs={{0,16},{1,17},{2,18},{3,19},{4,20},{5,21},{6,22},{7,23},{8,24},{9,... | collective-permute-start | bytes 442376 | tf_op jit(solution)/shard_map/ppermute | solution.py:409
  80.7 4.9 %collective-permute-done.23.refs_3_ = bf16[192,384]{1,0:T(8,128)(2,1)S(1)} collective-permute-done((bf16[192,384]{1,0:T(8,128)(2,1)S(1)}, bf16[192,384]{1,0:T(8,128)(2,1)S(1)}, u32[]{:S(2)}, u32[]{:S(2)}) %collective-permute-start.23) | collective-permute-done | bytes 147488 | tf_op jit(solution)/shard_map/ppermute | solution.py:409
  85.6 0.3 collective-permute-done.26.refs_6_
  85.9 1.4 %second_solve.1.refs_0_ = bf16[192,384]{1,0:T(8,128)(2,1)S(1)} custom-call(s32[5]{0:T(128)S(1)} %stack.47.place_ref, bf16[192,384]{1,0:T(8,128)(2,1)S(1)} %collective-permute-done.20.refs_0_, bf16[192,384]{1,0:T(8,128)(2,1)S(1)} %collective-permute-done.21.refs_1_, bf16[192,384]{1,0:T(8,128)(2,1)S(1)} %collective-permute-done.22.refs_2_, ...), custom_call_target="tpu_custom_call" | custom-call | flops 339738624 | bytes 1769472 | tf_op jit(solution)/shard_map/second_solve/pallas_call | solution.py:340
  87.3 0.9 collective-permute-start.30
  88.2 0.6 collective-permute-start.27
  88.9 3.5 %collective-permute-start.28 = (bf16[192,384]{1,0:T(8,128)(2,1)S(1)}, bf16[192,384]{1,0:T(8,128)(2,1)S(1)}, u32[]{:S(2)}, u32[]{:S(2)}) collective-permute-start(bf16[192,384]{1,0:T(8,128)(2,1)S(1)} %second_solve.1.refs_0_), channel_id=1, source_target_pairs={{0,64},{32,96},{64,0},{96,32},{1,65},{33,97},{65,1},{97,33},{2,66}... | collective-permute-start | bytes 442376 | tf_op jit(solution)/shard_map/ppermute | solution.py:430
  92.4 0.9 collective-permute-start.29
  93.3 1.1 %collective-permute-start.31 = (bf16[192,384]{1,0:T(8,128)(2,1)S(1)}, bf16[192,384]{1,0:T(8,128)(2,1)S(1)}, u32[]{:S(2)}, u32[]{:S(2)}) collective-permute-start(bf16[192,384]{1,0:T(8,128)(2,1)S(1)} %collective-permute-done.30.refs_4_), channel_id=1, source_target_pairs={{0,32},{32,64},{64,96},{96,0},{1,33},{33,65},{65,97},{97,1},{2,34}... | collective-permute-start | bytes 442376 | tf_op jit(solution)/shard_map/ppermute | solution.py:430
  94.4 2.5 %collective-permute-start.32 = (bf16[192,384]{1,0:T(8,128)(2,1)S(1)}, bf16[192,384]{1,0:T(8,128)(2,1)S(1)}, u32[]{:S(2)}, u32[]{:S(2)}) collective-permute-start(bf16[192,384]{1,0:T(8,128)(2,1)S(1)} %collective-permute-done.30.refs_4_), channel_id=1, source_target_pairs={{0,64},{32,96},{64,0},{96,32},{1,65},{33,97},{65,1},{97,33},{2,66}... | collective-permute-start | bytes 442376 | tf_op jit(solution)/shard_map/ppermute | solution.py:430
  97.0 0.9 collective-permute-start.33
  97.8 1.8 %join_one.1.refs_8_ = bf16[2,384,1536]{2,1,0:T(8,128)(2,1)} custom-call(s32[5]{0:T(128)S(1)} %stack.47.place_ref, bf16[4,192,384]{2,1,0:T(8,128)(2,1)S(1)} %pad_maximum_fusion.own_ref, bf16[4,192,384]{2,1,0:T(8,128)(2,1)S(1)} %collective-permute-done.19.other_ref), custom_call_target="tpu_custom_call" | custom-call | flops 589824 | bytes 2359296 | tf_op jit(solution)/shard_map/join_one/pallas_call | solution.py:387
  99.7 0.8 collective-permute-done.28.refs_2_
  100.4 2.1 %collective-permute-done.31.refs_5_ = bf16[192,384]{1,0:T(8,128)(2,1)S(1)} collective-permute-done((bf16[192,384]{1,0:T(8,128)(2,1)S(1)}, bf16[192,384]{1,0:T(8,128)(2,1)S(1)}, u32[]{:S(2)}, u32[]{:S(2)}) %collective-permute-start.31) | collective-permute-done | bytes 147488 | tf_op jit(solution)/shard_map/ppermute | solution.py:430
  102.5 2.1 %collective-permute-done.32.refs_6_ = bf16[192,384]{1,0:T(8,128)(2,1)S(1)} collective-permute-done((bf16[192,384]{1,0:T(8,128)(2,1)S(1)}, bf16[192,384]{1,0:T(8,128)(2,1)S(1)}, u32[]{:S(2)}, u32[]{:S(2)}) %collective-permute-start.32) | collective-permute-done | bytes 147488 | tf_op jit(solution)/shard_map/ppermute | solution.py:430
  104.6 1.8 %join_two.1 = bf16[2,384,1536]{2,1,0:T(8,128)(2,1)} custom-call(s32[5]{0:T(128)S(1)} %stack.47.place_ref, bf16[192,384]{1,0:T(8,128)(2,1)S(1)} %second_solve.1.refs_0_, bf16[192,384]{1,0:T(8,128)(2,1)S(1)} %collective-permute-done.27.refs_1_, bf16[192,384]{1,0:T(8,128)(2,1)S(1)} %collective-permute-done.28.refs_2_, ...), custom_call_target="tpu_custom_call", output_to_operand_aliasing={{}: (9, {})} | custom-call | flops 589824 | bytes 2359296 | tf_op jit(solution)/shard_map/join_two/pallas_call | solution.py:387
  (43 shorter events, 0.6 us)
Async XLA Ops:
  6.6 12.5 %collective-permute-start = (bf16[192,384]{1,0:T(8,128)(2,1)S(1)}, bf16[192,384]{1,0:T(8,128)(2,1)S(1)}, u32[]{:S(2)}, u32[]{:S(2)}) collective-permute-start(bf16[192,384]{1,0:T(8,128)(2,1)S(1)} %get-tuple-element.52), channel_id=1, source_target_pairs={{0,48},{1,49},{2,50},{3,51},{4,52},{5,53},{6,54},{7,55},{8,56},{9,... | collective-permute-start | bytes 442376 | tf_op jit(solution)/shard_map/ppermute | solution.py:409
  9.7 11.1 %collective-permute-start.1 = (bf16[192,384]{1,0:T(8,128)(2,1)S(1)}, bf16[192,384]{1,0:T(8,128)(2,1)S(1)}, u32[]{:S(2)}, u32[]{:S(2)}) collective-permute-start(bf16[192,384]{1,0:T(8,128)(2,1)S(1)} %get-tuple-element.51), channel_id=1, source_target_pairs={{0,32},{1,33},{2,34},{3,35},{4,36},{5,37},{6,38},{7,39},{8,40},{9,... | collective-permute-start | bytes 442376 | tf_op jit(solution)/shard_map/ppermute | solution.py:409
  10.1 11.1 %collective-permute-start.2 = (bf16[192,384]{1,0:T(8,128)(2,1)S(1)}, bf16[192,384]{1,0:T(8,128)(2,1)S(1)}, u32[]{:S(2)}, u32[]{:S(2)}) collective-permute-start(bf16[192,384]{1,0:T(8,128)(2,1)S(1)} %get-tuple-element.54), channel_id=1, source_target_pairs={{0,112},{1,113},{2,114},{3,115},{4,116},{5,117},{6,118},{7,119},{8... | collective-permute-start | bytes 442376 | tf_op jit(solution)/shard_map/ppermute | solution.py:409
  12.7 8.5 %collective-permute-start.3 = (bf16[192,384]{1,0:T(8,128)(2,1)S(1)}, bf16[192,384]{1,0:T(8,128)(2,1)S(1)}, u32[]{:S(2)}, u32[]{:S(2)}) collective-permute-start(bf16[192,384]{1,0:T(8,128)(2,1)S(1)} %get-tuple-element.53), channel_id=1, source_target_pairs={{0,96},{1,97},{2,98},{3,99},{4,100},{5,101},{6,102},{7,103},{8,104... | collective-permute-start | bytes 442376 | tf_op jit(solution)/shard_map/ppermute | solution.py:409
  13.2 5.9 %copy-start.1 = (f32[32,32]{1,0:T(8,128)S(1)}, f32[32,32]{1,0:T(8,128)}, u32[]{:S(2)}) copy-start(f32[32,32]{1,0:T(8,128)} %param.9) | copy-start | bytes 12292
  13.2 7.9 %copy-start = (f32[2,384,384]{2,1,0:T(8,128)S(1)}, f32[2,384,384]{2,1,0:T(8,128)}, u32[]{:S(2)}) copy-start(f32[2,384,384]{2,1,0:T(8,128)} %param.8) | copy-start | bytes 3538948
  15.8 9.2 %collective-permute-start.4 = (bf16[192,384]{1,0:T(8,128)(2,1)S(1)}, bf16[192,384]{1,0:T(8,128)(2,1)S(1)}, u32[]{:S(2)}, u32[]{:S(2)}) collective-permute-start(bf16[192,384]{1,0:T(8,128)(2,1)S(1)} %get-tuple-element.64), channel_id=1, source_target_pairs={{0,80},{1,81},{2,82},{3,83},{4,84},{5,85},{6,86},{7,87},{8,88},{9,... | collective-permute-start | bytes 442376 | tf_op jit(solution)/shard_map/ppermute | solution.py:409
  19.1 7.4 %collective-permute-start.5 = (bf16[192,384]{1,0:T(8,128)(2,1)S(1)}, bf16[192,384]{1,0:T(8,128)(2,1)S(1)}, u32[]{:S(2)}, u32[]{:S(2)}) collective-permute-start(bf16[192,384]{1,0:T(8,128)(2,1)S(1)} %get-tuple-element.65), channel_id=1, source_target_pairs={{0,64},{1,65},{2,66},{3,67},{4,68},{5,69},{6,70},{7,71},{8,72},{9,... | collective-permute-start | bytes 442376 | tf_op jit(solution)/shard_map/ppermute | solution.py:409
  20.8 5.7 %collective-permute-start.6 = (bf16[192,384]{1,0:T(8,128)(2,1)S(1)}, bf16[192,384]{1,0:T(8,128)(2,1)S(1)}, u32[]{:S(2)}, u32[]{:S(2)}) collective-permute-start(bf16[192,384]{1,0:T(8,128)(2,1)S(1)} %get-tuple-element.66), channel_id=1, source_target_pairs={{0,16},{1,17},{2,18},{3,19},{4,20},{5,21},{6,22},{7,23},{8,24},{9,... | collective-permute-start | bytes 442376 | tf_op jit(solution)/shard_map/ppermute | solution.py:409
  28.3 19.8 %collective-permute-start.7 = (bf16[192,384]{1,0:T(8,128)(2,1)S(1)}, bf16[192,384]{1,0:T(8,128)(2,1)S(1)}, u32[]{:S(2)}, u32[]{:S(2)}) collective-permute-start(bf16[192,384]{1,0:T(8,128)(2,1)S(1)} %get-tuple-element.68), channel_id=1, source_target_pairs={{0,0},{1,1},{2,16},{3,17},{4,36},{5,37},{6,52},{7,53},{8,72},{9,73... | collective-permute-start | bytes 442376 | tf_op jit(solution)/shard_map/ppermute | solution.py:409
  29.0 19.2 %collective-permute-start.8 = (bf16[192,384]{1,0:T(8,128)(2,1)S(1)}, bf16[192,384]{1,0:T(8,128)(2,1)S(1)}, u32[]{:S(2)}, u32[]{:S(2)}) collective-permute-start(bf16[192,384]{1,0:T(8,128)(2,1)S(1)} %get-tuple-element.68), channel_id=1, source_target_pairs={{0,10},{1,11},{2,26},{3,27},{4,46},{5,47},{6,62},{7,63},{8,66},{9,... | collective-permute-start | bytes 442376 | tf_op jit(solution)/shard_map/ppermute | solution.py:409
  41.2 10.4 %collective-permute-start.18 = (bf16[192,384]{1,0:T(8,128)(2,1)S(1)}, bf16[192,384]{1,0:T(8,128)(2,1)S(1)}, u32[]{:S(2)}, u32[]{:S(2)}) collective-permute-start(bf16[192,384]{1,0:T(8,128)(2,1)S(1)} %get-tuple-element.82), channel_id=1, source_target_pairs={{0,96},{32,0},{64,32},{96,64},{1,97},{33,1},{65,33},{97,65},{2,98}... | collective-permute-start | bytes 442376 | tf_op jit(solution)/shard_map/ppermute | solution.py:430
  41.2 11.5 %collective-permute-start.17 = (bf16[192,384]{1,0:T(8,128)(2,1)S(1)}, bf16[192,384]{1,0:T(8,128)(2,1)S(1)}, u32[]{:S(2)}, u32[]{:S(2)}) collective-permute-start(bf16[192,384]{1,0:T(8,128)(2,1)S(1)} %get-tuple-element.82), channel_id=1, source_target_pairs={{0,64},{32,96},{64,0},{96,32},{1,65},{33,97},{65,1},{97,33},{2,66}... | collective-permute-start | bytes 442376 | tf_op jit(solution)/shard_map/ppermute | solution.py:430
  45.2 7.5 %collective-permute-start.16 = (bf16[192,384]{1,0:T(8,128)(2,1)S(1)}, bf16[192,384]{1,0:T(8,128)(2,1)S(1)}, u32[]{:S(2)}, u32[]{:S(2)}) collective-permute-start(bf16[192,384]{1,0:T(8,128)(2,1)S(1)} %get-tuple-element.82), channel_id=1, source_target_pairs={{0,32},{32,64},{64,96},{96,0},{1,33},{33,65},{65,97},{97,1},{2,34}... | collective-permute-start | bytes 442376 | tf_op jit(solution)/shard_map/ppermute | solution.py:430
  48.2 9.2 %collective-permute-start.9 = (bf16[2,192,384]{2,1,0:T(8,128)(2,1)S(1)}, bf16[2,192,384]{2,1,0:T(8,128)(2,1)S(1)}, u32[]{:S(2)}, u32[]{:S(2)}) collective-permute-start(bf16[2,192,384]{2,1,0:T(8,128)(2,1)S(1)} %pad_maximum_fusion.1.refs_0_), channel_id=1, source_target_pairs={{0,4},{4,8},{8,12},{12,0},{1,5},{5,9},{9,13},{13,1},{2,6},{6,10},{... | collective-permute-start | bytes 884744 | tf_op jit(solution)/shard_map/ppermute | solution.py:430
  48.3 12.2 %collective-permute-start.10 = (bf16[2,192,384]{2,1,0:T(8,128)(2,1)S(1)}, bf16[2,192,384]{2,1,0:T(8,128)(2,1)S(1)}, u32[]{:S(2)}, u32[]{:S(2)}) collective-permute-start(bf16[2,192,384]{2,1,0:T(8,128)(2,1)S(1)} %pad_maximum_fusion.1.refs_0_), channel_id=1, source_target_pairs={{0,8},{4,12},{8,0},{12,4},{1,9},{5,13},{9,1},{13,5},{2,10},{6,14},... | collective-permute-start | bytes 884744 | tf_op jit(solution)/shard_map/ppermute | solution.py:430
  51.6 9.0 %collective-permute-start.11 = (bf16[2,192,384]{2,1,0:T(8,128)(2,1)S(1)}, bf16[2,192,384]{2,1,0:T(8,128)(2,1)S(1)}, u32[]{:S(2)}, u32[]{:S(2)}) collective-permute-start(bf16[2,192,384]{2,1,0:T(8,128)(2,1)S(1)} %pad_maximum_fusion.1.refs_0_), channel_id=1, source_target_pairs={{0,12},{4,0},{8,4},{12,8},{1,13},{5,1},{9,5},{13,9},{2,14},{6,2},{... | collective-permute-start | bytes 884744 | tf_op jit(solution)/shard_map/ppermute | solution.py:430
  52.8 13.9 %collective-permute-start.19 = (bf16[4,192,384]{2,1,0:T(8,128)(2,1)S(1)}, bf16[4,192,384]{2,1,0:T(8,128)(2,1)S(1)}, u32[]{:S(2)}, u32[]{:S(2)}) collective-permute-start(bf16[4,192,384]{2,1,0:T(8,128)(2,1)S(1)} %pad_maximum_fusion.own_ref), channel_id=1, source_target_pairs={{0,16},{16,0},{1,17},{17,1},{2,18},{18,2},{3,19},{19,3},{4,20},{20... | collective-permute-start | bytes 1769480 | tf_op jit(solution)/shard_map/ppermute | solution.py:457
  55.5 8.2 %collective-permute-start.12 = (bf16[2,192,384]{2,1,0:T(8,128)(2,1)S(1)}, bf16[2,192,384]{2,1,0:T(8,128)(2,1)S(1)}, u32[]{:S(2)}, u32[]{:S(2)}) collective-permute-start(bf16[2,192,384]{2,1,0:T(8,128)(2,1)S(1)} %pad_maximum_fusion.1.refs_0_), channel_id=1, source_target_pairs={{0,1},{1,0},{2,3},{3,2},{4,5},{5,4},{6,7},{7,6},{8,9},{9,8},{10,11... | collective-permute-start | bytes 884744 | tf_op jit(solution)/shard_map/ppermute | solution.py:458
  57.4 6.4 %collective-permute-start.13 = (bf16[2,192,384]{2,1,0:T(8,128)(2,1)S(1)}, bf16[2,192,384]{2,1,0:T(8,128)(2,1)S(1)}, u32[]{:S(2)}, u32[]{:S(2)}) collective-permute-start(bf16[2,192,384]{2,1,0:T(8,128)(2,1)S(1)} %collective-permute-done.9.refs_1_), channel_id=1, source_target_pairs={{0,1},{1,0},{2,3},{3,2},{4,5},{5,4},{6,7},{7,6},{8,9},{9,8},{10,11... | collective-permute-start | bytes 884744 | tf_op jit(solution)/shard_map/ppermute | solution.py:458
  60.5 3.3 %collective-permute-start.14 = (bf16[2,192,384]{2,1,0:T(8,128)(2,1)S(1)}, bf16[2,192,384]{2,1,0:T(8,128)(2,1)S(1)}, u32[]{:S(2)}, u32[]{:S(2)}) collective-permute-start(bf16[2,192,384]{2,1,0:T(8,128)(2,1)S(1)} %collective-permute-done.10.refs_2_), channel_id=1, source_target_pairs={{0,1},{1,0},{2,3},{3,2},{4,5},{5,4},{6,7},{7,6},{8,9},{9,8},{10,11... | collective-permute-start | bytes 884744 | tf_op jit(solution)/shard_map/ppermute | solution.py:458
  60.5 3.3 %collective-permute-start.15 = (bf16[2,192,384]{2,1,0:T(8,128)(2,1)S(1)}, bf16[2,192,384]{2,1,0:T(8,128)(2,1)S(1)}, u32[]{:S(2)}, u32[]{:S(2)}) collective-permute-start(bf16[2,192,384]{2,1,0:T(8,128)(2,1)S(1)} %collective-permute-done.11.refs_3_), channel_id=1, source_target_pairs={{0,1},{1,0},{2,3},{3,2},{4,5},{5,4},{6,7},{7,6},{8,9},{9,8},{10,11... | collective-permute-start | bytes 884744 | tf_op jit(solution)/shard_map/ppermute | solution.py:458
  66.7 11.2 %collective-permute-start.20 = (bf16[192,384]{1,0:T(8,128)(2,1)S(1)}, bf16[192,384]{1,0:T(8,128)(2,1)S(1)}, u32[]{:S(2)}, u32[]{:S(2)}) collective-permute-start(bf16[192,384]{1,0:T(8,128)(2,1)S(1)} %get-tuple-element.83), channel_id=1, source_target_pairs={{0,48},{1,49},{2,50},{3,51},{4,52},{5,53},{6,54},{7,55},{8,56},{9,... | collective-permute-start | bytes 442376 | tf_op jit(solution)/shard_map/ppermute | solution.py:409
  68.7 10.4 %collective-permute-start.21 = (bf16[192,384]{1,0:T(8,128)(2,1)S(1)}, bf16[192,384]{1,0:T(8,128)(2,1)S(1)}, u32[]{:S(2)}, u32[]{:S(2)}) collective-permute-start(bf16[192,384]{1,0:T(8,128)(2,1)S(1)} %get-tuple-element.84), channel_id=1, source_target_pairs={{0,32},{1,33},{2,34},{3,35},{4,36},{5,37},{6,38},{7,39},{8,40},{9,... | collective-permute-start | bytes 442376 | tf_op jit(solution)/shard_map/ppermute | solution.py:409
  68.7 12.0 %collective-permute-start.22 = (bf16[192,384]{1,0:T(8,128)(2,1)S(1)}, bf16[192,384]{1,0:T(8,128)(2,1)S(1)}, u32[]{:S(2)}, u32[]{:S(2)}) collective-permute-start(bf16[192,384]{1,0:T(8,128)(2,1)S(1)} %get-tuple-element.85), channel_id=1, source_target_pairs={{0,112},{1,113},{2,114},{3,115},{4,116},{5,117},{6,118},{7,119},{8... | collective-permute-start | bytes 442376 | tf_op jit(solution)/shard_map/ppermute | solution.py:409
  72.1 13.5 %collective-permute-start.23 = (bf16[192,384]{1,0:T(8,128)(2,1)S(1)}, bf16[192,384]{1,0:T(8,128)(2,1)S(1)}, u32[]{:S(2)}, u32[]{:S(2)}) collective-permute-start(bf16[192,384]{1,0:T(8,128)(2,1)S(1)} %get-tuple-element.86), channel_id=1, source_target_pairs={{0,96},{1,97},{2,98},{3,99},{4,100},{5,101},{6,102},{7,103},{8,104... | collective-permute-start | bytes 442376 | tf_op jit(solution)/shard_map/ppermute | solution.py:409
  75.6 10.0 %collective-permute-start.24 = (bf16[192,384]{1,0:T(8,128)(2,1)S(1)}, bf16[192,384]{1,0:T(8,128)(2,1)S(1)}, u32[]{:S(2)}, u32[]{:S(2)}) collective-permute-start(bf16[192,384]{1,0:T(8,128)(2,1)S(1)} %get-tuple-element.89), channel_id=1, source_target_pairs={{0,80},{1,81},{2,82},{3,83},{4,84},{5,85},{6,86},{7,87},{8,88},{9,... | collective-permute-start | bytes 442376 | tf_op jit(solution)/shard_map/ppermute | solution.py:409
  77.9 7.7 %collective-permute-start.25 = (bf16[192,384]{1,0:T(8,128)(2,1)S(1)}, bf16[192,384]{1,0:T(8,128)(2,1)S(1)}, u32[]{:S(2)}, u32[]{:S(2)}) collective-permute-start(bf16[192,384]{1,0:T(8,128)(2,1)S(1)} %get-tuple-element.90), channel_id=1, source_target_pairs={{0,64},{1,65},{2,66},{3,67},{4,68},{5,69},{6,70},{7,71},{8,72},{9,... | collective-permute-start | bytes 442376 | tf_op jit(solution)/shard_map/ppermute | solution.py:409
  79.1 6.8 %collective-permute-start.26 = (bf16[192,384]{1,0:T(8,128)(2,1)S(1)}, bf16[192,384]{1,0:T(8,128)(2,1)S(1)}, u32[]{:S(2)}, u32[]{:S(2)}) collective-permute-start(bf16[192,384]{1,0:T(8,128)(2,1)S(1)} %get-tuple-element.91), channel_id=1, source_target_pairs={{0,16},{1,17},{2,18},{3,19},{4,20},{5,21},{6,22},{7,23},{8,24},{9,... | collective-permute-start | bytes 442376 | tf_op jit(solution)/shard_map/ppermute | solution.py:409
  87.3 6.0 %collective-permute-start.30 = (bf16[192,384]{1,0:T(8,128)(2,1)S(1)}, bf16[192,384]{1,0:T(8,128)(2,1)S(1)}, u32[]{:S(2)}, u32[]{:S(2)}) collective-permute-start(bf16[192,384]{1,0:T(8,128)(2,1)S(1)} %second_solve.1.refs_0_), channel_id=1, source_target_pairs={{0,16},{16,0},{1,17},{17,1},{2,18},{18,2},{3,19},{19,3},{4,20},{20... | collective-permute-start | bytes 442376 | tf_op jit(solution)/shard_map/ppermute | solution.py:470
  88.2 8.7 %collective-permute-start.27 = (bf16[192,384]{1,0:T(8,128)(2,1)S(1)}, bf16[192,384]{1,0:T(8,128)(2,1)S(1)}, u32[]{:S(2)}, u32[]{:S(2)}) collective-permute-start(bf16[192,384]{1,0:T(8,128)(2,1)S(1)} %second_solve.1.refs_0_), channel_id=1, source_target_pairs={{0,32},{32,64},{64,96},{96,0},{1,33},{33,65},{65,97},{97,1},{2,34}... | collective-permute-start | bytes 442376 | tf_op jit(solution)/shard_map/ppermute | solution.py:430
  88.9 11.6 %collective-permute-start.28 = (bf16[192,384]{1,0:T(8,128)(2,1)S(1)}, bf16[192,384]{1,0:T(8,128)(2,1)S(1)}, u32[]{:S(2)}, u32[]{:S(2)}) collective-permute-start(bf16[192,384]{1,0:T(8,128)(2,1)S(1)} %second_solve.1.refs_0_), channel_id=1, source_target_pairs={{0,64},{32,96},{64,0},{96,32},{1,65},{33,97},{65,1},{97,33},{2,66}... | collective-permute-start | bytes 442376 | tf_op jit(solution)/shard_map/ppermute | solution.py:430
  92.4 8.0 %collective-permute-start.29 = (bf16[192,384]{1,0:T(8,128)(2,1)S(1)}, bf16[192,384]{1,0:T(8,128)(2,1)S(1)}, u32[]{:S(2)}, u32[]{:S(2)}) collective-permute-start(bf16[192,384]{1,0:T(8,128)(2,1)S(1)} %second_solve.1.refs_0_), channel_id=1, source_target_pairs={{0,96},{32,0},{64,32},{96,64},{1,97},{33,1},{65,33},{97,65},{2,98}... | collective-permute-start | bytes 442376 | tf_op jit(solution)/shard_map/ppermute | solution.py:430
  93.3 9.2 %collective-permute-start.31 = (bf16[192,384]{1,0:T(8,128)(2,1)S(1)}, bf16[192,384]{1,0:T(8,128)(2,1)S(1)}, u32[]{:S(2)}, u32[]{:S(2)}) collective-permute-start(bf16[192,384]{1,0:T(8,128)(2,1)S(1)} %collective-permute-done.30.refs_4_), channel_id=1, source_target_pairs={{0,32},{32,64},{64,96},{96,0},{1,33},{33,65},{65,97},{97,1},{2,34}... | collective-permute-start | bytes 442376 | tf_op jit(solution)/shard_map/ppermute | solution.py:430
  94.4 10.1 %collective-permute-start.32 = (bf16[192,384]{1,0:T(8,128)(2,1)S(1)}, bf16[192,384]{1,0:T(8,128)(2,1)S(1)}, u32[]{:S(2)}, u32[]{:S(2)}) collective-permute-start(bf16[192,384]{1,0:T(8,128)(2,1)S(1)} %collective-permute-done.30.refs_4_), channel_id=1, source_target_pairs={{0,64},{32,96},{64,0},{96,32},{1,65},{33,97},{65,1},{97,33},{2,66}... | collective-permute-start | bytes 442376 | tf_op jit(solution)/shard_map/ppermute | solution.py:430
  97.0 7.6 %collective-permute-start.33 = (bf16[192,384]{1,0:T(8,128)(2,1)S(1)}, bf16[192,384]{1,0:T(8,128)(2,1)S(1)}, u32[]{:S(2)}, u32[]{:S(2)}) collective-permute-start(bf16[192,384]{1,0:T(8,128)(2,1)S(1)} %collective-permute-done.30.refs_4_), channel_id=1, source_target_pairs={{0,96},{32,0},{64,32},{96,64},{1,97},{33,1},{65,33},{97,65},{2,98}... | collective-permute-start | bytes 442376 | tf_op jit(solution)/shard_map/ppermute | solution.py:430

commit v15 on v14

--- a/solution.py
+++ b/solution.py
@@ -449,10 +449,11 @@
     )
     pair = [move(energy, turn(0)), move(energy, turn(1))]
     ones = spread(front_one, "y")
-    later, _ = lax.optimization_barrier((place, energy))
+    own = spread(jnp.stack(pair), "x")
+    later, _ = lax.optimization_barrier((place, pair))
     even_resident = bring_even(later, resident)
-    pair, even_resident = lax.optimization_barrier((pair, even_resident))
-    own = spread(jnp.stack(pair), "x")
+    for d in (1, 2, 3):
+        own[d], _ = lax.optimization_barrier((own[d], even_resident))
     ones = jnp.stack(ones)
     others = lax.ppermute(ones, "zl", SWAP)
     other = [lax.ppermute(pair, "c", SWAP) for pair in own]

time: 107 us -> 110 us (1.028)
  starting transfers between devices: 58.2 us -> 62.4 us
  waiting for transfers between devices: 16.6 us -> 15.2 us
    ppermute x12, starting transfers between devices: 18.1 us -> 30 us  [spread(): pairs[d] = lax.ppermute(pair, axis, [(i, (i + d) % 4) for i in range(4)])]
    ppermute x16, starting transfers between devices: 35.9 us -> 30.3 us  [move(): return lax.ppermute(value, ALL, pairs)]
    ppermute x1, starting transfers between devices: 2.74 us -> 0.09 us  [per_device(): others = lax.ppermute(ones, 'zl', SWAP)]
    ppermute x12, waiting for transfers between devices: 9.9 us -> 7.65 us  [spread(): pairs[d] = lax.ppermute(pair, axis, [(i, (i + d) % 4) for i in range(4)])]
where the time goes in v15:
time: 110 us; the launch traced here: 109 us
  starting transfers between devices  62.4 us (57%)
  Pallas kernels  31 us (28%)
  waiting for transfers between devices  15.2 us (14%)
    ppermute x16, starting transfers between devices, move(): return lax.ppermute(value, ALL, pairs)  30.3 us
    ppermute x12, starting transfers between devices, spread(): pairs[d] = lax.ppermute(pair, axis, [(i, (i + d) % 4) for i in range(4)])  30 us
    ppermute x12, waiting for transfers between devices, spread(): pairs[d] = lax.ppermute(pair, axis, [(i, (i + d) % 4) for i in range(4)])  7.65 us
    ppermute x16, waiting for transfers between devices, move(): return lax.ppermute(value, ALL, pairs)  7.55 us
    pallas_call x1, Pallas kernels, first_product(): pl.pallas_call(first_product_kernel, in_specs=[SMEM] + [pl.BlockSpec(memo...  6.5 us
    pallas_call x2, Pallas kernels, second_product(): pl.pallas_call(kernel, in_specs=[SMEM] + [VMEM] * 3, out_specs=[VMEM] * 4...  4.41 us
    pallas_call x1, Pallas kernels, bring_odd(): pl.pallas_call(bring_odd_kernel, in_specs=[SMEM] + [HBM] * 3, out_specs=[...  3.83 us
    pallas_call x2, Pallas kernels, join(): pl.pallas_call(kernel, in_specs=in_specs, out_specs=HBM, out_shape=jax.Sh...  3.61 us
  transfers between devices with their start and end apart: 34, of which 8 were waited for; matrix products, arithmetic and copies ran while one was open for 0% of the time, Pallas kernels for 18%

profile of v15, /device:TPU:0, one launch (start us, length us, event | category | flops | bytes accessed | tf_op | source)
XLA Modules:
  0.0 109.4 jit_solution(16574157342228528131)
XLA Ops:
  0.1 6.5 %first_product.1 = (bf16[192,384]{1,0:T(8,128)(2,1)S(1)}, bf16[192,384]{1,0:T(8,128)(2,1)S(1)}, bf16[192,384]{1,0:T(8,128)(2,1)S(1)}, bf16[192,384]{1,0:T(8,128)...) custom-call(s32[5]{0:T(128)S(1)} %stack.47.place_ref, bf16[2,384,3072]{2,1,0:T(8,128)(2,1)} %memory_ref.3, ...), custom_call_target="tpu_custom_call" | custom-call | flops 1811939328 | bytes 18874368 | tf_op jit(solution)/shard_map/first_product/pallas_call | solution.py:112
  6.6 3.1 %collective-permute-start = (bf16[192,384]{1,0:T(8,128)(2,1)S(1)}, bf16[192,384]{1,0:T(8,128)(2,1)S(1)}, u32[]{:S(2)}, u32[]{:S(2)}) collective-permute-start(bf16[192,384]{1,0:T(8,128)(2,1)S(1)} %get-tuple-element.52), channel_id=1, source_target_pairs={{0,48},{1,49},{2,50},{3,51},{4,52},{5,53},{6,54},{7,55},{8,56},{9,... | collective-permute-start | bytes 442376 | tf_op jit(solution)/shard_map/ppermute | solution.py:409
  9.7 0.5 collective-permute-start.1
  10.1 2.6 %collective-permute-start.2 = (bf16[192,384]{1,0:T(8,128)(2,1)S(1)}, bf16[192,384]{1,0:T(8,128)(2,1)S(1)}, u32[]{:S(2)}, u32[]{:S(2)}) collective-permute-start(bf16[192,384]{1,0:T(8,128)(2,1)S(1)} %get-tuple-element.54), channel_id=1, source_target_pairs={{0,112},{1,113},{2,114},{3,115},{4,116},{5,117},{6,118},{7,119},{8... | collective-permute-start | bytes 442376 | tf_op jit(solution)/shard_map/ppermute | solution.py:409
  12.7 0.5 collective-permute-start.3
  13.2 2.7 %half_product.1 = (bf16[192,384]{1,0:T(8,128)(2,1)S(1)}, bf16[192,384]{1,0:T(8,128)(2,1)S(1)}, bf16[192,384]{1,0:T(8,128)(2,1)S(1)}, bf16[192,384]{1,0:T(8,128)(2,1)S(1)}) custom-call(s32[5]{0:T(128)S(1)} %stack.47.place_ref, bf16[384,3072]{1,0:T(8,128)(2,1)S(1)} %get-tuple-element.55.lhs_ref, bf16[3072,768]{1,0:T(8,128)(2,1)S(1)} %get-tuple-element.56.resident_ref), custom_call_target="tpu_custom_call" | custom-call | flops 1811939328 | bytes 294912 | tf_op jit(solution)/shard_map/half_product/pallas_call | solution.py:60
  15.8 3.2 %collective-permute-start.4 = (bf16[192,384]{1,0:T(8,128)(2,1)S(1)}, bf16[192,384]{1,0:T(8,128)(2,1)S(1)}, u32[]{:S(2)}, u32[]{:S(2)}) collective-permute-start(bf16[192,384]{1,0:T(8,128)(2,1)S(1)} %get-tuple-element.64), channel_id=1, source_target_pairs={{0,80},{1,81},{2,82},{3,83},{4,84},{5,85},{6,86},{7,87},{8,88},{9,... | collective-permute-start | bytes 442376 | tf_op jit(solution)/shard_map/ppermute | solution.py:409
  19.1 1.6 %collective-permute-start.5 = (bf16[192,384]{1,0:T(8,128)(2,1)S(1)}, bf16[192,384]{1,0:T(8,128)(2,1)S(1)}, u32[]{:S(2)}, u32[]{:S(2)}) collective-permute-start(bf16[192,384]{1,0:T(8,128)(2,1)S(1)} %get-tuple-element.65), channel_id=1, source_target_pairs={{0,64},{1,65},{2,66},{3,67},{4,68},{5,69},{6,70},{7,71},{8,72},{9,... | collective-permute-start | bytes 442376 | tf_op jit(solution)/shard_map/ppermute | solution.py:409
  20.8 0.3 collective-permute-start.6
  21.2 3.8 %bring_odd.1 = (bf16[384,3072]{1,0:T(8,128)(2,1)S(1)}, bf16[192,384]{1,0:T(8,128)(2,1)S(1)}, bf16[192,384]{1,0:T(8,128)(2,1)S(1)}, bf16[3072,768]{1,0:T(8,128)(2,1)S(1)}) custom-call(s32[5]{0:T(128)S(1)} %stack.47.place_ref, bf16[2,384,3072]{2,1,0:T(8,128)(2,1)} %memory_ref.3, bf16[2,384,1536]{2,1,0:T(8,128)(2,1)} %previous_ref.1, ...), custom_call_target="tpu_custom_call" | custom-call | bytes 7077888 | tf_op jit(solution)/shard_map/bring_odd/pallas_call | solution.py:220
  25.1 1.4 %collective-permute-done.5.refs_5_ = bf16[192,384]{1,0:T(8,128)(2,1)S(1)} collective-permute-done((bf16[192,384]{1,0:T(8,128)(2,1)S(1)}, bf16[192,384]{1,0:T(8,128)(2,1)S(1)}, u32[]{:S(2)}, u32[]{:S(2)}) %collective-permute-start.5) | collective-permute-done | bytes 147488 | tf_op jit(solution)/shard_map/ppermute | solution.py:409
  26.5 1.8 %first_solve.1 = (bf16[192,384]{1,0:T(8,128)(2,1)S(1)}, bf16[192,384]{1,0:T(8,128)(2,1)S(1)}) custom-call(s32[5]{0:T(128)S(1)} %stack.47.place_ref, bf16[192,384]{1,0:T(8,128)(2,1)S(1)} %collective-permute-done.refs_0_, bf16[192,384]{1,0:T(8,128)(2,1)S(1)} %collective-permute-done.1.refs_1_, bf16[192,384]{1,0:T(8,128)(2,1)S(1)} %collective-permute-done.2.refs_2_, ...), custom_call_target="tpu_custom_call" | custom-call | flops 339738624 | bytes 1769472 | tf_op jit(solution)/shard_map/first_solve/pallas_call | solution.py:340
  28.3 6.1 %collective-permute-start.8 = (bf16[192,384]{1,0:T(8,128)(2,1)S(1)}, bf16[192,384]{1,0:T(8,128)(2,1)S(1)}, u32[]{:S(2)}, u32[]{:S(2)}) collective-permute-start(bf16[192,384]{1,0:T(8,128)(2,1)S(1)} %get-tuple-element.68), channel_id=1, source_target_pairs={{0,10},{1,11},{2,26},{3,27},{4,46},{5,47},{6,62},{7,63},{8,66},{9,... | collective-permute-start | bytes 442376 | tf_op jit(solution)/shard_map/ppermute | solution.py:409
  34.4 0.7 collective-permute-start.7
  35.1 7.3 %collective-permute-start.18 = (bf16[192,384]{1,0:T(8,128)(2,1)S(1)}, bf16[192,384]{1,0:T(8,128)(2,1)S(1)}, u32[]{:S(2)}, u32[]{:S(2)}) collective-permute-start(bf16[192,384]{1,0:T(8,128)(2,1)S(1)} %get-tuple-element.83), channel_id=1, source_target_pairs={{0,96},{32,0},{64,32},{96,64},{1,97},{33,1},{65,33},{97,65},{2,98}... | collective-permute-start | bytes 442376 | tf_op jit(solution)/shard_map/ppermute | solution.py:430
  42.4 2.7 %collective-permute-start.17 = (bf16[192,384]{1,0:T(8,128)(2,1)S(1)}, bf16[192,384]{1,0:T(8,128)(2,1)S(1)}, u32[]{:S(2)}, u32[]{:S(2)}) collective-permute-start(bf16[192,384]{1,0:T(8,128)(2,1)S(1)} %get-tuple-element.83), channel_id=1, source_target_pairs={{0,64},{32,96},{64,0},{96,32},{1,65},{33,97},{65,1},{97,33},{2,66}... | collective-permute-start | bytes 442376 | tf_op jit(solution)/shard_map/ppermute | solution.py:430
  45.1 1.3 %collective-permute-start.16 = (bf16[192,384]{1,0:T(8,128)(2,1)S(1)}, bf16[192,384]{1,0:T(8,128)(2,1)S(1)}, u32[]{:S(2)}, u32[]{:S(2)}) collective-permute-start(bf16[192,384]{1,0:T(8,128)(2,1)S(1)} %get-tuple-element.83), channel_id=1, source_target_pairs={{0,32},{32,64},{64,96},{96,0},{1,33},{33,65},{65,97},{97,1},{2,34}... | collective-permute-start | bytes 442376 | tf_op jit(solution)/shard_map/ppermute | solution.py:430
  46.6 6.3 %collective-permute-start.10 = (bf16[2,192,384]{2,1,0:T(8,128)(2,1)S(1)}, bf16[2,192,384]{2,1,0:T(8,128)(2,1)S(1)}, u32[]{:S(2)}, u32[]{:S(2)}) collective-permute-start(bf16[2,192,384]{2,1,0:T(8,128)(2,1)S(1)} %pad_maximum_fusion.1.refs_0_), channel_id=1, source_target_pairs={{0,8},{4,12},{8,0},{12,4},{1,9},{5,13},{9,1},{13,5},{2,10},{6,14},... | collective-permute-start | bytes 884744 | tf_op jit(solution)/shard_map/ppermute | solution.py:430
  52.9 2.5 %collective-permute-start.11 = (bf16[2,192,384]{2,1,0:T(8,128)(2,1)S(1)}, bf16[2,192,384]{2,1,0:T(8,128)(2,1)S(1)}, u32[]{:S(2)}, u32[]{:S(2)}) collective-permute-start(bf16[2,192,384]{2,1,0:T(8,128)(2,1)S(1)} %pad_maximum_fusion.1.refs_0_), channel_id=1, source_target_pairs={{0,12},{4,0},{8,4},{12,8},{1,13},{5,1},{9,5},{13,9},{2,14},{6,2},{... | collective-permute-start | bytes 884744 | tf_op jit(solution)/shard_map/ppermute | solution.py:430
  55.7 2.9 %bring_even.1.resident_ref = bf16[3072,768]{1,0:T(8,128)(2,1)S(1)} custom-call(s32[5]{0:T(128)S(1)} %stack.47.place_ref, bf16[3072,1536]{1,0:T(8,128)(2,1)} %resident_ref.5), custom_call_target="tpu_custom_call" | custom-call | bytes 4718592 | tf_op jit(solution)/shard_map/bring_even/pallas_call | solution.py:244
  58.6 2.0 %collective-permute-done.10.refs_2_ = bf16[2,192,384]{2,1,0:T(8,128)(2,1)S(1)} collective-permute-done((bf16[2,192,384]{2,1,0:T(8,128)(2,1)S(1)}, bf16[2,192,384]{2,1,0:T(8,128)(2,1)S(1)}, u32[]{:S(2)}, u32[]{:S(2)}) %collective-permute-start.10) | collective-permute-done | bytes 294944 | tf_op jit(solution)/shard_map/ppermute | solution.py:430
  60.7 0.5 collective-permute-start.14
  61.2 1.1 next_memory.2.lhs_ref.own_ref
  62.3 1.6 %early_product.1.early_ref = f32[384,768]{1,0:T(8,128)S(1)} custom-call(s32[5]{0:T(128)S(1)} %stack.47.place_ref, bf16[384,1536]{1,0:T(8,128)(2,1)S(1)} %next_memory.2.lhs_ref.own_ref, bf16[3072,768]{1,0:T(8,128)(2,1)S(1)} %get-tuple-element.73.resident_ref), custom_call_target="tpu_custom_call" | custom-call | flops 905969664 | bytes 1179648 | tf_op jit(solution)/shard_map/early_product/pallas_call | solution.py:142
  63.9 1.1 %next_memory.3.lhs_ref.other_ref = bf16[384,1536]{1,0:T(8,128)(2,1)S(1)} custom-call(s32[5]{0:T(128)S(1)} %stack.47.place_ref, bf16[384,3072]{1,0:T(8,128)(2,1)S(1)} %get-tuple-element.59.memory_ref, bf16[2,192,384]{2,1,0:T(8,128)(2,1)S(1)} %collective-permute-done.12.refs_0_, bf16[2,192,384]{2,1,0:T(8,128)(2,1)S(1)} %collective-permute-done.13.refs_1_, ...), custom_call_target="tpu_custom_call" | custom-call | flops 1179648 | bytes 3538944 | tf_op jit(solution)/shard_map/next_memory/pallas_call | solution.py:280
  65.1 1.8 %late_product.1 = (bf16[192,384]{1,0:T(8,128)(2,1)S(1)}, bf16[192,384]{1,0:T(8,128)(2,1)S(1)}, bf16[192,384]{1,0:T(8,128)(2,1)S(1)}, bf16[192,384]{1,0:T(8,128)(2,1)S(1)}) custom-call(s32[5]{0:T(128)S(1)} %stack.47.place_ref, f32[384,768]{1,0:T(8,128)S(1)} %early_product.1.early_ref, bf16[384,1536]{1,0:T(8,128)(2,1)S(1)} %next_memory.3.lhs_ref.other_ref, ...), custom_call_target="tpu_custom_call" | custom-call | flops 905969664 | bytes 1179648 | tf_op jit(solution)/shard_map/late_product/pallas_call | solution.py:175
  66.8 1.2 %collective-permute-start.20 = (bf16[192,384]{1,0:T(8,128)(2,1)S(1)}, bf16[192,384]{1,0:T(8,128)(2,1)S(1)}, u32[]{:S(2)}, u32[]{:S(2)}) collective-permute-start(bf16[192,384]{1,0:T(8,128)(2,1)S(1)} %get-tuple-element.84), channel_id=1, source_target_pairs={{0,48},{1,49},{2,50},{3,51},{4,52},{5,53},{6,54},{7,55},{8,56},{9,... | collective-permute-start | bytes 442376 | tf_op jit(solution)/shard_map/ppermute | solution.py:409
  68.0 1.6 %collective-permute-start.21 = (bf16[192,384]{1,0:T(8,128)(2,1)S(1)}, bf16[192,384]{1,0:T(8,128)(2,1)S(1)}, u32[]{:S(2)}, u32[]{:S(2)}) collective-permute-start(bf16[192,384]{1,0:T(8,128)(2,1)S(1)} %get-tuple-element.85), channel_id=1, source_target_pairs={{0,32},{1,33},{2,34},{3,35},{4,36},{5,37},{6,38},{7,39},{8,40},{9,... | collective-permute-start | bytes 442376 | tf_op jit(solution)/shard_map/ppermute | solution.py:409
  69.6 2.1 %collective-permute-start.22 = (bf16[192,384]{1,0:T(8,128)(2,1)S(1)}, bf16[192,384]{1,0:T(8,128)(2,1)S(1)}, u32[]{:S(2)}, u32[]{:S(2)}) collective-permute-start(bf16[192,384]{1,0:T(8,128)(2,1)S(1)} %get-tuple-element.86), channel_id=1, source_target_pairs={{0,112},{1,113},{2,114},{3,115},{4,116},{5,117},{6,118},{7,119},{8... | collective-permute-start | bytes 442376 | tf_op jit(solution)/shard_map/ppermute | solution.py:409
  71.7 1.8 %collective-permute-start.23 = (bf16[192,384]{1,0:T(8,128)(2,1)S(1)}, bf16[192,384]{1,0:T(8,128)(2,1)S(1)}, u32[]{:S(2)}, u32[]{:S(2)}) collective-permute-start(bf16[192,384]{1,0:T(8,128)(2,1)S(1)} %get-tuple-element.87), channel_id=1, source_target_pairs={{0,96},{1,97},{2,98},{3,99},{4,100},{5,101},{6,102},{7,103},{8,104... | collective-permute-start | bytes 442376 | tf_op jit(solution)/shard_map/ppermute | solution.py:409
  73.6 2.7 %both_product.1 = (bf16[192,384]{1,0:T(8,128)(2,1)S(1)}, bf16[192,384]{1,0:T(8,128)(2,1)S(1)}, bf16[192,384]{1,0:T(8,128)(2,1)S(1)}, bf16[192,384]{1,0:T(8,128)(2,1)S(1)}) custom-call(s32[5]{0:T(128)S(1)} %stack.47.place_ref, bf16[384,1536]{1,0:T(8,128)(2,1)S(1)} %next_memory.2.lhs_ref.own_ref, bf16[384,1536]{1,0:T(8,128)(2,1)S(1)} %next_memory.3.lhs_ref.other_ref, ...), custom_call_target="tpu_custom_call" | custom-call | flops 905969664 | bytes 1179648 | tf_op jit(solution)/shard_map/both_product/pallas_call | solution.py:175
  76.2 2.4 %collective-permute-start.24 = (bf16[192,384]{1,0:T(8,128)(2,1)S(1)}, bf16[192,384]{1,0:T(8,128)(2,1)S(1)}, u32[]{:S(2)}, u32[]{:S(2)}) collective-permute-start(bf16[192,384]{1,0:T(8,128)(2,1)S(1)} %get-tuple-element.89), channel_id=1, source_target_pairs={{0,80},{1,81},{2,82},{3,83},{4,84},{5,85},{6,86},{7,87},{8,88},{9,... | collective-permute-start | bytes 442376 | tf_op jit(solution)/shard_map/ppermute | solution.py:409
  78.7 2.1 %collective-permute-start.25 = (bf16[192,384]{1,0:T(8,128)(2,1)S(1)}, bf16[192,384]{1,0:T(8,128)(2,1)S(1)}, u32[]{:S(2)}, u32[]{:S(2)}) collective-permute-start(bf16[192,384]{1,0:T(8,128)(2,1)S(1)} %get-tuple-element.90), channel_id=1, source_target_pairs={{0,64},{1,65},{2,66},{3,67},{4,68},{5,69},{6,70},{7,71},{8,72},{9,... | collective-permute-start | bytes 442376 | tf_op jit(solution)/shard_map/ppermute | solution.py:409
  80.7 0.6 collective-permute-start.26
  81.3 4.2 %collective-permute-done.24.refs_4_ = bf16[192,384]{1,0:T(8,128)(2,1)S(1)} collective-permute-done((bf16[192,384]{1,0:T(8,128)(2,1)S(1)}, bf16[192,384]{1,0:T(8,128)(2,1)S(1)}, u32[]{:S(2)}, u32[]{:S(2)}) %collective-permute-start.24) | collective-permute-done | bytes 147488 | tf_op jit(solution)/shard_map/ppermute | solution.py:409
  85.5 1.8 %collective-permute-done.25.refs_5_ = bf16[192,384]{1,0:T(8,128)(2,1)S(1)} collective-permute-done((bf16[192,384]{1,0:T(8,128)(2,1)S(1)}, bf16[192,384]{1,0:T(8,128)(2,1)S(1)}, u32[]{:S(2)}, u32[]{:S(2)}) %collective-permute-start.25) | collective-permute-done | bytes 147488 | tf_op jit(solution)/shard_map/ppermute | solution.py:409
  87.4 1.4 %second_solve.1.refs_0_ = bf16[192,384]{1,0:T(8,128)(2,1)S(1)} custom-call(s32[5]{0:T(128)S(1)} %stack.47.place_ref, bf16[192,384]{1,0:T(8,128)(2,1)S(1)} %collective-permute-done.20.refs_0_, bf16[192,384]{1,0:T(8,128)(2,1)S(1)} %collective-permute-done.21.refs_1_, bf16[192,384]{1,0:T(8,128)(2,1)S(1)} %collective-permute-done.22.refs_2_, ...), custom_call_target="tpu_custom_call" | custom-call | flops 339738624 | bytes 1769472 | tf_op jit(solution)/shard_map/second_solve/pallas_call | solution.py:340
  88.9 1.4 %collective-permute-start.30 = (bf16[192,384]{1,0:T(8,128)(2,1)S(1)}, bf16[192,384]{1,0:T(8,128)(2,1)S(1)}, u32[]{:S(2)}, u32[]{:S(2)}) collective-permute-start(bf16[192,384]{1,0:T(8,128)(2,1)S(1)} %second_solve.1.refs_0_), channel_id=1, source_target_pairs={{0,16},{16,0},{1,17},{17,1},{2,18},{18,2},{3,19},{19,3},{4,20},{20... | collective-permute-start | bytes 442376 | tf_op jit(solution)/shard_map/ppermute | solution.py:471
  90.3 4.4 %collective-permute-start.28 = (bf16[192,384]{1,0:T(8,128)(2,1)S(1)}, bf16[192,384]{1,0:T(8,128)(2,1)S(1)}, u32[]{:S(2)}, u32[]{:S(2)}) collective-permute-start(bf16[192,384]{1,0:T(8,128)(2,1)S(1)} %second_solve.1.refs_0_), channel_id=1, source_target_pairs={{0,64},{32,96},{64,0},{96,32},{1,65},{33,97},{65,1},{97,33},{2,66}... | collective-permute-start | bytes 442376 | tf_op jit(solution)/shard_map/ppermute | solution.py:430
  94.7 0.1 collective-permute-start.29
  94.9 1.9 %collective-permute-start.31 = (bf16[192,384]{1,0:T(8,128)(2,1)S(1)}, bf16[192,384]{1,0:T(8,128)(2,1)S(1)}, u32[]{:S(2)}, u32[]{:S(2)}) collective-permute-start(bf16[192,384]{1,0:T(8,128)(2,1)S(1)} %collective-permute-done.30.refs_4_), channel_id=1, source_target_pairs={{0,32},{32,64},{64,96},{96,0},{1,33},{33,65},{65,97},{97,1},{2,34}... | collective-permute-start | bytes 442376 | tf_op jit(solution)/shard_map/ppermute | solution.py:430
  96.7 1.8 %collective-permute-start.32 = (bf16[192,384]{1,0:T(8,128)(2,1)S(1)}, bf16[192,384]{1,0:T(8,128)(2,1)S(1)}, u32[]{:S(2)}, u32[]{:S(2)}) collective-permute-start(bf16[192,384]{1,0:T(8,128)(2,1)S(1)} %collective-permute-done.30.refs_4_), channel_id=1, source_target_pairs={{0,64},{32,96},{64,0},{96,32},{1,65},{33,97},{65,1},{97,33},{2,66}... | collective-permute-start | bytes 442376 | tf_op jit(solution)/shard_map/ppermute | solution.py:430
  98.5 1.5 %collective-permute-start.33 = (bf16[192,384]{1,0:T(8,128)(2,1)S(1)}, bf16[192,384]{1,0:T(8,128)(2,1)S(1)}, u32[]{:S(2)}, u32[]{:S(2)}) collective-permute-start(bf16[192,384]{1,0:T(8,128)(2,1)S(1)} %collective-permute-done.30.refs_4_), channel_id=1, source_target_pairs={{0,96},{32,0},{64,32},{96,64},{1,97},{33,1},{65,33},{97,65},{2,98}... | collective-permute-start | bytes 442376 | tf_op jit(solution)/shard_map/ppermute | solution.py:430
  100.0 1.8 %join_one.1.refs_8_ = bf16[2,384,1536]{2,1,0:T(8,128)(2,1)} custom-call(s32[5]{0:T(128)S(1)} %stack.47.place_ref, bf16[4,192,384]{2,1,0:T(8,128)(2,1)S(1)} %pad_maximum_fusion.own_ref, bf16[4,192,384]{2,1,0:T(8,128)(2,1)S(1)} %collective-permute-done.19.other_ref), custom_call_target="tpu_custom_call" | custom-call | flops 589824 | bytes 2359296 | tf_op jit(solution)/shard_map/join_one/pallas_call | solution.py:387
  101.8 0.8 collective-permute-done.28.refs_2_
  102.6 1.2 %collective-permute-done.31.refs_5_ = bf16[192,384]{1,0:T(8,128)(2,1)S(1)} collective-permute-done((bf16[192,384]{1,0:T(8,128)(2,1)S(1)}, bf16[192,384]{1,0:T(8,128)(2,1)S(1)}, u32[]{:S(2)}, u32[]{:S(2)}) %collective-permute-start.31) | collective-permute-done | bytes 147488 | tf_op jit(solution)/shard_map/ppermute | solution.py:430
  103.8 3.6 %collective-permute-done.32.refs_6_ = bf16[192,384]{1,0:T(8,128)(2,1)S(1)} collective-permute-done((bf16[192,384]{1,0:T(8,128)(2,1)S(1)}, bf16[192,384]{1,0:T(8,128)(2,1)S(1)}, u32[]{:S(2)}, u32[]{:S(2)}) %collective-permute-start.32) | collective-permute-done | bytes 147488 | tf_op jit(solution)/shard_map/ppermute | solution.py:430
  107.5 1.8 %join_two.1 = bf16[2,384,1536]{2,1,0:T(8,128)(2,1)} custom-call(s32[5]{0:T(128)S(1)} %stack.47.place_ref, bf16[192,384]{1,0:T(8,128)(2,1)S(1)} %second_solve.1.refs_0_, bf16[192,384]{1,0:T(8,128)(2,1)S(1)} %collective-permute-done.27.refs_1_, bf16[192,384]{1,0:T(8,128)(2,1)S(1)} %collective-permute-done.28.refs_2_, ...), custom_call_target="tpu_custom_call", output_to_operand_aliasing={{}: (9, {})} | custom-call | flops 589824 | bytes 2359296 | tf_op jit(solution)/shard_map/join_two/pallas_call | solution.py:387
  (43 shorter events, 0.8 us)
Async XLA Ops:
  6.6 12.5 %collective-permute-start = (bf16[192,384]{1,0:T(8,128)(2,1)S(1)}, bf16[192,384]{1,0:T(8,128)(2,1)S(1)}, u32[]{:S(2)}, u32[]{:S(2)}) collective-permute-start(bf16[192,384]{1,0:T(8,128)(2,1)S(1)} %get-tuple-element.52), channel_id=1, source_target_pairs={{0,48},{1,49},{2,50},{3,51},{4,52},{5,53},{6,54},{7,55},{8,56},{9,... | collective-permute-start | bytes 442376 | tf_op jit(solution)/shard_map/ppermute | solution.py:409
  9.7 11.1 %collective-permute-start.1 = (bf16[192,384]{1,0:T(8,128)(2,1)S(1)}, bf16[192,384]{1,0:T(8,128)(2,1)S(1)}, u32[]{:S(2)}, u32[]{:S(2)}) collective-permute-start(bf16[192,384]{1,0:T(8,128)(2,1)S(1)} %get-tuple-element.51), channel_id=1, source_target_pairs={{0,32},{1,33},{2,34},{3,35},{4,36},{5,37},{6,38},{7,39},{8,40},{9,... | collective-permute-start | bytes 442376 | tf_op jit(solution)/shard_map/ppermute | solution.py:409
  10.1 11.1 %collective-permute-start.2 = (bf16[192,384]{1,0:T(8,128)(2,1)S(1)}, bf16[192,384]{1,0:T(8,128)(2,1)S(1)}, u32[]{:S(2)}, u32[]{:S(2)}) collective-permute-start(bf16[192,384]{1,0:T(8,128)(2,1)S(1)} %get-tuple-element.54), channel_id=1, source_target_pairs={{0,112},{1,113},{2,114},{3,115},{4,116},{5,117},{6,118},{7,119},{8... | collective-permute-start | bytes 442376 | tf_op jit(solution)/shard_map/ppermute | solution.py:409
  12.7 8.5 %collective-permute-start.3 = (bf16[192,384]{1,0:T(8,128)(2,1)S(1)}, bf16[192,384]{1,0:T(8,128)(2,1)S(1)}, u32[]{:S(2)}, u32[]{:S(2)}) collective-permute-start(bf16[192,384]{1,0:T(8,128)(2,1)S(1)} %get-tuple-element.53), channel_id=1, source_target_pairs={{0,96},{1,97},{2,98},{3,99},{4,100},{5,101},{6,102},{7,103},{8,104... | collective-permute-start | bytes 442376 | tf_op jit(solution)/shard_map/ppermute | solution.py:409
  13.2 5.9 %copy-start.1 = (f32[32,32]{1,0:T(8,128)S(1)}, f32[32,32]{1,0:T(8,128)}, u32[]{:S(2)}) copy-start(f32[32,32]{1,0:T(8,128)} %param.9) | copy-start | bytes 12292
  13.2 7.9 %copy-start = (f32[2,384,384]{2,1,0:T(8,128)S(1)}, f32[2,384,384]{2,1,0:T(8,128)}, u32[]{:S(2)}) copy-start(f32[2,384,384]{2,1,0:T(8,128)} %param.8) | copy-start | bytes 3538948
  15.8 9.2 %collective-permute-start.4 = (bf16[192,384]{1,0:T(8,128)(2,1)S(1)}, bf16[192,384]{1,0:T(8,128)(2,1)S(1)}, u32[]{:S(2)}, u32[]{:S(2)}) collective-permute-start(bf16[192,384]{1,0:T(8,128)(2,1)S(1)} %get-tuple-element.64), channel_id=1, source_target_pairs={{0,80},{1,81},{2,82},{3,83},{4,84},{5,85},{6,86},{7,87},{8,88},{9,... | collective-permute-start | bytes 442376 | tf_op jit(solution)/shard_map/ppermute | solution.py:409
  19.1 7.4 %collective-permute-start.5 = (bf16[192,384]{1,0:T(8,128)(2,1)S(1)}, bf16[192,384]{1,0:T(8,128)(2,1)S(1)}, u32[]{:S(2)}, u32[]{:S(2)}) collective-permute-start(bf16[192,384]{1,0:T(8,128)(2,1)S(1)} %get-tuple-element.65), channel_id=1, source_target_pairs={{0,64},{1,65},{2,66},{3,67},{4,68},{5,69},{6,70},{7,71},{8,72},{9,... | collective-permute-start | bytes 442376 | tf_op jit(solution)/shard_map/ppermute | solution.py:409
  20.8 5.7 %collective-permute-start.6 = (bf16[192,384]{1,0:T(8,128)(2,1)S(1)}, bf16[192,384]{1,0:T(8,128)(2,1)S(1)}, u32[]{:S(2)}, u32[]{:S(2)}) collective-permute-start(bf16[192,384]{1,0:T(8,128)(2,1)S(1)} %get-tuple-element.66), channel_id=1, source_target_pairs={{0,16},{1,17},{2,18},{3,19},{4,20},{5,21},{6,22},{7,23},{8,24},{9,... | collective-permute-start | bytes 442376 | tf_op jit(solution)/shard_map/ppermute | solution.py:409
  28.3 18.2 %collective-permute-start.8 = (bf16[192,384]{1,0:T(8,128)(2,1)S(1)}, bf16[192,384]{1,0:T(8,128)(2,1)S(1)}, u32[]{:S(2)}, u32[]{:S(2)}) collective-permute-start(bf16[192,384]{1,0:T(8,128)(2,1)S(1)} %get-tuple-element.68), channel_id=1, source_target_pairs={{0,10},{1,11},{2,26},{3,27},{4,46},{5,47},{6,62},{7,63},{8,66},{9,... | collective-permute-start | bytes 442376 | tf_op jit(solution)/shard_map/ppermute | solution.py:409
  34.4 12.1 %collective-permute-start.7 = (bf16[192,384]{1,0:T(8,128)(2,1)S(1)}, bf16[192,384]{1,0:T(8,128)(2,1)S(1)}, u32[]{:S(2)}, u32[]{:S(2)}) collective-permute-start(bf16[192,384]{1,0:T(8,128)(2,1)S(1)} %get-tuple-element.68), channel_id=1, source_target_pairs={{0,0},{1,1},{2,16},{3,17},{4,36},{5,37},{6,52},{7,53},{8,72},{9,73... | collective-permute-start | bytes 442376 | tf_op jit(solution)/shard_map/ppermute | solution.py:409
  35.1 17.8 %collective-permute-start.18 = (bf16[192,384]{1,0:T(8,128)(2,1)S(1)}, bf16[192,384]{1,0:T(8,128)(2,1)S(1)}, u32[]{:S(2)}, u32[]{:S(2)}) collective-permute-start(bf16[192,384]{1,0:T(8,128)(2,1)S(1)} %get-tuple-element.83), channel_id=1, source_target_pairs={{0,96},{32,0},{64,32},{96,64},{1,97},{33,1},{65,33},{97,65},{2,98}... | collective-permute-start | bytes 442376 | tf_op jit(solution)/shard_map/ppermute | solution.py:430
  42.4 13.0 %collective-permute-start.17 = (bf16[192,384]{1,0:T(8,128)(2,1)S(1)}, bf16[192,384]{1,0:T(8,128)(2,1)S(1)}, u32[]{:S(2)}, u32[]{:S(2)}) collective-permute-start(bf16[192,384]{1,0:T(8,128)(2,1)S(1)} %get-tuple-element.83), channel_id=1, source_target_pairs={{0,64},{32,96},{64,0},{96,32},{1,65},{33,97},{65,1},{97,33},{2,66}... | collective-permute-start | bytes 442376 | tf_op jit(solution)/shard_map/ppermute | solution.py:430
  45.1 10.3 %collective-permute-start.16 = (bf16[192,384]{1,0:T(8,128)(2,1)S(1)}, bf16[192,384]{1,0:T(8,128)(2,1)S(1)}, u32[]{:S(2)}, u32[]{:S(2)}) collective-permute-start(bf16[192,384]{1,0:T(8,128)(2,1)S(1)} %get-tuple-element.83), channel_id=1, source_target_pairs={{0,32},{32,64},{64,96},{96,0},{1,33},{33,65},{65,97},{97,1},{2,34}... | collective-permute-start | bytes 442376 | tf_op jit(solution)/shard_map/ppermute | solution.py:430
  46.5 12.1 %collective-permute-start.9 = (bf16[2,192,384]{2,1,0:T(8,128)(2,1)S(1)}, bf16[2,192,384]{2,1,0:T(8,128)(2,1)S(1)}, u32[]{:S(2)}, u32[]{:S(2)}) collective-permute-start(bf16[2,192,384]{2,1,0:T(8,128)(2,1)S(1)} %pad_maximum_fusion.1.refs_0_), channel_id=1, source_target_pairs={{0,4},{4,8},{8,12},{12,0},{1,5},{5,9},{9,13},{13,1},{2,6},{6,10},{... | collective-permute-start | bytes 884744 | tf_op jit(solution)/shard_map/ppermute | solution.py:430
  46.6 14.1 %collective-permute-start.10 = (bf16[2,192,384]{2,1,0:T(8,128)(2,1)S(1)}, bf16[2,192,384]{2,1,0:T(8,128)(2,1)S(1)}, u32[]{:S(2)}, u32[]{:S(2)}) collective-permute-start(bf16[2,192,384]{2,1,0:T(8,128)(2,1)S(1)} %pad_maximum_fusion.1.refs_0_), channel_id=1, source_target_pairs={{0,8},{4,12},{8,0},{12,4},{1,9},{5,13},{9,1},{13,5},{2,10},{6,14},... | collective-permute-start | bytes 884744 | tf_op jit(solution)/shard_map/ppermute | solution.py:430
  52.9 7.8 %collective-permute-start.11 = (bf16[2,192,384]{2,1,0:T(8,128)(2,1)S(1)}, bf16[2,192,384]{2,1,0:T(8,128)(2,1)S(1)}, u32[]{:S(2)}, u32[]{:S(2)}) collective-permute-start(bf16[2,192,384]{2,1,0:T(8,128)(2,1)S(1)} %pad_maximum_fusion.1.refs_0_), channel_id=1, source_target_pairs={{0,12},{4,0},{8,4},{12,8},{1,13},{5,1},{9,5},{13,9},{2,14},{6,2},{... | collective-permute-start | bytes 884744 | tf_op jit(solution)/shard_map/ppermute | solution.py:430
  55.5 11.3 %collective-permute-start.19 = (bf16[4,192,384]{2,1,0:T(8,128)(2,1)S(1)}, bf16[4,192,384]{2,1,0:T(8,128)(2,1)S(1)}, u32[]{:S(2)}, u32[]{:S(2)}) collective-permute-start(bf16[4,192,384]{2,1,0:T(8,128)(2,1)S(1)} %pad_maximum_fusion.own_ref), channel_id=1, source_target_pairs={{0,16},{16,0},{1,17},{17,1},{2,18},{18,2},{3,19},{19,3},{4,20},{20... | collective-permute-start | bytes 1769480 | tf_op jit(solution)/shard_map/ppermute | solution.py:458
  55.6 8.3 %collective-permute-start.12 = (bf16[2,192,384]{2,1,0:T(8,128)(2,1)S(1)}, bf16[2,192,384]{2,1,0:T(8,128)(2,1)S(1)}, u32[]{:S(2)}, u32[]{:S(2)}) collective-permute-start(bf16[2,192,384]{2,1,0:T(8,128)(2,1)S(1)} %pad_maximum_fusion.1.refs_0_), channel_id=1, source_target_pairs={{0,1},{1,0},{2,3},{3,2},{4,5},{5,4},{6,7},{7,6},{8,9},{9,8},{10,11... | collective-permute-start | bytes 884744 | tf_op jit(solution)/shard_map/ppermute | solution.py:459
  60.7 3.3 %collective-permute-start.13 = (bf16[2,192,384]{2,1,0:T(8,128)(2,1)S(1)}, bf16[2,192,384]{2,1,0:T(8,128)(2,1)S(1)}, u32[]{:S(2)}, u32[]{:S(2)}) collective-permute-start(bf16[2,192,384]{2,1,0:T(8,128)(2,1)S(1)} %collective-permute-done.9.refs_1_), channel_id=1, source_target_pairs={{0,1},{1,0},{2,3},{3,2},{4,5},{5,4},{6,7},{7,6},{8,9},{9,8},{10,11... | collective-permute-start | bytes 884744 | tf_op jit(solution)/shard_map/ppermute | solution.py:459
  60.7 3.3 %collective-permute-start.14 = (bf16[2,192,384]{2,1,0:T(8,128)(2,1)S(1)}, bf16[2,192,384]{2,1,0:T(8,128)(2,1)S(1)}, u32[]{:S(2)}, u32[]{:S(2)}) collective-permute-start(bf16[2,192,384]{2,1,0:T(8,128)(2,1)S(1)} %collective-permute-done.10.refs_2_), channel_id=1, source_target_pairs={{0,1},{1,0},{2,3},{3,2},{4,5},{5,4},{6,7},{7,6},{8,9},{9,8},{10,11... | collective-permute-start | bytes 884744 | tf_op jit(solution)/shard_map/ppermute | solution.py:459
  61.2 2.8 %collective-permute-start.15 = (bf16[2,192,384]{2,1,0:T(8,128)(2,1)S(1)}, bf16[2,192,384]{2,1,0:T(8,128)(2,1)S(1)}, u32[]{:S(2)}, u32[]{:S(2)}) collective-permute-start(bf16[2,192,384]{2,1,0:T(8,128)(2,1)S(1)} %collective-permute-done.11.refs_3_), channel_id=1, source_target_pairs={{0,1},{1,0},{2,3},{3,2},{4,5},{5,4},{6,7},{7,6},{8,9},{9,8},{10,11... | collective-permute-start | bytes 884744 | tf_op jit(solution)/shard_map/ppermute | solution.py:459
  66.8 11.8 %collective-permute-start.20 = (bf16[192,384]{1,0:T(8,128)(2,1)S(1)}, bf16[192,384]{1,0:T(8,128)(2,1)S(1)}, u32[]{:S(2)}, u32[]{:S(2)}) collective-permute-start(bf16[192,384]{1,0:T(8,128)(2,1)S(1)} %get-tuple-element.84), channel_id=1, source_target_pairs={{0,48},{1,49},{2,50},{3,51},{4,52},{5,53},{6,54},{7,55},{8,56},{9,... | collective-permute-start | bytes 442376 | tf_op jit(solution)/shard_map/ppermute | solution.py:409
  68.0 12.7 %collective-permute-start.21 = (bf16[192,384]{1,0:T(8,128)(2,1)S(1)}, bf16[192,384]{1,0:T(8,128)(2,1)S(1)}, u32[]{:S(2)}, u32[]{:S(2)}) collective-permute-start(bf16[192,384]{1,0:T(8,128)(2,1)S(1)} %get-tuple-element.85), channel_id=1, source_target_pairs={{0,32},{1,33},{2,34},{3,35},{4,36},{5,37},{6,38},{7,39},{8,40},{9,... | collective-permute-start | bytes 442376 | tf_op jit(solution)/shard_map/ppermute | solution.py:409
  69.6 11.7 %collective-permute-start.22 = (bf16[192,384]{1,0:T(8,128)(2,1)S(1)}, bf16[192,384]{1,0:T(8,128)(2,1)S(1)}, u32[]{:S(2)}, u32[]{:S(2)}) collective-permute-start(bf16[192,384]{1,0:T(8,128)(2,1)S(1)} %get-tuple-element.86), channel_id=1, source_target_pairs={{0,112},{1,113},{2,114},{3,115},{4,116},{5,117},{6,118},{7,119},{8... | collective-permute-start | bytes 442376 | tf_op jit(solution)/shard_map/ppermute | solution.py:409
  71.7 9.6 %collective-permute-start.23 = (bf16[192,384]{1,0:T(8,128)(2,1)S(1)}, bf16[192,384]{1,0:T(8,128)(2,1)S(1)}, u32[]{:S(2)}, u32[]{:S(2)}) collective-permute-start(bf16[192,384]{1,0:T(8,128)(2,1)S(1)} %get-tuple-element.87), channel_id=1, source_target_pairs={{0,96},{1,97},{2,98},{3,99},{4,100},{5,101},{6,102},{7,103},{8,104... | collective-permute-start | bytes 442376 | tf_op jit(solution)/shard_map/ppermute | solution.py:409
  76.2 9.3 %collective-permute-start.24 = (bf16[192,384]{1,0:T(8,128)(2,1)S(1)}, bf16[192,384]{1,0:T(8,128)(2,1)S(1)}, u32[]{:S(2)}, u32[]{:S(2)}) collective-permute-start(bf16[192,384]{1,0:T(8,128)(2,1)S(1)} %get-tuple-element.89), channel_id=1, source_target_pairs={{0,80},{1,81},{2,82},{3,83},{4,84},{5,85},{6,86},{7,87},{8,88},{9,... | collective-permute-start | bytes 442376 | tf_op jit(solution)/shard_map/ppermute | solution.py:409
  78.7 8.6 %collective-permute-start.25 = (bf16[192,384]{1,0:T(8,128)(2,1)S(1)}, bf16[192,384]{1,0:T(8,128)(2,1)S(1)}, u32[]{:S(2)}, u32[]{:S(2)}) collective-permute-start(bf16[192,384]{1,0:T(8,128)(2,1)S(1)} %get-tuple-element.90), channel_id=1, source_target_pairs={{0,64},{1,65},{2,66},{3,67},{4,68},{5,69},{6,70},{7,71},{8,72},{9,... | collective-permute-start | bytes 442376 | tf_op jit(solution)/shard_map/ppermute | solution.py:409
  80.7 6.7 %collective-permute-start.26 = (bf16[192,384]{1,0:T(8,128)(2,1)S(1)}, bf16[192,384]{1,0:T(8,128)(2,1)S(1)}, u32[]{:S(2)}, u32[]{:S(2)}) collective-permute-start(bf16[192,384]{1,0:T(8,128)(2,1)S(1)} %get-tuple-element.91), channel_id=1, source_target_pairs={{0,16},{1,17},{2,18},{3,19},{4,20},{5,21},{6,22},{7,23},{8,24},{9,... | collective-permute-start | bytes 442376 | tf_op jit(solution)/shard_map/ppermute | solution.py:409
  88.9 6.0 %collective-permute-start.30 = (bf16[192,384]{1,0:T(8,128)(2,1)S(1)}, bf16[192,384]{1,0:T(8,128)(2,1)S(1)}, u32[]{:S(2)}, u32[]{:S(2)}) collective-permute-start(bf16[192,384]{1,0:T(8,128)(2,1)S(1)} %second_solve.1.refs_0_), channel_id=1, source_target_pairs={{0,16},{16,0},{1,17},{17,1},{2,18},{18,2},{3,19},{19,3},{4,20},{20... | collective-permute-start | bytes 442376 | tf_op jit(solution)/shard_map/ppermute | solution.py:471
  90.3 8.2 %collective-permute-start.27 = (bf16[192,384]{1,0:T(8,128)(2,1)S(1)}, bf16[192,384]{1,0:T(8,128)(2,1)S(1)}, u32[]{:S(2)}, u32[]{:S(2)}) collective-permute-start(bf16[192,384]{1,0:T(8,128)(2,1)S(1)} %second_solve.1.refs_0_), channel_id=1, source_target_pairs={{0,32},{32,64},{64,96},{96,0},{1,33},{33,65},{65,97},{97,1},{2,34}... | collective-permute-start | bytes 442376 | tf_op jit(solution)/shard_map/ppermute | solution.py:430
  90.3 12.3 %collective-permute-start.28 = (bf16[192,384]{1,0:T(8,128)(2,1)S(1)}, bf16[192,384]{1,0:T(8,128)(2,1)S(1)}, u32[]{:S(2)}, u32[]{:S(2)}) collective-permute-start(bf16[192,384]{1,0:T(8,128)(2,1)S(1)} %second_solve.1.refs_0_), channel_id=1, source_target_pairs={{0,64},{32,96},{64,0},{96,32},{1,65},{33,97},{65,1},{97,33},{2,66}... | collective-permute-start | bytes 442376 | tf_op jit(solution)/shard_map/ppermute | solution.py:430
  94.7 7.9 %collective-permute-start.29 = (bf16[192,384]{1,0:T(8,128)(2,1)S(1)}, bf16[192,384]{1,0:T(8,128)(2,1)S(1)}, u32[]{:S(2)}, u32[]{:S(2)}) collective-permute-start(bf16[192,384]{1,0:T(8,128)(2,1)S(1)} %second_solve.1.refs_0_), channel_id=1, source_target_pairs={{0,96},{32,0},{64,32},{96,64},{1,97},{33,1},{65,33},{97,65},{2,98}... | collective-permute-start | bytes 442376 | tf_op jit(solution)/shard_map/ppermute | solution.py:430
  94.9 9.0 %collective-permute-start.31 = (bf16[192,384]{1,0:T(8,128)(2,1)S(1)}, bf16[192,384]{1,0:T(8,128)(2,1)S(1)}, u32[]{:S(2)}, u32[]{:S(2)}) collective-permute-start(bf16[192,384]{1,0:T(8,128)(2,1)S(1)} %collective-permute-done.30.refs_4_), channel_id=1, source_target_pairs={{0,32},{32,64},{64,96},{96,0},{1,33},{33,65},{65,97},{97,1},{2,34}... | collective-permute-start | bytes 442376 | tf_op jit(solution)/shard_map/ppermute | solution.py:430
  96.7 10.7 %collective-permute-start.32 = (bf16[192,384]{1,0:T(8,128)(2,1)S(1)}, bf16[192,384]{1,0:T(8,128)(2,1)S(1)}, u32[]{:S(2)}, u32[]{:S(2)}) collective-permute-start(bf16[192,384]{1,0:T(8,128)(2,1)S(1)} %collective-permute-done.30.refs_4_), channel_id=1, source_target_pairs={{0,64},{32,96},{64,0},{96,32},{1,65},{33,97},{65,1},{97,33},{2,66}... | collective-permute-start | bytes 442376 | tf_op jit(solution)/shard_map/ppermute | solution.py:430
  98.5 8.9 %collective-permute-start.33 = (bf16[192,384]{1,0:T(8,128)(2,1)S(1)}, bf16[192,384]{1,0:T(8,128)(2,1)S(1)}, u32[]{:S(2)}, u32[]{:S(2)}) collective-permute-start(bf16[192,384]{1,0:T(8,128)(2,1)S(1)} %collective-permute-done.30.refs_4_), channel_id=1, source_target_pairs={{0,96},{32,0},{64,32},{96,64},{1,97},{33,1},{65,33},{97,65},{2,98}... | collective-permute-start | bytes 442376 | tf_op jit(solution)/shard_map/ppermute | solution.py:430
